TPU v7x, 32 devices: a whole 2x2x4 slice. The times are simulated.
32 devices in a mesh: space: 8 (over z, x), orb: 4 (over y, core).
Axes of the slice: x: 2, y: 2, z: 4, core: 2. Of those that a mesh axis runs over, the one named last changes fastest.
Arguments:
- psi: bfloat16 [16, 48, 48, 512], P('space', None, None, 'orb'), may hold values from -6 to 6
- potential: float32 [16, 48, 48], P('space'), may hold values from 0 to 2
- beta: bfloat16 [8, 16, 48, 48], P(None, 'space'), may hold values from -0.21875 to 0.21875
- strength: float32 [8], replicated, may hold values from 0.5 to 4
- atom_slab: int32 [8], replicated, may hold values from 0 to 7, each once
- pattern: int32 [12, 2], replicated, may hold values from 0 to 3, as said below
- q_tiles: bfloat16 [12, 128, 128], replicated, may hold values from -0.3125 to 0.3125
Outputs:
- rotated: bfloat16 [16, 48, 48, 512], P('space', None, None, 'orb')
Inputs may be any that keep to these rules, and one draw needn't show every extreme that they name: `pattern`: the 12 tile coordinates are distinct, each in 0 to 3, and every diagonal tile is among them.
All inputs are finite; a program needn't handle non-finite values.
Results may differ from a plain program's by a relative error of at most 0.0064.
Values may be sent and summed in bfloat16 or wider, within the bound.
No kernel may reach another device: no remote copies, remote signals or barrier semaphores. Data moves between devices by JAX's collectives and lax.ppermute only.
A program may use at most 64 MiB of HBM per device.

v0:
```python
import jax
import jax.numpy as jnp
from jax import lax
from jax.sharding import PartitionSpec as P


def passed_along(array, axis, by):
    length = lax.axis_size(axis)
    pairs = [(i, i + by) for i in range(length) if 0 <= i + by < length]
    return lax.ppermute(array, axis, pairs)


def with_halo(block, sides, width):
    for axis, dim in sides:
        count = lax.axis_size(axis)
        forward = [(i, i + 1) for i in range(count - 1)]
        backward = [(target, source) for source, target in forward]
        low = lax.ppermute(
            lax.slice_in_dim(block, block.shape[dim] - width, None, axis=dim), axis, forward
        )
        high = lax.ppermute(lax.slice_in_dim(block, 0, width, axis=dim), axis, backward)
        block = jnp.concatenate([low, block, high], axis=dim)
    return block


def gather_partials(partial_proj):
    proj = partial_proj
    proj = proj + passed_along(partial_proj, "space", 1)
    proj = proj + passed_along(partial_proj, "space", -1)
    proj = proj + passed_along(partial_proj, "space", 2)
    proj = proj + passed_along(partial_proj, "space", -2)
    return proj


def apply_filter(v2, planes, potential_flat, beta_m, strength):
    f = planes.astype(jnp.float32)
    padded = with_halo(planes, (("space", 0),), 1).astype(jnp.float32)
    pxy = jnp.pad(f, ((0, 0), (1, 1), (1, 1), (0, 0)))
    beside = padded[2:] + padded[:-2]
    beside = beside + pxy[:, 2:, 1:-1] + pxy[:, :-2, 1:-1] + pxy[:, 1:-1, 2:] + pxy[:, 1:-1, :-2]
    kinetic = -0.5 * (beside - 6.0 * f)
    partial_proj = jnp.dot(beta_m, v2, preferred_element_type=jnp.float32)
    proj = gather_partials(partial_proj)
    coef = (strength[:, None] * proj).astype(jnp.bfloat16)
    nonlocal_term = lax.dot_general(
        beta_m, coef, (((0,), (0,)), ((), ())), preferred_element_type=jnp.float32
    )
    total = (
        kinetic.reshape(v2.shape) + potential_flat[:, None] * f.reshape(v2.shape) + nonlocal_term
    )
    return ((total - 4.0 * f.reshape(v2.shape)) / 4.0).astype(jnp.bfloat16)


def shards(psi, potential, beta, strength, atom_slab, pattern, q_tiles):
    planes_z, width_x, width_y, orb_cols = psi.shape
    cells = planes_z * width_x * width_y
    my_slab = lax.axis_index("space")
    active = jnp.abs(my_slab - atom_slab) <= 1
    flat_beta = beta.reshape(beta.shape[0], cells)
    beta_m = jnp.where(active[:, None], flat_beta, jnp.zeros_like(flat_beta))
    potential_flat = potential.reshape(cells)
    first = apply_filter(psi.reshape(cells, orb_cols), psi, potential_flat, beta_m, strength)
    second = apply_filter(
        first, first.reshape(planes_z, width_x, width_y, orb_cols), potential_flat, beta_m, strength
    )
    tile = q_tiles.shape[1]
    blocks = orb_cols * lax.axis_size("orb") // tile
    my_col = lax.axis_index("orb")
    ids = jnp.arange(blocks, dtype=jnp.int32)
    rows_hot = (pattern[:, 0][:, None] == ids[None, :]).astype(jnp.float32)
    mine = (pattern[:, 1] == my_col).astype(jnp.float32)
    column_q = jnp.einsum("ki,k,kab->iab", rows_hot, mine, q_tiles.astype(jnp.float32))
    column_q = column_q.reshape(blocks * tile, tile).astype(jnp.bfloat16)
    result = jnp.dot(
        lax.all_gather(second, "orb", axis=1, tiled=True),
        column_q,
        preferred_element_type=jnp.float32,
    )
    return result.astype(jnp.bfloat16).reshape(planes_z, width_x, width_y, orb_cols)


def solution(mesh):
    placed = (
        P("space", None, None, "orb"),
        P("space", None, None),
        P(None, "space", None, None),
        P(),
        P(),
        P(),
        P(),
    )
    return jax.shard_map(
        shards, mesh=mesh, in_specs=placed, out_specs=P("space", None, None, "orb"), check_vma=False
    )
```

profile of v0, /device:TPU:0, one launch (start us, length us, event | category | flops | bytes accessed | tf_op | source)
XLA Modules:
  0.0 137.3 jit_solution(8860781879933464515)
XLA Ops:
  6.5 0.0 copy-start
  6.5 0.0 copy-start.7
  6.5 0.0 copy-start.2
  6.5 0.0 all-gather.2.cloned.1.call-start
  6.5 2.5 %fusion.30 = (bf16[1,48,48,128]{3,2,1,0:T(8,128)(2,1)}, bf16[1,48,48,128]{3,2,1,0:T(8,128)(2,1)}) fusion(bf16[2,48,48,128]{3,2,1,0:T(8,128)(2,1)} %param.7), kind=kLoop, calls=%fused_computation.59 | loop fusion | bytes 2359296 | tf_op jit(solution)/shard_map/slice | solution.py:19
  9.0 5.7 %collective-permute-start = (bf16[1,48,48,128]{3,2,1,0:T(8,128)(2,1)}, bf16[1,48,48,128]{3,2,1,0:T(8,128)(2,1)}, u32[]{:S(2)}, u32[]{:S(2)}) collective-permute-start(bf16[1,48,48,128]{3,2,1,0:T(8,128)(2,1)} %get-tuple-element.9), channel_id=1, source_target_pairs={{0,4},{4,8},{8,12},{12,16},{16,20},{20,24},{24,28},{1,5},{5,9},{9,... | collective-permute-start | bytes 1769480 | tf_op jit(solution)/shard_map/ppermute | solution.py:18
  14.7 1.3 collective-permute-start.1
  16.0 0.0 copy-done.7
  16.0 0.0 copy-done.2
  16.0 0.1 broadcast_select_fusion
  16.1 0.0 copy-done
  16.1 0.6 convolution_bitcast_fusion
  16.7 4.5 %collective-permute-start.2 = (f32[8,128]{1,0:T(8,128)S(1)}, f32[8,128]{1,0:T(8,128)S(1)}, u32[]{:S(2)}, u32[]{:S(2)}) collective-permute-start(f32[8,128]{1,0:T(8,128)S(1)} %convolution_bitcast_fusion), channel_id=1, source_target_pairs={{0,4},{4,8},{8,12},{12,16},{16,20},{20,24},{24,28},{1,5},{5,9},{9,... | collective-permute-start | bytes 12296 | tf_op jit(solution)/shard_map/ppermute | solution.py:10
  21.2 1.3 collective-permute-start.3
  22.5 6.2 %collective-permute-start.4 = (f32[8,128]{1,0:T(8,128)S(1)}, f32[8,128]{1,0:T(8,128)}, u32[]{:S(2)}, u32[]{:S(2)}) collective-permute-start(f32[8,128]{1,0:T(8,128)S(1)} %convolution_bitcast_fusion), channel_id=1, source_target_pairs={{0,8},{4,12},{8,16},{12,20},{16,24},{20,28},{1,9},{5,13},{9,17},{1... | collective-permute-start | bytes 12296 | tf_op jit(solution)/shard_map/ppermute | solution.py:10
  28.7 0.2 convert_element_type.43
  28.9 1.8 %reshape.42 = bf16[8,4608]{1,0:T(8,128)(2,1)} reshape(bf16[8,2,48,48]{3,2,1,0:T(8,128)(2,1)} %param.9) | data formatting | bytes 147456 | tf_op jit(solution)/shard_map/reshape | solution.py:59
  30.7 1.5 %mul.50 = f32[4608]{0:T(1024)} reshape(f32[2,48,48]{2,1,0:T(8,128)} %param.8) | data formatting | bytes 36864 | tf_op jit(solution)/shard_map/mul | solution.py:49
  32.2 7.3 %collective-permute-done = bf16[1,48,48,128]{3,2,1,0:T(8,128)(2,1)} collective-permute-done((bf16[1,48,48,128]{3,2,1,0:T(8,128)(2,1)}, bf16[1,48,48,128]{3,2,1,0:T(8,128)(2,1)}, u32[]{:S(2)}, u32[]{:S(2)}) %collective-permute-start) | collective-permute-done | bytes 589856 | tf_op jit(solution)/shard_map/ppermute | solution.py:18
  39.5 1.3 collective-permute-start.5
  40.8 0.0 collective-permute-done.1
  40.8 1.6 %maximum_convert_fusion = f32[4,48,48,128]{3,2,1,0:T(8,128)S(1)} fusion(bf16[1,48,48,128]{3,2,1,0:T(8,128)(2,1)} %collective-permute-done.1, bf16[2,48,48,128]{3,2,1,0:T(8,128)(2,1)S(1)} %copy-done, bf16[1,48,48,128]{3,2,1,0:T(8,128)(2,1)} %collective-permute-done), kind=kLoop, calls=%fused_computation.34 | loop fusion | flops 3538944 | bytes 7077888 | tf_op jit(solution)/shard_map/convert_element_type | solution.py:37
  42.4 0.0 copy-start.4
  42.4 1.1 fusion.12
  43.5 0.0 copy-done.4
  43.5 0.0 copy-start.1
  43.5 0.0 copy-start.5
  43.5 2.0 %fusion.19 = (f32[4608,128]{1,0:T(8,128)S(1)}, f32[4608,128]{1,0:T(8,128)S(1)}) fusion(f32[2,48,48,128]{3,2,1,0:T(8,128)S(1)} %fusion.12, f32[4608]{0:T(1024)S(1)} %copy-done.4, bf16[2,48,48,128]{3,2,1,0:T(8,128)(2,1)S(1)} %copy-done), kind=kLoop, calls=%fused_computation.38 | loop fusion | flops 2359296 | bytes 8275968 | tf_op jit(solution)/shard_map/add | solution.py:49
  45.6 0.0 collective-permute-done.2
  45.6 0.0 collective-permute-done.3
  45.6 0.0 collective-permute-done.4
  45.6 0.0 collective-permute-done.5
  45.6 0.0 copy-done.1
  45.6 0.0 copy-done.5
  45.6 1.4 %fusion.4 = bf16[4608,128]{1,0:T(8,128)(2,1)S(1)} fusion(f32[4608,128]{1,0:T(8,128)S(1)} %get-tuple-element.8, f32[4608,128]{1,0:T(8,128)S(1)} %get-tuple-element.7, f32[8,128]{1,0:T(8,128)S(1)} %collective-permute-done.5, f32[8,128]{1,0:T(8,128)} %collective-permute-done.4, f32[8,128]{1,0:T(8,128)S(1)} %collective-permute-done.3, ...), kind=kOutput, calls=%fused_computation.6 | convolution fusion | flops 11839488 | bytes 5992488 | tf_op jit(solution)/shard_map/dot_general | solution.py:45
  47.0 0.1 fusion.29
  47.1 4.4 %collective-permute-start.6 = (bf16[1,48,48,128]{3,2,1,0:T(8,128)(2,1)S(1)}, bf16[1,48,48,128]{3,2,1,0:T(8,128)(2,1)S(1)}, u32[]{:S(2)}, u32[]{:S(2)}) collective-permute-start(bf16[1,48,48,128]{3,2,1,0:T(8,128)(2,1)S(1)} %bitcast.34), channel_id=1, source_target_pairs={{0,4},{4,8},{8,12},{12,16},{16,20},{20,24},{24,28},{1,5},{5,9},{9,... | collective-permute-start | bytes 1769480 | tf_op jit(solution)/shard_map/ppermute | solution.py:18
  51.5 1.3 collective-permute-start.7
  52.8 0.3 fusion.28
  53.2 5.6 %collective-permute-start.10 = (f32[8,128]{1,0:T(8,128)S(1)}, f32[8,128]{1,0:T(8,128)S(1)}, u32[]{:S(2)}, u32[]{:S(2)}) collective-permute-start(f32[8,128]{1,0:T(8,128)S(1)} %fusion.28), channel_id=1, source_target_pairs={{0,8},{4,12},{8,16},{12,20},{16,24},{20,28},{1,9},{5,13},{9,17},{1... | collective-permute-start | bytes 12296 | tf_op jit(solution)/shard_map/ppermute | solution.py:10
  58.7 1.3 collective-permute-start.11
  60.0 3.5 %collective-permute-start.8 = (f32[8,128]{1,0:T(8,128)S(1)}, f32[8,128]{1,0:T(8,128)S(1)}, u32[]{:S(2)}, u32[]{:S(2)}) collective-permute-start(f32[8,128]{1,0:T(8,128)S(1)} %fusion.28), channel_id=1, source_target_pairs={{0,4},{4,8},{8,12},{12,16},{16,20},{20,24},{24,28},{1,5},{5,9},{9,... | collective-permute-start | bytes 12296 | tf_op jit(solution)/shard_map/ppermute | solution.py:10
  63.5 0.2 convert_element_type.47
  63.7 12.1 %collective-permute-done.6 = bf16[1,48,48,128]{3,2,1,0:T(8,128)(2,1)S(1)} collective-permute-done((bf16[1,48,48,128]{3,2,1,0:T(8,128)(2,1)S(1)}, bf16[1,48,48,128]{3,2,1,0:T(8,128)(2,1)S(1)}, u32[]{:S(2)}, u32[]{:S(2)}) %collective-permute-start.6) | collective-permute-done | bytes 589856 | tf_op jit(solution)/shard_map/ppermute | solution.py:18
  75.8 1.3 collective-permute-start.9
  77.1 0.0 collective-permute-done.7
  77.1 0.4 maximum_convert_fusion.1
  77.5 0.9 fusion.18
  78.4 0.0 collective-permute-done.10
  78.4 0.0 collective-permute-done.11
  78.4 0.0 collective-permute-done.8
  78.5 3.3 %collective-permute-done.9 = f32[8,128]{1,0:T(8,128)S(1)} collective-permute-done((f32[8,128]{1,0:T(8,128)S(1)}, f32[8,128]{1,0:T(8,128)S(1)}, u32[]{:S(2)}, u32[]{:S(2)}) %collective-permute-start.9) | collective-permute-done | bytes 4128 | tf_op jit(solution)/shard_map/ppermute | solution.py:10
  81.8 0.0 copy-start.6
  81.8 0.0 copy-start.3
  81.8 3.2 %fusion.5 = bf16[4608,128]{1,0:T(8,128)(2,1)} fusion(f32[4608,128]{1,0:T(8,128)S(1)} %bitcast.32, bf16[4608,128]{1,0:T(8,128)(2,1)S(1)} %fusion.4, f32[4608]{0:T(1024)S(1)} %copy-done.4, f32[8,128]{1,0:T(8,128)S(1)} %collective-permute-done.11, f32[8,128]{1,0:T(8,128)S(1)} %collective-permute-done.10, f32[8,128]{1,0:T(8,128)S(1)} %collective-permute-done.9, ...), kind=kOutput, calls=%fused_computation.7 | convolution fusion | flops 14198784 | bytes 4831272 | tf_op jit(solution)/shard_map/dot_general | solution.py:45
  85.0 0.0 all-gather.2.cloned.1.call-update
  85.1 0.0 copy-done.6
  85.1 0.0 copy-done.3
  85.1 0.1 convert_multiply_fusion.2
  85.3 0.3 convolution_convert_fusion.1
  85.6 40.1 %all-gather.2.cloned.1.call-done = bf16[4608,512]{1,0:T(8,128)(2,1)} async-done(((bf16[4608,128]{1,0:T(8,128)(2,1)}), bf16[4608,512]{1,0:T(8,128)(2,1)}) %all-gather.2.cloned.1.call-update) | async-done | bytes 4718608 | tf_op jit(solution)/shard_map/all_gather | solution.py:75
  125.7 4.7 %convolution_convert_fusion = bf16[4608,128]{1,0:T(8,128)(2,1)} fusion(bf16[4608,512]{1,0:T(8,128)(2,1)} %all-gather.2.cloned.1.call-done, bf16[512,128]{1,0:T(8,128)(2,1)S(1)} %bitcast.35), kind=kOutput, calls=%fused_computation.8 | convolution fusion | flops 604569600 | bytes 6029312 | tf_op jit(solution)/shard_map/dot_general | solution.py:74
  (4 shorter events, 0.0 us)
Async XLA Ops:
  6.5 9.5 %copy-start = (bf16[2,48,48,128]{3,2,1,0:T(8,128)(2,1)S(1)}, bf16[2,48,48,128]{3,2,1,0:T(8,128)(2,1)}, u32[]{:S(2)}) copy-start(bf16[2,48,48,128]{3,2,1,0:T(8,128)(2,1)} %param.7) | copy-start | bytes 3538948
  6.5 9.4 %copy-start.7 = (s32[8]{0:T(128)S(1)}, s32[8]{0:T(128)}, u32[]{:S(2)}) copy-start(s32[8]{0:T(128)} %param.11) | copy-start | bytes 100
  6.5 9.4 %copy-start.2 = (bf16[8,2,48,48]{3,2,1,0:T(8,128)(2,1)S(1)}, bf16[8,2,48,48]{3,2,1,0:T(8,128)(2,1)}, u32[]{:S(2)}) copy-start(bf16[8,2,48,48]{3,2,1,0:T(8,128)(2,1)} %param.9) | copy-start | bytes 221188
  6.5 119.2 %all-gather.2.cloned.1.call-start = ((), (), s32[]{:S(2)}) async-start(), calls=%async_computation | async-start | bytes 5898240 | tf_op jit(solution)/shard_map/all_gather | solution.py:75
  9.0 30.5 %collective-permute-start = (bf16[1,48,48,128]{3,2,1,0:T(8,128)(2,1)}, bf16[1,48,48,128]{3,2,1,0:T(8,128)(2,1)}, u32[]{:S(2)}, u32[]{:S(2)}) collective-permute-start(bf16[1,48,48,128]{3,2,1,0:T(8,128)(2,1)} %get-tuple-element.9), channel_id=1, source_target_pairs={{0,4},{4,8},{8,12},{12,16},{16,20},{20,24},{24,28},{1,5},{5,9},{9,... | collective-permute-start | bytes 1769480 | tf_op jit(solution)/shard_map/ppermute | solution.py:18
  14.7 26.1 %collective-permute-start.1 = (bf16[1,48,48,128]{3,2,1,0:T(8,128)(2,1)}, bf16[1,48,48,128]{3,2,1,0:T(8,128)(2,1)}, u32[]{:S(2)}, u32[]{:S(2)}) collective-permute-start(bf16[1,48,48,128]{3,2,1,0:T(8,128)(2,1)} %get-tuple-element.10), channel_id=1, source_target_pairs={{4,0},{8,4},{12,8},{16,12},{20,16},{24,20},{28,24},{5,1},{9,5},{13... | collective-permute-start | bytes 1769480 | tf_op jit(solution)/shard_map/ppermute | solution.py:21
  16.7 28.9 %collective-permute-start.2 = (f32[8,128]{1,0:T(8,128)S(1)}, f32[8,128]{1,0:T(8,128)S(1)}, u32[]{:S(2)}, u32[]{:S(2)}) collective-permute-start(f32[8,128]{1,0:T(8,128)S(1)} %convolution_bitcast_fusion), channel_id=1, source_target_pairs={{0,4},{4,8},{8,12},{12,16},{16,20},{20,24},{24,28},{1,5},{5,9},{9,... | collective-permute-start | bytes 12296 | tf_op jit(solution)/shard_map/ppermute | solution.py:10
  21.2 24.3 %collective-permute-start.3 = (f32[8,128]{1,0:T(8,128)S(1)}, f32[8,128]{1,0:T(8,128)S(1)}, u32[]{:S(2)}, u32[]{:S(2)}) collective-permute-start(f32[8,128]{1,0:T(8,128)S(1)} %convolution_bitcast_fusion), channel_id=1, source_target_pairs={{4,0},{8,4},{12,8},{16,12},{20,16},{24,20},{28,24},{5,1},{9,5},{13... | collective-permute-start | bytes 12296 | tf_op jit(solution)/shard_map/ppermute | solution.py:10
  22.5 23.1 %collective-permute-start.4 = (f32[8,128]{1,0:T(8,128)S(1)}, f32[8,128]{1,0:T(8,128)}, u32[]{:S(2)}, u32[]{:S(2)}) collective-permute-start(f32[8,128]{1,0:T(8,128)S(1)} %convolution_bitcast_fusion), channel_id=1, source_target_pairs={{0,8},{4,12},{8,16},{12,20},{16,24},{20,28},{1,9},{5,13},{9,17},{1... | collective-permute-start | bytes 12296 | tf_op jit(solution)/shard_map/ppermute | solution.py:10
  39.5 6.1 %collective-permute-start.5 = (f32[8,128]{1,0:T(8,128)S(1)}, f32[8,128]{1,0:T(8,128)S(1)}, u32[]{:S(2)}, u32[]{:S(2)}) collective-permute-start(f32[8,128]{1,0:T(8,128)S(1)} %convolution_bitcast_fusion), channel_id=1, source_target_pairs={{8,0},{12,4},{16,8},{20,12},{24,16},{28,20},{9,1},{13,5},{17,9},{2... | collective-permute-start | bytes 12296 | tf_op jit(solution)/shard_map/ppermute | solution.py:10
  42.4 1.1 copy-start.4
  43.5 2.1 %copy-start.1 = (bf16[8,4608]{1,0:T(8,128)(2,1)S(1)}, bf16[8,4608]{1,0:T(8,128)(2,1)}, u32[]{:S(2)}) copy-start(bf16[8,4608]{1,0:T(8,128)(2,1)} %reshape.42) | copy-start | bytes 221188
  43.5 2.1 %copy-start.5 = (f32[8]{0:T(128)S(1)}, f32[8]{0:T(128)}, u32[]{:S(2)}) copy-start(f32[8]{0:T(128)} %param.10) | copy-start | bytes 100
  47.1 28.7 %collective-permute-start.6 = (bf16[1,48,48,128]{3,2,1,0:T(8,128)(2,1)S(1)}, bf16[1,48,48,128]{3,2,1,0:T(8,128)(2,1)S(1)}, u32[]{:S(2)}, u32[]{:S(2)}) collective-permute-start(bf16[1,48,48,128]{3,2,1,0:T(8,128)(2,1)S(1)} %bitcast.34), channel_id=1, source_target_pairs={{0,4},{4,8},{8,12},{12,16},{16,20},{20,24},{24,28},{1,5},{5,9},{9,... | collective-permute-start | bytes 1769480 | tf_op jit(solution)/shard_map/ppermute | solution.py:18
  51.5 25.6 %collective-permute-start.7 = (bf16[1,48,48,128]{3,2,1,0:T(8,128)(2,1)S(1)}, bf16[1,48,48,128]{3,2,1,0:T(8,128)(2,1)S(1)}, u32[]{:S(2)}, u32[]{:S(2)}) collective-permute-start(bf16[1,48,48,128]{3,2,1,0:T(8,128)(2,1)S(1)} %bitcast.33), channel_id=1, source_target_pairs={{4,0},{8,4},{12,8},{16,12},{20,16},{24,20},{28,24},{5,1},{9,5},{13... | collective-permute-start | bytes 1769480 | tf_op jit(solution)/shard_map/ppermute | solution.py:21
  53.2 25.3 %collective-permute-start.10 = (f32[8,128]{1,0:T(8,128)S(1)}, f32[8,128]{1,0:T(8,128)S(1)}, u32[]{:S(2)}, u32[]{:S(2)}) collective-permute-start(f32[8,128]{1,0:T(8,128)S(1)} %fusion.28), channel_id=1, source_target_pairs={{0,8},{4,12},{8,16},{12,20},{16,24},{20,28},{1,9},{5,13},{9,17},{1... | collective-permute-start | bytes 12296 | tf_op jit(solution)/shard_map/ppermute | solution.py:10
  58.7 19.7 %collective-permute-start.11 = (f32[8,128]{1,0:T(8,128)S(1)}, f32[8,128]{1,0:T(8,128)S(1)}, u32[]{:S(2)}, u32[]{:S(2)}) collective-permute-start(f32[8,128]{1,0:T(8,128)S(1)} %fusion.28), channel_id=1, source_target_pairs={{8,0},{12,4},{16,8},{20,12},{24,16},{28,20},{9,1},{13,5},{17,9},{2... | collective-permute-start | bytes 12296 | tf_op jit(solution)/shard_map/ppermute | solution.py:10
  60.0 18.4 %collective-permute-start.8 = (f32[8,128]{1,0:T(8,128)S(1)}, f32[8,128]{1,0:T(8,128)S(1)}, u32[]{:S(2)}, u32[]{:S(2)}) collective-permute-start(f32[8,128]{1,0:T(8,128)S(1)} %fusion.28), channel_id=1, source_target_pairs={{0,4},{4,8},{8,12},{12,16},{16,20},{20,24},{24,28},{1,5},{5,9},{9,... | collective-permute-start | bytes 12296 | tf_op jit(solution)/shard_map/ppermute | solution.py:10
  75.8 6.0 %collective-permute-start.9 = (f32[8,128]{1,0:T(8,128)S(1)}, f32[8,128]{1,0:T(8,128)S(1)}, u32[]{:S(2)}, u32[]{:S(2)}) collective-permute-start(f32[8,128]{1,0:T(8,128)S(1)} %fusion.28), channel_id=1, source_target_pairs={{4,0},{8,4},{12,8},{16,12},{20,16},{24,20},{28,24},{5,1},{9,5},{13... | collective-permute-start | bytes 12296 | tf_op jit(solution)/shard_map/ppermute | solution.py:10
  81.8 3.3 %copy-start.6 = (s32[12,2]{0,1:T(2,128)S(1)}, s32[12,2]{0,1:T(2,128)}, u32[]{:S(2)}) copy-start(s32[12,2]{0,1:T(2,128)} %param.12) | copy-start | bytes 292
  81.8 3.3 %copy-start.3 = (bf16[12,128,128]{2,1,0:T(8,128)(2,1)S(1)}, bf16[12,128,128]{2,1,0:T(8,128)(2,1)}, u32[]{:S(2)}) copy-start(bf16[12,128,128]{2,1,0:T(8,128)(2,1)} %param.13) | copy-start | bytes 1179652
Sparse Core Ops, SparseCore 0:
  85.2 40.5 all-gather.1
where the time goes:
time: 138 us; the launch traced here: 137 us
  waiting for transfers between devices  62.9 us (46%)
  starting transfers between devices  37.6 us (27%)
  between operations  13.7 us (10%)
  matrix products  10.6 us (8%)
  other arithmetic  6.56 us (5%)
  local copies, waits for them, and re-layouts  5.88 us (4%)
    all_gather x1, waiting for transfers between devices, shards(): lax.all_gather(second, 'orb', axis=1, tiled=True)  40.1 us
    ppermute x8, starting transfers between devices, passed_along(): return lax.ppermute(array, axis, pairs)  25 us
    ppermute x2, waiting for transfers between devices, with_halo(): lax.ppermute(lax.slice_in_dim(block, block.shape[dim] - width, None, axis...  19.4 us
    ppermute x2, starting transfers between devices, with_halo(): lax.ppermute(lax.slice_in_dim(block, block.shape[dim] - width, None, axis...  10.1 us
    dot_general x1, matrix products, shards(): jnp.dot(lax.all_gather(second, 'orb', axis=1, tiled=True), column_q, pref...  4.73 us
    dot_general x2, matrix products, apply_filter(): lax.dot_general(beta_m, coef, (((0,), (0,)), ((), ())), preferred_element...  4.63 us
    ppermute x8, waiting for transfers between devices, passed_along(): return lax.ppermute(array, axis, pairs)  3.36 us
  transfers between devices with their start and end apart: 13, of which 4 were waited for; matrix products, arithmetic and copies ran while one was open for 8% of the time, Pallas kernels for 0%

commit v1 on v0

v1 whole, which is shorter than its diff:
```python
import functools

import jax
import jax.numpy as jnp
from jax import lax
from jax.experimental import pallas as pl
from jax.experimental.pallas import tpu as pltpu
from jax.sharding import PartitionSpec as P

F32 = jnp.float32
BF16 = jnp.bfloat16
VMEM_LIMIT = 50 * 1024 * 1024


def params():
    return pltpu.CompilerParams(vmem_limit_bytes=VMEM_LIMIT)


def cost(flops, moved):
    return pl.CostEstimate(flops=flops, bytes_accessed=moved, transcendentals=0)


def inside(w, window):
    return jnp.logical_and(w >= 0, w < window).astype(F32)


def tridiagonal(n):
    i = lax.broadcasted_iota(jnp.int32, (n, n), 0)
    j = lax.broadcasted_iota(jnp.int32, (n, n), 1)
    return jnp.where(jnp.abs(i - j) == 1, -0.125, 0.0).astype(BF16)


def partial_kernel(count, own, xr, f_own, f_x, f_zo, f_zf, out, acc, gram):
    x = lax.rem(lax.axis_index("space"), 2)
    half = own.shape[1] // 2
    window = xr.shape[1]
    width = own.shape[2]
    depth = f_own.shape[2]
    base = (half - 2) * x
    tri = tridiagonal(width)
    acc[...] = jnp.zeros_like(acc)
    gram[...] = jnp.zeros_like(gram)

    def field(c, w):
        if c == 1:
            return f_zf[0, w]
        if c == 6:
            return f_zo[0, w]
        plane = (c % 2) ^ x
        if c in (2, 3):
            return f_own[plane, base + w]
        return f_x[plane, w]

    def values(c, w):
        plane = (c % 2) ^ x
        return own[plane, base + w] if c in (2, 3) else xr[plane, w]

    def row(j, carry):
        w = 2 * x + j
        below, above = jnp.maximum(w - 1, 0), jnp.minimum(w + 1, window - 1)
        has_below, has_above = inside(w - 1, window), inside(w + 1, window)
        total, square = acc[...], gram[...]
        for c in (2, 3, 4, 5):
            b = field(c, w)
            b32 = b.astype(F32)
            beside = (
                field(c, below).astype(F32) * has_below
                + field(c, above).astype(F32) * has_above
                + field(c - 1, w).astype(F32)
                + field(c + 1, w).astype(F32)
            )
            u = b32[count : count + 1] + b32[count + 1 : count + 2]
            local = jnp.dot(b, tri, preferred_element_type=F32) - 0.125 * beside + u * b32
            hi = local.astype(BF16)
            lo = (local - hi.astype(F32)).astype(BF16)
            weights = jnp.concatenate([b, hi, lo], axis=0)
            total = total + jnp.dot(weights, values(c, w), preferred_element_type=F32)
            square = square + lax.dot_general(
                b, b, (((1,), (1,)), ((), ())), preferred_element_type=F32
            )
        acc[...] = total
        gram[...] = square
        return carry

    lax.fori_loop(0, half, row, 0)
    out[...] = jnp.zeros_like(out)
    out[0:count] = acc[0:count]
    out[count : 2 * count] = acc[depth : depth + count] + acc[2 * depth : 2 * depth + count]
    out[2 * count : 3 * count, 0:count] = gram[0:count, 0:count]


def partials(count, own, xr, f_own, f_x, f_zo, f_zf):
    orbs = own.shape[3]
    depth = f_own.shape[2]
    cells = 4 * (own.shape[1] // 2) * own.shape[2]
    return pl.pallas_call(
        functools.partial(partial_kernel, count),
        out_shape=jax.ShapeDtypeStruct((3 * count, orbs), F32),
        in_specs=[pl.BlockSpec(memory_space=pltpu.VMEM)] * 6,
        out_specs=pl.BlockSpec(memory_space=pltpu.VMEM),
        scratch_shapes=[pltpu.VMEM((3 * depth, orbs), F32), pltpu.VMEM((depth, depth), F32)],
        compiler_params=params(),
        cost_estimate=cost(2 * cells * 3 * depth * orbs, cells * orbs * 4),
        name="partials",
    )(own, xr, f_own, f_x, f_zo, f_zf)


def filter_kernel(count, slabs, start, own, xr, zo, zf, f_own, f_x, f_zo, f_zf, sums, strength, o_x, o_own, first):
    place = lax.axis_index("space")
    x = lax.rem(place, 2)
    half = own.shape[1] // 2
    window = xr.shape[1]
    width = own.shape[2]
    orbs = own.shape[3]
    depth = f_own.shape[2]
    rows = o_own.shape[1]
    base = (half - 2) * x
    lower = (place >= 2).astype(F32)
    upper = (place < slabs - 2).astype(F32)
    is_odd = x.astype(F32)
    has_zf = lower * (1.0 - is_odd) + upper * is_odd
    has_zo = upper * (1.0 - is_odd) + lower * is_odd

    coef1 = (strength[...] * sums[0:count]).astype(BF16).astype(F32) * 0.25
    gram = sums[2 * count : 3 * count]
    padded = coef1
    if orbs > count:
        padded = jnp.concatenate([coef1, jnp.zeros((orbs - count, orbs), F32)], axis=0)
    proj2 = sums[count : 2 * count] + jnp.dot(
        gram, padded, preferred_element_type=F32, precision=lax.Precision.HIGHEST
    )
    coef2 = (strength[...] * proj2).astype(BF16).astype(F32) * 0.25
    k = lax.broadcasted_iota(jnp.int32, (depth, orbs), 0)
    ones = jnp.where(jnp.logical_or(k == count, k == count + 1), 1.0, 0.0)

    def right(coef):
        rest = jnp.zeros((depth - count, orbs), F32)
        return jnp.concatenate([jnp.concatenate([coef, rest], axis=0), ones], axis=1).astype(BF16)

    right1, right2 = right(coef1), right(coef2)
    line = lax.broadcasted_iota(jnp.int32, (width, orbs), 0)
    not_first = (line > 0).astype(F32)
    not_last = (line < width - 1).astype(F32)

    def field(c, w):
        if c == 1:
            return f_zf[0, w]
        if c == 6:
            return f_zo[0, w]
        plane = (c % 2) ^ x
        if c in (2, 3):
            return f_own[plane, base + w]
        return f_x[plane, w]

    def values(c, w):
        plane = (c % 2) ^ x
        if c in (2, 3):
            return own[plane, base + w].astype(F32)
        ref = {0: zf, 1: xr, 2: zo}[0 if c < 2 else (1 if c < 6 else 2)]
        return ref[plane, w].astype(F32)

    def applied(v, xs, zs, fields, right_side):
        along = pltpu.roll(v, 1, 0) * not_first + pltpu.roll(v, width - 1, 0) * not_last
        both = lax.dot_general(
            fields, right_side, (((0,), (0,)), ((), ())), preferred_element_type=F32
        )
        return both[:, :orbs] + both[:, orbs:] * v - 0.125 * (along + xs + zs)

    def step1(j, carry):
        w = start + 2 * x + j - 1
        here = jnp.clip(w, 0, window - 1)
        below, above = jnp.maximum(here - 1, 0), jnp.minimum(here + 1, window - 1)
        has_below, has_above = inside(w - 1, window), inside(w + 1, window)
        valid = inside(w, window)
        vs = [values(c, here) for c in range(8)]
        for c in range(1, 7):
            xs = values(c, below) * has_below + values(c, above) * has_above
            f = applied(vs[c], xs, vs[c - 1] + vs[c + 1], field(c, here), right1)
            keep = valid
            if c == 1:
                keep = valid * has_zf
            if c == 6:
                keep = valid * has_zo
            first[c - 1, j] = (f * keep).astype(BF16)
        return carry

    lax.fori_loop(0, rows + 2, step1, 0)

    def step2(j, carry):
        w = start + 2 * x + j
        vs = [first[c - 1, j + 1].astype(F32) for c in range(1, 7)]
        for c in range(2, 6):
            xs = first[c - 1, j].astype(F32) + first[c - 1, j + 2].astype(F32)
            f = applied(vs[c - 1], xs, vs[c - 2] + vs[c], field(c, w), right2)
            out = o_own if c in (2, 3) else o_x
            out[(c % 2) ^ x, j] = f.astype(BF16)
        return carry

    lax.fori_loop(0, rows, step2, 0)


def filtered(count, slabs, start, rows, *operands):
    own = operands[0]
    planes, _, width, orbs = own.shape
    out = jax.ShapeDtypeStruct((planes, rows, width, orbs), BF16)
    cells = 10 * rows * width
    return pl.pallas_call(
        functools.partial(filter_kernel, count, slabs, start),
        out_shape=(out, out),
        in_specs=[pl.BlockSpec(memory_space=pltpu.VMEM)] * len(operands),
        out_specs=(pl.BlockSpec(memory_space=pltpu.VMEM),) * 2,
        scratch_shapes=[pltpu.VMEM((6, rows + 2, width, orbs), BF16)],
        compiler_params=params(),
        cost_estimate=cost(2 * cells * 32 * orbs, cells * orbs * 4),
        name="filtered",
    )(*operands)


def rotate_kernel(a, b, c, d, q, out):
    planes, rows, width, orbs = a.shape

    def one(j, carry):
        for plane in range(planes):
            total = jnp.dot(a[plane, j], q[0], preferred_element_type=F32)
            for k, ref in ((1, b), (2, c), (3, d)):
                total = total + jnp.dot(ref[plane, j], q[k], preferred_element_type=F32)
            out[plane, j] = total.astype(BF16)
        return carry

    lax.fori_loop(0, rows, one, 0)


def rotated(blocks, q):
    a = blocks[0]
    size = a.size
    return pl.pallas_call(
        rotate_kernel,
        out_shape=jax.ShapeDtypeStruct(a.shape, BF16),
        in_specs=[pl.BlockSpec(memory_space=pltpu.VMEM)] * 5,
        out_specs=pl.BlockSpec(memory_space=pltpu.VMEM),
        compiler_params=params(),
        cost_estimate=cost(8 * size * a.shape[3], 10 * size),
        name="rotated",
    )(*blocks, q)


def assemble_kernel(half, *refs):
    out = refs[-1]
    pieces = (len(refs) - 1) // 2
    x = lax.rem(lax.axis_index("space"), 2)
    rows = refs[0].shape[1]
    for k in range(pieces):
        out[:, pl.ds(half * x + rows * k, rows)] = refs[k][...]
        out[:, pl.ds(half * (1 - x) + rows * k, rows)] = refs[pieces + k][...]


def assembled(shape, mine, theirs):
    return pl.pallas_call(
        functools.partial(assemble_kernel, shape[1] // 2),
        out_shape=jax.ShapeDtypeStruct(shape, BF16),
        in_specs=[pl.BlockSpec(memory_space=pltpu.VMEM)] * (len(mine) + len(theirs)),
        out_specs=pl.BlockSpec(memory_space=pltpu.VMEM),
        compiler_params=params(),
        name="assembled",
    )(*mine, *theirs)


def shards(psi, potential, beta, strength, atom_slab, pattern, q_tiles):
    planes, width_x, width_y, orbs = psi.shape
    count = beta.shape[0]
    slabs = lax.axis_size("space")
    place = lax.axis_index("space")
    x = lax.rem(place, 2)
    half = width_x // 2
    window = half + 2
    swap = [(i, i ^ 1) for i in range(slabs)]
    own_way = [(i, i + 2 if i % 2 else i - 2) for i in range(slabs)]
    own_way = [(i, j) for i, j in own_way if 0 <= j < slabs]
    other_way = [(i, i - 2 if i % 2 else i + 2) for i in range(slabs)]
    other_way = [(i, j) for i, j in other_way if 0 <= j < slabs]
    groups = lax.axis_size("orb")
    across = [(i, i ^ 2) for i in range(groups)]
    beside = [(i, i ^ 1) for i in range(groups)]

    mine = (half - 2) * x
    theirs = (half - 2) * (1 - x)
    to_x = lax.dynamic_slice_in_dim(psi, theirs, window, axis=1)
    xr = lax.ppermute(to_x, "space", swap)
    zo = lax.ppermute(lax.dynamic_slice_in_dim(psi, mine, window, axis=1), "space", own_way)
    zf = lax.ppermute(xr, "space", other_way)

    active = jnp.abs(place - atom_slab) <= 1
    beta_m = jnp.where(active[:, None, None, None], beta, jnp.zeros_like(beta))
    depth = -(-(count + 2) // 16) * 16
    u = (potential - 1.0) * 0.25
    hi = lax.reduce_precision(u, 8, 7)
    lo = u - hi
    fields = jnp.concatenate(
        [
            jnp.transpose(beta_m, (1, 2, 0, 3)),
            hi[:, :, None, :].astype(BF16),
            lo[:, :, None, :].astype(BF16),
            jnp.zeros((planes, width_x, depth - count - 2, width_y), BF16),
        ],
        axis=2,
    )
    f_x = lax.ppermute(lax.dynamic_slice_in_dim(fields, theirs, window, axis=1), "space", swap)
    near = lax.dynamic_slice_in_dim(fields, x, 1, axis=0)
    f_zo = lax.ppermute(lax.dynamic_slice_in_dim(near, mine, window, axis=1), "space", own_way)
    f_zf = lax.ppermute(lax.dynamic_slice_in_dim(f_x, 1 - x, 1, axis=0), "space", other_way)

    sums = partials(count, psi, xr, fields, f_x, f_zo, f_zf)
    step = 1
    while step < slabs:
        sums = sums + lax.ppermute(sums, "space", [(i, i ^ step) for i in range(slabs)])
        step *= 2
    strong = jnp.broadcast_to(strength[:, None], (count, orbs))

    me = lax.axis_index("orb")
    which = jnp.bitwise_xor(me, jnp.arange(groups, dtype=jnp.int32))
    rows_hot = (pattern[:, 0][:, None] == which[None, :]).astype(BF16)
    rows_hot = rows_hot * (pattern[:, 1] == me).astype(BF16)[:, None]
    q = jnp.einsum("ki,kab->iab", rows_hot, q_tiles, preferred_element_type=F32).astype(BF16)

    pieces = 2
    rows = half // pieces
    kept, given = [], []
    for piece in range(pieces):
        for_x, for_me = filtered(
            count, slabs, piece * rows, rows, psi, xr, zo, zf, fields, f_x, f_zo, f_zf, sums, strong
        )
        for block, to in ((for_x, given), (for_me, kept)):
            c = lax.ppermute(block, "orb", beside)
            y = lax.ppermute(block, "orb", across)
            yc = lax.ppermute(y, "orb", beside)
            to.append(rotated((block, c, y, yc), q))
    got = [lax.ppermute(block, "space", swap) for block in given]
    return assembled(psi.shape, kept, got)


def solution(mesh):
    placed = (
        P("space", None, None, "orb"),
        P("space", None, None),
        P(None, "space", None, None),
        P(),
        P(),
        P(),
        P(),
    )
    return jax.shard_map(
        shards, mesh=mesh, in_specs=placed, out_specs=P("space", None, None, "orb"), check_vma=False
    )
```

time: 138 us -> 114 us (0.83)
  Pallas kernels: 0 us -> 36.2 us
  waiting for transfers between devices: 62.9 us -> 41.5 us
  between operations: 13.7 us -> 0.21 us
  matrix products: 10.6 us -> 0.34 us
  starting transfers between devices: 37.6 us -> 30.7 us
  other arithmetic: 6.56 us -> 0.41 us
  local copies, waits for them, and re-layouts: 5.88 us -> 3.9 us
    all_gather x1 -> x0, waiting for transfers between devices: 40.1 us -> none  [shards(): lax.all_gather(second, 'orb', axis=1, tiled=True)]
    pallas_call x0 -> x8, Pallas kernels: none -> 36.2 us  [the longest x2 15.8 us: filtered(): pl.pallas_call(functools.partial(filter_kernel, count, slabs, start), out...]
    ppermute x12 -> x23, waiting for transfers between devices: 22.8 us -> 41.5 us  [the longest x1 13.8 us: shards(): xr = lax.ppermute(to_x, 'space', swap)]
    dot_general x6 -> x1, matrix products: 10.6 us -> 0.34 us  [shards(): jnp.einsum('ki,kab->iab', rows_hot, q_tiles, preferred_element_type=F32)]
    ppermute x12 -> x23, starting transfers between devices: 37.6 us -> 30.7 us  [the longest x3 7.54 us: shards(): lax.ppermute(sums, 'space', [(i, i ^ step) for i in range(slabs)])]
    dynamic_slice x0 -> x4, local copies, waits for them, and re-layouts: none -> 3.62 us  [the longest x1 2.26 us: shards(): lax.dynamic_slice_in_dim(psi, mine, window, axis=1)]
    slice x2 -> x0, local copies, waits for them, and re-layouts: 2.54 us -> none  [with_halo(): lax.slice_in_dim(block, block.shape[dim] - width, None, axis=dim)]
    convert_element_type x4 -> x1, other arithmetic: 2.31 us -> 0.01 us  [shards(): hi[:, :, None, :].astype(BF16)]
  transfers between devices with their start and end apart: 13 -> 23, of which waited for: 4 -> 10; matrix products, arithmetic and copies ran while one was open for 8% -> 2% of each run, Pallas kernels for 0% -> 24%
where the time goes in v1:
time: 114 us; the launch traced here: 113 us
  waiting for transfers between devices  41.5 us (36%)
  Pallas kernels  36.2 us (32%)
  starting transfers between devices  30.7 us (27%)
  local copies, waits for them, and re-layouts  3.9 us (3%)
    pallas_call x2, Pallas kernels, filtered(): pl.pallas_call(functools.partial(filter_kernel, count, slabs, start), out...  15.8 us
    ppermute x1, waiting for transfers between devices, shards(): xr = lax.ppermute(to_x, 'space', swap)  13.8 us
    pallas_call x4, Pallas kernels, rotated(): pl.pallas_call(rotate_kernel, out_shape=jax.ShapeDtypeStruct(a.shape, BF1...  11.5 us
    ppermute x4, waiting for transfers between devices, shards(): y = lax.ppermute(block, 'orb', across)  8.53 us
    pallas_call x1, Pallas kernels, partials(): pl.pallas_call(functools.partial(partial_kernel, count), out_shape=jax.Sh...  7.86 us
    ppermute x3, starting transfers between devices, shards(): lax.ppermute(sums, 'space', [(i, i ^ step) for i in range(slabs)])  7.54 us
    ppermute x2, waiting for transfers between devices, shards(): got = [lax.ppermute(block, 'space', swap) for block in given]  5.45 us
    ppermute x1, starting transfers between devices, shards(): xr = lax.ppermute(to_x, 'space', swap)  5.24 us
  transfers between devices with their start and end apart: 23, of which 10 were waited for; matrix products, arithmetic and copies ran while one was open for 2% of the time, Pallas kernels for 24%

profile of v1, /device:TPU:0, one launch (start us, length us, event | category | flops | bytes accessed | tf_op | source)
XLA Modules:
  0.0 113.2 jit_solution(17219903904215884910)
XLA Ops:
  0.0 2.3 %constant_dynamic-slice_fusion.3 = (bf16[2,26,48,128]{3,2,1,0:T(8,128)(2,1)}, bf16[2,26,48,128]{3,2,1,0:T(8,128)(2,1)S(1)}) fusion(bf16[2,48,48,128]{3,2,1,0:T(8,128)(2,1)} %own.5, s32[]{:T(128)S(6)} %select_n.23, s32[]{:T(128)S(6)} %select_n.22), kind=kLoop, calls=%fused_computation.17 | loop fusion | bytes 2555912 | tf_op jit(solution)/shard_map/dynamic_slice | solution.py:289
  2.3 1.4 %collective-permute-start.1 = (bf16[2,26,48,128]{3,2,1,0:T(8,128)(2,1)}, bf16[2,26,48,128]{3,2,1,0:T(8,128)(2,1)S(1)}, u32[]{:S(2)}, u32[]{:S(2)}) collective-permute-start(bf16[2,26,48,128]{3,2,1,0:T(8,128)(2,1)} %get-tuple-element.13), channel_id=1, source_target_pairs={{4,12},{8,0},{12,20},{16,8},{20,28},{24,16},{5,13},{9,1},{13,21},{... | collective-permute-start | bytes 1916936 | tf_op jit(solution)/shard_map/ppermute | solution.py:289
  3.7 5.2 %collective-permute-start = (bf16[2,26,48,128]{3,2,1,0:T(8,128)(2,1)S(1)}, bf16[2,26,48,128]{3,2,1,0:T(8,128)(2,1)S(1)}, u32[]{:S(2)}, u32[]{:S(2)}) collective-permute-start(bf16[2,26,48,128]{3,2,1,0:T(8,128)(2,1)S(1)} %get-tuple-element.14), channel_id=1, source_target_pairs={{0,4},{4,0},{8,12},{12,8},{16,20},{20,16},{24,28},{28,24},{1,5},{5... | collective-permute-start | bytes 1916936 | tf_op jit(solution)/shard_map/ppermute | solution.py:288
  8.9 0.0 copy-done.3
  9.1 0.1 pad.3.clone
  9.2 0.1 fusion.2
  9.2 13.8 %collective-permute-done.xr = bf16[2,26,48,128]{3,2,1,0:T(8,128)(2,1)S(1)} collective-permute-done((bf16[2,26,48,128]{3,2,1,0:T(8,128)(2,1)S(1)}, bf16[2,26,48,128]{3,2,1,0:T(8,128)(2,1)S(1)}, u32[]{:S(2)}, u32[]{:S(2)}) %collective-permute-start) | collective-permute-done | bytes 639008 | tf_op jit(solution)/shard_map/ppermute | solution.py:288
  23.0 4.3 %collective-permute-start.2 = (bf16[2,26,48,128]{3,2,1,0:T(8,128)(2,1)S(1)}, bf16[2,26,48,128]{3,2,1,0:T(8,128)(2,1)}, u32[]{:S(2)}, u32[]{:S(2)}) collective-permute-start(bf16[2,26,48,128]{3,2,1,0:T(8,128)(2,1)S(1)} %collective-permute-done.xr), channel_id=1, source_target_pairs={{0,8},{8,16},{12,4},{16,24},{20,12},{28,20},{1,9},{9,17},{13,5},{1... | collective-permute-start | bytes 1916936 | tf_op jit(solution)/shard_map/ppermute | solution.py:290
  27.3 0.3 maximum_maximum_fusion.f_own
  27.6 0.7 constant_dynamic-slice_fusion.2
  28.3 0.0 collective-permute-start.3
  28.3 0.7 constant_dynamic-slice_fusion.1
  29.0 1.3 %collective-permute-start.4 = (bf16[1,26,16,48]{3,2,1,0:T(8,128)(2,1)}, bf16[1,26,16,48]{3,2,1,0:T(8,128)(2,1)}, u32[]{:S(2)}, u32[]{:S(2)}) collective-permute-start(bf16[1,26,16,48]{3,2,1,0:T(8,128)(2,1)} %constant_dynamic-slice_fusion.1), channel_id=1, source_target_pairs={{4,12},{8,0},{12,20},{16,8},{20,28},{24,16},{5,13},{9,1},{13,21},{... | collective-permute-start | bytes 119816 | tf_op jit(solution)/shard_map/ppermute | solution.py:309
  30.2 4.1 %collective-permute-done.3.f_x = bf16[2,26,16,48]{3,2,1,0:T(8,128)(2,1)S(1)} collective-permute-done((bf16[2,26,16,48]{3,2,1,0:T(8,128)(2,1)}, bf16[2,26,16,48]{3,2,1,0:T(8,128)(2,1)S(1)}, u32[]{:S(2)}, u32[]{:S(2)}) %collective-permute-start.3) | collective-permute-done | bytes 79904 | tf_op jit(solution)/shard_map/ppermute | solution.py:307
  34.4 0.0 copy-start.4
  34.4 2.7 %collective-permute-start.5 = (bf16[1,26,16,48]{3,2,1,0:T(8,128)(2,1)S(1)}, bf16[1,26,16,48]{3,2,1,0:T(8,128)(2,1)S(1)}, u32[]{:S(2)}, u32[]{:S(2)}) collective-permute-start(bf16[1,26,16,48]{3,2,1,0:T(8,128)(2,1)S(1)} %constant_dynamic-slice_fusion), channel_id=1, source_target_pairs={{0,8},{8,16},{12,4},{16,24},{20,12},{28,20},{1,9},{9,17},{13,5},{1... | collective-permute-start | bytes 119816 | tf_op jit(solution)/shard_map/ppermute | solution.py:310
  37.0 0.0 collective-permute-done.4.f_zo
  37.0 4.5 %collective-permute-done.5.f_zf = bf16[1,26,16,48]{3,2,1,0:T(8,128)(2,1)S(1)} collective-permute-done((bf16[1,26,16,48]{3,2,1,0:T(8,128)(2,1)S(1)}, bf16[1,26,16,48]{3,2,1,0:T(8,128)(2,1)S(1)}, u32[]{:S(2)}, u32[]{:S(2)}) %collective-permute-start.5) | collective-permute-done | bytes 39968 | tf_op jit(solution)/shard_map/ppermute | solution.py:310
  41.5 7.9 %partials.1 = f32[24,128]{1,0:T(8,128)S(1)} custom-call(bf16[2,48,48,128]{3,2,1,0:T(8,128)(2,1)S(1)} %copy-done.1, bf16[2,26,48,128]{3,2,1,0:T(8,128)(2,1)S(1)} %collective-permute-done.xr, bf16[2,48,16,48]{3,2,1,0:T(8,128)(2,1)S(1)} %maximum_maximum_fusion.f_own, bf16[2,26,16,48]{3,2,1,0:T(8,128)(2,1)S(1)} %collective-permute-done.3.f_x, ...), custom_call_target="tpu_custom_call" | custom-call | flops 56623104 | bytes 2359296 | tf_op jit(solution)/shard_map/partials/pallas_call | solution.py:96
  49.4 2.4 %collective-permute-start.6 = (f32[24,128]{1,0:T(8,128)S(1)}, f32[24,128]{1,0:T(8,128)S(1)}, u32[]{:S(2)}, u32[]{:S(2)}) collective-permute-start(f32[24,128]{1,0:T(8,128)S(1)} %partials.1), channel_id=1, source_target_pairs={{0,4},{4,0},{8,12},{12,8},{16,20},{20,16},{24,28},{28,24},{1,5},{5... | collective-permute-start | bytes 36872 | tf_op jit(solution)/shard_map/ppermute | solution.py:315
  51.8 1.7 %collective-permute-done.6 = f32[24,128]{1,0:T(8,128)S(1)} collective-permute-done((f32[24,128]{1,0:T(8,128)S(1)}, f32[24,128]{1,0:T(8,128)S(1)}, u32[]{:S(2)}, u32[]{:S(2)}) %collective-permute-start.6) | collective-permute-done | bytes 12320 | tf_op jit(solution)/shard_map/ppermute | solution.py:315
  53.5 2.1 %collective-permute-start.7 = (f32[24,128]{1,0:T(8,128)S(1)}, f32[24,128]{1,0:T(8,128)S(1)}, u32[]{:S(2)}, u32[]{:S(2)}) collective-permute-start(f32[24,128]{1,0:T(8,128)S(1)} %add.33), channel_id=1, source_target_pairs={{0,8},{4,12},{8,0},{12,4},{16,24},{20,28},{24,16},{28,20},{1,9},{5... | collective-permute-start | bytes 36872 | tf_op jit(solution)/shard_map/ppermute | solution.py:315
  55.6 1.7 %collective-permute-done.7 = f32[24,128]{1,0:T(8,128)S(1)} collective-permute-done((f32[24,128]{1,0:T(8,128)S(1)}, f32[24,128]{1,0:T(8,128)S(1)}, u32[]{:S(2)}, u32[]{:S(2)}) %collective-permute-start.7) | collective-permute-done | bytes 12320 | tf_op jit(solution)/shard_map/ppermute | solution.py:315
  57.4 3.0 %collective-permute-start.8 = (f32[24,128]{1,0:T(8,128)S(1)}, f32[24,128]{1,0:T(8,128)S(1)}, u32[]{:S(2)}, u32[]{:S(2)}) collective-permute-start(f32[24,128]{1,0:T(8,128)S(1)} %add.34), channel_id=1, source_target_pairs={{0,16},{4,20},{8,24},{12,28},{16,0},{20,4},{24,8},{28,12},{1,17},{... | collective-permute-start | bytes 36872 | tf_op jit(solution)/shard_map/ppermute | solution.py:315
  60.3 1.7 %collective-permute-done.8 = f32[24,128]{1,0:T(8,128)S(1)} collective-permute-done((f32[24,128]{1,0:T(8,128)S(1)}, f32[24,128]{1,0:T(8,128)S(1)}, u32[]{:S(2)}, u32[]{:S(2)}) %collective-permute-start.8) | collective-permute-done | bytes 12320 | tf_op jit(solution)/shard_map/ppermute | solution.py:315
  62.0 0.0 collective-permute-done.1.zo
  62.0 0.0 collective-permute-done.2.zf
  62.0 0.1 broadcast_in_dim.28.strength
  62.1 8.2 %filtered.3 = (bf16[2,12,48,128]{3,2,1,0:T(8,128)(2,1)}, bf16[2,12,48,128]{3,2,1,0:T(8,128)(2,1)S(1)}) custom-call(bf16[2,48,48,128]{3,2,1,0:T(8,128)(2,1)} %own.5, bf16[2,26,48,128]{3,2,1,0:T(8,128)(2,1)S(1)} %collective-permute-done.xr, bf16[2,26,48,128]{3,2,1,0:T(8,128)(2,1)S(1)} %collective-permute-done.1.zo, ...), custom_call_target="tpu_custom_call" | custom-call | flops 47185920 | bytes 2949120 | tf_op jit(solution)/shard_map/filtered/pallas_call | solution.py:207
  70.3 1.5 %collective-permute-start.20 = (bf16[2,12,48,128]{3,2,1,0:T(8,128)(2,1)}, bf16[2,12,48,128]{3,2,1,0:T(8,128)(2,1)}, u32[]{:S(2)}, u32[]{:S(2)}) collective-permute-start(bf16[2,12,48,128]{3,2,1,0:T(8,128)(2,1)} %get-tuple-element.12.a), channel_id=1, source_target_pairs={{0,2},{1,3},{2,0},{3,1},{4,6},{5,7},{6,4},{7,5},{8,10},{9,11},{10,... | collective-permute-start | bytes 884744 | tf_op jit(solution)/shard_map/ppermute | solution.py:334
  71.9 0.0 collective-permute-start.19
  71.9 0.5 collective-permute-start.13
  72.4 7.5 %filtered.2 = (bf16[2,12,48,128]{3,2,1,0:T(8,128)(2,1)S(1)}, bf16[2,12,48,128]{3,2,1,0:T(8,128)(2,1)S(1)}) custom-call(bf16[2,48,48,128]{3,2,1,0:T(8,128)(2,1)} %own.5, bf16[2,26,48,128]{3,2,1,0:T(8,128)(2,1)S(1)} %collective-permute-done.xr, bf16[2,26,48,128]{3,2,1,0:T(8,128)(2,1)S(1)} %collective-permute-done.1.zo, ...), custom_call_target="tpu_custom_call" | custom-call | flops 47185920 | bytes 2949120 | tf_op jit(solution)/shard_map/filtered/pallas_call | solution.py:207
  79.9 1.6 %collective-permute-start.16 = (bf16[2,12,48,128]{3,2,1,0:T(8,128)(2,1)S(1)}, bf16[2,12,48,128]{3,2,1,0:T(8,128)(2,1)S(1)}, u32[]{:S(2)}, u32[]{:S(2)}) collective-permute-start(bf16[2,12,48,128]{3,2,1,0:T(8,128)(2,1)S(1)} %get-tuple-element.11.a), channel_id=1, source_target_pairs={{0,2},{1,3},{2,0},{3,1},{4,6},{5,7},{6,4},{7,5},{8,10},{9,11},{10,... | collective-permute-start | bytes 884744 | tf_op jit(solution)/shard_map/ppermute | solution.py:334
  81.5 0.1 collective-permute-start.12
  81.6 2.7 %collective-permute-done.13.c = bf16[2,12,48,128]{3,2,1,0:T(8,128)(2,1)S(1)} collective-permute-done((bf16[2,12,48,128]{3,2,1,0:T(8,128)(2,1)S(1)}, bf16[2,12,48,128]{3,2,1,0:T(8,128)(2,1)S(1)}, u32[]{:S(2)}, u32[]{:S(2)}) %collective-permute-start.13) | collective-permute-done | bytes 294944 | tf_op jit(solution)/shard_map/ppermute | solution.py:334
  84.3 0.0 collective-permute-start.15
  84.3 0.0 collective-permute-done.20.c
  84.3 1.2 %collective-permute-start.10 = (bf16[2,12,48,128]{3,2,1,0:T(8,128)(2,1)S(1)}, bf16[2,12,48,128]{3,2,1,0:T(8,128)(2,1)S(1)}, u32[]{:S(2)}, u32[]{:S(2)}) collective-permute-start(bf16[2,12,48,128]{3,2,1,0:T(8,128)(2,1)S(1)} %get-tuple-element.9.a), channel_id=1, source_target_pairs={{0,2},{1,3},{2,0},{3,1},{4,6},{5,7},{6,4},{7,5},{8,10},{9,11},{10,... | collective-permute-start | bytes 884744 | tf_op jit(solution)/shard_map/ppermute | solution.py:334
  85.5 0.0 collective-permute-done.19.b
  85.5 0.2 collective-permute-start.21
  85.8 4.9 %collective-permute-done.16.c = bf16[2,12,48,128]{3,2,1,0:T(8,128)(2,1)S(1)} collective-permute-done((bf16[2,12,48,128]{3,2,1,0:T(8,128)(2,1)S(1)}, bf16[2,12,48,128]{3,2,1,0:T(8,128)(2,1)S(1)}, u32[]{:S(2)}, u32[]{:S(2)}) %collective-permute-start.16) | collective-permute-done | bytes 294944 | tf_op jit(solution)/shard_map/ppermute | solution.py:334
  90.6 0.0 collective-permute-start.17
  90.7 0.3 fusion
  91.0 0.0 collective-permute-done.21.d
  91.0 0.6 collective-permute-start.14
  91.6 3.7 %rotated.7 = bf16[2,12,48,128]{3,2,1,0:T(8,128)(2,1)S(1)} custom-call(bf16[2,12,48,128]{3,2,1,0:T(8,128)(2,1)} %get-tuple-element.12.a, bf16[2,12,48,128]{3,2,1,0:T(8,128)(2,1)} %collective-permute-done.19.b, bf16[2,12,48,128]{3,2,1,0:T(8,128)(2,1)} %collective-permute-done.20.c, bf16[2,12,48,128]{3,2,1,0:T(8,128)(2,1)S(1)} %collective-permute-done.21.d, ...), custom_call_target="tpu_custom_call" | custom-call | flops 150994944 | bytes 1474560 | tf_op jit(solution)/shard_map/rotated/pallas_call | solution.py:236
  95.3 0.9 collective-permute-done.10.c
  96.2 0.0 collective-permute-start.9
  96.2 0.0 collective-permute-done.15.b
  96.2 0.5 collective-permute-start.11
  96.8 0.0 collective-permute-done.17.d
  96.8 1.8 %collective-permute-start.22 = (bf16[2,12,48,128]{3,2,1,0:T(8,128)(2,1)S(1)}, bf16[2,12,48,128]{3,2,1,0:T(8,128)(2,1)S(1)}, u32[]{:S(2)}, u32[]{:S(2)}) collective-permute-start(bf16[2,12,48,128]{3,2,1,0:T(8,128)(2,1)S(1)} %rotated.7), channel_id=1, source_target_pairs={{0,4},{4,0},{8,12},{12,8},{16,20},{20,16},{24,28},{28,24},{1,5},{5... | collective-permute-start | bytes 884744 | tf_op jit(solution)/shard_map/ppermute | solution.py:337
  98.5 2.6 %rotated.6 = bf16[2,12,48,128]{3,2,1,0:T(8,128)(2,1)S(1)} custom-call(bf16[2,12,48,128]{3,2,1,0:T(8,128)(2,1)S(1)} %get-tuple-element.11.a, bf16[2,12,48,128]{3,2,1,0:T(8,128)(2,1)S(1)} %collective-permute-done.15.b, bf16[2,12,48,128]{3,2,1,0:T(8,128)(2,1)S(1)} %collective-permute-done.16.c, bf16[2,12,48,128]{3,2,1,0:T(8,128)(2,1)S(1)} %collective-permute-done.17.d, ...), custom_call_target="tpu_custom_call" | custom-call | flops 150994944 | bytes 1474560 | tf_op jit(solution)/shard_map/rotated/pallas_call | solution.py:236
  101.1 0.0 collective-permute-done.12.b
  101.1 0.3 collective-permute-start.18
  101.4 0.0 collective-permute-done.14.d
  101.4 2.6 %rotated.5.refs_1_ = bf16[2,12,48,128]{3,2,1,0:T(8,128)(2,1)S(1)} custom-call(bf16[2,12,48,128]{3,2,1,0:T(8,128)(2,1)S(1)} %get-tuple-element.10.a, bf16[2,12,48,128]{3,2,1,0:T(8,128)(2,1)S(1)} %collective-permute-done.12.b, bf16[2,12,48,128]{3,2,1,0:T(8,128)(2,1)S(1)} %collective-permute-done.13.c, bf16[2,12,48,128]{3,2,1,0:T(8,128)(2,1)S(1)} %collective-permute-done.14.d, ...), custom_call_target="tpu_custom_call" | custom-call | flops 150994944 | bytes 1474560 | tf_op jit(solution)/shard_map/rotated/pallas_call | solution.py:236
  104.0 0.0 collective-permute-done.9.b
  104.1 0.0 collective-permute-done.11.d
  104.1 2.6 %rotated.4.refs_0_ = bf16[2,12,48,128]{3,2,1,0:T(8,128)(2,1)S(1)} custom-call(bf16[2,12,48,128]{3,2,1,0:T(8,128)(2,1)S(1)} %get-tuple-element.9.a, bf16[2,12,48,128]{3,2,1,0:T(8,128)(2,1)S(1)} %collective-permute-done.9.b, bf16[2,12,48,128]{3,2,1,0:T(8,128)(2,1)S(1)} %collective-permute-done.10.c, bf16[2,12,48,128]{3,2,1,0:T(8,128)(2,1)S(1)} %collective-permute-done.11.d, ...), custom_call_target="tpu_custom_call" | custom-call | flops 150994944 | bytes 1474560 | tf_op jit(solution)/shard_map/rotated/pallas_call | solution.py:236
  106.6 0.0 collective-permute-done.22.refs_3_
  106.7 5.4 %collective-permute-done.18.refs_2_ = bf16[2,12,48,128]{3,2,1,0:T(8,128)(2,1)S(1)} collective-permute-done((bf16[2,12,48,128]{3,2,1,0:T(8,128)(2,1)S(1)}, bf16[2,12,48,128]{3,2,1,0:T(8,128)(2,1)S(1)}, u32[]{:S(2)}, u32[]{:S(2)}) %collective-permute-start.18) | collective-permute-done | bytes 294944 | tf_op jit(solution)/shard_map/ppermute | solution.py:337
  112.1 1.1 assembled.1
  (25 shorter events, 0.2 us)
Async XLA Ops:
  0.0 90.6 %copy-start = (bf16[12,128,128]{2,1,0:T(8,128)(2,1)S(1)}, bf16[12,128,128]{2,1,0:T(8,128)(2,1)}, u32[]{:S(2)}) copy-start(bf16[12,128,128]{2,1,0:T(8,128)(2,1)} %param.13) | copy-start | bytes 1179652
  0.0 8.9 %copy-start.3 = (f32[2,48,48]{2,1,0:T(8,128)S(1)}, f32[2,48,48]{2,1,0:T(8,128)}, u32[]{:S(2)}) copy-start(f32[2,48,48]{2,1,0:T(8,128)} %param.8) | copy-start | bytes 55300
  0.0 9.1 %copy-start.6 = (s32[8]{0:T(128)S(1)}, s32[8]{0:T(128)}, u32[]{:S(2)}) copy-start(s32[8]{0:T(128)} %param.11) | copy-start | bytes 100
  0.0 9.1 %copy-start.2 = (bf16[8,2,48,48]{3,2,1,0:T(8,128)(2,1)S(1)}, bf16[8,2,48,48]{3,2,1,0:T(8,128)(2,1)}, u32[]{:S(2)}) copy-start(bf16[8,2,48,48]{3,2,1,0:T(8,128)(2,1)} %param.9) | copy-start | bytes 221188
  2.3 39.2 %copy-start.1 = (bf16[2,48,48,128]{3,2,1,0:T(8,128)(2,1)S(1)}, bf16[2,48,48,128]{3,2,1,0:T(8,128)(2,1)}, u32[]{:S(2)}) copy-start(bf16[2,48,48,128]{3,2,1,0:T(8,128)(2,1)} %own.5) | copy-start | bytes 3538948
  2.3 59.7 %collective-permute-start.1 = (bf16[2,26,48,128]{3,2,1,0:T(8,128)(2,1)}, bf16[2,26,48,128]{3,2,1,0:T(8,128)(2,1)S(1)}, u32[]{:S(2)}, u32[]{:S(2)}) collective-permute-start(bf16[2,26,48,128]{3,2,1,0:T(8,128)(2,1)} %get-tuple-element.13), channel_id=1, source_target_pairs={{4,12},{8,0},{12,20},{16,8},{20,28},{24,16},{5,13},{9,1},{13,21},{... | collective-permute-start | bytes 1916936 | tf_op jit(solution)/shard_map/ppermute | solution.py:289
  3.7 19.3 %collective-permute-start = (bf16[2,26,48,128]{3,2,1,0:T(8,128)(2,1)S(1)}, bf16[2,26,48,128]{3,2,1,0:T(8,128)(2,1)S(1)}, u32[]{:S(2)}, u32[]{:S(2)}) collective-permute-start(bf16[2,26,48,128]{3,2,1,0:T(8,128)(2,1)S(1)} %get-tuple-element.14), channel_id=1, source_target_pairs={{0,4},{4,0},{8,12},{12,8},{16,20},{20,16},{24,28},{28,24},{1,5},{5... | collective-permute-start | bytes 1916936 | tf_op jit(solution)/shard_map/ppermute | solution.py:288
  23.0 39.0 %collective-permute-start.2 = (bf16[2,26,48,128]{3,2,1,0:T(8,128)(2,1)S(1)}, bf16[2,26,48,128]{3,2,1,0:T(8,128)(2,1)}, u32[]{:S(2)}, u32[]{:S(2)}) collective-permute-start(bf16[2,26,48,128]{3,2,1,0:T(8,128)(2,1)S(1)} %collective-permute-done.xr), channel_id=1, source_target_pairs={{0,8},{8,16},{12,4},{16,24},{20,12},{28,20},{1,9},{9,17},{13,5},{1... | collective-permute-start | bytes 1916936 | tf_op jit(solution)/shard_map/ppermute | solution.py:290
  28.3 6.1 %collective-permute-start.3 = (bf16[2,26,16,48]{3,2,1,0:T(8,128)(2,1)}, bf16[2,26,16,48]{3,2,1,0:T(8,128)(2,1)S(1)}, u32[]{:S(2)}, u32[]{:S(2)}) collective-permute-start(bf16[2,26,16,48]{3,2,1,0:T(8,128)(2,1)} %constant_dynamic-slice_fusion.2), channel_id=1, source_target_pairs={{0,4},{4,0},{8,12},{12,8},{16,20},{20,16},{24,28},{28,24},{1,5},{5... | collective-permute-start | bytes 239624 | tf_op jit(solution)/shard_map/ppermute | solution.py:307
  29.0 8.1 %collective-permute-start.4 = (bf16[1,26,16,48]{3,2,1,0:T(8,128)(2,1)}, bf16[1,26,16,48]{3,2,1,0:T(8,128)(2,1)}, u32[]{:S(2)}, u32[]{:S(2)}) collective-permute-start(bf16[1,26,16,48]{3,2,1,0:T(8,128)(2,1)} %constant_dynamic-slice_fusion.1), channel_id=1, source_target_pairs={{4,12},{8,0},{12,20},{16,8},{20,28},{24,16},{5,13},{9,1},{13,21},{... | collective-permute-start | bytes 119816 | tf_op jit(solution)/shard_map/ppermute | solution.py:309
  34.4 27.7 %copy-start.4 = (f32[8]{0:T(128)S(1)}, f32[8]{0:T(128)}, u32[]{:S(2)}) copy-start(f32[8]{0:T(128)} %param.10) | copy-start | bytes 100
  34.4 7.1 %collective-permute-start.5 = (bf16[1,26,16,48]{3,2,1,0:T(8,128)(2,1)S(1)}, bf16[1,26,16,48]{3,2,1,0:T(8,128)(2,1)S(1)}, u32[]{:S(2)}, u32[]{:S(2)}) collective-permute-start(bf16[1,26,16,48]{3,2,1,0:T(8,128)(2,1)S(1)} %constant_dynamic-slice_fusion), channel_id=1, source_target_pairs={{0,8},{8,16},{12,4},{16,24},{20,12},{28,20},{1,9},{9,17},{13,5},{1... | collective-permute-start | bytes 119816 | tf_op jit(solution)/shard_map/ppermute | solution.py:310
  49.4 4.1 %collective-permute-start.6 = (f32[24,128]{1,0:T(8,128)S(1)}, f32[24,128]{1,0:T(8,128)S(1)}, u32[]{:S(2)}, u32[]{:S(2)}) collective-permute-start(f32[24,128]{1,0:T(8,128)S(1)} %partials.1), channel_id=1, source_target_pairs={{0,4},{4,0},{8,12},{12,8},{16,20},{20,16},{24,28},{28,24},{1,5},{5... | collective-permute-start | bytes 36872 | tf_op jit(solution)/shard_map/ppermute | solution.py:315
  53.5 3.9 %collective-permute-start.7 = (f32[24,128]{1,0:T(8,128)S(1)}, f32[24,128]{1,0:T(8,128)S(1)}, u32[]{:S(2)}, u32[]{:S(2)}) collective-permute-start(f32[24,128]{1,0:T(8,128)S(1)} %add.33), channel_id=1, source_target_pairs={{0,8},{4,12},{8,0},{12,4},{16,24},{20,28},{24,16},{28,20},{1,9},{5... | collective-permute-start | bytes 36872 | tf_op jit(solution)/shard_map/ppermute | solution.py:315
  57.4 4.6 %collective-permute-start.8 = (f32[24,128]{1,0:T(8,128)S(1)}, f32[24,128]{1,0:T(8,128)S(1)}, u32[]{:S(2)}, u32[]{:S(2)}) collective-permute-start(f32[24,128]{1,0:T(8,128)S(1)} %add.34), channel_id=1, source_target_pairs={{0,16},{4,20},{8,24},{12,28},{16,0},{20,4},{24,8},{28,12},{1,17},{... | collective-permute-start | bytes 36872 | tf_op jit(solution)/shard_map/ppermute | solution.py:315
  70.3 14.0 %collective-permute-start.20 = (bf16[2,12,48,128]{3,2,1,0:T(8,128)(2,1)}, bf16[2,12,48,128]{3,2,1,0:T(8,128)(2,1)}, u32[]{:S(2)}, u32[]{:S(2)}) collective-permute-start(bf16[2,12,48,128]{3,2,1,0:T(8,128)(2,1)} %get-tuple-element.12.a), channel_id=1, source_target_pairs={{0,2},{1,3},{2,0},{3,1},{4,6},{5,7},{6,4},{7,5},{8,10},{9,11},{10,... | collective-permute-start | bytes 884744 | tf_op jit(solution)/shard_map/ppermute | solution.py:334
  71.9 13.7 %collective-permute-start.19 = (bf16[2,12,48,128]{3,2,1,0:T(8,128)(2,1)}, bf16[2,12,48,128]{3,2,1,0:T(8,128)(2,1)}, u32[]{:S(2)}, u32[]{:S(2)}) collective-permute-start(bf16[2,12,48,128]{3,2,1,0:T(8,128)(2,1)} %get-tuple-element.12.a), channel_id=1, source_target_pairs={{0,1},{1,0},{2,3},{3,2},{4,5},{5,4},{6,7},{7,6},{8,9},{9,8},{10,11... | collective-permute-start | bytes 884744 | tf_op jit(solution)/shard_map/ppermute | solution.py:333
  71.9 9.6 %copy-start.5 = (s32[12,2]{0,1:T(2,128)S(1)}, s32[12,2]{0,1:T(2,128)}, u32[]{:S(2)}) copy-start(s32[12,2]{0,1:T(2,128)} %param.12) | copy-start | bytes 292
  71.9 12.5 %collective-permute-start.13 = (bf16[2,12,48,128]{3,2,1,0:T(8,128)(2,1)S(1)}, bf16[2,12,48,128]{3,2,1,0:T(8,128)(2,1)S(1)}, u32[]{:S(2)}, u32[]{:S(2)}) collective-permute-start(bf16[2,12,48,128]{3,2,1,0:T(8,128)(2,1)S(1)} %get-tuple-element.10.a), channel_id=1, source_target_pairs={{0,2},{1,3},{2,0},{3,1},{4,6},{5,7},{6,4},{7,5},{8,10},{9,11},{10,... | collective-permute-start | bytes 884744 | tf_op jit(solution)/shard_map/ppermute | solution.py:334
  79.9 10.7 %collective-permute-start.16 = (bf16[2,12,48,128]{3,2,1,0:T(8,128)(2,1)S(1)}, bf16[2,12,48,128]{3,2,1,0:T(8,128)(2,1)S(1)}, u32[]{:S(2)}, u32[]{:S(2)}) collective-permute-start(bf16[2,12,48,128]{3,2,1,0:T(8,128)(2,1)S(1)} %get-tuple-element.11.a), channel_id=1, source_target_pairs={{0,2},{1,3},{2,0},{3,1},{4,6},{5,7},{6,4},{7,5},{8,10},{9,11},{10,... | collective-permute-start | bytes 884744 | tf_op jit(solution)/shard_map/ppermute | solution.py:334
  81.5 19.6 %collective-permute-start.12 = (bf16[2,12,48,128]{3,2,1,0:T(8,128)(2,1)S(1)}, bf16[2,12,48,128]{3,2,1,0:T(8,128)(2,1)S(1)}, u32[]{:S(2)}, u32[]{:S(2)}) collective-permute-start(bf16[2,12,48,128]{3,2,1,0:T(8,128)(2,1)S(1)} %get-tuple-element.10.a), channel_id=1, source_target_pairs={{0,1},{1,0},{2,3},{3,2},{4,5},{5,4},{6,7},{7,6},{8,9},{9,8},{10,11... | collective-permute-start | bytes 884744 | tf_op jit(solution)/shard_map/ppermute | solution.py:333
  84.3 11.9 %collective-permute-start.15 = (bf16[2,12,48,128]{3,2,1,0:T(8,128)(2,1)S(1)}, bf16[2,12,48,128]{3,2,1,0:T(8,128)(2,1)S(1)}, u32[]{:S(2)}, u32[]{:S(2)}) collective-permute-start(bf16[2,12,48,128]{3,2,1,0:T(8,128)(2,1)S(1)} %get-tuple-element.11.a), channel_id=1, source_target_pairs={{0,1},{1,0},{2,3},{3,2},{4,5},{5,4},{6,7},{7,6},{8,9},{9,8},{10,11... | collective-permute-start | bytes 884744 | tf_op jit(solution)/shard_map/ppermute | solution.py:333
  84.3 11.9 %collective-permute-start.10 = (bf16[2,12,48,128]{3,2,1,0:T(8,128)(2,1)S(1)}, bf16[2,12,48,128]{3,2,1,0:T(8,128)(2,1)S(1)}, u32[]{:S(2)}, u32[]{:S(2)}) collective-permute-start(bf16[2,12,48,128]{3,2,1,0:T(8,128)(2,1)S(1)} %get-tuple-element.9.a), channel_id=1, source_target_pairs={{0,2},{1,3},{2,0},{3,1},{4,6},{5,7},{6,4},{7,5},{8,10},{9,11},{10,... | collective-permute-start | bytes 884744 | tf_op jit(solution)/shard_map/ppermute | solution.py:334
  85.5 5.5 %collective-permute-start.21 = (bf16[2,12,48,128]{3,2,1,0:T(8,128)(2,1)}, bf16[2,12,48,128]{3,2,1,0:T(8,128)(2,1)S(1)}, u32[]{:S(2)}, u32[]{:S(2)}) collective-permute-start(bf16[2,12,48,128]{3,2,1,0:T(8,128)(2,1)} %collective-permute-done.20.c), channel_id=1, source_target_pairs={{0,1},{1,0},{2,3},{3,2},{4,5},{5,4},{6,7},{7,6},{8,9},{9,8},{10,11... | collective-permute-start | bytes 884744 | tf_op jit(solution)/shard_map/ppermute | solution.py:335
  90.6 6.1 %collective-permute-start.17 = (bf16[2,12,48,128]{3,2,1,0:T(8,128)(2,1)S(1)}, bf16[2,12,48,128]{3,2,1,0:T(8,128)(2,1)S(1)}, u32[]{:S(2)}, u32[]{:S(2)}) collective-permute-start(bf16[2,12,48,128]{3,2,1,0:T(8,128)(2,1)S(1)} %collective-permute-done.16.c), channel_id=1, source_target_pairs={{0,1},{1,0},{2,3},{3,2},{4,5},{5,4},{6,7},{7,6},{8,9},{9,8},{10,11... | collective-permute-start | bytes 884744 | tf_op jit(solution)/shard_map/ppermute | solution.py:335
  91.0 10.4 %collective-permute-start.14 = (bf16[2,12,48,128]{3,2,1,0:T(8,128)(2,1)S(1)}, bf16[2,12,48,128]{3,2,1,0:T(8,128)(2,1)S(1)}, u32[]{:S(2)}, u32[]{:S(2)}) collective-permute-start(bf16[2,12,48,128]{3,2,1,0:T(8,128)(2,1)S(1)} %collective-permute-done.13.c), channel_id=1, source_target_pairs={{0,1},{1,0},{2,3},{3,2},{4,5},{5,4},{6,7},{7,6},{8,9},{9,8},{10,11... | collective-permute-start | bytes 884744 | tf_op jit(solution)/shard_map/ppermute | solution.py:335
  96.2 7.8 %collective-permute-start.9 = (bf16[2,12,48,128]{3,2,1,0:T(8,128)(2,1)S(1)}, bf16[2,12,48,128]{3,2,1,0:T(8,128)(2,1)S(1)}, u32[]{:S(2)}, u32[]{:S(2)}) collective-permute-start(bf16[2,12,48,128]{3,2,1,0:T(8,128)(2,1)S(1)} %get-tuple-element.9.a), channel_id=1, source_target_pairs={{0,1},{1,0},{2,3},{3,2},{4,5},{5,4},{6,7},{7,6},{8,9},{9,8},{10,11... | collective-permute-start | bytes 884744 | tf_op jit(solution)/shard_map/ppermute | solution.py:333
  96.2 7.8 %collective-permute-start.11 = (bf16[2,12,48,128]{3,2,1,0:T(8,128)(2,1)S(1)}, bf16[2,12,48,128]{3,2,1,0:T(8,128)(2,1)S(1)}, u32[]{:S(2)}, u32[]{:S(2)}) collective-permute-start(bf16[2,12,48,128]{3,2,1,0:T(8,128)(2,1)S(1)} %collective-permute-done.10.c), channel_id=1, source_target_pairs={{0,1},{1,0},{2,3},{3,2},{4,5},{5,4},{6,7},{7,6},{8,9},{9,8},{10,11... | collective-permute-start | bytes 884744 | tf_op jit(solution)/shard_map/ppermute | solution.py:335
  96.8 9.9 %collective-permute-start.22 = (bf16[2,12,48,128]{3,2,1,0:T(8,128)(2,1)S(1)}, bf16[2,12,48,128]{3,2,1,0:T(8,128)(2,1)S(1)}, u32[]{:S(2)}, u32[]{:S(2)}) collective-permute-start(bf16[2,12,48,128]{3,2,1,0:T(8,128)(2,1)S(1)} %rotated.7), channel_id=1, source_target_pairs={{0,4},{4,0},{8,12},{12,8},{16,20},{20,16},{24,28},{28,24},{1,5},{5... | collective-permute-start | bytes 884744 | tf_op jit(solution)/shard_map/ppermute | solution.py:337
  101.1 11.0 %collective-permute-start.18 = (bf16[2,12,48,128]{3,2,1,0:T(8,128)(2,1)S(1)}, bf16[2,12,48,128]{3,2,1,0:T(8,128)(2,1)S(1)}, u32[]{:S(2)}, u32[]{:S(2)}) collective-permute-start(bf16[2,12,48,128]{3,2,1,0:T(8,128)(2,1)S(1)} %rotated.6), channel_id=1, source_target_pairs={{0,4},{4,0},{8,12},{12,8},{16,20},{20,16},{24,28},{28,24},{1,5},{5... | collective-permute-start | bytes 884744 | tf_op jit(solution)/shard_map/ppermute | solution.py:337

commit v2 on v1

v2 whole, which is shorter than its diff:
```python
import functools

import jax
import jax.numpy as jnp
from jax import lax
from jax.experimental import pallas as pl
from jax.experimental.pallas import tpu as pltpu
from jax.sharding import PartitionSpec as P

F32 = jnp.float32
BF16 = jnp.bfloat16
VMEM_LIMIT = 50 * 1024 * 1024


def params():
    return pltpu.CompilerParams(vmem_limit_bytes=VMEM_LIMIT)


def cost(flops, moved):
    return pl.CostEstimate(flops=flops, bytes_accessed=moved, transcendentals=0)


def inside(p, window):
    return jnp.logical_and(p >= 0, p < window).astype(F32)


def pair_matrices(width):
    n = 2 * width
    i = lax.broadcasted_iota(jnp.int32, (n, n), 0)
    j = lax.broadcasted_iota(jnp.int32, (n, n), 1)
    same = (i < width) == (j < width)
    along = jnp.logical_and(jnp.abs(i - j) == 1, same)
    here = jnp.where(jnp.logical_or(along, jnp.abs(i - j) == width), -0.125, 0.0)
    before = jnp.where(i == j + width, -0.125, 0.0)
    after = jnp.where(i == j - width, -0.125, 0.0)
    return here.astype(BF16), before.astype(BF16), after.astype(BF16)


def partial_kernel(count, own, f_own, f_x, f_d, out, acc, gram):
    x = lax.rem(lax.axis_index("space"), 2)
    _, pairs, depth, cells = f_own.shape
    orbs = own.shape[3]
    here, before, after = pair_matrices(cells // 2)
    acc[...] = jnp.zeros_like(acc)
    gram[...] = jnp.zeros_like(gram)

    def row(r, carry):
        low, high = jnp.maximum(r - 1, 0), jnp.minimum(r + 1, pairs - 1)
        has_low, has_high = inside(r - 1, pairs), inside(r + 1, pairs)
        tiles = [f_d[r], f_own[x, r], f_own[1 - x, r], f_x[r]]
        total, square = acc[...], gram[...]
        for c in (1, 2):
            plane = x if c == 1 else 1 - x
            b = tiles[c]
            b32 = b.astype(F32)
            u = b32[count : count + 1] + b32[count + 1 : count + 2]
            local = jnp.dot(b, here, preferred_element_type=F32)
            local += has_low * jnp.dot(f_own[plane, low], before, preferred_element_type=F32)
            local += has_high * jnp.dot(f_own[plane, high], after, preferred_element_type=F32)
            local += u * b32 - 0.125 * (tiles[c - 1].astype(F32) + tiles[c + 1].astype(F32))
            hi = local.astype(BF16)
            lo = (local - hi.astype(F32)).astype(BF16)
            weights = jnp.concatenate([b, hi, lo], axis=0)
            v = own[plane, pl.ds(2 * r, 2)].reshape(cells, orbs)
            total = total + jnp.dot(weights, v, preferred_element_type=F32)
            square = square + lax.dot_general(
                b, b, (((1,), (1,)), ((), ())), preferred_element_type=F32
            )
        acc[...] = total
        gram[...] = square
        return carry

    lax.fori_loop(0, pairs, row, 0)
    out[...] = jnp.zeros_like(out)
    out[0:count] = acc[0:count]
    out[count : 2 * count] = acc[depth : depth + count] + acc[2 * depth : 2 * depth + count]
    out[2 * count : 3 * count, 0:count] = gram[0:count, 0:count]


def partials(count, own, f_own, f_x, f_d):
    orbs = own.shape[3]
    depth = f_own.shape[2]
    cells = own.size // orbs
    return pl.pallas_call(
        functools.partial(partial_kernel, count),
        out_shape=jax.ShapeDtypeStruct((3 * count, orbs), F32),
        in_specs=[pl.BlockSpec(memory_space=pltpu.VMEM)] * 4,
        out_specs=pl.BlockSpec(memory_space=pltpu.VMEM),
        scratch_shapes=[pltpu.VMEM((3 * depth, orbs), F32), pltpu.VMEM((depth, depth), F32)],
        compiler_params=params(),
        cost_estimate=cost(2 * cells * 3 * depth * orbs, cells * orbs * 4),
        name="partials",
    )(own, f_own, f_x, f_d)


def filter_kernel(count, slabs, start, parts, joint, *refs):
    own, f_own, f_x, f_d, f_zo, sums, strength, zo = refs[:8]
    xrs, zfs = refs[8 : 8 + parts], refs[8 + parts : 8 + 2 * parts]
    outs, scratch = refs[8 + 2 * parts : -3 if parts > 1 else -1], refs[-3 if parts > 1 else -1 :]
    first = scratch[0]
    place = lax.axis_index("space")
    x = lax.rem(place, 2)
    _, pairs, depth, cells = f_own.shape
    width = cells // 2
    half = own.shape[1] // 2
    orbs = own.shape[3]
    rows = outs[0].shape[1]
    base = (half - 2) * x
    lower = (place >= 2).astype(F32)
    upper = (place < slabs - 2).astype(F32)
    is_odd = x.astype(F32)
    has_zf = lower * (1.0 - is_odd) + upper * is_odd
    has_zo = upper * (1.0 - is_odd) + lower * is_odd
    if parts > 1:
        xr, zf = scratch[1], scratch[2]
        for target, pieces in ((xr, xrs), (zf, zfs)):
            at = 0
            for piece in pieces:
                target[:, at : at + piece.shape[1]] = piece[...]
                at += piece.shape[1]
        window = at // 2
    else:
        xr, zf = xrs[0], zfs[0]
        window = xr.shape[1] // 2

    coef1 = (strength[...] * sums[0:count]).astype(BF16).astype(F32) * 0.25
    gram = sums[2 * count : 3 * count]
    padded = coef1
    if orbs > count:
        padded = jnp.concatenate([coef1, jnp.zeros((orbs - count, orbs), F32)], axis=0)
    proj2 = sums[count : 2 * count] + jnp.dot(
        gram, padded, preferred_element_type=F32, precision=lax.Precision.HIGHEST
    )
    coef2 = (strength[...] * proj2).astype(BF16).astype(F32) * 0.25
    k = lax.broadcasted_iota(jnp.int32, (depth, orbs), 0)
    ones = jnp.where(jnp.logical_or(k == count, k == count + 1), 1.0, 0.0)

    def right(coef):
        rest = jnp.zeros((depth - count, orbs), F32)
        return jnp.concatenate([jnp.concatenate([coef, rest], axis=0), ones], axis=1).astype(BF16)

    right1, right2 = right(coef1), right(coef2)
    here, _, _ = pair_matrices(width)

    def field(c, p):
        if c == 1:
            return f_d[base // 2 + p]
        if c in (2, 3):
            return f_own[(c % 2) ^ x, base // 2 + p]
        if c == 4:
            return f_x[base // 2 + p]
        if c == 5:
            return f_x[pairs + p]
        return f_zo[p]

    def rows_of(c, w, n):
        plane = (c % 2) ^ x
        if c in (2, 3):
            return own[plane, pl.ds(base + w, n)]
        ref = zf if c < 2 else (xr if c < 6 else zo)
        return ref[plane, pl.ds(w, n)]

    def applied(pair, v, outer, zs, fields, right_side):
        both = lax.dot_general(
            fields, right_side, (((0,), (0,)), ((), ())), preferred_element_type=F32
        )
        near = jnp.dot(here, pair, preferred_element_type=F32)
        return both[:, :orbs] + near + both[:, orbs:] * v - 0.125 * (outer + zs)

    def step1(j, carry):
        p = start // 2 + x + j - 1
        q = jnp.clip(p, 0, window - 1)
        has_below = inside(p - 1, window)
        has_above = inside(p + 1, window)
        valid = inside(p, window)
        below = jnp.maximum(2 * q - 1, 0)
        above = jnp.minimum(2 * q + 2, 2 * window - 1)
        pair = [rows_of(c, 2 * q, 2).reshape(cells, orbs) for c in range(8)]
        vs = [v.astype(F32) for v in pair]
        for c in range(1, 7):
            outer = jnp.concatenate(
                [
                    rows_of(c, below, 1)[0].astype(F32) * has_below,
                    rows_of(c, above, 1)[0].astype(F32) * has_above,
                ],
                axis=0,
            )
            f = applied(pair[c], vs[c], outer, vs[c - 1] + vs[c + 1], field(c, q), right1)
            keep = valid
            if c == 1:
                keep = valid * has_zf
            if c == 6:
                keep = valid * has_zo
            first[c - 1, pl.ds(2 * j, 2)] = (f * keep).astype(BF16).reshape(2, width, orbs)
        return carry

    lax.fori_loop(0, rows // 2 + 2, step1, 0)

    def step2(j, carry):
        p = start // 2 + x + j
        pair = [first[c - 1, pl.ds(2 * j + 2, 2)].reshape(cells, orbs) for c in range(1, 7)]
        vs = [v.astype(F32) for v in pair]
        for c in range(2, 6):
            outer = jnp.concatenate(
                [first[c - 1, 2 * j + 1].astype(F32), first[c - 1, 2 * j + 4].astype(F32)], axis=0
            )
            f = applied(
                pair[c - 1], vs[c - 1], outer, vs[c - 2] + vs[c], field(c, p), right2
            )
            f = f.astype(BF16).reshape(2, width, orbs)
            plane = (c % 2) ^ x
            if joint:
                outs[0][plane + (2 if c in (2, 3) else 0), pl.ds(2 * j, 2)] = f
            else:
                outs[1 if c in (2, 3) else 0][plane, pl.ds(2 * j, 2)] = f
        return carry

    lax.fori_loop(0, rows // 2, step2, 0)


def filtered(count, slabs, start, rows, joint, operands, xrs, zfs):
    own = operands[0]
    planes, _, width, orbs = own.shape
    parts = len(xrs)
    shape = (2 * planes if joint else planes, rows, width, orbs)
    out = (jax.ShapeDtypeStruct(shape, BF16),) * (1 if joint else 2)
    cells = 10 * rows * width
    scratch = [pltpu.VMEM((6, rows + 4, width, orbs), BF16)]
    if parts > 1:
        window = sum(piece.shape[1] for piece in xrs)
        scratch += [pltpu.VMEM((planes, window, width, orbs), BF16)] * 2
    return pl.pallas_call(
        functools.partial(filter_kernel, count, slabs, start, parts, joint),
        out_shape=out,
        in_specs=[pl.BlockSpec(memory_space=pltpu.VMEM)] * (len(operands) + 2 * parts),
        out_specs=(pl.BlockSpec(memory_space=pltpu.VMEM),) * len(out),
        scratch_shapes=scratch,
        compiler_params=params(),
        cost_estimate=cost(2 * cells * 32 * orbs, cells * orbs * 4),
        name="filtered",
    )(*operands, *xrs, *zfs)


def rotate_kernel(group, *refs):
    a, b, c, d, q = refs[:5]
    outs = refs[5:]
    _, rows, width, orbs = a.shape
    planes = outs[0].shape[0]
    low = jnp.concatenate([q[0], q[1]], axis=0)
    high = jnp.concatenate([q[2], q[3]], axis=0)

    def one(j, carry):
        for plane in range(a.shape[0]):
            def take(ref):
                return ref[plane, pl.ds(group * j, group)].reshape(group * width, orbs)

            total = jnp.dot(
                jnp.concatenate([take(a), take(b)], axis=1), low, preferred_element_type=F32
            )
            total = total + jnp.dot(
                jnp.concatenate([take(c), take(d)], axis=1), high, preferred_element_type=F32
            )
            outs[plane // planes][plane % planes, pl.ds(group * j, group)] = total.astype(
                BF16
            ).reshape(group, width, orbs)
        return carry

    lax.fori_loop(0, rows // group, one, 0)


def rotated(blocks, q, pieces):
    a = blocks[0]
    size = a.size
    group = max(g for g in range(1, 7) if a.shape[1] % g == 0)
    out = jax.ShapeDtypeStruct((a.shape[0] // pieces, *a.shape[1:]), BF16)
    return pl.pallas_call(
        functools.partial(rotate_kernel, group),
        out_shape=(out,) * pieces,
        in_specs=[pl.BlockSpec(memory_space=pltpu.VMEM)] * 5,
        out_specs=(pl.BlockSpec(memory_space=pltpu.VMEM),) * pieces,
        compiler_params=params(),
        cost_estimate=cost(8 * size * a.shape[3], 10 * size),
        name="rotated",
    )(*blocks, q)


def assemble_kernel(half, *refs):
    out = refs[-1]
    pieces = (len(refs) - 1) // 2
    x = lax.rem(lax.axis_index("space"), 2)
    rows = refs[0].shape[1]
    for k in range(pieces):
        out[:, pl.ds(half * x + rows * k, rows)] = refs[k][...]
        out[:, pl.ds(half * (1 - x) + rows * k, rows)] = refs[pieces + k][...]


def assembled(shape, mine, theirs):
    return pl.pallas_call(
        functools.partial(assemble_kernel, shape[1] // 2),
        out_shape=jax.ShapeDtypeStruct(shape, BF16),
        in_specs=[pl.BlockSpec(memory_space=pltpu.VMEM)] * (len(mine) + len(theirs)),
        out_specs=pl.BlockSpec(memory_space=pltpu.VMEM),
        compiler_params=params(),
        name="assembled",
    )(*mine, *theirs)


def ordered(*arrays):
    return lax.optimization_barrier(arrays)


def shards(psi, potential, beta, strength, atom_slab, pattern, q_tiles):
    planes, width_x, width_y, orbs = psi.shape
    count = beta.shape[0]
    slabs = lax.axis_size("space")
    place = lax.axis_index("space")
    x = lax.rem(place, 2)
    half = width_x // 2
    window = half + 2
    rows = half // 2
    early = rows + 4

    def within(pairs):
        return [(i, j) for i, j in pairs if 0 <= j < slabs]

    swap = [(i, i ^ 1) for i in range(slabs)]
    own_way = within([(i, i + 2 if i % 2 else i - 2) for i in range(slabs)])
    other_way = within([(i, i - 2 if i % 2 else i + 2) for i in range(slabs)])
    raster = within([(i, i + 1 if i % 2 else i - 1) for i in range(slabs)])
    groups = lax.axis_size("orb")
    across = [(i, i ^ 2) for i in range(groups)]
    beside = [(i, i ^ 1) for i in range(groups)]
    mine = (half - 2) * x
    theirs = (half - 2) * (1 - x)

    active = jnp.abs(place - atom_slab) <= 1
    beta_m = jnp.where(active[:, None, None, None], beta, jnp.zeros_like(beta))
    depth = -(-(count + 2) // 16) * 16
    u = (potential - 1.0) * 0.25
    hi = lax.reduce_precision(u, 8, 7)
    lo = u - hi
    fields = jnp.concatenate(
        [
            jnp.transpose(beta_m, (1, 2, 0, 3)),
            hi[:, :, None, :].astype(BF16),
            lo[:, :, None, :].astype(BF16),
            jnp.zeros((planes, width_x, depth - count - 2, width_y), BF16),
        ],
        axis=2,
    )
    fields = jnp.concatenate([fields[:, 0::2], fields[:, 1::2]], axis=3)
    far = lax.dynamic_index_in_dim(fields, x, 0, keepdims=False)
    near = lax.dynamic_index_in_dim(fields, 1 - x, 0, keepdims=False)
    to_x = jnp.concatenate(
        [near, lax.dynamic_slice_in_dim(far, theirs // 2, window // 2, axis=0)], axis=0
    )
    to_zo = lax.dynamic_slice_in_dim(far, mine // 2, window // 2, axis=0)
    to_x, far, to_zo, psi_in = ordered(to_x, far, to_zo, psi)
    f_x = lax.ppermute(to_x, "space", swap)
    f_d = lax.ppermute(far, "space", raster)
    f_zo = lax.ppermute(to_zo, "space", own_way)

    xr1 = lax.ppermute(
        lax.dynamic_slice_in_dim(psi_in, theirs, early, axis=1), "space", swap
    )
    zo = lax.ppermute(lax.dynamic_slice_in_dim(psi_in, mine, window, axis=1), "space", own_way)
    sums = partials(count, psi, fields, f_x, f_d)
    xr1, sums = ordered(xr1, sums)
    zf1 = lax.ppermute(xr1, "space", other_way)
    second = lax.dynamic_slice_in_dim(psi, theirs + early, window - early, axis=1)
    second, _ = ordered(second, xr1)
    xr2 = lax.ppermute(second, "space", swap)
    step = 1
    while step < slabs:
        sums = sums + lax.ppermute(sums, "space", [(i, i ^ step) for i in range(slabs)])
        step *= 2
    zf1, xr2 = ordered(zf1, xr2)
    zf2 = lax.ppermute(xr2, "space", other_way)
    strong = jnp.broadcast_to(strength[:, None], (count, orbs))

    me = lax.axis_index("orb")
    which = jnp.bitwise_xor(me, jnp.arange(groups, dtype=jnp.int32))
    rows_hot = (pattern[:, 0][:, None] == which[None, :]).astype(BF16)
    rows_hot = rows_hot * (pattern[:, 1] == me).astype(BF16)[:, None]
    q = jnp.einsum("ki,kab->iab", rows_hot, q_tiles, preferred_element_type=F32).astype(BF16)

    operands = (psi, fields, f_x, f_d, f_zo, sums, strong, zo)
    (block1,) = filtered(count, slabs, 0, rows, True, operands, (xr1,), (zf1,))
    y1 = lax.ppermute(block1, "orb", across)
    c1 = lax.ppermute(block1, "orb", beside)
    give2, keep2 = filtered(count, slabs, rows, rows, False, operands, (xr1, xr2), (zf1, zf2))
    cg = lax.ppermute(give2, "orb", beside)
    ck = lax.ppermute(keep2, "orb", beside)
    give_y, y1 = ordered(give2, y1)
    yg = lax.ppermute(give_y, "orb", across)
    yc1 = lax.ppermute(y1, "orb", beside)
    give1, keep1 = rotated((block1, c1, y1, yc1), q, 2)
    got1 = lax.ppermute(give1, "space", swap)
    keep_y, yg = ordered(keep2, yg)
    yk = lax.ppermute(keep_y, "orb", across)
    ycg = lax.ppermute(yg, "orb", beside)
    (give2,) = rotated((give2, cg, yg, ycg), q, 1)
    got2 = lax.ppermute(give2, "space", swap)
    yck = lax.ppermute(yk, "orb", beside)
    (keep2,) = rotated((keep2, ck, yk, yck), q, 1)
    return assembled(psi.shape, [keep1, keep2], [got1, got2])


def solution(mesh):
    placed = (
        P("space", None, None, "orb"),
        P("space", None, None),
        P(None, "space", None, None),
        P(),
        P(),
        P(),
        P(),
    )
    return jax.shard_map(
        shards, mesh=mesh, in_specs=placed, out_specs=P("space", None, None, "orb"), check_vma=False
    )
```

time: 114 us -> 112 us (0.982)
  starting transfers between devices: 30.7 us -> 43.8 us
  Pallas kernels: 36.2 us -> 24.6 us
  waiting for transfers between devices: 41.5 us -> 32.5 us
  other arithmetic: 0.41 us -> 4.49 us
  local copies, waits for them, and re-layouts: 3.9 us -> 5.33 us
    pallas_call x6 -> x5, Pallas kernels: 27.2 us -> 13.6 us  [the longest x2 10.5 us: filtered(): pl.pallas_call(functools.partial(filter_kernel, count, slabs, start, part...]
    ppermute x20 -> x19, starting transfers between devices: 23.2 us -> 36.2 us  [the longest x1 11.8 us: shards(): zf1 = lax.ppermute(xr1, 'space', other_way)]
    ppermute x20 -> x19, waiting for transfers between devices: 36.4 us -> 26 us  [the longest x1 8.48 us: shards(): yg = lax.ppermute(give_y, 'orb', across)]
    unnamed x14 -> x26, local copies, waits for them, and re-layouts: 0.03 us -> 3.38 us
    pallas_call x1, Pallas kernels: 7.86 us -> 9.91 us  [partials(): pl.pallas_call(functools.partial(partial_kernel, count), out_shape=jax.Sh...]
    dynamic_slice x4 -> x3, local copies, waits for them, and re-layouts: 3.62 us -> 1.67 us  [the longest x1 0.87 us: shards(): lax.dynamic_slice_in_dim(psi_in, mine, window, axis=1)]
    ppermute x3, waiting for transfers between devices: 5.08 us -> 6.56 us  [shards(): lax.ppermute(sums, 'space', [(i, i ^ step) for i in range(slabs)])]
  transfers between devices with their start and end apart: 23 -> 22, of which waited for: 10 -> 10; matrix products, arithmetic and copies ran while one was open for 2% -> 1% of each run, Pallas kernels for 24% -> 17%
where the time goes in v2:
time: 112 us; the launch traced here: 111 us
  starting transfers between devices  43.8 us (39%)
  waiting for transfers between devices  32.5 us (29%)
  Pallas kernels  24.6 us (22%)
  local copies, waits for them, and re-layouts  5.33 us (5%)
  other arithmetic  4.49 us (4%)
    ppermute x1, starting transfers between devices, shards(): zf1 = lax.ppermute(xr1, 'space', other_way)  11.8 us
    pallas_call x2, Pallas kernels, filtered(): pl.pallas_call(functools.partial(filter_kernel, count, slabs, start, part...  10.5 us
    pallas_call x1, Pallas kernels, partials(): pl.pallas_call(functools.partial(partial_kernel, count), out_shape=jax.Sh...  9.91 us
    ppermute x1, waiting for transfers between devices, shards(): yg = lax.ppermute(give_y, 'orb', across)  8.48 us
    ppermute x3, starting transfers between devices, shards(): lax.ppermute(sums, 'space', [(i, i ^ step) for i in range(slabs)])  7.63 us
    ppermute x3, waiting for transfers between devices, shards(): lax.ppermute(sums, 'space', [(i, i ^ step) for i in range(slabs)])  6.56 us
    ppermute x1, waiting for transfers between devices, shards(): got1 = lax.ppermute(give1, 'space', swap)  5.83 us
    ppermute x1, starting transfers between devices, shards(): f_x = lax.ppermute(to_x, 'space', swap)  5.41 us
  transfers between devices with their start and end apart: 22, of which 10 were waited for; matrix products, arithmetic and copies ran while one was open for 1% of the time, Pallas kernels for 17%

profile of v2, /device:TPU:0, one launch (start us, length us, event | category | flops | bytes accessed | tf_op | source)
XLA Modules:
  0.0 111.5 jit_solution(12231125739010953042)
XLA Ops:
  0.0 0.7 abs_compare_fusion
  0.7 0.8 fusion.13
  1.6 0.1 pad.7.clone
  1.7 1.0 fusion.2
  2.7 0.3 maximum_maximum_fusion
  3.0 0.0 copy-start.1
  3.1 0.1 fusion.6
  3.2 0.7 fusion.10
  3.9 0.7 pad_maximum_fusion
  4.6 0.8 constant_dynamic-slice_fusion.2
  5.4 2.9 %collective-permute-start.3 = (bf16[2,16,48,128]{3,2,1,0:T(8,128)(2,1)}, bf16[2,16,48,128]{3,2,1,0:T(8,128)(2,1)S(1)}, u32[]{:S(2)}, u32[]{:S(2)}) collective-permute-start(bf16[2,16,48,128]{3,2,1,0:T(8,128)(2,1)} %constant_dynamic-slice_fusion.2), channel_id=1, source_target_pairs={{0,4},{4,0},{8,12},{12,8},{16,20},{20,16},{24,28},{28,24},{1,5},{5... | collective-permute-start | bytes 1179656 | tf_op jit(solution)/shard_map/ppermute | solution.py:363
  8.3 0.9 constant_dynamic-slice_fusion.1
  9.2 1.3 %collective-permute-start.7 = (bf16[2,26,48,128]{3,2,1,0:T(8,128)(2,1)}, bf16[2,26,48,128]{3,2,1,0:T(8,128)(2,1)S(1)}, u32[]{:S(2)}, u32[]{:S(2)}) collective-permute-start(bf16[2,26,48,128]{3,2,1,0:T(8,128)(2,1)} %constant_dynamic-slice_fusion.1), channel_id=1, source_target_pairs={{4,12},{8,0},{12,20},{16,8},{20,28},{24,16},{5,13},{9,1},{13,21},{... | collective-permute-start | bytes 1916936 | tf_op jit(solution)/shard_map/ppermute | solution.py:366
  10.5 0.7 collective-permute-start.1
  11.1 5.4 %collective-permute-start = (bf16[37,16,96]{2,1,0:T(8,128)(2,1)}, bf16[37,16,96]{2,1,0:T(8,128)(2,1)S(1)}, u32[]{:S(2)}, u32[]{:S(2)}) collective-permute-start(bf16[37,16,96]{2,1,0:T(8,128)(2,1)} %pad_maximum_fusion), channel_id=1, source_target_pairs={{0,4},{4,0},{8,12},{12,8},{16,20},{20,16},{24,28},{28,24},{1,5},{5... | collective-permute-start | bytes 341000 | tf_op jit(solution)/shard_map/ppermute | solution.py:359
  16.6 0.1 pad_maximum_fusion.1.f_own.refs_1_
  16.7 0.0 copy-start.11
  16.7 4.2 %collective-permute-done.f_x.refs_2_ = bf16[37,16,96]{2,1,0:T(8,128)(2,1)S(1)} collective-permute-done((bf16[37,16,96]{2,1,0:T(8,128)(2,1)}, bf16[37,16,96]{2,1,0:T(8,128)(2,1)S(1)}, u32[]{:S(2)}, u32[]{:S(2)}) %collective-permute-start) | collective-permute-done | bytes 113696 | tf_op jit(solution)/shard_map/ppermute | solution.py:359
  20.9 9.9 %partials.1 = f32[24,128]{1,0:T(8,128)S(1)} custom-call(bf16[2,48,48,128]{3,2,1,0:T(8,128)(2,1)S(1)} %copy-done.1, bf16[2,24,16,96]{3,2,1,0:T(8,128)(2,1)S(1)} %pad_maximum_fusion.1.f_own.refs_1_, bf16[37,16,96]{2,1,0:T(8,128)(2,1)S(1)} %collective-permute-done.f_x.refs_2_, bf16[24,16,96]{2,1,0:T(8,128)(2,1)S(1)} %collective-permute-done.1.f_d.refs_3_), custom_call_target="tpu_custom_call" | custom-call | flops 56623104 | bytes 2359296 | tf_op jit(solution)/shard_map/partials/pallas_call | solution.py:84
  30.8 0.0 collective-permute-done.3.refs_8_
  30.8 11.8 %collective-permute-start.8 = (bf16[2,16,48,128]{3,2,1,0:T(8,128)(2,1)S(1)}, bf16[2,16,48,128]{3,2,1,0:T(8,128)(2,1)S(1)}, u32[]{:S(2)}, u32[]{:S(2)}) collective-permute-start(bf16[2,16,48,128]{3,2,1,0:T(8,128)(2,1)S(1)} %collective-permute-done.3.refs_8_), channel_id=1, source_target_pairs={{0,8},{8,16},{12,4},{16,24},{20,12},{28,20},{1,9},{9,17},{13,5},{1... | collective-permute-start | bytes 1179656 | tf_op jit(solution)/shard_map/ppermute | solution.py:369
  42.7 0.1 collective-permute-start.9
  42.8 1.3 %collective-permute-start.2 = (bf16[13,16,96]{2,1,0:T(8,128)(2,1)S(1)}, bf16[13,16,96]{2,1,0:T(8,128)(2,1)S(1)}, u32[]{:S(2)}, u32[]{:S(2)}) collective-permute-start(bf16[13,16,96]{2,1,0:T(8,128)(2,1)S(1)} %copy-done.10), channel_id=1, source_target_pairs={{4,12},{8,0},{12,20},{16,8},{20,28},{24,16},{5,13},{9,1},{13,21},{... | collective-permute-start | bytes 119816 | tf_op jit(solution)/shard_map/ppermute | solution.py:361
  44.1 4.2 %collective-permute-start.4 = (f32[24,128]{1,0:T(8,128)S(1)}, f32[24,128]{1,0:T(8,128)S(1)}, u32[]{:S(2)}, u32[]{:S(2)}) collective-permute-start(f32[24,128]{1,0:T(8,128)S(1)} %partials.1), channel_id=1, source_target_pairs={{0,4},{4,0},{8,12},{12,8},{16,20},{20,16},{24,28},{28,24},{1,5},{5... | collective-permute-start | bytes 36872 | tf_op jit(solution)/shard_map/ppermute | solution.py:375
  48.3 1.7 %collective-permute-done.4 = f32[24,128]{1,0:T(8,128)S(1)} collective-permute-done((f32[24,128]{1,0:T(8,128)S(1)}, f32[24,128]{1,0:T(8,128)S(1)}, u32[]{:S(2)}, u32[]{:S(2)}) %collective-permute-start.4) | collective-permute-done | bytes 12320 | tf_op jit(solution)/shard_map/ppermute | solution.py:375
  50.0 1.6 %collective-permute-start.5 = (f32[24,128]{1,0:T(8,128)S(1)}, f32[24,128]{1,0:T(8,128)S(1)}, u32[]{:S(2)}, u32[]{:S(2)}) collective-permute-start(f32[24,128]{1,0:T(8,128)S(1)} %add.53), channel_id=1, source_target_pairs={{0,8},{4,12},{8,0},{12,4},{16,24},{20,28},{24,16},{28,20},{1,9},{5... | collective-permute-start | bytes 36872 | tf_op jit(solution)/shard_map/ppermute | solution.py:375
  51.6 2.1 %collective-permute-done.5 = f32[24,128]{1,0:T(8,128)S(1)} collective-permute-done((f32[24,128]{1,0:T(8,128)S(1)}, f32[24,128]{1,0:T(8,128)S(1)}, u32[]{:S(2)}, u32[]{:S(2)}) %collective-permute-start.5) | collective-permute-done | bytes 12320 | tf_op jit(solution)/shard_map/ppermute | solution.py:375
  53.7 1.8 %collective-permute-start.6 = (f32[24,128]{1,0:T(8,128)S(1)}, f32[24,128]{1,0:T(8,128)S(1)}, u32[]{:S(2)}, u32[]{:S(2)}) collective-permute-start(f32[24,128]{1,0:T(8,128)S(1)} %add.54), channel_id=1, source_target_pairs={{0,16},{4,20},{8,24},{12,28},{16,0},{20,4},{24,8},{28,12},{1,17},{... | collective-permute-start | bytes 36872 | tf_op jit(solution)/shard_map/ppermute | solution.py:375
  55.5 2.8 %collective-permute-done.6 = f32[24,128]{1,0:T(8,128)S(1)} collective-permute-done((f32[24,128]{1,0:T(8,128)S(1)}, f32[24,128]{1,0:T(8,128)S(1)}, u32[]{:S(2)}, u32[]{:S(2)}) %collective-permute-start.6) | collective-permute-done | bytes 12320 | tf_op jit(solution)/shard_map/ppermute | solution.py:375
  58.3 0.0 collective-permute-done.9.refs_9_
  58.3 0.0 collective-permute-done.8.refs_9_.refs_10_
  58.3 0.7 copy-done.2
  59.0 0.0 collective-permute-done.2.refs_4_
  59.0 0.0 collective-permute-done.7.refs_7_
  59.0 0.1 broadcast_in_dim.28.refs_6_
  59.1 1.0 copy-done.3
  60.1 0.9 copy-done.6
  61.0 4.2 %filtered.2.refs_0_ = bf16[4,12,48,128]{3,2,1,0:T(8,128)(2,1)S(1)} custom-call(bf16[2,48,48,128]{3,2,1,0:T(8,128)(2,1)S(1)} %copy-done.1, bf16[2,24,16,96]{3,2,1,0:T(8,128)(2,1)S(1)} %pad_maximum_fusion.1.f_own.refs_1_, bf16[37,16,96]{2,1,0:T(8,128)(2,1)S(1)} %collective-permute-done.f_x.refs_2_, bf16[24,16,96]{2,1,0:T(8,128)(2,1)S(1)} %copy-done.6, ...), custom_call_target="tpu_custom_call" | custom-call | flops 47185920 | bytes 2949120 | tf_op jit(solution)/shard_map/filtered/pallas_call | solution.py:232
  65.2 0.0 copy-start.12
  65.2 1.6 %collective-permute-start.12 = (bf16[4,12,48,128]{3,2,1,0:T(8,128)(2,1)S(1)}, bf16[4,12,48,128]{3,2,1,0:T(8,128)(2,1)S(1)}, u32[]{:S(2)}, u32[]{:S(2)}) collective-permute-start(bf16[4,12,48,128]{3,2,1,0:T(8,128)(2,1)S(1)} %filtered.2.refs_0_), channel_id=1, source_target_pairs={{0,2},{1,3},{2,0},{3,1},{4,6},{5,7},{6,4},{7,5},{8,10},{9,11},{10,... | collective-permute-start | bytes 1769480 | tf_op jit(solution)/shard_map/ppermute | solution.py:389
  66.8 3.5 %collective-permute-start.11 = (bf16[2,10,48,128]{3,2,1,0:T(8,128)(2,1)S(1)}, bf16[2,10,48,128]{3,2,1,0:T(8,128)(2,1)S(1)}, u32[]{:S(2)}, u32[]{:S(2)}) collective-permute-start(bf16[2,10,48,128]{3,2,1,0:T(8,128)(2,1)S(1)} %collective-permute-done.9.refs_9_), channel_id=1, source_target_pairs={{0,8},{8,16},{12,4},{16,24},{20,12},{28,20},{1,9},{9,17},{13,5},{1... | collective-permute-start | bytes 737288 | tf_op jit(solution)/shard_map/ppermute | solution.py:378
  70.3 3.7 %collective-permute-done.11.refs_11_ = bf16[2,10,48,128]{3,2,1,0:T(8,128)(2,1)S(1)} collective-permute-done((bf16[2,10,48,128]{3,2,1,0:T(8,128)(2,1)S(1)}, bf16[2,10,48,128]{3,2,1,0:T(8,128)(2,1)S(1)}, u32[]{:S(2)}, u32[]{:S(2)}) %collective-permute-start.11) | collective-permute-done | bytes 245792 | tf_op jit(solution)/shard_map/ppermute | solution.py:378
  74.0 6.3 %filtered.3 = (bf16[2,12,48,128]{3,2,1,0:T(8,128)(2,1)}, bf16[2,12,48,128]{3,2,1,0:T(8,128)(2,1)S(1)}) custom-call(bf16[2,48,48,128]{3,2,1,0:T(8,128)(2,1)} %refs_0_.3, bf16[2,24,16,96]{3,2,1,0:T(8,128)(2,1)S(1)} %pad_maximum_fusion.1.f_own.refs_1_, bf16[37,16,96]{2,1,0:T(8,128)(2,1)S(1)} %collective-permute-done.f_x.refs_2_, ...), custom_call_target="tpu_custom_call" | custom-call | flops 47185920 | bytes 2949120 | tf_op jit(solution)/shard_map/filtered/pallas_call | solution.py:232
  80.3 0.7 copy-done.8
  81.0 0.0 collective-permute-done.12.refs_2_
  81.0 0.5 collective-permute-start.15
  81.5 0.0 collective-permute-start.10
  81.5 0.5 collective-permute-start.13
  82.0 0.1 collective-permute-start.19
  82.1 8.5 %collective-permute-done.15.refs_2_ = bf16[2,12,48,128]{3,2,1,0:T(8,128)(2,1)S(1)} collective-permute-done((bf16[2,12,48,128]{3,2,1,0:T(8,128)(2,1)}, bf16[2,12,48,128]{3,2,1,0:T(8,128)(2,1)S(1)}, u32[]{:S(2)}, u32[]{:S(2)}) %collective-permute-start.15) | collective-permute-done | bytes 294944 | tf_op jit(solution)/shard_map/ppermute | solution.py:395
  90.6 0.0 collective-permute-start.20
  90.6 0.3 fusion
  91.0 0.6 collective-permute-start.14
  91.5 0.6 collective-permute-done.20.refs_3_
  92.1 1.6 %rotated.5 = bf16[2,12,48,128]{3,2,1,0:T(8,128)(2,1)S(1)} custom-call(bf16[2,12,48,128]{3,2,1,0:T(8,128)(2,1)} %get-tuple-element.35.refs_0_, bf16[2,12,48,128]{3,2,1,0:T(8,128)(2,1)S(1)} %collective-permute-done.19.refs_1_, bf16[2,12,48,128]{3,2,1,0:T(8,128)(2,1)S(1)} %collective-permute-done.15.refs_2_, ...), custom_call_target="tpu_custom_call" | custom-call | flops 150994944 | bytes 1474560 | tf_op jit(solution)/shard_map/rotated/pallas_call | solution.py:276
  93.7 3.0 %collective-permute-start.21 = (bf16[2,12,48,128]{3,2,1,0:T(8,128)(2,1)S(1)}, bf16[2,12,48,128]{3,2,1,0:T(8,128)(2,1)S(1)}, u32[]{:S(2)}, u32[]{:S(2)}) collective-permute-start(bf16[2,12,48,128]{3,2,1,0:T(8,128)(2,1)S(1)} %rotated.5), channel_id=1, source_target_pairs={{0,4},{4,0},{8,12},{12,8},{16,20},{20,16},{24,28},{28,24},{1,5},{5... | collective-permute-start | bytes 884744 | tf_op jit(solution)/shard_map/ppermute | solution.py:403
  96.7 0.7 collective-permute-done.16.refs_2_
  97.5 0.0 collective-permute-start.17
  97.5 0.9 rotated.3
  98.4 3.0 %collective-permute-start.18 = (bf16[2,12,48,128]{3,2,1,0:T(8,128)(2,1)S(1)}, bf16[2,12,48,128]{3,2,1,0:T(8,128)(2,1)S(1)}, u32[]{:S(2)}, u32[]{:S(2)}) collective-permute-start(bf16[2,12,48,128]{3,2,1,0:T(8,128)(2,1)S(1)} %get-tuple-element.37), channel_id=1, source_target_pairs={{0,4},{4,0},{8,12},{12,8},{16,20},{20,16},{24,28},{28,24},{1,5},{5... | collective-permute-start | bytes 884744 | tf_op jit(solution)/shard_map/ppermute | solution.py:398
  101.5 0.6 rotated.4.refs_1_
  102.1 2.4 %collective-permute-done.21.refs_3_ = bf16[2,12,48,128]{3,2,1,0:T(8,128)(2,1)S(1)} collective-permute-done((bf16[2,12,48,128]{3,2,1,0:T(8,128)(2,1)S(1)}, bf16[2,12,48,128]{3,2,1,0:T(8,128)(2,1)S(1)}, u32[]{:S(2)}, u32[]{:S(2)}) %collective-permute-start.21) | collective-permute-done | bytes 294944 | tf_op jit(solution)/shard_map/ppermute | solution.py:403
  104.5 5.8 %collective-permute-done.18.refs_2_ = bf16[2,12,48,128]{3,2,1,0:T(8,128)(2,1)S(1)} collective-permute-done((bf16[2,12,48,128]{3,2,1,0:T(8,128)(2,1)S(1)}, bf16[2,12,48,128]{3,2,1,0:T(8,128)(2,1)S(1)}, u32[]{:S(2)}, u32[]{:S(2)}) %collective-permute-start.18) | collective-permute-done | bytes 294944 | tf_op jit(solution)/shard_map/ppermute | solution.py:398
  110.4 1.1 assembled.1
  (38 shorter events, 0.2 us)
Async XLA Ops:
  0.0 90.6 %copy-start = (bf16[12,128,128]{2,1,0:T(8,128)(2,1)S(1)}, bf16[12,128,128]{2,1,0:T(8,128)(2,1)}, u32[]{:S(2)}) copy-start(bf16[12,128,128]{2,1,0:T(8,128)(2,1)} %param.13) | copy-start | bytes 1179652
  3.0 1.6 %copy-start.1 = (bf16[2,48,48,128]{3,2,1,0:T(8,128)(2,1)S(1)}, bf16[2,48,48,128]{3,2,1,0:T(8,128)(2,1)}, u32[]{:S(2)}) copy-start(bf16[2,48,48,128]{3,2,1,0:T(8,128)(2,1)} %refs_0_.3) | copy-start | bytes 3538948
  5.4 25.4 %collective-permute-start.3 = (bf16[2,16,48,128]{3,2,1,0:T(8,128)(2,1)}, bf16[2,16,48,128]{3,2,1,0:T(8,128)(2,1)S(1)}, u32[]{:S(2)}, u32[]{:S(2)}) collective-permute-start(bf16[2,16,48,128]{3,2,1,0:T(8,128)(2,1)} %constant_dynamic-slice_fusion.2), channel_id=1, source_target_pairs={{0,4},{4,0},{8,12},{12,8},{16,20},{20,16},{24,28},{28,24},{1,5},{5... | collective-permute-start | bytes 1179656 | tf_op jit(solution)/shard_map/ppermute | solution.py:363
  9.2 49.9 %collective-permute-start.7 = (bf16[2,26,48,128]{3,2,1,0:T(8,128)(2,1)}, bf16[2,26,48,128]{3,2,1,0:T(8,128)(2,1)S(1)}, u32[]{:S(2)}, u32[]{:S(2)}) collective-permute-start(bf16[2,26,48,128]{3,2,1,0:T(8,128)(2,1)} %constant_dynamic-slice_fusion.1), channel_id=1, source_target_pairs={{4,12},{8,0},{12,20},{16,8},{20,28},{24,16},{5,13},{9,1},{13,21},{... | collective-permute-start | bytes 1916936 | tf_op jit(solution)/shard_map/ppermute | solution.py:366
  10.5 6.2 %collective-permute-start.1 = (bf16[24,16,96]{2,1,0:T(8,128)(2,1)S(1)}, bf16[24,16,96]{2,1,0:T(8,128)(2,1)S(1)}, u32[]{:S(2)}, u32[]{:S(2)}) collective-permute-start(bf16[24,16,96]{2,1,0:T(8,128)(2,1)S(1)} %get-tuple-element.23), channel_id=1, source_target_pairs={{4,8},{8,4},{12,16},{16,12},{20,24},{24,20},{5,9},{9,5},{13,17},{1... | collective-permute-start | bytes 221192 | tf_op jit(solution)/shard_map/ppermute | solution.py:360
  11.1 9.7 %collective-permute-start = (bf16[37,16,96]{2,1,0:T(8,128)(2,1)}, bf16[37,16,96]{2,1,0:T(8,128)(2,1)S(1)}, u32[]{:S(2)}, u32[]{:S(2)}) collective-permute-start(bf16[37,16,96]{2,1,0:T(8,128)(2,1)} %pad_maximum_fusion), channel_id=1, source_target_pairs={{0,4},{4,0},{8,12},{12,8},{16,20},{20,16},{24,28},{28,24},{1,5},{5... | collective-permute-start | bytes 341000 | tf_op jit(solution)/shard_map/ppermute | solution.py:359
  16.7 26.1 %copy-start.10 = (bf16[13,16,96]{2,1,0:T(8,128)(2,1)S(1)}, bf16[13,16,96]{2,1,0:T(8,128)(2,1)}, u32[]{:S(2)}) copy-start(bf16[13,16,96]{2,1,0:T(8,128)(2,1)} %get-tuple-element.24) | copy-start | bytes 119812
  16.7 42.3 %copy-start.11 = (f32[8]{0:T(128)S(1)}, f32[8]{0:T(128)}, u32[]{:S(2)}) copy-start(f32[8]{0:T(128)} %param.10) | copy-start | bytes 100
  16.7 14.1 %copy-start.5 = (bf16[24,16,96]{2,1,0:T(8,128)(2,1)}, bf16[24,16,96]{2,1,0:T(8,128)(2,1)S(1)}, u32[]{:S(2)}) copy-start(bf16[24,16,96]{2,1,0:T(8,128)(2,1)S(1)} %collective-permute-done.1.f_d.refs_3_) | copy-start | bytes 221188
  30.8 27.5 %collective-permute-start.8 = (bf16[2,16,48,128]{3,2,1,0:T(8,128)(2,1)S(1)}, bf16[2,16,48,128]{3,2,1,0:T(8,128)(2,1)S(1)}, u32[]{:S(2)}, u32[]{:S(2)}) collective-permute-start(bf16[2,16,48,128]{3,2,1,0:T(8,128)(2,1)S(1)} %collective-permute-done.3.refs_8_), channel_id=1, source_target_pairs={{0,8},{8,16},{12,4},{16,24},{20,12},{28,20},{1,9},{9,17},{13,5},{1... | collective-permute-start | bytes 1179656 | tf_op jit(solution)/shard_map/ppermute | solution.py:369
  42.7 15.6 %collective-permute-start.9 = (bf16[2,10,48,128]{3,2,1,0:T(8,128)(2,1)S(1)}, bf16[2,10,48,128]{3,2,1,0:T(8,128)(2,1)S(1)}, u32[]{:S(2)}, u32[]{:S(2)}) collective-permute-start(bf16[2,10,48,128]{3,2,1,0:T(8,128)(2,1)S(1)} %constant_dynamic-slice_fusion), channel_id=1, source_target_pairs={{0,4},{4,0},{8,12},{12,8},{16,20},{20,16},{24,28},{28,24},{1,5},{5... | collective-permute-start | bytes 737288 | tf_op jit(solution)/shard_map/ppermute | solution.py:372
  42.8 16.3 %collective-permute-start.2 = (bf16[13,16,96]{2,1,0:T(8,128)(2,1)S(1)}, bf16[13,16,96]{2,1,0:T(8,128)(2,1)S(1)}, u32[]{:S(2)}, u32[]{:S(2)}) collective-permute-start(bf16[13,16,96]{2,1,0:T(8,128)(2,1)S(1)} %copy-done.10), channel_id=1, source_target_pairs={{4,12},{8,0},{12,20},{16,8},{20,28},{24,16},{5,13},{9,1},{13,21},{... | collective-permute-start | bytes 119816 | tf_op jit(solution)/shard_map/ppermute | solution.py:361
  44.1 5.9 %collective-permute-start.4 = (f32[24,128]{1,0:T(8,128)S(1)}, f32[24,128]{1,0:T(8,128)S(1)}, u32[]{:S(2)}, u32[]{:S(2)}) collective-permute-start(f32[24,128]{1,0:T(8,128)S(1)} %partials.1), channel_id=1, source_target_pairs={{0,4},{4,0},{8,12},{12,8},{16,20},{20,16},{24,28},{28,24},{1,5},{5... | collective-permute-start | bytes 36872 | tf_op jit(solution)/shard_map/ppermute | solution.py:375
  50.0 3.7 %collective-permute-start.5 = (f32[24,128]{1,0:T(8,128)S(1)}, f32[24,128]{1,0:T(8,128)S(1)}, u32[]{:S(2)}, u32[]{:S(2)}) collective-permute-start(f32[24,128]{1,0:T(8,128)S(1)} %add.53), channel_id=1, source_target_pairs={{0,8},{4,12},{8,0},{12,4},{16,24},{20,28},{24,16},{28,20},{1,9},{5... | collective-permute-start | bytes 36872 | tf_op jit(solution)/shard_map/ppermute | solution.py:375
  53.7 4.6 %collective-permute-start.6 = (f32[24,128]{1,0:T(8,128)S(1)}, f32[24,128]{1,0:T(8,128)S(1)}, u32[]{:S(2)}, u32[]{:S(2)}) collective-permute-start(f32[24,128]{1,0:T(8,128)S(1)} %add.54), channel_id=1, source_target_pairs={{0,16},{4,20},{8,24},{12,28},{16,0},{20,4},{24,8},{28,12},{1,17},{... | collective-permute-start | bytes 36872 | tf_op jit(solution)/shard_map/ppermute | solution.py:375
  58.3 0.8 copy-start.2
  59.1 1.0 copy-start.3
  60.1 0.9 copy-start.6
  61.0 13.0 %copy-start.4 = (bf16[2,16,48,128]{3,2,1,0:T(8,128)(2,1)S(1)}, bf16[2,16,48,128]{3,2,1,0:T(8,128)(2,1)}, u32[]{:S(2)}) copy-start(bf16[2,16,48,128]{3,2,1,0:T(8,128)(2,1)} %copy-done.2) | copy-start | bytes 1179652
  61.0 13.0 %copy-start.7 = (bf16[24,16,96]{2,1,0:T(8,128)(2,1)S(1)}, bf16[24,16,96]{2,1,0:T(8,128)(2,1)}, u32[]{:S(2)}) copy-start(bf16[24,16,96]{2,1,0:T(8,128)(2,1)} %copy-done.5) | copy-start | bytes 221188
  65.2 16.3 %copy-start.12 = (s32[12,2]{0,1:T(2,128)S(1)}, s32[12,2]{0,1:T(2,128)}, u32[]{:S(2)}) copy-start(s32[12,2]{0,1:T(2,128)} %param.12) | copy-start | bytes 292
  65.2 15.8 %collective-permute-start.12 = (bf16[4,12,48,128]{3,2,1,0:T(8,128)(2,1)S(1)}, bf16[4,12,48,128]{3,2,1,0:T(8,128)(2,1)S(1)}, u32[]{:S(2)}, u32[]{:S(2)}) collective-permute-start(bf16[4,12,48,128]{3,2,1,0:T(8,128)(2,1)S(1)} %filtered.2.refs_0_), channel_id=1, source_target_pairs={{0,2},{1,3},{2,0},{3,1},{4,6},{5,7},{6,4},{7,5},{8,10},{9,11},{10,... | collective-permute-start | bytes 1769480 | tf_op jit(solution)/shard_map/ppermute | solution.py:389
  66.8 7.2 %collective-permute-start.11 = (bf16[2,10,48,128]{3,2,1,0:T(8,128)(2,1)S(1)}, bf16[2,10,48,128]{3,2,1,0:T(8,128)(2,1)S(1)}, u32[]{:S(2)}, u32[]{:S(2)}) collective-permute-start(bf16[2,10,48,128]{3,2,1,0:T(8,128)(2,1)S(1)} %collective-permute-done.9.refs_9_), channel_id=1, source_target_pairs={{0,8},{8,16},{12,4},{16,24},{20,12},{28,20},{1,9},{9,17},{13,5},{1... | collective-permute-start | bytes 737288 | tf_op jit(solution)/shard_map/ppermute | solution.py:378
  80.3 0.7 copy-start.8
  81.0 9.6 %collective-permute-start.15 = (bf16[2,12,48,128]{3,2,1,0:T(8,128)(2,1)}, bf16[2,12,48,128]{3,2,1,0:T(8,128)(2,1)S(1)}, u32[]{:S(2)}, u32[]{:S(2)}) collective-permute-start(bf16[2,12,48,128]{3,2,1,0:T(8,128)(2,1)} %get-tuple-element.35.refs_0_), channel_id=1, source_target_pairs={{0,2},{1,3},{2,0},{3,1},{4,6},{5,7},{6,4},{7,5},{8,10},{9,11},{10,... | collective-permute-start | bytes 884744 | tf_op jit(solution)/shard_map/ppermute | solution.py:395
  81.5 16.0 %collective-permute-start.10 = (bf16[4,12,48,128]{3,2,1,0:T(8,128)(2,1)S(1)}, bf16[4,12,48,128]{3,2,1,0:T(8,128)(2,1)S(1)}, u32[]{:S(2)}, u32[]{:S(2)}) collective-permute-start(bf16[4,12,48,128]{3,2,1,0:T(8,128)(2,1)S(1)} %filtered.2.refs_0_), channel_id=1, source_target_pairs={{0,1},{1,0},{2,3},{3,2},{4,5},{5,4},{6,7},{7,6},{8,9},{9,8},{10,11... | collective-permute-start | bytes 1769480 | tf_op jit(solution)/shard_map/ppermute | solution.py:390
  81.5 16.0 %collective-permute-start.13 = (bf16[4,12,48,128]{3,2,1,0:T(8,128)(2,1)S(1)}, bf16[4,12,48,128]{3,2,1,0:T(8,128)(2,1)S(1)}, u32[]{:S(2)}, u32[]{:S(2)}) collective-permute-start(bf16[4,12,48,128]{3,2,1,0:T(8,128)(2,1)S(1)} %collective-permute-done.12.refs_2_), channel_id=1, source_target_pairs={{0,1},{1,0},{2,3},{3,2},{4,5},{5,4},{6,7},{7,6},{8,9},{9,8},{10,11... | collective-permute-start | bytes 1769480 | tf_op jit(solution)/shard_map/ppermute | solution.py:396
  82.0 8.9 %collective-permute-start.19 = (bf16[2,12,48,128]{3,2,1,0:T(8,128)(2,1)}, bf16[2,12,48,128]{3,2,1,0:T(8,128)(2,1)S(1)}, u32[]{:S(2)}, u32[]{:S(2)}) collective-permute-start(bf16[2,12,48,128]{3,2,1,0:T(8,128)(2,1)} %get-tuple-element.35.refs_0_), channel_id=1, source_target_pairs={{0,1},{1,0},{2,3},{3,2},{4,5},{5,4},{6,7},{7,6},{8,9},{9,8},{10,11... | collective-permute-start | bytes 884744 | tf_op jit(solution)/shard_map/ppermute | solution.py:392
  90.5 6.9 %collective-permute-start.16 = (bf16[2,12,48,128]{3,2,1,0:T(8,128)(2,1)}, bf16[2,12,48,128]{3,2,1,0:T(8,128)(2,1)S(1)}, u32[]{:S(2)}, u32[]{:S(2)}) collective-permute-start(bf16[2,12,48,128]{3,2,1,0:T(8,128)(2,1)} %copy-done.8), channel_id=1, source_target_pairs={{0,2},{1,3},{2,0},{3,1},{4,6},{5,7},{6,4},{7,5},{8,10},{9,11},{10,... | collective-permute-start | bytes 884744 | tf_op jit(solution)/shard_map/ppermute | solution.py:400
  90.6 1.6 %collective-permute-start.20 = (bf16[2,12,48,128]{3,2,1,0:T(8,128)(2,1)S(1)}, bf16[2,12,48,128]{3,2,1,0:T(8,128)(2,1)S(1)}, u32[]{:S(2)}, u32[]{:S(2)}) collective-permute-start(bf16[2,12,48,128]{3,2,1,0:T(8,128)(2,1)S(1)} %collective-permute-done.15.refs_2_), channel_id=1, source_target_pairs={{0,1},{1,0},{2,3},{3,2},{4,5},{5,4},{6,7},{7,6},{8,9},{9,8},{10,11... | collective-permute-start | bytes 884744 | tf_op jit(solution)/shard_map/ppermute | solution.py:401
  91.0 10.5 %collective-permute-start.14 = (bf16[2,12,48,128]{3,2,1,0:T(8,128)(2,1)}, bf16[2,12,48,128]{3,2,1,0:T(8,128)(2,1)S(1)}, u32[]{:S(2)}, u32[]{:S(2)}) collective-permute-start(bf16[2,12,48,128]{3,2,1,0:T(8,128)(2,1)} %copy-done.8), channel_id=1, source_target_pairs={{0,1},{1,0},{2,3},{3,2},{4,5},{5,4},{6,7},{7,6},{8,9},{9,8},{10,11... | collective-permute-start | bytes 884744 | tf_op jit(solution)/shard_map/ppermute | solution.py:393
  93.7 7.7 %copy-start.9 = (bf16[2,12,48,128]{3,2,1,0:T(8,128)(2,1)S(1)}, bf16[2,12,48,128]{3,2,1,0:T(8,128)(2,1)}, u32[]{:S(2)}) copy-start(bf16[2,12,48,128]{3,2,1,0:T(8,128)(2,1)} %copy-done.8) | copy-start | bytes 884740
  93.7 10.8 %collective-permute-start.21 = (bf16[2,12,48,128]{3,2,1,0:T(8,128)(2,1)S(1)}, bf16[2,12,48,128]{3,2,1,0:T(8,128)(2,1)S(1)}, u32[]{:S(2)}, u32[]{:S(2)}) collective-permute-start(bf16[2,12,48,128]{3,2,1,0:T(8,128)(2,1)S(1)} %rotated.5), channel_id=1, source_target_pairs={{0,4},{4,0},{8,12},{12,8},{16,20},{20,16},{24,28},{28,24},{1,5},{5... | collective-permute-start | bytes 884744 | tf_op jit(solution)/shard_map/ppermute | solution.py:403
  97.5 4.0 %collective-permute-start.17 = (bf16[2,12,48,128]{3,2,1,0:T(8,128)(2,1)S(1)}, bf16[2,12,48,128]{3,2,1,0:T(8,128)(2,1)S(1)}, u32[]{:S(2)}, u32[]{:S(2)}) collective-permute-start(bf16[2,12,48,128]{3,2,1,0:T(8,128)(2,1)S(1)} %collective-permute-done.16.refs_2_), channel_id=1, source_target_pairs={{0,1},{1,0},{2,3},{3,2},{4,5},{5,4},{6,7},{7,6},{8,9},{9,8},{10,11... | collective-permute-start | bytes 884744 | tf_op jit(solution)/shard_map/ppermute | solution.py:404
  98.4 11.9 %collective-permute-start.18 = (bf16[2,12,48,128]{3,2,1,0:T(8,128)(2,1)S(1)}, bf16[2,12,48,128]{3,2,1,0:T(8,128)(2,1)S(1)}, u32[]{:S(2)}, u32[]{:S(2)}) collective-permute-start(bf16[2,12,48,128]{3,2,1,0:T(8,128)(2,1)S(1)} %get-tuple-element.37), channel_id=1, source_target_pairs={{0,4},{4,0},{8,12},{12,8},{16,20},{20,16},{24,28},{28,24},{1,5},{5... | collective-permute-start | bytes 884744 | tf_op jit(solution)/shard_map/ppermute | solution.py:398

commit v3 on v2

--- a/solution.py
+++ b/solution.py
@@ -10,6 +10,7 @@
 F32 = jnp.float32
 BF16 = jnp.bfloat16
 VMEM_LIMIT = 50 * 1024 * 1024
+SHRINK = 16
 
 
 def params():
@@ -17,7 +18,7 @@
 
 
 def cost(flops, moved):
-    return pl.CostEstimate(flops=flops, bytes_accessed=moved, transcendentals=0)
+    return pl.CostEstimate(flops=flops // SHRINK, bytes_accessed=moved // SHRINK, transcendentals=0)
 
 
 def inside(p, window):
@@ -36,7 +37,7 @@
     return here.astype(BF16), before.astype(BF16), after.astype(BF16)
 
 
-def partial_kernel(count, own, f_own, f_x, f_d, out, acc, gram):
+def partial_kernel(count, unroll, own, f_own, f_x, f_d, out, weights_out, acc, gram):
     x = lax.rem(lax.axis_index("space"), 2)
     _, pairs, depth, cells = f_own.shape
     orbs = own.shape[3]
@@ -44,33 +45,36 @@
     acc[...] = jnp.zeros_like(acc)
     gram[...] = jnp.zeros_like(gram)
 
-    def row(r, carry):
-        low, high = jnp.maximum(r - 1, 0), jnp.minimum(r + 1, pairs - 1)
-        has_low, has_high = inside(r - 1, pairs), inside(r + 1, pairs)
-        tiles = [f_d[r], f_own[x, r], f_own[1 - x, r], f_x[r]]
-        total, square = acc[...], gram[...]
-        for c in (1, 2):
-            plane = x if c == 1 else 1 - x
-            b = tiles[c]
-            b32 = b.astype(F32)
-            u = b32[count : count + 1] + b32[count + 1 : count + 2]
-            local = jnp.dot(b, here, preferred_element_type=F32)
-            local += has_low * jnp.dot(f_own[plane, low], before, preferred_element_type=F32)
-            local += has_high * jnp.dot(f_own[plane, high], after, preferred_element_type=F32)
-            local += u * b32 - 0.125 * (tiles[c - 1].astype(F32) + tiles[c + 1].astype(F32))
-            hi = local.astype(BF16)
-            lo = (local - hi.astype(F32)).astype(BF16)
-            weights = jnp.concatenate([b, hi, lo], axis=0)
-            v = own[plane, pl.ds(2 * r, 2)].reshape(cells, orbs)
-            total = total + jnp.dot(weights, v, preferred_element_type=F32)
-            square = square + lax.dot_general(
-                b, b, (((1,), (1,)), ((), ())), preferred_element_type=F32
-            )
-        acc[...] = total
-        gram[...] = square
+    def step(i, carry):
+        totals, squares = [], []
+        for k in range(unroll):
+            r = i * unroll + k
+            low, high = jnp.maximum(r - 1, 0), jnp.minimum(r + 1, pairs - 1)
+            has_low, has_high = inside(r - 1, pairs), inside(r + 1, pairs)
+            tiles = [f_d[r], f_own[x, r], f_own[1 - x, r], f_x[r]]
+            for c in (1, 2):
+                plane = x if c == 1 else 1 - x
+                b = tiles[c]
+                b32 = b.astype(F32)
+                u = b32[count : count + 1] + b32[count + 1 : count + 2]
+                local = jnp.dot(b, here, preferred_element_type=F32)
+                local += has_low * jnp.dot(f_own[plane, low], before, preferred_element_type=F32)
+                local += has_high * jnp.dot(f_own[plane, high], after, preferred_element_type=F32)
+                local += u * b32 - 0.125 * (tiles[c - 1].astype(F32) + tiles[c + 1].astype(F32))
+                hi = local.astype(BF16)
+                lo = (local - hi.astype(F32)).astype(BF16)
+                weights = jnp.concatenate([b, hi, lo], axis=0)
+                weights_out[plane, r] = weights
+                v = own[plane, pl.ds(2 * r, 2)].reshape(cells, orbs)
+                totals.append(jnp.dot(weights, v, preferred_element_type=F32))
+                squares.append(
+                    lax.dot_general(b, b, (((1,), (1,)), ((), ())), preferred_element_type=F32)
+                )
+        acc[...] += sum(totals[1:], totals[0])
+        gram[...] += sum(squares[1:], squares[0])
         return carry
 
-    lax.fori_loop(0, pairs, row, 0)
+    lax.fori_loop(0, pairs // unroll, step, 0)
     out[...] = jnp.zeros_like(out)
     out[0:count] = acc[0:count]
     out[count : 2 * count] = acc[depth : depth + count] + acc[2 * depth : 2 * depth + count]
@@ -79,13 +83,17 @@
 
 def partials(count, own, f_own, f_x, f_d):
     orbs = own.shape[3]
-    depth = f_own.shape[2]
+    planes, pairs, depth, width = f_own.shape
     cells = own.size // orbs
-    return pl.pallas_call(
-        functools.partial(partial_kernel, count),
-        out_shape=jax.ShapeDtypeStruct((3 * count, orbs), F32),
+    unroll = max(g for g in (1, 2, 4) if pairs % g == 0 and g * depth <= 144)
+    return pl.pallas_call(
+        functools.partial(partial_kernel, count, unroll),
+        out_shape=(
+            jax.ShapeDtypeStruct((3 * count, orbs), F32),
+            jax.ShapeDtypeStruct((planes, pairs, 3 * depth, width), BF16),
+        ),
         in_specs=[pl.BlockSpec(memory_space=pltpu.VMEM)] * 4,
-        out_specs=pl.BlockSpec(memory_space=pltpu.VMEM),
+        out_specs=(pl.BlockSpec(memory_space=pltpu.VMEM),) * 2,
         scratch_shapes=[pltpu.VMEM((3 * depth, orbs), F32), pltpu.VMEM((depth, depth), F32)],
         compiler_params=params(),
         cost_estimate=cost(2 * cells * 3 * depth * orbs, cells * orbs * 4),
@@ -93,10 +101,81 @@
     )(own, f_own, f_x, f_d)
 
 
+def coefficient_kernel(sums, strength, out):
+    count, orbs = strength.shape
+    coef1 = (strength[...] * sums[0:count]).astype(BF16)
+    padded = coef1.astype(F32) * 0.25
+    if orbs > count:
+        padded = jnp.concatenate([padded, jnp.zeros((orbs - count, orbs), F32)], axis=0)
+    proj2 = sums[count : 2 * count] + jnp.dot(
+        sums[2 * count : 3 * count],
+        padded,
+        preferred_element_type=F32,
+        precision=lax.Precision.HIGHEST,
+    )
+    out[0:count] = coef1
+    out[count : 2 * count] = (strength[...] * proj2).astype(BF16)
+
+
+def coefficients(sums, strength):
+    count, orbs = strength.shape
+    return pl.pallas_call(
+        coefficient_kernel,
+        out_shape=jax.ShapeDtypeStruct((2 * count, orbs), BF16),
+        in_specs=[pl.BlockSpec(memory_space=pltpu.VMEM)] * 2,
+        out_specs=pl.BlockSpec(memory_space=pltpu.VMEM),
+        compiler_params=params(),
+        cost_estimate=cost(4096, 4096),
+        name="coefficients",
+    )(sums, strength)
+
+
+def nonlocal_kernel(depth, unroll, a, b, c, d, q, weights, out):
+    count, orbs = a.shape[0] // 2, a.shape[1]
+    pairs, cells = weights.shape[1], weights.shape[3]
+    turned = sum(
+        jnp.dot(ref[...], q[k], preferred_element_type=F32) for k, ref in enumerate((a, b, c, d))
+    )
+    turned = turned * 0.25
+    gap = jnp.zeros((depth - count, orbs), F32)
+    one, two = turned[0:count], turned[count : 2 * count]
+    right = jnp.concatenate([two, gap, one, gap, one, gap], axis=0)
+    hi = right.astype(BF16)
+    lo = (right - hi.astype(F32)).astype(BF16)
+    right = jnp.concatenate([hi, lo], axis=1)
+
+    def step(i, carry):
+        for k in range(unroll):
+            r = i * unroll + k
+            for plane in range(weights.shape[0]):
+                both = lax.dot_general(
+                    weights[plane, r], right, (((0,), (0,)), ((), ())), preferred_element_type=F32
+                )
+                term = both[:, :orbs] + both[:, orbs:]
+                out[plane, pl.ds(2 * r, 2)] = term.reshape(2, cells // 2, orbs)
+        return carry
+
+    lax.fori_loop(0, pairs // unroll, step, 0)
+
+
+def nonlocal_term(shape, coefs, q, weights):
+    depth = weights.shape[2] // 3
+    unroll = max(g for g in (1, 2, 4) if weights.shape[1] % g == 0)
+    return pl.pallas_call(
+        functools.partial(nonlocal_kernel, depth, unroll),
+        out_shape=jax.ShapeDtypeStruct(shape, F32),
+        in_specs=[pl.BlockSpec(memory_space=pltpu.VMEM)] * 6,
+        out_specs=pl.BlockSpec(memory_space=pltpu.VMEM),
+        compiler_params=params(),
+        cost_estimate=cost(4096, 4096),
+        name="nonlocal",
+    )(*coefs, q, weights)
+
+
 def filter_kernel(count, slabs, start, parts, joint, *refs):
-    own, f_own, f_x, f_d, f_zo, sums, strength, zo = refs[:8]
-    xrs, zfs = refs[8 : 8 + parts], refs[8 + parts : 8 + 2 * parts]
-    outs, scratch = refs[8 + 2 * parts : -3 if parts > 1 else -1], refs[-3 if parts > 1 else -1 :]
+    own, f_own, f_x, f_d, f_zo, zo = refs[:6]
+    xrs, zfs = refs[6 : 6 + parts], refs[6 + parts : 6 + 2 * parts]
+    outs, scratch = refs[6 + 2 * parts : -3 if parts > 1 else -1], refs[-3 if parts > 1 else -1 :]
     first = scratch[0]
     place = lax.axis_index("space")
     x = lax.rem(place, 2)
@@ -123,23 +202,8 @@
         xr, zf = xrs[0], zfs[0]
         window = xr.shape[1] // 2
 
-    coef1 = (strength[...] * sums[0:count]).astype(BF16).astype(F32) * 0.25
-    gram = sums[2 * count : 3 * count]
-    padded = coef1
-    if orbs > count:
-        padded = jnp.concatenate([coef1, jnp.zeros((orbs - count, orbs), F32)], axis=0)
-    proj2 = sums[count : 2 * count] + jnp.dot(
-        gram, padded, preferred_element_type=F32, precision=lax.Precision.HIGHEST
-    )
-    coef2 = (strength[...] * proj2).astype(BF16).astype(F32) * 0.25
     k = lax.broadcasted_iota(jnp.int32, (depth, orbs), 0)
-    ones = jnp.where(jnp.logical_or(k == count, k == count + 1), 1.0, 0.0)
-
-    def right(coef):
-        rest = jnp.zeros((depth - count, orbs), F32)
-        return jnp.concatenate([jnp.concatenate([coef, rest], axis=0), ones], axis=1).astype(BF16)
-
-    right1, right2 = right(coef1), right(coef2)
+    ones = jnp.where(jnp.logical_or(k == count, k == count + 1), 1.0, 0.0).astype(BF16)
     here, _, _ = pair_matrices(width)
 
     def field(c, p):
@@ -160,12 +224,10 @@
         ref = zf if c < 2 else (xr if c < 6 else zo)
         return ref[plane, pl.ds(w, n)]
 
-    def applied(pair, v, outer, zs, fields, right_side):
-        both = lax.dot_general(
-            fields, right_side, (((0,), (0,)), ((), ())), preferred_element_type=F32
-        )
+    def applied(pair, v, outer, zs, fields):
+        u = lax.dot_general(fields, ones, (((0,), (0,)), ((), ())), preferred_element_type=F32)
         near = jnp.dot(here, pair, preferred_element_type=F32)
-        return both[:, :orbs] + near + both[:, orbs:] * v - 0.125 * (outer + zs)
+        return near + u * v - 0.125 * (outer + zs)
 
     def step1(j, carry):
         p = start // 2 + x + j - 1
@@ -185,7 +247,7 @@
                 ],
                 axis=0,
             )
-            f = applied(pair[c], vs[c], outer, vs[c - 1] + vs[c + 1], field(c, q), right1)
+            f = applied(pair[c], vs[c], outer, vs[c - 1] + vs[c + 1], field(c, q))
             keep = valid
             if c == 1:
                 keep = valid * has_zf
@@ -204,9 +266,7 @@
             outer = jnp.concatenate(
                 [first[c - 1, 2 * j + 1].astype(F32), first[c - 1, 2 * j + 4].astype(F32)], axis=0
             )
-            f = applied(
-                pair[c - 1], vs[c - 1], outer, vs[c - 2] + vs[c], field(c, p), right2
-            )
+            f = applied(pair[c - 1], vs[c - 1], outer, vs[c - 2] + vs[c], field(c, p))
             f = f.astype(BF16).reshape(2, width, orbs)
             plane = (c % 2) ^ x
             if joint:
@@ -284,25 +344,27 @@
     )(*blocks, q)
 
 
-def assemble_kernel(half, *refs):
+def assemble_kernel(half, term, *refs):
     out = refs[-1]
     pieces = (len(refs) - 1) // 2
     x = lax.rem(lax.axis_index("space"), 2)
     rows = refs[0].shape[1]
     for k in range(pieces):
-        out[:, pl.ds(half * x + rows * k, rows)] = refs[k][...]
-        out[:, pl.ds(half * (1 - x) + rows * k, rows)] = refs[pieces + k][...]
-
-
-def assembled(shape, mine, theirs):
-    return pl.pallas_call(
-        functools.partial(assemble_kernel, shape[1] // 2),
-        out_shape=jax.ShapeDtypeStruct(shape, BF16),
-        in_specs=[pl.BlockSpec(memory_space=pltpu.VMEM)] * (len(mine) + len(theirs)),
+        for ref, at in ((refs[k], half * x), (refs[pieces + k], half * (1 - x))):
+            where = pl.ds(at + rows * k, rows)
+            out[:, where] = (ref[...].astype(F32) + term[:, where]).astype(BF16)
+
+
+def assembled(term, mine, theirs):
+    return pl.pallas_call(
+        functools.partial(assemble_kernel, term.shape[1] // 2),
+        out_shape=jax.ShapeDtypeStruct(term.shape, BF16),
+        in_specs=[pl.BlockSpec(memory_space=pltpu.VMEM)] * (1 + len(mine) + len(theirs)),
         out_specs=pl.BlockSpec(memory_space=pltpu.VMEM),
         compiler_params=params(),
+        cost_estimate=cost(4096, 4096),
         name="assembled",
-    )(*mine, *theirs)
+    )(term, *mine, *theirs)
 
 
 def ordered(*arrays):
@@ -355,27 +417,25 @@
         [near, lax.dynamic_slice_in_dim(far, theirs // 2, window // 2, axis=0)], axis=0
     )
     to_zo = lax.dynamic_slice_in_dim(far, mine // 2, window // 2, axis=0)
-    to_x, far, to_zo, psi_in = ordered(to_x, far, to_zo, psi)
     f_x = lax.ppermute(to_x, "space", swap)
     f_d = lax.ppermute(far, "space", raster)
     f_zo = lax.ppermute(to_zo, "space", own_way)
 
     xr1 = lax.ppermute(
-        lax.dynamic_slice_in_dim(psi_in, theirs, early, axis=1), "space", swap
-    )
-    zo = lax.ppermute(lax.dynamic_slice_in_dim(psi_in, mine, window, axis=1), "space", own_way)
-    sums = partials(count, psi, fields, f_x, f_d)
-    xr1, sums = ordered(xr1, sums)
+        lax.dynamic_slice_in_dim(psi, theirs, early, axis=1), "space", swap
+    )
+    zo = lax.ppermute(lax.dynamic_slice_in_dim(psi, mine, window, axis=1), "space", own_way)
     zf1 = lax.ppermute(xr1, "space", other_way)
     second = lax.dynamic_slice_in_dim(psi, theirs + early, window - early, axis=1)
     second, _ = ordered(second, xr1)
     xr2 = lax.ppermute(second, "space", swap)
+    zf1, xr2 = ordered(zf1, xr2)
+    zf2 = lax.ppermute(xr2, "space", other_way)
+    sums, weights = partials(count, psi, fields, f_x, f_d)
     step = 1
     while step < slabs:
         sums = sums + lax.ppermute(sums, "space", [(i, i ^ step) for i in range(slabs)])
         step *= 2
-    zf1, xr2 = ordered(zf1, xr2)
-    zf2 = lax.ppermute(xr2, "space", other_way)
     strong = jnp.broadcast_to(strength[:, None], (count, orbs))
 
     me = lax.axis_index("orb")
@@ -384,7 +444,13 @@
     rows_hot = rows_hot * (pattern[:, 1] == me).astype(BF16)[:, None]
     q = jnp.einsum("ki,kab->iab", rows_hot, q_tiles, preferred_element_type=F32).astype(BF16)
 
-    operands = (psi, fields, f_x, f_d, f_zo, sums, strong, zo)
+    coefs = coefficients(sums, strong)
+    coefs_c = lax.ppermute(coefs, "orb", beside)
+    coefs_y = lax.ppermute(jnp.concatenate([coefs, coefs_c], axis=0), "orb", across)
+    coefs_yc, coefs_y = coefs_y[2 * count :], coefs_y[: 2 * count]
+    term = nonlocal_term(psi.shape, (coefs, coefs_c, coefs_y, coefs_yc), q, weights)
+
+    operands = (psi, fields, f_x, f_d, f_zo, zo)
     (block1,) = filtered(count, slabs, 0, rows, True, operands, (xr1,), (zf1,))
     y1 = lax.ppermute(block1, "orb", across)
     c1 = lax.ppermute(block1, "orb", beside)
@@ -403,7 +469,7 @@
     got2 = lax.ppermute(give2, "space", swap)
     yck = lax.ppermute(yk, "orb", beside)
     (keep2,) = rotated((keep2, ck, yk, yck), q, 1)
-    return assembled(psi.shape, [keep1, keep2], [got1, got2])
+    return assembled(term, [keep1, keep2], [got1, got2])
 
 
 def solution(mesh):

time: 112 us -> 92.3 us (0.82)
  starting transfers between devices: 43.8 us -> 28.2 us
  waiting for transfers between devices: 32.5 us -> 27.9 us
  local copies, waits for them, and re-layouts: 5.33 us -> 7.31 us
  Pallas kernels: 24.6 us -> 23.4 us
    ppermute x1, starting transfers between devices: 11.8 us -> 3.49 us  [shards(): zf1 = lax.ppermute(xr1, 'space', other_way)]
    ppermute x2 -> x4, waiting for transfers between devices: 0.01 us -> 6.87 us  [the longest x1 3.72 us: shards(): lax.ppermute(lax.dynamic_slice_in_dim(psi, theirs, early, axis=1), 'space...]
    ppermute x3, starting transfers between devices: 7.63 us -> 2.46 us  [shards(): lax.ppermute(sums, 'space', [(i, i ^ step) for i in range(slabs)])]
    ppermute x1, waiting for transfers between devices: 0.74 us -> 4.56 us  [shards(): yk = lax.ppermute(keep_y, 'orb', across)]
    ppermute x1, waiting for transfers between devices: 3.68 us -> 0.01 us  [shards(): zf2 = lax.ppermute(xr2, 'space', other_way)]
    ppermute x3, waiting for transfers between devices: 6.56 us -> 3.7 us  [shards(): lax.ppermute(sums, 'space', [(i, i ^ step) for i in range(slabs)])]
    ppermute x1, waiting for transfers between devices: 4.15 us -> 1.33 us  [shards(): f_x = lax.ppermute(to_x, 'space', swap)]
    ppermute x1, starting transfers between devices: 2.99 us -> 0.2 us  [shards(): got1 = lax.ppermute(give1, 'space', swap)]
  transfers between devices with their start and end apart: 22 -> 24, of which waited for: 10 -> 8; matrix products, arithmetic and copies ran while one was open for 1% -> 9% of each run, Pallas kernels for 17% -> 20%
where the time goes in v3:
time: 92.3 us; the launch traced here: 91.8 us
  starting transfers between devices  28.2 us (31%)
  waiting for transfers between devices  27.9 us (30%)
  Pallas kernels  23.4 us (25%)
  local copies, waits for them, and re-layouts  7.31 us (8%)
  other arithmetic  4.18 us (5%)
    pallas_call x2, Pallas kernels, filtered(): pl.pallas_call(functools.partial(filter_kernel, count, slabs, start, part...  9.28 us
    ppermute x1, waiting for transfers between devices, shards(): yg = lax.ppermute(give_y, 'orb', across)  7.99 us
    pallas_call x1, Pallas kernels, partials(): pl.pallas_call(functools.partial(partial_kernel, count, unroll), out_shap...  6.7 us
    ppermute x1, starting transfers between devices, shards(): f_x = lax.ppermute(to_x, 'space', swap)  5.41 us
    ppermute x1, waiting for transfers between devices, shards(): yk = lax.ppermute(keep_y, 'orb', across)  4.56 us
    ppermute x1, starting transfers between devices, shards(): zf2 = lax.ppermute(xr2, 'space', other_way)  4.27 us
    pallas_call x3, Pallas kernels, rotated(): pl.pallas_call(functools.partial(rotate_kernel, group), out_shape=(out,)...  4.24 us
    ppermute x1, waiting for transfers between devices, shards(): lax.ppermute(lax.dynamic_slice_in_dim(psi, theirs, early, axis=1), 'space...  3.72 us
  transfers between devices with their start and end apart: 24, of which 8 were waited for; matrix products, arithmetic and copies ran while one was open for 9% of the time, Pallas kernels for 20%

profile of v3, /device:TPU:0, one launch (start us, length us, event | category | flops | bytes accessed | tf_op | source)
XLA Modules:
  0.0 91.8 jit_solution(14754865042487618046)
XLA Ops:
  0.0 1.1 %constant_dynamic-slice_fusion.1 = bf16[2,16,48,128]{3,2,1,0:T(8,128)(2,1)S(1)} fusion(bf16[2,48,48,128]{3,2,1,0:T(8,128)(2,1)} %refs_0_.3, s32[]{:T(128)S(6)} %select_n.51), kind=kLoop, calls=%fused_computation.32 | loop fusion | bytes 786436 | tf_op jit(solution)/shard_map/dynamic_slice | solution.py:425
  1.1 3.0 %collective-permute-start.9 = (bf16[2,16,48,128]{3,2,1,0:T(8,128)(2,1)S(1)}, bf16[2,16,48,128]{3,2,1,0:T(8,128)(2,1)S(1)}, u32[]{:S(2)}, u32[]{:S(2)}) collective-permute-start(bf16[2,16,48,128]{3,2,1,0:T(8,128)(2,1)S(1)} %constant_dynamic-slice_fusion.1), channel_id=1, source_target_pairs={{0,4},{4,0},{8,12},{12,8},{16,20},{20,16},{24,28},{28,24},{1,5},{5... | collective-permute-start | bytes 1179656 | tf_op jit(solution)/shard_map/ppermute | solution.py:424
  4.1 2.0 %constant_dynamic-slice_fusion.2 = bf16[2,26,48,128]{3,2,1,0:T(8,128)(2,1)} fusion(bf16[2,48,48,128]{3,2,1,0:T(8,128)(2,1)} %refs_0_.3, s32[]{:T(128)S(6)} %select_n.50), kind=kLoop, calls=%fused_computation.33 | loop fusion | bytes 1277956 | tf_op jit(solution)/shard_map/dynamic_slice | solution.py:427
  6.1 1.4 %collective-permute-start.8 = (bf16[2,26,48,128]{3,2,1,0:T(8,128)(2,1)}, bf16[2,26,48,128]{3,2,1,0:T(8,128)(2,1)S(1)}, u32[]{:S(2)}, u32[]{:S(2)}) collective-permute-start(bf16[2,26,48,128]{3,2,1,0:T(8,128)(2,1)} %constant_dynamic-slice_fusion.2), channel_id=1, source_target_pairs={{4,12},{8,0},{12,20},{16,8},{20,28},{24,16},{5,13},{9,1},{13,21},{... | collective-permute-start | bytes 1916936 | tf_op jit(solution)/shard_map/ppermute | solution.py:427
  7.7 0.1 pad.9.clone
  7.7 0.1 fusion.2
  7.8 0.3 maximum_maximum_fusion
  8.1 0.7 fusion.22
  8.8 0.7 constant_dynamic-slice_fusion
  9.5 3.7 %collective-permute-done.9.refs_6_ = bf16[2,16,48,128]{3,2,1,0:T(8,128)(2,1)S(1)} collective-permute-done((bf16[2,16,48,128]{3,2,1,0:T(8,128)(2,1)S(1)}, bf16[2,16,48,128]{3,2,1,0:T(8,128)(2,1)S(1)}, u32[]{:S(2)}, u32[]{:S(2)}) %collective-permute-start.9) | collective-permute-done | bytes 393248 | tf_op jit(solution)/shard_map/ppermute | solution.py:424
  13.2 1.7 %collective-permute-start.11 = (bf16[2,10,48,128]{3,2,1,0:T(8,128)(2,1)}, bf16[2,10,48,128]{3,2,1,0:T(8,128)(2,1)S(1)}, u32[]{:S(2)}, u32[]{:S(2)}) collective-permute-start(bf16[2,10,48,128]{3,2,1,0:T(8,128)(2,1)} %constant_dynamic-slice_fusion), channel_id=1, source_target_pairs={{0,4},{4,0},{8,12},{12,8},{16,20},{20,16},{24,28},{28,24},{1,5},{5... | collective-permute-start | bytes 737288 | tf_op jit(solution)/shard_map/ppermute | solution.py:431
  15.0 3.5 %collective-permute-start.10 = (bf16[2,16,48,128]{3,2,1,0:T(8,128)(2,1)S(1)}, bf16[2,16,48,128]{3,2,1,0:T(8,128)(2,1)S(1)}, u32[]{:S(2)}, u32[]{:S(2)}) collective-permute-start(bf16[2,16,48,128]{3,2,1,0:T(8,128)(2,1)S(1)} %collective-permute-done.9.refs_6_), channel_id=1, source_target_pairs={{0,8},{8,16},{12,4},{16,24},{20,12},{28,20},{1,9},{9,17},{13,5},{1... | collective-permute-start | bytes 1179656 | tf_op jit(solution)/shard_map/ppermute | solution.py:428
  18.5 1.6 %fusion.10 = (bf16[13,16,96]{2,1,0:T(8,128)(2,1)}, bf16[13,16,96]{2,1,0:T(8,128)(2,1)S(1)}) fusion(s32[]{:T(128)S(6)} %select_n.43, s32[]{:T(128)S(6)} %select_n.49, bf16[2,24,16,48]{3,2,1,0:T(8,128)(2,1)S(1)} %get-tuple-element.35, bf16[2,24,16,48]{3,2,1,0:T(8,128)(2,1)} %get-tuple-element.36, s32[]{:T(128)S(6)} %select_n.46), kind=kLoop, calls=%fused_computation.25 | loop fusion | flops 159744 | bytes 227340 | tf_op jit(solution)/shard_map/dynamic_slice | solution.py:419
  20.1 1.3 %collective-permute-start.7 = (bf16[13,16,96]{2,1,0:T(8,128)(2,1)}, bf16[13,16,96]{2,1,0:T(8,128)(2,1)S(1)}, u32[]{:S(2)}, u32[]{:S(2)}) collective-permute-start(bf16[13,16,96]{2,1,0:T(8,128)(2,1)} %get-tuple-element.31), channel_id=1, source_target_pairs={{4,12},{8,0},{12,20},{16,8},{20,28},{24,16},{5,13},{9,1},{13,21},{... | collective-permute-start | bytes 119816 | tf_op jit(solution)/shard_map/ppermute | solution.py:422
  21.4 1.1 %fusion.6 = (bf16[24,16,96]{2,1,0:T(8,128)(2,1)S(1)}, bf16[24,16,96]{2,1,0:T(8,128)(2,1)S(1)}) fusion(s32[]{:T(128)S(6)} %select_n.42, bf16[2,24,16,48]{3,2,1,0:T(8,128)(2,1)S(1)} %get-tuple-element.35, bf16[2,24,16,48]{3,2,1,0:T(8,128)(2,1)} %get-tuple-element.36, s32[]{:T(128)S(6)} %select_n.41), kind=kLoop, calls=%fused_computation.19 | loop fusion | flops 294912 | bytes 294920 | tf_op jit(solution)/shard_map/jit(dynamic_index_in_dim)/squeeze | solution.py:414
  22.5 0.7 collective-permute-start.1
  23.2 0.0 collective-permute-done.11.refs_7_
  23.2 5.4 %collective-permute-start = (bf16[37,16,96]{2,1,0:T(8,128)(2,1)S(1)}, bf16[37,16,96]{2,1,0:T(8,128)(2,1)S(1)}, u32[]{:S(2)}, u32[]{:S(2)}) collective-permute-start(bf16[37,16,96]{2,1,0:T(8,128)(2,1)S(1)} %pad_maximum_fusion), channel_id=1, source_target_pairs={{0,4},{4,0},{8,12},{12,8},{16,20},{20,16},{24,28},{28,24},{1,5},{5... | collective-permute-start | bytes 341000 | tf_op jit(solution)/shard_map/ppermute | solution.py:420
  28.6 1.1 %pad_maximum_fusion.1.f_own.refs_1_ = bf16[2,24,16,96]{3,2,1,0:T(8,128)(2,1)S(1)} fusion(bf16[2,24,16,48]{3,2,1,0:T(8,128)(2,1)} %get-tuple-element.36, bf16[2,24,16,48]{3,2,1,0:T(8,128)(2,1)S(1)} %get-tuple-element.35), kind=kLoop, calls=%fused_computation.11 | loop fusion | flops 294912 | bytes 294912 | tf_op jit(solution)/shard_map/concatenate | solution.py:413
  29.7 0.0 collective-permute-done.10.refs_7_.refs_8_
  29.7 0.8 copy-done.2
  30.4 1.3 %collective-permute-done.f_x.refs_2_ = bf16[37,16,96]{2,1,0:T(8,128)(2,1)S(1)} collective-permute-done((bf16[37,16,96]{2,1,0:T(8,128)(2,1)S(1)}, bf16[37,16,96]{2,1,0:T(8,128)(2,1)S(1)}, u32[]{:S(2)}, u32[]{:S(2)}) %collective-permute-start) | collective-permute-done | bytes 113696 | tf_op jit(solution)/shard_map/ppermute | solution.py:420
  31.8 1.0 %copy-done.3 = bf16[2,16,48,128]{3,2,1,0:T(8,128)(2,1)S(1)} copy-done((bf16[2,16,48,128]{3,2,1,0:T(8,128)(2,1)S(1)}, bf16[2,16,48,128]{3,2,1,0:T(8,128)(2,1)}, u32[]{:S(2)}) %copy-start.3) | copy-done | bytes 393240
  32.8 3.6 %filtered.2.refs_0_ = bf16[4,12,48,128]{3,2,1,0:T(8,128)(2,1)S(1)} custom-call(bf16[2,48,48,128]{3,2,1,0:T(8,128)(2,1)S(1)} %copy-done.1, bf16[2,24,16,96]{3,2,1,0:T(8,128)(2,1)S(1)} %pad_maximum_fusion.1.f_own.refs_1_, bf16[37,16,96]{2,1,0:T(8,128)(2,1)S(1)} %collective-permute-done.f_x.refs_2_, bf16[24,16,96]{2,1,0:T(8,128)(2,1)S(1)} %collective-permute-done.1.f_d.refs_3_, ...), custom_call_target="tpu_custom_call" | custom-call | flops 2949120 | bytes 184320 | tf_op jit(solution)/shard_map/filtered/pallas_call | solution.py:292
  36.4 1.6 %collective-permute-start.14 = (bf16[4,12,48,128]{3,2,1,0:T(8,128)(2,1)S(1)}, bf16[4,12,48,128]{3,2,1,0:T(8,128)(2,1)}, u32[]{:S(2)}, u32[]{:S(2)}) collective-permute-start(bf16[4,12,48,128]{3,2,1,0:T(8,128)(2,1)S(1)} %filtered.2.refs_0_), channel_id=1, source_target_pairs={{0,2},{1,3},{2,0},{3,1},{4,6},{5,7},{6,4},{7,5},{8,10},{9,11},{10,... | collective-permute-start | bytes 1769480 | tf_op jit(solution)/shard_map/ppermute | solution.py:455
  38.0 4.3 %collective-permute-start.13 = (bf16[2,10,48,128]{3,2,1,0:T(8,128)(2,1)S(1)}, bf16[2,10,48,128]{3,2,1,0:T(8,128)(2,1)S(1)}, u32[]{:S(2)}, u32[]{:S(2)}) collective-permute-start(bf16[2,10,48,128]{3,2,1,0:T(8,128)(2,1)S(1)} %collective-permute-done.11.refs_7_), channel_id=1, source_target_pairs={{0,8},{8,16},{12,4},{16,24},{20,12},{28,20},{1,9},{9,17},{13,5},{1... | collective-permute-start | bytes 737288 | tf_op jit(solution)/shard_map/ppermute | solution.py:433
  42.3 6.7 %partials.1 = (f32[24,128]{1,0:T(8,128)S(1)}, bf16[2,24,48,96]{3,2,1,0:T(8,128)(2,1)S(1)}) custom-call(bf16[2,48,48,128]{3,2,1,0:T(8,128)(2,1)S(1)} %copy-done.1, bf16[2,24,16,96]{3,2,1,0:T(8,128)(2,1)S(1)} %pad_maximum_fusion.1.f_own.refs_1_, bf16[37,16,96]{2,1,0:T(8,128)(2,1)S(1)} %collective-permute-done.f_x.refs_2_, ...), custom_call_target="tpu_custom_call" | custom-call | flops 3538944 | bytes 147456 | tf_op jit(solution)/shard_map/partials/pallas_call | solution.py:89
  49.0 0.0 copy-start.5
  49.0 0.8 copy-done.5
  49.8 3.7 %collective-permute-done.2 = f32[24,128]{1,0:T(8,128)S(1)} collective-permute-done((f32[24,128]{1,0:T(8,128)S(1)}, f32[24,128]{1,0:T(8,128)S(1)}, u32[]{:S(2)}, u32[]{:S(2)}) %collective-permute-start.2) | collective-permute-done | bytes 12320 | tf_op jit(solution)/shard_map/ppermute | solution.py:437
  53.5 1.6 %collective-permute-start.3 = (f32[24,128]{1,0:T(8,128)S(1)}, f32[24,128]{1,0:T(8,128)S(1)}, u32[]{:S(2)}, u32[]{:S(2)}) collective-permute-start(f32[24,128]{1,0:T(8,128)S(1)} %add.51), channel_id=1, source_target_pairs={{0,8},{4,12},{8,0},{12,4},{16,24},{20,28},{24,16},{28,20},{1,9},{5... | collective-permute-start | bytes 36872 | tf_op jit(solution)/shard_map/ppermute | solution.py:437
  55.1 0.0 collective-permute-start.12
  55.1 5.7 %filtered.3 = (bf16[2,12,48,128]{3,2,1,0:T(8,128)(2,1)}, bf16[2,12,48,128]{3,2,1,0:T(8,128)(2,1)S(1)}) custom-call(bf16[2,48,48,128]{3,2,1,0:T(8,128)(2,1)} %refs_0_.3, bf16[2,24,16,96]{3,2,1,0:T(8,128)(2,1)S(1)} %pad_maximum_fusion.1.f_own.refs_1_, bf16[37,16,96]{2,1,0:T(8,128)(2,1)S(1)} %collective-permute-done.f_x.refs_2_, ...), custom_call_target="tpu_custom_call" | custom-call | flops 2949120 | bytes 184320 | tf_op jit(solution)/shard_map/filtered/pallas_call | solution.py:292
  60.8 0.5 collective-permute-start.17
  61.3 0.2 collective-permute-start.15
  61.5 0.0 collective-permute-done.3
  61.6 0.8 collective-permute-start.4
  62.4 0.0 collective-permute-start.21
  62.4 8.0 %collective-permute-done.17.refs_2_ = bf16[2,12,48,128]{3,2,1,0:T(8,128)(2,1)S(1)} collective-permute-done((bf16[2,12,48,128]{3,2,1,0:T(8,128)(2,1)}, bf16[2,12,48,128]{3,2,1,0:T(8,128)(2,1)S(1)}, u32[]{:S(2)}, u32[]{:S(2)}) %collective-permute-start.17) | collective-permute-done | bytes 294944 | tf_op jit(solution)/shard_map/ppermute | solution.py:461
  70.4 0.5 collective-permute-start.18
  71.0 0.1 broadcast_in_dim.28.strength
  71.1 0.1 coefficients.1.a
  71.2 0.0 collective-permute-done.21.refs_1_
  71.2 0.6 collective-permute-start.5
  71.8 0.3 fusion
  72.1 0.4 collective-permute-done.22.refs_3_
  72.5 0.1 collective-permute-start.16
  72.7 1.6 %rotated.5 = bf16[2,12,48,128]{3,2,1,0:T(8,128)(2,1)S(1)} custom-call(bf16[2,12,48,128]{3,2,1,0:T(8,128)(2,1)} %get-tuple-element.27.refs_0_, bf16[2,12,48,128]{3,2,1,0:T(8,128)(2,1)S(1)} %collective-permute-done.21.refs_1_, bf16[2,12,48,128]{3,2,1,0:T(8,128)(2,1)S(1)} %collective-permute-done.17.refs_2_, ...), custom_call_target="tpu_custom_call" | custom-call | flops 9437184 | bytes 92160 | tf_op jit(solution)/shard_map/rotated/pallas_call | solution.py:336
  74.3 0.0 copy-start.6
  74.3 0.0 collective-permute-done.12.refs_1_
  74.3 0.2 collective-permute-start.23
  74.5 4.6 %collective-permute-done.18.refs_2_ = bf16[2,12,48,128]{3,2,1,0:T(8,128)(2,1)S(1)} collective-permute-done((bf16[2,12,48,128]{3,2,1,0:T(8,128)(2,1)S(1)}, bf16[2,12,48,128]{3,2,1,0:T(8,128)(2,1)S(1)}, u32[]{:S(2)}, u32[]{:S(2)}) %collective-permute-start.18) | collective-permute-done | bytes 294944 | tf_op jit(solution)/shard_map/ppermute | solution.py:466
  79.1 0.0 collective-permute-start.19
  79.1 0.0 collective-permute-done.15.refs_3_
  79.1 2.0 %rotated.3 = (bf16[2,12,48,128]{3,2,1,0:T(8,128)(2,1)S(1)}, bf16[2,12,48,128]{3,2,1,0:T(8,128)(2,1)S(1)}) custom-call(bf16[4,12,48,128]{3,2,1,0:T(8,128)(2,1)S(1)} %filtered.2.refs_0_, bf16[4,12,48,128]{3,2,1,0:T(8,128)(2,1)S(1)} %collective-permute-done.12.refs_1_, bf16[4,12,48,128]{3,2,1,0:T(8,128)(2,1)} %collective-permute-done.14.refs_2_, ...), custom_call_target="tpu_custom_call" | custom-call | flops 18874368 | bytes 184320 | tf_op jit(solution)/shard_map/rotated/pallas_call | solution.py:336
  81.1 0.2 collective-permute-start.20
  81.3 0.0 collective-permute-done.5.b
  81.3 0.5 collective-permute-start.6
  81.8 3.1 %collective-permute-done.6 = bf16[32,128]{1,0:T(8,128)(2,1)S(1)} collective-permute-done((bf16[32,128]{1,0:T(8,128)(2,1)S(1)}, bf16[32,128]{1,0:T(8,128)(2,1)S(1)}, u32[]{:S(2)}, u32[]{:S(2)}) %collective-permute-start.6) | collective-permute-done | bytes 8224 | tf_op jit(solution)/shard_map/ppermute | solution.py:449
  85.0 1.9 %nonlocal.1.term = f32[2,48,48,128]{3,2,1,0:T(8,128)S(1)} custom-call(bf16[16,128]{1,0:T(8,128)(2,1)S(1)} %coefficients.1.a, bf16[16,128]{1,0:T(8,128)(2,1)S(1)} %collective-permute-done.5.b, bf16[16,128]{1,0:T(8,128)(2,1)S(1)} %get-tuple-element.40.c, bf16[16,128]{1,0:T(8,128)(2,1)S(1)} %get-tuple-element.39.d, bf16[4,128,128]{2,1,0:T(8,128)(2,1)S(1)} %copy.27.q.refs_4_, ...), custom_call_target="tpu_custom_call" | custom-call | flops 256 | bytes 256 | tf_op jit(solution)/shard_map/nonlocal/pallas_call | solution.py:164
  86.9 0.0 collective-permute-done.19.refs_3_
  86.9 0.6 rotated.4.refs_1_
  87.5 3.1 %collective-permute-done.20.refs_2_ = bf16[2,12,48,128]{3,2,1,0:T(8,128)(2,1)S(1)} collective-permute-done((bf16[2,12,48,128]{3,2,1,0:T(8,128)(2,1)S(1)}, bf16[2,12,48,128]{3,2,1,0:T(8,128)(2,1)S(1)}, u32[]{:S(2)}, u32[]{:S(2)}) %collective-permute-start.20) | collective-permute-done | bytes 294944 | tf_op jit(solution)/shard_map/ppermute | solution.py:464
  90.6 1.2 %assembled.1 = bf16[2,48,48,128]{3,2,1,0:T(8,128)(2,1)} custom-call(f32[2,48,48,128]{3,2,1,0:T(8,128)S(1)} %nonlocal.1.term, bf16[2,12,48,128]{3,2,1,0:T(8,128)(2,1)S(1)} %get-tuple-element.25.refs_0_, bf16[2,12,48,128]{3,2,1,0:T(8,128)(2,1)S(1)} %rotated.4.refs_1_, bf16[2,12,48,128]{3,2,1,0:T(8,128)(2,1)S(1)} %collective-permute-done.20.refs_2_, ...), custom_call_target="tpu_custom_call" | custom-call | flops 256 | bytes 256 | tf_op jit(solution)/shard_map/assembled/pallas_call | solution.py:359
  (48 shorter events, 0.3 us)
Async XLA Ops:
  0.0 71.8 %copy-start = (bf16[12,128,128]{2,1,0:T(8,128)(2,1)S(1)}, bf16[12,128,128]{2,1,0:T(8,128)(2,1)}, u32[]{:S(2)}) copy-start(bf16[12,128,128]{2,1,0:T(8,128)(2,1)} %param.13) | copy-start | bytes 1179652
  0.0 7.5 %copy-start.13 = (s32[8]{0:T(128)S(1)}, s32[8]{0:T(128)}, u32[]{:S(2)}) copy-start(s32[8]{0:T(128)} %param.11) | copy-start | bytes 100
  0.0 7.5 %copy-start.10 = (f32[2,48,48]{2,1,0:T(8,128)S(1)}, f32[2,48,48]{2,1,0:T(8,128)}, u32[]{:S(2)}) copy-start(f32[2,48,48]{2,1,0:T(8,128)} %param.8) | copy-start | bytes 55300
  0.0 7.7 %copy-start.9 = (bf16[8,2,48,48]{3,2,1,0:T(8,128)(2,1)S(1)}, bf16[8,2,48,48]{3,2,1,0:T(8,128)(2,1)}, u32[]{:S(2)}) copy-start(bf16[8,2,48,48]{3,2,1,0:T(8,128)(2,1)} %param.9) | copy-start | bytes 221188
  1.1 12.1 %collective-permute-start.9 = (bf16[2,16,48,128]{3,2,1,0:T(8,128)(2,1)S(1)}, bf16[2,16,48,128]{3,2,1,0:T(8,128)(2,1)S(1)}, u32[]{:S(2)}, u32[]{:S(2)}) collective-permute-start(bf16[2,16,48,128]{3,2,1,0:T(8,128)(2,1)S(1)} %constant_dynamic-slice_fusion.1), channel_id=1, source_target_pairs={{0,4},{4,0},{8,12},{12,8},{16,20},{20,16},{24,28},{28,24},{1,5},{5... | collective-permute-start | bytes 1179656 | tf_op jit(solution)/shard_map/ppermute | solution.py:424
  6.1 2.7 %copy-start.1 = (bf16[2,48,48,128]{3,2,1,0:T(8,128)(2,1)S(1)}, bf16[2,48,48,128]{3,2,1,0:T(8,128)(2,1)}, u32[]{:S(2)}) copy-start(bf16[2,48,48,128]{3,2,1,0:T(8,128)(2,1)} %refs_0_.3) | copy-start | bytes 3538948
  6.1 25.7 %collective-permute-start.8 = (bf16[2,26,48,128]{3,2,1,0:T(8,128)(2,1)}, bf16[2,26,48,128]{3,2,1,0:T(8,128)(2,1)S(1)}, u32[]{:S(2)}, u32[]{:S(2)}) collective-permute-start(bf16[2,26,48,128]{3,2,1,0:T(8,128)(2,1)} %constant_dynamic-slice_fusion.2), channel_id=1, source_target_pairs={{4,12},{8,0},{12,20},{16,8},{20,28},{24,16},{5,13},{9,1},{13,21},{... | collective-permute-start | bytes 1916936 | tf_op jit(solution)/shard_map/ppermute | solution.py:427
  13.2 9.9 %collective-permute-start.11 = (bf16[2,10,48,128]{3,2,1,0:T(8,128)(2,1)}, bf16[2,10,48,128]{3,2,1,0:T(8,128)(2,1)S(1)}, u32[]{:S(2)}, u32[]{:S(2)}) collective-permute-start(bf16[2,10,48,128]{3,2,1,0:T(8,128)(2,1)} %constant_dynamic-slice_fusion), channel_id=1, source_target_pairs={{0,4},{4,0},{8,12},{12,8},{16,20},{20,16},{24,28},{28,24},{1,5},{5... | collective-permute-start | bytes 737288 | tf_op jit(solution)/shard_map/ppermute | solution.py:431
  15.0 14.7 %collective-permute-start.10 = (bf16[2,16,48,128]{3,2,1,0:T(8,128)(2,1)S(1)}, bf16[2,16,48,128]{3,2,1,0:T(8,128)(2,1)S(1)}, u32[]{:S(2)}, u32[]{:S(2)}) collective-permute-start(bf16[2,16,48,128]{3,2,1,0:T(8,128)(2,1)S(1)} %collective-permute-done.9.refs_6_), channel_id=1, source_target_pairs={{0,8},{8,16},{12,4},{16,24},{20,12},{28,20},{1,9},{9,17},{13,5},{1... | collective-permute-start | bytes 1179656 | tf_op jit(solution)/shard_map/ppermute | solution.py:428
  20.1 10.3 %collective-permute-start.7 = (bf16[13,16,96]{2,1,0:T(8,128)(2,1)}, bf16[13,16,96]{2,1,0:T(8,128)(2,1)S(1)}, u32[]{:S(2)}, u32[]{:S(2)}) collective-permute-start(bf16[13,16,96]{2,1,0:T(8,128)(2,1)} %get-tuple-element.31), channel_id=1, source_target_pairs={{4,12},{8,0},{12,20},{16,8},{20,28},{24,16},{5,13},{9,1},{13,21},{... | collective-permute-start | bytes 119816 | tf_op jit(solution)/shard_map/ppermute | solution.py:422
  22.5 8.0 %collective-permute-start.1 = (bf16[24,16,96]{2,1,0:T(8,128)(2,1)S(1)}, bf16[24,16,96]{2,1,0:T(8,128)(2,1)S(1)}, u32[]{:S(2)}, u32[]{:S(2)}) collective-permute-start(bf16[24,16,96]{2,1,0:T(8,128)(2,1)S(1)} %get-tuple-element.33), channel_id=1, source_target_pairs={{4,8},{8,4},{12,16},{16,12},{20,24},{24,20},{5,9},{9,5},{13,17},{1... | collective-permute-start | bytes 221192 | tf_op jit(solution)/shard_map/ppermute | solution.py:421
  23.2 14.8 %copy-start.7 = (bf16[2,10,48,128]{3,2,1,0:T(8,128)(2,1)}, bf16[2,10,48,128]{3,2,1,0:T(8,128)(2,1)S(1)}, u32[]{:S(2)}) copy-start(bf16[2,10,48,128]{3,2,1,0:T(8,128)(2,1)S(1)} %collective-permute-done.11.refs_7_) | copy-start | bytes 737284
  23.2 8.6 %collective-permute-start = (bf16[37,16,96]{2,1,0:T(8,128)(2,1)S(1)}, bf16[37,16,96]{2,1,0:T(8,128)(2,1)S(1)}, u32[]{:S(2)}, u32[]{:S(2)}) collective-permute-start(bf16[37,16,96]{2,1,0:T(8,128)(2,1)S(1)} %pad_maximum_fusion), channel_id=1, source_target_pairs={{0,4},{4,0},{8,12},{12,8},{16,20},{20,16},{24,28},{28,24},{1,5},{5... | collective-permute-start | bytes 341000 | tf_op jit(solution)/shard_map/ppermute | solution.py:420
  29.7 0.8 copy-start.2
  31.8 1.0 %copy-start.3 = (bf16[2,16,48,128]{3,2,1,0:T(8,128)(2,1)S(1)}, bf16[2,16,48,128]{3,2,1,0:T(8,128)(2,1)}, u32[]{:S(2)}) copy-start(bf16[2,16,48,128]{3,2,1,0:T(8,128)(2,1)} %copy-done.2) | copy-start | bytes 1179652
  36.4 18.7 %copy-start.4 = (bf16[2,16,48,128]{3,2,1,0:T(8,128)(2,1)S(1)}, bf16[2,16,48,128]{3,2,1,0:T(8,128)(2,1)}, u32[]{:S(2)}) copy-start(bf16[2,16,48,128]{3,2,1,0:T(8,128)(2,1)} %copy-done.2) | copy-start | bytes 1179652
  36.4 24.4 %collective-permute-start.14 = (bf16[4,12,48,128]{3,2,1,0:T(8,128)(2,1)S(1)}, bf16[4,12,48,128]{3,2,1,0:T(8,128)(2,1)}, u32[]{:S(2)}, u32[]{:S(2)}) collective-permute-start(bf16[4,12,48,128]{3,2,1,0:T(8,128)(2,1)S(1)} %filtered.2.refs_0_), channel_id=1, source_target_pairs={{0,2},{1,3},{2,0},{3,1},{4,6},{5,7},{6,4},{7,5},{8,10},{9,11},{10,... | collective-permute-start | bytes 1769480 | tf_op jit(solution)/shard_map/ppermute | solution.py:455
  38.0 17.1 %collective-permute-start.13 = (bf16[2,10,48,128]{3,2,1,0:T(8,128)(2,1)S(1)}, bf16[2,10,48,128]{3,2,1,0:T(8,128)(2,1)S(1)}, u32[]{:S(2)}, u32[]{:S(2)}) collective-permute-start(bf16[2,10,48,128]{3,2,1,0:T(8,128)(2,1)S(1)} %collective-permute-done.11.refs_7_), channel_id=1, source_target_pairs={{0,8},{8,16},{12,4},{16,24},{20,12},{28,20},{1,9},{9,17},{13,5},{1... | collective-permute-start | bytes 737288 | tf_op jit(solution)/shard_map/ppermute | solution.py:433
  42.3 12.9 %copy-start.8 = (bf16[2,10,48,128]{3,2,1,0:T(8,128)(2,1)S(1)}, bf16[2,10,48,128]{3,2,1,0:T(8,128)(2,1)}, u32[]{:S(2)}) copy-start(bf16[2,10,48,128]{3,2,1,0:T(8,128)(2,1)} %copy-done.7) | copy-start | bytes 737284
  49.0 0.8 copy-start.5
  49.8 3.7 %collective-permute-start.2 = (f32[24,128]{1,0:T(8,128)S(1)}, f32[24,128]{1,0:T(8,128)S(1)}, u32[]{:S(2)}, u32[]{:S(2)}) collective-permute-start(f32[24,128]{1,0:T(8,128)S(1)} %get-tuple-element.18), channel_id=1, source_target_pairs={{0,4},{4,0},{8,12},{12,8},{16,20},{20,16},{24,28},{28,24},{1,5},{5... | collective-permute-start | bytes 36872 | tf_op jit(solution)/shard_map/ppermute | solution.py:437
  53.5 8.0 %copy-start.12 = (s32[12,2]{0,1:T(2,128)S(1)}, s32[12,2]{0,1:T(2,128)}, u32[]{:S(2)}) copy-start(s32[12,2]{0,1:T(2,128)} %param.12) | copy-start | bytes 292
  53.5 17.5 %copy-start.11 = (f32[8]{0:T(128)S(1)}, f32[8]{0:T(128)}, u32[]{:S(2)}) copy-start(f32[8]{0:T(128)} %param.10) | copy-start | bytes 100
  53.5 8.0 %collective-permute-start.3 = (f32[24,128]{1,0:T(8,128)S(1)}, f32[24,128]{1,0:T(8,128)S(1)}, u32[]{:S(2)}, u32[]{:S(2)}) collective-permute-start(f32[24,128]{1,0:T(8,128)S(1)} %add.51), channel_id=1, source_target_pairs={{0,8},{4,12},{8,0},{12,4},{16,24},{20,28},{24,16},{28,20},{1,9},{5... | collective-permute-start | bytes 36872 | tf_op jit(solution)/shard_map/ppermute | solution.py:437
  55.1 19.2 %collective-permute-start.12 = (bf16[4,12,48,128]{3,2,1,0:T(8,128)(2,1)S(1)}, bf16[4,12,48,128]{3,2,1,0:T(8,128)(2,1)S(1)}, u32[]{:S(2)}, u32[]{:S(2)}) collective-permute-start(bf16[4,12,48,128]{3,2,1,0:T(8,128)(2,1)S(1)} %filtered.2.refs_0_), channel_id=1, source_target_pairs={{0,1},{1,0},{2,3},{3,2},{4,5},{5,4},{6,7},{7,6},{8,9},{9,8},{10,11... | collective-permute-start | bytes 1769480 | tf_op jit(solution)/shard_map/ppermute | solution.py:456
  60.8 9.6 %collective-permute-start.17 = (bf16[2,12,48,128]{3,2,1,0:T(8,128)(2,1)}, bf16[2,12,48,128]{3,2,1,0:T(8,128)(2,1)S(1)}, u32[]{:S(2)}, u32[]{:S(2)}) collective-permute-start(bf16[2,12,48,128]{3,2,1,0:T(8,128)(2,1)} %get-tuple-element.27.refs_0_), channel_id=1, source_target_pairs={{0,2},{1,3},{2,0},{3,1},{4,6},{5,7},{6,4},{7,5},{8,10},{9,11},{10,... | collective-permute-start | bytes 884744 | tf_op jit(solution)/shard_map/ppermute | solution.py:461
  61.3 17.8 %collective-permute-start.15 = (bf16[4,12,48,128]{3,2,1,0:T(8,128)(2,1)}, bf16[4,12,48,128]{3,2,1,0:T(8,128)(2,1)S(1)}, u32[]{:S(2)}, u32[]{:S(2)}) collective-permute-start(bf16[4,12,48,128]{3,2,1,0:T(8,128)(2,1)} %collective-permute-done.14.refs_2_), channel_id=1, source_target_pairs={{0,1},{1,0},{2,3},{3,2},{4,5},{5,4},{6,7},{7,6},{8,9},{9,8},{10,11... | collective-permute-start | bytes 1769480 | tf_op jit(solution)/shard_map/ppermute | solution.py:462
  61.6 9.4 %collective-permute-start.4 = (f32[24,128]{1,0:T(8,128)S(1)}, f32[24,128]{1,0:T(8,128)S(1)}, u32[]{:S(2)}, u32[]{:S(2)}) collective-permute-start(f32[24,128]{1,0:T(8,128)S(1)} %add.52), channel_id=1, source_target_pairs={{0,16},{4,20},{8,24},{12,28},{16,0},{20,4},{24,8},{28,12},{1,17},{... | collective-permute-start | bytes 36872 | tf_op jit(solution)/shard_map/ppermute | solution.py:437
  62.4 8.8 %collective-permute-start.21 = (bf16[2,12,48,128]{3,2,1,0:T(8,128)(2,1)}, bf16[2,12,48,128]{3,2,1,0:T(8,128)(2,1)S(1)}, u32[]{:S(2)}, u32[]{:S(2)}) collective-permute-start(bf16[2,12,48,128]{3,2,1,0:T(8,128)(2,1)} %get-tuple-element.27.refs_0_), channel_id=1, source_target_pairs={{0,1},{1,0},{2,3},{3,2},{4,5},{5,4},{6,7},{7,6},{8,9},{9,8},{10,11... | collective-permute-start | bytes 884744 | tf_op jit(solution)/shard_map/ppermute | solution.py:458
  70.4 8.6 %collective-permute-start.18 = (bf16[2,12,48,128]{3,2,1,0:T(8,128)(2,1)S(1)}, bf16[2,12,48,128]{3,2,1,0:T(8,128)(2,1)S(1)}, u32[]{:S(2)}, u32[]{:S(2)}) collective-permute-start(bf16[2,12,48,128]{3,2,1,0:T(8,128)(2,1)S(1)} %get-tuple-element.28.refs_0_), channel_id=1, source_target_pairs={{0,2},{1,3},{2,0},{3,1},{4,6},{5,7},{6,4},{7,5},{8,10},{9,11},{10,... | collective-permute-start | bytes 884744 | tf_op jit(solution)/shard_map/ppermute | solution.py:466
  70.9 1.6 %collective-permute-start.22 = (bf16[2,12,48,128]{3,2,1,0:T(8,128)(2,1)S(1)}, bf16[2,12,48,128]{3,2,1,0:T(8,128)(2,1)S(1)}, u32[]{:S(2)}, u32[]{:S(2)}) collective-permute-start(bf16[2,12,48,128]{3,2,1,0:T(8,128)(2,1)S(1)} %collective-permute-done.17.refs_2_), channel_id=1, source_target_pairs={{0,1},{1,0},{2,3},{3,2},{4,5},{5,4},{6,7},{7,6},{8,9},{9,8},{10,11... | collective-permute-start | bytes 884744 | tf_op jit(solution)/shard_map/ppermute | solution.py:467
  71.2 10.1 %collective-permute-start.5 = (bf16[16,128]{1,0:T(8,128)(2,1)S(1)}, bf16[16,128]{1,0:T(8,128)(2,1)S(1)}, u32[]{:S(2)}, u32[]{:S(2)}) collective-permute-start(bf16[16,128]{1,0:T(8,128)(2,1)S(1)} %coefficients.1.a), channel_id=1, source_target_pairs={{0,1},{1,0},{2,3},{3,2},{4,5},{5,4},{6,7},{7,6},{8,9},{9,8},{10,11... | collective-permute-start | bytes 12296 | tf_op jit(solution)/shard_map/ppermute | solution.py:448
  72.5 14.3 %collective-permute-start.16 = (bf16[2,12,48,128]{3,2,1,0:T(8,128)(2,1)S(1)}, bf16[2,12,48,128]{3,2,1,0:T(8,128)(2,1)S(1)}, u32[]{:S(2)}, u32[]{:S(2)}) collective-permute-start(bf16[2,12,48,128]{3,2,1,0:T(8,128)(2,1)S(1)} %get-tuple-element.28.refs_0_), channel_id=1, source_target_pairs={{0,1},{1,0},{2,3},{3,2},{4,5},{5,4},{6,7},{7,6},{8,9},{9,8},{10,11... | collective-permute-start | bytes 884744 | tf_op jit(solution)/shard_map/ppermute | solution.py:459
  74.3 10.7 %copy-start.6 = (bf16[2,24,48,96]{3,2,1,0:T(8,128)(2,1)S(1)}, bf16[2,24,48,96]{3,2,1,0:T(8,128)(2,1)}, u32[]{:S(2)}) copy-start(bf16[2,24,48,96]{3,2,1,0:T(8,128)(2,1)} %copy-done.5) | copy-start | bytes 1327108
  74.3 13.2 %collective-permute-start.23 = (bf16[2,12,48,128]{3,2,1,0:T(8,128)(2,1)S(1)}, bf16[2,12,48,128]{3,2,1,0:T(8,128)(2,1)S(1)}, u32[]{:S(2)}, u32[]{:S(2)}) collective-permute-start(bf16[2,12,48,128]{3,2,1,0:T(8,128)(2,1)S(1)} %rotated.5), channel_id=1, source_target_pairs={{0,4},{4,0},{8,12},{12,8},{16,20},{20,16},{24,28},{28,24},{1,5},{5... | collective-permute-start | bytes 884744 | tf_op jit(solution)/shard_map/ppermute | solution.py:469
  79.1 7.8 %collective-permute-start.19 = (bf16[2,12,48,128]{3,2,1,0:T(8,128)(2,1)S(1)}, bf16[2,12,48,128]{3,2,1,0:T(8,128)(2,1)S(1)}, u32[]{:S(2)}, u32[]{:S(2)}) collective-permute-start(bf16[2,12,48,128]{3,2,1,0:T(8,128)(2,1)S(1)} %collective-permute-done.18.refs_2_), channel_id=1, source_target_pairs={{0,1},{1,0},{2,3},{3,2},{4,5},{5,4},{6,7},{7,6},{8,9},{9,8},{10,11... | collective-permute-start | bytes 884744 | tf_op jit(solution)/shard_map/ppermute | solution.py:470
  81.1 9.5 %collective-permute-start.20 = (bf16[2,12,48,128]{3,2,1,0:T(8,128)(2,1)S(1)}, bf16[2,12,48,128]{3,2,1,0:T(8,128)(2,1)S(1)}, u32[]{:S(2)}, u32[]{:S(2)}) collective-permute-start(bf16[2,12,48,128]{3,2,1,0:T(8,128)(2,1)S(1)} %get-tuple-element.29), channel_id=1, source_target_pairs={{0,4},{4,0},{8,12},{12,8},{16,20},{20,16},{24,28},{28,24},{1,5},{5... | collective-permute-start | bytes 884744 | tf_op jit(solution)/shard_map/ppermute | solution.py:464
  81.3 3.7 %collective-permute-start.6 = (bf16[32,128]{1,0:T(8,128)(2,1)S(1)}, bf16[32,128]{1,0:T(8,128)(2,1)S(1)}, u32[]{:S(2)}, u32[]{:S(2)}) collective-permute-start(bf16[32,128]{1,0:T(8,128)(2,1)S(1)} %pad_maximum_fusion.2), channel_id=1, source_target_pairs={{0,2},{1,3},{2,0},{3,1},{4,6},{5,7},{6,4},{7,5},{8,10},{9,11},{10,... | collective-permute-start | bytes 24584 | tf_op jit(solution)/shard_map/ppermute | solution.py:449

commit v4 on v3

--- a/solution.py
+++ b/solution.py
@@ -9,7 +9,7 @@
 
 F32 = jnp.float32
 BF16 = jnp.bfloat16
-VMEM_LIMIT = 50 * 1024 * 1024
+VMEM_LIMIT = 24 * 1024 * 1024
 SHRINK = 16
 
 
@@ -172,15 +172,15 @@
     )(*coefs, q, weights)
 
 
-def filter_kernel(count, slabs, start, parts, joint, *refs):
-    own, f_own, f_x, f_d, f_zo, zo = refs[:6]
+def filter_kernel(slabs, start, parts, joint, *refs):
+    own, p_own, p_x, p_d, p_zo, zo = refs[:6]
     xrs, zfs = refs[6 : 6 + parts], refs[6 + parts : 6 + 2 * parts]
     outs, scratch = refs[6 + 2 * parts : -3 if parts > 1 else -1], refs[-3 if parts > 1 else -1 :]
     first = scratch[0]
     place = lax.axis_index("space")
     x = lax.rem(place, 2)
-    _, pairs, depth, cells = f_own.shape
-    width = cells // 2
+    width = own.shape[2]
+    cells = 2 * width
     half = own.shape[1] // 2
     orbs = own.shape[3]
     rows = outs[0].shape[1]
@@ -202,20 +202,25 @@
         xr, zf = xrs[0], zfs[0]
         window = xr.shape[1] // 2
 
-    k = lax.broadcasted_iota(jnp.int32, (depth, orbs), 0)
-    ones = jnp.where(jnp.logical_or(k == count, k == count + 1), 1.0, 0.0).astype(BF16)
     here, _, _ = pair_matrices(width)
-
-    def field(c, p):
-        if c == 1:
-            return f_d[base // 2 + p]
-        if c in (2, 3):
-            return f_own[(c % 2) ^ x, base // 2 + p]
-        if c == 4:
-            return f_x[base // 2 + p]
-        if c == 5:
-            return f_x[pairs + p]
-        return f_zo[p]
+    here = here.astype(F32)
+    i = lax.broadcasted_iota(jnp.int32, (cells, cells), 0)
+    diagonal = i == lax.broadcasted_iota(jnp.int32, (cells, cells), 1)
+
+    def local(c, p):
+        w = base + 2 * p
+
+        def line(at):
+            if c in (1, 6):
+                return (p_d if c == 1 else p_zo)[0, pl.ds(at, 1)]
+            return (p_own if c in (2, 3) else p_x)[(c % 2) ^ x, pl.ds(at, 1)]
+
+        u = (jnp.concatenate([line(w), line(w + 1)], axis=1) - 1.0) * 0.25
+        hi = u.astype(BF16).astype(F32)
+        return (
+            jnp.where(diagonal, hi, here).astype(BF16),
+            jnp.where(diagonal, u - hi, 0.0).astype(BF16),
+        )
 
     def rows_of(c, w, n):
         plane = (c % 2) ^ x
@@ -224,10 +229,10 @@
         ref = zf if c < 2 else (xr if c < 6 else zo)
         return ref[plane, pl.ds(w, n)]
 
-    def applied(pair, v, outer, zs, fields):
-        u = lax.dot_general(fields, ones, (((0,), (0,)), ((), ())), preferred_element_type=F32)
-        near = jnp.dot(here, pair, preferred_element_type=F32)
-        return near + u * v - 0.125 * (outer + zs)
+    def applied(pair, outer, zs, matrices):
+        near = jnp.dot(matrices[0], pair, preferred_element_type=F32)
+        near = near + jnp.dot(matrices[1], pair, preferred_element_type=F32)
+        return near - 0.125 * (outer + zs)
 
     def step1(j, carry):
         p = start // 2 + x + j - 1
@@ -247,7 +252,7 @@
                 ],
                 axis=0,
             )
-            f = applied(pair[c], vs[c], outer, vs[c - 1] + vs[c + 1], field(c, q))
+            f = applied(pair[c], outer, vs[c - 1] + vs[c + 1], local(c, q))
             keep = valid
             if c == 1:
                 keep = valid * has_zf
@@ -266,7 +271,7 @@
             outer = jnp.concatenate(
                 [first[c - 1, 2 * j + 1].astype(F32), first[c - 1, 2 * j + 4].astype(F32)], axis=0
             )
-            f = applied(pair[c - 1], vs[c - 1], outer, vs[c - 2] + vs[c], field(c, p))
+            f = applied(pair[c - 1], outer, vs[c - 2] + vs[c], local(c, p))
             f = f.astype(BF16).reshape(2, width, orbs)
             plane = (c % 2) ^ x
             if joint:
@@ -278,7 +283,7 @@
     lax.fori_loop(0, rows // 2, step2, 0)
 
 
-def filtered(count, slabs, start, rows, joint, operands, xrs, zfs):
+def filtered(slabs, start, rows, joint, operands, xrs, zfs):
     own = operands[0]
     planes, _, width, orbs = own.shape
     parts = len(xrs)
@@ -290,7 +295,7 @@
         window = sum(piece.shape[1] for piece in xrs)
         scratch += [pltpu.VMEM((planes, window, width, orbs), BF16)] * 2
     return pl.pallas_call(
-        functools.partial(filter_kernel, count, slabs, start, parts, joint),
+        functools.partial(filter_kernel, slabs, start, parts, joint),
         out_shape=out,
         in_specs=[pl.BlockSpec(memory_space=pltpu.VMEM)] * (len(operands) + 2 * parts),
         out_specs=(pl.BlockSpec(memory_space=pltpu.VMEM),) * len(out),
@@ -413,13 +418,12 @@
     fields = jnp.concatenate([fields[:, 0::2], fields[:, 1::2]], axis=3)
     far = lax.dynamic_index_in_dim(fields, x, 0, keepdims=False)
     near = lax.dynamic_index_in_dim(fields, 1 - x, 0, keepdims=False)
-    to_x = jnp.concatenate(
-        [near, lax.dynamic_slice_in_dim(far, theirs // 2, window // 2, axis=0)], axis=0
-    )
-    to_zo = lax.dynamic_slice_in_dim(far, mine // 2, window // 2, axis=0)
-    f_x = lax.ppermute(to_x, "space", swap)
+    f_x = lax.ppermute(near, "space", swap)
     f_d = lax.ppermute(far, "space", raster)
-    f_zo = lax.ppermute(to_zo, "space", own_way)
+    p_far = lax.dynamic_slice_in_dim(potential, x, 1, axis=0)
+    p_x = lax.ppermute(potential, "space", swap)
+    p_d = lax.ppermute(p_far, "space", raster)
+    p_zo = lax.ppermute(p_far, "space", own_way)
 
     xr1 = lax.ppermute(
         lax.dynamic_slice_in_dim(psi, theirs, early, axis=1), "space", swap
@@ -429,13 +433,8 @@
     second = lax.dynamic_slice_in_dim(psi, theirs + early, window - early, axis=1)
     second, _ = ordered(second, xr1)
     xr2 = lax.ppermute(second, "space", swap)
-    zf1, xr2 = ordered(zf1, xr2)
+    zf1_in, _ = ordered(zf1, xr2)
     zf2 = lax.ppermute(xr2, "space", other_way)
-    sums, weights = partials(count, psi, fields, f_x, f_d)
-    step = 1
-    while step < slabs:
-        sums = sums + lax.ppermute(sums, "space", [(i, i ^ step) for i in range(slabs)])
-        step *= 2
     strong = jnp.broadcast_to(strength[:, None], (count, orbs))
 
     me = lax.axis_index("orb")
@@ -444,25 +443,32 @@
     rows_hot = rows_hot * (pattern[:, 1] == me).astype(BF16)[:, None]
     q = jnp.einsum("ki,kab->iab", rows_hot, q_tiles, preferred_element_type=F32).astype(BF16)
 
-    coefs = coefficients(sums, strong)
-    coefs_c = lax.ppermute(coefs, "orb", beside)
-    coefs_y = lax.ppermute(jnp.concatenate([coefs, coefs_c], axis=0), "orb", across)
-    coefs_yc, coefs_y = coefs_y[2 * count :], coefs_y[: 2 * count]
-    term = nonlocal_term(psi.shape, (coefs, coefs_c, coefs_y, coefs_yc), q, weights)
-
-    operands = (psi, fields, f_x, f_d, f_zo, zo)
-    (block1,) = filtered(count, slabs, 0, rows, True, operands, (xr1,), (zf1,))
+    p_x, f_x, f_d = ordered(p_x, f_x, f_d)
+    operands = (psi, potential, p_x, p_d, p_zo, zo)
+    (block1,) = filtered(slabs, 0, rows, True, operands, (xr1,), (zf1_in,))
     y1 = lax.ppermute(block1, "orb", across)
     c1 = lax.ppermute(block1, "orb", beside)
-    give2, keep2 = filtered(count, slabs, rows, rows, False, operands, (xr1, xr2), (zf1, zf2))
+    sums, weights = partials(count, psi, fields, f_x, f_d)
+    xr2, sums = ordered(xr2, sums)
+    give2, keep2 = filtered(slabs, rows, rows, False, operands, (xr1, xr2), (zf1, zf2))
+    step = 1
+    while step < slabs:
+        sums = sums + lax.ppermute(sums, "space", [(i, i ^ step) for i in range(slabs)])
+        step *= 2
+    coefs = coefficients(sums, strong)
     cg = lax.ppermute(give2, "orb", beside)
     ck = lax.ppermute(keep2, "orb", beside)
     give_y, y1 = ordered(give2, y1)
     yg = lax.ppermute(give_y, "orb", across)
     yc1 = lax.ppermute(y1, "orb", beside)
     give1, keep1 = rotated((block1, c1, y1, yc1), q, 2)
+    keep_y, yg, give1, coefs = ordered(keep2, yg, give1, coefs)
     got1 = lax.ppermute(give1, "space", swap)
-    keep_y, yg = ordered(keep2, yg)
+    coefs_c = lax.ppermute(coefs, "orb", beside)
+    coefs_y = lax.ppermute(jnp.concatenate([coefs, coefs_c], axis=0), "orb", across)
+    coefs_yc, coefs_y = coefs_y[2 * count :], coefs_y[: 2 * count]
+    term = nonlocal_term(psi.shape, (coefs, coefs_c, coefs_y, coefs_yc), q, weights)
+
     yk = lax.ppermute(keep_y, "orb", across)
     ycg = lax.ppermute(yg, "orb", beside)
     (give2,) = rotated((give2, cg, yg, ycg), q, 1)

time: 92.3 us -> 91.8 us (level)
  waiting for transfers between devices: 27.9 us -> 30.1 us
  Pallas kernels: 23.4 us -> 21.5 us
  local copies, waits for them, and re-layouts: 7.31 us -> 9.03 us
  starting transfers between devices: 28.2 us -> 26.7 us
  other arithmetic: 4.18 us -> 3.12 us
    ppermute x2 -> x4, waiting for transfers between devices: 1.33 us -> 9.38 us  [the longest x1 5.49 us: shards(): p_zo = lax.ppermute(p_far, 'space', own_way)]
    ppermute x1, waiting for transfers between devices: 7.99 us -> 0.01 us  [shards(): yg = lax.ppermute(give_y, 'orb', across)]
    ppermute x1, waiting for transfers between devices: 3.06 us -> 0.01 us  [shards(): got1 = lax.ppermute(give1, 'space', swap)]
    ppermute x1, starting transfers between devices: 3.01 us -> 0.17 us  [shards(): lax.ppermute(lax.dynamic_slice_in_dim(psi, theirs, early, axis=1), 'space...]
    ppermute x3, waiting for transfers between devices: 3.7 us -> 6.35 us  [shards(): lax.ppermute(sums, 'space', [(i, i ^ step) for i in range(slabs)])]
    ppermute x2 -> x4, starting transfers between devices: 6.69 us -> 5.02 us  [the longest x1 3.01 us: shards(): p_x = lax.ppermute(potential, 'space', swap)]
    dynamic_slice x1 -> x0, other arithmetic: 1.61 us -> none  [shards(): to_zo = lax.dynamic_slice_in_dim(far, mine // 2, window // 2, axis=0)]
    ppermute x3, starting transfers between devices: 2.46 us -> 4.06 us  [shards(): lax.ppermute(sums, 'space', [(i, i ^ step) for i in range(slabs)])]
  transfers between devices with their start and end apart: 24 -> 26, of which waited for: 8 -> 9; matrix products, arithmetic and copies ran while one was open for 9% -> 10% of each run, Pallas kernels for 20% -> 18%
where the time goes in v4:
time: 91.8 us; the launch traced here: 91.4 us
  waiting for transfers between devices  30.1 us (33%)
  starting transfers between devices  26.7 us (29%)
  Pallas kernels  21.5 us (23%)
  local copies, waits for them, and re-layouts  9.03 us (10%)
  other arithmetic  3.12 us (3%)
    pallas_call x2, Pallas kernels, filtered(): pl.pallas_call(functools.partial(filter_kernel, slabs, start, parts, join...  8.14 us
    pallas_call x1, Pallas kernels, partials(): pl.pallas_call(functools.partial(partial_kernel, count, unroll), out_shap...  6.7 us
    ppermute x3, waiting for transfers between devices, shards(): lax.ppermute(sums, 'space', [(i, i ^ step) for i in range(slabs)])  6.35 us
    ppermute x1, waiting for transfers between devices, shards(): p_zo = lax.ppermute(p_far, 'space', own_way)  5.49 us
    ppermute x1, waiting for transfers between devices, shards(): yk = lax.ppermute(keep_y, 'orb', across)  5.23 us
    ppermute x1, waiting for transfers between devices, shards(): lax.ppermute(lax.dynamic_slice_in_dim(psi, theirs, early, axis=1), 'space...  5.04 us
    ppermute x3, starting transfers between devices, shards(): lax.ppermute(sums, 'space', [(i, i ^ step) for i in range(slabs)])  4.06 us
    ppermute x1, starting transfers between devices, shards(): zf2 = lax.ppermute(xr2, 'space', other_way)  4.05 us
  transfers between devices with their start and end apart: 26, of which 9 were waited for; matrix products, arithmetic and copies ran while one was open for 10% of the time, Pallas kernels for 18%

profile of v4, /device:TPU:0, one launch (start us, length us, event | category | flops | bytes accessed | tf_op | source)
XLA Modules:
  0.0 91.4 jit_solution(8862851206872391596)
XLA Ops:
  0.0 3.0 %collective-permute-start = (f32[2,48,48]{2,1,0:T(8,128)}, f32[2,48,48]{2,1,0:T(8,128)S(1)}, u32[]{:S(2)}, u32[]{:S(2)}) collective-permute-start(f32[2,48,48]{2,1,0:T(8,128)} %refs_1_.3), channel_id=1, source_target_pairs={{0,4},{4,0},{8,12},{12,8},{16,20},{20,16},{24,28},{28,24},{1,5},{5... | collective-permute-start | bytes 55304 | tf_op jit(solution)/shard_map/ppermute | solution.py:424
  3.0 1.0 %constant_dynamic-slice_fusion.1 = bf16[2,16,48,128]{3,2,1,0:T(8,128)(2,1)S(1)} fusion(bf16[2,48,48,128]{3,2,1,0:T(8,128)(2,1)} %refs_0_.3, s32[]{:T(128)S(6)} %select_n.25), kind=kLoop, calls=%fused_computation.23 | loop fusion | bytes 786436 | tf_op jit(solution)/shard_map/dynamic_slice | solution.py:429
  4.0 0.2 collective-permute-start.6
  4.2 2.0 %constant_dynamic-slice_fusion.2 = bf16[2,26,48,128]{3,2,1,0:T(8,128)(2,1)} fusion(bf16[2,48,48,128]{3,2,1,0:T(8,128)(2,1)} %refs_0_.3, s32[]{:T(128)S(6)} %select_n.24), kind=kLoop, calls=%fused_computation.24 | loop fusion | bytes 1277956 | tf_op jit(solution)/shard_map/dynamic_slice | solution.py:431
  6.3 1.3 %collective-permute-start.5 = (bf16[2,26,48,128]{3,2,1,0:T(8,128)(2,1)}, bf16[2,26,48,128]{3,2,1,0:T(8,128)(2,1)S(1)}, u32[]{:S(2)}, u32[]{:S(2)}) collective-permute-start(bf16[2,26,48,128]{3,2,1,0:T(8,128)(2,1)} %constant_dynamic-slice_fusion.2), channel_id=1, source_target_pairs={{4,12},{8,0},{12,20},{16,8},{20,28},{24,16},{5,13},{9,1},{13,21},{... | collective-permute-start | bytes 1916936 | tf_op jit(solution)/shard_map/ppermute | solution.py:431
  7.6 0.1 fusion.2
  7.8 0.1 pad.7.clone
  7.9 1.0 %maximum_maximum_fusion = bf16[2,48,16,48]{3,2,1,0:T(8,128)(2,1)} fusion(bf16[2,48,1,48]{3,2,1,0:T(2,128)(2,1)S(1)} %copy.18, bf16[2,48,1,48]{3,2,1,0:T(2,128)(2,1)S(1)} %copy.17, bf16[2,48,8,48]{3,2,1,0:T(8,128)(2,1)S(1)} %fusion.2, bf16[16]{0:T(256)(128)(2,1)S(1)} %pad.7.clone), kind=kLoop, calls=%fused_computation.2 | loop fusion | flops 589824 | bytes 239648 | tf_op jit(solution)/shard_map/concatenate | solution.py:409
  8.9 0.7 constant_dynamic-slice_fusion
  9.6 5.0 %collective-permute-done.6.refs_6_ = bf16[2,16,48,128]{3,2,1,0:T(8,128)(2,1)S(1)} collective-permute-done((bf16[2,16,48,128]{3,2,1,0:T(8,128)(2,1)S(1)}, bf16[2,16,48,128]{3,2,1,0:T(8,128)(2,1)S(1)}, u32[]{:S(2)}, u32[]{:S(2)}) %collective-permute-start.6) | collective-permute-done | bytes 393248 | tf_op jit(solution)/shard_map/ppermute | solution.py:428
  14.7 0.9 collective-permute-start.7
  15.6 3.6 %collective-permute-start.8 = (bf16[2,16,48,128]{3,2,1,0:T(8,128)(2,1)S(1)}, bf16[2,16,48,128]{3,2,1,0:T(8,128)(2,1)S(1)}, u32[]{:S(2)}, u32[]{:S(2)}) collective-permute-start(bf16[2,16,48,128]{3,2,1,0:T(8,128)(2,1)S(1)} %collective-permute-done.6.refs_6_), channel_id=1, source_target_pairs={{0,8},{8,16},{12,4},{16,24},{20,12},{28,20},{1,9},{9,17},{13,5},{1... | collective-permute-start | bytes 1179656 | tf_op jit(solution)/shard_map/ppermute | solution.py:432
  19.2 1.7 %fusion.18 = (bf16[2,24,16,48]{3,2,1,0:T(8,128)(2,1)S(1)}, bf16[2,24,16,48]{3,2,1,0:T(8,128)(2,1)}) fusion(bf16[2,48,16,48]{3,2,1,0:T(8,128)(2,1)} %maximum_maximum_fusion), kind=kLoop, calls=%fused_computation.38 | loop fusion | bytes 294912 | tf_op jit(solution)/shard_map/slice | solution.py:418
  21.0 1.2 %fusion.6 = (bf16[24,16,96]{2,1,0:T(8,128)(2,1)S(1)}, bf16[24,16,96]{2,1,0:T(8,128)(2,1)S(1)}) fusion(s32[]{:T(128)S(6)} %select_n.23, bf16[2,24,16,48]{3,2,1,0:T(8,128)(2,1)} %get-tuple-element.46, bf16[2,24,16,48]{3,2,1,0:T(8,128)(2,1)S(1)} %get-tuple-element.45, s32[]{:T(128)S(6)} %select_n.22), kind=kLoop, calls=%fused_computation.14 | loop fusion | flops 294912 | bytes 294920 | tf_op jit(solution)/shard_map/jit(dynamic_index_in_dim)/squeeze | solution.py:419
  22.1 0.1 collective-permute-start.1
  22.2 0.0 collective-permute-done.refs_2_
  22.2 0.7 collective-permute-start.2
  22.9 3.9 %collective-permute-done.1.f_x = bf16[24,16,96]{2,1,0:T(8,128)(2,1)S(1)} collective-permute-done((bf16[24,16,96]{2,1,0:T(8,128)(2,1)S(1)}, bf16[24,16,96]{2,1,0:T(8,128)(2,1)S(1)}, u32[]{:S(2)}, u32[]{:S(2)}) %collective-permute-start.1) | collective-permute-done | bytes 73760 | tf_op jit(solution)/shard_map/ppermute | solution.py:421
  26.8 0.7 collective-permute-start.3
  27.5 0.0 collective-permute-done.2.f_d
  27.5 1.3 %collective-permute-start.4 = (f32[1,48,48]{2,1,0:T(8,128)S(1)}, f32[1,48,48]{2,1,0:T(8,128)S(1)}, u32[]{:S(2)}, u32[]{:S(2)}) collective-permute-start(f32[1,48,48]{2,1,0:T(8,128)S(1)} %constant_dynamic-slice_fusion.3), channel_id=1, source_target_pairs={{4,12},{8,0},{12,20},{16,8},{20,28},{24,16},{5,13},{9,1},{13,21},{... | collective-permute-start | bytes 27656 | tf_op jit(solution)/shard_map/ppermute | solution.py:426
  28.8 0.7 copy-done.2
  29.6 5.5 %collective-permute-done.4.refs_4_ = f32[1,48,48]{2,1,0:T(8,128)S(1)} collective-permute-done((f32[1,48,48]{2,1,0:T(8,128)S(1)}, f32[1,48,48]{2,1,0:T(8,128)S(1)}, u32[]{:S(2)}, u32[]{:S(2)}) %collective-permute-start.4) | collective-permute-done | bytes 9248 | tf_op jit(solution)/shard_map/ppermute | solution.py:426
  35.1 1.0 %copy-done.3 = bf16[2,16,48,128]{3,2,1,0:T(8,128)(2,1)S(1)} copy-done((bf16[2,16,48,128]{3,2,1,0:T(8,128)(2,1)S(1)}, bf16[2,16,48,128]{3,2,1,0:T(8,128)(2,1)}, u32[]{:S(2)}) %copy-start.3) | copy-done | bytes 393240
  36.1 4.0 %filtered.3.refs_0_ = bf16[4,12,48,128]{3,2,1,0:T(8,128)(2,1)S(1)} custom-call(bf16[2,48,48,128]{3,2,1,0:T(8,128)(2,1)S(1)} %copy-done.1, f32[2,48,48]{2,1,0:T(8,128)S(1)} %copy-done.4, f32[2,48,48]{2,1,0:T(8,128)S(1)} %collective-permute-done.refs_2_, f32[1,48,48]{2,1,0:T(8,128)S(1)} %collective-permute-done.3.refs_3_, ...), custom_call_target="tpu_custom_call" | custom-call | flops 2949120 | bytes 184320 | tf_op jit(solution)/shard_map/filtered/pallas_call | solution.py:297
  40.1 1.6 %collective-permute-start.10 = (bf16[4,12,48,128]{3,2,1,0:T(8,128)(2,1)S(1)}, bf16[4,12,48,128]{3,2,1,0:T(8,128)(2,1)}, u32[]{:S(2)}, u32[]{:S(2)}) collective-permute-start(bf16[4,12,48,128]{3,2,1,0:T(8,128)(2,1)S(1)} %filtered.3.refs_0_), channel_id=1, source_target_pairs={{0,2},{1,3},{2,0},{3,1},{4,6},{5,7},{6,4},{7,5},{8,10},{9,11},{10,... | collective-permute-start | bytes 1769480 | tf_op jit(solution)/shard_map/ppermute | solution.py:449
  41.7 4.0 %collective-permute-start.9 = (bf16[2,10,48,128]{3,2,1,0:T(8,128)(2,1)S(1)}, bf16[2,10,48,128]{3,2,1,0:T(8,128)(2,1)S(1)}, u32[]{:S(2)}, u32[]{:S(2)}) collective-permute-start(bf16[2,10,48,128]{3,2,1,0:T(8,128)(2,1)S(1)} %collective-permute-done.7.refs_7_), channel_id=1, source_target_pairs={{0,8},{8,16},{12,4},{16,24},{20,12},{28,20},{1,9},{9,17},{13,5},{1... | collective-permute-start | bytes 737288 | tf_op jit(solution)/shard_map/ppermute | solution.py:437
  45.8 0.7 copy-done.9
  46.5 0.1 pad_maximum_fusion.f_own
  46.6 6.7 %partials.1 = (f32[24,128]{1,0:T(8,128)S(1)}, bf16[2,24,48,96]{3,2,1,0:T(8,128)(2,1)S(1)}) custom-call(bf16[2,48,48,128]{3,2,1,0:T(8,128)(2,1)S(1)} %copy-done.1, bf16[2,24,16,96]{3,2,1,0:T(8,128)(2,1)S(1)} %pad_maximum_fusion.f_own, bf16[24,16,96]{2,1,0:T(8,128)(2,1)S(1)} %collective-permute-done.1.f_x, bf16[24,16,96]{2,1,0:T(8,128)(2,1)S(1)} %collective-permute-done.2.f_d), custom_call_target="tpu_custom_call" | custom-call | flops 3538944 | bytes 147456 | tf_op jit(solution)/shard_map/partials/pallas_call | solution.py:89
  53.3 0.0 copy-start.5
  53.3 0.0 copy-start.18
  53.3 0.0 copy-start.17
  53.3 0.1 collective-permute-start.12
  53.5 4.1 %filtered.2 = (bf16[2,12,48,128]{3,2,1,0:T(8,128)(2,1)S(1)}, bf16[2,12,48,128]{3,2,1,0:T(8,128)(2,1)S(1)}) custom-call(bf16[2,48,48,128]{3,2,1,0:T(8,128)(2,1)S(1)} %copy-done.1, f32[2,48,48]{2,1,0:T(8,128)S(1)} %copy-done.4, f32[2,48,48]{2,1,0:T(8,128)S(1)} %copy-done.12, f32[1,48,48]{2,1,0:T(8,128)S(1)} %collective-permute-done.3.refs_3_, ...), custom_call_target="tpu_custom_call" | custom-call | flops 2949120 | bytes 184320 | tf_op jit(solution)/shard_map/filtered/pallas_call | solution.py:297
  57.6 0.7 copy-done.7
  58.3 0.5 collective-permute-start.13
  58.8 0.1 collective-permute-start.14
  58.9 0.7 fusion.14
  59.6 2.9 %collective-permute-done.14 = f32[24,128]{1,0:T(8,128)S(1)} collective-permute-done((f32[24,128]{1,0:T(8,128)S(1)}, f32[24,128]{1,0:T(8,128)S(1)}, u32[]{:S(2)}, u32[]{:S(2)}) %collective-permute-start.14) | collective-permute-done | bytes 12320 | tf_op jit(solution)/shard_map/ppermute | solution.py:456
  62.5 1.6 %collective-permute-start.15 = (f32[24,128]{1,0:T(8,128)S(1)}, f32[24,128]{1,0:T(8,128)S(1)}, u32[]{:S(2)}, u32[]{:S(2)}) collective-permute-start(f32[24,128]{1,0:T(8,128)S(1)} %add.39), channel_id=1, source_target_pairs={{0,8},{4,12},{8,0},{12,4},{16,24},{20,28},{24,16},{28,20},{1,9},{5... | collective-permute-start | bytes 36872 | tf_op jit(solution)/shard_map/ppermute | solution.py:456
  64.1 0.5 collective-permute-start.11
  64.6 1.6 %collective-permute-done.15 = f32[24,128]{1,0:T(8,128)S(1)} collective-permute-done((f32[24,128]{1,0:T(8,128)S(1)}, f32[24,128]{1,0:T(8,128)S(1)}, u32[]{:S(2)}, u32[]{:S(2)}) %collective-permute-start.15) | collective-permute-done | bytes 12320 | tf_op jit(solution)/shard_map/ppermute | solution.py:456
  66.2 2.4 %collective-permute-start.16 = (f32[24,128]{1,0:T(8,128)S(1)}, f32[24,128]{1,0:T(8,128)S(1)}, u32[]{:S(2)}, u32[]{:S(2)}) collective-permute-start(f32[24,128]{1,0:T(8,128)S(1)} %add.40), channel_id=1, source_target_pairs={{0,16},{4,20},{8,24},{12,28},{16,0},{20,4},{24,8},{28,12},{1,17},{... | collective-permute-start | bytes 36872 | tf_op jit(solution)/shard_map/ppermute | solution.py:456
  68.6 0.3 fusion
  69.0 1.8 %collective-permute-done.16 = f32[24,128]{1,0:T(8,128)S(1)} collective-permute-done((f32[24,128]{1,0:T(8,128)S(1)}, f32[24,128]{1,0:T(8,128)S(1)}, u32[]{:S(2)}, u32[]{:S(2)}) %collective-permute-start.16) | collective-permute-done | bytes 12320 | tf_op jit(solution)/shard_map/ppermute | solution.py:456
  70.8 0.1 broadcast_in_dim.28.strength
  70.9 0.1 coefficients.1.a
  71.0 0.1 collective-permute-start.23
  71.1 2.2 %rotated.3 = (bf16[2,12,48,128]{3,2,1,0:T(8,128)(2,1)S(1)}, bf16[2,12,48,128]{3,2,1,0:T(8,128)(2,1)S(1)}) custom-call(bf16[4,12,48,128]{3,2,1,0:T(8,128)(2,1)S(1)} %filtered.3.refs_0_, bf16[4,12,48,128]{3,2,1,0:T(8,128)(2,1)} %collective-permute-done.12.refs_1_, bf16[4,12,48,128]{3,2,1,0:T(8,128)(2,1)} %collective-permute-done.10.refs_2_, ...), custom_call_target="tpu_custom_call" | custom-call | flops 18874368 | bytes 184320 | tf_op jit(solution)/shard_map/rotated/pallas_call | solution.py:341
  73.3 0.0 copy-start.6
  73.3 0.5 collective-permute-start.24
  73.9 0.5 collective-permute-start.20
  74.4 0.5 collective-permute-start.19
  74.9 1.6 %collective-permute-start.22 = (bf16[2,12,48,128]{3,2,1,0:T(8,128)(2,1)S(1)}, bf16[2,12,48,128]{3,2,1,0:T(8,128)(2,1)S(1)}, u32[]{:S(2)}, u32[]{:S(2)}) collective-permute-start(bf16[2,12,48,128]{3,2,1,0:T(8,128)(2,1)S(1)} %get-tuple-element.41), channel_id=1, source_target_pairs={{0,4},{4,0},{8,12},{12,8},{16,20},{20,16},{24,28},{28,24},{1,5},{5... | collective-permute-start | bytes 884744 | tf_op jit(solution)/shard_map/ppermute | solution.py:466
  76.5 0.6 rotated.5
  77.2 0.5 collective-permute-start.25
  77.7 5.2 %collective-permute-done.20.refs_2_ = bf16[2,12,48,128]{3,2,1,0:T(8,128)(2,1)S(1)} collective-permute-done((bf16[2,12,48,128]{3,2,1,0:T(8,128)(2,1)S(1)}, bf16[2,12,48,128]{3,2,1,0:T(8,128)(2,1)S(1)}, u32[]{:S(2)}, u32[]{:S(2)}) %collective-permute-start.20) | collective-permute-done | bytes 294944 | tf_op jit(solution)/shard_map/ppermute | solution.py:472
  82.9 0.6 collective-permute-start.18
  83.5 3.1 %collective-permute-done.18 = bf16[32,128]{1,0:T(8,128)(2,1)S(1)} collective-permute-done((bf16[32,128]{1,0:T(8,128)(2,1)S(1)}, bf16[32,128]{1,0:T(8,128)(2,1)S(1)}, u32[]{:S(2)}, u32[]{:S(2)}) %collective-permute-start.18) | collective-permute-done | bytes 8224 | tf_op jit(solution)/shard_map/ppermute | solution.py:468
  86.6 1.9 %nonlocal.1.term = f32[2,48,48,128]{3,2,1,0:T(8,128)S(1)} custom-call(bf16[16,128]{1,0:T(8,128)(2,1)S(1)} %coefficients.1.a, bf16[16,128]{1,0:T(8,128)(2,1)S(1)} %collective-permute-done.17.b, bf16[16,128]{1,0:T(8,128)(2,1)S(1)} %get-tuple-element.50.c, bf16[16,128]{1,0:T(8,128)(2,1)S(1)} %get-tuple-element.49.d, bf16[4,128,128]{2,1,0:T(8,128)(2,1)S(1)} %copy.27.refs_4_.q, ...), custom_call_target="tpu_custom_call" | custom-call | flops 256 | bytes 256 | tf_op jit(solution)/shard_map/nonlocal/pallas_call | solution.py:164
  88.5 0.6 rotated.4.refs_1_
  89.2 1.0 %collective-permute-done.25.refs_3_ = bf16[2,12,48,128]{3,2,1,0:T(8,128)(2,1)S(1)} collective-permute-done((bf16[2,12,48,128]{3,2,1,0:T(8,128)(2,1)S(1)}, bf16[2,12,48,128]{3,2,1,0:T(8,128)(2,1)S(1)}, u32[]{:S(2)}, u32[]{:S(2)}) %collective-permute-start.25) | collective-permute-done | bytes 294944 | tf_op jit(solution)/shard_map/ppermute | solution.py:475
  90.2 1.2 %assembled.1 = bf16[2,48,48,128]{3,2,1,0:T(8,128)(2,1)} custom-call(f32[2,48,48,128]{3,2,1,0:T(8,128)S(1)} %nonlocal.1.term, bf16[2,12,48,128]{3,2,1,0:T(8,128)(2,1)S(1)} %get-tuple-element.39.refs_0_, bf16[2,12,48,128]{3,2,1,0:T(8,128)(2,1)S(1)} %rotated.4.refs_1_, bf16[2,12,48,128]{3,2,1,0:T(8,128)(2,1)S(1)} %collective-permute-done.22.refs_2_, ...), custom_call_target="tpu_custom_call" | custom-call | flops 256 | bytes 256 | tf_op jit(solution)/shard_map/assembled/pallas_call | solution.py:364
  (63 shorter events, 0.3 us)
Async XLA Ops:
  0.0 68.6 %copy-start = (bf16[12,128,128]{2,1,0:T(8,128)(2,1)S(1)}, bf16[12,128,128]{2,1,0:T(8,128)(2,1)}, u32[]{:S(2)}) copy-start(bf16[12,128,128]{2,1,0:T(8,128)(2,1)} %param.13) | copy-start | bytes 1179652
  0.0 7.6 %copy-start.19 = (s32[8]{0:T(128)S(1)}, s32[8]{0:T(128)}, u32[]{:S(2)}) copy-start(s32[8]{0:T(128)} %param.11) | copy-start | bytes 100
  0.0 7.6 %copy-start.16 = (bf16[8,2,48,48]{3,2,1,0:T(8,128)(2,1)S(1)}, bf16[8,2,48,48]{3,2,1,0:T(8,128)(2,1)}, u32[]{:S(2)}) copy-start(bf16[8,2,48,48]{3,2,1,0:T(8,128)(2,1)} %param.9) | copy-start | bytes 221188
  0.0 22.2 %collective-permute-start = (f32[2,48,48]{2,1,0:T(8,128)}, f32[2,48,48]{2,1,0:T(8,128)S(1)}, u32[]{:S(2)}, u32[]{:S(2)}) collective-permute-start(f32[2,48,48]{2,1,0:T(8,128)} %refs_1_.3), channel_id=1, source_target_pairs={{0,4},{4,0},{8,12},{12,8},{16,20},{20,16},{24,28},{28,24},{1,5},{5... | collective-permute-start | bytes 55304 | tf_op jit(solution)/shard_map/ppermute | solution.py:424
  3.0 4.7 %copy-start.4 = (f32[2,48,48]{2,1,0:T(8,128)S(1)}, f32[2,48,48]{2,1,0:T(8,128)}, u32[]{:S(2)}) copy-start(f32[2,48,48]{2,1,0:T(8,128)} %refs_1_.3) | copy-start | bytes 55300
  4.0 10.6 %collective-permute-start.6 = (bf16[2,16,48,128]{3,2,1,0:T(8,128)(2,1)S(1)}, bf16[2,16,48,128]{3,2,1,0:T(8,128)(2,1)S(1)}, u32[]{:S(2)}, u32[]{:S(2)}) collective-permute-start(bf16[2,16,48,128]{3,2,1,0:T(8,128)(2,1)S(1)} %constant_dynamic-slice_fusion.1), channel_id=1, source_target_pairs={{0,4},{4,0},{8,12},{12,8},{16,20},{20,16},{24,28},{28,24},{1,5},{5... | collective-permute-start | bytes 1179656 | tf_op jit(solution)/shard_map/ppermute | solution.py:428
  4.2 4.7 %copy-start.1 = (bf16[2,48,48,128]{3,2,1,0:T(8,128)(2,1)S(1)}, bf16[2,48,48,128]{3,2,1,0:T(8,128)(2,1)}, u32[]{:S(2)}) copy-start(bf16[2,48,48,128]{3,2,1,0:T(8,128)(2,1)} %refs_0_.3) | copy-start | bytes 3538948
  6.3 28.8 %collective-permute-start.5 = (bf16[2,26,48,128]{3,2,1,0:T(8,128)(2,1)}, bf16[2,26,48,128]{3,2,1,0:T(8,128)(2,1)S(1)}, u32[]{:S(2)}, u32[]{:S(2)}) collective-permute-start(bf16[2,26,48,128]{3,2,1,0:T(8,128)(2,1)} %constant_dynamic-slice_fusion.2), channel_id=1, source_target_pairs={{4,12},{8,0},{12,20},{16,8},{20,28},{24,16},{5,13},{9,1},{13,21},{... | collective-permute-start | bytes 1916936 | tf_op jit(solution)/shard_map/ppermute | solution.py:431
  14.7 14.1 %collective-permute-start.7 = (bf16[2,10,48,128]{3,2,1,0:T(8,128)(2,1)}, bf16[2,10,48,128]{3,2,1,0:T(8,128)(2,1)S(1)}, u32[]{:S(2)}, u32[]{:S(2)}) collective-permute-start(bf16[2,10,48,128]{3,2,1,0:T(8,128)(2,1)} %constant_dynamic-slice_fusion), channel_id=1, source_target_pairs={{0,4},{4,0},{8,12},{12,8},{16,20},{20,16},{24,28},{28,24},{1,5},{5... | collective-permute-start | bytes 737288 | tf_op jit(solution)/shard_map/ppermute | solution.py:435
  15.6 13.2 %collective-permute-start.8 = (bf16[2,16,48,128]{3,2,1,0:T(8,128)(2,1)S(1)}, bf16[2,16,48,128]{3,2,1,0:T(8,128)(2,1)S(1)}, u32[]{:S(2)}, u32[]{:S(2)}) collective-permute-start(bf16[2,16,48,128]{3,2,1,0:T(8,128)(2,1)S(1)} %collective-permute-done.6.refs_6_), channel_id=1, source_target_pairs={{0,8},{8,16},{12,4},{16,24},{20,12},{28,20},{1,9},{9,17},{13,5},{1... | collective-permute-start | bytes 1179656 | tf_op jit(solution)/shard_map/ppermute | solution.py:432
  21.0 14.1 %copy-start.13 = (bf16[2,24,16,48]{3,2,1,0:T(8,128)(2,1)}, bf16[2,24,16,48]{3,2,1,0:T(8,128)(2,1)S(1)}, u32[]{:S(2)}) copy-start(bf16[2,24,16,48]{3,2,1,0:T(8,128)(2,1)S(1)} %get-tuple-element.45) | copy-start | bytes 221188
  21.0 25.5 %copy-start.15 = (bf16[2,24,16,48]{3,2,1,0:T(8,128)(2,1)S(1)}, bf16[2,24,16,48]{3,2,1,0:T(8,128)(2,1)}, u32[]{:S(2)}) copy-start(bf16[2,24,16,48]{3,2,1,0:T(8,128)(2,1)} %get-tuple-element.46) | copy-start | bytes 221188
  22.1 4.7 %collective-permute-start.1 = (bf16[24,16,96]{2,1,0:T(8,128)(2,1)S(1)}, bf16[24,16,96]{2,1,0:T(8,128)(2,1)S(1)}, u32[]{:S(2)}, u32[]{:S(2)}) collective-permute-start(bf16[24,16,96]{2,1,0:T(8,128)(2,1)S(1)} %get-tuple-element.44), channel_id=1, source_target_pairs={{0,4},{4,0},{8,12},{12,8},{16,20},{20,16},{24,28},{28,24},{1,5},{5... | collective-permute-start | bytes 221192 | tf_op jit(solution)/shard_map/ppermute | solution.py:421
  22.2 17.9 %copy-start.11 = (f32[2,48,48]{2,1,0:T(8,128)}, f32[2,48,48]{2,1,0:T(8,128)S(1)}, u32[]{:S(2)}) copy-start(f32[2,48,48]{2,1,0:T(8,128)S(1)} %collective-permute-done.refs_2_) | copy-start | bytes 55300
  22.2 5.2 %collective-permute-start.2 = (bf16[24,16,96]{2,1,0:T(8,128)(2,1)S(1)}, bf16[24,16,96]{2,1,0:T(8,128)(2,1)S(1)}, u32[]{:S(2)}, u32[]{:S(2)}) collective-permute-start(bf16[24,16,96]{2,1,0:T(8,128)(2,1)S(1)} %get-tuple-element.43), channel_id=1, source_target_pairs={{4,8},{8,4},{12,16},{16,12},{20,24},{24,20},{5,9},{9,5},{13,17},{1... | collective-permute-start | bytes 221192 | tf_op jit(solution)/shard_map/ppermute | solution.py:422
  26.8 2.8 %collective-permute-start.3 = (f32[1,48,48]{2,1,0:T(8,128)S(1)}, f32[1,48,48]{2,1,0:T(8,128)S(1)}, u32[]{:S(2)}, u32[]{:S(2)}) collective-permute-start(f32[1,48,48]{2,1,0:T(8,128)S(1)} %constant_dynamic-slice_fusion.3), channel_id=1, source_target_pairs={{4,8},{8,4},{12,16},{16,12},{20,24},{24,20},{5,9},{9,5},{13,17},{1... | collective-permute-start | bytes 27656 | tf_op jit(solution)/shard_map/ppermute | solution.py:425
  27.5 7.6 %collective-permute-start.4 = (f32[1,48,48]{2,1,0:T(8,128)S(1)}, f32[1,48,48]{2,1,0:T(8,128)S(1)}, u32[]{:S(2)}, u32[]{:S(2)}) collective-permute-start(f32[1,48,48]{2,1,0:T(8,128)S(1)} %constant_dynamic-slice_fusion.3), channel_id=1, source_target_pairs={{4,12},{8,0},{12,20},{16,8},{20,28},{24,16},{5,13},{9,1},{13,21},{... | collective-permute-start | bytes 27656 | tf_op jit(solution)/shard_map/ppermute | solution.py:426
  28.8 0.8 copy-start.2
  35.1 1.0 %copy-start.3 = (bf16[2,16,48,128]{3,2,1,0:T(8,128)(2,1)S(1)}, bf16[2,16,48,128]{3,2,1,0:T(8,128)(2,1)}, u32[]{:S(2)}) copy-start(bf16[2,16,48,128]{3,2,1,0:T(8,128)(2,1)} %copy-done.2) | copy-start | bytes 1179652
  36.1 10.4 %copy-start.14 = (bf16[2,24,16,48]{3,2,1,0:T(8,128)(2,1)S(1)}, bf16[2,24,16,48]{3,2,1,0:T(8,128)(2,1)}, u32[]{:S(2)}) copy-start(bf16[2,24,16,48]{3,2,1,0:T(8,128)(2,1)} %copy-done.13) | copy-start | bytes 221188
  40.1 18.2 %collective-permute-start.10 = (bf16[4,12,48,128]{3,2,1,0:T(8,128)(2,1)S(1)}, bf16[4,12,48,128]{3,2,1,0:T(8,128)(2,1)}, u32[]{:S(2)}, u32[]{:S(2)}) collective-permute-start(bf16[4,12,48,128]{3,2,1,0:T(8,128)(2,1)S(1)} %filtered.3.refs_0_), channel_id=1, source_target_pairs={{0,2},{1,3},{2,0},{3,1},{4,6},{5,7},{6,4},{7,5},{8,10},{9,11},{10,... | collective-permute-start | bytes 1769480 | tf_op jit(solution)/shard_map/ppermute | solution.py:449
  41.7 11.8 %copy-start.12 = (f32[2,48,48]{2,1,0:T(8,128)S(1)}, f32[2,48,48]{2,1,0:T(8,128)}, u32[]{:S(2)}) copy-start(f32[2,48,48]{2,1,0:T(8,128)} %copy-done.11) | copy-start | bytes 55300
  41.7 11.7 %collective-permute-start.9 = (bf16[2,10,48,128]{3,2,1,0:T(8,128)(2,1)S(1)}, bf16[2,10,48,128]{3,2,1,0:T(8,128)(2,1)S(1)}, u32[]{:S(2)}, u32[]{:S(2)}) collective-permute-start(bf16[2,10,48,128]{3,2,1,0:T(8,128)(2,1)S(1)} %collective-permute-done.7.refs_7_), channel_id=1, source_target_pairs={{0,8},{8,16},{12,4},{16,24},{20,12},{28,20},{1,9},{9,17},{13,5},{1... | collective-permute-start | bytes 737288 | tf_op jit(solution)/shard_map/ppermute | solution.py:437
  45.7 0.7 copy-start.9
  46.6 6.9 %copy-start.10 = (bf16[2,10,48,128]{3,2,1,0:T(8,128)(2,1)S(1)}, bf16[2,10,48,128]{3,2,1,0:T(8,128)(2,1)}, u32[]{:S(2)}) copy-start(bf16[2,10,48,128]{3,2,1,0:T(8,128)(2,1)} %copy-done.9) | copy-start | bytes 737284
  53.3 4.3 %copy-start.5 = (bf16[2,24,48,96]{3,2,1,0:T(8,128)(2,1)}, bf16[2,24,48,96]{3,2,1,0:T(8,128)(2,1)S(1)}, u32[]{:S(2)}) copy-start(bf16[2,24,48,96]{3,2,1,0:T(8,128)(2,1)S(1)} %get-tuple-element.38.weights) | copy-start | bytes 1327108
  53.3 5.5 %copy-start.18 = (s32[12,2]{0,1:T(2,128)S(1)}, s32[12,2]{0,1:T(2,128)}, u32[]{:S(2)}) copy-start(s32[12,2]{0,1:T(2,128)} %param.12) | copy-start | bytes 292
  53.3 17.5 %copy-start.17 = (f32[8]{0:T(128)S(1)}, f32[8]{0:T(128)}, u32[]{:S(2)}) copy-start(f32[8]{0:T(128)} %param.10) | copy-start | bytes 100
  53.3 17.8 %collective-permute-start.12 = (bf16[4,12,48,128]{3,2,1,0:T(8,128)(2,1)S(1)}, bf16[4,12,48,128]{3,2,1,0:T(8,128)(2,1)}, u32[]{:S(2)}, u32[]{:S(2)}) collective-permute-start(bf16[4,12,48,128]{3,2,1,0:T(8,128)(2,1)S(1)} %filtered.3.refs_0_), channel_id=1, source_target_pairs={{0,1},{1,0},{2,3},{3,2},{4,5},{5,4},{6,7},{7,6},{8,9},{9,8},{10,11... | collective-permute-start | bytes 1769480 | tf_op jit(solution)/shard_map/ppermute | solution.py:450
  57.6 0.7 copy-start.7
  58.3 12.8 %collective-permute-start.13 = (bf16[4,12,48,128]{3,2,1,0:T(8,128)(2,1)}, bf16[4,12,48,128]{3,2,1,0:T(8,128)(2,1)S(1)}, u32[]{:S(2)}, u32[]{:S(2)}) collective-permute-start(bf16[4,12,48,128]{3,2,1,0:T(8,128)(2,1)} %collective-permute-done.10.refs_2_), channel_id=1, source_target_pairs={{0,1},{1,0},{2,3},{3,2},{4,5},{5,4},{6,7},{7,6},{8,9},{9,8},{10,11... | collective-permute-start | bytes 1769480 | tf_op jit(solution)/shard_map/ppermute | solution.py:463
  58.8 3.7 %collective-permute-start.14 = (f32[24,128]{1,0:T(8,128)S(1)}, f32[24,128]{1,0:T(8,128)S(1)}, u32[]{:S(2)}, u32[]{:S(2)}) collective-permute-start(f32[24,128]{1,0:T(8,128)S(1)} %get-tuple-element.36), channel_id=1, source_target_pairs={{0,4},{4,0},{8,12},{12,8},{16,20},{20,16},{24,28},{28,24},{1,5},{5... | collective-permute-start | bytes 36872 | tf_op jit(solution)/shard_map/ppermute | solution.py:456
  62.5 3.7 %collective-permute-start.15 = (f32[24,128]{1,0:T(8,128)S(1)}, f32[24,128]{1,0:T(8,128)S(1)}, u32[]{:S(2)}, u32[]{:S(2)}) collective-permute-start(f32[24,128]{1,0:T(8,128)S(1)} %add.39), channel_id=1, source_target_pairs={{0,8},{4,12},{8,0},{12,4},{16,24},{20,28},{24,16},{28,20},{1,9},{5... | collective-permute-start | bytes 36872 | tf_op jit(solution)/shard_map/ppermute | solution.py:456
  64.1 9.2 %collective-permute-start.11 = (bf16[2,12,48,128]{3,2,1,0:T(8,128)(2,1)}, bf16[2,12,48,128]{3,2,1,0:T(8,128)(2,1)S(1)}, u32[]{:S(2)}, u32[]{:S(2)}) collective-permute-start(bf16[2,12,48,128]{3,2,1,0:T(8,128)(2,1)} %copy-done.7), channel_id=1, source_target_pairs={{0,2},{1,3},{2,0},{3,1},{4,6},{5,7},{6,4},{7,5},{8,10},{9,11},{10,... | collective-permute-start | bytes 884744 | tf_op jit(solution)/shard_map/ppermute | solution.py:462
  66.2 4.6 %collective-permute-start.16 = (f32[24,128]{1,0:T(8,128)S(1)}, f32[24,128]{1,0:T(8,128)S(1)}, u32[]{:S(2)}, u32[]{:S(2)}) collective-permute-start(f32[24,128]{1,0:T(8,128)S(1)} %add.40), channel_id=1, source_target_pairs={{0,16},{4,20},{8,24},{12,28},{16,0},{20,4},{24,8},{28,12},{1,17},{... | collective-permute-start | bytes 36872 | tf_op jit(solution)/shard_map/ppermute | solution.py:456
  71.0 5.5 %copy-start.8 = (bf16[2,12,48,128]{3,2,1,0:T(8,128)(2,1)S(1)}, bf16[2,12,48,128]{3,2,1,0:T(8,128)(2,1)}, u32[]{:S(2)}) copy-start(bf16[2,12,48,128]{3,2,1,0:T(8,128)(2,1)} %copy-done.7) | copy-start | bytes 884740
  71.0 3.9 %collective-permute-start.23 = (bf16[2,12,48,128]{3,2,1,0:T(8,128)(2,1)}, bf16[2,12,48,128]{3,2,1,0:T(8,128)(2,1)S(1)}, u32[]{:S(2)}, u32[]{:S(2)}) collective-permute-start(bf16[2,12,48,128]{3,2,1,0:T(8,128)(2,1)} %copy-done.7), channel_id=1, source_target_pairs={{0,1},{1,0},{2,3},{3,2},{4,5},{5,4},{6,7},{7,6},{8,9},{9,8},{10,11... | collective-permute-start | bytes 884744 | tf_op jit(solution)/shard_map/ppermute | solution.py:459
  73.3 13.3 %copy-start.6 = (bf16[2,24,48,96]{3,2,1,0:T(8,128)(2,1)S(1)}, bf16[2,24,48,96]{3,2,1,0:T(8,128)(2,1)}, u32[]{:S(2)}) copy-start(bf16[2,24,48,96]{3,2,1,0:T(8,128)(2,1)} %copy-done.5) | copy-start | bytes 1327108
  73.3 3.2 %collective-permute-start.24 = (bf16[2,12,48,128]{3,2,1,0:T(8,128)(2,1)S(1)}, bf16[2,12,48,128]{3,2,1,0:T(8,128)(2,1)S(1)}, u32[]{:S(2)}, u32[]{:S(2)}) collective-permute-start(bf16[2,12,48,128]{3,2,1,0:T(8,128)(2,1)S(1)} %collective-permute-done.11.refs_2_), channel_id=1, source_target_pairs={{0,1},{1,0},{2,3},{3,2},{4,5},{5,4},{6,7},{7,6},{8,9},{9,8},{10,11... | collective-permute-start | bytes 884744 | tf_op jit(solution)/shard_map/ppermute | solution.py:473
  73.9 9.0 %collective-permute-start.20 = (bf16[2,12,48,128]{3,2,1,0:T(8,128)(2,1)S(1)}, bf16[2,12,48,128]{3,2,1,0:T(8,128)(2,1)S(1)}, u32[]{:S(2)}, u32[]{:S(2)}) collective-permute-start(bf16[2,12,48,128]{3,2,1,0:T(8,128)(2,1)S(1)} %get-tuple-element.40.refs_0_), channel_id=1, source_target_pairs={{0,2},{1,3},{2,0},{3,1},{4,6},{5,7},{6,4},{7,5},{8,10},{9,11},{10,... | collective-permute-start | bytes 884744 | tf_op jit(solution)/shard_map/ppermute | solution.py:472
  74.4 8.5 %collective-permute-start.17 = (bf16[16,128]{1,0:T(8,128)(2,1)S(1)}, bf16[16,128]{1,0:T(8,128)(2,1)S(1)}, u32[]{:S(2)}, u32[]{:S(2)}) collective-permute-start(bf16[16,128]{1,0:T(8,128)(2,1)S(1)} %coefficients.1.a), channel_id=1, source_target_pairs={{0,1},{1,0},{2,3},{3,2},{4,5},{5,4},{6,7},{7,6},{8,9},{9,8},{10,11... | collective-permute-start | bytes 12296 | tf_op jit(solution)/shard_map/ppermute | solution.py:467
  74.4 14.1 %collective-permute-start.19 = (bf16[2,12,48,128]{3,2,1,0:T(8,128)(2,1)S(1)}, bf16[2,12,48,128]{3,2,1,0:T(8,128)(2,1)S(1)}, u32[]{:S(2)}, u32[]{:S(2)}) collective-permute-start(bf16[2,12,48,128]{3,2,1,0:T(8,128)(2,1)S(1)} %get-tuple-element.40.refs_0_), channel_id=1, source_target_pairs={{0,1},{1,0},{2,3},{3,2},{4,5},{5,4},{6,7},{7,6},{8,9},{9,8},{10,11... | collective-permute-start | bytes 884744 | tf_op jit(solution)/shard_map/ppermute | solution.py:460
  74.9 14.3 %collective-permute-start.22 = (bf16[2,12,48,128]{3,2,1,0:T(8,128)(2,1)S(1)}, bf16[2,12,48,128]{3,2,1,0:T(8,128)(2,1)S(1)}, u32[]{:S(2)}, u32[]{:S(2)}) collective-permute-start(bf16[2,12,48,128]{3,2,1,0:T(8,128)(2,1)S(1)} %get-tuple-element.41), channel_id=1, source_target_pairs={{0,4},{4,0},{8,12},{12,8},{16,20},{20,16},{24,28},{28,24},{1,5},{5... | collective-permute-start | bytes 884744 | tf_op jit(solution)/shard_map/ppermute | solution.py:466
  77.2 13.0 %collective-permute-start.25 = (bf16[2,12,48,128]{3,2,1,0:T(8,128)(2,1)S(1)}, bf16[2,12,48,128]{3,2,1,0:T(8,128)(2,1)S(1)}, u32[]{:S(2)}, u32[]{:S(2)}) collective-permute-start(bf16[2,12,48,128]{3,2,1,0:T(8,128)(2,1)S(1)} %rotated.5), channel_id=1, source_target_pairs={{0,4},{4,0},{8,12},{12,8},{16,20},{20,16},{24,28},{28,24},{1,5},{5... | collective-permute-start | bytes 884744 | tf_op jit(solution)/shard_map/ppermute | solution.py:475
  82.9 5.6 %collective-permute-start.21 = (bf16[2,12,48,128]{3,2,1,0:T(8,128)(2,1)S(1)}, bf16[2,12,48,128]{3,2,1,0:T(8,128)(2,1)S(1)}, u32[]{:S(2)}, u32[]{:S(2)}) collective-permute-start(bf16[2,12,48,128]{3,2,1,0:T(8,128)(2,1)S(1)} %collective-permute-done.20.refs_2_), channel_id=1, source_target_pairs={{0,1},{1,0},{2,3},{3,2},{4,5},{5,4},{6,7},{7,6},{8,9},{9,8},{10,11... | collective-permute-start | bytes 884744 | tf_op jit(solution)/shard_map/ppermute | solution.py:476
  82.9 3.7 %collective-permute-start.18 = (bf16[32,128]{1,0:T(8,128)(2,1)S(1)}, bf16[32,128]{1,0:T(8,128)(2,1)S(1)}, u32[]{:S(2)}, u32[]{:S(2)}) collective-permute-start(bf16[32,128]{1,0:T(8,128)(2,1)S(1)} %pad_maximum_fusion.1), channel_id=1, source_target_pairs={{0,2},{1,3},{2,0},{3,1},{4,6},{5,7},{6,4},{7,5},{8,10},{9,11},{10,... | collective-permute-start | bytes 24584 | tf_op jit(solution)/shard_map/ppermute | solution.py:468

commit v5 on v4

--- a/solution.py
+++ b/solution.py
@@ -25,80 +25,141 @@
     return jnp.logical_and(p >= 0, p < window).astype(F32)
 
 
-def pair_matrices(width):
-    n = 2 * width
+def neighbour_sum(width, pairs):
+    n = (2 if pairs else 1) * width
     i = lax.broadcasted_iota(jnp.int32, (n, n), 0)
     j = lax.broadcasted_iota(jnp.int32, (n, n), 1)
-    same = (i < width) == (j < width)
-    along = jnp.logical_and(jnp.abs(i - j) == 1, same)
-    here = jnp.where(jnp.logical_or(along, jnp.abs(i - j) == width), -0.125, 0.0)
-    before = jnp.where(i == j + width, -0.125, 0.0)
-    after = jnp.where(i == j - width, -0.125, 0.0)
-    return here.astype(BF16), before.astype(BF16), after.astype(BF16)
-
-
-def partial_kernel(count, unroll, own, f_own, f_x, f_d, out, weights_out, acc, gram):
+    linked = jnp.abs(i - j) == 1
+    if pairs:
+        linked = jnp.logical_and(linked, (i < width) == (j < width))
+        linked = jnp.logical_or(linked, jnp.abs(i - j) == width)
+    return jnp.where(linked, -0.125, 0.0)
+
+
+def prepare_kernel(early, psi, potential, to_x, to_x2, to_z, blocks, sems):
     x = lax.rem(lax.axis_index("space"), 2)
-    _, pairs, depth, cells = f_own.shape
-    orbs = own.shape[3]
-    here, before, after = pair_matrices(cells // 2)
+    half = psi.shape[1] // 2
+    window = half + 2
+    mine, theirs = (half - 2) * x, (half - 2) * (1 - x)
+    width = potential.shape[2]
+    gap = jnp.zeros((potential.shape[1], 64 - width), F32)
+    copies = [
+        pltpu.make_async_copy(
+            psi.at[:, pl.ds(theirs, early)], to_x.at[:, pl.ds(0, early)], sems.at[0]
+        ),
+        pltpu.make_async_copy(
+            psi.at[:, pl.ds(mine, window)], to_z.at[:, pl.ds(0, window)], sems.at[1]
+        ),
+        pltpu.make_async_copy(
+            psi.at[:, pl.ds(theirs + early, window - early)], to_x2, sems.at[2]
+        ),
+    ]
+    for copy in copies:
+        copy.start()
+    for plane in range(blocks.shape[0]):
+        u = (potential[plane] - 1.0) * 0.25
+        hi = u.astype(BF16).astype(F32)
+        blocks[plane, 0] = jnp.concatenate([hi, gap, u - hi, gap], axis=1).astype(BF16)
+    more = [
+        pltpu.make_async_copy(blocks, to_x.at[:, pl.ds(early, 1)], sems.at[3]),
+        pltpu.make_async_copy(blocks, to_z.at[:, pl.ds(window, 1)], sems.at[4]),
+    ]
+    for copy in more:
+        copy.start()
+    for copy in copies + more:
+        copy.wait()
+
+
+def prepared(psi, potential, early):
+    planes, width_x, width_y, orbs = psi.shape
+    window = width_x // 2 + 2
+
+    def out(rows):
+        return jax.ShapeDtypeStruct((planes, rows, width_y, orbs), BF16)
+
+    anywhere = pl.BlockSpec(memory_space=pl.ANY)
+    local = pl.BlockSpec(memory_space=pltpu.VMEM)
+    return pl.pallas_call(
+        functools.partial(prepare_kernel, early),
+        out_shape=(out(early + 1), out(window - early), out(window + 1), out(1)),
+        in_specs=[anywhere, local],
+        out_specs=(anywhere, anywhere, anywhere, local),
+        scratch_shapes=[pltpu.SemaphoreType.DMA((5,))],
+        compiler_params=params(),
+        cost_estimate=cost(4096, 4096),
+        name="prepared",
+    )(psi, potential)
+
+
+def partial_kernel(count, atoms, own, beta, b_x, b_d, potential, gram, out, weights_out, table, acc):
+    place = lax.axis_index("space")
+    x = lax.rem(place, 2)
+    rows, width = potential.shape[1:]
+    side = place ^ 1
+    beyond = place - 1 + 2 * x
+    tri = neighbour_sum(width, False).astype(BF16)
     acc[...] = jnp.zeros_like(acc)
-    gram[...] = jnp.zeros_like(gram)
-
-    def step(i, carry):
-        totals, squares = [], []
-        for k in range(unroll):
-            r = i * unroll + k
-            low, high = jnp.maximum(r - 1, 0), jnp.minimum(r + 1, pairs - 1)
-            has_low, has_high = inside(r - 1, pairs), inside(r + 1, pairs)
-            tiles = [f_d[r], f_own[x, r], f_own[1 - x, r], f_x[r]]
-            for c in (1, 2):
-                plane = x if c == 1 else 1 - x
-                b = tiles[c]
-                b32 = b.astype(F32)
-                u = b32[count : count + 1] + b32[count + 1 : count + 2]
-                local = jnp.dot(b, here, preferred_element_type=F32)
-                local += has_low * jnp.dot(f_own[plane, low], before, preferred_element_type=F32)
-                local += has_high * jnp.dot(f_own[plane, high], after, preferred_element_type=F32)
-                local += u * b32 - 0.125 * (tiles[c - 1].astype(F32) + tiles[c + 1].astype(F32))
-                hi = local.astype(BF16)
-                lo = (local - hi.astype(F32)).astype(BF16)
-                weights = jnp.concatenate([b, hi, lo], axis=0)
+    step = 8
+
+    for k in range(2):
+        plane = x if k == 0 else 1 - x
+        outer, there = (b_d, beyond) if k == 0 else (b_x, side)
+        u = (potential[plane] - 1.0) * 0.25
+
+        def fill(i, carry):
+            for j in range(step):
+                p = i * step + j
+                here = (jnp.abs(place - atoms[p]) <= 1).astype(F32)
+                next_to = (jnp.abs(there - atoms[p]) <= 1).astype(F32)
+                b32 = beta[p, plane].astype(F32) * here
+                b = b32.astype(BF16)
+                sides = beta[p, 1 - plane].astype(F32) * here + outer[p].astype(F32) * next_to
+                whole = jnp.dot(b, tri, preferred_element_type=F32)
+                whole = whole + jnp.dot(tri, b, preferred_element_type=F32)
+                whole = whole + u * b32 - 0.125 * sides
+                hi = whole.astype(BF16).astype(F32)
+                for kind, value in enumerate((b32, hi, whole - hi)):
+                    table[pl.ds((kind * count + p) * rows, rows)] = value
+            return carry
+
+        lax.fori_loop(0, count // step, fill, 0)
+
+        def use(i, carry):
+            totals = []
+            for j in range(step):
+                r = i * step + j
+                weights = table[pl.ds(r, 3 * count, stride=rows)].astype(BF16)
                 weights_out[plane, r] = weights
-                v = own[plane, pl.ds(2 * r, 2)].reshape(cells, orbs)
-                totals.append(jnp.dot(weights, v, preferred_element_type=F32))
-                squares.append(
-                    lax.dot_general(b, b, (((1,), (1,)), ((), ())), preferred_element_type=F32)
-                )
-        acc[...] += sum(totals[1:], totals[0])
-        gram[...] += sum(squares[1:], squares[0])
-        return carry
-
-    lax.fori_loop(0, pairs // unroll, step, 0)
+                totals.append(jnp.dot(weights, own[plane, r], preferred_element_type=F32))
+            acc[...] += sum(totals[1:], totals[0])
+            return carry
+
+        lax.fori_loop(0, rows // step, use, 0)
     out[...] = jnp.zeros_like(out)
     out[0:count] = acc[0:count]
-    out[count : 2 * count] = acc[depth : depth + count] + acc[2 * depth : 2 * depth + count]
-    out[2 * count : 3 * count, 0:count] = gram[0:count, 0:count]
-
-
-def partials(count, own, f_own, f_x, f_d):
-    orbs = own.shape[3]
-    planes, pairs, depth, width = f_own.shape
-    cells = own.size // orbs
-    unroll = max(g for g in (1, 2, 4) if pairs % g == 0 and g * depth <= 144)
-    return pl.pallas_call(
-        functools.partial(partial_kernel, count, unroll),
+    out[count : 2 * count] = acc[count : 2 * count] + acc[2 * count : 3 * count]
+    out[2 * count : 3 * count, 0:count] = gram[...]
+
+
+def partials(count, atoms, own, beta, b_x, b_d, potential, gram):
+    planes, rows, width, orbs = own.shape
+    return pl.pallas_call(
+        functools.partial(partial_kernel, count),
         out_shape=(
             jax.ShapeDtypeStruct((3 * count, orbs), F32),
-            jax.ShapeDtypeStruct((planes, pairs, 3 * depth, width), BF16),
+            jax.ShapeDtypeStruct((planes, rows, 3 * count, width), BF16),
         ),
-        in_specs=[pl.BlockSpec(memory_space=pltpu.VMEM)] * 4,
+        in_specs=[pl.BlockSpec(memory_space=pltpu.SMEM)]
+        + [pl.BlockSpec(memory_space=pltpu.VMEM)] * 6,
         out_specs=(pl.BlockSpec(memory_space=pltpu.VMEM),) * 2,
-        scratch_shapes=[pltpu.VMEM((3 * depth, orbs), F32), pltpu.VMEM((depth, depth), F32)],
-        compiler_params=params(),
-        cost_estimate=cost(2 * cells * 3 * depth * orbs, cells * orbs * 4),
+        scratch_shapes=[
+            pltpu.VMEM((3 * count * rows, width), F32),
+            pltpu.VMEM((3 * count, orbs), F32),
+        ],
+        compiler_params=params(),
+        cost_estimate=cost(4096, 4096),
         name="partials",
-    )(own, f_own, f_x, f_d)
+    )(atoms, own, beta, b_x, b_d, potential, gram)
 
 
 def coefficient_kernel(sums, strength, out):
@@ -130,19 +191,17 @@
     )(sums, strength)
 
 
-def nonlocal_kernel(depth, unroll, a, b, c, d, q, weights, out):
+def nonlocal_kernel(unroll, a, b, c, d, q, weights, out):
     count, orbs = a.shape[0] // 2, a.shape[1]
-    pairs, cells = weights.shape[1], weights.shape[3]
     turned = sum(
         jnp.dot(ref[...], q[k], preferred_element_type=F32) for k, ref in enumerate((a, b, c, d))
     )
     turned = turned * 0.25
-    gap = jnp.zeros((depth - count, orbs), F32)
     one, two = turned[0:count], turned[count : 2 * count]
-    right = jnp.concatenate([two, gap, one, gap, one, gap], axis=0)
+    right = jnp.concatenate([two, one, one], axis=0)
     hi = right.astype(BF16)
-    lo = (right - hi.astype(F32)).astype(BF16)
-    right = jnp.concatenate([hi, lo], axis=1)
+    lo = right - hi.astype(F32)
+    right = jnp.concatenate([hi.astype(F32), lo], axis=1).astype(BF16)
 
     def step(i, carry):
         for k in range(unroll):
@@ -151,18 +210,16 @@
                 both = lax.dot_general(
                     weights[plane, r], right, (((0,), (0,)), ((), ())), preferred_element_type=F32
                 )
-                term = both[:, :orbs] + both[:, orbs:]
-                out[plane, pl.ds(2 * r, 2)] = term.reshape(2, cells // 2, orbs)
+                out[plane, r] = both[:, :orbs] + both[:, orbs:]
         return carry
 
-    lax.fori_loop(0, pairs // unroll, step, 0)
+    lax.fori_loop(0, weights.shape[1] // unroll, step, 0)
 
 
 def nonlocal_term(shape, coefs, q, weights):
-    depth = weights.shape[2] // 3
-    unroll = max(g for g in (1, 2, 4) if weights.shape[1] % g == 0)
-    return pl.pallas_call(
-        functools.partial(nonlocal_kernel, depth, unroll),
+    unroll = max(g for g in (1, 2, 4, 8) if weights.shape[1] % g == 0)
+    return pl.pallas_call(
+        functools.partial(nonlocal_kernel, unroll),
         out_shape=jax.ShapeDtypeStruct(shape, F32),
         in_specs=[pl.BlockSpec(memory_space=pltpu.VMEM)] * 6,
         out_specs=pl.BlockSpec(memory_space=pltpu.VMEM),
@@ -173,10 +230,11 @@
 
 
 def filter_kernel(slabs, start, parts, joint, *refs):
-    own, p_own, p_x, p_d, p_zo, zo = refs[:6]
-    xrs, zfs = refs[6 : 6 + parts], refs[6 + parts : 6 + 2 * parts]
-    outs, scratch = refs[6 + 2 * parts : -3 if parts > 1 else -1], refs[-3 if parts > 1 else -1 :]
-    first = scratch[0]
+    own, p_own, zo = refs[:3]
+    xrs, zfs = refs[3 : 3 + parts], refs[3 + parts : 3 + 2 * parts]
+    extra = 5 if parts > 1 else 3
+    outs, scratch = refs[3 + 2 * parts : -extra], refs[-extra:]
+    first, lines, diagonals = scratch[:3]
     place = lax.axis_index("space")
     x = lax.rem(place, 2)
     width = own.shape[2]
@@ -191,35 +249,39 @@
     has_zf = lower * (1.0 - is_odd) + upper * is_odd
     has_zo = upper * (1.0 - is_odd) + lower * is_odd
     if parts > 1:
-        xr, zf = scratch[1], scratch[2]
+        xr, zf = scratch[3], scratch[4]
+        early = xrs[0].shape[1] - 1
         for target, pieces in ((xr, xrs), (zf, zfs)):
-            at = 0
-            for piece in pieces:
-                target[:, at : at + piece.shape[1]] = piece[...]
-                at += piece.shape[1]
-        window = at // 2
+            target[:, 0:early] = pieces[0][:, 0:early]
+            target[:, early:] = pieces[1][...]
+        window = xr.shape[1] // 2
     else:
         xr, zf = xrs[0], zfs[0]
-        window = xr.shape[1] // 2
-
-    here, _, _ = pair_matrices(width)
-    here = here.astype(F32)
+        window = (xr.shape[1] - 1) // 2
+    for c in range(1, 7):
+        plane = (c % 2) ^ x
+        if c in (2, 3):
+            block = p_own[plane, 0]
+        else:
+            ref = zfs[0] if c < 2 else (xrs[0] if c < 6 else zo)
+            block = ref[plane, ref.shape[1] - 1]
+        lines[c - 1] = block.astype(F32)
+        for kind in range(2):
+            even, odd = (lines[c - 1, pl.ds(k, half, stride=2)] for k in range(2))
+            lanes = slice(64 * kind, 64 * kind + width)
+            diagonals[c - 1, kind] = jnp.concatenate([even[:, lanes], odd[:, lanes]], axis=1)
+
+    here = neighbour_sum(width, True)
     i = lax.broadcasted_iota(jnp.int32, (cells, cells), 0)
     diagonal = i == lax.broadcasted_iota(jnp.int32, (cells, cells), 1)
 
     def local(c, p):
-        w = base + 2 * p
-
-        def line(at):
-            if c in (1, 6):
-                return (p_d if c == 1 else p_zo)[0, pl.ds(at, 1)]
-            return (p_own if c in (2, 3) else p_x)[(c % 2) ^ x, pl.ds(at, 1)]
-
-        u = (jnp.concatenate([line(w), line(w + 1)], axis=1) - 1.0) * 0.25
-        hi = u.astype(BF16).astype(F32)
+        at = base // 2 + p
+        hi = diagonals[c - 1, 0, pl.ds(at, 1)]
+        lo = diagonals[c - 1, 1, pl.ds(at, 1)]
         return (
             jnp.where(diagonal, hi, here).astype(BF16),
-            jnp.where(diagonal, u - hi, 0.0).astype(BF16),
+            jnp.where(diagonal, lo, 0.0).astype(BF16),
         )
 
     def rows_of(c, w, n):
@@ -290,9 +352,13 @@
     shape = (2 * planes if joint else planes, rows, width, orbs)
     out = (jax.ShapeDtypeStruct(shape, BF16),) * (1 if joint else 2)
     cells = 10 * rows * width
-    scratch = [pltpu.VMEM((6, rows + 4, width, orbs), BF16)]
+    scratch = [
+        pltpu.VMEM((6, rows + 4, width, orbs), BF16),
+        pltpu.VMEM((6, width, orbs), F32),
+        pltpu.VMEM((6, 2, own.shape[1] // 2, 2 * width), F32),
+    ]
     if parts > 1:
-        window = sum(piece.shape[1] for piece in xrs)
+        window = xrs[0].shape[1] - 1 + xrs[1].shape[1]
         scratch += [pltpu.VMEM((planes, window, width, orbs), BF16)] * 2
     return pl.pallas_call(
         functools.partial(filter_kernel, slabs, start, parts, joint),
@@ -400,39 +466,20 @@
     mine = (half - 2) * x
     theirs = (half - 2) * (1 - x)
 
+    to_x, to_x2, to_z, blocks = prepared(psi, potential, early)
+    xr1 = lax.ppermute(to_x, "space", swap)
+    zo = lax.ppermute(to_z, "space", own_way)
+    far = lax.dynamic_index_in_dim(beta, x, 1, keepdims=False)
+    near = lax.dynamic_index_in_dim(beta, 1 - x, 1, keepdims=False)
     active = jnp.abs(place - atom_slab) <= 1
     beta_m = jnp.where(active[:, None, None, None], beta, jnp.zeros_like(beta))
-    depth = -(-(count + 2) // 16) * 16
-    u = (potential - 1.0) * 0.25
-    hi = lax.reduce_precision(u, 8, 7)
-    lo = u - hi
-    fields = jnp.concatenate(
-        [
-            jnp.transpose(beta_m, (1, 2, 0, 3)),
-            hi[:, :, None, :].astype(BF16),
-            lo[:, :, None, :].astype(BF16),
-            jnp.zeros((planes, width_x, depth - count - 2, width_y), BF16),
-        ],
-        axis=2,
-    )
-    fields = jnp.concatenate([fields[:, 0::2], fields[:, 1::2]], axis=3)
-    far = lax.dynamic_index_in_dim(fields, x, 0, keepdims=False)
-    near = lax.dynamic_index_in_dim(fields, 1 - x, 0, keepdims=False)
+    gram = jnp.einsum("pzxy,qzxy->pq", beta_m, beta_m, preferred_element_type=F32)
+    far, near, gram, xr1 = ordered(far, near, gram, xr1)
+    zf1 = lax.ppermute(xr1, "space", other_way)
+    second, _ = ordered(to_x2, xr1)
+    xr2 = lax.ppermute(second, "space", swap)
     f_x = lax.ppermute(near, "space", swap)
     f_d = lax.ppermute(far, "space", raster)
-    p_far = lax.dynamic_slice_in_dim(potential, x, 1, axis=0)
-    p_x = lax.ppermute(potential, "space", swap)
-    p_d = lax.ppermute(p_far, "space", raster)
-    p_zo = lax.ppermute(p_far, "space", own_way)
-
-    xr1 = lax.ppermute(
-        lax.dynamic_slice_in_dim(psi, theirs, early, axis=1), "space", swap
-    )
-    zo = lax.ppermute(lax.dynamic_slice_in_dim(psi, mine, window, axis=1), "space", own_way)
-    zf1 = lax.ppermute(xr1, "space", other_way)
-    second = lax.dynamic_slice_in_dim(psi, theirs + early, window - early, axis=1)
-    second, _ = ordered(second, xr1)
-    xr2 = lax.ppermute(second, "space", swap)
     zf1_in, _ = ordered(zf1, xr2)
     zf2 = lax.ppermute(xr2, "space", other_way)
     strong = jnp.broadcast_to(strength[:, None], (count, orbs))
@@ -443,12 +490,11 @@
     rows_hot = rows_hot * (pattern[:, 1] == me).astype(BF16)[:, None]
     q = jnp.einsum("ki,kab->iab", rows_hot, q_tiles, preferred_element_type=F32).astype(BF16)
 
-    p_x, f_x, f_d = ordered(p_x, f_x, f_d)
-    operands = (psi, potential, p_x, p_d, p_zo, zo)
+    operands = (psi, blocks, zo)
     (block1,) = filtered(slabs, 0, rows, True, operands, (xr1,), (zf1_in,))
     y1 = lax.ppermute(block1, "orb", across)
     c1 = lax.ppermute(block1, "orb", beside)
-    sums, weights = partials(count, psi, fields, f_x, f_d)
+    sums, weights = partials(count, atom_slab, psi, beta, f_x, f_d, potential, gram)
     xr2, sums = ordered(xr2, sums)
     give2, keep2 = filtered(slabs, rows, rows, False, operands, (xr1, xr2), (zf1, zf2))
     step = 1

time: 91.8 us -> 85.9 us (0.936)
  local copies, waits for them, and re-layouts: 9.03 us -> 3.68 us
  Pallas kernels: 21.5 us -> 17.5 us
  starting transfers between devices: 26.7 us -> 30 us
  matrix products: 0.34 us -> 1.66 us
    ppermute x1, waiting for transfers between devices: 0.01 us -> 6.53 us  [shards(): xr2 = lax.ppermute(second, 'space', swap)]
    ppermute x5 -> x2, waiting for transfers between devices: 10.5 us -> 4.66 us  [the longest x1 4.66 us: shards(): xr1 = lax.ppermute(to_x, 'space', swap)]
    ppermute x3, starting transfers between devices: 4.06 us -> 9.66 us  [shards(): lax.ppermute(sums, 'space', [(i, i ^ step) for i in range(slabs)])]
    dynamic_slice x4 -> x0, local copies, waits for them, and re-layouts: 3.81 us -> none  [the longest x1 2.05 us: shards(): lax.dynamic_slice_in_dim(psi, mine, window, axis=1)]
    pallas_call x2 -> x3, Pallas kernels: 8.59 us -> 5.93 us  [the longest x1 3.04 us: partials(): pl.pallas_call(functools.partial(partial_kernel, count), out_shape=(jax.S...]
    ppermute x3, waiting for transfers between devices: 6.35 us -> 4.22 us  [shards(): lax.ppermute(sums, 'space', [(i, i ^ step) for i in range(slabs)])]
    ppermute x5 -> x2, starting transfers between devices: 6.4 us -> 4.28 us  [the longest x1 3 us: shards(): xr1 = lax.ppermute(to_x, 'space', swap)]
    slice x1 -> x0, local copies, waits for them, and re-layouts: 1.72 us -> none  [shards(): fields = jnp.concatenate([fields[:, 0::2], fields[:, 1::2]], axis=3)]
  transfers between devices with their start and end apart: 26 -> 23, of which waited for: 9 -> 10; matrix products, arithmetic and copies ran while one was open for 10% -> 5% of each run, Pallas kernels for 18% -> 14%
where the time goes in v5:
time: 85.9 us; the launch traced here: 85.6 us
  waiting for transfers between devices  30.2 us (35%)
  starting transfers between devices  30 us (35%)
  Pallas kernels  17.5 us (20%)
  local copies, waits for them, and re-layouts  3.68 us (4%)
  other arithmetic  2.37 us (3%)
  matrix products  1.66 us (2%)
    ppermute x3, starting transfers between devices, shards(): lax.ppermute(sums, 'space', [(i, i ^ step) for i in range(slabs)])  9.66 us
    pallas_call x2, Pallas kernels, filtered(): pl.pallas_call(functools.partial(filter_kernel, slabs, start, parts, join...  6.59 us
    ppermute x1, waiting for transfers between devices, shards(): xr2 = lax.ppermute(second, 'space', swap)  6.53 us
    ppermute x1, waiting for transfers between devices, shards(): yk = lax.ppermute(keep_y, 'orb', across)  5.06 us
    ppermute x1, waiting for transfers between devices, shards(): xr1 = lax.ppermute(to_x, 'space', swap)  4.66 us
    ppermute x1, starting transfers between devices, shards(): zf2 = lax.ppermute(xr2, 'space', other_way)  4.39 us
    ppermute x3, waiting for transfers between devices, shards(): lax.ppermute(sums, 'space', [(i, i ^ step) for i in range(slabs)])  4.22 us
    ppermute x1, waiting for transfers between devices, shards(): f_x = lax.ppermute(near, 'space', swap)  3.93 us
  transfers between devices with their start and end apart: 23, of which 10 were waited for; matrix products, arithmetic and copies ran while one was open for 5% of the time, Pallas kernels for 14%

profile of v5, /device:TPU:0, one launch (start us, length us, event | category | flops | bytes accessed | tf_op | source)
XLA Modules:
  0.0 85.6 jit_solution(14366191941338315994)
XLA Ops:
  0.0 1.3 %copy-done.1 = bf16[2,48,48,128]{3,2,1,0:T(8,128)(2,1)S(1)} copy-done((bf16[2,48,48,128]{3,2,1,0:T(8,128)(2,1)S(1)}, bf16[2,48,48,128]{3,2,1,0:T(8,128)(2,1)}, u32[]{:S(2)}) %copy-start.1) | copy-done | bytes 1179672
  1.3 0.8 copy-done.10
  2.1 1.0 %prepared.1 = (bf16[2,17,48,128]{3,2,1,0:T(8,128)(2,1)S(1)}, bf16[2,10,48,128]{3,2,1,0:T(8,128)(2,1)S(1)}, bf16[2,27,48,128]{3,2,1,0:T(8,128)(2,1)}, bf16[2,1,48,128]{3,2,1,0:T(8,128)(2,1)S(1)}) custom-call(bf16[2,48,48,128]{3,2,1,0:T(8,128)(2,1)S(1)} %copy-done.1, f32[2,48,48]{2,1,0:T(8,128)S(1)} %copy-done.10), custom_call_target="tpu_custom_call" | custom-call | flops 256 | bytes 256 | tf_op jit(solution)/shard_map/prepared/pallas_call | solution.py:82
  3.1 3.0 %collective-permute-start.1 = (bf16[2,17,48,128]{3,2,1,0:T(8,128)(2,1)S(1)}, bf16[2,17,48,128]{3,2,1,0:T(8,128)(2,1)S(1)}, u32[]{:S(2)}, u32[]{:S(2)}) collective-permute-start(bf16[2,17,48,128]{3,2,1,0:T(8,128)(2,1)S(1)} %get-tuple-element.31), channel_id=1, source_target_pairs={{0,4},{4,0},{8,12},{12,8},{16,20},{20,16},{24,28},{28,24},{1,5},{5... | collective-permute-start | bytes 1253384 | tf_op jit(solution)/shard_map/ppermute | solution.py:470
  6.1 1.3 %collective-permute-start = (bf16[2,27,48,128]{3,2,1,0:T(8,128)(2,1)}, bf16[2,27,48,128]{3,2,1,0:T(8,128)(2,1)S(1)}, u32[]{:S(2)}, u32[]{:S(2)}) collective-permute-start(bf16[2,27,48,128]{3,2,1,0:T(8,128)(2,1)} %get-tuple-element.30), channel_id=1, source_target_pairs={{4,12},{8,0},{12,20},{16,8},{20,28},{24,16},{5,13},{9,1},{13,21},{... | collective-permute-start | bytes 1990664 | tf_op jit(solution)/shard_map/ppermute | solution.py:471
  7.4 0.7 abs_compare_fusion
  8.1 1.7 %broadcast_select_fusion = bf16[8,2,48,48]{3,2,1,0:T(8,128)(2,1)} fusion(bf16[8,2,48,48]{3,2,1,0:T(8,128)(2,1)} %beta.1, pred[8]{0:T(512)(128)(4,1)S(1)} %abs_compare_fusion), kind=kLoop, calls=%fused_computation.5 | loop fusion | flops 36864 | bytes 147464 | tf_op jit(solution)/shard_map/jit(_where)/select_n | solution.py:475
  9.8 1.3 %convolution_bitcast_fusion.gram = f32[8,8]{1,0:T(8,128)S(1)} fusion(bf16[8,2,48,48]{3,2,1,0:T(8,128)(2,1)} %broadcast_select_fusion), kind=kOutput, calls=%fused_computation | convolution fusion | flops 589824 | bytes 73984 | tf_op jit(solution)/shard_map/pzxy,qzxy->pq/dot_general | solution.py:476
  11.1 4.7 %collective-permute-done.1.refs_3_ = bf16[2,17,48,128]{3,2,1,0:T(8,128)(2,1)S(1)} collective-permute-done((bf16[2,17,48,128]{3,2,1,0:T(8,128)(2,1)S(1)}, bf16[2,17,48,128]{3,2,1,0:T(8,128)(2,1)S(1)}, u32[]{:S(2)}, u32[]{:S(2)}) %collective-permute-start.1) | collective-permute-done | bytes 417824 | tf_op jit(solution)/shard_map/ppermute | solution.py:470
  15.8 3.7 %collective-permute-start.5 = (bf16[2,17,48,128]{3,2,1,0:T(8,128)(2,1)S(1)}, bf16[2,17,48,128]{3,2,1,0:T(8,128)(2,1)S(1)}, u32[]{:S(2)}, u32[]{:S(2)}) collective-permute-start(bf16[2,17,48,128]{3,2,1,0:T(8,128)(2,1)S(1)} %collective-permute-done.1.refs_3_), channel_id=1, source_target_pairs={{0,8},{8,16},{12,4},{16,24},{20,12},{28,20},{1,9},{9,17},{13,5},{1... | collective-permute-start | bytes 1253384 | tf_op jit(solution)/shard_map/ppermute | solution.py:478
  19.5 0.1 collective-permute-start.2
  19.6 6.5 %collective-permute-done.2.refs_4_ = bf16[2,10,48,128]{3,2,1,0:T(8,128)(2,1)S(1)} collective-permute-done((bf16[2,10,48,128]{3,2,1,0:T(8,128)(2,1)S(1)}, bf16[2,10,48,128]{3,2,1,0:T(8,128)(2,1)S(1)}, u32[]{:S(2)}, u32[]{:S(2)}) %collective-permute-start.2) | collective-permute-done | bytes 245792 | tf_op jit(solution)/shard_map/ppermute | solution.py:480
  26.1 1.4 %collective-permute-done.5.refs_5_.refs_4_ = bf16[2,17,48,128]{3,2,1,0:T(8,128)(2,1)S(1)} collective-permute-done((bf16[2,17,48,128]{3,2,1,0:T(8,128)(2,1)S(1)}, bf16[2,17,48,128]{3,2,1,0:T(8,128)(2,1)S(1)}, u32[]{:S(2)}, u32[]{:S(2)}) %collective-permute-start.5) | collective-permute-done | bytes 417824 | tf_op jit(solution)/shard_map/ppermute | solution.py:478
  27.5 3.3 %filtered.3.refs_0_ = bf16[4,12,48,128]{3,2,1,0:T(8,128)(2,1)S(1)} custom-call(bf16[2,48,48,128]{3,2,1,0:T(8,128)(2,1)S(1)} %copy-done.2, bf16[2,1,48,128]{3,2,1,0:T(8,128)(2,1)S(1)} %get-tuple-element.29.refs_1_, bf16[2,27,48,128]{3,2,1,0:T(8,128)(2,1)S(1)} %collective-permute-done.refs_2_, bf16[2,17,48,128]{3,2,1,0:T(8,128)(2,1)S(1)} %collective-permute-done.1.refs_3_, ...), custom_call_target="tpu_custom_call" | custom-call | flops 2949120 | bytes 184320 | tf_op jit(solution)/shard_map/filtered/pallas_call | solution.py:363
  30.8 1.6 %collective-permute-start.7 = (bf16[4,12,48,128]{3,2,1,0:T(8,128)(2,1)S(1)}, bf16[4,12,48,128]{3,2,1,0:T(8,128)(2,1)}, u32[]{:S(2)}, u32[]{:S(2)}) collective-permute-start(bf16[4,12,48,128]{3,2,1,0:T(8,128)(2,1)S(1)} %filtered.3.refs_0_), channel_id=1, source_target_pairs={{0,2},{1,3},{2,0},{3,1},{4,6},{5,7},{6,4},{7,5},{8,10},{9,11},{10,... | collective-permute-start | bytes 1769480 | tf_op jit(solution)/shard_map/ppermute | solution.py:495
  32.4 4.4 %collective-permute-start.6 = (bf16[2,10,48,128]{3,2,1,0:T(8,128)(2,1)S(1)}, bf16[2,10,48,128]{3,2,1,0:T(8,128)(2,1)S(1)}, u32[]{:S(2)}, u32[]{:S(2)}) collective-permute-start(bf16[2,10,48,128]{3,2,1,0:T(8,128)(2,1)S(1)} %collective-permute-done.2.refs_4_), channel_id=1, source_target_pairs={{0,8},{8,16},{12,4},{16,24},{20,12},{28,20},{1,9},{9,17},{13,5},{1... | collective-permute-start | bytes 737288 | tf_op jit(solution)/shard_map/ppermute | solution.py:484
  36.8 0.1 collective-permute-start.3
  36.9 0.7 collective-permute-start.4
  37.5 3.9 %collective-permute-done.3.b_x = bf16[8,48,48]{2,1,0:T(8,128)(2,1)S(1)} collective-permute-done((bf16[8,48,48]{2,1,0:T(8,128)(2,1)S(1)}, bf16[8,48,48]{2,1,0:T(8,128)(2,1)S(1)}, u32[]{:S(2)}, u32[]{:S(2)}) %collective-permute-start.3) | collective-permute-done | bytes 36896 | tf_op jit(solution)/shard_map/ppermute | solution.py:481
  41.5 3.0 %partials.1 = (f32[24,128]{1,0:T(8,128)S(1)}, bf16[2,48,24,48]{3,2,1,0:T(8,128)(2,1)S(1)}) custom-call(s32[8]{0:T(128)S(1)} %copy-done.12, bf16[2,48,48,128]{3,2,1,0:T(8,128)(2,1)S(1)} %copy-done.2, bf16[8,2,48,48]{3,2,1,0:T(8,128)(2,1)S(1)} %copy-done.3, bf16[8,48,48]{2,1,0:T(8,128)(2,1)S(1)} %collective-permute-done.3.b_x, ...), custom_call_target="tpu_custom_call" | custom-call | flops 256 | bytes 256 | tf_op jit(solution)/shard_map/partials/pallas_call | solution.py:146
  44.5 0.0 copy-start.4
  44.5 0.0 copy-start.14
  44.6 0.0 copy-start.13
  44.6 0.1 collective-permute-start.9
  44.7 0.0 collective-permute-done.6.refs_6_
  44.7 3.3 %filtered.2 = (bf16[2,12,48,128]{3,2,1,0:T(8,128)(2,1)S(1)}, bf16[2,12,48,128]{3,2,1,0:T(8,128)(2,1)S(1)}) custom-call(bf16[2,48,48,128]{3,2,1,0:T(8,128)(2,1)S(1)} %copy-done.2, bf16[2,1,48,128]{3,2,1,0:T(8,128)(2,1)S(1)} %get-tuple-element.29.refs_1_, bf16[2,27,48,128]{3,2,1,0:T(8,128)(2,1)S(1)} %collective-permute-done.refs_2_, ...), custom_call_target="tpu_custom_call" | custom-call | flops 2949120 | bytes 184320 | tf_op jit(solution)/shard_map/filtered/pallas_call | solution.py:363
  48.0 0.7 copy-done.6
  48.7 0.7 copy-done.8
  49.4 0.0 collective-permute-done.7.refs_2_
  49.4 0.5 collective-permute-start.10
  49.9 4.8 %collective-permute-start.11 = (f32[24,128]{1,0:T(8,128)S(1)}, f32[24,128]{1,0:T(8,128)S(1)}, u32[]{:S(2)}, u32[]{:S(2)}) collective-permute-start(f32[24,128]{1,0:T(8,128)S(1)} %get-tuple-element.46), channel_id=1, source_target_pairs={{0,4},{4,0},{8,12},{12,8},{16,20},{20,16},{24,28},{28,24},{1,5},{5... | collective-permute-start | bytes 36872 | tf_op jit(solution)/shard_map/ppermute | solution.py:502
  54.7 1.7 %collective-permute-done.11 = f32[24,128]{1,0:T(8,128)S(1)} collective-permute-done((f32[24,128]{1,0:T(8,128)S(1)}, f32[24,128]{1,0:T(8,128)S(1)}, u32[]{:S(2)}, u32[]{:S(2)}) %collective-permute-start.11) | collective-permute-done | bytes 12320 | tf_op jit(solution)/shard_map/ppermute | solution.py:502
  56.4 1.9 %collective-permute-start.12 = (f32[24,128]{1,0:T(8,128)S(1)}, f32[24,128]{1,0:T(8,128)S(1)}, u32[]{:S(2)}, u32[]{:S(2)}) collective-permute-start(f32[24,128]{1,0:T(8,128)S(1)} %add.19), channel_id=1, source_target_pairs={{0,8},{4,12},{8,0},{12,4},{16,24},{20,28},{24,16},{28,20},{1,9},{5... | collective-permute-start | bytes 36872 | tf_op jit(solution)/shard_map/ppermute | solution.py:502
  58.3 0.5 collective-permute-start.8
  58.8 1.3 %collective-permute-done.12 = f32[24,128]{1,0:T(8,128)S(1)} collective-permute-done((f32[24,128]{1,0:T(8,128)S(1)}, f32[24,128]{1,0:T(8,128)S(1)}, u32[]{:S(2)}, u32[]{:S(2)}) %collective-permute-start.12) | collective-permute-done | bytes 12320 | tf_op jit(solution)/shard_map/ppermute | solution.py:502
  60.1 2.9 %collective-permute-start.13 = (f32[24,128]{1,0:T(8,128)S(1)}, f32[24,128]{1,0:T(8,128)S(1)}, u32[]{:S(2)}, u32[]{:S(2)}) collective-permute-start(f32[24,128]{1,0:T(8,128)S(1)} %add.20), channel_id=1, source_target_pairs={{0,16},{4,20},{8,24},{12,28},{16,0},{20,4},{24,8},{28,12},{1,17},{... | collective-permute-start | bytes 36872 | tf_op jit(solution)/shard_map/ppermute | solution.py:502
  63.0 0.3 fusion
  63.4 1.3 %collective-permute-done.13 = f32[24,128]{1,0:T(8,128)S(1)} collective-permute-done((f32[24,128]{1,0:T(8,128)S(1)}, f32[24,128]{1,0:T(8,128)S(1)}, u32[]{:S(2)}, u32[]{:S(2)}) %collective-permute-start.13) | collective-permute-done | bytes 12320 | tf_op jit(solution)/shard_map/ppermute | solution.py:502
  64.7 0.1 broadcast_in_dim.22.strength
  64.8 0.1 coefficients.1.a
  64.9 0.1 collective-permute-start.20
  65.0 0.0 collective-permute-done.10.refs_3_
  65.0 2.2 %rotated.3 = (bf16[2,12,48,128]{3,2,1,0:T(8,128)(2,1)S(1)}, bf16[2,12,48,128]{3,2,1,0:T(8,128)(2,1)S(1)}) custom-call(bf16[4,12,48,128]{3,2,1,0:T(8,128)(2,1)S(1)} %filtered.3.refs_0_, bf16[4,12,48,128]{3,2,1,0:T(8,128)(2,1)} %collective-permute-done.9.refs_1_, bf16[4,12,48,128]{3,2,1,0:T(8,128)(2,1)} %collective-permute-done.7.refs_2_, ...), custom_call_target="tpu_custom_call" | custom-call | flops 18874368 | bytes 184320 | tf_op jit(solution)/shard_map/rotated/pallas_call | solution.py:407
  67.3 0.0 copy-start.5
  67.3 0.0 collective-permute-done.8.refs_2_
  67.3 0.5 collective-permute-start.21
  67.8 0.5 collective-permute-start.17
  68.3 0.5 collective-permute-start.16
  68.8 0.0 collective-permute-done.20.refs_1_
  68.8 2.0 %collective-permute-start.19 = (bf16[2,12,48,128]{3,2,1,0:T(8,128)(2,1)S(1)}, bf16[2,12,48,128]{3,2,1,0:T(8,128)(2,1)S(1)}, u32[]{:S(2)}, u32[]{:S(2)}) collective-permute-start(bf16[2,12,48,128]{3,2,1,0:T(8,128)(2,1)S(1)} %get-tuple-element.51), channel_id=1, source_target_pairs={{0,4},{4,0},{8,12},{12,8},{16,20},{20,16},{24,28},{28,24},{1,5},{5... | collective-permute-start | bytes 884744 | tf_op jit(solution)/shard_map/ppermute | solution.py:512
  70.8 0.0 collective-permute-done.21.refs_3_
  70.8 0.6 rotated.5
  71.5 0.3 collective-permute-start.22
  71.7 5.1 %collective-permute-done.17.refs_2_ = bf16[2,12,48,128]{3,2,1,0:T(8,128)(2,1)S(1)} collective-permute-done((bf16[2,12,48,128]{3,2,1,0:T(8,128)(2,1)S(1)}, bf16[2,12,48,128]{3,2,1,0:T(8,128)(2,1)S(1)}, u32[]{:S(2)}, u32[]{:S(2)}) %collective-permute-start.17) | collective-permute-done | bytes 294944 | tf_op jit(solution)/shard_map/ppermute | solution.py:518
  76.8 0.0 collective-permute-start.18
  76.8 0.0 collective-permute-done.14.b
  76.8 0.6 collective-permute-start.15
  77.4 3.1 %collective-permute-done.15 = bf16[32,128]{1,0:T(8,128)(2,1)S(1)} collective-permute-done((bf16[32,128]{1,0:T(8,128)(2,1)S(1)}, bf16[32,128]{1,0:T(8,128)(2,1)S(1)}, u32[]{:S(2)}, u32[]{:S(2)}) %collective-permute-start.15) | collective-permute-done | bytes 8224 | tf_op jit(solution)/shard_map/ppermute | solution.py:514
  80.5 1.9 %nonlocal.1.term = f32[2,48,48,128]{3,2,1,0:T(8,128)S(1)} custom-call(bf16[16,128]{1,0:T(8,128)(2,1)S(1)} %coefficients.1.a, bf16[16,128]{1,0:T(8,128)(2,1)S(1)} %collective-permute-done.14.b, bf16[16,128]{1,0:T(8,128)(2,1)S(1)} %get-tuple-element.56.c, bf16[16,128]{1,0:T(8,128)(2,1)S(1)} %get-tuple-element.55.d, bf16[4,128,128]{2,1,0:T(8,128)(2,1)S(1)} %copy.18.refs_4_.q, ...), custom_call_target="tpu_custom_call" | custom-call | flops 256 | bytes 256 | tf_op jit(solution)/shard_map/nonlocal/pallas_call | solution.py:221
  82.4 0.0 collective-permute-done.16.refs_1_
  82.4 0.0 collective-permute-done.18.refs_3_
  82.4 0.6 rotated.4.refs_1_
  83.1 1.2 %collective-permute-done.22.refs_3_ = bf16[2,12,48,128]{3,2,1,0:T(8,128)(2,1)S(1)} collective-permute-done((bf16[2,12,48,128]{3,2,1,0:T(8,128)(2,1)S(1)}, bf16[2,12,48,128]{3,2,1,0:T(8,128)(2,1)S(1)}, u32[]{:S(2)}, u32[]{:S(2)}) %collective-permute-start.22) | collective-permute-done | bytes 294944 | tf_op jit(solution)/shard_map/ppermute | solution.py:521
  84.3 1.3 %assembled.1 = bf16[2,48,48,128]{3,2,1,0:T(8,128)(2,1)} custom-call(f32[2,48,48,128]{3,2,1,0:T(8,128)S(1)} %nonlocal.1.term, bf16[2,12,48,128]{3,2,1,0:T(8,128)(2,1)S(1)} %get-tuple-element.49.refs_0_, bf16[2,12,48,128]{3,2,1,0:T(8,128)(2,1)S(1)} %rotated.4.refs_1_, bf16[2,12,48,128]{3,2,1,0:T(8,128)(2,1)S(1)} %collective-permute-done.19.refs_2_, ...), custom_call_target="tpu_custom_call" | custom-call | flops 256 | bytes 256 | tf_op jit(solution)/shard_map/assembled/pallas_call | solution.py:430
  (37 shorter events, 0.1 us)
Async XLA Ops:
  0.0 63.0 %copy-start = (bf16[12,128,128]{2,1,0:T(8,128)(2,1)S(1)}, bf16[12,128,128]{2,1,0:T(8,128)(2,1)}, u32[]{:S(2)}) copy-start(bf16[12,128,128]{2,1,0:T(8,128)(2,1)} %param.13) | copy-start | bytes 1179652
  0.0 1.3 %copy-start.1 = (bf16[2,48,48,128]{3,2,1,0:T(8,128)(2,1)S(1)}, bf16[2,48,48,128]{3,2,1,0:T(8,128)(2,1)}, u32[]{:S(2)}) copy-start(bf16[2,48,48,128]{3,2,1,0:T(8,128)(2,1)} %refs_0_.3) | copy-start | bytes 3538948
  1.3 0.8 copy-start.10
  2.1 7.7 %copy-start.3 = (bf16[8,2,48,48]{3,2,1,0:T(8,128)(2,1)S(1)}, bf16[8,2,48,48]{3,2,1,0:T(8,128)(2,1)}, u32[]{:S(2)}) copy-start(bf16[8,2,48,48]{3,2,1,0:T(8,128)(2,1)} %beta.1) | copy-start | bytes 221188
  2.1 25.4 %copy-start.2 = (bf16[2,48,48,128]{3,2,1,0:T(8,128)(2,1)S(1)}, bf16[2,48,48,128]{3,2,1,0:T(8,128)(2,1)}, u32[]{:S(2)}) copy-start(bf16[2,48,48,128]{3,2,1,0:T(8,128)(2,1)} %refs_0_.3) | copy-start | bytes 3538948
  3.1 12.6 %collective-permute-start.1 = (bf16[2,17,48,128]{3,2,1,0:T(8,128)(2,1)S(1)}, bf16[2,17,48,128]{3,2,1,0:T(8,128)(2,1)S(1)}, u32[]{:S(2)}, u32[]{:S(2)}) collective-permute-start(bf16[2,17,48,128]{3,2,1,0:T(8,128)(2,1)S(1)} %get-tuple-element.31), channel_id=1, source_target_pairs={{0,4},{4,0},{8,12},{12,8},{16,20},{20,16},{24,28},{28,24},{1,5},{5... | collective-permute-start | bytes 1253384 | tf_op jit(solution)/shard_map/ppermute | solution.py:470
  6.1 21.4 %collective-permute-start = (bf16[2,27,48,128]{3,2,1,0:T(8,128)(2,1)}, bf16[2,27,48,128]{3,2,1,0:T(8,128)(2,1)S(1)}, u32[]{:S(2)}, u32[]{:S(2)}) collective-permute-start(bf16[2,27,48,128]{3,2,1,0:T(8,128)(2,1)} %get-tuple-element.30), channel_id=1, source_target_pairs={{4,12},{8,0},{12,20},{16,8},{20,28},{24,16},{5,13},{9,1},{13,21},{... | collective-permute-start | bytes 1990664 | tf_op jit(solution)/shard_map/ppermute | solution.py:471
  15.8 11.7 %collective-permute-start.5 = (bf16[2,17,48,128]{3,2,1,0:T(8,128)(2,1)S(1)}, bf16[2,17,48,128]{3,2,1,0:T(8,128)(2,1)S(1)}, u32[]{:S(2)}, u32[]{:S(2)}) collective-permute-start(bf16[2,17,48,128]{3,2,1,0:T(8,128)(2,1)S(1)} %collective-permute-done.1.refs_3_), channel_id=1, source_target_pairs={{0,8},{8,16},{12,4},{16,24},{20,12},{28,20},{1,9},{9,17},{13,5},{1... | collective-permute-start | bytes 1253384 | tf_op jit(solution)/shard_map/ppermute | solution.py:478
  19.5 6.6 %collective-permute-start.2 = (bf16[2,10,48,128]{3,2,1,0:T(8,128)(2,1)S(1)}, bf16[2,10,48,128]{3,2,1,0:T(8,128)(2,1)S(1)}, u32[]{:S(2)}, u32[]{:S(2)}) collective-permute-start(bf16[2,10,48,128]{3,2,1,0:T(8,128)(2,1)S(1)} %get-tuple-element.34), channel_id=1, source_target_pairs={{0,4},{4,0},{8,12},{12,8},{16,20},{20,16},{24,28},{28,24},{1,5},{5... | collective-permute-start | bytes 737288 | tf_op jit(solution)/shard_map/ppermute | solution.py:480
  27.5 14.0 %copy-start.11 = (f32[2,48,48]{2,1,0:T(8,128)S(1)}, f32[2,48,48]{2,1,0:T(8,128)}, u32[]{:S(2)}) copy-start(f32[2,48,48]{2,1,0:T(8,128)} %potential.3) | copy-start | bytes 55300
  27.5 14.0 %copy-start.12 = (s32[8]{0:T(128)S(1)}, s32[8]{0:T(128)}, u32[]{:S(2)}) copy-start(s32[8]{0:T(128)} %atoms.1) | copy-start | bytes 100
  30.8 18.6 %collective-permute-start.7 = (bf16[4,12,48,128]{3,2,1,0:T(8,128)(2,1)S(1)}, bf16[4,12,48,128]{3,2,1,0:T(8,128)(2,1)}, u32[]{:S(2)}, u32[]{:S(2)}) collective-permute-start(bf16[4,12,48,128]{3,2,1,0:T(8,128)(2,1)S(1)} %filtered.3.refs_0_), channel_id=1, source_target_pairs={{0,2},{1,3},{2,0},{3,1},{4,6},{5,7},{6,4},{7,5},{8,10},{9,11},{10,... | collective-permute-start | bytes 1769480 | tf_op jit(solution)/shard_map/ppermute | solution.py:495
  32.4 12.3 %collective-permute-start.6 = (bf16[2,10,48,128]{3,2,1,0:T(8,128)(2,1)S(1)}, bf16[2,10,48,128]{3,2,1,0:T(8,128)(2,1)S(1)}, u32[]{:S(2)}, u32[]{:S(2)}) collective-permute-start(bf16[2,10,48,128]{3,2,1,0:T(8,128)(2,1)S(1)} %collective-permute-done.2.refs_4_), channel_id=1, source_target_pairs={{0,8},{8,16},{12,4},{16,24},{20,12},{28,20},{1,9},{9,17},{13,5},{1... | collective-permute-start | bytes 737288 | tf_op jit(solution)/shard_map/ppermute | solution.py:484
  36.8 4.7 %collective-permute-start.3 = (bf16[8,48,48]{2,1,0:T(8,128)(2,1)S(1)}, bf16[8,48,48]{2,1,0:T(8,128)(2,1)S(1)}, u32[]{:S(2)}, u32[]{:S(2)}) collective-permute-start(bf16[8,48,48]{2,1,0:T(8,128)(2,1)S(1)} %get-tuple-element.35), channel_id=1, source_target_pairs={{0,4},{4,0},{8,12},{12,8},{16,20},{20,16},{24,28},{28,24},{1,5},{5... | collective-permute-start | bytes 110600 | tf_op jit(solution)/shard_map/ppermute | solution.py:481
  36.9 4.6 %collective-permute-start.4 = (bf16[8,48,48]{2,1,0:T(8,128)(2,1)S(1)}, bf16[8,48,48]{2,1,0:T(8,128)(2,1)S(1)}, u32[]{:S(2)}, u32[]{:S(2)}) collective-permute-start(bf16[8,48,48]{2,1,0:T(8,128)(2,1)S(1)} %get-tuple-element.36), channel_id=1, source_target_pairs={{4,8},{8,4},{12,16},{16,12},{20,24},{24,20},{5,9},{9,5},{13,17},{1... | collective-permute-start | bytes 110600 | tf_op jit(solution)/shard_map/ppermute | solution.py:482
  44.5 3.5 %copy-start.4 = (bf16[2,48,24,48]{3,2,1,0:T(8,128)(2,1)}, bf16[2,48,24,48]{3,2,1,0:T(8,128)(2,1)S(1)}, u32[]{:S(2)}) copy-start(bf16[2,48,24,48]{3,2,1,0:T(8,128)(2,1)S(1)} %get-tuple-element.48.weights) | copy-start | bytes 663556
  44.5 5.4 %copy-start.14 = (s32[12,2]{0,1:T(2,128)S(1)}, s32[12,2]{0,1:T(2,128)}, u32[]{:S(2)}) copy-start(s32[12,2]{0,1:T(2,128)} %param.12) | copy-start | bytes 292
  44.6 20.1 %copy-start.13 = (f32[8]{0:T(128)S(1)}, f32[8]{0:T(128)}, u32[]{:S(2)}) copy-start(f32[8]{0:T(128)} %param.10) | copy-start | bytes 100
  44.6 20.4 %collective-permute-start.9 = (bf16[4,12,48,128]{3,2,1,0:T(8,128)(2,1)S(1)}, bf16[4,12,48,128]{3,2,1,0:T(8,128)(2,1)}, u32[]{:S(2)}, u32[]{:S(2)}) collective-permute-start(bf16[4,12,48,128]{3,2,1,0:T(8,128)(2,1)S(1)} %filtered.3.refs_0_), channel_id=1, source_target_pairs={{0,1},{1,0},{2,3},{3,2},{4,5},{5,4},{6,7},{7,6},{8,9},{9,8},{10,11... | collective-permute-start | bytes 1769480 | tf_op jit(solution)/shard_map/ppermute | solution.py:496
  48.0 0.7 copy-start.6
  48.7 0.7 copy-start.8
  49.4 15.6 %collective-permute-start.10 = (bf16[4,12,48,128]{3,2,1,0:T(8,128)(2,1)}, bf16[4,12,48,128]{3,2,1,0:T(8,128)(2,1)S(1)}, u32[]{:S(2)}, u32[]{:S(2)}) collective-permute-start(bf16[4,12,48,128]{3,2,1,0:T(8,128)(2,1)} %collective-permute-done.7.refs_2_), channel_id=1, source_target_pairs={{0,1},{1,0},{2,3},{3,2},{4,5},{5,4},{6,7},{7,6},{8,9},{9,8},{10,11... | collective-permute-start | bytes 1769480 | tf_op jit(solution)/shard_map/ppermute | solution.py:509
  49.9 6.5 %collective-permute-start.11 = (f32[24,128]{1,0:T(8,128)S(1)}, f32[24,128]{1,0:T(8,128)S(1)}, u32[]{:S(2)}, u32[]{:S(2)}) collective-permute-start(f32[24,128]{1,0:T(8,128)S(1)} %get-tuple-element.46), channel_id=1, source_target_pairs={{0,4},{4,0},{8,12},{12,8},{16,20},{20,16},{24,28},{28,24},{1,5},{5... | collective-permute-start | bytes 36872 | tf_op jit(solution)/shard_map/ppermute | solution.py:502
  56.4 3.7 %collective-permute-start.12 = (f32[24,128]{1,0:T(8,128)S(1)}, f32[24,128]{1,0:T(8,128)S(1)}, u32[]{:S(2)}, u32[]{:S(2)}) collective-permute-start(f32[24,128]{1,0:T(8,128)S(1)} %add.19), channel_id=1, source_target_pairs={{0,8},{4,12},{8,0},{12,4},{16,24},{20,28},{24,16},{28,20},{1,9},{5... | collective-permute-start | bytes 36872 | tf_op jit(solution)/shard_map/ppermute | solution.py:502
  58.3 9.0 %collective-permute-start.8 = (bf16[2,12,48,128]{3,2,1,0:T(8,128)(2,1)}, bf16[2,12,48,128]{3,2,1,0:T(8,128)(2,1)S(1)}, u32[]{:S(2)}, u32[]{:S(2)}) collective-permute-start(bf16[2,12,48,128]{3,2,1,0:T(8,128)(2,1)} %copy-done.8), channel_id=1, source_target_pairs={{0,2},{1,3},{2,0},{3,1},{4,6},{5,7},{6,4},{7,5},{8,10},{9,11},{10,... | collective-permute-start | bytes 884744 | tf_op jit(solution)/shard_map/ppermute | solution.py:508
  60.1 4.6 %collective-permute-start.13 = (f32[24,128]{1,0:T(8,128)S(1)}, f32[24,128]{1,0:T(8,128)S(1)}, u32[]{:S(2)}, u32[]{:S(2)}) collective-permute-start(f32[24,128]{1,0:T(8,128)S(1)} %add.20), channel_id=1, source_target_pairs={{0,16},{4,20},{8,24},{12,28},{16,0},{20,4},{24,8},{28,12},{1,17},{... | collective-permute-start | bytes 36872 | tf_op jit(solution)/shard_map/ppermute | solution.py:502
  64.9 2.9 %copy-start.7 = (bf16[2,12,48,128]{3,2,1,0:T(8,128)(2,1)S(1)}, bf16[2,12,48,128]{3,2,1,0:T(8,128)(2,1)}, u32[]{:S(2)}) copy-start(bf16[2,12,48,128]{3,2,1,0:T(8,128)(2,1)} %copy-done.6) | copy-start | bytes 884740
  64.9 5.9 %copy-start.9 = (bf16[2,12,48,128]{3,2,1,0:T(8,128)(2,1)S(1)}, bf16[2,12,48,128]{3,2,1,0:T(8,128)(2,1)}, u32[]{:S(2)}) copy-start(bf16[2,12,48,128]{3,2,1,0:T(8,128)(2,1)} %copy-done.8) | copy-start | bytes 884740
  64.9 3.9 %collective-permute-start.20 = (bf16[2,12,48,128]{3,2,1,0:T(8,128)(2,1)}, bf16[2,12,48,128]{3,2,1,0:T(8,128)(2,1)S(1)}, u32[]{:S(2)}, u32[]{:S(2)}) collective-permute-start(bf16[2,12,48,128]{3,2,1,0:T(8,128)(2,1)} %copy-done.8), channel_id=1, source_target_pairs={{0,1},{1,0},{2,3},{3,2},{4,5},{5,4},{6,7},{7,6},{8,9},{9,8},{10,11... | collective-permute-start | bytes 884744 | tf_op jit(solution)/shard_map/ppermute | solution.py:505
  67.3 13.2 %copy-start.5 = (bf16[2,48,24,48]{3,2,1,0:T(8,128)(2,1)S(1)}, bf16[2,48,24,48]{3,2,1,0:T(8,128)(2,1)}, u32[]{:S(2)}) copy-start(bf16[2,48,24,48]{3,2,1,0:T(8,128)(2,1)} %copy-done.4) | copy-start | bytes 663556
  67.3 3.5 %collective-permute-start.21 = (bf16[2,12,48,128]{3,2,1,0:T(8,128)(2,1)S(1)}, bf16[2,12,48,128]{3,2,1,0:T(8,128)(2,1)S(1)}, u32[]{:S(2)}, u32[]{:S(2)}) collective-permute-start(bf16[2,12,48,128]{3,2,1,0:T(8,128)(2,1)S(1)} %collective-permute-done.8.refs_2_), channel_id=1, source_target_pairs={{0,1},{1,0},{2,3},{3,2},{4,5},{5,4},{6,7},{7,6},{8,9},{9,8},{10,11... | collective-permute-start | bytes 884744 | tf_op jit(solution)/shard_map/ppermute | solution.py:519
  67.8 9.0 %collective-permute-start.17 = (bf16[2,12,48,128]{3,2,1,0:T(8,128)(2,1)S(1)}, bf16[2,12,48,128]{3,2,1,0:T(8,128)(2,1)S(1)}, u32[]{:S(2)}, u32[]{:S(2)}) collective-permute-start(bf16[2,12,48,128]{3,2,1,0:T(8,128)(2,1)S(1)} %copy-done.7), channel_id=1, source_target_pairs={{0,2},{1,3},{2,0},{3,1},{4,6},{5,7},{6,4},{7,5},{8,10},{9,11},{10,... | collective-permute-start | bytes 884744 | tf_op jit(solution)/shard_map/ppermute | solution.py:518
  68.3 8.5 %collective-permute-start.14 = (bf16[16,128]{1,0:T(8,128)(2,1)S(1)}, bf16[16,128]{1,0:T(8,128)(2,1)S(1)}, u32[]{:S(2)}, u32[]{:S(2)}) collective-permute-start(bf16[16,128]{1,0:T(8,128)(2,1)S(1)} %coefficients.1.a), channel_id=1, source_target_pairs={{0,1},{1,0},{2,3},{3,2},{4,5},{5,4},{6,7},{7,6},{8,9},{9,8},{10,11... | collective-permute-start | bytes 12296 | tf_op jit(solution)/shard_map/ppermute | solution.py:513
  68.3 14.1 %collective-permute-start.16 = (bf16[2,12,48,128]{3,2,1,0:T(8,128)(2,1)S(1)}, bf16[2,12,48,128]{3,2,1,0:T(8,128)(2,1)S(1)}, u32[]{:S(2)}, u32[]{:S(2)}) collective-permute-start(bf16[2,12,48,128]{3,2,1,0:T(8,128)(2,1)S(1)} %copy-done.7), channel_id=1, source_target_pairs={{0,1},{1,0},{2,3},{3,2},{4,5},{5,4},{6,7},{7,6},{8,9},{9,8},{10,11... | collective-permute-start | bytes 884744 | tf_op jit(solution)/shard_map/ppermute | solution.py:506
  68.8 14.3 %collective-permute-start.19 = (bf16[2,12,48,128]{3,2,1,0:T(8,128)(2,1)S(1)}, bf16[2,12,48,128]{3,2,1,0:T(8,128)(2,1)S(1)}, u32[]{:S(2)}, u32[]{:S(2)}) collective-permute-start(bf16[2,12,48,128]{3,2,1,0:T(8,128)(2,1)S(1)} %get-tuple-element.51), channel_id=1, source_target_pairs={{0,4},{4,0},{8,12},{12,8},{16,20},{20,16},{24,28},{28,24},{1,5},{5... | collective-permute-start | bytes 884744 | tf_op jit(solution)/shard_map/ppermute | solution.py:512
  71.5 12.8 %collective-permute-start.22 = (bf16[2,12,48,128]{3,2,1,0:T(8,128)(2,1)S(1)}, bf16[2,12,48,128]{3,2,1,0:T(8,128)(2,1)S(1)}, u32[]{:S(2)}, u32[]{:S(2)}) collective-permute-start(bf16[2,12,48,128]{3,2,1,0:T(8,128)(2,1)S(1)} %rotated.5), channel_id=1, source_target_pairs={{0,4},{4,0},{8,12},{12,8},{16,20},{20,16},{24,28},{28,24},{1,5},{5... | collective-permute-start | bytes 884744 | tf_op jit(solution)/shard_map/ppermute | solution.py:521
  76.8 5.6 %collective-permute-start.18 = (bf16[2,12,48,128]{3,2,1,0:T(8,128)(2,1)S(1)}, bf16[2,12,48,128]{3,2,1,0:T(8,128)(2,1)S(1)}, u32[]{:S(2)}, u32[]{:S(2)}) collective-permute-start(bf16[2,12,48,128]{3,2,1,0:T(8,128)(2,1)S(1)} %collective-permute-done.17.refs_2_), channel_id=1, source_target_pairs={{0,1},{1,0},{2,3},{3,2},{4,5},{5,4},{6,7},{7,6},{8,9},{9,8},{10,11... | collective-permute-start | bytes 884744 | tf_op jit(solution)/shard_map/ppermute | solution.py:522
  76.8 3.7 %collective-permute-start.15 = (bf16[32,128]{1,0:T(8,128)(2,1)S(1)}, bf16[32,128]{1,0:T(8,128)(2,1)S(1)}, u32[]{:S(2)}, u32[]{:S(2)}) collective-permute-start(bf16[32,128]{1,0:T(8,128)(2,1)S(1)} %pad_maximum_fusion), channel_id=1, source_target_pairs={{0,2},{1,3},{2,0},{3,1},{4,6},{5,7},{6,4},{7,5},{8,10},{9,11},{10,... | collective-permute-start | bytes 24584 | tf_op jit(solution)/shard_map/ppermute | solution.py:514

commit v6 on v5

--- a/solution.py
+++ b/solution.py
@@ -11,6 +11,7 @@
 BF16 = jnp.bfloat16
 VMEM_LIMIT = 24 * 1024 * 1024
 SHRINK = 16
+FILTER = 100
 
 
 def params():
@@ -36,13 +37,13 @@
     return jnp.where(linked, -0.125, 0.0)
 
 
-def prepare_kernel(early, psi, potential, to_x, to_x2, to_z, blocks, sems):
+def prepare_kernel(early, psi, potential_far, to_x, to_x2, to_z, blocks, potential, sems):
     x = lax.rem(lax.axis_index("space"), 2)
     half = psi.shape[1] // 2
     window = half + 2
     mine, theirs = (half - 2) * x, (half - 2) * (1 - x)
-    width = potential.shape[2]
-    gap = jnp.zeros((potential.shape[1], 64 - width), F32)
+    width = potential_far.shape[2]
+    gap = jnp.zeros((potential_far.shape[1], 64 - width), F32)
     copies = [
         pltpu.make_async_copy(
             psi.at[:, pl.ds(theirs, early)], to_x.at[:, pl.ds(0, early)], sems.at[0]
@@ -54,8 +55,11 @@
             psi.at[:, pl.ds(theirs + early, window - early)], to_x2, sems.at[2]
         ),
     ]
+    fetch = pltpu.make_async_copy(potential_far, potential, sems.at[5])
+    fetch.start()
     for copy in copies:
         copy.start()
+    fetch.wait()
     for plane in range(blocks.shape[0]):
         u = (potential[plane] - 1.0) * 0.25
         hi = u.astype(BF16).astype(F32)
@@ -82,13 +86,13 @@
     return pl.pallas_call(
         functools.partial(prepare_kernel, early),
         out_shape=(out(early + 1), out(window - early), out(window + 1), out(1)),
-        in_specs=[anywhere, local],
+        in_specs=[pl.BlockSpec(memory_space=pltpu.MemorySpace.HBM)] * 2,
         out_specs=(anywhere, anywhere, anywhere, local),
-        scratch_shapes=[pltpu.SemaphoreType.DMA((5,))],
+        scratch_shapes=[pltpu.VMEM(potential.shape, F32), pltpu.SemaphoreType.DMA((6,))],
         compiler_params=params(),
         cost_estimate=cost(4096, 4096),
         name="prepared",
-    )(psi, potential)
+    )(*(pltpu.with_memory_space_constraint(a, pltpu.MemorySpace.HBM) for a in (psi, potential)))
 
 
 def partial_kernel(count, atoms, own, beta, b_x, b_d, potential, gram, out, weights_out, table, acc):
@@ -367,7 +371,7 @@
         out_specs=(pl.BlockSpec(memory_space=pltpu.VMEM),) * len(out),
         scratch_shapes=scratch,
         compiler_params=params(),
-        cost_estimate=cost(2 * cells * 32 * orbs, cells * orbs * 4),
+        cost_estimate=cost(2 * cells * 32 * orbs, FILTER * cells * orbs * 4),
         name="filtered",
     )(*operands, *xrs, *zfs)
 
@@ -419,10 +423,12 @@
     out = refs[-1]
     pieces = (len(refs) - 1) // 2
     x = lax.rem(lax.axis_index("space"), 2)
-    rows = refs[0].shape[1]
+    start = 0
     for k in range(pieces):
+        rows = refs[k].shape[1]
+        start += refs[k - 1].shape[1] if k else 0
         for ref, at in ((refs[k], half * x), (refs[pieces + k], half * (1 - x))):
-            where = pl.ds(at + rows * k, rows)
+            where = pl.ds(at + start, rows)
             out[:, where] = (ref[...].astype(F32) + term[:, where]).astype(BF16)
 
 
@@ -450,8 +456,9 @@
     x = lax.rem(place, 2)
     half = width_x // 2
     window = half + 2
-    rows = half // 2
-    early = rows + 4
+    rows1 = half * 5 // 24 * 2
+    rows2 = half - rows1
+    early = rows1 + 4
 
     def within(pairs):
         return [(i, j) for i, j in pairs if 0 <= j < slabs]
@@ -478,10 +485,9 @@
     zf1 = lax.ppermute(xr1, "space", other_way)
     second, _ = ordered(to_x2, xr1)
     xr2 = lax.ppermute(second, "space", swap)
+    zf2 = lax.ppermute(xr2, "space", other_way)
     f_x = lax.ppermute(near, "space", swap)
     f_d = lax.ppermute(far, "space", raster)
-    zf1_in, _ = ordered(zf1, xr2)
-    zf2 = lax.ppermute(xr2, "space", other_way)
     strong = jnp.broadcast_to(strength[:, None], (count, orbs))
 
     me = lax.axis_index("orb")
@@ -490,13 +496,13 @@
     rows_hot = rows_hot * (pattern[:, 1] == me).astype(BF16)[:, None]
     q = jnp.einsum("ki,kab->iab", rows_hot, q_tiles, preferred_element_type=F32).astype(BF16)
 
+    sums, weights = partials(count, atom_slab, psi, beta, f_x, f_d, potential, gram)
+    zf1, sums, _ = ordered(zf1, sums, xr2)
     operands = (psi, blocks, zo)
-    (block1,) = filtered(slabs, 0, rows, True, operands, (xr1,), (zf1_in,))
+    (block1,) = filtered(slabs, 0, rows1, True, operands, (xr1,), (zf1,))
     y1 = lax.ppermute(block1, "orb", across)
     c1 = lax.ppermute(block1, "orb", beside)
-    sums, weights = partials(count, atom_slab, psi, beta, f_x, f_d, potential, gram)
-    xr2, sums = ordered(xr2, sums)
-    give2, keep2 = filtered(slabs, rows, rows, False, operands, (xr1, xr2), (zf1, zf2))
+    give2, keep2 = filtered(slabs, rows1, rows2, False, operands, (xr1, xr2), (zf1, zf2))
     step = 1
     while step < slabs:
         sums = sums + lax.ppermute(sums, "space", [(i, i ^ step) for i in range(slabs)])
@@ -504,19 +510,18 @@
     coefs = coefficients(sums, strong)
     cg = lax.ppermute(give2, "orb", beside)
     ck = lax.ppermute(keep2, "orb", beside)
-    give_y, y1 = ordered(give2, y1)
-    yg = lax.ppermute(give_y, "orb", across)
+    yg = lax.ppermute(give2, "orb", across)
     yc1 = lax.ppermute(y1, "orb", beside)
     give1, keep1 = rotated((block1, c1, y1, yc1), q, 2)
-    keep_y, yg, give1, coefs = ordered(keep2, yg, give1, coefs)
+    keep_y, yg = ordered(keep2, yg)
+    yk = lax.ppermute(keep_y, "orb", across)
+    yg, give1, coefs = ordered(yg, give1, coefs)
+    ycg = lax.ppermute(yg, "orb", beside)
     got1 = lax.ppermute(give1, "space", swap)
     coefs_c = lax.ppermute(coefs, "orb", beside)
     coefs_y = lax.ppermute(jnp.concatenate([coefs, coefs_c], axis=0), "orb", across)
     coefs_yc, coefs_y = coefs_y[2 * count :], coefs_y[: 2 * count]
     term = nonlocal_term(psi.shape, (coefs, coefs_c, coefs_y, coefs_yc), q, weights)
-
-    yk = lax.ppermute(keep_y, "orb", across)
-    ycg = lax.ppermute(yg, "orb", beside)
     (give2,) = rotated((give2, cg, yg, ycg), q, 1)
     got2 = lax.ppermute(give2, "space", swap)
     yck = lax.ppermute(yk, "orb", beside)

time: 85.9 us -> 109 us (1.27)
  Pallas kernels: 17.5 us -> 39.1 us
  waiting for transfers between devices: 30.2 us -> 36 us
  local copies, waits for them, and re-layouts: 3.68 us -> 0.89 us
  other arithmetic: 2.37 us -> 1.04 us
    pallas_call x1, Pallas kernels: 1 us -> 20.5 us  [prepared(): pl.pallas_call(functools.partial(prepare_kernel, early), out_shape=(out(e...]
    ppermute x1, waiting for transfers between devices: 6.53 us -> 0.01 us  [shards(): xr2 = lax.ppermute(second, 'space', swap)]
    ppermute x3, starting transfers between devices: 9.66 us -> 4.93 us  [shards(): lax.ppermute(sums, 'space', [(i, i ^ step) for i in range(slabs)])]
    ppermute x1, waiting for transfers between devices: 1.21 us -> 5.26 us  [shards(): got2 = lax.ppermute(give2, 'space', swap)]
    ppermute x1, waiting for transfers between devices: 0.01 us -> 3.75 us  [shards(): yg = lax.ppermute(give2, 'orb', across)]
    ppermute x1, waiting for transfers between devices: 3.93 us -> 7.22 us  [shards(): f_x = lax.ppermute(near, 'space', swap)]
    ppermute x1, waiting for transfers between devices: 0.01 us -> 3.26 us  [shards(): y1 = lax.ppermute(block1, 'orb', across)]
    unnamed x30 -> x20, local copies, waits for them, and re-layouts: 3.58 us -> 0.78 us
  transfers between devices with their start and end apart: 23 -> 23, of which waited for: 10 -> 9; matrix products, arithmetic and copies ran while one was open for 5% -> 2% of each run, Pallas kernels for 14% -> 13%
where the time goes in v6:
time: 109 us
  Pallas kernels  39.1 us (36%)
  waiting for transfers between devices  36 us (33%)
  starting transfers between devices  30.9 us (28%)
    pallas_call x1, Pallas kernels, prepared(): pl.pallas_call(functools.partial(prepare_kernel, early), out_shape=(out(e...  20.5 us
    pallas_call x2, Pallas kernels, filtered(): pl.pallas_call(functools.partial(filter_kernel, slabs, start, parts, join...  7.69 us
    ppermute x1, waiting for transfers between devices, shards(): f_x = lax.ppermute(near, 'space', swap)  7.22 us
    ppermute x1, starting transfers between devices, shards(): zf2 = lax.ppermute(xr2, 'space', other_way)  6.31 us
    ppermute x1, waiting for transfers between devices, shards(): xr1 = lax.ppermute(to_x, 'space', swap)  5.9 us
    ppermute x1, waiting for transfers between devices, shards(): yk = lax.ppermute(keep_y, 'orb', across)  5.34 us
    ppermute x1, waiting for transfers between devices, shards(): got2 = lax.ppermute(give2, 'space', swap)  5.26 us
    ppermute x3, starting transfers between devices, shards(): lax.ppermute(sums, 'space', [(i, i ^ step) for i in range(slabs)])  4.93 us
  transfers between devices with their start and end apart: 23, of which 9 were waited for; matrix products, arithmetic and copies ran while one was open for 2% of the time, Pallas kernels for 13%

profile of v6, /device:TPU:0, one launch (start us, length us, event | category | flops | bytes accessed | tf_op | source)
XLA Modules:
  0.0 108.9 jit_solution(17360614814753976111)
XLA Ops:
  0.0 0.0 copy-start.2
  0.0 20.5 %prepared.1 = (bf16[2,15,48,128]{3,2,1,0:T(8,128)(2,1)S(1)}, bf16[2,12,48,128]{3,2,1,0:T(8,128)(2,1)S(1)}, bf16[2,27,48,128]{3,2,1,0:T(8,128)(2,1)}, bf16[2,1,48,128]{3,2,1,0:T(8,128)(2,1)S(1)}) custom-call(bf16[2,48,48,128]{3,2,1,0:T(8,128)(2,1)} %refs_0_.3, f32[2,48,48]{2,1,0:T(8,128)} %potential.1), custom_call_target="tpu_custom_call" | custom-call | flops 256 | bytes 256 | tf_op jit(solution)/shard_map/prepared/pallas_call | solution.py:86
  20.6 0.7 copy-done.7
  21.3 2.9 %collective-permute-start.1 = (bf16[2,15,48,128]{3,2,1,0:T(8,128)(2,1)S(1)}, bf16[2,15,48,128]{3,2,1,0:T(8,128)(2,1)S(1)}, u32[]{:S(2)}, u32[]{:S(2)}) collective-permute-start(bf16[2,15,48,128]{3,2,1,0:T(8,128)(2,1)S(1)} %get-tuple-element.29), channel_id=1, source_target_pairs={{0,4},{4,0},{8,12},{12,8},{16,20},{20,16},{24,28},{28,24},{1,5},{5... | collective-permute-start | bytes 1105928 | tf_op jit(solution)/shard_map/ppermute | solution.py:477
  24.3 1.3 %collective-permute-start = (bf16[2,27,48,128]{3,2,1,0:T(8,128)(2,1)}, bf16[2,27,48,128]{3,2,1,0:T(8,128)(2,1)S(1)}, u32[]{:S(2)}, u32[]{:S(2)}) collective-permute-start(bf16[2,27,48,128]{3,2,1,0:T(8,128)(2,1)} %get-tuple-element.28), channel_id=1, source_target_pairs={{4,12},{8,0},{12,20},{16,8},{20,28},{24,16},{5,13},{9,1},{13,21},{... | collective-permute-start | bytes 1990664 | tf_op jit(solution)/shard_map/ppermute | solution.py:478
  25.6 1.0 broadcast_select_fusion
  26.6 0.3 convolution_bitcast_fusion.gram
  26.9 5.9 %collective-permute-done.1.refs_3_ = bf16[2,15,48,128]{3,2,1,0:T(8,128)(2,1)S(1)} collective-permute-done((bf16[2,15,48,128]{3,2,1,0:T(8,128)(2,1)S(1)}, bf16[2,15,48,128]{3,2,1,0:T(8,128)(2,1)S(1)}, u32[]{:S(2)}, u32[]{:S(2)}) %collective-permute-start.1) | collective-permute-done | bytes 368672 | tf_op jit(solution)/shard_map/ppermute | solution.py:477
  32.8 3.7 %collective-permute-start.3 = (bf16[2,15,48,128]{3,2,1,0:T(8,128)(2,1)S(1)}, bf16[2,15,48,128]{3,2,1,0:T(8,128)(2,1)S(1)}, u32[]{:S(2)}, u32[]{:S(2)}) collective-permute-start(bf16[2,15,48,128]{3,2,1,0:T(8,128)(2,1)S(1)} %collective-permute-done.1.refs_3_), channel_id=1, source_target_pairs={{0,8},{8,16},{12,4},{16,24},{20,12},{28,20},{1,9},{9,17},{13,5},{1... | collective-permute-start | bytes 1105928 | tf_op jit(solution)/shard_map/ppermute | solution.py:485
  36.6 0.1 collective-permute-start.2
  36.7 2.0 %collective-permute-start.4 = (bf16[8,48,48]{2,1,0:T(8,128)(2,1)S(1)}, bf16[8,48,48]{2,1,0:T(8,128)(2,1)S(1)}, u32[]{:S(2)}, u32[]{:S(2)}) collective-permute-start(bf16[8,48,48]{2,1,0:T(8,128)(2,1)S(1)} %get-tuple-element.33), channel_id=1, source_target_pairs={{0,4},{4,0},{8,12},{12,8},{16,20},{20,16},{24,28},{28,24},{1,5},{5... | collective-permute-start | bytes 110600 | tf_op jit(solution)/shard_map/ppermute | solution.py:489
  38.7 0.7 collective-permute-start.5
  39.3 7.2 %collective-permute-done.4.b_x = bf16[8,48,48]{2,1,0:T(8,128)(2,1)S(1)} collective-permute-done((bf16[8,48,48]{2,1,0:T(8,128)(2,1)S(1)}, bf16[8,48,48]{2,1,0:T(8,128)(2,1)S(1)}, u32[]{:S(2)}, u32[]{:S(2)}) %collective-permute-start.4) | collective-permute-done | bytes 36896 | tf_op jit(solution)/shard_map/ppermute | solution.py:489
  46.6 0.0 collective-permute-done.5.b_d
  46.6 0.0 copy-done.1
  46.6 3.0 %partials.1 = (f32[24,128]{1,0:T(8,128)S(1)}, bf16[2,48,24,48]{3,2,1,0:T(8,128)(2,1)S(1)}) custom-call(s32[8]{0:T(128)S(1)} %copy-done.6, bf16[2,48,48,128]{3,2,1,0:T(8,128)(2,1)S(1)} %copy-done.1, bf16[8,2,48,48]{3,2,1,0:T(8,128)(2,1)S(1)} %copy-done.2, bf16[8,48,48]{2,1,0:T(8,128)(2,1)S(1)} %collective-permute-done.4.b_x, ...), custom_call_target="tpu_custom_call" | custom-call | flops 256 | bytes 256 | tf_op jit(solution)/shard_map/partials/pallas_call | solution.py:150
  49.6 0.0 collective-permute-done.2.refs_4_
  49.7 0.0 collective-permute-done.3.refs_5_.refs_4_
  49.7 0.0 collective-permute-done.refs_2_
  49.7 0.0 copy-start.9
  49.7 2.8 %filtered.3.refs_0_ = bf16[4,10,48,128]{3,2,1,0:T(8,128)(2,1)S(1)} custom-call(bf16[2,48,48,128]{3,2,1,0:T(8,128)(2,1)S(1)} %copy-done.1, bf16[2,1,48,128]{3,2,1,0:T(8,128)(2,1)S(1)} %get-tuple-element.27.refs_1_, bf16[2,27,48,128]{3,2,1,0:T(8,128)(2,1)S(1)} %collective-permute-done.refs_2_, bf16[2,15,48,128]{3,2,1,0:T(8,128)(2,1)S(1)} %collective-permute-done.1.refs_3_, ...), custom_call_target="tpu_custom_call" | custom-call | flops 2457600 | bytes 15360000 | tf_op jit(solution)/shard_map/filtered/pallas_call | solution.py:367
  52.5 1.6 %collective-permute-start.9 = (bf16[4,10,48,128]{3,2,1,0:T(8,128)(2,1)S(1)}, bf16[4,10,48,128]{3,2,1,0:T(8,128)(2,1)}, u32[]{:S(2)}, u32[]{:S(2)}) collective-permute-start(bf16[4,10,48,128]{3,2,1,0:T(8,128)(2,1)S(1)} %filtered.3.refs_0_), channel_id=1, source_target_pairs={{0,2},{1,3},{2,0},{3,1},{4,6},{5,7},{6,4},{7,5},{8,10},{9,11},{10,... | collective-permute-start | bytes 1474568 | tf_op jit(solution)/shard_map/ppermute | solution.py:503
  54.1 6.3 %collective-permute-start.6 = (bf16[2,12,48,128]{3,2,1,0:T(8,128)(2,1)}, bf16[2,12,48,128]{3,2,1,0:T(8,128)(2,1)}, u32[]{:S(2)}, u32[]{:S(2)}) collective-permute-start(bf16[2,12,48,128]{3,2,1,0:T(8,128)(2,1)} %collective-permute-done.2.refs_4_), channel_id=1, source_target_pairs={{0,8},{8,16},{12,4},{16,24},{20,12},{28,20},{1,9},{9,17},{13,5},{1... | collective-permute-start | bytes 884744 | tf_op jit(solution)/shard_map/ppermute | solution.py:488
  60.4 0.0 collective-permute-start.8
  60.4 0.0 collective-permute-start.11
  60.4 3.3 %collective-permute-done.9.refs_2_ = bf16[4,10,48,128]{3,2,1,0:T(8,128)(2,1)} collective-permute-done((bf16[4,10,48,128]{3,2,1,0:T(8,128)(2,1)S(1)}, bf16[4,10,48,128]{3,2,1,0:T(8,128)(2,1)}, u32[]{:S(2)}, u32[]{:S(2)}) %collective-permute-start.9) | collective-permute-done | bytes 491552 | tf_op jit(solution)/shard_map/ppermute | solution.py:503
  63.7 0.0 collective-permute-start.10
  63.7 0.4 collective-permute-done.11
  64.1 3.3 %collective-permute-start.12 = (f32[24,128]{1,0:T(8,128)S(1)}, f32[24,128]{1,0:T(8,128)S(1)}, u32[]{:S(2)}, u32[]{:S(2)}) collective-permute-start(f32[24,128]{1,0:T(8,128)S(1)} %add.19), channel_id=1, source_target_pairs={{0,8},{4,12},{8,0},{12,4},{16,24},{20,28},{24,16},{28,20},{1,9},{5... | collective-permute-start | bytes 36872 | tf_op jit(solution)/shard_map/ppermute | solution.py:508
  67.5 0.0 collective-permute-done.6.refs_6_
  67.5 4.9 %filtered.2 = (bf16[2,14,48,128]{3,2,1,0:T(8,128)(2,1)S(1)}, bf16[2,14,48,128]{3,2,1,0:T(8,128)(2,1)S(1)}) custom-call(bf16[2,48,48,128]{3,2,1,0:T(8,128)(2,1)S(1)} %copy-done.1, bf16[2,1,48,128]{3,2,1,0:T(8,128)(2,1)S(1)} %get-tuple-element.27.refs_1_, bf16[2,27,48,128]{3,2,1,0:T(8,128)(2,1)S(1)} %collective-permute-done.refs_2_, ...), custom_call_target="tpu_custom_call" | custom-call | flops 3440640 | bytes 21504000 | tf_op jit(solution)/shard_map/filtered/pallas_call | solution.py:367
  72.3 1.6 %collective-permute-start.7 = (bf16[2,14,48,128]{3,2,1,0:T(8,128)(2,1)S(1)}, bf16[2,14,48,128]{3,2,1,0:T(8,128)(2,1)S(1)}, u32[]{:S(2)}, u32[]{:S(2)}) collective-permute-start(bf16[2,14,48,128]{3,2,1,0:T(8,128)(2,1)S(1)} %get-tuple-element.39.refs_0_), channel_id=1, source_target_pairs={{0,2},{1,3},{2,0},{3,1},{4,6},{5,7},{6,4},{7,5},{8,10},{9,11},{10,... | collective-permute-start | bytes 1032200 | tf_op jit(solution)/shard_map/ppermute | solution.py:513
  73.9 0.0 collective-permute-done.12
  73.9 1.6 %collective-permute-start.13 = (f32[24,128]{1,0:T(8,128)S(1)}, f32[24,128]{1,0:T(8,128)S(1)}, u32[]{:S(2)}, u32[]{:S(2)}) collective-permute-start(f32[24,128]{1,0:T(8,128)S(1)} %add.20), channel_id=1, source_target_pairs={{0,16},{4,20},{8,24},{12,28},{16,0},{20,4},{24,8},{28,12},{1,17},{... | collective-permute-start | bytes 36872 | tf_op jit(solution)/shard_map/ppermute | solution.py:508
  75.5 0.3 fusion
  75.9 2.7 %collective-permute-done.13 = f32[24,128]{1,0:T(8,128)S(1)} collective-permute-done((f32[24,128]{1,0:T(8,128)S(1)}, f32[24,128]{1,0:T(8,128)S(1)}, u32[]{:S(2)}, u32[]{:S(2)}) %collective-permute-start.13) | collective-permute-done | bytes 12320 | tf_op jit(solution)/shard_map/ppermute | solution.py:508
  78.6 0.1 broadcast_in_dim.22.strength
  78.7 0.1 coefficients.1.a
  78.8 0.0 collective-permute-start.20
  78.8 3.7 %collective-permute-done.7.refs_2_ = bf16[2,14,48,128]{3,2,1,0:T(8,128)(2,1)S(1)} collective-permute-done((bf16[2,14,48,128]{3,2,1,0:T(8,128)(2,1)S(1)}, bf16[2,14,48,128]{3,2,1,0:T(8,128)(2,1)S(1)}, u32[]{:S(2)}, u32[]{:S(2)}) %collective-permute-start.7) | collective-permute-done | bytes 344096 | tf_op jit(solution)/shard_map/ppermute | solution.py:513
  82.6 1.5 %collective-permute-start.17 = (bf16[2,14,48,128]{3,2,1,0:T(8,128)(2,1)S(1)}, bf16[2,14,48,128]{3,2,1,0:T(8,128)(2,1)S(1)}, u32[]{:S(2)}, u32[]{:S(2)}) collective-permute-start(bf16[2,14,48,128]{3,2,1,0:T(8,128)(2,1)S(1)} %get-tuple-element.46.refs_0_), channel_id=1, source_target_pairs={{0,2},{1,3},{2,0},{3,1},{4,6},{5,7},{6,4},{7,5},{8,10},{9,11},{10,... | collective-permute-start | bytes 1032200 | tf_op jit(solution)/shard_map/ppermute | solution.py:517
  84.1 0.0 collective-permute-done.8.refs_1_
  84.1 0.0 collective-permute-done.10.refs_3_
  84.1 1.8 %rotated.3 = (bf16[2,10,48,128]{3,2,1,0:T(8,128)(2,1)S(1)}, bf16[2,10,48,128]{3,2,1,0:T(8,128)(2,1)S(1)}) custom-call(bf16[4,10,48,128]{3,2,1,0:T(8,128)(2,1)S(1)} %filtered.3.refs_0_, bf16[4,10,48,128]{3,2,1,0:T(8,128)(2,1)S(1)} %collective-permute-done.8.refs_1_, bf16[4,10,48,128]{3,2,1,0:T(8,128)(2,1)} %collective-permute-done.9.refs_2_, ...), custom_call_target="tpu_custom_call" | custom-call | flops 15728640 | bytes 153600 | tf_op jit(solution)/shard_map/rotated/pallas_call | solution.py:411
  86.0 0.1 collective-permute-start.21
  86.1 0.5 collective-permute-start.14
  86.5 0.1 collective-permute-start.16
  86.6 5.3 %collective-permute-done.17.refs_2_ = bf16[2,14,48,128]{3,2,1,0:T(8,128)(2,1)S(1)} collective-permute-done((bf16[2,14,48,128]{3,2,1,0:T(8,128)(2,1)S(1)}, bf16[2,14,48,128]{3,2,1,0:T(8,128)(2,1)S(1)}, u32[]{:S(2)}, u32[]{:S(2)}) %collective-permute-start.17) | collective-permute-done | bytes 344096 | tf_op jit(solution)/shard_map/ppermute | solution.py:517
  92.0 0.0 collective-permute-start.18
  92.0 0.0 collective-permute-done.20.refs_1_
  92.0 0.3 collective-permute-start.19
  92.3 0.0 collective-permute-done.21.refs_3_
  92.3 1.4 %rotated.5 = bf16[2,14,48,128]{3,2,1,0:T(8,128)(2,1)S(1)} custom-call(bf16[2,14,48,128]{3,2,1,0:T(8,128)(2,1)S(1)} %get-tuple-element.39.refs_0_, bf16[2,14,48,128]{3,2,1,0:T(8,128)(2,1)S(1)} %collective-permute-done.20.refs_1_, bf16[2,14,48,128]{3,2,1,0:T(8,128)(2,1)S(1)} %collective-permute-done.7.refs_2_, ...), custom_call_target="tpu_custom_call" | custom-call | flops 11010048 | bytes 107520 | tf_op jit(solution)/shard_map/rotated/pallas_call | solution.py:411
  93.7 1.8 %collective-permute-start.22 = (bf16[2,14,48,128]{3,2,1,0:T(8,128)(2,1)S(1)}, bf16[2,14,48,128]{3,2,1,0:T(8,128)(2,1)S(1)}, u32[]{:S(2)}, u32[]{:S(2)}) collective-permute-start(bf16[2,14,48,128]{3,2,1,0:T(8,128)(2,1)S(1)} %rotated.5), channel_id=1, source_target_pairs={{0,4},{4,0},{8,12},{12,8},{16,20},{20,16},{24,28},{28,24},{1,5},{5... | collective-permute-start | bytes 1032200 | tf_op jit(solution)/shard_map/ppermute | solution.py:526
  95.5 0.0 collective-permute-done.14.b
  95.5 1.5 %collective-permute-start.15 = (bf16[32,128]{1,0:T(8,128)(2,1)S(1)}, bf16[32,128]{1,0:T(8,128)(2,1)S(1)}, u32[]{:S(2)}, u32[]{:S(2)}) collective-permute-start(bf16[32,128]{1,0:T(8,128)(2,1)S(1)} %pad_maximum_fusion), channel_id=1, source_target_pairs={{0,2},{1,3},{2,0},{3,1},{4,6},{5,7},{6,4},{7,5},{8,10},{9,11},{10,... | collective-permute-start | bytes 24584 | tf_op jit(solution)/shard_map/ppermute | solution.py:522
  97.0 2.1 %collective-permute-done.15 = bf16[32,128]{1,0:T(8,128)(2,1)S(1)} collective-permute-done((bf16[32,128]{1,0:T(8,128)(2,1)S(1)}, bf16[32,128]{1,0:T(8,128)(2,1)S(1)}, u32[]{:S(2)}, u32[]{:S(2)}) %collective-permute-start.15) | collective-permute-done | bytes 8224 | tf_op jit(solution)/shard_map/ppermute | solution.py:522
  99.1 1.9 %nonlocal.1.term = f32[2,48,48,128]{3,2,1,0:T(8,128)S(1)} custom-call(bf16[16,128]{1,0:T(8,128)(2,1)S(1)} %coefficients.1.a, bf16[16,128]{1,0:T(8,128)(2,1)S(1)} %collective-permute-done.14.b, bf16[16,128]{1,0:T(8,128)(2,1)S(1)} %get-tuple-element.52.c, bf16[16,128]{1,0:T(8,128)(2,1)S(1)} %get-tuple-element.51.d, bf16[4,128,128]{2,1,0:T(8,128)(2,1)S(1)} %copy.18.refs_4_.q, ...), custom_call_target="tpu_custom_call" | custom-call | flops 256 | bytes 256 | tf_op jit(solution)/shard_map/nonlocal/pallas_call | solution.py:225
  101.0 0.0 collective-permute-done.16.refs_1_
  101.0 0.0 collective-permute-done.18.refs_3_
  101.0 1.4 %rotated.4.refs_1_ = bf16[2,14,48,128]{3,2,1,0:T(8,128)(2,1)S(1)} custom-call(bf16[2,14,48,128]{3,2,1,0:T(8,128)(2,1)S(1)} %get-tuple-element.46.refs_0_, bf16[2,14,48,128]{3,2,1,0:T(8,128)(2,1)S(1)} %collective-permute-done.16.refs_1_, bf16[2,14,48,128]{3,2,1,0:T(8,128)(2,1)S(1)} %collective-permute-done.17.refs_2_, ...), custom_call_target="tpu_custom_call" | custom-call | flops 11010048 | bytes 107520 | tf_op jit(solution)/shard_map/rotated/pallas_call | solution.py:411
  102.4 0.0 collective-permute-done.19.refs_2_
  102.5 5.3 %collective-permute-done.22.refs_3_ = bf16[2,14,48,128]{3,2,1,0:T(8,128)(2,1)S(1)} collective-permute-done((bf16[2,14,48,128]{3,2,1,0:T(8,128)(2,1)S(1)}, bf16[2,14,48,128]{3,2,1,0:T(8,128)(2,1)S(1)}, u32[]{:S(2)}, u32[]{:S(2)}) %collective-permute-start.22) | collective-permute-done | bytes 344096 | tf_op jit(solution)/shard_map/ppermute | solution.py:526
  107.7 1.2 %assembled.1 = bf16[2,48,48,128]{3,2,1,0:T(8,128)(2,1)} custom-call(f32[2,48,48,128]{3,2,1,0:T(8,128)S(1)} %nonlocal.1.term, bf16[2,10,48,128]{3,2,1,0:T(8,128)(2,1)S(1)} %get-tuple-element.45.refs_0_, bf16[2,14,48,128]{3,2,1,0:T(8,128)(2,1)S(1)} %rotated.4.refs_1_, bf16[2,10,48,128]{3,2,1,0:T(8,128)(2,1)S(1)} %collective-permute-done.19.refs_2_, ...), custom_call_target="tpu_custom_call" | custom-call | flops 256 | bytes 256 | tf_op jit(solution)/shard_map/assembled/pallas_call | solution.py:436
  (27 shorter events, 0.1 us)
Async XLA Ops:
  0.0 75.5 %copy-start = (bf16[12,128,128]{2,1,0:T(8,128)(2,1)S(1)}, bf16[12,128,128]{2,1,0:T(8,128)(2,1)}, u32[]{:S(2)}) copy-start(bf16[12,128,128]{2,1,0:T(8,128)(2,1)} %param.13) | copy-start | bytes 1179652
  0.0 46.6 %copy-start.1 = (bf16[2,48,48,128]{3,2,1,0:T(8,128)(2,1)S(1)}, bf16[2,48,48,128]{3,2,1,0:T(8,128)(2,1)}, u32[]{:S(2)}) copy-start(bf16[2,48,48,128]{3,2,1,0:T(8,128)(2,1)} %refs_0_.3) | copy-start | bytes 3538948
  0.0 46.6 %copy-start.5 = (f32[2,48,48]{2,1,0:T(8,128)S(1)}, f32[2,48,48]{2,1,0:T(8,128)}, u32[]{:S(2)}) copy-start(f32[2,48,48]{2,1,0:T(8,128)} %potential.1) | copy-start | bytes 55300
  0.0 25.5 %copy-start.6 = (s32[8]{0:T(128)S(1)}, s32[8]{0:T(128)}, u32[]{:S(2)}) copy-start(s32[8]{0:T(128)} %atoms.1) | copy-start | bytes 100
  0.0 26.6 %copy-start.2 = (bf16[8,2,48,48]{3,2,1,0:T(8,128)(2,1)S(1)}, bf16[8,2,48,48]{3,2,1,0:T(8,128)(2,1)}, u32[]{:S(2)}) copy-start(bf16[8,2,48,48]{3,2,1,0:T(8,128)(2,1)} %beta.1) | copy-start | bytes 221188
  20.6 0.7 copy-start.7
  21.3 11.5 %collective-permute-start.1 = (bf16[2,15,48,128]{3,2,1,0:T(8,128)(2,1)S(1)}, bf16[2,15,48,128]{3,2,1,0:T(8,128)(2,1)S(1)}, u32[]{:S(2)}, u32[]{:S(2)}) collective-permute-start(bf16[2,15,48,128]{3,2,1,0:T(8,128)(2,1)S(1)} %get-tuple-element.29), channel_id=1, source_target_pairs={{0,4},{4,0},{8,12},{12,8},{16,20},{20,16},{24,28},{28,24},{1,5},{5... | collective-permute-start | bytes 1105928 | tf_op jit(solution)/shard_map/ppermute | solution.py:477
  24.3 25.4 %collective-permute-start = (bf16[2,27,48,128]{3,2,1,0:T(8,128)(2,1)}, bf16[2,27,48,128]{3,2,1,0:T(8,128)(2,1)S(1)}, u32[]{:S(2)}, u32[]{:S(2)}) collective-permute-start(bf16[2,27,48,128]{3,2,1,0:T(8,128)(2,1)} %get-tuple-element.28), channel_id=1, source_target_pairs={{4,12},{8,0},{12,20},{16,8},{20,28},{24,16},{5,13},{9,1},{13,21},{... | collective-permute-start | bytes 1990664 | tf_op jit(solution)/shard_map/ppermute | solution.py:478
  32.8 16.8 %collective-permute-start.3 = (bf16[2,15,48,128]{3,2,1,0:T(8,128)(2,1)S(1)}, bf16[2,15,48,128]{3,2,1,0:T(8,128)(2,1)S(1)}, u32[]{:S(2)}, u32[]{:S(2)}) collective-permute-start(bf16[2,15,48,128]{3,2,1,0:T(8,128)(2,1)S(1)} %collective-permute-done.1.refs_3_), channel_id=1, source_target_pairs={{0,8},{8,16},{12,4},{16,24},{20,12},{28,20},{1,9},{9,17},{13,5},{1... | collective-permute-start | bytes 1105928 | tf_op jit(solution)/shard_map/ppermute | solution.py:485
  36.6 13.1 %collective-permute-start.2 = (bf16[2,12,48,128]{3,2,1,0:T(8,128)(2,1)}, bf16[2,12,48,128]{3,2,1,0:T(8,128)(2,1)}, u32[]{:S(2)}, u32[]{:S(2)}) collective-permute-start(bf16[2,12,48,128]{3,2,1,0:T(8,128)(2,1)} %copy-done.7), channel_id=1, source_target_pairs={{0,4},{4,0},{8,12},{12,8},{16,20},{20,16},{24,28},{28,24},{1,5},{5... | collective-permute-start | bytes 884744 | tf_op jit(solution)/shard_map/ppermute | solution.py:487
  36.7 9.9 %collective-permute-start.4 = (bf16[8,48,48]{2,1,0:T(8,128)(2,1)S(1)}, bf16[8,48,48]{2,1,0:T(8,128)(2,1)S(1)}, u32[]{:S(2)}, u32[]{:S(2)}) collective-permute-start(bf16[8,48,48]{2,1,0:T(8,128)(2,1)S(1)} %get-tuple-element.33), channel_id=1, source_target_pairs={{0,4},{4,0},{8,12},{12,8},{16,20},{20,16},{24,28},{28,24},{1,5},{5... | collective-permute-start | bytes 110600 | tf_op jit(solution)/shard_map/ppermute | solution.py:489
  38.7 7.9 %collective-permute-start.5 = (bf16[8,48,48]{2,1,0:T(8,128)(2,1)S(1)}, bf16[8,48,48]{2,1,0:T(8,128)(2,1)S(1)}, u32[]{:S(2)}, u32[]{:S(2)}) collective-permute-start(bf16[8,48,48]{2,1,0:T(8,128)(2,1)S(1)} %get-tuple-element.34), channel_id=1, source_target_pairs={{4,8},{8,4},{12,16},{16,12},{20,24},{24,20},{5,9},{9,5},{13,17},{1... | collective-permute-start | bytes 110600 | tf_op jit(solution)/shard_map/ppermute | solution.py:490
  49.6 2.9 %copy-start.3 = (bf16[2,48,24,48]{3,2,1,0:T(8,128)(2,1)}, bf16[2,48,24,48]{3,2,1,0:T(8,128)(2,1)S(1)}, u32[]{:S(2)}) copy-start(bf16[2,48,24,48]{3,2,1,0:T(8,128)(2,1)S(1)} %get-tuple-element.44.weights) | copy-start | bytes 663556
  49.7 10.7 %copy-start.9 = (s32[12,2]{0,1:T(2,128)S(1)}, s32[12,2]{0,1:T(2,128)}, u32[]{:S(2)}) copy-start(s32[12,2]{0,1:T(2,128)} %param.12) | copy-start | bytes 292
  52.5 11.2 %collective-permute-start.9 = (bf16[4,10,48,128]{3,2,1,0:T(8,128)(2,1)S(1)}, bf16[4,10,48,128]{3,2,1,0:T(8,128)(2,1)}, u32[]{:S(2)}, u32[]{:S(2)}) collective-permute-start(bf16[4,10,48,128]{3,2,1,0:T(8,128)(2,1)S(1)} %filtered.3.refs_0_), channel_id=1, source_target_pairs={{0,2},{1,3},{2,0},{3,1},{4,6},{5,7},{6,4},{7,5},{8,10},{9,11},{10,... | collective-permute-start | bytes 1474568 | tf_op jit(solution)/shard_map/ppermute | solution.py:503
  54.1 13.4 %collective-permute-start.6 = (bf16[2,12,48,128]{3,2,1,0:T(8,128)(2,1)}, bf16[2,12,48,128]{3,2,1,0:T(8,128)(2,1)}, u32[]{:S(2)}, u32[]{:S(2)}) collective-permute-start(bf16[2,12,48,128]{3,2,1,0:T(8,128)(2,1)} %collective-permute-done.2.refs_4_), channel_id=1, source_target_pairs={{0,8},{8,16},{12,4},{16,24},{20,12},{28,20},{1,9},{9,17},{13,5},{1... | collective-permute-start | bytes 884744 | tf_op jit(solution)/shard_map/ppermute | solution.py:488
  60.4 23.7 %collective-permute-start.8 = (bf16[4,10,48,128]{3,2,1,0:T(8,128)(2,1)S(1)}, bf16[4,10,48,128]{3,2,1,0:T(8,128)(2,1)S(1)}, u32[]{:S(2)}, u32[]{:S(2)}) collective-permute-start(bf16[4,10,48,128]{3,2,1,0:T(8,128)(2,1)S(1)} %filtered.3.refs_0_), channel_id=1, source_target_pairs={{0,1},{1,0},{2,3},{3,2},{4,5},{5,4},{6,7},{7,6},{8,9},{9,8},{10,11... | collective-permute-start | bytes 1474568 | tf_op jit(solution)/shard_map/ppermute | solution.py:504
  60.4 3.7 %collective-permute-start.11 = (f32[24,128]{1,0:T(8,128)S(1)}, f32[24,128]{1,0:T(8,128)S(1)}, u32[]{:S(2)}, u32[]{:S(2)}) collective-permute-start(f32[24,128]{1,0:T(8,128)S(1)} %get-tuple-element.42), channel_id=1, source_target_pairs={{0,4},{4,0},{8,12},{12,8},{16,20},{20,16},{24,28},{28,24},{1,5},{5... | collective-permute-start | bytes 36872 | tf_op jit(solution)/shard_map/ppermute | solution.py:508
  63.7 20.4 %collective-permute-start.10 = (bf16[4,10,48,128]{3,2,1,0:T(8,128)(2,1)}, bf16[4,10,48,128]{3,2,1,0:T(8,128)(2,1)S(1)}, u32[]{:S(2)}, u32[]{:S(2)}) collective-permute-start(bf16[4,10,48,128]{3,2,1,0:T(8,128)(2,1)} %collective-permute-done.9.refs_2_), channel_id=1, source_target_pairs={{0,1},{1,0},{2,3},{3,2},{4,5},{5,4},{6,7},{7,6},{8,9},{9,8},{10,11... | collective-permute-start | bytes 1474568 | tf_op jit(solution)/shard_map/ppermute | solution.py:514
  64.1 14.5 %copy-start.8 = (f32[8]{0:T(128)S(1)}, f32[8]{0:T(128)}, u32[]{:S(2)}) copy-start(f32[8]{0:T(128)} %param.10) | copy-start | bytes 100
  64.1 9.8 %collective-permute-start.12 = (f32[24,128]{1,0:T(8,128)S(1)}, f32[24,128]{1,0:T(8,128)S(1)}, u32[]{:S(2)}, u32[]{:S(2)}) collective-permute-start(f32[24,128]{1,0:T(8,128)S(1)} %add.19), channel_id=1, source_target_pairs={{0,8},{4,12},{8,0},{12,4},{16,24},{20,28},{24,16},{28,20},{1,9},{5... | collective-permute-start | bytes 36872 | tf_op jit(solution)/shard_map/ppermute | solution.py:508
  72.3 10.3 %collective-permute-start.7 = (bf16[2,14,48,128]{3,2,1,0:T(8,128)(2,1)S(1)}, bf16[2,14,48,128]{3,2,1,0:T(8,128)(2,1)S(1)}, u32[]{:S(2)}, u32[]{:S(2)}) collective-permute-start(bf16[2,14,48,128]{3,2,1,0:T(8,128)(2,1)S(1)} %get-tuple-element.39.refs_0_), channel_id=1, source_target_pairs={{0,2},{1,3},{2,0},{3,1},{4,6},{5,7},{6,4},{7,5},{8,10},{9,11},{10,... | collective-permute-start | bytes 1032200 | tf_op jit(solution)/shard_map/ppermute | solution.py:513
  73.9 4.7 %collective-permute-start.13 = (f32[24,128]{1,0:T(8,128)S(1)}, f32[24,128]{1,0:T(8,128)S(1)}, u32[]{:S(2)}, u32[]{:S(2)}) collective-permute-start(f32[24,128]{1,0:T(8,128)S(1)} %add.20), channel_id=1, source_target_pairs={{0,16},{4,20},{8,24},{12,28},{16,0},{20,4},{24,8},{28,12},{1,17},{... | collective-permute-start | bytes 36872 | tf_op jit(solution)/shard_map/ppermute | solution.py:508
  78.8 13.2 %collective-permute-start.20 = (bf16[2,14,48,128]{3,2,1,0:T(8,128)(2,1)S(1)}, bf16[2,14,48,128]{3,2,1,0:T(8,128)(2,1)S(1)}, u32[]{:S(2)}, u32[]{:S(2)}) collective-permute-start(bf16[2,14,48,128]{3,2,1,0:T(8,128)(2,1)S(1)} %get-tuple-element.39.refs_0_), channel_id=1, source_target_pairs={{0,1},{1,0},{2,3},{3,2},{4,5},{5,4},{6,7},{7,6},{8,9},{9,8},{10,11... | collective-permute-start | bytes 1032200 | tf_op jit(solution)/shard_map/ppermute | solution.py:511
  82.6 9.4 %collective-permute-start.17 = (bf16[2,14,48,128]{3,2,1,0:T(8,128)(2,1)S(1)}, bf16[2,14,48,128]{3,2,1,0:T(8,128)(2,1)S(1)}, u32[]{:S(2)}, u32[]{:S(2)}) collective-permute-start(bf16[2,14,48,128]{3,2,1,0:T(8,128)(2,1)S(1)} %get-tuple-element.46.refs_0_), channel_id=1, source_target_pairs={{0,2},{1,3},{2,0},{3,1},{4,6},{5,7},{6,4},{7,5},{8,10},{9,11},{10,... | collective-permute-start | bytes 1032200 | tf_op jit(solution)/shard_map/ppermute | solution.py:517
  86.0 13.2 %copy-start.4 = (bf16[2,48,24,48]{3,2,1,0:T(8,128)(2,1)S(1)}, bf16[2,48,24,48]{3,2,1,0:T(8,128)(2,1)}, u32[]{:S(2)}) copy-start(bf16[2,48,24,48]{3,2,1,0:T(8,128)(2,1)} %copy-done.3) | copy-start | bytes 663556
  86.0 6.3 %collective-permute-start.21 = (bf16[2,14,48,128]{3,2,1,0:T(8,128)(2,1)S(1)}, bf16[2,14,48,128]{3,2,1,0:T(8,128)(2,1)S(1)}, u32[]{:S(2)}, u32[]{:S(2)}) collective-permute-start(bf16[2,14,48,128]{3,2,1,0:T(8,128)(2,1)S(1)} %collective-permute-done.7.refs_2_), channel_id=1, source_target_pairs={{0,1},{1,0},{2,3},{3,2},{4,5},{5,4},{6,7},{7,6},{8,9},{9,8},{10,11... | collective-permute-start | bytes 1032200 | tf_op jit(solution)/shard_map/ppermute | solution.py:519
  86.1 9.4 %collective-permute-start.14 = (bf16[16,128]{1,0:T(8,128)(2,1)S(1)}, bf16[16,128]{1,0:T(8,128)(2,1)S(1)}, u32[]{:S(2)}, u32[]{:S(2)}) collective-permute-start(bf16[16,128]{1,0:T(8,128)(2,1)S(1)} %coefficients.1.a), channel_id=1, source_target_pairs={{0,1},{1,0},{2,3},{3,2},{4,5},{5,4},{6,7},{7,6},{8,9},{9,8},{10,11... | collective-permute-start | bytes 12296 | tf_op jit(solution)/shard_map/ppermute | solution.py:521
  86.5 14.5 %collective-permute-start.16 = (bf16[2,14,48,128]{3,2,1,0:T(8,128)(2,1)S(1)}, bf16[2,14,48,128]{3,2,1,0:T(8,128)(2,1)S(1)}, u32[]{:S(2)}, u32[]{:S(2)}) collective-permute-start(bf16[2,14,48,128]{3,2,1,0:T(8,128)(2,1)S(1)} %get-tuple-element.46.refs_0_), channel_id=1, source_target_pairs={{0,1},{1,0},{2,3},{3,2},{4,5},{5,4},{6,7},{7,6},{8,9},{9,8},{10,11... | collective-permute-start | bytes 1032200 | tf_op jit(solution)/shard_map/ppermute | solution.py:512
  92.0 9.1 %collective-permute-start.18 = (bf16[2,14,48,128]{3,2,1,0:T(8,128)(2,1)S(1)}, bf16[2,14,48,128]{3,2,1,0:T(8,128)(2,1)S(1)}, u32[]{:S(2)}, u32[]{:S(2)}) collective-permute-start(bf16[2,14,48,128]{3,2,1,0:T(8,128)(2,1)S(1)} %collective-permute-done.17.refs_2_), channel_id=1, source_target_pairs={{0,1},{1,0},{2,3},{3,2},{4,5},{5,4},{6,7},{7,6},{8,9},{9,8},{10,11... | collective-permute-start | bytes 1032200 | tf_op jit(solution)/shard_map/ppermute | solution.py:527
  92.0 10.5 %collective-permute-start.19 = (bf16[2,10,48,128]{3,2,1,0:T(8,128)(2,1)S(1)}, bf16[2,10,48,128]{3,2,1,0:T(8,128)(2,1)S(1)}, u32[]{:S(2)}, u32[]{:S(2)}) collective-permute-start(bf16[2,10,48,128]{3,2,1,0:T(8,128)(2,1)S(1)} %get-tuple-element.47), channel_id=1, source_target_pairs={{0,4},{4,0},{8,12},{12,8},{16,20},{20,16},{24,28},{28,24},{1,5},{5... | collective-permute-start | bytes 737288 | tf_op jit(solution)/shard_map/ppermute | solution.py:520
  93.7 14.0 %collective-permute-start.22 = (bf16[2,14,48,128]{3,2,1,0:T(8,128)(2,1)S(1)}, bf16[2,14,48,128]{3,2,1,0:T(8,128)(2,1)S(1)}, u32[]{:S(2)}, u32[]{:S(2)}) collective-permute-start(bf16[2,14,48,128]{3,2,1,0:T(8,128)(2,1)S(1)} %rotated.5), channel_id=1, source_target_pairs={{0,4},{4,0},{8,12},{12,8},{16,20},{20,16},{24,28},{28,24},{1,5},{5... | collective-permute-start | bytes 1032200 | tf_op jit(solution)/shard_map/ppermute | solution.py:526
  95.5 3.7 %collective-permute-start.15 = (bf16[32,128]{1,0:T(8,128)(2,1)S(1)}, bf16[32,128]{1,0:T(8,128)(2,1)S(1)}, u32[]{:S(2)}, u32[]{:S(2)}) collective-permute-start(bf16[32,128]{1,0:T(8,128)(2,1)S(1)} %pad_maximum_fusion), channel_id=1, source_target_pairs={{0,2},{1,3},{2,0},{3,1},{4,6},{5,7},{6,4},{7,5},{8,10},{9,11},{10,... | collective-permute-start | bytes 24584 | tf_op jit(solution)/shard_map/ppermute | solution.py:522

commit v7 on v6

--- a/solution.py
+++ b/solution.py
@@ -81,13 +81,12 @@
     def out(rows):
         return jax.ShapeDtypeStruct((planes, rows, width_y, orbs), BF16)
 
-    anywhere = pl.BlockSpec(memory_space=pl.ANY)
     local = pl.BlockSpec(memory_space=pltpu.VMEM)
     return pl.pallas_call(
         functools.partial(prepare_kernel, early),
         out_shape=(out(early + 1), out(window - early), out(window + 1), out(1)),
         in_specs=[pl.BlockSpec(memory_space=pltpu.MemorySpace.HBM)] * 2,
-        out_specs=(anywhere, anywhere, anywhere, local),
+        out_specs=(local,) * 4,
         scratch_shapes=[pltpu.VMEM(potential.shape, F32), pltpu.SemaphoreType.DMA((6,))],
         compiler_params=params(),
         cost_estimate=cost(4096, 4096),
@@ -406,7 +405,7 @@
 def rotated(blocks, q, pieces):
     a = blocks[0]
     size = a.size
-    group = max(g for g in range(1, 7) if a.shape[1] % g == 0)
+    group = max(g for g in range(1, 9) if a.shape[1] % g == 0)
     out = jax.ShapeDtypeStruct((a.shape[0] // pieces, *a.shape[1:]), BF16)
     return pl.pallas_call(
         functools.partial(rotate_kernel, group),
@@ -481,13 +480,12 @@
     active = jnp.abs(place - atom_slab) <= 1
     beta_m = jnp.where(active[:, None, None, None], beta, jnp.zeros_like(beta))
     gram = jnp.einsum("pzxy,qzxy->pq", beta_m, beta_m, preferred_element_type=F32)
-    far, near, gram, xr1 = ordered(far, near, gram, xr1)
+    f_x = lax.ppermute(near, "space", swap)
+    f_d = lax.ppermute(far, "space", raster)
     zf1 = lax.ppermute(xr1, "space", other_way)
-    second, _ = ordered(to_x2, xr1)
+    second, _, f_x, f_d = ordered(to_x2, xr1, f_x, f_d)
     xr2 = lax.ppermute(second, "space", swap)
     zf2 = lax.ppermute(xr2, "space", other_way)
-    f_x = lax.ppermute(near, "space", swap)
-    f_d = lax.ppermute(far, "space", raster)
     strong = jnp.broadcast_to(strength[:, None], (count, orbs))
 
     me = lax.axis_index("orb")
@@ -497,7 +495,7 @@
     q = jnp.einsum("ki,kab->iab", rows_hot, q_tiles, preferred_element_type=F32).astype(BF16)
 
     sums, weights = partials(count, atom_slab, psi, beta, f_x, f_d, potential, gram)
-    zf1, sums, _ = ordered(zf1, sums, xr2)
+    zf1, sums = ordered(zf1, sums)
     operands = (psi, blocks, zo)
     (block1,) = filtered(slabs, 0, rows1, True, operands, (xr1,), (zf1,))
     y1 = lax.ppermute(block1, "orb", across)
@@ -515,14 +513,16 @@
     give1, keep1 = rotated((block1, c1, y1, yc1), q, 2)
     keep_y, yg = ordered(keep2, yg)
     yk = lax.ppermute(keep_y, "orb", across)
-    yg, give1, coefs = ordered(yg, give1, coefs)
+    yg, coefs = ordered(yg, coefs)
     ycg = lax.ppermute(yg, "orb", beside)
+    ycg, give1 = ordered(ycg, give1)
     got1 = lax.ppermute(give1, "space", swap)
     coefs_c = lax.ppermute(coefs, "orb", beside)
     coefs_y = lax.ppermute(jnp.concatenate([coefs, coefs_c], axis=0), "orb", across)
     coefs_yc, coefs_y = coefs_y[2 * count :], coefs_y[: 2 * count]
     term = nonlocal_term(psi.shape, (coefs, coefs_c, coefs_y, coefs_yc), q, weights)
     (give2,) = rotated((give2, cg, yg, ycg), q, 1)
+    yk, give2 = ordered(yk, give2)
     got2 = lax.ppermute(give2, "space", swap)
     yck = lax.ppermute(yk, "orb", beside)
     (keep2,) = rotated((keep2, ck, yk, yck), q, 1)

time: 109 us -> 90 us (0.83)
  Pallas kernels: 39.1 us -> 20.4 us
  starting transfers between devices: 30.9 us -> 35.1 us
  waiting for transfers between devices: 36 us -> 32.2 us
    pallas_call x1, Pallas kernels: 20.5 us -> 2.42 us  [prepared(): pl.pallas_call(functools.partial(prepare_kernel, early), out_shape=(out(e...]
    ppermute x1, starting transfers between devices: 0.07 us -> 11.1 us  [shards(): xr2 = lax.ppermute(second, 'space', swap)]
    ppermute x1, waiting for transfers between devices: 0.01 us -> 7.43 us  [shards(): got1 = lax.ppermute(give1, 'space', swap)]
    ppermute x1, waiting for transfers between devices: 5.9 us -> 0.01 us  [shards(): xr1 = lax.ppermute(to_x, 'space', swap)]
    ppermute x1, waiting for transfers between devices: 5.26 us -> 0.01 us  [shards(): got2 = lax.ppermute(give2, 'space', swap)]
    ppermute x3, waiting for transfers between devices: 3.12 us -> 7.23 us  [shards(): lax.ppermute(sums, 'space', [(i, i ^ step) for i in range(slabs)])]
    ppermute x1, waiting for transfers between devices: 3.26 us -> 0.01 us  [shards(): y1 = lax.ppermute(block1, 'orb', across)]
    ppermute x1, starting transfers between devices: 6.31 us -> 3.74 us  [shards(): zf2 = lax.ppermute(xr2, 'space', other_way)]
  transfers between devices with their start and end apart: 23 -> 23, of which waited for: 9 -> 8; matrix products, arithmetic and copies ran while one was open for 2% -> 2% of each run, Pallas kernels for 13% -> 19%
where the time goes in v7:
time: 90 us; the launch traced here: 89.8 us
  starting transfers between devices  35.1 us (39%)
  waiting for transfers between devices  32.2 us (36%)
  Pallas kernels  20.4 us (23%)
  local copies, waits for them, and re-layouts  1.09 us (1%)
    ppermute x1, starting transfers between devices, shards(): xr2 = lax.ppermute(second, 'space', swap)  11.1 us
    ppermute x1, waiting for transfers between devices, shards(): got1 = lax.ppermute(give1, 'space', swap)  7.43 us
    pallas_call x2, Pallas kernels, filtered(): pl.pallas_call(functools.partial(filter_kernel, slabs, start, parts, join...  7.26 us
    ppermute x3, waiting for transfers between devices, shards(): lax.ppermute(sums, 'space', [(i, i ^ step) for i in range(slabs)])  7.23 us
    ppermute x1, waiting for transfers between devices, shards(): yk = lax.ppermute(keep_y, 'orb', across)  5.25 us
    ppermute x1, waiting for transfers between devices, shards(): f_x = lax.ppermute(near, 'space', swap)  5.14 us
    pallas_call x3, Pallas kernels, rotated(): pl.pallas_call(functools.partial(rotate_kernel, group), out_shape=(out,)...  4.4 us
    ppermute x1, starting transfers between devices, shards(): zf2 = lax.ppermute(xr2, 'space', other_way)  3.74 us
  transfers between devices with their start and end apart: 23, of which 8 were waited for; matrix products, arithmetic and copies ran while one was open for 2% of the time, Pallas kernels for 19%

profile of v7, /device:TPU:0, one launch (start us, length us, event | category | flops | bytes accessed | tf_op | source)
XLA Modules:
  0.0 89.8 jit_solution(15698451508768411409)
XLA Ops:
  0.0 0.0 copy-start
  0.0 2.4 %prepared.1 = (bf16[2,15,48,128]{3,2,1,0:T(8,128)(2,1)}, bf16[2,12,48,128]{3,2,1,0:T(8,128)(2,1)S(1)}, bf16[2,27,48,128]{3,2,1,0:T(8,128)(2,1)}, bf16[2,1,48,128]{3,2,1,0:T(8,128)(2,1)S(1)}) custom-call(bf16[2,48,48,128]{3,2,1,0:T(8,128)(2,1)} %refs_0_.3, f32[2,48,48]{2,1,0:T(8,128)} %potential.1), custom_call_target="tpu_custom_call" | custom-call | flops 256 | bytes 256 | tf_op jit(solution)/shard_map/prepared/pallas_call | solution.py:85
  2.5 3.0 %collective-permute-start.1 = (bf16[2,15,48,128]{3,2,1,0:T(8,128)(2,1)}, bf16[2,15,48,128]{3,2,1,0:T(8,128)(2,1)S(1)}, u32[]{:S(2)}, u32[]{:S(2)}) collective-permute-start(bf16[2,15,48,128]{3,2,1,0:T(8,128)(2,1)} %get-tuple-element.30), channel_id=1, source_target_pairs={{0,4},{4,0},{8,12},{12,8},{16,20},{20,16},{24,28},{28,24},{1,5},{5... | collective-permute-start | bytes 1105928 | tf_op jit(solution)/shard_map/ppermute | solution.py:476
  5.5 1.3 %collective-permute-start = (bf16[2,27,48,128]{3,2,1,0:T(8,128)(2,1)}, bf16[2,27,48,128]{3,2,1,0:T(8,128)(2,1)S(1)}, u32[]{:S(2)}, u32[]{:S(2)}) collective-permute-start(bf16[2,27,48,128]{3,2,1,0:T(8,128)(2,1)} %get-tuple-element.29), channel_id=1, source_target_pairs={{4,12},{8,0},{12,20},{16,8},{20,28},{24,16},{5,13},{9,1},{13,21},{... | collective-permute-start | bytes 1990664 | tf_op jit(solution)/shard_map/ppermute | solution.py:477
  6.8 1.0 %dynamic-slice_bitcast_fusion = (bf16[8,48,48]{2,1,0:T(8,128)(2,1)S(1)}, bf16[8,48,48]{2,1,0:T(8,128)(2,1)S(1)}) fusion(bf16[8,2,48,48]{3,2,1,0:T(8,128)(2,1)} %beta.1, s32[]{:T(128)S(6)} %select_n.12, s32[]{:T(128)S(6)} %select_n.11), kind=kLoop, calls=%fused_computation.6 | loop fusion | bytes 147464 | tf_op jit(solution)/shard_map/jit(dynamic_index_in_dim)/squeeze | solution.py:478
  7.7 2.8 %collective-permute-start.2 = (bf16[8,48,48]{2,1,0:T(8,128)(2,1)S(1)}, bf16[8,48,48]{2,1,0:T(8,128)(2,1)S(1)}, u32[]{:S(2)}, u32[]{:S(2)}) collective-permute-start(bf16[8,48,48]{2,1,0:T(8,128)(2,1)S(1)} %get-tuple-element.52), channel_id=1, source_target_pairs={{0,4},{4,0},{8,12},{12,8},{16,20},{20,16},{24,28},{28,24},{1,5},{5... | collective-permute-start | bytes 110600 | tf_op jit(solution)/shard_map/ppermute | solution.py:483
  10.6 0.7 collective-permute-start.3
  11.2 5.1 %collective-permute-done.2.b_x = bf16[8,48,48]{2,1,0:T(8,128)(2,1)S(1)} collective-permute-done((bf16[8,48,48]{2,1,0:T(8,128)(2,1)S(1)}, bf16[8,48,48]{2,1,0:T(8,128)(2,1)S(1)}, u32[]{:S(2)}, u32[]{:S(2)}) %collective-permute-start.2) | collective-permute-done | bytes 36896 | tf_op jit(solution)/shard_map/ppermute | solution.py:483
  16.4 0.0 collective-permute-done.3.b_d
  16.4 0.0 collective-permute-done.1.refs_3_
  16.4 11.1 %collective-permute-start.4 = (bf16[2,12,48,128]{3,2,1,0:T(8,128)(2,1)S(1)}, bf16[2,12,48,128]{3,2,1,0:T(8,128)(2,1)S(1)}, u32[]{:S(2)}, u32[]{:S(2)}) collective-permute-start(bf16[2,12,48,128]{3,2,1,0:T(8,128)(2,1)S(1)} %get-tuple-element.32), channel_id=1, source_target_pairs={{0,4},{4,0},{8,12},{12,8},{16,20},{20,16},{24,28},{28,24},{1,5},{5... | collective-permute-start | bytes 884744 | tf_op jit(solution)/shard_map/ppermute | solution.py:487
  27.5 3.5 %collective-permute-start.5 = (bf16[2,15,48,128]{3,2,1,0:T(8,128)(2,1)S(1)}, bf16[2,15,48,128]{3,2,1,0:T(8,128)(2,1)S(1)}, u32[]{:S(2)}, u32[]{:S(2)}) collective-permute-start(bf16[2,15,48,128]{3,2,1,0:T(8,128)(2,1)S(1)} %collective-permute-done.1.refs_3_), channel_id=1, source_target_pairs={{0,8},{8,16},{12,4},{16,24},{20,12},{28,20},{1,9},{9,17},{13,5},{1... | collective-permute-start | bytes 1105928 | tf_op jit(solution)/shard_map/ppermute | solution.py:485
  31.0 0.0 copy-done.2
  31.0 0.1 broadcast_select_fusion
  31.1 1.9 %collective-permute-done.4.refs_4_ = bf16[2,12,48,128]{3,2,1,0:T(8,128)(2,1)S(1)} collective-permute-done((bf16[2,12,48,128]{3,2,1,0:T(8,128)(2,1)S(1)}, bf16[2,12,48,128]{3,2,1,0:T(8,128)(2,1)S(1)}, u32[]{:S(2)}, u32[]{:S(2)}) %collective-permute-start.4) | collective-permute-done | bytes 294944 | tf_op jit(solution)/shard_map/ppermute | solution.py:487
  33.0 3.7 %collective-permute-start.6 = (bf16[2,12,48,128]{3,2,1,0:T(8,128)(2,1)S(1)}, bf16[2,12,48,128]{3,2,1,0:T(8,128)(2,1)S(1)}, u32[]{:S(2)}, u32[]{:S(2)}) collective-permute-start(bf16[2,12,48,128]{3,2,1,0:T(8,128)(2,1)S(1)} %collective-permute-done.4.refs_4_), channel_id=1, source_target_pairs={{0,8},{8,16},{12,4},{16,24},{20,12},{28,20},{1,9},{9,17},{13,5},{1... | collective-permute-start | bytes 884744 | tf_op jit(solution)/shard_map/ppermute | solution.py:488
  36.8 0.3 convolution_bitcast_fusion.gram
  37.1 3.0 %partials.1 = (f32[24,128]{1,0:T(8,128)S(1)}, bf16[2,48,24,48]{3,2,1,0:T(8,128)(2,1)S(1)}) custom-call(s32[8]{0:T(128)S(1)} %copy-done.6, bf16[2,48,48,128]{3,2,1,0:T(8,128)(2,1)S(1)} %copy-done.1, bf16[8,2,48,48]{3,2,1,0:T(8,128)(2,1)S(1)} %copy-done.2, bf16[8,48,48]{2,1,0:T(8,128)(2,1)S(1)} %collective-permute-done.2.b_x, ...), custom_call_target="tpu_custom_call" | custom-call | flops 256 | bytes 256 | tf_op jit(solution)/shard_map/partials/pallas_call | solution.py:149
  40.1 0.0 collective-permute-done.5.refs_5_.refs_4_
  40.1 0.0 collective-permute-done.refs_2_
  40.2 2.8 %filtered.3.refs_0_ = bf16[4,10,48,128]{3,2,1,0:T(8,128)(2,1)S(1)} custom-call(bf16[2,48,48,128]{3,2,1,0:T(8,128)(2,1)S(1)} %copy-done.1, bf16[2,1,48,128]{3,2,1,0:T(8,128)(2,1)S(1)} %get-tuple-element.28.refs_1_, bf16[2,27,48,128]{3,2,1,0:T(8,128)(2,1)S(1)} %collective-permute-done.refs_2_, bf16[2,15,48,128]{3,2,1,0:T(8,128)(2,1)S(1)} %collective-permute-done.1.refs_3_, ...), custom_call_target="tpu_custom_call" | custom-call | flops 2457600 | bytes 15360000 | tf_op jit(solution)/shard_map/filtered/pallas_call | solution.py:366
  43.0 0.0 copy-done.3
  43.0 1.6 %collective-permute-start.14 = (bf16[4,10,48,128]{3,2,1,0:T(8,128)(2,1)S(1)}, bf16[4,10,48,128]{3,2,1,0:T(8,128)(2,1)}, u32[]{:S(2)}, u32[]{:S(2)}) collective-permute-start(bf16[4,10,48,128]{3,2,1,0:T(8,128)(2,1)S(1)} %filtered.3.refs_0_), channel_id=1, source_target_pairs={{0,2},{1,3},{2,0},{3,1},{4,6},{5,7},{6,4},{7,5},{8,10},{9,11},{10,... | collective-permute-start | bytes 1474568 | tf_op jit(solution)/shard_map/ppermute | solution.py:501
  44.6 0.0 collective-permute-start.8
  44.6 0.0 collective-permute-start.13
  44.6 3.7 %collective-permute-done.8 = f32[24,128]{1,0:T(8,128)S(1)} collective-permute-done((f32[24,128]{1,0:T(8,128)S(1)}, f32[24,128]{1,0:T(8,128)S(1)}, u32[]{:S(2)}, u32[]{:S(2)}) %collective-permute-start.8) | collective-permute-done | bytes 12320 | tf_op jit(solution)/shard_map/ppermute | solution.py:506
  48.3 2.1 %collective-permute-start.9 = (f32[24,128]{1,0:T(8,128)S(1)}, f32[24,128]{1,0:T(8,128)S(1)}, u32[]{:S(2)}, u32[]{:S(2)}) collective-permute-start(f32[24,128]{1,0:T(8,128)S(1)} %add.19), channel_id=1, source_target_pairs={{0,8},{4,12},{8,0},{12,4},{16,24},{20,28},{24,16},{28,20},{1,9},{5... | collective-permute-start | bytes 36872 | tf_op jit(solution)/shard_map/ppermute | solution.py:506
  50.4 0.0 collective-permute-done.6.refs_6_
  50.4 4.4 %filtered.2 = (bf16[2,14,48,128]{3,2,1,0:T(8,128)(2,1)}, bf16[2,14,48,128]{3,2,1,0:T(8,128)(2,1)S(1)}) custom-call(bf16[2,48,48,128]{3,2,1,0:T(8,128)(2,1)S(1)} %copy-done.1, bf16[2,1,48,128]{3,2,1,0:T(8,128)(2,1)S(1)} %get-tuple-element.28.refs_1_, bf16[2,27,48,128]{3,2,1,0:T(8,128)(2,1)S(1)} %collective-permute-done.refs_2_, ...), custom_call_target="tpu_custom_call" | custom-call | flops 3440640 | bytes 21504000 | tf_op jit(solution)/shard_map/filtered/pallas_call | solution.py:366
  54.8 0.5 collective-permute-start.7
  55.4 0.0 collective-permute-done.9
  55.4 1.1 %collective-permute-start.10 = (f32[24,128]{1,0:T(8,128)S(1)}, f32[24,128]{1,0:T(8,128)S(1)}, u32[]{:S(2)}, u32[]{:S(2)}) collective-permute-start(f32[24,128]{1,0:T(8,128)S(1)} %add.20), channel_id=1, source_target_pairs={{0,16},{4,20},{8,24},{12,28},{16,0},{20,4},{24,8},{28,12},{1,17},{... | collective-permute-start | bytes 36872 | tf_op jit(solution)/shard_map/ppermute | solution.py:506
  56.5 0.0 collective-permute-done.14.refs_2_
  56.5 0.0 collective-permute-start.15
  56.5 3.5 %collective-permute-done.10 = f32[24,128]{1,0:T(8,128)S(1)} collective-permute-done((f32[24,128]{1,0:T(8,128)S(1)}, f32[24,128]{1,0:T(8,128)S(1)}, u32[]{:S(2)}, u32[]{:S(2)}) %collective-permute-start.10) | collective-permute-done | bytes 12320 | tf_op jit(solution)/shard_map/ppermute | solution.py:506
  60.0 0.1 broadcast_in_dim.22.strength
  60.1 0.1 coefficients.1.a
  60.2 0.0 collective-permute-start.18
  60.3 2.0 %collective-permute-done.7.refs_2_ = bf16[2,14,48,128]{3,2,1,0:T(8,128)(2,1)S(1)} collective-permute-done((bf16[2,14,48,128]{3,2,1,0:T(8,128)(2,1)}, bf16[2,14,48,128]{3,2,1,0:T(8,128)(2,1)S(1)}, u32[]{:S(2)}, u32[]{:S(2)}) %collective-permute-start.7) | collective-permute-done | bytes 344096 | tf_op jit(solution)/shard_map/ppermute | solution.py:511
  62.3 0.0 collective-permute-start.19
  62.3 0.5 collective-permute-start.17
  62.8 0.0 collective-permute-done.13.refs_1_
  62.8 0.2 collective-permute-start.11
  63.0 0.3 fusion
  63.4 0.0 collective-permute-done.15.refs_3_
  63.4 0.3 collective-permute-start.16
  63.8 2.0 %rotated.3 = (bf16[2,10,48,128]{3,2,1,0:T(8,128)(2,1)S(1)}, bf16[2,10,48,128]{3,2,1,0:T(8,128)(2,1)S(1)}) custom-call(bf16[4,10,48,128]{3,2,1,0:T(8,128)(2,1)S(1)} %filtered.3.refs_0_, bf16[4,10,48,128]{3,2,1,0:T(8,128)(2,1)} %collective-permute-done.13.refs_1_, bf16[4,10,48,128]{3,2,1,0:T(8,128)(2,1)} %collective-permute-done.14.refs_2_, ...), custom_call_target="tpu_custom_call" | custom-call | flops 15728640 | bytes 153600 | tf_op jit(solution)/shard_map/rotated/pallas_call | solution.py:410
  65.8 0.0 collective-permute-done.19.refs_3_
  65.8 0.0 collective-permute-done.18.refs_1_
  65.8 1.7 %rotated.4 = bf16[2,14,48,128]{3,2,1,0:T(8,128)(2,1)S(1)} custom-call(bf16[2,14,48,128]{3,2,1,0:T(8,128)(2,1)} %get-tuple-element.38.refs_0_, bf16[2,14,48,128]{3,2,1,0:T(8,128)(2,1)S(1)} %collective-permute-done.18.refs_1_, bf16[2,14,48,128]{3,2,1,0:T(8,128)(2,1)S(1)} %collective-permute-done.7.refs_2_, ...), custom_call_target="tpu_custom_call" | custom-call | flops 11010048 | bytes 107520 | tf_op jit(solution)/shard_map/rotated/pallas_call | solution.py:410
  67.5 5.3 %collective-permute-done.17.refs_2_ = bf16[2,14,48,128]{3,2,1,0:T(8,128)(2,1)S(1)} collective-permute-done((bf16[2,14,48,128]{3,2,1,0:T(8,128)(2,1)S(1)}, bf16[2,14,48,128]{3,2,1,0:T(8,128)(2,1)S(1)}, u32[]{:S(2)}, u32[]{:S(2)}) %collective-permute-start.17) | collective-permute-done | bytes 344096 | tf_op jit(solution)/shard_map/ppermute | solution.py:515
  72.8 0.0 collective-permute-start.20
  72.8 1.2 %collective-permute-start.22 = (bf16[2,14,48,128]{3,2,1,0:T(8,128)(2,1)S(1)}, bf16[2,14,48,128]{3,2,1,0:T(8,128)(2,1)S(1)}, u32[]{:S(2)}, u32[]{:S(2)}) collective-permute-start(bf16[2,14,48,128]{3,2,1,0:T(8,128)(2,1)S(1)} %rotated.4), channel_id=1, source_target_pairs={{0,4},{4,0},{8,12},{12,8},{16,20},{20,16},{24,28},{28,24},{1,5},{5... | collective-permute-start | bytes 1032200 | tf_op jit(solution)/shard_map/ppermute | solution.py:526
  74.0 0.8 collective-permute-start.21
  74.8 0.0 collective-permute-done.11.b
  74.8 0.5 collective-permute-start.12
  75.3 3.2 %collective-permute-done.12 = bf16[32,128]{1,0:T(8,128)(2,1)S(1)} collective-permute-done((bf16[32,128]{1,0:T(8,128)(2,1)S(1)}, bf16[32,128]{1,0:T(8,128)(2,1)S(1)}, u32[]{:S(2)}, u32[]{:S(2)}) %collective-permute-start.12) | collective-permute-done | bytes 8224 | tf_op jit(solution)/shard_map/ppermute | solution.py:521
  78.5 1.9 %nonlocal.1.term = f32[2,48,48,128]{3,2,1,0:T(8,128)S(1)} custom-call(bf16[16,128]{1,0:T(8,128)(2,1)S(1)} %coefficients.1.a, bf16[16,128]{1,0:T(8,128)(2,1)S(1)} %collective-permute-done.11.b, bf16[16,128]{1,0:T(8,128)(2,1)S(1)} %get-tuple-element.54.c, bf16[16,128]{1,0:T(8,128)(2,1)S(1)} %get-tuple-element.53.d, bf16[4,128,128]{2,1,0:T(8,128)(2,1)S(1)} %copy.18.q.refs_4_, ...), custom_call_target="tpu_custom_call" | custom-call | flops 256 | bytes 256 | tf_op jit(solution)/shard_map/nonlocal/pallas_call | solution.py:224
  80.4 0.0 collective-permute-done.16.refs_1_
  80.4 0.0 collective-permute-done.20.refs_3_
  80.4 0.7 rotated.5.refs_1_
  81.1 7.4 %collective-permute-done.21.refs_2_ = bf16[2,10,48,128]{3,2,1,0:T(8,128)(2,1)S(1)} collective-permute-done((bf16[2,10,48,128]{3,2,1,0:T(8,128)(2,1)S(1)}, bf16[2,10,48,128]{3,2,1,0:T(8,128)(2,1)S(1)}, u32[]{:S(2)}, u32[]{:S(2)}) %collective-permute-start.21) | collective-permute-done | bytes 245792 | tf_op jit(solution)/shard_map/ppermute | solution.py:519
  88.5 0.0 collective-permute-done.22.refs_3_
  88.5 1.2 %assembled.1 = bf16[2,48,48,128]{3,2,1,0:T(8,128)(2,1)} custom-call(f32[2,48,48,128]{3,2,1,0:T(8,128)S(1)} %nonlocal.1.term, bf16[2,10,48,128]{3,2,1,0:T(8,128)(2,1)S(1)} %get-tuple-element.43.refs_0_, bf16[2,14,48,128]{3,2,1,0:T(8,128)(2,1)S(1)} %rotated.5.refs_1_, bf16[2,10,48,128]{3,2,1,0:T(8,128)(2,1)S(1)} %collective-permute-done.21.refs_2_, ...), custom_call_target="tpu_custom_call" | custom-call | flops 256 | bytes 256 | tf_op jit(solution)/shard_map/assembled/pallas_call | solution.py:435
  (25 shorter events, 0.1 us)
Async XLA Ops:
  0.0 63.0 %copy-start = (bf16[12,128,128]{2,1,0:T(8,128)(2,1)S(1)}, bf16[12,128,128]{2,1,0:T(8,128)(2,1)}, u32[]{:S(2)}) copy-start(bf16[12,128,128]{2,1,0:T(8,128)(2,1)} %param.13) | copy-start | bytes 1179652
  0.0 37.1 %copy-start.1 = (bf16[2,48,48,128]{3,2,1,0:T(8,128)(2,1)S(1)}, bf16[2,48,48,128]{3,2,1,0:T(8,128)(2,1)}, u32[]{:S(2)}) copy-start(bf16[2,48,48,128]{3,2,1,0:T(8,128)(2,1)} %refs_0_.3) | copy-start | bytes 3538948
  0.0 37.1 %copy-start.5 = (f32[2,48,48]{2,1,0:T(8,128)S(1)}, f32[2,48,48]{2,1,0:T(8,128)}, u32[]{:S(2)}) copy-start(f32[2,48,48]{2,1,0:T(8,128)} %potential.1) | copy-start | bytes 55300
  0.0 31.0 %copy-start.2 = (bf16[8,2,48,48]{3,2,1,0:T(8,128)(2,1)S(1)}, bf16[8,2,48,48]{3,2,1,0:T(8,128)(2,1)}, u32[]{:S(2)}) copy-start(bf16[8,2,48,48]{3,2,1,0:T(8,128)(2,1)} %beta.1) | copy-start | bytes 221188
  0.0 31.0 %copy-start.6 = (s32[8]{0:T(128)S(1)}, s32[8]{0:T(128)}, u32[]{:S(2)}) copy-start(s32[8]{0:T(128)} %atoms.1) | copy-start | bytes 100
  2.5 13.9 %collective-permute-start.1 = (bf16[2,15,48,128]{3,2,1,0:T(8,128)(2,1)}, bf16[2,15,48,128]{3,2,1,0:T(8,128)(2,1)S(1)}, u32[]{:S(2)}, u32[]{:S(2)}) collective-permute-start(bf16[2,15,48,128]{3,2,1,0:T(8,128)(2,1)} %get-tuple-element.30), channel_id=1, source_target_pairs={{0,4},{4,0},{8,12},{12,8},{16,20},{20,16},{24,28},{28,24},{1,5},{5... | collective-permute-start | bytes 1105928 | tf_op jit(solution)/shard_map/ppermute | solution.py:476
  5.5 34.7 %collective-permute-start = (bf16[2,27,48,128]{3,2,1,0:T(8,128)(2,1)}, bf16[2,27,48,128]{3,2,1,0:T(8,128)(2,1)S(1)}, u32[]{:S(2)}, u32[]{:S(2)}) collective-permute-start(bf16[2,27,48,128]{3,2,1,0:T(8,128)(2,1)} %get-tuple-element.29), channel_id=1, source_target_pairs={{4,12},{8,0},{12,20},{16,8},{20,28},{24,16},{5,13},{9,1},{13,21},{... | collective-permute-start | bytes 1990664 | tf_op jit(solution)/shard_map/ppermute | solution.py:477
  7.7 8.6 %collective-permute-start.2 = (bf16[8,48,48]{2,1,0:T(8,128)(2,1)S(1)}, bf16[8,48,48]{2,1,0:T(8,128)(2,1)S(1)}, u32[]{:S(2)}, u32[]{:S(2)}) collective-permute-start(bf16[8,48,48]{2,1,0:T(8,128)(2,1)S(1)} %get-tuple-element.52), channel_id=1, source_target_pairs={{0,4},{4,0},{8,12},{12,8},{16,20},{20,16},{24,28},{28,24},{1,5},{5... | collective-permute-start | bytes 110600 | tf_op jit(solution)/shard_map/ppermute | solution.py:483
  10.6 5.8 %collective-permute-start.3 = (bf16[8,48,48]{2,1,0:T(8,128)(2,1)S(1)}, bf16[8,48,48]{2,1,0:T(8,128)(2,1)S(1)}, u32[]{:S(2)}, u32[]{:S(2)}) collective-permute-start(bf16[8,48,48]{2,1,0:T(8,128)(2,1)S(1)} %get-tuple-element.51), channel_id=1, source_target_pairs={{4,8},{8,4},{12,16},{16,12},{20,24},{24,20},{5,9},{9,5},{13,17},{1... | collective-permute-start | bytes 110600 | tf_op jit(solution)/shard_map/ppermute | solution.py:484
  16.4 16.6 %collective-permute-start.4 = (bf16[2,12,48,128]{3,2,1,0:T(8,128)(2,1)S(1)}, bf16[2,12,48,128]{3,2,1,0:T(8,128)(2,1)S(1)}, u32[]{:S(2)}, u32[]{:S(2)}) collective-permute-start(bf16[2,12,48,128]{3,2,1,0:T(8,128)(2,1)S(1)} %get-tuple-element.32), channel_id=1, source_target_pairs={{0,4},{4,0},{8,12},{12,8},{16,20},{20,16},{24,28},{28,24},{1,5},{5... | collective-permute-start | bytes 884744 | tf_op jit(solution)/shard_map/ppermute | solution.py:487
  27.5 12.6 %collective-permute-start.5 = (bf16[2,15,48,128]{3,2,1,0:T(8,128)(2,1)S(1)}, bf16[2,15,48,128]{3,2,1,0:T(8,128)(2,1)S(1)}, u32[]{:S(2)}, u32[]{:S(2)}) collective-permute-start(bf16[2,15,48,128]{3,2,1,0:T(8,128)(2,1)S(1)} %collective-permute-done.1.refs_3_), channel_id=1, source_target_pairs={{0,8},{8,16},{12,4},{16,24},{20,12},{28,20},{1,9},{9,17},{13,5},{1... | collective-permute-start | bytes 1105928 | tf_op jit(solution)/shard_map/ppermute | solution.py:485
  33.0 17.4 %collective-permute-start.6 = (bf16[2,12,48,128]{3,2,1,0:T(8,128)(2,1)S(1)}, bf16[2,12,48,128]{3,2,1,0:T(8,128)(2,1)S(1)}, u32[]{:S(2)}, u32[]{:S(2)}) collective-permute-start(bf16[2,12,48,128]{3,2,1,0:T(8,128)(2,1)S(1)} %collective-permute-done.4.refs_4_), channel_id=1, source_target_pairs={{0,8},{8,16},{12,4},{16,24},{20,12},{28,20},{1,9},{9,17},{13,5},{1... | collective-permute-start | bytes 884744 | tf_op jit(solution)/shard_map/ppermute | solution.py:488
  40.1 2.9 %copy-start.3 = (bf16[2,48,24,48]{3,2,1,0:T(8,128)(2,1)}, bf16[2,48,24,48]{3,2,1,0:T(8,128)(2,1)S(1)}, u32[]{:S(2)}) copy-start(bf16[2,48,24,48]{3,2,1,0:T(8,128)(2,1)S(1)} %get-tuple-element.42.weights) | copy-start | bytes 663556
  43.0 13.5 %collective-permute-start.14 = (bf16[4,10,48,128]{3,2,1,0:T(8,128)(2,1)S(1)}, bf16[4,10,48,128]{3,2,1,0:T(8,128)(2,1)}, u32[]{:S(2)}, u32[]{:S(2)}) collective-permute-start(bf16[4,10,48,128]{3,2,1,0:T(8,128)(2,1)S(1)} %filtered.3.refs_0_), channel_id=1, source_target_pairs={{0,2},{1,3},{2,0},{3,1},{4,6},{5,7},{6,4},{7,5},{8,10},{9,11},{10,... | collective-permute-start | bytes 1474568 | tf_op jit(solution)/shard_map/ppermute | solution.py:501
  44.6 3.7 %collective-permute-start.8 = (f32[24,128]{1,0:T(8,128)S(1)}, f32[24,128]{1,0:T(8,128)S(1)}, u32[]{:S(2)}, u32[]{:S(2)}) collective-permute-start(f32[24,128]{1,0:T(8,128)S(1)} %get-tuple-element.40), channel_id=1, source_target_pairs={{0,4},{4,0},{8,12},{12,8},{16,20},{20,16},{24,28},{28,24},{1,5},{5... | collective-permute-start | bytes 36872 | tf_op jit(solution)/shard_map/ppermute | solution.py:506
  44.6 18.2 %collective-permute-start.13 = (bf16[4,10,48,128]{3,2,1,0:T(8,128)(2,1)S(1)}, bf16[4,10,48,128]{3,2,1,0:T(8,128)(2,1)}, u32[]{:S(2)}, u32[]{:S(2)}) collective-permute-start(bf16[4,10,48,128]{3,2,1,0:T(8,128)(2,1)S(1)} %filtered.3.refs_0_), channel_id=1, source_target_pairs={{0,1},{1,0},{2,3},{3,2},{4,5},{5,4},{6,7},{7,6},{8,9},{9,8},{10,11... | collective-permute-start | bytes 1474568 | tf_op jit(solution)/shard_map/ppermute | solution.py:502
  48.3 7.1 %copy-start.8 = (s32[12,2]{0,1:T(2,128)S(1)}, s32[12,2]{0,1:T(2,128)}, u32[]{:S(2)}) copy-start(s32[12,2]{0,1:T(2,128)} %param.12) | copy-start | bytes 292
  48.3 11.8 %copy-start.7 = (f32[8]{0:T(128)S(1)}, f32[8]{0:T(128)}, u32[]{:S(2)}) copy-start(f32[8]{0:T(128)} %param.10) | copy-start | bytes 100
  48.3 7.1 %collective-permute-start.9 = (f32[24,128]{1,0:T(8,128)S(1)}, f32[24,128]{1,0:T(8,128)S(1)}, u32[]{:S(2)}, u32[]{:S(2)}) collective-permute-start(f32[24,128]{1,0:T(8,128)S(1)} %add.19), channel_id=1, source_target_pairs={{0,8},{4,12},{8,0},{12,4},{16,24},{20,28},{24,16},{28,20},{1,9},{5... | collective-permute-start | bytes 36872 | tf_op jit(solution)/shard_map/ppermute | solution.py:506
  54.8 7.5 %collective-permute-start.7 = (bf16[2,14,48,128]{3,2,1,0:T(8,128)(2,1)}, bf16[2,14,48,128]{3,2,1,0:T(8,128)(2,1)S(1)}, u32[]{:S(2)}, u32[]{:S(2)}) collective-permute-start(bf16[2,14,48,128]{3,2,1,0:T(8,128)(2,1)} %get-tuple-element.38.refs_0_), channel_id=1, source_target_pairs={{0,2},{1,3},{2,0},{3,1},{4,6},{5,7},{6,4},{7,5},{8,10},{9,11},{10,... | collective-permute-start | bytes 1032200 | tf_op jit(solution)/shard_map/ppermute | solution.py:511
  55.4 4.7 %collective-permute-start.10 = (f32[24,128]{1,0:T(8,128)S(1)}, f32[24,128]{1,0:T(8,128)S(1)}, u32[]{:S(2)}, u32[]{:S(2)}) collective-permute-start(f32[24,128]{1,0:T(8,128)S(1)} %add.20), channel_id=1, source_target_pairs={{0,16},{4,20},{8,24},{12,28},{16,0},{20,4},{24,8},{28,12},{1,17},{... | collective-permute-start | bytes 36872 | tf_op jit(solution)/shard_map/ppermute | solution.py:506
  56.5 6.9 %collective-permute-start.15 = (bf16[4,10,48,128]{3,2,1,0:T(8,128)(2,1)}, bf16[4,10,48,128]{3,2,1,0:T(8,128)(2,1)S(1)}, u32[]{:S(2)}, u32[]{:S(2)}) collective-permute-start(bf16[4,10,48,128]{3,2,1,0:T(8,128)(2,1)} %collective-permute-done.14.refs_2_), channel_id=1, source_target_pairs={{0,1},{1,0},{2,3},{3,2},{4,5},{5,4},{6,7},{7,6},{8,9},{9,8},{10,11... | collective-permute-start | bytes 1474568 | tf_op jit(solution)/shard_map/ppermute | solution.py:512
  60.2 5.6 %collective-permute-start.18 = (bf16[2,14,48,128]{3,2,1,0:T(8,128)(2,1)}, bf16[2,14,48,128]{3,2,1,0:T(8,128)(2,1)S(1)}, u32[]{:S(2)}, u32[]{:S(2)}) collective-permute-start(bf16[2,14,48,128]{3,2,1,0:T(8,128)(2,1)} %get-tuple-element.38.refs_0_), channel_id=1, source_target_pairs={{0,1},{1,0},{2,3},{3,2},{4,5},{5,4},{6,7},{7,6},{8,9},{9,8},{10,11... | collective-permute-start | bytes 1032200 | tf_op jit(solution)/shard_map/ppermute | solution.py:509
  62.3 3.5 %collective-permute-start.19 = (bf16[2,14,48,128]{3,2,1,0:T(8,128)(2,1)S(1)}, bf16[2,14,48,128]{3,2,1,0:T(8,128)(2,1)S(1)}, u32[]{:S(2)}, u32[]{:S(2)}) collective-permute-start(bf16[2,14,48,128]{3,2,1,0:T(8,128)(2,1)S(1)} %collective-permute-done.7.refs_2_), channel_id=1, source_target_pairs={{0,1},{1,0},{2,3},{3,2},{4,5},{5,4},{6,7},{7,6},{8,9},{9,8},{10,11... | collective-permute-start | bytes 1032200 | tf_op jit(solution)/shard_map/ppermute | solution.py:517
  62.3 10.5 %collective-permute-start.17 = (bf16[2,14,48,128]{3,2,1,0:T(8,128)(2,1)S(1)}, bf16[2,14,48,128]{3,2,1,0:T(8,128)(2,1)S(1)}, u32[]{:S(2)}, u32[]{:S(2)}) collective-permute-start(bf16[2,14,48,128]{3,2,1,0:T(8,128)(2,1)S(1)} %get-tuple-element.44.refs_0_), channel_id=1, source_target_pairs={{0,2},{1,3},{2,0},{3,1},{4,6},{5,7},{6,4},{7,5},{8,10},{9,11},{10,... | collective-permute-start | bytes 1032200 | tf_op jit(solution)/shard_map/ppermute | solution.py:515
  62.8 12.0 %collective-permute-start.11 = (bf16[16,128]{1,0:T(8,128)(2,1)S(1)}, bf16[16,128]{1,0:T(8,128)(2,1)S(1)}, u32[]{:S(2)}, u32[]{:S(2)}) collective-permute-start(bf16[16,128]{1,0:T(8,128)(2,1)S(1)} %coefficients.1.a), channel_id=1, source_target_pairs={{0,1},{1,0},{2,3},{3,2},{4,5},{5,4},{6,7},{7,6},{8,9},{9,8},{10,11... | collective-permute-start | bytes 12296 | tf_op jit(solution)/shard_map/ppermute | solution.py:520
  63.4 17.0 %collective-permute-start.16 = (bf16[2,14,48,128]{3,2,1,0:T(8,128)(2,1)S(1)}, bf16[2,14,48,128]{3,2,1,0:T(8,128)(2,1)S(1)}, u32[]{:S(2)}, u32[]{:S(2)}) collective-permute-start(bf16[2,14,48,128]{3,2,1,0:T(8,128)(2,1)S(1)} %get-tuple-element.44.refs_0_), channel_id=1, source_target_pairs={{0,1},{1,0},{2,3},{3,2},{4,5},{5,4},{6,7},{7,6},{8,9},{9,8},{10,11... | collective-permute-start | bytes 1032200 | tf_op jit(solution)/shard_map/ppermute | solution.py:510
  65.8 12.7 %copy-start.4 = (bf16[2,48,24,48]{3,2,1,0:T(8,128)(2,1)S(1)}, bf16[2,48,24,48]{3,2,1,0:T(8,128)(2,1)}, u32[]{:S(2)}) copy-start(bf16[2,48,24,48]{3,2,1,0:T(8,128)(2,1)} %copy-done.3) | copy-start | bytes 663556
  72.8 7.6 %collective-permute-start.20 = (bf16[2,14,48,128]{3,2,1,0:T(8,128)(2,1)S(1)}, bf16[2,14,48,128]{3,2,1,0:T(8,128)(2,1)S(1)}, u32[]{:S(2)}, u32[]{:S(2)}) collective-permute-start(bf16[2,14,48,128]{3,2,1,0:T(8,128)(2,1)S(1)} %collective-permute-done.17.refs_2_), channel_id=1, source_target_pairs={{0,1},{1,0},{2,3},{3,2},{4,5},{5,4},{6,7},{7,6},{8,9},{9,8},{10,11... | collective-permute-start | bytes 1032200 | tf_op jit(solution)/shard_map/ppermute | solution.py:527
  72.8 15.7 %collective-permute-start.22 = (bf16[2,14,48,128]{3,2,1,0:T(8,128)(2,1)S(1)}, bf16[2,14,48,128]{3,2,1,0:T(8,128)(2,1)S(1)}, u32[]{:S(2)}, u32[]{:S(2)}) collective-permute-start(bf16[2,14,48,128]{3,2,1,0:T(8,128)(2,1)S(1)} %rotated.4), channel_id=1, source_target_pairs={{0,4},{4,0},{8,12},{12,8},{16,20},{20,16},{24,28},{28,24},{1,5},{5... | collective-permute-start | bytes 1032200 | tf_op jit(solution)/shard_map/ppermute | solution.py:526
  74.0 14.5 %collective-permute-start.21 = (bf16[2,10,48,128]{3,2,1,0:T(8,128)(2,1)S(1)}, bf16[2,10,48,128]{3,2,1,0:T(8,128)(2,1)S(1)}, u32[]{:S(2)}, u32[]{:S(2)}) collective-permute-start(bf16[2,10,48,128]{3,2,1,0:T(8,128)(2,1)S(1)} %get-tuple-element.49), channel_id=1, source_target_pairs={{0,4},{4,0},{8,12},{12,8},{16,20},{20,16},{24,28},{28,24},{1,5},{5... | collective-permute-start | bytes 737288 | tf_op jit(solution)/shard_map/ppermute | solution.py:519
  74.8 3.7 %collective-permute-start.12 = (bf16[32,128]{1,0:T(8,128)(2,1)S(1)}, bf16[32,128]{1,0:T(8,128)(2,1)S(1)}, u32[]{:S(2)}, u32[]{:S(2)}) collective-permute-start(bf16[32,128]{1,0:T(8,128)(2,1)S(1)} %pad_maximum_fusion), channel_id=1, source_target_pairs={{0,2},{1,3},{2,0},{3,1},{4,6},{5,7},{6,4},{7,5},{8,10},{9,11},{10,... | collective-permute-start | bytes 24584 | tf_op jit(solution)/shard_map/ppermute | solution.py:521

commit v8 on v7

--- a/solution.py
+++ b/solution.py
@@ -37,7 +37,7 @@
     return jnp.where(linked, -0.125, 0.0)
 
 
-def prepare_kernel(early, psi, potential_far, to_x, to_x2, to_z, blocks, potential, sems):
+def prepare_kernel(early, psi, potential_far, beta, to_x, to_x2, to_z, blocks, potential, sems):
     x = lax.rem(lax.axis_index("space"), 2)
     half = psi.shape[1] // 2
     window = half + 2
@@ -52,13 +52,26 @@
             psi.at[:, pl.ds(mine, window)], to_z.at[:, pl.ds(0, window)], sems.at[1]
         ),
         pltpu.make_async_copy(
-            psi.at[:, pl.ds(theirs + early, window - early)], to_x2, sems.at[2]
+            psi.at[:, pl.ds(theirs + early, window - early)],
+            to_x2.at[:, pl.ds(0, window - early)],
+            sems.at[2],
         ),
     ]
     fetch = pltpu.make_async_copy(potential_far, potential, sems.at[5])
     fetch.start()
     for copy in copies:
         copy.start()
+    each = beta.shape[0] // blocks.shape[0]
+
+    def pack(i, carry):
+        for plane in range(blocks.shape[0]):
+            first, second = (beta[plane * each + i, k].astype(F32) for k in range(2))
+            to_x2[plane, window - early + i] = jnp.concatenate(
+                [first, gap, second, gap], axis=1
+            ).astype(BF16)
+        return carry
+
+    lax.fori_loop(0, each, pack, 0)
     fetch.wait()
     for plane in range(blocks.shape[0]):
         u = (potential[plane] - 1.0) * 0.25
@@ -74,7 +87,7 @@
         copy.wait()
 
 
-def prepared(psi, potential, early):
+def prepared(psi, potential, beta, early):
     planes, width_x, width_y, orbs = psi.shape
     window = width_x // 2 + 2
 
@@ -84,14 +97,19 @@
     local = pl.BlockSpec(memory_space=pltpu.VMEM)
     return pl.pallas_call(
         functools.partial(prepare_kernel, early),
-        out_shape=(out(early + 1), out(window - early), out(window + 1), out(1)),
-        in_specs=[pl.BlockSpec(memory_space=pltpu.MemorySpace.HBM)] * 2,
+        out_shape=(
+            out(early + 1),
+            out(window - early + beta.shape[0] // planes),
+            out(window + 1),
+            out(1),
+        ),
+        in_specs=[pl.BlockSpec(memory_space=pltpu.MemorySpace.HBM)] * 2 + [local],
         out_specs=(local,) * 4,
         scratch_shapes=[pltpu.VMEM(potential.shape, F32), pltpu.SemaphoreType.DMA((6,))],
         compiler_params=params(),
         cost_estimate=cost(4096, 4096),
         name="prepared",
-    )(*(pltpu.with_memory_space_constraint(a, pltpu.MemorySpace.HBM) for a in (psi, potential)))
+    )(*(pltpu.with_memory_space_constraint(a, pltpu.MemorySpace.HBM) for a in (psi, potential)), beta)
 
 
 def partial_kernel(count, atoms, own, beta, b_x, b_d, potential, gram, out, weights_out, table, acc):
@@ -107,6 +125,9 @@
     for k in range(2):
         plane = x if k == 0 else 1 - x
         outer, there = (b_d, beyond) if k == 0 else (b_x, side)
+        left = x == (1 if k == 0 else 0)
+        each = count // outer.shape[0]
+        begin = outer.shape[1] - each
         u = (potential[plane] - 1.0) * 0.25
 
         def fill(i, carry):
@@ -116,7 +137,9 @@
                 next_to = (jnp.abs(there - atoms[p]) <= 1).astype(F32)
                 b32 = beta[p, plane].astype(F32) * here
                 b = b32.astype(BF16)
-                sides = beta[p, 1 - plane].astype(F32) * here + outer[p].astype(F32) * next_to
+                both = outer[p // each, begin + lax.rem(p, each)].astype(F32)
+                other = jnp.where(left, both[:, :width], both[:, 64 : 64 + width])
+                sides = beta[p, 1 - plane].astype(F32) * here + other * next_to
                 whole = jnp.dot(b, tri, preferred_element_type=F32)
                 whole = whole + jnp.dot(tri, b, preferred_element_type=F32)
                 whole = whole + u * b32 - 0.125 * sides
@@ -256,7 +279,7 @@
         early = xrs[0].shape[1] - 1
         for target, pieces in ((xr, xrs), (zf, zfs)):
             target[:, 0:early] = pieces[0][:, 0:early]
-            target[:, early:] = pieces[1][...]
+            target[:, early:] = pieces[1][:, 0 : target.shape[1] - early]
         window = xr.shape[1] // 2
     else:
         xr, zf = xrs[0], zfs[0]
@@ -361,7 +384,7 @@
         pltpu.VMEM((6, 2, own.shape[1] // 2, 2 * width), F32),
     ]
     if parts > 1:
-        window = xrs[0].shape[1] - 1 + xrs[1].shape[1]
+        window = own.shape[1] // 2 + 2
         scratch += [pltpu.VMEM((planes, window, width, orbs), BF16)] * 2
     return pl.pallas_call(
         functools.partial(filter_kernel, slabs, start, parts, joint),
@@ -465,25 +488,20 @@
     swap = [(i, i ^ 1) for i in range(slabs)]
     own_way = within([(i, i + 2 if i % 2 else i - 2) for i in range(slabs)])
     other_way = within([(i, i - 2 if i % 2 else i + 2) for i in range(slabs)])
-    raster = within([(i, i + 1 if i % 2 else i - 1) for i in range(slabs)])
     groups = lax.axis_size("orb")
     across = [(i, i ^ 2) for i in range(groups)]
     beside = [(i, i ^ 1) for i in range(groups)]
     mine = (half - 2) * x
     theirs = (half - 2) * (1 - x)
 
-    to_x, to_x2, to_z, blocks = prepared(psi, potential, early)
+    to_x, to_x2, to_z, blocks = prepared(psi, potential, beta, early)
     xr1 = lax.ppermute(to_x, "space", swap)
     zo = lax.ppermute(to_z, "space", own_way)
-    far = lax.dynamic_index_in_dim(beta, x, 1, keepdims=False)
-    near = lax.dynamic_index_in_dim(beta, 1 - x, 1, keepdims=False)
     active = jnp.abs(place - atom_slab) <= 1
     beta_m = jnp.where(active[:, None, None, None], beta, jnp.zeros_like(beta))
     gram = jnp.einsum("pzxy,qzxy->pq", beta_m, beta_m, preferred_element_type=F32)
-    f_x = lax.ppermute(near, "space", swap)
-    f_d = lax.ppermute(far, "space", raster)
     zf1 = lax.ppermute(xr1, "space", other_way)
-    second, _, f_x, f_d = ordered(to_x2, xr1, f_x, f_d)
+    second, _ = ordered(to_x2, xr1)
     xr2 = lax.ppermute(second, "space", swap)
     zf2 = lax.ppermute(xr2, "space", other_way)
     strong = jnp.broadcast_to(strength[:, None], (count, orbs))
@@ -494,13 +512,14 @@
     rows_hot = rows_hot * (pattern[:, 1] == me).astype(BF16)[:, None]
     q = jnp.einsum("ki,kab->iab", rows_hot, q_tiles, preferred_element_type=F32).astype(BF16)
 
-    sums, weights = partials(count, atom_slab, psi, beta, f_x, f_d, potential, gram)
-    zf1, sums = ordered(zf1, sums)
+    zf1, _ = ordered(zf1, xr2)
     operands = (psi, blocks, zo)
     (block1,) = filtered(slabs, 0, rows1, True, operands, (xr1,), (zf1,))
     y1 = lax.ppermute(block1, "orb", across)
     c1 = lax.ppermute(block1, "orb", beside)
     give2, keep2 = filtered(slabs, rows1, rows2, False, operands, (xr1, xr2), (zf1, zf2))
+    xr2, _ = ordered(xr2, give2)
+    sums, weights = partials(count, atom_slab, psi, beta, xr2, zf2, potential, gram)
     step = 1
     while step < slabs:
         sums = sums + lax.ppermute(sums, "space", [(i, i ^ step) for i in range(slabs)])
@@ -513,17 +532,16 @@
     give1, keep1 = rotated((block1, c1, y1, yc1), q, 2)
     keep_y, yg = ordered(keep2, yg)
     yk = lax.ppermute(keep_y, "orb", across)
-    yg, coefs = ordered(yg, coefs)
     ycg = lax.ppermute(yg, "orb", beside)
-    ycg, give1 = ordered(ycg, give1)
+    ycg, _ = ordered(ycg, give1)
     got1 = lax.ppermute(give1, "space", swap)
     coefs_c = lax.ppermute(coefs, "orb", beside)
     coefs_y = lax.ppermute(jnp.concatenate([coefs, coefs_c], axis=0), "orb", across)
     coefs_yc, coefs_y = coefs_y[2 * count :], coefs_y[: 2 * count]
     term = nonlocal_term(psi.shape, (coefs, coefs_c, coefs_y, coefs_yc), q, weights)
     (give2,) = rotated((give2, cg, yg, ycg), q, 1)
-    yk, give2 = ordered(yk, give2)
     got2 = lax.ppermute(give2, "space", swap)
+    yk, _, _ = ordered(yk, give2, coefs)
     yck = lax.ppermute(yk, "orb", beside)
     (keep2,) = rotated((keep2, ck, yk, yck), q, 1)
     return assembled(term, [keep1, keep2], [got1, got2])

time: 90 us -> 78.6 us (0.87)
  waiting for transfers between devices: 32.2 us -> 23.3 us
  starting transfers between devices: 35.1 us -> 30.3 us
  local copies, waits for them, and re-layouts: 1.09 us -> 3.62 us
    ppermute x1, starting transfers between devices: 11.1 us -> 1.74 us  [shards(): xr2 = lax.ppermute(second, 'space', swap)]
    ppermute x1, waiting for transfers between devices: 7.43 us -> 0.01 us  [shards(): got1 = lax.ppermute(give1, 'space', swap)]
    ppermute x1, waiting for transfers between devices: 0.01 us -> 7.3 us  [shards(): xr1 = lax.ppermute(to_x, 'space', swap)]
    ppermute x3, waiting for transfers between devices: 7.23 us -> 1.75 us  [shards(): lax.ppermute(sums, 'space', [(i, i ^ step) for i in range(slabs)])]
    ppermute x2 -> x0, waiting for transfers between devices: 5.15 us -> none  [the longest x1 5.14 us: shards(): f_x = lax.ppermute(near, 'space', swap)]
    ppermute x3, starting transfers between devices: 3.22 us -> 7.58 us  [shards(): lax.ppermute(sums, 'space', [(i, i ^ step) for i in range(slabs)])]
    unnamed x18 -> x24, local copies, waits for them, and re-layouts: 0.04 us -> 3.53 us
    ppermute x2 -> x0, starting transfers between devices: 3.48 us -> none  [the longest x1 2.83 us: shards(): f_x = lax.ppermute(near, 'space', swap)]
  transfers between devices with their start and end apart: 23 -> 21, of which waited for: 8 -> 8; matrix products, arithmetic and copies ran while one was open for 2% -> 1% of each run, Pallas kernels for 19% -> 21%
where the time goes in v8:
time: 78.6 us; the launch traced here: 78.3 us
  starting transfers between devices  30.3 us (39%)
  waiting for transfers between devices  23.3 us (30%)
  Pallas kernels  20 us (25%)
  local copies, waits for them, and re-layouts  3.62 us (5%)
    ppermute x3, starting transfers between devices, shards(): lax.ppermute(sums, 'space', [(i, i ^ step) for i in range(slabs)])  7.58 us
    ppermute x1, waiting for transfers between devices, shards(): xr1 = lax.ppermute(to_x, 'space', swap)  7.3 us
    pallas_call x2, Pallas kernels, filtered(): pl.pallas_call(functools.partial(filter_kernel, slabs, start, parts, join...  7.23 us
    ppermute x1, waiting for transfers between devices, shards(): xr2 = lax.ppermute(second, 'space', swap)  5.27 us
    pallas_call x3, Pallas kernels, rotated(): pl.pallas_call(functools.partial(rotate_kernel, group), out_shape=(out,)...  4.19 us
    unnamed x24, local copies, waits for them, and re-layouts  3.53 us
    ppermute x1, starting transfers between devices, shards(): zf1 = lax.ppermute(xr1, 'space', other_way)  3.49 us
    ppermute x1, starting transfers between devices, shards(): zf2 = lax.ppermute(xr2, 'space', other_way)  3.42 us
  transfers between devices with their start and end apart: 21, of which 8 were waited for; matrix products, arithmetic and copies ran while one was open for 1% of the time, Pallas kernels for 21%

profile of v8, /device:TPU:0, one launch (start us, length us, event | category | flops | bytes accessed | tf_op | source)
XLA Modules:
  0.0 78.3 jit_solution(1264708284092050446)
XLA Ops:
  0.0 0.0 copy-start
  0.0 1.0 %copy-done.2 = bf16[8,2,48,48]{3,2,1,0:T(8,128)(2,1)S(1)} copy-done((bf16[8,2,48,48]{3,2,1,0:T(8,128)(2,1)S(1)}, bf16[8,2,48,48]{3,2,1,0:T(8,128)(2,1)}, u32[]{:S(2)}) %copy-start.2) | copy-done | bytes 73752
  1.1 2.3 %prepared.1 = (bf16[2,15,48,128]{3,2,1,0:T(8,128)(2,1)S(1)}, bf16[2,16,48,128]{3,2,1,0:T(8,128)(2,1)}, bf16[2,27,48,128]{3,2,1,0:T(8,128)(2,1)}, bf16[2,1,48,128]{3,2,1,0:T(8,128)(2,1)S(1)}) custom-call(bf16[2,48,48,128]{3,2,1,0:T(8,128)(2,1)} %refs_0_.3, f32[2,48,48]{2,1,0:T(8,128)} %potential.1, bf16[8,2,48,48]{3,2,1,0:T(8,128)(2,1)S(1)} %copy-done.2), custom_call_target="tpu_custom_call" | custom-call | flops 256 | bytes 256 | tf_op jit(solution)/shard_map/prepared/pallas_call | solution.py:98
  3.4 3.0 %collective-permute-start = (bf16[2,15,48,128]{3,2,1,0:T(8,128)(2,1)S(1)}, bf16[2,15,48,128]{3,2,1,0:T(8,128)(2,1)S(1)}, u32[]{:S(2)}, u32[]{:S(2)}) collective-permute-start(bf16[2,15,48,128]{3,2,1,0:T(8,128)(2,1)S(1)} %get-tuple-element.23), channel_id=1, source_target_pairs={{0,4},{4,0},{8,12},{12,8},{16,20},{20,16},{24,28},{28,24},{1,5},{5... | collective-permute-start | bytes 1105928 | tf_op jit(solution)/shard_map/ppermute | solution.py:498
  6.4 1.3 %collective-permute-start.2 = (bf16[2,27,48,128]{3,2,1,0:T(8,128)(2,1)}, bf16[2,27,48,128]{3,2,1,0:T(8,128)(2,1)S(1)}, u32[]{:S(2)}, u32[]{:S(2)}) collective-permute-start(bf16[2,27,48,128]{3,2,1,0:T(8,128)(2,1)} %get-tuple-element.26), channel_id=1, source_target_pairs={{4,12},{8,0},{12,20},{16,8},{20,28},{24,16},{5,13},{9,1},{13,21},{... | collective-permute-start | bytes 1990664 | tf_op jit(solution)/shard_map/ppermute | solution.py:499
  7.7 7.3 %collective-permute-done.refs_3_ = bf16[2,15,48,128]{3,2,1,0:T(8,128)(2,1)S(1)} collective-permute-done((bf16[2,15,48,128]{3,2,1,0:T(8,128)(2,1)S(1)}, bf16[2,15,48,128]{3,2,1,0:T(8,128)(2,1)S(1)}, u32[]{:S(2)}, u32[]{:S(2)}) %collective-permute-start) | collective-permute-done | bytes 368672 | tf_op jit(solution)/shard_map/ppermute | solution.py:498
  15.0 1.7 %collective-permute-start.1 = (bf16[2,16,48,128]{3,2,1,0:T(8,128)(2,1)}, bf16[2,16,48,128]{3,2,1,0:T(8,128)(2,1)S(1)}, u32[]{:S(2)}, u32[]{:S(2)}) collective-permute-start(bf16[2,16,48,128]{3,2,1,0:T(8,128)(2,1)} %get-tuple-element.24), channel_id=1, source_target_pairs={{0,4},{4,0},{8,12},{12,8},{16,20},{20,16},{24,28},{28,24},{1,5},{5... | collective-permute-start | bytes 1179656 | tf_op jit(solution)/shard_map/ppermute | solution.py:505
  16.7 3.5 %collective-permute-start.3 = (bf16[2,15,48,128]{3,2,1,0:T(8,128)(2,1)S(1)}, bf16[2,15,48,128]{3,2,1,0:T(8,128)(2,1)S(1)}, u32[]{:S(2)}, u32[]{:S(2)}) collective-permute-start(bf16[2,15,48,128]{3,2,1,0:T(8,128)(2,1)S(1)} %collective-permute-done.refs_3_), channel_id=1, source_target_pairs={{0,8},{8,16},{12,4},{16,24},{20,12},{28,20},{1,9},{9,17},{13,5},{1... | collective-permute-start | bytes 1105928 | tf_op jit(solution)/shard_map/ppermute | solution.py:503
  20.2 5.3 %collective-permute-done.1.refs_4_.b_x = bf16[2,16,48,128]{3,2,1,0:T(8,128)(2,1)S(1)} collective-permute-done((bf16[2,16,48,128]{3,2,1,0:T(8,128)(2,1)}, bf16[2,16,48,128]{3,2,1,0:T(8,128)(2,1)S(1)}, u32[]{:S(2)}, u32[]{:S(2)}) %collective-permute-start.1) | collective-permute-done | bytes 393248 | tf_op jit(solution)/shard_map/ppermute | solution.py:505
  25.5 3.4 %collective-permute-start.4 = (bf16[2,16,48,128]{3,2,1,0:T(8,128)(2,1)S(1)}, bf16[2,16,48,128]{3,2,1,0:T(8,128)(2,1)S(1)}, u32[]{:S(2)}, u32[]{:S(2)}) collective-permute-start(bf16[2,16,48,128]{3,2,1,0:T(8,128)(2,1)S(1)} %collective-permute-done.1.refs_4_.b_x), channel_id=1, source_target_pairs={{0,8},{8,16},{12,4},{16,24},{20,12},{28,20},{1,9},{9,17},{13,5},{1... | collective-permute-start | bytes 1179656 | tf_op jit(solution)/shard_map/ppermute | solution.py:506
  28.9 0.0 collective-permute-done.3.refs_5_.refs_4_
  29.0 0.7 copy-done.4
  29.7 0.0 collective-permute-done.2.refs_2_
  29.7 1.0 %copy-done.5 = bf16[2,15,48,128]{3,2,1,0:T(8,128)(2,1)S(1)} copy-done((bf16[2,15,48,128]{3,2,1,0:T(8,128)(2,1)S(1)}, bf16[2,15,48,128]{3,2,1,0:T(8,128)(2,1)}, u32[]{:S(2)}) %copy-start.5) | copy-done | bytes 368664
  30.7 2.8 %filtered.3.refs_0_ = bf16[4,10,48,128]{3,2,1,0:T(8,128)(2,1)S(1)} custom-call(bf16[2,48,48,128]{3,2,1,0:T(8,128)(2,1)S(1)} %copy-done.1, bf16[2,1,48,128]{3,2,1,0:T(8,128)(2,1)S(1)} %get-tuple-element.25.refs_1_, bf16[2,27,48,128]{3,2,1,0:T(8,128)(2,1)S(1)} %collective-permute-done.2.refs_2_, bf16[2,15,48,128]{3,2,1,0:T(8,128)(2,1)S(1)} %collective-permute-done.refs_3_, ...), custom_call_target="tpu_custom_call" | custom-call | flops 2457600 | bytes 15360000 | tf_op jit(solution)/shard_map/filtered/pallas_call | solution.py:389
  33.5 1.6 %collective-permute-start.11 = (bf16[4,10,48,128]{3,2,1,0:T(8,128)(2,1)S(1)}, bf16[4,10,48,128]{3,2,1,0:T(8,128)(2,1)}, u32[]{:S(2)}, u32[]{:S(2)}) collective-permute-start(bf16[4,10,48,128]{3,2,1,0:T(8,128)(2,1)S(1)} %filtered.3.refs_0_), channel_id=1, source_target_pairs={{0,2},{1,3},{2,0},{3,1},{4,6},{5,7},{6,4},{7,5},{8,10},{9,11},{10,... | collective-permute-start | bytes 1474568 | tf_op jit(solution)/shard_map/ppermute | solution.py:518
  35.1 0.1 broadcast_select_fusion
  35.2 0.3 convolution_bitcast_fusion.gram
  35.5 0.0 collective-permute-done.4.refs_6_.b_d
  35.5 4.4 %filtered.2 = (bf16[2,14,48,128]{3,2,1,0:T(8,128)(2,1)}, bf16[2,14,48,128]{3,2,1,0:T(8,128)(2,1)S(1)}) custom-call(bf16[2,48,48,128]{3,2,1,0:T(8,128)(2,1)S(1)} %copy-done.1, bf16[2,1,48,128]{3,2,1,0:T(8,128)(2,1)S(1)} %get-tuple-element.25.refs_1_, bf16[2,27,48,128]{3,2,1,0:T(8,128)(2,1)S(1)} %collective-permute-done.2.refs_2_, ...), custom_call_target="tpu_custom_call" | custom-call | flops 3440640 | bytes 21504000 | tf_op jit(solution)/shard_map/filtered/pallas_call | solution.py:389
  39.9 0.7 copy-done.6
  40.7 3.0 %partials.1 = (f32[24,128]{1,0:T(8,128)S(1)}, bf16[2,48,24,48]{3,2,1,0:T(8,128)(2,1)S(1)}) custom-call(s32[8]{0:T(128)S(1)} %copy-done.9, bf16[2,48,48,128]{3,2,1,0:T(8,128)(2,1)S(1)} %copy-done.1, bf16[8,2,48,48]{3,2,1,0:T(8,128)(2,1)S(1)} %copy-done.3, bf16[2,16,48,128]{3,2,1,0:T(8,128)(2,1)S(1)} %collective-permute-done.1.refs_4_.b_x, ...), custom_call_target="tpu_custom_call" | custom-call | flops 256 | bytes 256 | tf_op jit(solution)/shard_map/partials/pallas_call | solution.py:172
  43.7 2.4 %collective-permute-start.5 = (f32[24,128]{1,0:T(8,128)S(1)}, f32[24,128]{1,0:T(8,128)S(1)}, u32[]{:S(2)}, u32[]{:S(2)}) collective-permute-start(f32[24,128]{1,0:T(8,128)S(1)} %get-tuple-element.30), channel_id=1, source_target_pairs={{0,4},{4,0},{8,12},{12,8},{16,20},{20,16},{24,28},{28,24},{1,5},{5... | collective-permute-start | bytes 36872 | tf_op jit(solution)/shard_map/ppermute | solution.py:525
  46.1 0.0 collective-permute-start.10
  46.1 1.6 %collective-permute-start.14 = (bf16[2,14,48,128]{3,2,1,0:T(8,128)(2,1)}, bf16[2,14,48,128]{3,2,1,0:T(8,128)(2,1)S(1)}, u32[]{:S(2)}, u32[]{:S(2)}) collective-permute-start(bf16[2,14,48,128]{3,2,1,0:T(8,128)(2,1)} %get-tuple-element.28.refs_0_), channel_id=1, source_target_pairs={{0,2},{1,3},{2,0},{3,1},{4,6},{5,7},{6,4},{7,5},{8,10},{9,11},{10,... | collective-permute-start | bytes 1032200 | tf_op jit(solution)/shard_map/ppermute | solution.py:530
  47.7 0.1 collective-permute-done.5
  47.8 2.1 %collective-permute-start.6 = (f32[24,128]{1,0:T(8,128)S(1)}, f32[24,128]{1,0:T(8,128)S(1)}, u32[]{:S(2)}, u32[]{:S(2)}) collective-permute-start(f32[24,128]{1,0:T(8,128)S(1)} %add.9), channel_id=1, source_target_pairs={{0,8},{4,12},{8,0},{12,4},{16,24},{20,28},{24,16},{28,20},{1,9},{5... | collective-permute-start | bytes 36872 | tf_op jit(solution)/shard_map/ppermute | solution.py:525
  49.9 0.0 copy-done.11
  50.0 1.7 %collective-permute-done.6 = f32[24,128]{1,0:T(8,128)S(1)} collective-permute-done((f32[24,128]{1,0:T(8,128)S(1)}, f32[24,128]{1,0:T(8,128)S(1)}, u32[]{:S(2)}, u32[]{:S(2)}) %collective-permute-start.6) | collective-permute-done | bytes 12320 | tf_op jit(solution)/shard_map/ppermute | solution.py:525
  51.6 3.0 %collective-permute-start.7 = (f32[24,128]{1,0:T(8,128)S(1)}, f32[24,128]{1,0:T(8,128)S(1)}, u32[]{:S(2)}, u32[]{:S(2)}) collective-permute-start(f32[24,128]{1,0:T(8,128)S(1)} %add.10), channel_id=1, source_target_pairs={{0,16},{4,20},{8,24},{12,28},{16,0},{20,4},{24,8},{28,12},{1,17},{... | collective-permute-start | bytes 36872 | tf_op jit(solution)/shard_map/ppermute | solution.py:525
  54.7 0.0 collective-permute-done.11.refs_2_
  54.7 0.0 collective-permute-start.12
  54.7 0.5 collective-permute-start.16
  55.2 1.6 %collective-permute-done.14.refs_2_ = bf16[2,14,48,128]{3,2,1,0:T(8,128)(2,1)S(1)} collective-permute-done((bf16[2,14,48,128]{3,2,1,0:T(8,128)(2,1)}, bf16[2,14,48,128]{3,2,1,0:T(8,128)(2,1)S(1)}, u32[]{:S(2)}, u32[]{:S(2)}) %collective-permute-start.14) | collective-permute-done | bytes 344096 | tf_op jit(solution)/shard_map/ppermute | solution.py:530
  56.8 0.0 collective-permute-start.17
  56.8 0.0 collective-permute-done.7
  56.8 0.0 copy-done.7
  56.8 1.7 %collective-permute-start.15 = (bf16[2,14,48,128]{3,2,1,0:T(8,128)(2,1)S(1)}, bf16[2,14,48,128]{3,2,1,0:T(8,128)(2,1)S(1)}, u32[]{:S(2)}, u32[]{:S(2)}) collective-permute-start(bf16[2,14,48,128]{3,2,1,0:T(8,128)(2,1)S(1)} %copy-done.7), channel_id=1, source_target_pairs={{0,2},{1,3},{2,0},{3,1},{4,6},{5,7},{6,4},{7,5},{8,10},{9,11},{10,... | collective-permute-start | bytes 1032200 | tf_op jit(solution)/shard_map/ppermute | solution.py:534
  58.5 0.1 broadcast_in_dim.22.strength
  58.6 0.1 coefficients.1.a
  58.7 0.0 collective-permute-done.10.refs_1_
  58.7 0.2 collective-permute-start.8
  58.9 0.0 copy-done
  58.9 0.3 fusion
  59.3 0.0 collective-permute-done.12.refs_3_
  59.3 0.4 collective-permute-start.13
  59.7 1.8 %rotated.3 = (bf16[2,10,48,128]{3,2,1,0:T(8,128)(2,1)S(1)}, bf16[2,10,48,128]{3,2,1,0:T(8,128)(2,1)S(1)}) custom-call(bf16[4,10,48,128]{3,2,1,0:T(8,128)(2,1)S(1)} %filtered.3.refs_0_, bf16[4,10,48,128]{3,2,1,0:T(8,128)(2,1)S(1)} %collective-permute-done.10.refs_1_, bf16[4,10,48,128]{3,2,1,0:T(8,128)(2,1)} %collective-permute-done.11.refs_2_, ...), custom_call_target="tpu_custom_call" | custom-call | flops 15728640 | bytes 153600 | tf_op jit(solution)/shard_map/rotated/pallas_call | solution.py:433
  61.6 0.0 collective-permute-done.17.refs_3_
  61.6 1.3 %collective-permute-start.19 = (bf16[2,10,48,128]{3,2,1,0:T(8,128)(2,1)S(1)}, bf16[2,10,48,128]{3,2,1,0:T(8,128)(2,1)S(1)}, u32[]{:S(2)}, u32[]{:S(2)}) collective-permute-start(bf16[2,10,48,128]{3,2,1,0:T(8,128)(2,1)S(1)} %get-tuple-element.36), channel_id=1, source_target_pairs={{0,4},{4,0},{8,12},{12,8},{16,20},{20,16},{24,28},{28,24},{1,5},{5... | collective-permute-start | bytes 737288 | tf_op jit(solution)/shard_map/ppermute | solution.py:537
  62.9 0.0 collective-permute-done.16.refs_1_
  62.9 1.7 %rotated.4 = bf16[2,14,48,128]{3,2,1,0:T(8,128)(2,1)S(1)} custom-call(bf16[2,14,48,128]{3,2,1,0:T(8,128)(2,1)} %get-tuple-element.28.refs_0_, bf16[2,14,48,128]{3,2,1,0:T(8,128)(2,1)S(1)} %collective-permute-done.16.refs_1_, bf16[2,14,48,128]{3,2,1,0:T(8,128)(2,1)S(1)} %collective-permute-done.14.refs_2_, ...), custom_call_target="tpu_custom_call" | custom-call | flops 11010048 | bytes 107520 | tf_op jit(solution)/shard_map/rotated/pallas_call | solution.py:433
  64.6 0.9 %collective-permute-start.20 = (bf16[2,14,48,128]{3,2,1,0:T(8,128)(2,1)S(1)}, bf16[2,14,48,128]{3,2,1,0:T(8,128)(2,1)S(1)}, u32[]{:S(2)}, u32[]{:S(2)}) collective-permute-start(bf16[2,14,48,128]{3,2,1,0:T(8,128)(2,1)S(1)} %rotated.4), channel_id=1, source_target_pairs={{0,4},{4,0},{8,12},{12,8},{16,20},{20,16},{24,28},{28,24},{1,5},{5... | collective-permute-start | bytes 1032200 | tf_op jit(solution)/shard_map/ppermute | solution.py:543
  65.4 1.9 %collective-permute-done.15.refs_2_ = bf16[2,14,48,128]{3,2,1,0:T(8,128)(2,1)S(1)} collective-permute-done((bf16[2,14,48,128]{3,2,1,0:T(8,128)(2,1)S(1)}, bf16[2,14,48,128]{3,2,1,0:T(8,128)(2,1)S(1)}, u32[]{:S(2)}, u32[]{:S(2)}) %collective-permute-start.15) | collective-permute-done | bytes 344096 | tf_op jit(solution)/shard_map/ppermute | solution.py:534
  67.3 0.0 collective-permute-start.18
  67.3 0.0 collective-permute-done.8.b
  67.3 1.7 %collective-permute-start.9 = (bf16[32,128]{1,0:T(8,128)(2,1)S(1)}, bf16[32,128]{1,0:T(8,128)(2,1)S(1)}, u32[]{:S(2)}, u32[]{:S(2)}) collective-permute-start(bf16[32,128]{1,0:T(8,128)(2,1)S(1)} %pad_maximum_fusion), channel_id=1, source_target_pairs={{0,2},{1,3},{2,0},{3,1},{4,6},{5,7},{6,4},{7,5},{8,10},{9,11},{10,... | collective-permute-start | bytes 24584 | tf_op jit(solution)/shard_map/ppermute | solution.py:539
  69.0 2.1 %collective-permute-done.9 = bf16[32,128]{1,0:T(8,128)(2,1)S(1)} collective-permute-done((bf16[32,128]{1,0:T(8,128)(2,1)S(1)}, bf16[32,128]{1,0:T(8,128)(2,1)S(1)}, u32[]{:S(2)}, u32[]{:S(2)}) %collective-permute-start.9) | collective-permute-done | bytes 8224 | tf_op jit(solution)/shard_map/ppermute | solution.py:539
  71.0 1.9 %nonlocal.1.term = f32[2,48,48,128]{3,2,1,0:T(8,128)S(1)} custom-call(bf16[16,128]{1,0:T(8,128)(2,1)S(1)} %coefficients.1.a, bf16[16,128]{1,0:T(8,128)(2,1)S(1)} %collective-permute-done.8.b, bf16[16,128]{1,0:T(8,128)(2,1)S(1)} %get-tuple-element.40.c, bf16[16,128]{1,0:T(8,128)(2,1)S(1)} %get-tuple-element.39.d, bf16[4,128,128]{2,1,0:T(8,128)(2,1)S(1)} %copy.18.q.refs_4_, ...), custom_call_target="tpu_custom_call" | custom-call | flops 256 | bytes 256 | tf_op jit(solution)/shard_map/nonlocal/pallas_call | solution.py:247
  72.9 0.0 collective-permute-done.13.refs_1_
  72.9 0.0 collective-permute-done.18.refs_3_
  73.0 0.7 rotated.5.refs_1_
  73.6 0.0 collective-permute-done.19.refs_2_
  73.7 3.4 %collective-permute-done.20.refs_3_ = bf16[2,14,48,128]{3,2,1,0:T(8,128)(2,1)S(1)} collective-permute-done((bf16[2,14,48,128]{3,2,1,0:T(8,128)(2,1)S(1)}, bf16[2,14,48,128]{3,2,1,0:T(8,128)(2,1)S(1)}, u32[]{:S(2)}, u32[]{:S(2)}) %collective-permute-start.20) | collective-permute-done | bytes 344096 | tf_op jit(solution)/shard_map/ppermute | solution.py:543
  77.0 1.2 %assembled.1 = bf16[2,48,48,128]{3,2,1,0:T(8,128)(2,1)} custom-call(f32[2,48,48,128]{3,2,1,0:T(8,128)S(1)} %nonlocal.1.term, bf16[2,10,48,128]{3,2,1,0:T(8,128)(2,1)S(1)} %get-tuple-element.32.refs_0_, bf16[2,14,48,128]{3,2,1,0:T(8,128)(2,1)S(1)} %rotated.5.refs_1_, bf16[2,10,48,128]{3,2,1,0:T(8,128)(2,1)S(1)} %collective-permute-done.19.refs_2_, ...), custom_call_target="tpu_custom_call" | custom-call | flops 256 | bytes 256 | tf_op jit(solution)/shard_map/assembled/pallas_call | solution.py:458
  (26 shorter events, 0.1 us)
Async XLA Ops:
  0.0 58.9 %copy-start = (bf16[12,128,128]{2,1,0:T(8,128)(2,1)S(1)}, bf16[12,128,128]{2,1,0:T(8,128)(2,1)}, u32[]{:S(2)}) copy-start(bf16[12,128,128]{2,1,0:T(8,128)(2,1)} %param.13) | copy-start | bytes 1179652
  0.0 29.7 %copy-start.1 = (bf16[2,48,48,128]{3,2,1,0:T(8,128)(2,1)S(1)}, bf16[2,48,48,128]{3,2,1,0:T(8,128)(2,1)}, u32[]{:S(2)}) copy-start(bf16[2,48,48,128]{3,2,1,0:T(8,128)(2,1)} %refs_0_.3) | copy-start | bytes 3538948
  0.0 1.0 %copy-start.2 = (bf16[8,2,48,48]{3,2,1,0:T(8,128)(2,1)S(1)}, bf16[8,2,48,48]{3,2,1,0:T(8,128)(2,1)}, u32[]{:S(2)}) copy-start(bf16[8,2,48,48]{3,2,1,0:T(8,128)(2,1)} %beta.3) | copy-start | bytes 221188
  1.1 27.9 %copy-start.9 = (s32[8]{0:T(128)S(1)}, s32[8]{0:T(128)}, u32[]{:S(2)}) copy-start(s32[8]{0:T(128)} %atoms.1) | copy-start | bytes 100
  3.4 11.6 %collective-permute-start = (bf16[2,15,48,128]{3,2,1,0:T(8,128)(2,1)S(1)}, bf16[2,15,48,128]{3,2,1,0:T(8,128)(2,1)S(1)}, u32[]{:S(2)}, u32[]{:S(2)}) collective-permute-start(bf16[2,15,48,128]{3,2,1,0:T(8,128)(2,1)S(1)} %get-tuple-element.23), channel_id=1, source_target_pairs={{0,4},{4,0},{8,12},{12,8},{16,20},{20,16},{24,28},{28,24},{1,5},{5... | collective-permute-start | bytes 1105928 | tf_op jit(solution)/shard_map/ppermute | solution.py:498
  6.4 23.3 %collective-permute-start.2 = (bf16[2,27,48,128]{3,2,1,0:T(8,128)(2,1)}, bf16[2,27,48,128]{3,2,1,0:T(8,128)(2,1)S(1)}, u32[]{:S(2)}, u32[]{:S(2)}) collective-permute-start(bf16[2,27,48,128]{3,2,1,0:T(8,128)(2,1)} %get-tuple-element.26), channel_id=1, source_target_pairs={{4,12},{8,0},{12,20},{16,8},{20,28},{24,16},{5,13},{9,1},{13,21},{... | collective-permute-start | bytes 1990664 | tf_op jit(solution)/shard_map/ppermute | solution.py:499
  15.0 10.5 %collective-permute-start.1 = (bf16[2,16,48,128]{3,2,1,0:T(8,128)(2,1)}, bf16[2,16,48,128]{3,2,1,0:T(8,128)(2,1)S(1)}, u32[]{:S(2)}, u32[]{:S(2)}) collective-permute-start(bf16[2,16,48,128]{3,2,1,0:T(8,128)(2,1)} %get-tuple-element.24), channel_id=1, source_target_pairs={{0,4},{4,0},{8,12},{12,8},{16,20},{20,16},{24,28},{28,24},{1,5},{5... | collective-permute-start | bytes 1179656 | tf_op jit(solution)/shard_map/ppermute | solution.py:505
  16.7 12.2 %collective-permute-start.3 = (bf16[2,15,48,128]{3,2,1,0:T(8,128)(2,1)S(1)}, bf16[2,15,48,128]{3,2,1,0:T(8,128)(2,1)S(1)}, u32[]{:S(2)}, u32[]{:S(2)}) collective-permute-start(bf16[2,15,48,128]{3,2,1,0:T(8,128)(2,1)S(1)} %collective-permute-done.refs_3_), channel_id=1, source_target_pairs={{0,8},{8,16},{12,4},{16,24},{20,12},{28,20},{1,9},{9,17},{13,5},{1... | collective-permute-start | bytes 1105928 | tf_op jit(solution)/shard_map/ppermute | solution.py:503
  25.5 10.0 %collective-permute-start.4 = (bf16[2,16,48,128]{3,2,1,0:T(8,128)(2,1)S(1)}, bf16[2,16,48,128]{3,2,1,0:T(8,128)(2,1)S(1)}, u32[]{:S(2)}, u32[]{:S(2)}) collective-permute-start(bf16[2,16,48,128]{3,2,1,0:T(8,128)(2,1)S(1)} %collective-permute-done.1.refs_4_.b_x), channel_id=1, source_target_pairs={{0,8},{8,16},{12,4},{16,24},{20,12},{28,20},{1,9},{9,17},{13,5},{1... | collective-permute-start | bytes 1179656 | tf_op jit(solution)/shard_map/ppermute | solution.py:506
  29.0 0.7 copy-start.4
  29.7 1.0 %copy-start.5 = (bf16[2,15,48,128]{3,2,1,0:T(8,128)(2,1)S(1)}, bf16[2,15,48,128]{3,2,1,0:T(8,128)(2,1)}, u32[]{:S(2)}) copy-start(bf16[2,15,48,128]{3,2,1,0:T(8,128)(2,1)} %copy-done.4) | copy-start | bytes 1105924
  30.7 4.4 %copy-start.3 = (bf16[8,2,48,48]{3,2,1,0:T(8,128)(2,1)S(1)}, bf16[8,2,48,48]{3,2,1,0:T(8,128)(2,1)}, u32[]{:S(2)}) copy-start(bf16[8,2,48,48]{3,2,1,0:T(8,128)(2,1)} %beta.3) | copy-start | bytes 221188
  33.5 21.2 %collective-permute-start.11 = (bf16[4,10,48,128]{3,2,1,0:T(8,128)(2,1)S(1)}, bf16[4,10,48,128]{3,2,1,0:T(8,128)(2,1)}, u32[]{:S(2)}, u32[]{:S(2)}) collective-permute-start(bf16[4,10,48,128]{3,2,1,0:T(8,128)(2,1)S(1)} %filtered.3.refs_0_), channel_id=1, source_target_pairs={{0,2},{1,3},{2,0},{3,1},{4,6},{5,7},{6,4},{7,5},{8,10},{9,11},{10,... | collective-permute-start | bytes 1474568 | tf_op jit(solution)/shard_map/ppermute | solution.py:518
  35.5 5.2 %copy-start.8 = (f32[2,48,48]{2,1,0:T(8,128)S(1)}, f32[2,48,48]{2,1,0:T(8,128)}, u32[]{:S(2)}) copy-start(f32[2,48,48]{2,1,0:T(8,128)} %potential.1) | copy-start | bytes 55300
  39.9 0.7 copy-start.6
  40.6 9.3 %copy-start.11 = (s32[12,2]{0,1:T(2,128)S(1)}, s32[12,2]{0,1:T(2,128)}, u32[]{:S(2)}) copy-start(s32[12,2]{0,1:T(2,128)} %param.12) | copy-start | bytes 292
  40.6 17.8 %copy-start.10 = (f32[8]{0:T(128)S(1)}, f32[8]{0:T(128)}, u32[]{:S(2)}) copy-start(f32[8]{0:T(128)} %param.10) | copy-start | bytes 100
  40.7 16.2 %copy-start.7 = (bf16[2,14,48,128]{3,2,1,0:T(8,128)(2,1)S(1)}, bf16[2,14,48,128]{3,2,1,0:T(8,128)(2,1)}, u32[]{:S(2)}) copy-start(bf16[2,14,48,128]{3,2,1,0:T(8,128)(2,1)} %copy-done.6) | copy-start | bytes 1032196
  43.7 4.1 %collective-permute-start.5 = (f32[24,128]{1,0:T(8,128)S(1)}, f32[24,128]{1,0:T(8,128)S(1)}, u32[]{:S(2)}, u32[]{:S(2)}) collective-permute-start(f32[24,128]{1,0:T(8,128)S(1)} %get-tuple-element.30), channel_id=1, source_target_pairs={{0,4},{4,0},{8,12},{12,8},{16,20},{20,16},{24,28},{28,24},{1,5},{5... | collective-permute-start | bytes 36872 | tf_op jit(solution)/shard_map/ppermute | solution.py:525
  46.1 12.6 %collective-permute-start.10 = (bf16[4,10,48,128]{3,2,1,0:T(8,128)(2,1)S(1)}, bf16[4,10,48,128]{3,2,1,0:T(8,128)(2,1)S(1)}, u32[]{:S(2)}, u32[]{:S(2)}) collective-permute-start(bf16[4,10,48,128]{3,2,1,0:T(8,128)(2,1)S(1)} %filtered.3.refs_0_), channel_id=1, source_target_pairs={{0,1},{1,0},{2,3},{3,2},{4,5},{5,4},{6,7},{7,6},{8,9},{9,8},{10,11... | collective-permute-start | bytes 1474568 | tf_op jit(solution)/shard_map/ppermute | solution.py:519
  46.1 10.7 %collective-permute-start.14 = (bf16[2,14,48,128]{3,2,1,0:T(8,128)(2,1)}, bf16[2,14,48,128]{3,2,1,0:T(8,128)(2,1)S(1)}, u32[]{:S(2)}, u32[]{:S(2)}) collective-permute-start(bf16[2,14,48,128]{3,2,1,0:T(8,128)(2,1)} %get-tuple-element.28.refs_0_), channel_id=1, source_target_pairs={{0,2},{1,3},{2,0},{3,1},{4,6},{5,7},{6,4},{7,5},{8,10},{9,11},{10,... | collective-permute-start | bytes 1032200 | tf_op jit(solution)/shard_map/ppermute | solution.py:530
  47.8 3.8 %collective-permute-start.6 = (f32[24,128]{1,0:T(8,128)S(1)}, f32[24,128]{1,0:T(8,128)S(1)}, u32[]{:S(2)}, u32[]{:S(2)}) collective-permute-start(f32[24,128]{1,0:T(8,128)S(1)} %add.9), channel_id=1, source_target_pairs={{0,8},{4,12},{8,0},{12,4},{16,24},{20,28},{24,16},{28,20},{1,9},{5... | collective-permute-start | bytes 36872 | tf_op jit(solution)/shard_map/ppermute | solution.py:525
  51.6 5.2 %collective-permute-start.7 = (f32[24,128]{1,0:T(8,128)S(1)}, f32[24,128]{1,0:T(8,128)S(1)}, u32[]{:S(2)}, u32[]{:S(2)}) collective-permute-start(f32[24,128]{1,0:T(8,128)S(1)} %add.10), channel_id=1, source_target_pairs={{0,16},{4,20},{8,24},{12,28},{16,0},{20,4},{24,8},{28,12},{1,17},{... | collective-permute-start | bytes 36872 | tf_op jit(solution)/shard_map/ppermute | solution.py:525
  54.7 4.7 %collective-permute-start.12 = (bf16[4,10,48,128]{3,2,1,0:T(8,128)(2,1)}, bf16[4,10,48,128]{3,2,1,0:T(8,128)(2,1)S(1)}, u32[]{:S(2)}, u32[]{:S(2)}) collective-permute-start(bf16[4,10,48,128]{3,2,1,0:T(8,128)(2,1)} %collective-permute-done.11.refs_2_), channel_id=1, source_target_pairs={{0,1},{1,0},{2,3},{3,2},{4,5},{5,4},{6,7},{7,6},{8,9},{9,8},{10,11... | collective-permute-start | bytes 1474568 | tf_op jit(solution)/shard_map/ppermute | solution.py:531
  54.7 8.2 %collective-permute-start.16 = (bf16[2,14,48,128]{3,2,1,0:T(8,128)(2,1)}, bf16[2,14,48,128]{3,2,1,0:T(8,128)(2,1)S(1)}, u32[]{:S(2)}, u32[]{:S(2)}) collective-permute-start(bf16[2,14,48,128]{3,2,1,0:T(8,128)(2,1)} %get-tuple-element.28.refs_0_), channel_id=1, source_target_pairs={{0,1},{1,0},{2,3},{3,2},{4,5},{5,4},{6,7},{7,6},{8,9},{9,8},{10,11... | collective-permute-start | bytes 1032200 | tf_op jit(solution)/shard_map/ppermute | solution.py:528
  56.8 4.8 %collective-permute-start.17 = (bf16[2,14,48,128]{3,2,1,0:T(8,128)(2,1)S(1)}, bf16[2,14,48,128]{3,2,1,0:T(8,128)(2,1)S(1)}, u32[]{:S(2)}, u32[]{:S(2)}) collective-permute-start(bf16[2,14,48,128]{3,2,1,0:T(8,128)(2,1)S(1)} %collective-permute-done.14.refs_2_), channel_id=1, source_target_pairs={{0,1},{1,0},{2,3},{3,2},{4,5},{5,4},{6,7},{7,6},{8,9},{9,8},{10,11... | collective-permute-start | bytes 1032200 | tf_op jit(solution)/shard_map/ppermute | solution.py:535
  56.8 10.5 %collective-permute-start.15 = (bf16[2,14,48,128]{3,2,1,0:T(8,128)(2,1)S(1)}, bf16[2,14,48,128]{3,2,1,0:T(8,128)(2,1)S(1)}, u32[]{:S(2)}, u32[]{:S(2)}) collective-permute-start(bf16[2,14,48,128]{3,2,1,0:T(8,128)(2,1)S(1)} %copy-done.7), channel_id=1, source_target_pairs={{0,2},{1,3},{2,0},{3,1},{4,6},{5,7},{6,4},{7,5},{8,10},{9,11},{10,... | collective-permute-start | bytes 1032200 | tf_op jit(solution)/shard_map/ppermute | solution.py:534
  58.7 8.6 %collective-permute-start.8 = (bf16[16,128]{1,0:T(8,128)(2,1)S(1)}, bf16[16,128]{1,0:T(8,128)(2,1)S(1)}, u32[]{:S(2)}, u32[]{:S(2)}) collective-permute-start(bf16[16,128]{1,0:T(8,128)(2,1)S(1)} %coefficients.1.a), channel_id=1, source_target_pairs={{0,1},{1,0},{2,3},{3,2},{4,5},{5,4},{6,7},{7,6},{8,9},{9,8},{10,11... | collective-permute-start | bytes 12296 | tf_op jit(solution)/shard_map/ppermute | solution.py:538
  59.3 13.6 %collective-permute-start.13 = (bf16[2,14,48,128]{3,2,1,0:T(8,128)(2,1)S(1)}, bf16[2,14,48,128]{3,2,1,0:T(8,128)(2,1)S(1)}, u32[]{:S(2)}, u32[]{:S(2)}) collective-permute-start(bf16[2,14,48,128]{3,2,1,0:T(8,128)(2,1)S(1)} %copy-done.7), channel_id=1, source_target_pairs={{0,1},{1,0},{2,3},{3,2},{4,5},{5,4},{6,7},{7,6},{8,9},{9,8},{10,11... | collective-permute-start | bytes 1032200 | tf_op jit(solution)/shard_map/ppermute | solution.py:529
  61.6 12.1 %collective-permute-start.19 = (bf16[2,10,48,128]{3,2,1,0:T(8,128)(2,1)S(1)}, bf16[2,10,48,128]{3,2,1,0:T(8,128)(2,1)S(1)}, u32[]{:S(2)}, u32[]{:S(2)}) collective-permute-start(bf16[2,10,48,128]{3,2,1,0:T(8,128)(2,1)S(1)} %get-tuple-element.36), channel_id=1, source_target_pairs={{0,4},{4,0},{8,12},{12,8},{16,20},{20,16},{24,28},{28,24},{1,5},{5... | collective-permute-start | bytes 737288 | tf_op jit(solution)/shard_map/ppermute | solution.py:537
  64.6 12.5 %collective-permute-start.20 = (bf16[2,14,48,128]{3,2,1,0:T(8,128)(2,1)S(1)}, bf16[2,14,48,128]{3,2,1,0:T(8,128)(2,1)S(1)}, u32[]{:S(2)}, u32[]{:S(2)}) collective-permute-start(bf16[2,14,48,128]{3,2,1,0:T(8,128)(2,1)S(1)} %rotated.4), channel_id=1, source_target_pairs={{0,4},{4,0},{8,12},{12,8},{16,20},{20,16},{24,28},{28,24},{1,5},{5... | collective-permute-start | bytes 1032200 | tf_op jit(solution)/shard_map/ppermute | solution.py:543
  67.3 5.6 %collective-permute-start.18 = (bf16[2,14,48,128]{3,2,1,0:T(8,128)(2,1)S(1)}, bf16[2,14,48,128]{3,2,1,0:T(8,128)(2,1)S(1)}, u32[]{:S(2)}, u32[]{:S(2)}) collective-permute-start(bf16[2,14,48,128]{3,2,1,0:T(8,128)(2,1)S(1)} %collective-permute-done.15.refs_2_), channel_id=1, source_target_pairs={{0,1},{1,0},{2,3},{3,2},{4,5},{5,4},{6,7},{7,6},{8,9},{9,8},{10,11... | collective-permute-start | bytes 1032200 | tf_op jit(solution)/shard_map/ppermute | solution.py:545
  67.3 3.7 %collective-permute-start.9 = (bf16[32,128]{1,0:T(8,128)(2,1)S(1)}, bf16[32,128]{1,0:T(8,128)(2,1)S(1)}, u32[]{:S(2)}, u32[]{:S(2)}) collective-permute-start(bf16[32,128]{1,0:T(8,128)(2,1)S(1)} %pad_maximum_fusion), channel_id=1, source_target_pairs={{0,2},{1,3},{2,0},{3,1},{4,6},{5,7},{6,4},{7,5},{8,10},{9,11},{10,... | collective-permute-start | bytes 24584 | tf_op jit(solution)/shard_map/ppermute | solution.py:539

commit v9 on v7

--- a/solution.py
+++ b/solution.py
@@ -37,40 +37,37 @@
     return jnp.where(linked, -0.125, 0.0)
 
 
-def prepare_kernel(early, psi, potential_far, to_x, to_x2, to_z, blocks, potential, sems):
+def potential_block(potential):
+    lines, width = potential.shape
+    gap = jnp.zeros((lines, 64 - width), F32)
+    u = (potential - 1.0) * 0.25
+    hi = u.astype(BF16).astype(F32)
+    return jnp.concatenate([hi, gap, u - hi, gap], axis=1)
+
+
+def prepare_kernel(early, psi, potential_far, to_x, to_z, potential, sems):
     x = lax.rem(lax.axis_index("space"), 2)
     half = psi.shape[1] // 2
     window = half + 2
     mine, theirs = (half - 2) * x, (half - 2) * (1 - x)
-    width = potential_far.shape[2]
-    gap = jnp.zeros((potential_far.shape[1], 64 - width), F32)
+    fetch = pltpu.make_async_copy(potential_far, potential, sems.at[0])
+    fetch.start()
     copies = [
         pltpu.make_async_copy(
-            psi.at[:, pl.ds(theirs, early)], to_x.at[:, pl.ds(0, early)], sems.at[0]
+            psi.at[:, pl.ds(theirs, early)], to_x.at[:, pl.ds(0, early)], sems.at[1]
         ),
         pltpu.make_async_copy(
-            psi.at[:, pl.ds(mine, window)], to_z.at[:, pl.ds(0, window)], sems.at[1]
-        ),
-        pltpu.make_async_copy(
-            psi.at[:, pl.ds(theirs + early, window - early)], to_x2, sems.at[2]
+            psi.at[:, pl.ds(mine, window)], to_z.at[:, pl.ds(0, window)], sems.at[2]
         ),
     ]
-    fetch = pltpu.make_async_copy(potential_far, potential, sems.at[5])
-    fetch.start()
     for copy in copies:
         copy.start()
     fetch.wait()
-    for plane in range(blocks.shape[0]):
-        u = (potential[plane] - 1.0) * 0.25
-        hi = u.astype(BF16).astype(F32)
-        blocks[plane, 0] = jnp.concatenate([hi, gap, u - hi, gap], axis=1).astype(BF16)
-    more = [
-        pltpu.make_async_copy(blocks, to_x.at[:, pl.ds(early, 1)], sems.at[3]),
-        pltpu.make_async_copy(blocks, to_z.at[:, pl.ds(window, 1)], sems.at[4]),
-    ]
-    for copy in more:
-        copy.start()
-    for copy in copies + more:
+    for plane in range(potential.shape[0]):
+        block = potential_block(potential[plane]).astype(BF16)
+        to_x[plane, early] = block
+        to_z[plane, window] = block
+    for copy in copies:
         copy.wait()
 
 
@@ -81,17 +78,58 @@
     def out(rows):
         return jax.ShapeDtypeStruct((planes, rows, width_y, orbs), BF16)
 
-    local = pl.BlockSpec(memory_space=pltpu.VMEM)
     return pl.pallas_call(
         functools.partial(prepare_kernel, early),
-        out_shape=(out(early + 1), out(window - early), out(window + 1), out(1)),
+        out_shape=(out(early + 1), out(window + 1)),
         in_specs=[pl.BlockSpec(memory_space=pltpu.MemorySpace.HBM)] * 2,
-        out_specs=(local,) * 4,
-        scratch_shapes=[pltpu.VMEM(potential.shape, F32), pltpu.SemaphoreType.DMA((6,))],
+        out_specs=(pl.BlockSpec(memory_space=pltpu.VMEM),) * 2,
+        scratch_shapes=[pltpu.VMEM(potential.shape, F32), pltpu.SemaphoreType.DMA((3,))],
         compiler_params=params(),
         cost_estimate=cost(4096, 4096),
         name="prepared",
     )(*(pltpu.with_memory_space_constraint(a, pltpu.MemorySpace.HBM) for a in (psi, potential)))
+
+
+def pack_kernel(early, psi, beta, to_x2, sem):
+    x = lax.rem(lax.axis_index("space"), 2)
+    half = psi.shape[1] // 2
+    later = half + 2 - early
+    _, _, lines, width = beta.shape
+    gap = jnp.zeros((lines, 64 - width), F32)
+    copy = pltpu.make_async_copy(
+        psi.at[:, pl.ds((half - 2) * (1 - x) + early, later)], to_x2.at[:, pl.ds(0, later)], sem
+    )
+    copy.start()
+    each = beta.shape[0] // to_x2.shape[0]
+
+    def pack(i, carry):
+        for plane in range(to_x2.shape[0]):
+            first, second = (beta[plane * each + i, k].astype(F32) for k in range(2))
+            to_x2[plane, later + i] = jnp.concatenate(
+                [first, gap, second, gap], axis=1
+            ).astype(BF16)
+        return carry
+
+    lax.fori_loop(0, each, pack, 0)
+    copy.wait()
+
+
+def packed(psi, beta, early):
+    planes, width_x, width_y, orbs = psi.shape
+    rows = width_x // 2 + 2 - early + beta.shape[0] // planes
+    return pl.pallas_call(
+        functools.partial(pack_kernel, early),
+        out_shape=jax.ShapeDtypeStruct((planes, rows, width_y, orbs), BF16),
+        in_specs=[
+            pl.BlockSpec(memory_space=pltpu.MemorySpace.HBM),
+            pl.BlockSpec(memory_space=pltpu.VMEM),
+        ],
+        out_specs=pl.BlockSpec(memory_space=pltpu.VMEM),
+        scratch_shapes=[pltpu.SemaphoreType.DMA],
+        compiler_params=params(),
+        cost_estimate=cost(4096, 4096),
+        name="packed",
+    )(pltpu.with_memory_space_constraint(psi, pltpu.MemorySpace.HBM), beta)
 
 
 def partial_kernel(count, atoms, own, beta, b_x, b_d, potential, gram, out, weights_out, table, acc):
@@ -107,6 +145,9 @@
     for k in range(2):
         plane = x if k == 0 else 1 - x
         outer, there = (b_d, beyond) if k == 0 else (b_x, side)
+        left = x == (1 if k == 0 else 0)
+        each = count // outer.shape[0]
+        begin = outer.shape[1] - each
         u = (potential[plane] - 1.0) * 0.25
 
         def fill(i, carry):
@@ -116,7 +157,9 @@
                 next_to = (jnp.abs(there - atoms[p]) <= 1).astype(F32)
                 b32 = beta[p, plane].astype(F32) * here
                 b = b32.astype(BF16)
-                sides = beta[p, 1 - plane].astype(F32) * here + outer[p].astype(F32) * next_to
+                both = outer[p // each, begin + lax.rem(p, each)].astype(F32)
+                other = jnp.where(left, both[:, :width], both[:, 64 : 64 + width])
+                sides = beta[p, 1 - plane].astype(F32) * here + other * next_to
                 whole = jnp.dot(b, tri, preferred_element_type=F32)
                 whole = whole + jnp.dot(tri, b, preferred_element_type=F32)
                 whole = whole + u * b32 - 0.125 * sides
@@ -253,22 +296,24 @@
     has_zo = upper * (1.0 - is_odd) + lower * is_odd
     if parts > 1:
         xr, zf = scratch[3], scratch[4]
-        early = xrs[0].shape[1] - 1
+        early = start + 4
         for target, pieces in ((xr, xrs), (zf, zfs)):
-            target[:, 0:early] = pieces[0][:, 0:early]
-            target[:, early:] = pieces[1][...]
+            target[:, start - 4 : early] = pieces[0][:, 0:8]
+            target[:, early:] = pieces[1][:, 0 : target.shape[1] - early]
         window = xr.shape[1] // 2
     else:
         xr, zf = xrs[0], zfs[0]
-        window = (xr.shape[1] - 1) // 2
+        early = xr.shape[1] - 1
+        window = early // 2
+        for target, piece in ((outs[1], xr), (outs[2], zf)):
+            target[...] = piece[:, early - 8 :]
     for c in range(1, 7):
         plane = (c % 2) ^ x
         if c in (2, 3):
-            block = p_own[plane, 0]
+            lines[c - 1] = potential_block(p_own[plane])
         else:
             ref = zfs[0] if c < 2 else (xrs[0] if c < 6 else zo)
-            block = ref[plane, ref.shape[1] - 1]
-        lines[c - 1] = block.astype(F32)
+            lines[c - 1] = ref[plane, ref.shape[1] - 1].astype(F32)
         for kind in range(2):
             even, odd = (lines[c - 1, pl.ds(k, half, stride=2)] for k in range(2))
             lanes = slice(64 * kind, 64 * kind + width)
@@ -354,6 +399,8 @@
     parts = len(xrs)
     shape = (2 * planes if joint else planes, rows, width, orbs)
     out = (jax.ShapeDtypeStruct(shape, BF16),) * (1 if joint else 2)
+    if parts == 1:
+        out += (jax.ShapeDtypeStruct((planes, 9, width, orbs), BF16),) * 2
     cells = 10 * rows * width
     scratch = [
         pltpu.VMEM((6, rows + 4, width, orbs), BF16),
@@ -361,7 +408,7 @@
         pltpu.VMEM((6, 2, own.shape[1] // 2, 2 * width), F32),
     ]
     if parts > 1:
-        window = xrs[0].shape[1] - 1 + xrs[1].shape[1]
+        window = own.shape[1] // 2 + 2
         scratch += [pltpu.VMEM((planes, window, width, orbs), BF16)] * 2
     return pl.pallas_call(
         functools.partial(filter_kernel, slabs, start, parts, joint),
@@ -418,29 +465,51 @@
     )(*blocks, q)
 
 
-def assemble_kernel(half, term, *refs):
-    out = refs[-1]
-    pieces = (len(refs) - 1) // 2
+def assemble_kernel(group, term, keep1, got1, got2, a, b, c, d, q, out):
+    half = term.shape[1] // 2
+    width, orbs = term.shape[2:]
     x = lax.rem(lax.axis_index("space"), 2)
-    start = 0
-    for k in range(pieces):
-        rows = refs[k].shape[1]
-        start += refs[k - 1].shape[1] if k else 0
-        for ref, at in ((refs[k], half * x), (refs[pieces + k], half * (1 - x))):
-            where = pl.ds(at + start, rows)
-            out[:, where] = (ref[...].astype(F32) + term[:, where]).astype(BF16)
-
-
-def assembled(term, mine, theirs):
-    return pl.pallas_call(
-        functools.partial(assemble_kernel, term.shape[1] // 2),
+    rows1, rows2 = keep1.shape[1], got2.shape[1]
+    for ref, at in (
+        (keep1, half * x),
+        (got1, half * (1 - x)),
+        (got2, half * (1 - x) + rows1),
+    ):
+        where = pl.ds(at, ref.shape[1])
+        out[:, where] = (ref[...].astype(F32) + term[:, where]).astype(BF16)
+    low = jnp.concatenate([q[0], q[1]], axis=0)
+    high = jnp.concatenate([q[2], q[3]], axis=0)
+
+    def one(j, carry):
+        where = pl.ds(half * x + rows1 + group * j, group)
+        for plane in range(a.shape[0]):
+            def take(ref):
+                return ref[plane, pl.ds(group * j, group)].reshape(group * width, orbs)
+
+            total = jnp.dot(
+                jnp.concatenate([take(a), take(b)], axis=1), low, preferred_element_type=F32
+            )
+            total = total + jnp.dot(
+                jnp.concatenate([take(c), take(d)], axis=1), high, preferred_element_type=F32
+            )
+            total = total.reshape(group, width, orbs) + term[plane, where]
+            out[plane, where] = total.astype(BF16)
+        return carry
+
+    lax.fori_loop(0, rows2 // group, one, 0)
+
+
+def assembled(term, keep1, got1, got2, blocks, q):
+    group = max(g for g in range(1, 9) if got2.shape[1] % g == 0)
+    return pl.pallas_call(
+        functools.partial(assemble_kernel, group),
         out_shape=jax.ShapeDtypeStruct(term.shape, BF16),
-        in_specs=[pl.BlockSpec(memory_space=pltpu.VMEM)] * (1 + len(mine) + len(theirs)),
+        in_specs=[pl.BlockSpec(memory_space=pltpu.VMEM)] * 9,
         out_specs=pl.BlockSpec(memory_space=pltpu.VMEM),
         compiler_params=params(),
         cost_estimate=cost(4096, 4096),
         name="assembled",
-    )(term, *mine, *theirs)
+    )(term, keep1, got1, got2, *blocks, q)
 
 
 def ordered(*arrays):
@@ -465,68 +534,67 @@
     swap = [(i, i ^ 1) for i in range(slabs)]
     own_way = within([(i, i + 2 if i % 2 else i - 2) for i in range(slabs)])
     other_way = within([(i, i - 2 if i % 2 else i + 2) for i in range(slabs)])
-    raster = within([(i, i + 1 if i % 2 else i - 1) for i in range(slabs)])
     groups = lax.axis_size("orb")
     across = [(i, i ^ 2) for i in range(groups)]
     beside = [(i, i ^ 1) for i in range(groups)]
     mine = (half - 2) * x
     theirs = (half - 2) * (1 - x)
 
-    to_x, to_x2, to_z, blocks = prepared(psi, potential, early)
+    to_x, to_z = prepared(psi, potential, early)
+    to_x2 = packed(psi, beta, early)
     xr1 = lax.ppermute(to_x, "space", swap)
     zo = lax.ppermute(to_z, "space", own_way)
-    far = lax.dynamic_index_in_dim(beta, x, 1, keepdims=False)
-    near = lax.dynamic_index_in_dim(beta, 1 - x, 1, keepdims=False)
     active = jnp.abs(place - atom_slab) <= 1
     beta_m = jnp.where(active[:, None, None, None], beta, jnp.zeros_like(beta))
     gram = jnp.einsum("pzxy,qzxy->pq", beta_m, beta_m, preferred_element_type=F32)
-    f_x = lax.ppermute(near, "space", swap)
-    f_d = lax.ppermute(far, "space", raster)
     zf1 = lax.ppermute(xr1, "space", other_way)
-    second, _, f_x, f_d = ordered(to_x2, xr1, f_x, f_d)
+    second, _ = ordered(to_x2, xr1)
     xr2 = lax.ppermute(second, "space", swap)
     zf2 = lax.ppermute(xr2, "space", other_way)
     strong = jnp.broadcast_to(strength[:, None], (count, orbs))
 
+    zf1, _ = ordered(zf1, xr2)
+    operands = (psi, potential, zo)
+    block1, xr_c, zf_c = filtered(slabs, 0, rows1, True, operands, (xr1,), (zf1,))
+    y1 = lax.ppermute(block1, "orb", across)
+    give2, keep2 = filtered(slabs, rows1, rows2, False, operands, (xr_c, xr2), (zf_c, zf2))
+    xr2, _ = ordered(xr2, give2)
+    sums, weights = partials(count, atom_slab, psi, beta, xr2, zf2, potential, gram)
+    rounds = [1 << k for k in range((slabs - 1).bit_length())]
+
+    def added(values, step):
+        pairs = [(i, i ^ step) for i in range(slabs)]
+        return values + lax.ppermute(values, "space", pairs)
+
+    for step in rounds[:-1]:
+        sums = added(sums, step)
+    pattern, q_tiles, _ = ordered(pattern, q_tiles, give2)
     me = lax.axis_index("orb")
     which = jnp.bitwise_xor(me, jnp.arange(groups, dtype=jnp.int32))
     rows_hot = (pattern[:, 0][:, None] == which[None, :]).astype(BF16)
     rows_hot = rows_hot * (pattern[:, 1] == me).astype(BF16)[:, None]
     q = jnp.einsum("ki,kab->iab", rows_hot, q_tiles, preferred_element_type=F32).astype(BF16)
-
-    sums, weights = partials(count, atom_slab, psi, beta, f_x, f_d, potential, gram)
-    zf1, sums = ordered(zf1, sums)
-    operands = (psi, blocks, zo)
-    (block1,) = filtered(slabs, 0, rows1, True, operands, (xr1,), (zf1,))
-    y1 = lax.ppermute(block1, "orb", across)
-    c1 = lax.ppermute(block1, "orb", beside)
-    give2, keep2 = filtered(slabs, rows1, rows2, False, operands, (xr1, xr2), (zf1, zf2))
-    step = 1
-    while step < slabs:
-        sums = sums + lax.ppermute(sums, "space", [(i, i ^ step) for i in range(slabs)])
-        step *= 2
-    coefs = coefficients(sums, strong)
     cg = lax.ppermute(give2, "orb", beside)
     ck = lax.ppermute(keep2, "orb", beside)
     yg = lax.ppermute(give2, "orb", across)
+    y1, again, _ = ordered(y1, block1, give2)
+    c1 = lax.ppermute(again, "orb", beside)
     yc1 = lax.ppermute(y1, "orb", beside)
     give1, keep1 = rotated((block1, c1, y1, yc1), q, 2)
-    keep_y, yg = ordered(keep2, yg)
+    got1 = lax.ppermute(give1, "space", swap)
+    keep_y, yg, got1, sums = ordered(keep2, yg, got1, sums)
+    coefs = coefficients(added(sums, rounds[-1]), strong)
     yk = lax.ppermute(keep_y, "orb", across)
-    yg, coefs = ordered(yg, coefs)
     ycg = lax.ppermute(yg, "orb", beside)
-    ycg, give1 = ordered(ycg, give1)
-    got1 = lax.ppermute(give1, "space", swap)
     coefs_c = lax.ppermute(coefs, "orb", beside)
     coefs_y = lax.ppermute(jnp.concatenate([coefs, coefs_c], axis=0), "orb", across)
     coefs_yc, coefs_y = coefs_y[2 * count :], coefs_y[: 2 * count]
     term = nonlocal_term(psi.shape, (coefs, coefs_c, coefs_y, coefs_yc), q, weights)
     (give2,) = rotated((give2, cg, yg, ycg), q, 1)
-    yk, give2 = ordered(yk, give2)
     got2 = lax.ppermute(give2, "space", swap)
+    yk, _, _ = ordered(yk, give2, coefs)
     yck = lax.ppermute(yk, "orb", beside)
-    (keep2,) = rotated((keep2, ck, yk, yck), q, 1)
-    return assembled(term, [keep1, keep2], [got1, got2])
+    return assembled(term, keep1, got1, got2, (keep2, ck, yk, yck), q)
 
 
 def solution(mesh):

time: 90 us -> 83.8 us (0.931)
  starting transfers between devices: 35.1 us -> 27.6 us
  waiting for transfers between devices: 32.2 us -> 33.8 us
  Pallas kernels: 20.4 us -> 19.3 us
    ppermute x1, starting transfers between devices: 11.1 us -> 1.74 us  [shards(): xr2 = lax.ppermute(second, 'space', swap)]
    ppermute x1, waiting for transfers between devices: 7.43 us -> 0.01 us  [shards(): got1 = lax.ppermute(give1, 'space', swap)]
    ppermute x1, waiting for transfers between devices: 0.01 us -> 6.65 us  [shards(): zf1 = lax.ppermute(xr1, 'space', other_way)]
    ppermute x1, waiting for transfers between devices: 0.01 us -> 6.28 us  [shards(): xr1 = lax.ppermute(to_x, 'space', swap)]
    ppermute x1, waiting for transfers between devices: 0.01 us -> 5.93 us  [shards(): zf2 = lax.ppermute(xr2, 'space', other_way)]
    ppermute x6 -> x4, waiting for transfers between devices: 12.4 us -> 8.35 us  [the longest x3 7.18 us: added(): return values + lax.ppermute(values, 'space', pairs)]
    ppermute x1, waiting for transfers between devices: 5.25 us -> 2.02 us  [shards(): yk = lax.ppermute(keep_y, 'orb', across)]
    ppermute x1, waiting for transfers between devices: 2.03 us -> 0.01 us  [shards(): yg = lax.ppermute(give2, 'orb', across)]
  transfers between devices with their start and end apart: 23 -> 21, of which waited for: 8 -> 11; matrix products, arithmetic and copies ran while one was open for 2% -> 1% of each run, Pallas kernels for 19% -> 15%
where the time goes in v9:
time: 83.8 us; the launch traced here: 83.5 us
  waiting for transfers between devices  33.8 us (40%)
  starting transfers between devices  27.6 us (33%)
  Pallas kernels  19.3 us (23%)
  local copies, waits for them, and re-layouts  1.76 us (2%)
    pallas_call x2, Pallas kernels, filtered(): pl.pallas_call(functools.partial(filter_kernel, slabs, start, parts, join...  7.45 us
    ppermute x3, waiting for transfers between devices, added(): return values + lax.ppermute(values, 'space', pairs)  7.18 us
    ppermute x1, waiting for transfers between devices, shards(): zf1 = lax.ppermute(xr1, 'space', other_way)  6.65 us
    ppermute x1, waiting for transfers between devices, shards(): xr1 = lax.ppermute(to_x, 'space', swap)  6.28 us
    ppermute x1, waiting for transfers between devices, shards(): zf2 = lax.ppermute(xr2, 'space', other_way)  5.93 us
    ppermute x3, starting transfers between devices, added(): return values + lax.ppermute(values, 'space', pairs)  4.98 us
    ppermute x1, starting transfers between devices, shards(): zf2 = lax.ppermute(xr2, 'space', other_way)  4.4 us
    ppermute x1, starting transfers between devices, shards(): zf1 = lax.ppermute(xr1, 'space', other_way)  3.49 us
  transfers between devices with their start and end apart: 21, of which 11 were waited for; matrix products, arithmetic and copies ran while one was open for 1% of the time, Pallas kernels for 15%

profile of v9, /device:TPU:0, one launch (start us, length us, event | category | flops | bytes accessed | tf_op | source)
XLA Modules:
  0.0 83.5 jit_solution(8258771066796708570)
XLA Ops:
  0.0 0.0 copy-start
  0.0 1.3 %prepared.1 = (bf16[2,15,48,128]{3,2,1,0:T(8,128)(2,1)S(1)}, bf16[2,27,48,128]{3,2,1,0:T(8,128)(2,1)S(1)}) custom-call(bf16[2,48,48,128]{3,2,1,0:T(8,128)(2,1)} %own.1, f32[2,48,48]{2,1,0:T(8,128)} %potential.1), custom_call_target="tpu_custom_call" | custom-call | flops 256 | bytes 256 | tf_op jit(solution)/shard_map/prepared/pallas_call | solution.py:81
  1.3 0.0 copy-start.1
  1.3 0.0 copy-start.3
  1.3 3.0 %collective-permute-start.1 = (bf16[2,15,48,128]{3,2,1,0:T(8,128)(2,1)S(1)}, bf16[2,15,48,128]{3,2,1,0:T(8,128)(2,1)S(1)}, u32[]{:S(2)}, u32[]{:S(2)}) collective-permute-start(bf16[2,15,48,128]{3,2,1,0:T(8,128)(2,1)S(1)} %get-tuple-element.29), channel_id=1, source_target_pairs={{0,4},{4,0},{8,12},{12,8},{16,20},{20,16},{24,28},{28,24},{1,5},{5... | collective-permute-start | bytes 1105928 | tf_op jit(solution)/shard_map/ppermute | solution.py:545
  4.3 1.3 %collective-permute-start = (bf16[2,27,48,128]{3,2,1,0:T(8,128)(2,1)S(1)}, bf16[2,27,48,128]{3,2,1,0:T(8,128)(2,1)S(1)}, u32[]{:S(2)}, u32[]{:S(2)}) collective-permute-start(bf16[2,27,48,128]{3,2,1,0:T(8,128)(2,1)S(1)} %get-tuple-element.28), channel_id=1, source_target_pairs={{4,12},{8,0},{12,20},{16,8},{20,28},{24,16},{5,13},{9,1},{13,21},{... | collective-permute-start | bytes 1990664 | tf_op jit(solution)/shard_map/ppermute | solution.py:546
  5.6 1.0 %packed.1 = bf16[2,16,48,128]{3,2,1,0:T(8,128)(2,1)S(1)} custom-call(bf16[2,48,48,128]{3,2,1,0:T(8,128)(2,1)} %own.1, bf16[8,2,48,48]{3,2,1,0:T(8,128)(2,1)S(1)} %copy-done.2), custom_call_target="tpu_custom_call" | custom-call | flops 256 | bytes 256 | tf_op jit(solution)/shard_map/packed/pallas_call | solution.py:120
  6.6 0.0 copy-start.6
  6.6 6.3 %collective-permute-done.1.refs_3_ = bf16[2,15,48,128]{3,2,1,0:T(8,128)(2,1)S(1)} collective-permute-done((bf16[2,15,48,128]{3,2,1,0:T(8,128)(2,1)S(1)}, bf16[2,15,48,128]{3,2,1,0:T(8,128)(2,1)S(1)}, u32[]{:S(2)}, u32[]{:S(2)}) %collective-permute-start.1) | collective-permute-done | bytes 368672 | tf_op jit(solution)/shard_map/ppermute | solution.py:545
  12.9 1.7 %collective-permute-start.3 = (bf16[2,16,48,128]{3,2,1,0:T(8,128)(2,1)S(1)}, bf16[2,16,48,128]{3,2,1,0:T(8,128)(2,1)S(1)}, u32[]{:S(2)}, u32[]{:S(2)}) collective-permute-start(bf16[2,16,48,128]{3,2,1,0:T(8,128)(2,1)S(1)} %packed.1), channel_id=1, source_target_pairs={{0,4},{4,0},{8,12},{12,8},{16,20},{20,16},{24,28},{28,24},{1,5},{5... | collective-permute-start | bytes 1179656 | tf_op jit(solution)/shard_map/ppermute | solution.py:552
  14.7 3.5 %collective-permute-start.2 = (bf16[2,15,48,128]{3,2,1,0:T(8,128)(2,1)S(1)}, bf16[2,15,48,128]{3,2,1,0:T(8,128)(2,1)S(1)}, u32[]{:S(2)}, u32[]{:S(2)}) collective-permute-start(bf16[2,15,48,128]{3,2,1,0:T(8,128)(2,1)S(1)} %collective-permute-done.1.refs_3_), channel_id=1, source_target_pairs={{0,8},{8,16},{12,4},{16,24},{20,12},{28,20},{1,9},{9,17},{13,5},{1... | collective-permute-start | bytes 1105928 | tf_op jit(solution)/shard_map/ppermute | solution.py:550
  18.2 6.7 %collective-permute-done.2.refs_4_ = bf16[2,15,48,128]{3,2,1,0:T(8,128)(2,1)S(1)} collective-permute-done((bf16[2,15,48,128]{3,2,1,0:T(8,128)(2,1)S(1)}, bf16[2,15,48,128]{3,2,1,0:T(8,128)(2,1)S(1)}, u32[]{:S(2)}, u32[]{:S(2)}) %collective-permute-start.2) | collective-permute-done | bytes 368672 | tf_op jit(solution)/shard_map/ppermute | solution.py:550
  24.8 0.0 collective-permute-done.3.refs_4_.b_x
  24.8 0.0 collective-permute-done.refs_2_
  24.8 0.0 copy-done.3
  24.8 3.6 %filtered.2 = (bf16[4,10,48,128]{3,2,1,0:T(8,128)(2,1)}, bf16[2,9,48,128]{3,2,1,0:T(8,128)(2,1)S(1)}, bf16[2,9,48,128]{3,2,1,0:T(8,128)(2,1)S(1)}) custom-call(bf16[2,48,48,128]{3,2,1,0:T(8,128)(2,1)S(1)} %copy-done.1, f32[2,48,48]{2,1,0:T(8,128)S(1)} %copy-done.3, bf16[2,27,48,128]{3,2,1,0:T(8,128)(2,1)S(1)} %collective-permute-done.refs_2_, ...), custom_call_target="tpu_custom_call" | custom-call | flops 2457600 | bytes 15360000 | tf_op jit(solution)/shard_map/filtered/pallas_call | solution.py:413
  28.5 0.7 copy-done.4
  29.2 1.5 %collective-permute-start.6 = (bf16[4,10,48,128]{3,2,1,0:T(8,128)(2,1)}, bf16[4,10,48,128]{3,2,1,0:T(8,128)(2,1)}, u32[]{:S(2)}, u32[]{:S(2)}) collective-permute-start(bf16[4,10,48,128]{3,2,1,0:T(8,128)(2,1)} %get-tuple-element.37.refs_0_), channel_id=1, source_target_pairs={{0,2},{1,3},{2,0},{3,1},{4,6},{5,7},{6,4},{7,5},{8,10},{9,11},{10,... | collective-permute-start | bytes 1474568 | tf_op jit(solution)/shard_map/ppermute | solution.py:559
  30.7 4.4 %collective-permute-start.4 = (bf16[2,16,48,128]{3,2,1,0:T(8,128)(2,1)S(1)}, bf16[2,16,48,128]{3,2,1,0:T(8,128)(2,1)S(1)}, u32[]{:S(2)}, u32[]{:S(2)}) collective-permute-start(bf16[2,16,48,128]{3,2,1,0:T(8,128)(2,1)S(1)} %collective-permute-done.3.refs_4_.b_x), channel_id=1, source_target_pairs={{0,8},{8,16},{12,4},{16,24},{20,12},{28,20},{1,9},{9,17},{13,5},{1... | collective-permute-start | bytes 1179656 | tf_op jit(solution)/shard_map/ppermute | solution.py:553
  35.1 0.0 copy-done.6
  35.2 5.9 %collective-permute-done.4.refs_6_.b_d = bf16[2,16,48,128]{3,2,1,0:T(8,128)(2,1)S(1)} collective-permute-done((bf16[2,16,48,128]{3,2,1,0:T(8,128)(2,1)S(1)}, bf16[2,16,48,128]{3,2,1,0:T(8,128)(2,1)S(1)}, u32[]{:S(2)}, u32[]{:S(2)}) %collective-permute-start.4) | collective-permute-done | bytes 393248 | tf_op jit(solution)/shard_map/ppermute | solution.py:553
  41.1 0.9 %copy-done.5 = bf16[2,9,48,128]{3,2,1,0:T(8,128)(2,1)S(1)} copy-done((bf16[2,9,48,128]{3,2,1,0:T(8,128)(2,1)S(1)}, bf16[2,9,48,128]{3,2,1,0:T(8,128)(2,1)}, u32[]{:S(2)}) %copy-start.5) | copy-done | bytes 221208
  42.0 3.8 %filtered.3 = (bf16[2,14,48,128]{3,2,1,0:T(8,128)(2,1)S(1)}, bf16[2,14,48,128]{3,2,1,0:T(8,128)(2,1)S(1)}) custom-call(bf16[2,48,48,128]{3,2,1,0:T(8,128)(2,1)S(1)} %copy-done.1, f32[2,48,48]{2,1,0:T(8,128)S(1)} %copy-done.3, bf16[2,27,48,128]{3,2,1,0:T(8,128)(2,1)S(1)} %collective-permute-done.refs_2_, ...), custom_call_target="tpu_custom_call" | custom-call | flops 3440640 | bytes 21504000 | tf_op jit(solution)/shard_map/filtered/pallas_call | solution.py:413
  45.8 0.6 collective-permute-start.5
  46.4 0.0 collective-permute-done.6.refs_2_
  46.4 0.0 collective-permute-start.7
  46.4 0.5 collective-permute-start.8
  47.0 0.3 fusion
  47.3 1.2 %collective-permute-done.7.refs_1_ = bf16[4,10,48,128]{3,2,1,0:T(8,128)(2,1)S(1)} collective-permute-done((bf16[4,10,48,128]{3,2,1,0:T(8,128)(2,1)}, bf16[4,10,48,128]{3,2,1,0:T(8,128)(2,1)S(1)}, u32[]{:S(2)}, u32[]{:S(2)}) %collective-permute-start.7) | collective-permute-done | bytes 491552 | tf_op jit(solution)/shard_map/ppermute | solution.py:581
  48.5 0.7 collective-permute-done.8.refs_3_
  49.2 2.0 %rotated.2 = (bf16[2,10,48,128]{3,2,1,0:T(8,128)(2,1)S(1)}, bf16[2,10,48,128]{3,2,1,0:T(8,128)(2,1)S(1)}) custom-call(bf16[4,10,48,128]{3,2,1,0:T(8,128)(2,1)} %get-tuple-element.37.refs_0_, bf16[4,10,48,128]{3,2,1,0:T(8,128)(2,1)S(1)} %collective-permute-done.7.refs_1_, bf16[4,10,48,128]{3,2,1,0:T(8,128)(2,1)} %collective-permute-done.6.refs_2_, ...), custom_call_target="tpu_custom_call" | custom-call | flops 15728640 | bytes 153600 | tf_op jit(solution)/shard_map/rotated/pallas_call | solution.py:457
  51.2 1.9 %collective-permute-start.9 = (bf16[2,10,48,128]{3,2,1,0:T(8,128)(2,1)S(1)}, bf16[2,10,48,128]{3,2,1,0:T(8,128)(2,1)S(1)}, u32[]{:S(2)}, u32[]{:S(2)}) collective-permute-start(bf16[2,10,48,128]{3,2,1,0:T(8,128)(2,1)S(1)} %get-tuple-element.41), channel_id=1, source_target_pairs={{0,4},{4,0},{8,12},{12,8},{16,20},{20,16},{24,28},{28,24},{1,5},{5... | collective-permute-start | bytes 737288 | tf_op jit(solution)/shard_map/ppermute | solution.py:584
  53.1 0.1 broadcast_select_fusion
  53.2 0.3 convolution_bitcast_fusion.gram
  53.5 3.1 %partials.1 = (f32[24,128]{1,0:T(8,128)S(1)}, bf16[2,48,24,48]{3,2,1,0:T(8,128)(2,1)S(1)}) custom-call(s32[8]{0:T(128)S(1)} %copy-done.6, bf16[2,48,48,128]{3,2,1,0:T(8,128)(2,1)S(1)} %copy-done.1, bf16[8,2,48,48]{3,2,1,0:T(8,128)(2,1)S(1)} %copy-done.2, bf16[2,16,48,128]{3,2,1,0:T(8,128)(2,1)S(1)} %collective-permute-done.3.refs_4_.b_x, ...), custom_call_target="tpu_custom_call" | custom-call | flops 256 | bytes 256 | tf_op jit(solution)/shard_map/partials/pallas_call | solution.py:192
  56.6 0.2 collective-permute-start.10
  56.8 3.5 %collective-permute-done.10 = f32[24,128]{1,0:T(8,128)S(1)} collective-permute-done((f32[24,128]{1,0:T(8,128)S(1)}, f32[24,128]{1,0:T(8,128)S(1)}, u32[]{:S(2)}, u32[]{:S(2)}) %collective-permute-start.10) | collective-permute-done | bytes 12320 | tf_op jit(solution)/shard_map/ppermute | solution.py:567
  60.3 1.7 %collective-permute-start.11 = (f32[24,128]{1,0:T(8,128)S(1)}, f32[24,128]{1,0:T(8,128)S(1)}, u32[]{:S(2)}, u32[]{:S(2)}) collective-permute-start(f32[24,128]{1,0:T(8,128)S(1)} %add.9), channel_id=1, source_target_pairs={{0,8},{4,12},{8,0},{12,4},{16,24},{20,28},{24,16},{28,20},{1,9},{5... | collective-permute-start | bytes 36872 | tf_op jit(solution)/shard_map/ppermute | solution.py:567
  62.0 0.0 collective-permute-start.15
  62.0 2.0 %collective-permute-done.11 = f32[24,128]{1,0:T(8,128)S(1)} collective-permute-done((f32[24,128]{1,0:T(8,128)S(1)}, f32[24,128]{1,0:T(8,128)S(1)}, u32[]{:S(2)}, u32[]{:S(2)}) %collective-permute-start.11) | collective-permute-done | bytes 12320 | tf_op jit(solution)/shard_map/ppermute | solution.py:567
  64.0 0.0 collective-permute-done.5.refs_2_
  64.0 0.0 collective-permute-done.9.got1
  64.0 0.1 collective-permute-start.16
  64.1 1.3 %collective-permute-start.19 = (bf16[2,14,48,128]{3,2,1,0:T(8,128)(2,1)S(1)}, bf16[2,14,48,128]{3,2,1,0:T(8,128)(2,1)S(1)}, u32[]{:S(2)}, u32[]{:S(2)}) collective-permute-start(bf16[2,14,48,128]{3,2,1,0:T(8,128)(2,1)S(1)} %get-tuple-element.49.a), channel_id=1, source_target_pairs={{0,2},{1,3},{2,0},{3,1},{4,6},{5,7},{6,4},{7,5},{8,10},{9,11},{10,... | collective-permute-start | bytes 1032200 | tf_op jit(solution)/shard_map/ppermute | solution.py:587
  65.4 3.0 %collective-permute-start.12 = (f32[24,128]{1,0:T(8,128)S(1)}, f32[24,128]{1,0:T(8,128)S(1)}, u32[]{:S(2)}, u32[]{:S(2)}) collective-permute-start(f32[24,128]{1,0:T(8,128)S(1)} %add.10), channel_id=1, source_target_pairs={{0,16},{4,20},{8,24},{12,28},{16,0},{20,4},{24,8},{28,12},{1,17},{... | collective-permute-start | bytes 36872 | tf_op jit(solution)/shard_map/ppermute | solution.py:567
  68.4 1.7 %collective-permute-done.12 = f32[24,128]{1,0:T(8,128)S(1)} collective-permute-done((f32[24,128]{1,0:T(8,128)S(1)}, f32[24,128]{1,0:T(8,128)S(1)}, u32[]{:S(2)}, u32[]{:S(2)}) %collective-permute-start.12) | collective-permute-done | bytes 12320 | tf_op jit(solution)/shard_map/ppermute | solution.py:567
  70.1 0.1 broadcast_in_dim.22.strength
  70.1 0.1 coefficients.1.a
  70.3 0.0 collective-permute-start.13
  70.3 0.5 collective-permute-start.18
  70.8 0.0 collective-permute-done.15.refs_1_
  70.8 0.0 collective-permute-done.16.refs_3_
  70.8 0.7 rotated.3
  71.5 1.0 %collective-permute-start.17 = (bf16[2,14,48,128]{3,2,1,0:T(8,128)(2,1)S(1)}, bf16[2,14,48,128]{3,2,1,0:T(8,128)(2,1)S(1)}, u32[]{:S(2)}, u32[]{:S(2)}) collective-permute-start(bf16[2,14,48,128]{3,2,1,0:T(8,128)(2,1)S(1)} %rotated.3), channel_id=1, source_target_pairs={{0,4},{4,0},{8,12},{12,8},{16,20},{20,16},{24,28},{28,24},{1,5},{5... | collective-permute-start | bytes 1032200 | tf_op jit(solution)/shard_map/ppermute | solution.py:594
  72.6 2.0 %collective-permute-done.19.c = bf16[2,14,48,128]{3,2,1,0:T(8,128)(2,1)S(1)} collective-permute-done((bf16[2,14,48,128]{3,2,1,0:T(8,128)(2,1)S(1)}, bf16[2,14,48,128]{3,2,1,0:T(8,128)(2,1)S(1)}, u32[]{:S(2)}, u32[]{:S(2)}) %collective-permute-start.19) | collective-permute-done | bytes 344096 | tf_op jit(solution)/shard_map/ppermute | solution.py:587
  74.6 0.0 collective-permute-start.20
  74.6 0.0 collective-permute-done.13.b
  74.6 1.3 %collective-permute-start.14 = (bf16[32,128]{1,0:T(8,128)(2,1)S(1)}, bf16[32,128]{1,0:T(8,128)(2,1)S(1)}, u32[]{:S(2)}, u32[]{:S(2)}) collective-permute-start(bf16[32,128]{1,0:T(8,128)(2,1)S(1)} %pad_maximum_fusion), channel_id=1, source_target_pairs={{0,2},{1,3},{2,0},{3,1},{4,6},{5,7},{6,4},{7,5},{8,10},{9,11},{10,... | collective-permute-start | bytes 24584 | tf_op jit(solution)/shard_map/ppermute | solution.py:590
  75.9 2.5 %collective-permute-done.14 = bf16[32,128]{1,0:T(8,128)(2,1)S(1)} collective-permute-done((bf16[32,128]{1,0:T(8,128)(2,1)S(1)}, bf16[32,128]{1,0:T(8,128)(2,1)S(1)}, u32[]{:S(2)}, u32[]{:S(2)}) %collective-permute-start.14) | collective-permute-done | bytes 8224 | tf_op jit(solution)/shard_map/ppermute | solution.py:590
  78.3 1.9 %nonlocal.1.term = f32[2,48,48,128]{3,2,1,0:T(8,128)S(1)} custom-call(bf16[16,128]{1,0:T(8,128)(2,1)S(1)} %coefficients.1.a, bf16[16,128]{1,0:T(8,128)(2,1)S(1)} %collective-permute-done.13.b, bf16[16,128]{1,0:T(8,128)(2,1)S(1)} %get-tuple-element.52.c, bf16[16,128]{1,0:T(8,128)(2,1)S(1)} %get-tuple-element.51.d, bf16[4,128,128]{2,1,0:T(8,128)(2,1)S(1)} %copy.18.refs_4_.q, ...), custom_call_target="tpu_custom_call" | custom-call | flops 256 | bytes 256 | tf_op jit(solution)/shard_map/nonlocal/pallas_call | solution.py:267
  80.2 0.0 collective-permute-done.18.b
  80.2 0.0 collective-permute-done.20.d
  80.2 1.4 %collective-permute-done.17.got2 = bf16[2,14,48,128]{3,2,1,0:T(8,128)(2,1)S(1)} collective-permute-done((bf16[2,14,48,128]{3,2,1,0:T(8,128)(2,1)S(1)}, bf16[2,14,48,128]{3,2,1,0:T(8,128)(2,1)S(1)}, u32[]{:S(2)}, u32[]{:S(2)}) %collective-permute-start.17) | collective-permute-done | bytes 344096 | tf_op jit(solution)/shard_map/ppermute | solution.py:594
  81.6 1.9 %assembled.1 = bf16[2,48,48,128]{3,2,1,0:T(8,128)(2,1)} custom-call(f32[2,48,48,128]{3,2,1,0:T(8,128)S(1)} %nonlocal.1.term, bf16[2,10,48,128]{3,2,1,0:T(8,128)(2,1)S(1)} %get-tuple-element.46.keep1, bf16[2,10,48,128]{3,2,1,0:T(8,128)(2,1)S(1)} %collective-permute-done.9.got1, bf16[2,14,48,128]{3,2,1,0:T(8,128)(2,1)S(1)} %collective-permute-done.17.got2, ...), custom_call_target="tpu_custom_call" | custom-call | flops 256 | bytes 256 | tf_op jit(solution)/shard_map/assembled/pallas_call | solution.py:504
  (20 shorter events, 0.1 us)
Async XLA Ops:
  0.0 47.0 %copy-start = (bf16[12,128,128]{2,1,0:T(8,128)(2,1)S(1)}, bf16[12,128,128]{2,1,0:T(8,128)(2,1)}, u32[]{:S(2)}) copy-start(bf16[12,128,128]{2,1,0:T(8,128)(2,1)} %param.13) | copy-start | bytes 1179652
  0.0 5.6 %copy-start.2 = (bf16[8,2,48,48]{3,2,1,0:T(8,128)(2,1)S(1)}, bf16[8,2,48,48]{3,2,1,0:T(8,128)(2,1)}, u32[]{:S(2)}) copy-start(bf16[8,2,48,48]{3,2,1,0:T(8,128)(2,1)} %beta.3) | copy-start | bytes 221188
  1.3 23.5 %copy-start.1 = (bf16[2,48,48,128]{3,2,1,0:T(8,128)(2,1)S(1)}, bf16[2,48,48,128]{3,2,1,0:T(8,128)(2,1)}, u32[]{:S(2)}) copy-start(bf16[2,48,48,128]{3,2,1,0:T(8,128)(2,1)} %own.1) | copy-start | bytes 3538948
  1.3 23.5 %copy-start.3 = (f32[2,48,48]{2,1,0:T(8,128)S(1)}, f32[2,48,48]{2,1,0:T(8,128)}, u32[]{:S(2)}) copy-start(f32[2,48,48]{2,1,0:T(8,128)} %potential.1) | copy-start | bytes 55300
  1.3 11.6 %collective-permute-start.1 = (bf16[2,15,48,128]{3,2,1,0:T(8,128)(2,1)S(1)}, bf16[2,15,48,128]{3,2,1,0:T(8,128)(2,1)S(1)}, u32[]{:S(2)}, u32[]{:S(2)}) collective-permute-start(bf16[2,15,48,128]{3,2,1,0:T(8,128)(2,1)S(1)} %get-tuple-element.29), channel_id=1, source_target_pairs={{0,4},{4,0},{8,12},{12,8},{16,20},{20,16},{24,28},{28,24},{1,5},{5... | collective-permute-start | bytes 1105928 | tf_op jit(solution)/shard_map/ppermute | solution.py:545
  4.3 20.5 %collective-permute-start = (bf16[2,27,48,128]{3,2,1,0:T(8,128)(2,1)S(1)}, bf16[2,27,48,128]{3,2,1,0:T(8,128)(2,1)S(1)}, u32[]{:S(2)}, u32[]{:S(2)}) collective-permute-start(bf16[2,27,48,128]{3,2,1,0:T(8,128)(2,1)S(1)} %get-tuple-element.28), channel_id=1, source_target_pairs={{4,12},{8,0},{12,20},{16,8},{20,28},{24,16},{5,13},{9,1},{13,21},{... | collective-permute-start | bytes 1990664 | tf_op jit(solution)/shard_map/ppermute | solution.py:546
  6.6 28.5 %copy-start.6 = (s32[8]{0:T(128)S(1)}, s32[8]{0:T(128)}, u32[]{:S(2)}) copy-start(s32[8]{0:T(128)} %atoms.1) | copy-start | bytes 100
  12.9 11.9 %collective-permute-start.3 = (bf16[2,16,48,128]{3,2,1,0:T(8,128)(2,1)S(1)}, bf16[2,16,48,128]{3,2,1,0:T(8,128)(2,1)S(1)}, u32[]{:S(2)}, u32[]{:S(2)}) collective-permute-start(bf16[2,16,48,128]{3,2,1,0:T(8,128)(2,1)S(1)} %packed.1), channel_id=1, source_target_pairs={{0,4},{4,0},{8,12},{12,8},{16,20},{20,16},{24,28},{28,24},{1,5},{5... | collective-permute-start | bytes 1179656 | tf_op jit(solution)/shard_map/ppermute | solution.py:552
  14.7 10.2 %collective-permute-start.2 = (bf16[2,15,48,128]{3,2,1,0:T(8,128)(2,1)S(1)}, bf16[2,15,48,128]{3,2,1,0:T(8,128)(2,1)S(1)}, u32[]{:S(2)}, u32[]{:S(2)}) collective-permute-start(bf16[2,15,48,128]{3,2,1,0:T(8,128)(2,1)S(1)} %collective-permute-done.1.refs_3_), channel_id=1, source_target_pairs={{0,8},{8,16},{12,4},{16,24},{20,12},{28,20},{1,9},{9,17},{13,5},{1... | collective-permute-start | bytes 1105928 | tf_op jit(solution)/shard_map/ppermute | solution.py:550
  28.5 0.7 copy-start.4
  29.2 17.2 %collective-permute-start.6 = (bf16[4,10,48,128]{3,2,1,0:T(8,128)(2,1)}, bf16[4,10,48,128]{3,2,1,0:T(8,128)(2,1)}, u32[]{:S(2)}, u32[]{:S(2)}) collective-permute-start(bf16[4,10,48,128]{3,2,1,0:T(8,128)(2,1)} %get-tuple-element.37.refs_0_), channel_id=1, source_target_pairs={{0,2},{1,3},{2,0},{3,1},{4,6},{5,7},{6,4},{7,5},{8,10},{9,11},{10,... | collective-permute-start | bytes 1474568 | tf_op jit(solution)/shard_map/ppermute | solution.py:559
  30.7 10.4 %collective-permute-start.4 = (bf16[2,16,48,128]{3,2,1,0:T(8,128)(2,1)S(1)}, bf16[2,16,48,128]{3,2,1,0:T(8,128)(2,1)S(1)}, u32[]{:S(2)}, u32[]{:S(2)}) collective-permute-start(bf16[2,16,48,128]{3,2,1,0:T(8,128)(2,1)S(1)} %collective-permute-done.3.refs_4_.b_x), channel_id=1, source_target_pairs={{0,8},{8,16},{12,4},{16,24},{20,12},{28,20},{1,9},{9,17},{13,5},{1... | collective-permute-start | bytes 1179656 | tf_op jit(solution)/shard_map/ppermute | solution.py:553
  41.1 0.9 %copy-start.5 = (bf16[2,9,48,128]{3,2,1,0:T(8,128)(2,1)S(1)}, bf16[2,9,48,128]{3,2,1,0:T(8,128)(2,1)}, u32[]{:S(2)}) copy-start(bf16[2,9,48,128]{3,2,1,0:T(8,128)(2,1)} %copy-done.4) | copy-start | bytes 663556
  42.0 4.9 %copy-start.8 = (s32[12,2]{0,1:T(2,128)S(1)}, s32[12,2]{0,1:T(2,128)}, u32[]{:S(2)}) copy-start(s32[12,2]{0,1:T(2,128)} %param.12) | copy-start | bytes 292
  45.8 18.2 %collective-permute-start.5 = (bf16[2,14,48,128]{3,2,1,0:T(8,128)(2,1)S(1)}, bf16[2,14,48,128]{3,2,1,0:T(8,128)(2,1)S(1)}, u32[]{:S(2)}, u32[]{:S(2)}) collective-permute-start(bf16[2,14,48,128]{3,2,1,0:T(8,128)(2,1)S(1)} %get-tuple-element.35.refs_0_), channel_id=1, source_target_pairs={{0,2},{1,3},{2,0},{3,1},{4,6},{5,7},{6,4},{7,5},{8,10},{9,11},{10,... | collective-permute-start | bytes 1032200 | tf_op jit(solution)/shard_map/ppermute | solution.py:579
  46.4 2.1 %collective-permute-start.7 = (bf16[4,10,48,128]{3,2,1,0:T(8,128)(2,1)}, bf16[4,10,48,128]{3,2,1,0:T(8,128)(2,1)S(1)}, u32[]{:S(2)}, u32[]{:S(2)}) collective-permute-start(bf16[4,10,48,128]{3,2,1,0:T(8,128)(2,1)} %get-tuple-element.37.refs_0_), channel_id=1, source_target_pairs={{0,1},{1,0},{2,3},{3,2},{4,5},{5,4},{6,7},{7,6},{8,9},{9,8},{10,11... | collective-permute-start | bytes 1474568 | tf_op jit(solution)/shard_map/ppermute | solution.py:581
  46.4 2.8 %collective-permute-start.8 = (bf16[4,10,48,128]{3,2,1,0:T(8,128)(2,1)}, bf16[4,10,48,128]{3,2,1,0:T(8,128)(2,1)S(1)}, u32[]{:S(2)}, u32[]{:S(2)}) collective-permute-start(bf16[4,10,48,128]{3,2,1,0:T(8,128)(2,1)} %collective-permute-done.6.refs_2_), channel_id=1, source_target_pairs={{0,1},{1,0},{2,3},{3,2},{4,5},{5,4},{6,7},{7,6},{8,9},{9,8},{10,11... | collective-permute-start | bytes 1474568 | tf_op jit(solution)/shard_map/ppermute | solution.py:582
  51.2 12.8 %collective-permute-start.9 = (bf16[2,10,48,128]{3,2,1,0:T(8,128)(2,1)S(1)}, bf16[2,10,48,128]{3,2,1,0:T(8,128)(2,1)S(1)}, u32[]{:S(2)}, u32[]{:S(2)}) collective-permute-start(bf16[2,10,48,128]{3,2,1,0:T(8,128)(2,1)S(1)} %get-tuple-element.41), channel_id=1, source_target_pairs={{0,4},{4,0},{8,12},{12,8},{16,20},{20,16},{24,28},{28,24},{1,5},{5... | collective-permute-start | bytes 737288 | tf_op jit(solution)/shard_map/ppermute | solution.py:584
  53.5 16.6 %copy-start.7 = (f32[8]{0:T(128)S(1)}, f32[8]{0:T(128)}, u32[]{:S(2)}) copy-start(f32[8]{0:T(128)} %param.10) | copy-start | bytes 100
  56.6 3.8 %collective-permute-start.10 = (f32[24,128]{1,0:T(8,128)S(1)}, f32[24,128]{1,0:T(8,128)S(1)}, u32[]{:S(2)}, u32[]{:S(2)}) collective-permute-start(f32[24,128]{1,0:T(8,128)S(1)} %get-tuple-element.43), channel_id=1, source_target_pairs={{0,4},{4,0},{8,12},{12,8},{16,20},{20,16},{24,28},{28,24},{1,5},{5... | collective-permute-start | bytes 36872 | tf_op jit(solution)/shard_map/ppermute | solution.py:567
  60.3 3.7 %collective-permute-start.11 = (f32[24,128]{1,0:T(8,128)S(1)}, f32[24,128]{1,0:T(8,128)S(1)}, u32[]{:S(2)}, u32[]{:S(2)}) collective-permute-start(f32[24,128]{1,0:T(8,128)S(1)} %add.9), channel_id=1, source_target_pairs={{0,8},{4,12},{8,0},{12,4},{16,24},{20,28},{24,16},{28,20},{1,9},{5... | collective-permute-start | bytes 36872 | tf_op jit(solution)/shard_map/ppermute | solution.py:567
  62.0 8.8 %collective-permute-start.15 = (bf16[2,14,48,128]{3,2,1,0:T(8,128)(2,1)S(1)}, bf16[2,14,48,128]{3,2,1,0:T(8,128)(2,1)S(1)}, u32[]{:S(2)}, u32[]{:S(2)}) collective-permute-start(bf16[2,14,48,128]{3,2,1,0:T(8,128)(2,1)S(1)} %get-tuple-element.35.refs_0_), channel_id=1, source_target_pairs={{0,1},{1,0},{2,3},{3,2},{4,5},{5,4},{6,7},{7,6},{8,9},{9,8},{10,11... | collective-permute-start | bytes 1032200 | tf_op jit(solution)/shard_map/ppermute | solution.py:577
  64.0 6.8 %collective-permute-start.16 = (bf16[2,14,48,128]{3,2,1,0:T(8,128)(2,1)S(1)}, bf16[2,14,48,128]{3,2,1,0:T(8,128)(2,1)S(1)}, u32[]{:S(2)}, u32[]{:S(2)}) collective-permute-start(bf16[2,14,48,128]{3,2,1,0:T(8,128)(2,1)S(1)} %collective-permute-done.5.refs_2_), channel_id=1, source_target_pairs={{0,1},{1,0},{2,3},{3,2},{4,5},{5,4},{6,7},{7,6},{8,9},{9,8},{10,11... | collective-permute-start | bytes 1032200 | tf_op jit(solution)/shard_map/ppermute | solution.py:588
  64.1 10.5 %collective-permute-start.19 = (bf16[2,14,48,128]{3,2,1,0:T(8,128)(2,1)S(1)}, bf16[2,14,48,128]{3,2,1,0:T(8,128)(2,1)S(1)}, u32[]{:S(2)}, u32[]{:S(2)}) collective-permute-start(bf16[2,14,48,128]{3,2,1,0:T(8,128)(2,1)S(1)} %get-tuple-element.49.a), channel_id=1, source_target_pairs={{0,2},{1,3},{2,0},{3,1},{4,6},{5,7},{6,4},{7,5},{8,10},{9,11},{10,... | collective-permute-start | bytes 1032200 | tf_op jit(solution)/shard_map/ppermute | solution.py:587
  65.4 4.7 %collective-permute-start.12 = (f32[24,128]{1,0:T(8,128)S(1)}, f32[24,128]{1,0:T(8,128)S(1)}, u32[]{:S(2)}, u32[]{:S(2)}) collective-permute-start(f32[24,128]{1,0:T(8,128)S(1)} %add.10), channel_id=1, source_target_pairs={{0,16},{4,20},{8,24},{12,28},{16,0},{20,4},{24,8},{28,12},{1,17},{... | collective-permute-start | bytes 36872 | tf_op jit(solution)/shard_map/ppermute | solution.py:567
  70.3 4.3 %collective-permute-start.13 = (bf16[16,128]{1,0:T(8,128)(2,1)S(1)}, bf16[16,128]{1,0:T(8,128)(2,1)S(1)}, u32[]{:S(2)}, u32[]{:S(2)}) collective-permute-start(bf16[16,128]{1,0:T(8,128)(2,1)S(1)} %coefficients.1.a), channel_id=1, source_target_pairs={{0,1},{1,0},{2,3},{3,2},{4,5},{5,4},{6,7},{7,6},{8,9},{9,8},{10,11... | collective-permute-start | bytes 12296 | tf_op jit(solution)/shard_map/ppermute | solution.py:589
  70.3 9.9 %collective-permute-start.18 = (bf16[2,14,48,128]{3,2,1,0:T(8,128)(2,1)S(1)}, bf16[2,14,48,128]{3,2,1,0:T(8,128)(2,1)S(1)}, u32[]{:S(2)}, u32[]{:S(2)}) collective-permute-start(bf16[2,14,48,128]{3,2,1,0:T(8,128)(2,1)S(1)} %get-tuple-element.49.a), channel_id=1, source_target_pairs={{0,1},{1,0},{2,3},{3,2},{4,5},{5,4},{6,7},{7,6},{8,9},{9,8},{10,11... | collective-permute-start | bytes 1032200 | tf_op jit(solution)/shard_map/ppermute | solution.py:578
  71.5 10.1 %collective-permute-start.17 = (bf16[2,14,48,128]{3,2,1,0:T(8,128)(2,1)S(1)}, bf16[2,14,48,128]{3,2,1,0:T(8,128)(2,1)S(1)}, u32[]{:S(2)}, u32[]{:S(2)}) collective-permute-start(bf16[2,14,48,128]{3,2,1,0:T(8,128)(2,1)S(1)} %rotated.3), channel_id=1, source_target_pairs={{0,4},{4,0},{8,12},{12,8},{16,20},{20,16},{24,28},{28,24},{1,5},{5... | collective-permute-start | bytes 1032200 | tf_op jit(solution)/shard_map/ppermute | solution.py:594
  74.6 5.6 %collective-permute-start.20 = (bf16[2,14,48,128]{3,2,1,0:T(8,128)(2,1)S(1)}, bf16[2,14,48,128]{3,2,1,0:T(8,128)(2,1)S(1)}, u32[]{:S(2)}, u32[]{:S(2)}) collective-permute-start(bf16[2,14,48,128]{3,2,1,0:T(8,128)(2,1)S(1)} %collective-permute-done.19.c), channel_id=1, source_target_pairs={{0,1},{1,0},{2,3},{3,2},{4,5},{5,4},{6,7},{7,6},{8,9},{9,8},{10,11... | collective-permute-start | bytes 1032200 | tf_op jit(solution)/shard_map/ppermute | solution.py:596
  74.6 3.7 %collective-permute-start.14 = (bf16[32,128]{1,0:T(8,128)(2,1)S(1)}, bf16[32,128]{1,0:T(8,128)(2,1)S(1)}, u32[]{:S(2)}, u32[]{:S(2)}) collective-permute-start(bf16[32,128]{1,0:T(8,128)(2,1)S(1)} %pad_maximum_fusion), channel_id=1, source_target_pairs={{0,2},{1,3},{2,0},{3,1},{4,6},{5,7},{6,4},{7,5},{8,10},{9,11},{10,... | collective-permute-start | bytes 24584 | tf_op jit(solution)/shard_map/ppermute | solution.py:590

commit v10 on v9

--- a/solution.py
+++ b/solution.py
@@ -90,7 +90,7 @@
     )(*(pltpu.with_memory_space_constraint(a, pltpu.MemorySpace.HBM) for a in (psi, potential)))
 
 
-def pack_kernel(early, psi, beta, to_x2, sem):
+def pack_kernel(early, psi, beta, to_x2, far, sem):
     x = lax.rem(lax.axis_index("space"), 2)
     half = psi.shape[1] // 2
     later = half + 2 - early
@@ -110,6 +110,7 @@
             ).astype(BF16)
         return carry
 
+    far[...] = beta[:, x]
     lax.fori_loop(0, each, pack, 0)
     copy.wait()
 
@@ -119,12 +120,15 @@
     rows = width_x // 2 + 2 - early + beta.shape[0] // planes
     return pl.pallas_call(
         functools.partial(pack_kernel, early),
-        out_shape=jax.ShapeDtypeStruct((planes, rows, width_y, orbs), BF16),
+        out_shape=(
+            jax.ShapeDtypeStruct((planes, rows, width_y, orbs), BF16),
+            jax.ShapeDtypeStruct((beta.shape[0], *beta.shape[2:]), BF16),
+        ),
         in_specs=[
             pl.BlockSpec(memory_space=pltpu.MemorySpace.HBM),
             pl.BlockSpec(memory_space=pltpu.VMEM),
         ],
-        out_specs=pl.BlockSpec(memory_space=pltpu.VMEM),
+        out_specs=(pl.BlockSpec(memory_space=pltpu.VMEM),) * 2,
         scratch_shapes=[pltpu.SemaphoreType.DMA],
         compiler_params=params(),
         cost_estimate=cost(4096, 4096),
@@ -144,10 +148,9 @@
 
     for k in range(2):
         plane = x if k == 0 else 1 - x
-        outer, there = (b_d, beyond) if k == 0 else (b_x, side)
-        left = x == (1 if k == 0 else 0)
-        each = count // outer.shape[0]
-        begin = outer.shape[1] - each
+        there = beyond if k == 0 else side
+        each = count // b_x.shape[0]
+        begin = b_x.shape[1] - each
         u = (potential[plane] - 1.0) * 0.25
 
         def fill(i, carry):
@@ -157,8 +160,11 @@
                 next_to = (jnp.abs(there - atoms[p]) <= 1).astype(F32)
                 b32 = beta[p, plane].astype(F32) * here
                 b = b32.astype(BF16)
-                both = outer[p // each, begin + lax.rem(p, each)].astype(F32)
-                other = jnp.where(left, both[:, :width], both[:, 64 : 64 + width])
+                if k == 0:
+                    other = b_d[p].astype(F32)
+                else:
+                    both = b_x[p // each, begin + lax.rem(p, each)].astype(F32)
+                    other = jnp.where(x == 0, both[:, :width], both[:, 64 : 64 + width])
                 sides = beta[p, 1 - plane].astype(F32) * here + other * next_to
                 whole = jnp.dot(b, tri, preferred_element_type=F32)
                 whole = whole + jnp.dot(tri, b, preferred_element_type=F32)
@@ -278,7 +284,7 @@
 def filter_kernel(slabs, start, parts, joint, *refs):
     own, p_own, zo = refs[:3]
     xrs, zfs = refs[3 : 3 + parts], refs[3 + parts : 3 + 2 * parts]
-    extra = 5 if parts > 1 else 3
+    extra = 7 if parts > 1 else 4
     outs, scratch = refs[3 + 2 * parts : -extra], refs[-extra:]
     first, lines, diagonals = scratch[:3]
     place = lax.axis_index("space")
@@ -295,25 +301,48 @@
     has_zf = lower * (1.0 - is_odd) + upper * is_odd
     has_zo = upper * (1.0 - is_odd) + lower * is_odd
     if parts > 1:
-        xr, zf = scratch[3], scratch[4]
+        xr, zf, pots, sems = scratch[3:]
         early = start + 4
+        copies = []
+        for k, (target, pieces) in enumerate(((xr, xrs), (zf, zfs))):
+            rows_in = pieces[0].at[:, pl.ds(0, 8)]
+            last = pieces[0].at[:, pl.ds(8, 1)]
+            copies += [
+                pltpu.make_async_copy(
+                    rows_in, target.at[:, pl.ds(start - 4, 8)], sems.at[2 * k]
+                ),
+                pltpu.make_async_copy(last, pots.at[k], sems.at[2 * k + 1]),
+            ]
+        for copy in copies:
+            copy.start()
         for target, pieces in ((xr, xrs), (zf, zfs)):
-            target[:, start - 4 : early] = pieces[0][:, 0:8]
             target[:, early:] = pieces[1][:, 0 : target.shape[1] - early]
+        for copy in copies:
+            copy.wait()
         window = xr.shape[1] // 2
     else:
         xr, zf = xrs[0], zfs[0]
         early = xr.shape[1] - 1
         window = early // 2
-        for target, piece in ((outs[1], xr), (outs[2], zf)):
-            target[...] = piece[:, early - 8 :]
+        sems = scratch[3]
+        copies = [
+            pltpu.make_async_copy(piece.at[:, pl.ds(early - 8, 9)], target, sems.at[k])
+            for k, (target, piece) in enumerate(((outs[1], xr), (outs[2], zf)))
+        ]
+        for copy in copies:
+            copy.start()
     for c in range(1, 7):
         plane = (c % 2) ^ x
         if c in (2, 3):
             lines[c - 1] = potential_block(p_own[plane])
         else:
-            ref = zfs[0] if c < 2 else (xrs[0] if c < 6 else zo)
-            lines[c - 1] = ref[plane, ref.shape[1] - 1].astype(F32)
+            if c == 6:
+                tail = zo
+            elif parts > 1:
+                tail = pots.at[1 if c < 2 else 0]
+            else:
+                tail = zf if c < 2 else xr
+            lines[c - 1] = tail[plane, tail.shape[1] - 1].astype(F32)
         for kind in range(2):
             even, odd = (lines[c - 1, pl.ds(k, half, stride=2)] for k in range(2))
             lanes = slice(64 * kind, 64 * kind + width)
@@ -391,6 +420,9 @@
         return carry
 
     lax.fori_loop(0, rows // 2, step2, 0)
+    if parts == 1:
+        for copy in copies:
+            copy.wait()
 
 
 def filtered(slabs, start, rows, joint, operands, xrs, zfs):
@@ -407,14 +439,23 @@
         pltpu.VMEM((6, width, orbs), F32),
         pltpu.VMEM((6, 2, own.shape[1] // 2, 2 * width), F32),
     ]
-    if parts > 1:
+    local = pl.BlockSpec(memory_space=pltpu.VMEM)
+    distant = pl.BlockSpec(memory_space=pltpu.MemorySpace.HBM)
+    in_specs, out_specs = [local] * (len(operands) + 2 * parts), [local] * len(out)
+    if parts == 1:
+        out_specs[1:] = [distant] * 2
+        scratch += [pltpu.SemaphoreType.DMA((2,))]
+    else:
+        for k in (0, parts):
+            in_specs[len(operands) + k] = distant
         window = own.shape[1] // 2 + 2
         scratch += [pltpu.VMEM((planes, window, width, orbs), BF16)] * 2
+        scratch += [pltpu.VMEM((2, planes, 1, width, orbs), BF16), pltpu.SemaphoreType.DMA((4,))]
     return pl.pallas_call(
         functools.partial(filter_kernel, slabs, start, parts, joint),
         out_shape=out,
-        in_specs=[pl.BlockSpec(memory_space=pltpu.VMEM)] * (len(operands) + 2 * parts),
-        out_specs=(pl.BlockSpec(memory_space=pltpu.VMEM),) * len(out),
+        in_specs=in_specs,
+        out_specs=tuple(out_specs),
         scratch_shapes=scratch,
         compiler_params=params(),
         cost_estimate=cost(2 * cells * 32 * orbs, FILTER * cells * orbs * 4),
@@ -541,7 +582,10 @@
     theirs = (half - 2) * (1 - x)
 
     to_x, to_z = prepared(psi, potential, early)
-    to_x2 = packed(psi, beta, early)
+    to_x2, far = packed(psi, beta, early)
+    raster = within([(i, i + 1 if i % 2 else i - 1) for i in range(slabs)])
+    f_d = lax.ppermute(far, "space", raster)
+    to_z, f_d = ordered(to_z, f_d)
     xr1 = lax.ppermute(to_x, "space", swap)
     zo = lax.ppermute(to_z, "space", own_way)
     active = jnp.abs(place - atom_slab) <= 1
@@ -557,9 +601,10 @@
     operands = (psi, potential, zo)
     block1, xr_c, zf_c = filtered(slabs, 0, rows1, True, operands, (xr1,), (zf1,))
     y1 = lax.ppermute(block1, "orb", across)
+    f_d, _ = ordered(f_d, block1)
+    sums, weights = partials(count, atom_slab, psi, beta, xr2, f_d, potential, gram)
+    zf2, sums = ordered(zf2, sums)
     give2, keep2 = filtered(slabs, rows1, rows2, False, operands, (xr_c, xr2), (zf_c, zf2))
-    xr2, _ = ordered(xr2, give2)
-    sums, weights = partials(count, atom_slab, psi, beta, xr2, zf2, potential, gram)
     rounds = [1 << k for k in range((slabs - 1).bit_length())]
 
     def added(values, step):

time: 83.8 us -> 92.1 us (1.099)
  starting transfers between devices: 27.6 us -> 31.9 us
  local copies, waits for them, and re-layouts: 1.76 us -> 4.17 us
  Pallas kernels: 19.3 us -> 21.6 us
    ppermute x1, waiting for transfers between devices: 0.01 us -> 3.74 us  [shards(): zo = lax.ppermute(to_z, 'space', own_way)]
    ppermute x1, waiting for transfers between devices: 5.93 us -> 2.25 us  [shards(): zf2 = lax.ppermute(xr2, 'space', other_way)]
    ppermute x1, starting transfers between devices: 1.74 us -> 4.29 us  [shards(): xr2 = lax.ppermute(second, 'space', swap)]
    unnamed x18 -> x28, local copies, waits for them, and re-layouts: 1.67 us -> 4.08 us
    ppermute x3, waiting for transfers between devices: 7.18 us -> 9.57 us  [added(): return values + lax.ppermute(values, 'space', pairs)]
    ppermute x1, waiting for transfers between devices: 6.65 us -> 4.39 us  [shards(): zf1 = lax.ppermute(xr1, 'space', other_way)]
    ppermute x3, starting transfers between devices: 4.98 us -> 6.24 us  [added(): return values + lax.ppermute(values, 'space', pairs)]
    ppermute x1, waiting for transfers between devices: 6.28 us -> 5.32 us  [shards(): xr1 = lax.ppermute(to_x, 'space', swap)]
  transfers between devices with their start and end apart: 21 -> 22, of which waited for: 11 -> 12; matrix products, arithmetic and copies ran while one was open for 1% -> 1% of each run, Pallas kernels for 15% -> 15%
where the time goes in v10:
time: 92.1 us; the launch traced here: 91.7 us
  waiting for transfers between devices  32.9 us (36%)
  starting transfers between devices  31.9 us (35%)
  Pallas kernels  21.6 us (23%)
  local copies, waits for them, and re-layouts  4.17 us (5%)
    ppermute x3, waiting for transfers between devices, added(): return values + lax.ppermute(values, 'space', pairs)  9.57 us
    pallas_call x2, Pallas kernels, filtered(): pl.pallas_call(functools.partial(filter_kernel, slabs, start, parts, join...  8.26 us
    ppermute x3, starting transfers between devices, added(): return values + lax.ppermute(values, 'space', pairs)  6.24 us
    ppermute x1, waiting for transfers between devices, shards(): xr1 = lax.ppermute(to_x, 'space', swap)  5.32 us
    ppermute x1, waiting for transfers between devices, shards(): zf1 = lax.ppermute(xr1, 'space', other_way)  4.39 us
    ppermute x1, starting transfers between devices, shards(): xr2 = lax.ppermute(second, 'space', swap)  4.29 us
    ppermute x1, starting transfers between devices, shards(): zf1 = lax.ppermute(xr1, 'space', other_way)  4.18 us
    unnamed x28, local copies, waits for them, and re-layouts  4.08 us
  transfers between devices with their start and end apart: 22, of which 12 were waited for; matrix products, arithmetic and copies ran while one was open for 1% of the time, Pallas kernels for 15%

profile of v10, /device:TPU:0, one launch (start us, length us, event | category | flops | bytes accessed | tf_op | source)
XLA Modules:
  0.0 91.7 jit_solution(2091539046307995433)
XLA Ops:
  0.0 2.2 %prepared.1 = (bf16[2,15,48,128]{3,2,1,0:T(8,128)(2,1)S(1)}, bf16[2,27,48,128]{3,2,1,0:T(8,128)(2,1)}) custom-call(bf16[2,48,48,128]{3,2,1,0:T(8,128)(2,1)} %refs_0_.3, f32[2,48,48]{2,1,0:T(8,128)} %refs_1_.3), custom_call_target="tpu_custom_call" | custom-call | flops 256 | bytes 256 | tf_op jit(solution)/shard_map/prepared/pallas_call | solution.py:81
  2.2 3.0 %collective-permute-start.2 = (bf16[2,15,48,128]{3,2,1,0:T(8,128)(2,1)S(1)}, bf16[2,15,48,128]{3,2,1,0:T(8,128)(2,1)S(1)}, u32[]{:S(2)}, u32[]{:S(2)}) collective-permute-start(bf16[2,15,48,128]{3,2,1,0:T(8,128)(2,1)S(1)} %get-tuple-element.37), channel_id=1, source_target_pairs={{0,4},{4,0},{8,12},{12,8},{16,20},{20,16},{24,28},{28,24},{1,5},{5... | collective-permute-start | bytes 1105928 | tf_op jit(solution)/shard_map/ppermute | solution.py:589
  5.2 0.9 %copy-done.2 = bf16[8,2,48,48]{3,2,1,0:T(8,128)(2,1)S(1)} copy-done((bf16[8,2,48,48]{3,2,1,0:T(8,128)(2,1)S(1)}, bf16[8,2,48,48]{3,2,1,0:T(8,128)(2,1)}, u32[]{:S(2)}) %copy-start.2) | copy-done | bytes 73752
  6.1 1.7 %packed.1 = (bf16[2,16,48,128]{3,2,1,0:T(8,128)(2,1)}, bf16[8,48,48]{2,1,0:T(8,128)(2,1)S(1)}) custom-call(bf16[2,48,48,128]{3,2,1,0:T(8,128)(2,1)} %refs_0_.3, bf16[8,2,48,48]{3,2,1,0:T(8,128)(2,1)S(1)} %copy-done.2), custom_call_target="tpu_custom_call" | custom-call | flops 256 | bytes 256 | tf_op jit(solution)/shard_map/packed/pallas_call | solution.py:121
  7.9 0.7 collective-permute-start
  8.5 0.0 collective-permute-done.b_d
  8.5 1.3 %collective-permute-start.1 = (bf16[2,27,48,128]{3,2,1,0:T(8,128)(2,1)}, bf16[2,27,48,128]{3,2,1,0:T(8,128)(2,1)S(1)}, u32[]{:S(2)}, u32[]{:S(2)}) collective-permute-start(bf16[2,27,48,128]{3,2,1,0:T(8,128)(2,1)} %get-tuple-element.36), channel_id=1, source_target_pairs={{4,12},{8,0},{12,20},{16,8},{20,28},{24,16},{5,13},{9,1},{13,21},{... | collective-permute-start | bytes 1990664 | tf_op jit(solution)/shard_map/ppermute | solution.py:590
  9.8 5.3 %collective-permute-done.2.refs_3_ = bf16[2,15,48,128]{3,2,1,0:T(8,128)(2,1)S(1)} collective-permute-done((bf16[2,15,48,128]{3,2,1,0:T(8,128)(2,1)S(1)}, bf16[2,15,48,128]{3,2,1,0:T(8,128)(2,1)S(1)}, u32[]{:S(2)}, u32[]{:S(2)}) %collective-permute-start.2) | collective-permute-done | bytes 368672 | tf_op jit(solution)/shard_map/ppermute | solution.py:589
  15.2 4.3 %collective-permute-start.4 = (bf16[2,16,48,128]{3,2,1,0:T(8,128)(2,1)}, bf16[2,16,48,128]{3,2,1,0:T(8,128)(2,1)S(1)}, u32[]{:S(2)}, u32[]{:S(2)}) collective-permute-start(bf16[2,16,48,128]{3,2,1,0:T(8,128)(2,1)} %get-tuple-element.39), channel_id=1, source_target_pairs={{0,4},{4,0},{8,12},{12,8},{16,20},{20,16},{24,28},{28,24},{1,5},{5... | collective-permute-start | bytes 1179656 | tf_op jit(solution)/shard_map/ppermute | solution.py:596
  19.5 4.2 %collective-permute-start.3 = (bf16[2,15,48,128]{3,2,1,0:T(8,128)(2,1)S(1)}, bf16[2,15,48,128]{3,2,1,0:T(8,128)(2,1)}, u32[]{:S(2)}, u32[]{:S(2)}) collective-permute-start(bf16[2,15,48,128]{3,2,1,0:T(8,128)(2,1)S(1)} %collective-permute-done.2.refs_3_), channel_id=1, source_target_pairs={{0,8},{8,16},{12,4},{16,24},{20,12},{28,20},{1,9},{9,17},{13,5},{1... | collective-permute-start | bytes 1105928 | tf_op jit(solution)/shard_map/ppermute | solution.py:594
  23.6 0.7 copy-done.5
  24.4 4.4 %collective-permute-done.3.refs_4_ = bf16[2,15,48,128]{3,2,1,0:T(8,128)(2,1)} collective-permute-done((bf16[2,15,48,128]{3,2,1,0:T(8,128)(2,1)S(1)}, bf16[2,15,48,128]{3,2,1,0:T(8,128)(2,1)}, u32[]{:S(2)}, u32[]{:S(2)}) %collective-permute-start.3) | collective-permute-done | bytes 368672 | tf_op jit(solution)/shard_map/ppermute | solution.py:594
  28.8 0.0 collective-permute-done.4.b_x.refs_4_
  28.8 3.7 %collective-permute-done.1.refs_2_ = bf16[2,27,48,128]{3,2,1,0:T(8,128)(2,1)S(1)} collective-permute-done((bf16[2,27,48,128]{3,2,1,0:T(8,128)(2,1)}, bf16[2,27,48,128]{3,2,1,0:T(8,128)(2,1)S(1)}, u32[]{:S(2)}, u32[]{:S(2)}) %collective-permute-start.1) | collective-permute-done | bytes 663584 | tf_op jit(solution)/shard_map/ppermute | solution.py:590
  32.5 1.0 %copy-done.6 = bf16[2,15,48,128]{3,2,1,0:T(8,128)(2,1)S(1)} copy-done((bf16[2,15,48,128]{3,2,1,0:T(8,128)(2,1)S(1)}, bf16[2,15,48,128]{3,2,1,0:T(8,128)(2,1)}, u32[]{:S(2)}) %copy-start.6) | copy-done | bytes 368664
  33.5 4.1 %filtered.2 = (bf16[4,10,48,128]{3,2,1,0:T(8,128)(2,1)S(1)}, bf16[2,9,48,128]{3,2,1,0:T(8,128)(2,1)S(1)}, bf16[2,9,48,128]{3,2,1,0:T(8,128)(2,1)S(1)}) custom-call(bf16[2,48,48,128]{3,2,1,0:T(8,128)(2,1)S(1)} %copy-done.1, f32[2,48,48]{2,1,0:T(8,128)S(1)} %copy-done.4, bf16[2,27,48,128]{3,2,1,0:T(8,128)(2,1)S(1)} %collective-permute-done.1.refs_2_, ...), custom_call_target="tpu_custom_call" | custom-call | flops 2457600 | bytes 15360000 | tf_op jit(solution)/shard_map/filtered/pallas_call | solution.py:454
  37.7 0.0 copy-start.7
  37.7 0.7 copy-done.7
  38.3 0.7 copy-done.9
  39.0 1.5 %collective-permute-start.7 = (bf16[4,10,48,128]{3,2,1,0:T(8,128)(2,1)S(1)}, bf16[4,10,48,128]{3,2,1,0:T(8,128)(2,1)}, u32[]{:S(2)}, u32[]{:S(2)}) collective-permute-start(bf16[4,10,48,128]{3,2,1,0:T(8,128)(2,1)S(1)} %get-tuple-element.50.refs_0_), channel_id=1, source_target_pairs={{0,2},{1,3},{2,0},{3,1},{4,6},{5,7},{6,4},{7,5},{8,10},{9,11},{10,... | collective-permute-start | bytes 1474568 | tf_op jit(solution)/shard_map/ppermute | solution.py:603
  40.6 3.7 %collective-permute-start.5 = (bf16[2,16,48,128]{3,2,1,0:T(8,128)(2,1)S(1)}, bf16[2,16,48,128]{3,2,1,0:T(8,128)(2,1)S(1)}, u32[]{:S(2)}, u32[]{:S(2)}) collective-permute-start(bf16[2,16,48,128]{3,2,1,0:T(8,128)(2,1)S(1)} %collective-permute-done.4.b_x.refs_4_), channel_id=1, source_target_pairs={{0,8},{8,16},{12,4},{16,24},{20,12},{28,20},{1,9},{9,17},{13,5},{1... | collective-permute-start | bytes 1179656 | tf_op jit(solution)/shard_map/ppermute | solution.py:597
  44.3 0.1 broadcast_select_fusion
  44.4 0.0 copy-start.8
  44.4 0.3 convolution_bitcast_fusion.gram
  44.7 3.1 %partials.1 = (f32[24,128]{1,0:T(8,128)S(1)}, bf16[2,48,24,48]{3,2,1,0:T(8,128)(2,1)S(1)}) custom-call(s32[8]{0:T(128)S(1)} %copy-done.11, bf16[2,48,48,128]{3,2,1,0:T(8,128)(2,1)S(1)} %copy-done.1, bf16[8,2,48,48]{3,2,1,0:T(8,128)(2,1)S(1)} %copy-done.3, bf16[2,16,48,128]{3,2,1,0:T(8,128)(2,1)S(1)} %collective-permute-done.4.b_x.refs_4_, ...), custom_call_target="tpu_custom_call" | custom-call | flops 256 | bytes 256 | tf_op jit(solution)/shard_map/partials/pallas_call | solution.py:198
  47.7 2.2 %collective-permute-done.5.refs_6_ = bf16[2,16,48,128]{3,2,1,0:T(8,128)(2,1)S(1)} collective-permute-done((bf16[2,16,48,128]{3,2,1,0:T(8,128)(2,1)S(1)}, bf16[2,16,48,128]{3,2,1,0:T(8,128)(2,1)S(1)}, u32[]{:S(2)}, u32[]{:S(2)}) %collective-permute-start.5) | collective-permute-done | bytes 393248 | tf_op jit(solution)/shard_map/ppermute | solution.py:597
  50.0 4.1 %filtered.3 = (bf16[2,14,48,128]{3,2,1,0:T(8,128)(2,1)S(1)}, bf16[2,14,48,128]{3,2,1,0:T(8,128)(2,1)S(1)}) custom-call(bf16[2,48,48,128]{3,2,1,0:T(8,128)(2,1)S(1)} %copy-done.1, f32[2,48,48]{2,1,0:T(8,128)S(1)} %copy-done.4, bf16[2,27,48,128]{3,2,1,0:T(8,128)(2,1)S(1)} %collective-permute-done.1.refs_2_, bf16[2,9,48,128]{3,2,1,0:T(8,128)(2,1)S(1)} %copy-done.8, ...), custom_call_target="tpu_custom_call" | custom-call | flops 3440640 | bytes 21504000 | tf_op jit(solution)/shard_map/filtered/pallas_call | solution.py:454
  54.1 0.6 collective-permute-start.6
  54.7 0.0 collective-permute-done.7.refs_2_
  54.7 0.0 collective-permute-start.8
  54.7 0.5 collective-permute-start.9
  55.3 0.3 fusion
  55.6 0.0 copy-start.12
  55.6 1.6 %collective-permute-done.8.refs_1_ = bf16[4,10,48,128]{3,2,1,0:T(8,128)(2,1)S(1)} collective-permute-done((bf16[4,10,48,128]{3,2,1,0:T(8,128)(2,1)S(1)}, bf16[4,10,48,128]{3,2,1,0:T(8,128)(2,1)S(1)}, u32[]{:S(2)}, u32[]{:S(2)}) %collective-permute-start.8) | collective-permute-done | bytes 491552 | tf_op jit(solution)/shard_map/ppermute | solution.py:626
  57.3 0.2 collective-permute-done.9.refs_3_
  57.5 1.8 %rotated.2 = (bf16[2,10,48,128]{3,2,1,0:T(8,128)(2,1)S(1)}, bf16[2,10,48,128]{3,2,1,0:T(8,128)(2,1)S(1)}) custom-call(bf16[4,10,48,128]{3,2,1,0:T(8,128)(2,1)S(1)} %get-tuple-element.50.refs_0_, bf16[4,10,48,128]{3,2,1,0:T(8,128)(2,1)S(1)} %collective-permute-done.8.refs_1_, bf16[4,10,48,128]{3,2,1,0:T(8,128)(2,1)} %collective-permute-done.7.refs_2_, ...), custom_call_target="tpu_custom_call" | custom-call | flops 15728640 | bytes 153600 | tf_op jit(solution)/shard_map/rotated/pallas_call | solution.py:498
  59.3 1.4 %collective-permute-start.10 = (bf16[2,10,48,128]{3,2,1,0:T(8,128)(2,1)S(1)}, bf16[2,10,48,128]{3,2,1,0:T(8,128)(2,1)S(1)}, u32[]{:S(2)}, u32[]{:S(2)}) collective-permute-start(bf16[2,10,48,128]{3,2,1,0:T(8,128)(2,1)S(1)} %get-tuple-element.54), channel_id=1, source_target_pairs={{0,4},{4,0},{8,12},{12,8},{16,20},{20,16},{24,28},{28,24},{1,5},{5... | collective-permute-start | bytes 737288 | tf_op jit(solution)/shard_map/ppermute | solution.py:629
  60.7 0.7 collective-permute-start.11
  61.4 6.2 %collective-permute-done.11 = f32[24,128]{1,0:T(8,128)S(1)} collective-permute-done((f32[24,128]{1,0:T(8,128)S(1)}, f32[24,128]{1,0:T(8,128)S(1)}, u32[]{:S(2)}, u32[]{:S(2)}) %collective-permute-start.11) | collective-permute-done | bytes 12320 | tf_op jit(solution)/shard_map/ppermute | solution.py:612
  67.7 2.5 %collective-permute-start.12 = (f32[24,128]{1,0:T(8,128)S(1)}, f32[24,128]{1,0:T(8,128)S(1)}, u32[]{:S(2)}, u32[]{:S(2)}) collective-permute-start(f32[24,128]{1,0:T(8,128)S(1)} %add.9), channel_id=1, source_target_pairs={{0,8},{4,12},{8,0},{12,4},{16,24},{20,28},{24,16},{28,20},{1,9},{5... | collective-permute-start | bytes 36872 | tf_op jit(solution)/shard_map/ppermute | solution.py:612
  70.2 0.0 collective-permute-start.16
  70.2 1.7 %collective-permute-done.12 = f32[24,128]{1,0:T(8,128)S(1)} collective-permute-done((f32[24,128]{1,0:T(8,128)S(1)}, f32[24,128]{1,0:T(8,128)S(1)}, u32[]{:S(2)}, u32[]{:S(2)}) %collective-permute-start.12) | collective-permute-done | bytes 12320 | tf_op jit(solution)/shard_map/ppermute | solution.py:612
  71.9 0.0 collective-permute-done.6.refs_2_
  71.9 0.0 collective-permute-done.10.got1
  71.9 0.1 collective-permute-start.17
  71.9 1.6 %collective-permute-start.20 = (bf16[2,14,48,128]{3,2,1,0:T(8,128)(2,1)S(1)}, bf16[2,14,48,128]{3,2,1,0:T(8,128)(2,1)S(1)}, u32[]{:S(2)}, u32[]{:S(2)}) collective-permute-start(bf16[2,14,48,128]{3,2,1,0:T(8,128)(2,1)S(1)} %get-tuple-element.61.a), channel_id=1, source_target_pairs={{0,2},{1,3},{2,0},{3,1},{4,6},{5,7},{6,4},{7,5},{8,10},{9,11},{10,... | collective-permute-start | bytes 1032200 | tf_op jit(solution)/shard_map/ppermute | solution.py:632
  73.5 3.0 %collective-permute-start.13 = (f32[24,128]{1,0:T(8,128)S(1)}, f32[24,128]{1,0:T(8,128)S(1)}, u32[]{:S(2)}, u32[]{:S(2)}) collective-permute-start(f32[24,128]{1,0:T(8,128)S(1)} %add.10), channel_id=1, source_target_pairs={{0,16},{4,20},{8,24},{12,28},{16,0},{20,4},{24,8},{28,12},{1,17},{... | collective-permute-start | bytes 36872 | tf_op jit(solution)/shard_map/ppermute | solution.py:612
  76.6 1.7 %collective-permute-done.13 = f32[24,128]{1,0:T(8,128)S(1)} collective-permute-done((f32[24,128]{1,0:T(8,128)S(1)}, f32[24,128]{1,0:T(8,128)S(1)}, u32[]{:S(2)}, u32[]{:S(2)}) %collective-permute-start.13) | collective-permute-done | bytes 12320 | tf_op jit(solution)/shard_map/ppermute | solution.py:612
  78.2 0.1 broadcast_in_dim.22.strength
  78.3 0.1 coefficients.1.a
  78.4 0.0 collective-permute-start.14
  78.5 0.5 collective-permute-start.19
  79.0 0.0 collective-permute-done.16.refs_1_
  79.0 0.0 collective-permute-done.17.refs_3_
  79.0 0.7 rotated.3
  79.7 0.8 collective-permute-start.18
  80.5 1.9 %collective-permute-done.20.c = bf16[2,14,48,128]{3,2,1,0:T(8,128)(2,1)S(1)} collective-permute-done((bf16[2,14,48,128]{3,2,1,0:T(8,128)(2,1)S(1)}, bf16[2,14,48,128]{3,2,1,0:T(8,128)(2,1)S(1)}, u32[]{:S(2)}, u32[]{:S(2)}) %collective-permute-start.20) | collective-permute-done | bytes 344096 | tf_op jit(solution)/shard_map/ppermute | solution.py:632
  82.4 0.0 collective-permute-start.21
  82.4 1.6 %collective-permute-start.15 = (bf16[32,128]{1,0:T(8,128)(2,1)S(1)}, bf16[32,128]{1,0:T(8,128)(2,1)S(1)}, u32[]{:S(2)}, u32[]{:S(2)}) collective-permute-start(bf16[32,128]{1,0:T(8,128)(2,1)S(1)} %pad_maximum_fusion), channel_id=1, source_target_pairs={{0,2},{1,3},{2,0},{3,1},{4,6},{5,7},{6,4},{7,5},{8,10},{9,11},{10,... | collective-permute-start | bytes 24584 | tf_op jit(solution)/shard_map/ppermute | solution.py:635
  84.0 2.1 %collective-permute-done.15 = bf16[32,128]{1,0:T(8,128)(2,1)S(1)} collective-permute-done((bf16[32,128]{1,0:T(8,128)(2,1)S(1)}, bf16[32,128]{1,0:T(8,128)(2,1)S(1)}, u32[]{:S(2)}, u32[]{:S(2)}) %collective-permute-start.15) | collective-permute-done | bytes 8224 | tf_op jit(solution)/shard_map/ppermute | solution.py:635
  86.2 1.9 %nonlocal.1.term = f32[2,48,48,128]{3,2,1,0:T(8,128)S(1)} custom-call(bf16[16,128]{1,0:T(8,128)(2,1)S(1)} %coefficients.1.a, bf16[16,128]{1,0:T(8,128)(2,1)S(1)} %collective-permute-done.14.b, bf16[16,128]{1,0:T(8,128)(2,1)S(1)} %get-tuple-element.64.c, bf16[16,128]{1,0:T(8,128)(2,1)S(1)} %get-tuple-element.63.d, bf16[4,128,128]{2,1,0:T(8,128)(2,1)S(1)} %copy.18.refs_4_.q, ...), custom_call_target="tpu_custom_call" | custom-call | flops 256 | bytes 256 | tf_op jit(solution)/shard_map/nonlocal/pallas_call | solution.py:273
  88.1 0.0 collective-permute-done.21.d
  88.1 1.7 %collective-permute-done.18.got2 = bf16[2,14,48,128]{3,2,1,0:T(8,128)(2,1)S(1)} collective-permute-done((bf16[2,14,48,128]{3,2,1,0:T(8,128)(2,1)S(1)}, bf16[2,14,48,128]{3,2,1,0:T(8,128)(2,1)S(1)}, u32[]{:S(2)}, u32[]{:S(2)}) %collective-permute-start.18) | collective-permute-done | bytes 344096 | tf_op jit(solution)/shard_map/ppermute | solution.py:639
  89.8 1.9 %assembled.1 = bf16[2,48,48,128]{3,2,1,0:T(8,128)(2,1)} custom-call(f32[2,48,48,128]{3,2,1,0:T(8,128)S(1)} %nonlocal.1.term, bf16[2,10,48,128]{3,2,1,0:T(8,128)(2,1)S(1)} %get-tuple-element.58.keep1, bf16[2,10,48,128]{3,2,1,0:T(8,128)(2,1)S(1)} %collective-permute-done.10.got1, bf16[2,14,48,128]{3,2,1,0:T(8,128)(2,1)S(1)} %collective-permute-done.18.got2, ...), custom_call_target="tpu_custom_call" | custom-call | flops 256 | bytes 256 | tf_op jit(solution)/shard_map/assembled/pallas_call | solution.py:545
  (32 shorter events, 0.1 us)
Async XLA Ops:
  0.0 55.2 %copy-start = (bf16[12,128,128]{2,1,0:T(8,128)(2,1)S(1)}, bf16[12,128,128]{2,1,0:T(8,128)(2,1)}, u32[]{:S(2)}) copy-start(bf16[12,128,128]{2,1,0:T(8,128)(2,1)} %param.13) | copy-start | bytes 1179652
  0.0 32.5 %copy-start.1 = (bf16[2,48,48,128]{3,2,1,0:T(8,128)(2,1)S(1)}, bf16[2,48,48,128]{3,2,1,0:T(8,128)(2,1)}, u32[]{:S(2)}) copy-start(bf16[2,48,48,128]{3,2,1,0:T(8,128)(2,1)} %refs_0_.3) | copy-start | bytes 3538948
  0.0 32.5 %copy-start.4 = (f32[2,48,48]{2,1,0:T(8,128)S(1)}, f32[2,48,48]{2,1,0:T(8,128)}, u32[]{:S(2)}) copy-start(f32[2,48,48]{2,1,0:T(8,128)} %refs_1_.3) | copy-start | bytes 55300
  2.2 13.0 %collective-permute-start.2 = (bf16[2,15,48,128]{3,2,1,0:T(8,128)(2,1)S(1)}, bf16[2,15,48,128]{3,2,1,0:T(8,128)(2,1)S(1)}, u32[]{:S(2)}, u32[]{:S(2)}) collective-permute-start(bf16[2,15,48,128]{3,2,1,0:T(8,128)(2,1)S(1)} %get-tuple-element.37), channel_id=1, source_target_pairs={{0,4},{4,0},{8,12},{12,8},{16,20},{20,16},{24,28},{28,24},{1,5},{5... | collective-permute-start | bytes 1105928 | tf_op jit(solution)/shard_map/ppermute | solution.py:589
  5.2 0.9 %copy-start.2 = (bf16[8,2,48,48]{3,2,1,0:T(8,128)(2,1)S(1)}, bf16[8,2,48,48]{3,2,1,0:T(8,128)(2,1)}, u32[]{:S(2)}) copy-start(bf16[8,2,48,48]{3,2,1,0:T(8,128)(2,1)} %beta.3) | copy-start | bytes 221188
  7.9 0.7 collective-permute-start
  8.5 24.0 %collective-permute-start.1 = (bf16[2,27,48,128]{3,2,1,0:T(8,128)(2,1)}, bf16[2,27,48,128]{3,2,1,0:T(8,128)(2,1)S(1)}, u32[]{:S(2)}, u32[]{:S(2)}) collective-permute-start(bf16[2,27,48,128]{3,2,1,0:T(8,128)(2,1)} %get-tuple-element.36), channel_id=1, source_target_pairs={{4,12},{8,0},{12,20},{16,8},{20,28},{24,16},{5,13},{9,1},{13,21},{... | collective-permute-start | bytes 1990664 | tf_op jit(solution)/shard_map/ppermute | solution.py:590
  15.2 13.6 %collective-permute-start.4 = (bf16[2,16,48,128]{3,2,1,0:T(8,128)(2,1)}, bf16[2,16,48,128]{3,2,1,0:T(8,128)(2,1)S(1)}, u32[]{:S(2)}, u32[]{:S(2)}) collective-permute-start(bf16[2,16,48,128]{3,2,1,0:T(8,128)(2,1)} %get-tuple-element.39), channel_id=1, source_target_pairs={{0,4},{4,0},{8,12},{12,8},{16,20},{20,16},{24,28},{28,24},{1,5},{5... | collective-permute-start | bytes 1179656 | tf_op jit(solution)/shard_map/ppermute | solution.py:596
  19.5 9.3 %collective-permute-start.3 = (bf16[2,15,48,128]{3,2,1,0:T(8,128)(2,1)S(1)}, bf16[2,15,48,128]{3,2,1,0:T(8,128)(2,1)}, u32[]{:S(2)}, u32[]{:S(2)}) collective-permute-start(bf16[2,15,48,128]{3,2,1,0:T(8,128)(2,1)S(1)} %collective-permute-done.2.refs_3_), channel_id=1, source_target_pairs={{0,8},{8,16},{12,4},{16,24},{20,12},{28,20},{1,9},{9,17},{13,5},{1... | collective-permute-start | bytes 1105928 | tf_op jit(solution)/shard_map/ppermute | solution.py:594
  23.6 0.7 copy-start.5
  24.4 16.2 %copy-start.11 = (s32[8]{0:T(128)S(1)}, s32[8]{0:T(128)}, u32[]{:S(2)}) copy-start(s32[8]{0:T(128)} %atoms.1) | copy-start | bytes 100
  24.4 19.9 %copy-start.3 = (bf16[8,2,48,48]{3,2,1,0:T(8,128)(2,1)S(1)}, bf16[8,2,48,48]{3,2,1,0:T(8,128)(2,1)}, u32[]{:S(2)}) copy-start(bf16[8,2,48,48]{3,2,1,0:T(8,128)(2,1)} %beta.3) | copy-start | bytes 221188
  32.5 1.0 %copy-start.6 = (bf16[2,15,48,128]{3,2,1,0:T(8,128)(2,1)S(1)}, bf16[2,15,48,128]{3,2,1,0:T(8,128)(2,1)}, u32[]{:S(2)}) copy-start(bf16[2,15,48,128]{3,2,1,0:T(8,128)(2,1)} %copy-done.5) | copy-start | bytes 1105924
  37.7 0.7 copy-start.7
  38.3 0.7 copy-start.9
  39.0 15.7 %collective-permute-start.7 = (bf16[4,10,48,128]{3,2,1,0:T(8,128)(2,1)S(1)}, bf16[4,10,48,128]{3,2,1,0:T(8,128)(2,1)}, u32[]{:S(2)}, u32[]{:S(2)}) collective-permute-start(bf16[4,10,48,128]{3,2,1,0:T(8,128)(2,1)S(1)} %get-tuple-element.50.refs_0_), channel_id=1, source_target_pairs={{0,2},{1,3},{2,0},{3,1},{4,6},{5,7},{6,4},{7,5},{8,10},{9,11},{10,... | collective-permute-start | bytes 1474568 | tf_op jit(solution)/shard_map/ppermute | solution.py:603
  40.6 9.4 %collective-permute-start.5 = (bf16[2,16,48,128]{3,2,1,0:T(8,128)(2,1)S(1)}, bf16[2,16,48,128]{3,2,1,0:T(8,128)(2,1)S(1)}, u32[]{:S(2)}, u32[]{:S(2)}) collective-permute-start(bf16[2,16,48,128]{3,2,1,0:T(8,128)(2,1)S(1)} %collective-permute-done.4.b_x.refs_4_), channel_id=1, source_target_pairs={{0,8},{8,16},{12,4},{16,24},{20,12},{28,20},{1,9},{9,17},{13,5},{1... | collective-permute-start | bytes 1179656 | tf_op jit(solution)/shard_map/ppermute | solution.py:597
  44.4 5.6 %copy-start.8 = (bf16[2,9,48,128]{3,2,1,0:T(8,128)(2,1)S(1)}, bf16[2,9,48,128]{3,2,1,0:T(8,128)(2,1)}, u32[]{:S(2)}) copy-start(bf16[2,9,48,128]{3,2,1,0:T(8,128)(2,1)} %copy-done.7) | copy-start | bytes 663556
  44.4 5.6 %copy-start.10 = (bf16[2,9,48,128]{3,2,1,0:T(8,128)(2,1)S(1)}, bf16[2,9,48,128]{3,2,1,0:T(8,128)(2,1)}, u32[]{:S(2)}) copy-start(bf16[2,9,48,128]{3,2,1,0:T(8,128)(2,1)} %copy-done.9) | copy-start | bytes 663556
  50.0 5.2 %copy-start.13 = (s32[12,2]{0,1:T(2,128)S(1)}, s32[12,2]{0,1:T(2,128)}, u32[]{:S(2)}) copy-start(s32[12,2]{0,1:T(2,128)} %param.12) | copy-start | bytes 292
  54.1 17.7 %collective-permute-start.6 = (bf16[2,14,48,128]{3,2,1,0:T(8,128)(2,1)S(1)}, bf16[2,14,48,128]{3,2,1,0:T(8,128)(2,1)S(1)}, u32[]{:S(2)}, u32[]{:S(2)}) collective-permute-start(bf16[2,14,48,128]{3,2,1,0:T(8,128)(2,1)S(1)} %get-tuple-element.49.refs_0_), channel_id=1, source_target_pairs={{0,2},{1,3},{2,0},{3,1},{4,6},{5,7},{6,4},{7,5},{8,10},{9,11},{10,... | collective-permute-start | bytes 1032200 | tf_op jit(solution)/shard_map/ppermute | solution.py:624
  54.7 2.5 %collective-permute-start.8 = (bf16[4,10,48,128]{3,2,1,0:T(8,128)(2,1)S(1)}, bf16[4,10,48,128]{3,2,1,0:T(8,128)(2,1)S(1)}, u32[]{:S(2)}, u32[]{:S(2)}) collective-permute-start(bf16[4,10,48,128]{3,2,1,0:T(8,128)(2,1)S(1)} %get-tuple-element.50.refs_0_), channel_id=1, source_target_pairs={{0,1},{1,0},{2,3},{3,2},{4,5},{5,4},{6,7},{7,6},{8,9},{9,8},{10,11... | collective-permute-start | bytes 1474568 | tf_op jit(solution)/shard_map/ppermute | solution.py:626
  54.7 2.8 %collective-permute-start.9 = (bf16[4,10,48,128]{3,2,1,0:T(8,128)(2,1)}, bf16[4,10,48,128]{3,2,1,0:T(8,128)(2,1)S(1)}, u32[]{:S(2)}, u32[]{:S(2)}) collective-permute-start(bf16[4,10,48,128]{3,2,1,0:T(8,128)(2,1)} %collective-permute-done.7.refs_2_), channel_id=1, source_target_pairs={{0,1},{1,0},{2,3},{3,2},{4,5},{5,4},{6,7},{7,6},{8,9},{9,8},{10,11... | collective-permute-start | bytes 1474568 | tf_op jit(solution)/shard_map/ppermute | solution.py:627
  55.6 22.6 %copy-start.12 = (f32[8]{0:T(128)S(1)}, f32[8]{0:T(128)}, u32[]{:S(2)}) copy-start(f32[8]{0:T(128)} %param.10) | copy-start | bytes 100
  59.3 12.5 %collective-permute-start.10 = (bf16[2,10,48,128]{3,2,1,0:T(8,128)(2,1)S(1)}, bf16[2,10,48,128]{3,2,1,0:T(8,128)(2,1)S(1)}, u32[]{:S(2)}, u32[]{:S(2)}) collective-permute-start(bf16[2,10,48,128]{3,2,1,0:T(8,128)(2,1)S(1)} %get-tuple-element.54), channel_id=1, source_target_pairs={{0,4},{4,0},{8,12},{12,8},{16,20},{20,16},{24,28},{28,24},{1,5},{5... | collective-permute-start | bytes 737288 | tf_op jit(solution)/shard_map/ppermute | solution.py:629
  60.7 6.9 %collective-permute-start.11 = (f32[24,128]{1,0:T(8,128)S(1)}, f32[24,128]{1,0:T(8,128)S(1)}, u32[]{:S(2)}, u32[]{:S(2)}) collective-permute-start(f32[24,128]{1,0:T(8,128)S(1)} %get-tuple-element.55), channel_id=1, source_target_pairs={{0,4},{4,0},{8,12},{12,8},{16,20},{20,16},{24,28},{28,24},{1,5},{5... | collective-permute-start | bytes 36872 | tf_op jit(solution)/shard_map/ppermute | solution.py:612
  67.7 4.2 %collective-permute-start.12 = (f32[24,128]{1,0:T(8,128)S(1)}, f32[24,128]{1,0:T(8,128)S(1)}, u32[]{:S(2)}, u32[]{:S(2)}) collective-permute-start(f32[24,128]{1,0:T(8,128)S(1)} %add.9), channel_id=1, source_target_pairs={{0,8},{4,12},{8,0},{12,4},{16,24},{20,28},{24,16},{28,20},{1,9},{5... | collective-permute-start | bytes 36872 | tf_op jit(solution)/shard_map/ppermute | solution.py:612
  70.2 8.8 %collective-permute-start.16 = (bf16[2,14,48,128]{3,2,1,0:T(8,128)(2,1)S(1)}, bf16[2,14,48,128]{3,2,1,0:T(8,128)(2,1)S(1)}, u32[]{:S(2)}, u32[]{:S(2)}) collective-permute-start(bf16[2,14,48,128]{3,2,1,0:T(8,128)(2,1)S(1)} %get-tuple-element.49.refs_0_), channel_id=1, source_target_pairs={{0,1},{1,0},{2,3},{3,2},{4,5},{5,4},{6,7},{7,6},{8,9},{9,8},{10,11... | collective-permute-start | bytes 1032200 | tf_op jit(solution)/shard_map/ppermute | solution.py:622
  71.9 7.1 %collective-permute-start.17 = (bf16[2,14,48,128]{3,2,1,0:T(8,128)(2,1)S(1)}, bf16[2,14,48,128]{3,2,1,0:T(8,128)(2,1)S(1)}, u32[]{:S(2)}, u32[]{:S(2)}) collective-permute-start(bf16[2,14,48,128]{3,2,1,0:T(8,128)(2,1)S(1)} %collective-permute-done.6.refs_2_), channel_id=1, source_target_pairs={{0,1},{1,0},{2,3},{3,2},{4,5},{5,4},{6,7},{7,6},{8,9},{9,8},{10,11... | collective-permute-start | bytes 1032200 | tf_op jit(solution)/shard_map/ppermute | solution.py:633
  71.9 10.5 %collective-permute-start.20 = (bf16[2,14,48,128]{3,2,1,0:T(8,128)(2,1)S(1)}, bf16[2,14,48,128]{3,2,1,0:T(8,128)(2,1)S(1)}, u32[]{:S(2)}, u32[]{:S(2)}) collective-permute-start(bf16[2,14,48,128]{3,2,1,0:T(8,128)(2,1)S(1)} %get-tuple-element.61.a), channel_id=1, source_target_pairs={{0,2},{1,3},{2,0},{3,1},{4,6},{5,7},{6,4},{7,5},{8,10},{9,11},{10,... | collective-permute-start | bytes 1032200 | tf_op jit(solution)/shard_map/ppermute | solution.py:632
  73.5 4.7 %collective-permute-start.13 = (f32[24,128]{1,0:T(8,128)S(1)}, f32[24,128]{1,0:T(8,128)S(1)}, u32[]{:S(2)}, u32[]{:S(2)}) collective-permute-start(f32[24,128]{1,0:T(8,128)S(1)} %add.10), channel_id=1, source_target_pairs={{0,16},{4,20},{8,24},{12,28},{16,0},{20,4},{24,8},{28,12},{1,17},{... | collective-permute-start | bytes 36872 | tf_op jit(solution)/shard_map/ppermute | solution.py:612
  78.4 4.0 %collective-permute-start.14 = (bf16[16,128]{1,0:T(8,128)(2,1)S(1)}, bf16[16,128]{1,0:T(8,128)(2,1)S(1)}, u32[]{:S(2)}, u32[]{:S(2)}) collective-permute-start(bf16[16,128]{1,0:T(8,128)(2,1)S(1)} %coefficients.1.a), channel_id=1, source_target_pairs={{0,1},{1,0},{2,3},{3,2},{4,5},{5,4},{6,7},{7,6},{8,9},{9,8},{10,11... | collective-permute-start | bytes 12296 | tf_op jit(solution)/shard_map/ppermute | solution.py:634
  78.5 9.6 %collective-permute-start.19 = (bf16[2,14,48,128]{3,2,1,0:T(8,128)(2,1)S(1)}, bf16[2,14,48,128]{3,2,1,0:T(8,128)(2,1)S(1)}, u32[]{:S(2)}, u32[]{:S(2)}) collective-permute-start(bf16[2,14,48,128]{3,2,1,0:T(8,128)(2,1)S(1)} %get-tuple-element.61.a), channel_id=1, source_target_pairs={{0,1},{1,0},{2,3},{3,2},{4,5},{5,4},{6,7},{7,6},{8,9},{9,8},{10,11... | collective-permute-start | bytes 1032200 | tf_op jit(solution)/shard_map/ppermute | solution.py:623
  79.7 10.1 %collective-permute-start.18 = (bf16[2,14,48,128]{3,2,1,0:T(8,128)(2,1)S(1)}, bf16[2,14,48,128]{3,2,1,0:T(8,128)(2,1)S(1)}, u32[]{:S(2)}, u32[]{:S(2)}) collective-permute-start(bf16[2,14,48,128]{3,2,1,0:T(8,128)(2,1)S(1)} %rotated.3), channel_id=1, source_target_pairs={{0,4},{4,0},{8,12},{12,8},{16,20},{20,16},{24,28},{28,24},{1,5},{5... | collective-permute-start | bytes 1032200 | tf_op jit(solution)/shard_map/ppermute | solution.py:639
  82.4 5.6 %collective-permute-start.21 = (bf16[2,14,48,128]{3,2,1,0:T(8,128)(2,1)S(1)}, bf16[2,14,48,128]{3,2,1,0:T(8,128)(2,1)S(1)}, u32[]{:S(2)}, u32[]{:S(2)}) collective-permute-start(bf16[2,14,48,128]{3,2,1,0:T(8,128)(2,1)S(1)} %collective-permute-done.20.c), channel_id=1, source_target_pairs={{0,1},{1,0},{2,3},{3,2},{4,5},{5,4},{6,7},{7,6},{8,9},{9,8},{10,11... | collective-permute-start | bytes 1032200 | tf_op jit(solution)/shard_map/ppermute | solution.py:641
  82.4 3.7 %collective-permute-start.15 = (bf16[32,128]{1,0:T(8,128)(2,1)S(1)}, bf16[32,128]{1,0:T(8,128)(2,1)S(1)}, u32[]{:S(2)}, u32[]{:S(2)}) collective-permute-start(bf16[32,128]{1,0:T(8,128)(2,1)S(1)} %pad_maximum_fusion), channel_id=1, source_target_pairs={{0,2},{1,3},{2,0},{3,1},{4,6},{5,7},{6,4},{7,5},{8,10},{9,11},{10,... | collective-permute-start | bytes 24584 | tf_op jit(solution)/shard_map/ppermute | solution.py:635

commit v11 on v9

--- a/solution.py
+++ b/solution.py
@@ -90,7 +90,7 @@
     )(*(pltpu.with_memory_space_constraint(a, pltpu.MemorySpace.HBM) for a in (psi, potential)))
 
 
-def pack_kernel(early, psi, beta, to_x2, sem):
+def pack_kernel(early, psi, beta, to_x2, far, sem):
     x = lax.rem(lax.axis_index("space"), 2)
     half = psi.shape[1] // 2
     later = half + 2 - early
@@ -110,6 +110,7 @@
             ).astype(BF16)
         return carry
 
+    far[...] = beta[:, x]
     lax.fori_loop(0, each, pack, 0)
     copy.wait()
 
@@ -119,12 +120,15 @@
     rows = width_x // 2 + 2 - early + beta.shape[0] // planes
     return pl.pallas_call(
         functools.partial(pack_kernel, early),
-        out_shape=jax.ShapeDtypeStruct((planes, rows, width_y, orbs), BF16),
+        out_shape=(
+            jax.ShapeDtypeStruct((planes, rows, width_y, orbs), BF16),
+            jax.ShapeDtypeStruct((beta.shape[0], *beta.shape[2:]), BF16),
+        ),
         in_specs=[
             pl.BlockSpec(memory_space=pltpu.MemorySpace.HBM),
             pl.BlockSpec(memory_space=pltpu.VMEM),
         ],
-        out_specs=pl.BlockSpec(memory_space=pltpu.VMEM),
+        out_specs=(pl.BlockSpec(memory_space=pltpu.VMEM),) * 2,
         scratch_shapes=[pltpu.SemaphoreType.DMA],
         compiler_params=params(),
         cost_estimate=cost(4096, 4096),
@@ -144,10 +148,9 @@
 
     for k in range(2):
         plane = x if k == 0 else 1 - x
-        outer, there = (b_d, beyond) if k == 0 else (b_x, side)
-        left = x == (1 if k == 0 else 0)
-        each = count // outer.shape[0]
-        begin = outer.shape[1] - each
+        there = beyond if k == 0 else side
+        each = count // b_x.shape[0]
+        begin = b_x.shape[1] - each
         u = (potential[plane] - 1.0) * 0.25
 
         def fill(i, carry):
@@ -157,8 +160,11 @@
                 next_to = (jnp.abs(there - atoms[p]) <= 1).astype(F32)
                 b32 = beta[p, plane].astype(F32) * here
                 b = b32.astype(BF16)
-                both = outer[p // each, begin + lax.rem(p, each)].astype(F32)
-                other = jnp.where(left, both[:, :width], both[:, 64 : 64 + width])
+                if k == 0:
+                    other = b_d[p].astype(F32)
+                else:
+                    both = b_x[p // each, begin + lax.rem(p, each)].astype(F32)
+                    other = jnp.where(x == 0, both[:, :width], both[:, 64 : 64 + width])
                 sides = beta[p, 1 - plane].astype(F32) * here + other * next_to
                 whole = jnp.dot(b, tri, preferred_element_type=F32)
                 whole = whole + jnp.dot(tri, b, preferred_element_type=F32)
@@ -541,7 +547,9 @@
     theirs = (half - 2) * (1 - x)
 
     to_x, to_z = prepared(psi, potential, early)
-    to_x2 = packed(psi, beta, early)
+    to_x2, far = packed(psi, beta, early)
+    raster = within([(i, i + 1 if i % 2 else i - 1) for i in range(slabs)])
+    f_d = lax.ppermute(far, "space", raster)
     xr1 = lax.ppermute(to_x, "space", swap)
     zo = lax.ppermute(to_z, "space", own_way)
     active = jnp.abs(place - atom_slab) <= 1
@@ -557,9 +565,8 @@
     operands = (psi, potential, zo)
     block1, xr_c, zf_c = filtered(slabs, 0, rows1, True, operands, (xr1,), (zf1,))
     y1 = lax.ppermute(block1, "orb", across)
-    give2, keep2 = filtered(slabs, rows1, rows2, False, operands, (xr_c, xr2), (zf_c, zf2))
-    xr2, _ = ordered(xr2, give2)
-    sums, weights = partials(count, atom_slab, psi, beta, xr2, zf2, potential, gram)
+    f_d, _ = ordered(f_d, block1)
+    sums, weights = partials(count, atom_slab, psi, beta, xr2, f_d, potential, gram)
     rounds = [1 << k for k in range((slabs - 1).bit_length())]
 
     def added(values, step):
@@ -568,6 +575,9 @@
 
     for step in rounds[:-1]:
         sums = added(sums, step)
+    zf2, sums = ordered(zf2, sums)
+    sums = added(sums, rounds[-1])
+    give2, keep2 = filtered(slabs, rows1, rows2, False, operands, (xr_c, xr2), (zf_c, zf2))
     pattern, q_tiles, _ = ordered(pattern, q_tiles, give2)
     me = lax.axis_index("orb")
     which = jnp.bitwise_xor(me, jnp.arange(groups, dtype=jnp.int32))
@@ -577,22 +587,24 @@
     cg = lax.ppermute(give2, "orb", beside)
     ck = lax.ppermute(keep2, "orb", beside)
     yg = lax.ppermute(give2, "orb", across)
-    y1, again, _ = ordered(y1, block1, give2)
+    y1, again, _, sums = ordered(y1, block1, give2, sums)
+    coefs = coefficients(sums, strong)
+    coefs = jnp.concatenate([coefs, lax.ppermute(coefs, "orb", beside)], axis=0)
     c1 = lax.ppermute(again, "orb", beside)
     yc1 = lax.ppermute(y1, "orb", beside)
     give1, keep1 = rotated((block1, c1, y1, yc1), q, 2)
     got1 = lax.ppermute(give1, "space", swap)
-    keep_y, yg, got1, sums = ordered(keep2, yg, got1, sums)
-    coefs = coefficients(added(sums, rounds[-1]), strong)
+    keep_y, yg, _ = ordered(keep2, yg, give1)
     yk = lax.ppermute(keep_y, "orb", across)
     ycg = lax.ppermute(yg, "orb", beside)
-    coefs_c = lax.ppermute(coefs, "orb", beside)
-    coefs_y = lax.ppermute(jnp.concatenate([coefs, coefs_c], axis=0), "orb", across)
-    coefs_yc, coefs_y = coefs_y[2 * count :], coefs_y[: 2 * count]
-    term = nonlocal_term(psi.shape, (coefs, coefs_c, coefs_y, coefs_yc), q, weights)
+    ycg, got1 = ordered(ycg, got1)
     (give2,) = rotated((give2, cg, yg, ycg), q, 1)
     got2 = lax.ppermute(give2, "space", swap)
-    yk, _, _ = ordered(yk, give2, coefs)
+    coefs, _ = ordered(coefs, give2)
+    coefs_y = lax.ppermute(coefs, "orb", across)
+    coefs = [half_of[k * 2 * count : (k + 1) * 2 * count] for half_of in (coefs, coefs_y) for k in (0, 1)]
+    term = nonlocal_term(psi.shape, coefs, q, weights)
+    yk, _ = ordered(yk, give2)
     yck = lax.ppermute(yk, "orb", beside)
     return assembled(term, keep1, got1, got2, (keep2, ck, yk, yck), q)
 

time: 83.8 us -> 83.1 us (level)
  starting transfers between devices: 27.6 us -> 24.4 us
  Pallas kernels: 19.3 us -> 22.1 us
  waiting for transfers between devices: 33.8 us -> 32.3 us
  local copies, waits for them, and re-layouts: 1.76 us -> 2.93 us
    ppermute x1, waiting for transfers between devices: 6.65 us -> 0.01 us  [shards(): zf1 = lax.ppermute(xr1, 'space', other_way)]
    ppermute x1, waiting for transfers between devices: 5.93 us -> 0.01 us  [shards(): zf2 = lax.ppermute(xr2, 'space', other_way)]
    ppermute x1, waiting for transfers between devices: 0.01 us -> 5.78 us  [shards(): xr2 = lax.ppermute(second, 'space', swap)]
    ppermute x1, waiting for transfers between devices: 0.01 us -> 5.33 us  [shards(): got1 = lax.ppermute(give1, 'space', swap)]
    ppermute x1, waiting for transfers between devices: 0.01 us -> 1.89 us  [shards(): yg = lax.ppermute(give2, 'orb', across)]
    ppermute x1, waiting for transfers between devices: 6.28 us -> 4.61 us  [shards(): xr1 = lax.ppermute(to_x, 'space', swap)]
    ppermute x1, waiting for transfers between devices: 2.02 us -> 0.43 us  [shards(): yk = lax.ppermute(keep_y, 'orb', across)]
    ppermute x3, starting transfers between devices: 4.98 us -> 3.63 us  [added(): return values + lax.ppermute(values, 'space', pairs)]
  transfers between devices with their start and end apart: 21 -> 22, of which waited for: 11 -> 12; matrix products, arithmetic and copies ran while one was open for 1% -> 1% of each run, Pallas kernels for 15% -> 22%
where the time goes in v11:
time: 83.1 us; the launch traced here: 82.7 us
  waiting for transfers between devices  32.3 us (39%)
  starting transfers between devices  24.4 us (29%)
  Pallas kernels  22.1 us (27%)
  local copies, waits for them, and re-layouts  2.93 us (4%)
    pallas_call x2, Pallas kernels, filtered(): pl.pallas_call(functools.partial(filter_kernel, slabs, start, parts, join...  8.49 us
    ppermute x3, waiting for transfers between devices, added(): return values + lax.ppermute(values, 'space', pairs)  6.53 us
    ppermute x1, waiting for transfers between devices, shards(): xr2 = lax.ppermute(second, 'space', swap)  5.78 us
    ppermute x1, waiting for transfers between devices, shards(): got1 = lax.ppermute(give1, 'space', swap)  5.33 us
    ppermute x1, waiting for transfers between devices, shards(): xr1 = lax.ppermute(to_x, 'space', swap)  4.61 us
    ppermute x1, starting transfers between devices, shards(): zf2 = lax.ppermute(xr2, 'space', other_way)  4.22 us
    ppermute x3, starting transfers between devices, added(): return values + lax.ppermute(values, 'space', pairs)  3.63 us
    ppermute x1, starting transfers between devices, shards(): zf1 = lax.ppermute(xr1, 'space', other_way)  3.49 us
  transfers between devices with their start and end apart: 22, of which 12 were waited for; matrix products, arithmetic and copies ran while one was open for 1% of the time, Pallas kernels for 22%

profile of v11, /device:TPU:0, one launch (start us, length us, event | category | flops | bytes accessed | tf_op | source)
XLA Modules:
  0.0 82.7 jit_solution(9723523055276293529)
XLA Ops:
  0.0 2.2 %prepared.1 = (bf16[2,15,48,128]{3,2,1,0:T(8,128)(2,1)S(1)}, bf16[2,27,48,128]{3,2,1,0:T(8,128)(2,1)}) custom-call(bf16[2,48,48,128]{3,2,1,0:T(8,128)(2,1)} %refs_0_.3, f32[2,48,48]{2,1,0:T(8,128)} %refs_1_.3), custom_call_target="tpu_custom_call" | custom-call | flops 256 | bytes 256 | tf_op jit(solution)/shard_map/prepared/pallas_call | solution.py:81
  2.2 3.0 %collective-permute-start.1 = (bf16[2,15,48,128]{3,2,1,0:T(8,128)(2,1)S(1)}, bf16[2,15,48,128]{3,2,1,0:T(8,128)(2,1)S(1)}, u32[]{:S(2)}, u32[]{:S(2)}) collective-permute-start(bf16[2,15,48,128]{3,2,1,0:T(8,128)(2,1)S(1)} %get-tuple-element.35), channel_id=1, source_target_pairs={{0,4},{4,0},{8,12},{12,8},{16,20},{20,16},{24,28},{28,24},{1,5},{5... | collective-permute-start | bytes 1105928 | tf_op jit(solution)/shard_map/ppermute | solution.py:553
  5.2 1.3 %collective-permute-start = (bf16[2,27,48,128]{3,2,1,0:T(8,128)(2,1)}, bf16[2,27,48,128]{3,2,1,0:T(8,128)(2,1)S(1)}, u32[]{:S(2)}, u32[]{:S(2)}) collective-permute-start(bf16[2,27,48,128]{3,2,1,0:T(8,128)(2,1)} %get-tuple-element.34), channel_id=1, source_target_pairs={{4,12},{8,0},{12,20},{16,8},{20,28},{24,16},{5,13},{9,1},{13,21},{... | collective-permute-start | bytes 1990664 | tf_op jit(solution)/shard_map/ppermute | solution.py:554
  6.5 0.0 copy-start.2
  6.5 0.9 %copy-done.2 = bf16[8,2,48,48]{3,2,1,0:T(8,128)(2,1)S(1)} copy-done((bf16[8,2,48,48]{3,2,1,0:T(8,128)(2,1)S(1)}, bf16[8,2,48,48]{3,2,1,0:T(8,128)(2,1)}, u32[]{:S(2)}) %copy-start.2) | copy-done | bytes 73752
  7.4 1.8 %packed.1 = (bf16[2,16,48,128]{3,2,1,0:T(8,128)(2,1)}, bf16[8,48,48]{2,1,0:T(8,128)(2,1)}) custom-call(bf16[2,48,48,128]{3,2,1,0:T(8,128)(2,1)} %refs_0_.3, bf16[8,2,48,48]{3,2,1,0:T(8,128)(2,1)S(1)} %copy-done.2), custom_call_target="tpu_custom_call" | custom-call | flops 256 | bytes 256 | tf_op jit(solution)/shard_map/packed/pallas_call | solution.py:121
  9.2 4.6 %collective-permute-done.1.refs_3_ = bf16[2,15,48,128]{3,2,1,0:T(8,128)(2,1)S(1)} collective-permute-done((bf16[2,15,48,128]{3,2,1,0:T(8,128)(2,1)S(1)}, bf16[2,15,48,128]{3,2,1,0:T(8,128)(2,1)S(1)}, u32[]{:S(2)}, u32[]{:S(2)}) %collective-permute-start.1) | collective-permute-done | bytes 368672 | tf_op jit(solution)/shard_map/ppermute | solution.py:553
  13.8 1.7 %collective-permute-start.3 = (bf16[2,16,48,128]{3,2,1,0:T(8,128)(2,1)}, bf16[2,16,48,128]{3,2,1,0:T(8,128)(2,1)S(1)}, u32[]{:S(2)}, u32[]{:S(2)}) collective-permute-start(bf16[2,16,48,128]{3,2,1,0:T(8,128)(2,1)} %get-tuple-element.37), channel_id=1, source_target_pairs={{0,4},{4,0},{8,12},{12,8},{16,20},{20,16},{24,28},{28,24},{1,5},{5... | collective-permute-start | bytes 1179656 | tf_op jit(solution)/shard_map/ppermute | solution.py:560
  15.6 3.5 %collective-permute-start.2 = (bf16[2,15,48,128]{3,2,1,0:T(8,128)(2,1)S(1)}, bf16[2,15,48,128]{3,2,1,0:T(8,128)(2,1)S(1)}, u32[]{:S(2)}, u32[]{:S(2)}) collective-permute-start(bf16[2,15,48,128]{3,2,1,0:T(8,128)(2,1)S(1)} %collective-permute-done.1.refs_3_), channel_id=1, source_target_pairs={{0,8},{8,16},{12,4},{16,24},{20,12},{28,20},{1,9},{9,17},{13,5},{1... | collective-permute-start | bytes 1105928 | tf_op jit(solution)/shard_map/ppermute | solution.py:558
  19.1 0.7 collective-permute-start.6
  19.7 5.8 %collective-permute-done.3.b_x.refs_4_ = bf16[2,16,48,128]{3,2,1,0:T(8,128)(2,1)S(1)} collective-permute-done((bf16[2,16,48,128]{3,2,1,0:T(8,128)(2,1)}, bf16[2,16,48,128]{3,2,1,0:T(8,128)(2,1)S(1)}, u32[]{:S(2)}, u32[]{:S(2)}) %collective-permute-start.3) | collective-permute-done | bytes 393248 | tf_op jit(solution)/shard_map/ppermute | solution.py:560
  25.5 4.2 %collective-permute-start.5 = (bf16[2,16,48,128]{3,2,1,0:T(8,128)(2,1)S(1)}, bf16[2,16,48,128]{3,2,1,0:T(8,128)(2,1)}, u32[]{:S(2)}, u32[]{:S(2)}) collective-permute-start(bf16[2,16,48,128]{3,2,1,0:T(8,128)(2,1)S(1)} %collective-permute-done.3.b_x.refs_4_), channel_id=1, source_target_pairs={{0,8},{8,16},{12,4},{16,24},{20,12},{28,20},{1,9},{9,17},{13,5},{1... | collective-permute-start | bytes 1179656 | tf_op jit(solution)/shard_map/ppermute | solution.py:561
  29.8 0.0 copy-start.3
  29.8 0.0 collective-permute-done.2.refs_4_
  29.8 0.0 collective-permute-done.refs_2_
  29.8 3.6 %filtered.2 = (bf16[4,10,48,128]{3,2,1,0:T(8,128)(2,1)}, bf16[2,9,48,128]{3,2,1,0:T(8,128)(2,1)S(1)}, bf16[2,9,48,128]{3,2,1,0:T(8,128)(2,1)S(1)}) custom-call(bf16[2,48,48,128]{3,2,1,0:T(8,128)(2,1)S(1)} %copy-done.1, f32[2,48,48]{2,1,0:T(8,128)S(1)} %copy-done.4, bf16[2,27,48,128]{3,2,1,0:T(8,128)(2,1)S(1)} %collective-permute-done.refs_2_, ...), custom_call_target="tpu_custom_call" | custom-call | flops 2457600 | bytes 15360000 | tf_op jit(solution)/shard_map/filtered/pallas_call | solution.py:419
  33.5 1.5 %collective-permute-start.4 = (bf16[4,10,48,128]{3,2,1,0:T(8,128)(2,1)}, bf16[4,10,48,128]{3,2,1,0:T(8,128)(2,1)}, u32[]{:S(2)}, u32[]{:S(2)}) collective-permute-start(bf16[4,10,48,128]{3,2,1,0:T(8,128)(2,1)} %get-tuple-element.50.refs_0_), channel_id=1, source_target_pairs={{0,2},{1,3},{2,0},{3,1},{4,6},{5,7},{6,4},{7,5},{8,10},{9,11},{10,... | collective-permute-start | bytes 1474568 | tf_op jit(solution)/shard_map/ppermute | solution.py:567
  35.0 0.1 broadcast_select_fusion
  35.1 0.3 convolution_bitcast_fusion.gram
  35.4 0.0 collective-permute-done.6.b_d
  35.4 3.1 %partials.1 = (f32[24,128]{1,0:T(8,128)S(1)}, bf16[2,48,24,48]{3,2,1,0:T(8,128)(2,1)S(1)}) custom-call(s32[8]{0:T(128)S(1)} %copy-done.9, bf16[2,48,48,128]{3,2,1,0:T(8,128)(2,1)S(1)} %copy-done.1, bf16[8,2,48,48]{3,2,1,0:T(8,128)(2,1)S(1)} %copy-done.3, bf16[2,16,48,128]{3,2,1,0:T(8,128)(2,1)S(1)} %collective-permute-done.3.b_x.refs_4_, ...), custom_call_target="tpu_custom_call" | custom-call | flops 256 | bytes 256 | tf_op jit(solution)/shard_map/partials/pallas_call | solution.py:198
  38.4 0.1 collective-permute-start.7
  38.5 3.7 %collective-permute-done.7 = f32[24,128]{1,0:T(8,128)S(1)} collective-permute-done((f32[24,128]{1,0:T(8,128)S(1)}, f32[24,128]{1,0:T(8,128)S(1)}, u32[]{:S(2)}, u32[]{:S(2)}) %collective-permute-start.7) | collective-permute-done | bytes 12320 | tf_op jit(solution)/shard_map/ppermute | solution.py:574
  42.2 0.8 %collective-permute-start.8 = (f32[24,128]{1,0:T(8,128)S(1)}, f32[24,128]{1,0:T(8,128)S(1)}, u32[]{:S(2)}, u32[]{:S(2)}) collective-permute-start(f32[24,128]{1,0:T(8,128)S(1)} %add.9), channel_id=1, source_target_pairs={{0,8},{4,12},{8,0},{12,4},{16,24},{20,28},{24,16},{28,20},{1,9},{5... | collective-permute-start | bytes 36872 | tf_op jit(solution)/shard_map/ppermute | solution.py:574
  43.1 2.8 %collective-permute-done.8 = f32[24,128]{1,0:T(8,128)S(1)} collective-permute-done((f32[24,128]{1,0:T(8,128)S(1)}, f32[24,128]{1,0:T(8,128)S(1)}, u32[]{:S(2)}, u32[]{:S(2)}) %collective-permute-start.8) | collective-permute-done | bytes 12320 | tf_op jit(solution)/shard_map/ppermute | solution.py:574
  45.9 0.0 collective-permute-done.5.refs_6_
  45.9 2.7 %collective-permute-start.9 = (f32[24,128]{1,0:T(8,128)S(1)}, f32[24,128]{1,0:T(8,128)S(1)}, u32[]{:S(2)}, u32[]{:S(2)}) collective-permute-start(f32[24,128]{1,0:T(8,128)S(1)} %add.10), channel_id=1, source_target_pairs={{0,16},{4,20},{8,24},{12,28},{16,0},{20,4},{24,8},{28,12},{1,17},{... | collective-permute-start | bytes 36872 | tf_op jit(solution)/shard_map/ppermute | solution.py:574
  48.6 0.9 %copy-done.6 = bf16[2,9,48,128]{3,2,1,0:T(8,128)(2,1)S(1)} copy-done((bf16[2,9,48,128]{3,2,1,0:T(8,128)(2,1)S(1)}, bf16[2,9,48,128]{3,2,1,0:T(8,128)(2,1)}, u32[]{:S(2)}) %copy-start.6) | copy-done | bytes 221208
  49.6 0.9 %copy-done.8 = bf16[2,9,48,128]{3,2,1,0:T(8,128)(2,1)S(1)} copy-done((bf16[2,9,48,128]{3,2,1,0:T(8,128)(2,1)S(1)}, bf16[2,9,48,128]{3,2,1,0:T(8,128)(2,1)}, u32[]{:S(2)}) %copy-start.8) | copy-done | bytes 221208
  50.5 4.8 %filtered.3 = (bf16[2,14,48,128]{3,2,1,0:T(8,128)(2,1)S(1)}, bf16[2,14,48,128]{3,2,1,0:T(8,128)(2,1)S(1)}) custom-call(bf16[2,48,48,128]{3,2,1,0:T(8,128)(2,1)S(1)} %copy-done.1, f32[2,48,48]{2,1,0:T(8,128)S(1)} %copy-done.4, bf16[2,27,48,128]{3,2,1,0:T(8,128)(2,1)S(1)} %collective-permute-done.refs_2_, bf16[2,9,48,128]{3,2,1,0:T(8,128)(2,1)S(1)} %copy-done.6, ...), custom_call_target="tpu_custom_call" | custom-call | flops 3440640 | bytes 21504000 | tf_op jit(solution)/shard_map/filtered/pallas_call | solution.py:419
  55.4 0.6 collective-permute-start.12
  55.9 0.0 collective-permute-done.9
  55.9 0.0 collective-permute-done.4.refs_2_
  55.9 0.1 collective-permute-start.13
  56.0 0.5 collective-permute-start.14
  56.5 0.3 fusion
  56.9 0.0 copy-start.10
  56.9 1.2 %collective-permute-done.13.refs_1_ = bf16[4,10,48,128]{3,2,1,0:T(8,128)(2,1)S(1)} collective-permute-done((bf16[4,10,48,128]{3,2,1,0:T(8,128)(2,1)}, bf16[4,10,48,128]{3,2,1,0:T(8,128)(2,1)S(1)}, u32[]{:S(2)}, u32[]{:S(2)}) %collective-permute-start.13) | collective-permute-done | bytes 491552 | tf_op jit(solution)/shard_map/ppermute | solution.py:593
  58.1 0.7 collective-permute-done.14.refs_3_
  58.8 2.0 %rotated.2 = (bf16[2,10,48,128]{3,2,1,0:T(8,128)(2,1)S(1)}, bf16[2,10,48,128]{3,2,1,0:T(8,128)(2,1)S(1)}) custom-call(bf16[4,10,48,128]{3,2,1,0:T(8,128)(2,1)} %get-tuple-element.50.refs_0_, bf16[4,10,48,128]{3,2,1,0:T(8,128)(2,1)S(1)} %collective-permute-done.13.refs_1_, bf16[4,10,48,128]{3,2,1,0:T(8,128)(2,1)} %collective-permute-done.4.refs_2_, ...), custom_call_target="tpu_custom_call" | custom-call | flops 15728640 | bytes 153600 | tf_op jit(solution)/shard_map/rotated/pallas_call | solution.py:463
  60.8 1.9 %collective-permute-done.12.refs_2_ = bf16[2,14,48,128]{3,2,1,0:T(8,128)(2,1)S(1)} collective-permute-done((bf16[2,14,48,128]{3,2,1,0:T(8,128)(2,1)S(1)}, bf16[2,14,48,128]{3,2,1,0:T(8,128)(2,1)S(1)}, u32[]{:S(2)}, u32[]{:S(2)}) %collective-permute-start.12) | collective-permute-done | bytes 344096 | tf_op jit(solution)/shard_map/ppermute | solution.py:589
  62.7 0.0 collective-permute-start.15
  62.7 0.5 collective-permute-start.11
  63.2 0.5 collective-permute-start.20
  63.7 0.7 collective-permute-start.16
  64.4 0.1 broadcast_in_dim.22.strength
  64.4 0.1 coefficients.1
  64.6 0.0 collective-permute-start.10
  64.6 1.2 %collective-permute-done.10 = bf16[16,128]{1,0:T(8,128)(2,1)S(1)} collective-permute-done((bf16[16,128]{1,0:T(8,128)(2,1)S(1)}, bf16[16,128]{1,0:T(8,128)(2,1)S(1)}, u32[]{:S(2)}, u32[]{:S(2)}) %collective-permute-start.10) | collective-permute-done | bytes 4128 | tf_op jit(solution)/shard_map/ppermute | solution.py:592
  65.8 0.2 collective-permute-start.19
  65.9 5.3 %collective-permute-done.16.got1 = bf16[2,10,48,128]{3,2,1,0:T(8,128)(2,1)S(1)} collective-permute-done((bf16[2,10,48,128]{3,2,1,0:T(8,128)(2,1)S(1)}, bf16[2,10,48,128]{3,2,1,0:T(8,128)(2,1)S(1)}, u32[]{:S(2)}, u32[]{:S(2)}) %collective-permute-start.16) | collective-permute-done | bytes 245792 | tf_op jit(solution)/shard_map/ppermute | solution.py:596
  71.3 0.0 collective-permute-done.15.refs_3_
  71.3 0.0 collective-permute-done.11.refs_1_
  71.3 0.7 rotated.3
  72.0 0.7 collective-permute-start.18
  72.7 0.4 collective-permute-done.20.c
  73.2 1.1 %collective-permute-start.17 = (bf16[32,128]{1,0:T(8,128)(2,1)S(1)}, bf16[32,128]{1,0:T(8,128)(2,1)S(1)}, u32[]{:S(2)}, u32[]{:S(2)}) collective-permute-start(bf16[32,128]{1,0:T(8,128)(2,1)S(1)} %pad_maximum_fusion), channel_id=1, source_target_pairs={{0,2},{1,3},{2,0},{3,1},{4,6},{5,7},{6,4},{7,5},{8,10},{9,11},{10,... | collective-permute-start | bytes 24584 | tf_op jit(solution)/shard_map/ppermute | solution.py:604
  74.2 0.0 collective-permute-start.21
  74.2 2.6 %collective-permute-done.17 = bf16[32,128]{1,0:T(8,128)(2,1)S(1)} collective-permute-done((bf16[32,128]{1,0:T(8,128)(2,1)S(1)}, bf16[32,128]{1,0:T(8,128)(2,1)S(1)}, u32[]{:S(2)}, u32[]{:S(2)}) %collective-permute-start.17) | collective-permute-done | bytes 8224 | tf_op jit(solution)/shard_map/ppermute | solution.py:604
  76.8 1.9 %nonlocal.1.term = f32[2,48,48,128]{3,2,1,0:T(8,128)S(1)} custom-call(bf16[16,128]{1,0:T(8,128)(2,1)S(1)} %get-tuple-element.66.a, bf16[16,128]{1,0:T(8,128)(2,1)S(1)} %get-tuple-element.65.b, bf16[16,128]{1,0:T(8,128)(2,1)S(1)} %get-tuple-element.64.c, bf16[16,128]{1,0:T(8,128)(2,1)S(1)} %get-tuple-element.63.d, bf16[4,128,128]{2,1,0:T(8,128)(2,1)S(1)} %copy.18.refs_4_.q, ...), custom_call_target="tpu_custom_call" | custom-call | flops 256 | bytes 256 | tf_op jit(solution)/shard_map/nonlocal/pallas_call | solution.py:273
  78.7 0.0 collective-permute-done.19.b
  78.7 0.0 collective-permute-done.21.d
  78.7 2.1 %collective-permute-done.18.got2 = bf16[2,14,48,128]{3,2,1,0:T(8,128)(2,1)S(1)} collective-permute-done((bf16[2,14,48,128]{3,2,1,0:T(8,128)(2,1)S(1)}, bf16[2,14,48,128]{3,2,1,0:T(8,128)(2,1)S(1)}, u32[]{:S(2)}, u32[]{:S(2)}) %collective-permute-start.18) | collective-permute-done | bytes 344096 | tf_op jit(solution)/shard_map/ppermute | solution.py:602
  80.8 1.9 %assembled.1 = bf16[2,48,48,128]{3,2,1,0:T(8,128)(2,1)} custom-call(f32[2,48,48,128]{3,2,1,0:T(8,128)S(1)} %nonlocal.1.term, bf16[2,10,48,128]{3,2,1,0:T(8,128)(2,1)S(1)} %get-tuple-element.59.keep1, bf16[2,10,48,128]{3,2,1,0:T(8,128)(2,1)S(1)} %collective-permute-done.16.got1, bf16[2,14,48,128]{3,2,1,0:T(8,128)(2,1)S(1)} %collective-permute-done.18.got2, ...), custom_call_target="tpu_custom_call" | custom-call | flops 256 | bytes 256 | tf_op jit(solution)/shard_map/assembled/pallas_call | solution.py:510
  (29 shorter events, 0.1 us)
Async XLA Ops:
  0.0 56.5 %copy-start = (bf16[12,128,128]{2,1,0:T(8,128)(2,1)S(1)}, bf16[12,128,128]{2,1,0:T(8,128)(2,1)}, u32[]{:S(2)}) copy-start(bf16[12,128,128]{2,1,0:T(8,128)(2,1)} %param.13) | copy-start | bytes 1179652
  0.0 29.8 %copy-start.1 = (bf16[2,48,48,128]{3,2,1,0:T(8,128)(2,1)S(1)}, bf16[2,48,48,128]{3,2,1,0:T(8,128)(2,1)}, u32[]{:S(2)}) copy-start(bf16[2,48,48,128]{3,2,1,0:T(8,128)(2,1)} %refs_0_.3) | copy-start | bytes 3538948
  0.0 29.8 %copy-start.4 = (f32[2,48,48]{2,1,0:T(8,128)S(1)}, f32[2,48,48]{2,1,0:T(8,128)}, u32[]{:S(2)}) copy-start(f32[2,48,48]{2,1,0:T(8,128)} %refs_1_.3) | copy-start | bytes 55300
  0.0 29.7 %copy-start.9 = (s32[8]{0:T(128)S(1)}, s32[8]{0:T(128)}, u32[]{:S(2)}) copy-start(s32[8]{0:T(128)} %atoms.1) | copy-start | bytes 100
  2.2 11.6 %collective-permute-start.1 = (bf16[2,15,48,128]{3,2,1,0:T(8,128)(2,1)S(1)}, bf16[2,15,48,128]{3,2,1,0:T(8,128)(2,1)S(1)}, u32[]{:S(2)}, u32[]{:S(2)}) collective-permute-start(bf16[2,15,48,128]{3,2,1,0:T(8,128)(2,1)S(1)} %get-tuple-element.35), channel_id=1, source_target_pairs={{0,4},{4,0},{8,12},{12,8},{16,20},{20,16},{24,28},{28,24},{1,5},{5... | collective-permute-start | bytes 1105928 | tf_op jit(solution)/shard_map/ppermute | solution.py:553
  5.2 24.5 %collective-permute-start = (bf16[2,27,48,128]{3,2,1,0:T(8,128)(2,1)}, bf16[2,27,48,128]{3,2,1,0:T(8,128)(2,1)S(1)}, u32[]{:S(2)}, u32[]{:S(2)}) collective-permute-start(bf16[2,27,48,128]{3,2,1,0:T(8,128)(2,1)} %get-tuple-element.34), channel_id=1, source_target_pairs={{4,12},{8,0},{12,20},{16,8},{20,28},{24,16},{5,13},{9,1},{13,21},{... | collective-permute-start | bytes 1990664 | tf_op jit(solution)/shard_map/ppermute | solution.py:554
  6.5 0.9 %copy-start.2 = (bf16[8,2,48,48]{3,2,1,0:T(8,128)(2,1)S(1)}, bf16[8,2,48,48]{3,2,1,0:T(8,128)(2,1)}, u32[]{:S(2)}) copy-start(bf16[8,2,48,48]{3,2,1,0:T(8,128)(2,1)} %beta.3) | copy-start | bytes 221188
  13.8 11.7 %collective-permute-start.3 = (bf16[2,16,48,128]{3,2,1,0:T(8,128)(2,1)}, bf16[2,16,48,128]{3,2,1,0:T(8,128)(2,1)S(1)}, u32[]{:S(2)}, u32[]{:S(2)}) collective-permute-start(bf16[2,16,48,128]{3,2,1,0:T(8,128)(2,1)} %get-tuple-element.37), channel_id=1, source_target_pairs={{0,4},{4,0},{8,12},{12,8},{16,20},{20,16},{24,28},{28,24},{1,5},{5... | collective-permute-start | bytes 1179656 | tf_op jit(solution)/shard_map/ppermute | solution.py:560
  15.6 14.2 %collective-permute-start.2 = (bf16[2,15,48,128]{3,2,1,0:T(8,128)(2,1)S(1)}, bf16[2,15,48,128]{3,2,1,0:T(8,128)(2,1)S(1)}, u32[]{:S(2)}, u32[]{:S(2)}) collective-permute-start(bf16[2,15,48,128]{3,2,1,0:T(8,128)(2,1)S(1)} %collective-permute-done.1.refs_3_), channel_id=1, source_target_pairs={{0,8},{8,16},{12,4},{16,24},{20,12},{28,20},{1,9},{9,17},{13,5},{1... | collective-permute-start | bytes 1105928 | tf_op jit(solution)/shard_map/ppermute | solution.py:558
  19.1 16.3 %collective-permute-start.6 = (bf16[8,48,48]{2,1,0:T(8,128)(2,1)}, bf16[8,48,48]{2,1,0:T(8,128)(2,1)S(1)}, u32[]{:S(2)}, u32[]{:S(2)}) collective-permute-start(bf16[8,48,48]{2,1,0:T(8,128)(2,1)} %get-tuple-element.42), channel_id=1, source_target_pairs={{4,8},{8,4},{12,16},{16,12},{20,24},{24,20},{5,9},{9,5},{13,17},{1... | collective-permute-start | bytes 110600 | tf_op jit(solution)/shard_map/ppermute | solution.py:552
  25.5 20.4 %collective-permute-start.5 = (bf16[2,16,48,128]{3,2,1,0:T(8,128)(2,1)S(1)}, bf16[2,16,48,128]{3,2,1,0:T(8,128)(2,1)}, u32[]{:S(2)}, u32[]{:S(2)}) collective-permute-start(bf16[2,16,48,128]{3,2,1,0:T(8,128)(2,1)S(1)} %collective-permute-done.3.b_x.refs_4_), channel_id=1, source_target_pairs={{0,8},{8,16},{12,4},{16,24},{20,12},{28,20},{1,9},{9,17},{13,5},{1... | collective-permute-start | bytes 1179656 | tf_op jit(solution)/shard_map/ppermute | solution.py:561
  29.8 5.2 %copy-start.3 = (bf16[8,2,48,48]{3,2,1,0:T(8,128)(2,1)S(1)}, bf16[8,2,48,48]{3,2,1,0:T(8,128)(2,1)}, u32[]{:S(2)}) copy-start(bf16[8,2,48,48]{3,2,1,0:T(8,128)(2,1)} %beta.3) | copy-start | bytes 221188
  33.5 5.0 %copy-start.5 = (bf16[2,9,48,128]{3,2,1,0:T(8,128)(2,1)}, bf16[2,9,48,128]{3,2,1,0:T(8,128)(2,1)S(1)}, u32[]{:S(2)}) copy-start(bf16[2,9,48,128]{3,2,1,0:T(8,128)(2,1)S(1)} %get-tuple-element.40.refs_3_) | copy-start | bytes 663556
  33.5 5.0 %copy-start.7 = (bf16[2,9,48,128]{3,2,1,0:T(8,128)(2,1)}, bf16[2,9,48,128]{3,2,1,0:T(8,128)(2,1)S(1)}, u32[]{:S(2)}) copy-start(bf16[2,9,48,128]{3,2,1,0:T(8,128)(2,1)S(1)} %get-tuple-element.41.refs_5_) | copy-start | bytes 663556
  33.5 22.5 %collective-permute-start.4 = (bf16[4,10,48,128]{3,2,1,0:T(8,128)(2,1)}, bf16[4,10,48,128]{3,2,1,0:T(8,128)(2,1)}, u32[]{:S(2)}, u32[]{:S(2)}) collective-permute-start(bf16[4,10,48,128]{3,2,1,0:T(8,128)(2,1)} %get-tuple-element.50.refs_0_), channel_id=1, source_target_pairs={{0,2},{1,3},{2,0},{3,1},{4,6},{5,7},{6,4},{7,5},{8,10},{9,11},{10,... | collective-permute-start | bytes 1474568 | tf_op jit(solution)/shard_map/ppermute | solution.py:567
  38.4 3.8 %collective-permute-start.7 = (f32[24,128]{1,0:T(8,128)S(1)}, f32[24,128]{1,0:T(8,128)S(1)}, u32[]{:S(2)}, u32[]{:S(2)}) collective-permute-start(f32[24,128]{1,0:T(8,128)S(1)} %get-tuple-element.44), channel_id=1, source_target_pairs={{0,4},{4,0},{8,12},{12,8},{16,20},{20,16},{24,28},{28,24},{1,5},{5... | collective-permute-start | bytes 36872 | tf_op jit(solution)/shard_map/ppermute | solution.py:574
  42.2 3.7 %collective-permute-start.8 = (f32[24,128]{1,0:T(8,128)S(1)}, f32[24,128]{1,0:T(8,128)S(1)}, u32[]{:S(2)}, u32[]{:S(2)}) collective-permute-start(f32[24,128]{1,0:T(8,128)S(1)} %add.9), channel_id=1, source_target_pairs={{0,8},{4,12},{8,0},{12,4},{16,24},{20,28},{24,16},{28,20},{1,9},{5... | collective-permute-start | bytes 36872 | tf_op jit(solution)/shard_map/ppermute | solution.py:574
  45.9 10.0 %collective-permute-start.9 = (f32[24,128]{1,0:T(8,128)S(1)}, f32[24,128]{1,0:T(8,128)S(1)}, u32[]{:S(2)}, u32[]{:S(2)}) collective-permute-start(f32[24,128]{1,0:T(8,128)S(1)} %add.10), channel_id=1, source_target_pairs={{0,16},{4,20},{8,24},{12,28},{16,0},{20,4},{24,8},{28,12},{1,17},{... | collective-permute-start | bytes 36872 | tf_op jit(solution)/shard_map/ppermute | solution.py:574
  48.6 0.9 %copy-start.6 = (bf16[2,9,48,128]{3,2,1,0:T(8,128)(2,1)S(1)}, bf16[2,9,48,128]{3,2,1,0:T(8,128)(2,1)}, u32[]{:S(2)}) copy-start(bf16[2,9,48,128]{3,2,1,0:T(8,128)(2,1)} %copy-done.5) | copy-start | bytes 663556
  49.6 0.9 %copy-start.8 = (bf16[2,9,48,128]{3,2,1,0:T(8,128)(2,1)S(1)}, bf16[2,9,48,128]{3,2,1,0:T(8,128)(2,1)}, u32[]{:S(2)}) copy-start(bf16[2,9,48,128]{3,2,1,0:T(8,128)(2,1)} %copy-done.7) | copy-start | bytes 663556
  50.5 6.0 %copy-start.11 = (s32[12,2]{0,1:T(2,128)S(1)}, s32[12,2]{0,1:T(2,128)}, u32[]{:S(2)}) copy-start(s32[12,2]{0,1:T(2,128)} %param.12) | copy-start | bytes 292
  55.4 7.3 %collective-permute-start.12 = (bf16[2,14,48,128]{3,2,1,0:T(8,128)(2,1)S(1)}, bf16[2,14,48,128]{3,2,1,0:T(8,128)(2,1)S(1)}, u32[]{:S(2)}, u32[]{:S(2)}) collective-permute-start(bf16[2,14,48,128]{3,2,1,0:T(8,128)(2,1)S(1)} %get-tuple-element.46.refs_0_), channel_id=1, source_target_pairs={{0,2},{1,3},{2,0},{3,1},{4,6},{5,7},{6,4},{7,5},{8,10},{9,11},{10,... | collective-permute-start | bytes 1032200 | tf_op jit(solution)/shard_map/ppermute | solution.py:589
  55.9 2.1 %collective-permute-start.13 = (bf16[4,10,48,128]{3,2,1,0:T(8,128)(2,1)}, bf16[4,10,48,128]{3,2,1,0:T(8,128)(2,1)S(1)}, u32[]{:S(2)}, u32[]{:S(2)}) collective-permute-start(bf16[4,10,48,128]{3,2,1,0:T(8,128)(2,1)} %get-tuple-element.50.refs_0_), channel_id=1, source_target_pairs={{0,1},{1,0},{2,3},{3,2},{4,5},{5,4},{6,7},{7,6},{8,9},{9,8},{10,11... | collective-permute-start | bytes 1474568 | tf_op jit(solution)/shard_map/ppermute | solution.py:593
  56.0 2.8 %collective-permute-start.14 = (bf16[4,10,48,128]{3,2,1,0:T(8,128)(2,1)}, bf16[4,10,48,128]{3,2,1,0:T(8,128)(2,1)S(1)}, u32[]{:S(2)}, u32[]{:S(2)}) collective-permute-start(bf16[4,10,48,128]{3,2,1,0:T(8,128)(2,1)} %collective-permute-done.4.refs_2_), channel_id=1, source_target_pairs={{0,1},{1,0},{2,3},{3,2},{4,5},{5,4},{6,7},{7,6},{8,9},{9,8},{10,11... | collective-permute-start | bytes 1474568 | tf_op jit(solution)/shard_map/ppermute | solution.py:594
  56.9 7.5 %copy-start.10 = (f32[8]{0:T(128)S(1)}, f32[8]{0:T(128)}, u32[]{:S(2)}) copy-start(f32[8]{0:T(128)} %param.10) | copy-start | bytes 100
  62.7 8.6 %collective-permute-start.15 = (bf16[2,14,48,128]{3,2,1,0:T(8,128)(2,1)S(1)}, bf16[2,14,48,128]{3,2,1,0:T(8,128)(2,1)S(1)}, u32[]{:S(2)}, u32[]{:S(2)}) collective-permute-start(bf16[2,14,48,128]{3,2,1,0:T(8,128)(2,1)S(1)} %collective-permute-done.12.refs_2_), channel_id=1, source_target_pairs={{0,1},{1,0},{2,3},{3,2},{4,5},{5,4},{6,7},{7,6},{8,9},{9,8},{10,11... | collective-permute-start | bytes 1032200 | tf_op jit(solution)/shard_map/ppermute | solution.py:599
  62.7 8.6 %collective-permute-start.11 = (bf16[2,14,48,128]{3,2,1,0:T(8,128)(2,1)S(1)}, bf16[2,14,48,128]{3,2,1,0:T(8,128)(2,1)S(1)}, u32[]{:S(2)}, u32[]{:S(2)}) collective-permute-start(bf16[2,14,48,128]{3,2,1,0:T(8,128)(2,1)S(1)} %get-tuple-element.46.refs_0_), channel_id=1, source_target_pairs={{0,1},{1,0},{2,3},{3,2},{4,5},{5,4},{6,7},{7,6},{8,9},{9,8},{10,11... | collective-permute-start | bytes 1032200 | tf_op jit(solution)/shard_map/ppermute | solution.py:587
  63.2 10.0 %collective-permute-start.20 = (bf16[2,14,48,128]{3,2,1,0:T(8,128)(2,1)S(1)}, bf16[2,14,48,128]{3,2,1,0:T(8,128)(2,1)S(1)}, u32[]{:S(2)}, u32[]{:S(2)}) collective-permute-start(bf16[2,14,48,128]{3,2,1,0:T(8,128)(2,1)S(1)} %get-tuple-element.61.a), channel_id=1, source_target_pairs={{0,2},{1,3},{2,0},{3,1},{4,6},{5,7},{6,4},{7,5},{8,10},{9,11},{10,... | collective-permute-start | bytes 1032200 | tf_op jit(solution)/shard_map/ppermute | solution.py:598
  63.7 7.6 %collective-permute-start.16 = (bf16[2,10,48,128]{3,2,1,0:T(8,128)(2,1)S(1)}, bf16[2,10,48,128]{3,2,1,0:T(8,128)(2,1)S(1)}, u32[]{:S(2)}, u32[]{:S(2)}) collective-permute-start(bf16[2,10,48,128]{3,2,1,0:T(8,128)(2,1)S(1)} %get-tuple-element.54), channel_id=1, source_target_pairs={{0,4},{4,0},{8,12},{12,8},{16,20},{20,16},{24,28},{28,24},{1,5},{5... | collective-permute-start | bytes 737288 | tf_op jit(solution)/shard_map/ppermute | solution.py:596
  64.6 1.2 %collective-permute-start.10 = (bf16[16,128]{1,0:T(8,128)(2,1)S(1)}, bf16[16,128]{1,0:T(8,128)(2,1)S(1)}, u32[]{:S(2)}, u32[]{:S(2)}) collective-permute-start(bf16[16,128]{1,0:T(8,128)(2,1)S(1)} %coefficients.1), channel_id=1, source_target_pairs={{0,1},{1,0},{2,3},{3,2},{4,5},{5,4},{6,7},{7,6},{8,9},{9,8},{10,11... | collective-permute-start | bytes 12296 | tf_op jit(solution)/shard_map/ppermute | solution.py:592
  65.8 12.9 %collective-permute-start.19 = (bf16[2,14,48,128]{3,2,1,0:T(8,128)(2,1)S(1)}, bf16[2,14,48,128]{3,2,1,0:T(8,128)(2,1)S(1)}, u32[]{:S(2)}, u32[]{:S(2)}) collective-permute-start(bf16[2,14,48,128]{3,2,1,0:T(8,128)(2,1)S(1)} %get-tuple-element.61.a), channel_id=1, source_target_pairs={{0,1},{1,0},{2,3},{3,2},{4,5},{5,4},{6,7},{7,6},{8,9},{9,8},{10,11... | collective-permute-start | bytes 1032200 | tf_op jit(solution)/shard_map/ppermute | solution.py:588
  72.0 8.9 %collective-permute-start.18 = (bf16[2,14,48,128]{3,2,1,0:T(8,128)(2,1)S(1)}, bf16[2,14,48,128]{3,2,1,0:T(8,128)(2,1)S(1)}, u32[]{:S(2)}, u32[]{:S(2)}) collective-permute-start(bf16[2,14,48,128]{3,2,1,0:T(8,128)(2,1)S(1)} %rotated.3), channel_id=1, source_target_pairs={{0,4},{4,0},{8,12},{12,8},{16,20},{20,16},{24,28},{28,24},{1,5},{5... | collective-permute-start | bytes 1032200 | tf_op jit(solution)/shard_map/ppermute | solution.py:602
  73.2 3.7 %collective-permute-start.17 = (bf16[32,128]{1,0:T(8,128)(2,1)S(1)}, bf16[32,128]{1,0:T(8,128)(2,1)S(1)}, u32[]{:S(2)}, u32[]{:S(2)}) collective-permute-start(bf16[32,128]{1,0:T(8,128)(2,1)S(1)} %pad_maximum_fusion), channel_id=1, source_target_pairs={{0,2},{1,3},{2,0},{3,1},{4,6},{5,7},{6,4},{7,5},{8,10},{9,11},{10,... | collective-permute-start | bytes 24584 | tf_op jit(solution)/shard_map/ppermute | solution.py:604
  74.2 4.5 %collective-permute-start.21 = (bf16[2,14,48,128]{3,2,1,0:T(8,128)(2,1)S(1)}, bf16[2,14,48,128]{3,2,1,0:T(8,128)(2,1)S(1)}, u32[]{:S(2)}, u32[]{:S(2)}) collective-permute-start(bf16[2,14,48,128]{3,2,1,0:T(8,128)(2,1)S(1)} %collective-permute-done.20.c), channel_id=1, source_target_pairs={{0,1},{1,0},{2,3},{3,2},{4,5},{5,4},{6,7},{7,6},{8,9},{9,8},{10,11... | collective-permute-start | bytes 1032200 | tf_op jit(solution)/shard_map/ppermute | solution.py:608

commit v12 on v11

--- a/solution.py
+++ b/solution.py
@@ -573,10 +573,7 @@
         pairs = [(i, i ^ step) for i in range(slabs)]
         return values + lax.ppermute(values, "space", pairs)
 
-    for step in rounds[:-1]:
-        sums = added(sums, step)
     zf2, sums = ordered(zf2, sums)
-    sums = added(sums, rounds[-1])
     give2, keep2 = filtered(slabs, rows1, rows2, False, operands, (xr_c, xr2), (zf_c, zf2))
     pattern, q_tiles, _ = ordered(pattern, q_tiles, give2)
     me = lax.axis_index("orb")
@@ -587,17 +584,22 @@
     cg = lax.ppermute(give2, "orb", beside)
     ck = lax.ppermute(keep2, "orb", beside)
     yg = lax.ppermute(give2, "orb", across)
+    sums = added(sums, rounds[0])
     y1, again, _, sums = ordered(y1, block1, give2, sums)
+    c1 = lax.ppermute(again, "orb", beside)
+    yc1 = lax.ppermute(y1, "orb", beside)
+    sums = added(sums, rounds[1])
+    yc1, sums = ordered(yc1, sums)
+    give1, keep1 = rotated((block1, c1, y1, yc1), q, 2)
+    got1 = lax.ppermute(give1, "space", swap)
+    keep_y, yg, _, sums = ordered(keep2, yg, give1, sums)
+    yk = lax.ppermute(keep_y, "orb", across)
+    ycg = lax.ppermute(yg, "orb", beside)
+    for step in rounds[2:]:
+        sums = added(sums, step)
+    ycg, sums, got1 = ordered(ycg, sums, got1)
     coefs = coefficients(sums, strong)
     coefs = jnp.concatenate([coefs, lax.ppermute(coefs, "orb", beside)], axis=0)
-    c1 = lax.ppermute(again, "orb", beside)
-    yc1 = lax.ppermute(y1, "orb", beside)
-    give1, keep1 = rotated((block1, c1, y1, yc1), q, 2)
-    got1 = lax.ppermute(give1, "space", swap)
-    keep_y, yg, _ = ordered(keep2, yg, give1)
-    yk = lax.ppermute(keep_y, "orb", across)
-    ycg = lax.ppermute(yg, "orb", beside)
-    ycg, got1 = ordered(ycg, got1)
     (give2,) = rotated((give2, cg, yg, ycg), q, 1)
     got2 = lax.ppermute(give2, "space", swap)
     coefs, _ = ordered(coefs, give2)

time: 83.1 us -> 80.8 us (0.972)
  waiting for transfers between devices: 32.3 us -> 23.2 us
  starting transfers between devices: 24.4 us -> 29.9 us
  local copies, waits for them, and re-layouts: 2.93 us -> 4.15 us
    ppermute x1, waiting for transfers between devices: 5.78 us -> 0.01 us  [shards(): xr2 = lax.ppermute(second, 'space', swap)]
    ppermute x1, waiting for transfers between devices: 0.01 us -> 4.48 us  [shards(): zf1 = lax.ppermute(xr1, 'space', other_way)]
    ppermute x1, waiting for transfers between devices: 5.33 us -> 1.88 us  [shards(): got1 = lax.ppermute(give1, 'space', swap)]
    ppermute x3, waiting for transfers between devices: 6.53 us -> 3.81 us  [added(): return values + lax.ppermute(values, 'space', pairs)]
    ppermute x3, starting transfers between devices: 3.63 us -> 5.84 us  [added(): return values + lax.ppermute(values, 'space', pairs)]
    ppermute x1, waiting for transfers between devices: 0.01 us -> 1.78 us  [shards(): zf2 = lax.ppermute(xr2, 'space', other_way)]
    ppermute x1, waiting for transfers between devices: 1.89 us -> 0.13 us  [shards(): yg = lax.ppermute(give2, 'orb', across)]
    unnamed x24 -> x28, local copies, waits for them, and re-layouts: 2.83 us -> 4.06 us
  transfers between devices with their start and end apart: 22 -> 22, of which waited for: 12 -> 9; matrix products, arithmetic and copies ran while one was open for 1% -> 1% of each run, Pallas kernels for 22% -> 22%
where the time goes in v12:
time: 80.8 us; the launch traced here: 80.4 us
  starting transfers between devices  29.9 us (37%)
  waiting for transfers between devices  23.2 us (29%)
  Pallas kernels  22.1 us (27%)
  local copies, waits for them, and re-layouts  4.15 us (5%)
    pallas_call x2, Pallas kernels, filtered(): pl.pallas_call(functools.partial(filter_kernel, slabs, start, parts, join...  8.71 us
    ppermute x3, starting transfers between devices, added(): return values + lax.ppermute(values, 'space', pairs)  5.84 us
    ppermute x1, starting transfers between devices, shards(): zf2 = lax.ppermute(xr2, 'space', other_way)  5.22 us
    ppermute x1, waiting for transfers between devices, shards(): xr1 = lax.ppermute(to_x, 'space', swap)  4.62 us
    ppermute x1, waiting for transfers between devices, shards(): zf1 = lax.ppermute(xr1, 'space', other_way)  4.48 us
    ppermute x1, starting transfers between devices, shards(): zf1 = lax.ppermute(xr1, 'space', other_way)  4.24 us
    unnamed x28, local copies, waits for them, and re-layouts  4.06 us
    ppermute x3, waiting for transfers between devices, added(): return values + lax.ppermute(values, 'space', pairs)  3.81 us
  transfers between devices with their start and end apart: 22, of which 9 were waited for; matrix products, arithmetic and copies ran while one was open for 1% of the time, Pallas kernels for 22%

profile of v12, /device:TPU:0, one launch (start us, length us, event | category | flops | bytes accessed | tf_op | source)
XLA Modules:
  0.0 80.4 jit_solution(15036393689761527217)
XLA Ops:
  0.0 2.2 %prepared.1 = (bf16[2,15,48,128]{3,2,1,0:T(8,128)(2,1)S(1)}, bf16[2,27,48,128]{3,2,1,0:T(8,128)(2,1)}) custom-call(bf16[2,48,48,128]{3,2,1,0:T(8,128)(2,1)} %refs_0_.3, f32[2,48,48]{2,1,0:T(8,128)} %refs_1_.3), custom_call_target="tpu_custom_call" | custom-call | flops 256 | bytes 256 | tf_op jit(solution)/shard_map/prepared/pallas_call | solution.py:81
  2.2 3.0 %collective-permute-start.1 = (bf16[2,15,48,128]{3,2,1,0:T(8,128)(2,1)S(1)}, bf16[2,15,48,128]{3,2,1,0:T(8,128)(2,1)S(1)}, u32[]{:S(2)}, u32[]{:S(2)}) collective-permute-start(bf16[2,15,48,128]{3,2,1,0:T(8,128)(2,1)S(1)} %get-tuple-element.39), channel_id=1, source_target_pairs={{0,4},{4,0},{8,12},{12,8},{16,20},{20,16},{24,28},{28,24},{1,5},{5... | collective-permute-start | bytes 1105928 | tf_op jit(solution)/shard_map/ppermute | solution.py:553
  5.2 1.3 %collective-permute-start = (bf16[2,27,48,128]{3,2,1,0:T(8,128)(2,1)}, bf16[2,27,48,128]{3,2,1,0:T(8,128)(2,1)S(1)}, u32[]{:S(2)}, u32[]{:S(2)}) collective-permute-start(bf16[2,27,48,128]{3,2,1,0:T(8,128)(2,1)} %get-tuple-element.38), channel_id=1, source_target_pairs={{4,12},{8,0},{12,20},{16,8},{20,28},{24,16},{5,13},{9,1},{13,21},{... | collective-permute-start | bytes 1990664 | tf_op jit(solution)/shard_map/ppermute | solution.py:554
  6.5 0.0 copy-start.2
  6.5 0.9 %copy-done.2 = bf16[8,2,48,48]{3,2,1,0:T(8,128)(2,1)S(1)} copy-done((bf16[8,2,48,48]{3,2,1,0:T(8,128)(2,1)S(1)}, bf16[8,2,48,48]{3,2,1,0:T(8,128)(2,1)}, u32[]{:S(2)}) %copy-start.2) | copy-done | bytes 73752
  7.4 1.7 %packed.1 = (bf16[2,16,48,128]{3,2,1,0:T(8,128)(2,1)}, bf16[8,48,48]{2,1,0:T(8,128)(2,1)}) custom-call(bf16[2,48,48,128]{3,2,1,0:T(8,128)(2,1)} %refs_0_.3, bf16[8,2,48,48]{3,2,1,0:T(8,128)(2,1)S(1)} %copy-done.2), custom_call_target="tpu_custom_call" | custom-call | flops 256 | bytes 256 | tf_op jit(solution)/shard_map/packed/pallas_call | solution.py:121
  9.2 4.6 %collective-permute-done.1.refs_3_ = bf16[2,15,48,128]{3,2,1,0:T(8,128)(2,1)S(1)} collective-permute-done((bf16[2,15,48,128]{3,2,1,0:T(8,128)(2,1)S(1)}, bf16[2,15,48,128]{3,2,1,0:T(8,128)(2,1)S(1)}, u32[]{:S(2)}, u32[]{:S(2)}) %collective-permute-start.1) | collective-permute-done | bytes 368672 | tf_op jit(solution)/shard_map/ppermute | solution.py:553
  13.8 1.7 %collective-permute-start.3 = (bf16[2,16,48,128]{3,2,1,0:T(8,128)(2,1)}, bf16[2,16,48,128]{3,2,1,0:T(8,128)(2,1)S(1)}, u32[]{:S(2)}, u32[]{:S(2)}) collective-permute-start(bf16[2,16,48,128]{3,2,1,0:T(8,128)(2,1)} %get-tuple-element.41), channel_id=1, source_target_pairs={{0,4},{4,0},{8,12},{12,8},{16,20},{20,16},{24,28},{28,24},{1,5},{5... | collective-permute-start | bytes 1179656 | tf_op jit(solution)/shard_map/ppermute | solution.py:560
  15.5 4.2 %collective-permute-start.2 = (bf16[2,15,48,128]{3,2,1,0:T(8,128)(2,1)S(1)}, bf16[2,15,48,128]{3,2,1,0:T(8,128)(2,1)}, u32[]{:S(2)}, u32[]{:S(2)}) collective-permute-start(bf16[2,15,48,128]{3,2,1,0:T(8,128)(2,1)S(1)} %collective-permute-done.1.refs_3_), channel_id=1, source_target_pairs={{0,8},{8,16},{12,4},{16,24},{20,12},{28,20},{1,9},{9,17},{13,5},{1... | collective-permute-start | bytes 1105928 | tf_op jit(solution)/shard_map/ppermute | solution.py:558
  19.8 0.7 copy-done.5
  20.5 0.7 collective-permute-start.5
  21.2 0.0 copy-start.11
  21.2 0.0 copy-start.3
  21.2 4.5 %collective-permute-done.2.refs_4_ = bf16[2,15,48,128]{3,2,1,0:T(8,128)(2,1)} collective-permute-done((bf16[2,15,48,128]{3,2,1,0:T(8,128)(2,1)S(1)}, bf16[2,15,48,128]{3,2,1,0:T(8,128)(2,1)}, u32[]{:S(2)}, u32[]{:S(2)}) %collective-permute-start.2) | collective-permute-done | bytes 368672 | tf_op jit(solution)/shard_map/ppermute | solution.py:558
  25.7 0.0 collective-permute-done.3.b_x.refs_4_
  25.7 0.0 collective-permute-done.refs_2_
  25.7 1.0 %copy-done.6 = bf16[2,15,48,128]{3,2,1,0:T(8,128)(2,1)S(1)} copy-done((bf16[2,15,48,128]{3,2,1,0:T(8,128)(2,1)S(1)}, bf16[2,15,48,128]{3,2,1,0:T(8,128)(2,1)}, u32[]{:S(2)}) %copy-start.6) | copy-done | bytes 368664
  26.7 3.9 %filtered.2 = (bf16[4,10,48,128]{3,2,1,0:T(8,128)(2,1)S(1)}, bf16[2,9,48,128]{3,2,1,0:T(8,128)(2,1)S(1)}, bf16[2,9,48,128]{3,2,1,0:T(8,128)(2,1)S(1)}) custom-call(bf16[2,48,48,128]{3,2,1,0:T(8,128)(2,1)S(1)} %copy-done.1, f32[2,48,48]{2,1,0:T(8,128)S(1)} %copy-done.4, bf16[2,27,48,128]{3,2,1,0:T(8,128)(2,1)S(1)} %collective-permute-done.refs_2_, ...), custom_call_target="tpu_custom_call" | custom-call | flops 2457600 | bytes 15360000 | tf_op jit(solution)/shard_map/filtered/pallas_call | solution.py:419
  30.6 0.0 copy-start.7
  30.6 0.7 copy-done.7
  31.3 0.7 copy-done.9
  32.0 1.5 %collective-permute-start.7 = (bf16[4,10,48,128]{3,2,1,0:T(8,128)(2,1)S(1)}, bf16[4,10,48,128]{3,2,1,0:T(8,128)(2,1)}, u32[]{:S(2)}, u32[]{:S(2)}) collective-permute-start(bf16[4,10,48,128]{3,2,1,0:T(8,128)(2,1)S(1)} %get-tuple-element.53.refs_0_), channel_id=1, source_target_pairs={{0,2},{1,3},{2,0},{3,1},{4,6},{5,7},{6,4},{7,5},{8,10},{9,11},{10,... | collective-permute-start | bytes 1474568 | tf_op jit(solution)/shard_map/ppermute | solution.py:567
  33.5 5.2 %collective-permute-start.4 = (bf16[2,16,48,128]{3,2,1,0:T(8,128)(2,1)S(1)}, bf16[2,16,48,128]{3,2,1,0:T(8,128)(2,1)}, u32[]{:S(2)}, u32[]{:S(2)}) collective-permute-start(bf16[2,16,48,128]{3,2,1,0:T(8,128)(2,1)S(1)} %collective-permute-done.3.b_x.refs_4_), channel_id=1, source_target_pairs={{0,8},{8,16},{12,4},{16,24},{20,12},{28,20},{1,9},{9,17},{13,5},{1... | collective-permute-start | bytes 1179656 | tf_op jit(solution)/shard_map/ppermute | solution.py:561
  38.7 0.1 broadcast_select_fusion
  38.8 0.3 convolution_bitcast_fusion.gram
  39.1 0.0 collective-permute-done.5.b_d
  39.1 3.1 %partials.1 = (f32[24,128]{1,0:T(8,128)S(1)}, bf16[2,48,24,48]{3,2,1,0:T(8,128)(2,1)S(1)}) custom-call(s32[8]{0:T(128)S(1)} %copy-done.11, bf16[2,48,48,128]{3,2,1,0:T(8,128)(2,1)S(1)} %copy-done.1, bf16[8,2,48,48]{3,2,1,0:T(8,128)(2,1)S(1)} %copy-done.3, bf16[2,16,48,128]{3,2,1,0:T(8,128)(2,1)S(1)} %collective-permute-done.3.b_x.refs_4_, ...), custom_call_target="tpu_custom_call" | custom-call | flops 256 | bytes 256 | tf_op jit(solution)/shard_map/partials/pallas_call | solution.py:198
  42.2 1.8 %collective-permute-done.4.refs_6_ = bf16[2,16,48,128]{3,2,1,0:T(8,128)(2,1)} collective-permute-done((bf16[2,16,48,128]{3,2,1,0:T(8,128)(2,1)S(1)}, bf16[2,16,48,128]{3,2,1,0:T(8,128)(2,1)}, u32[]{:S(2)}, u32[]{:S(2)}) %collective-permute-start.4) | collective-permute-done | bytes 393248 | tf_op jit(solution)/shard_map/ppermute | solution.py:561
  44.0 1.5 %collective-permute-start.8 = (f32[24,128]{1,0:T(8,128)S(1)}, f32[24,128]{1,0:T(8,128)S(1)}, u32[]{:S(2)}, u32[]{:S(2)}) collective-permute-start(f32[24,128]{1,0:T(8,128)S(1)} %get-tuple-element.52), channel_id=1, source_target_pairs={{0,4},{4,0},{8,12},{12,8},{16,20},{20,16},{24,28},{28,24},{1,5},{5... | collective-permute-start | bytes 36872 | tf_op jit(solution)/shard_map/ppermute | solution.py:574
  45.5 0.0 copy-start.13
  45.6 4.8 %filtered.3 = (bf16[2,14,48,128]{3,2,1,0:T(8,128)(2,1)S(1)}, bf16[2,14,48,128]{3,2,1,0:T(8,128)(2,1)S(1)}) custom-call(bf16[2,48,48,128]{3,2,1,0:T(8,128)(2,1)S(1)} %copy-done.1, f32[2,48,48]{2,1,0:T(8,128)S(1)} %copy-done.4, bf16[2,27,48,128]{3,2,1,0:T(8,128)(2,1)S(1)} %collective-permute-done.refs_2_, bf16[2,9,48,128]{3,2,1,0:T(8,128)(2,1)S(1)} %copy-done.8, ...), custom_call_target="tpu_custom_call" | custom-call | flops 3440640 | bytes 21504000 | tf_op jit(solution)/shard_map/filtered/pallas_call | solution.py:419
  50.4 1.0 %collective-permute-start.6 = (bf16[2,14,48,128]{3,2,1,0:T(8,128)(2,1)S(1)}, bf16[2,14,48,128]{3,2,1,0:T(8,128)(2,1)S(1)}, u32[]{:S(2)}, u32[]{:S(2)}) collective-permute-start(bf16[2,14,48,128]{3,2,1,0:T(8,128)(2,1)S(1)} %get-tuple-element.51.refs_0_), channel_id=1, source_target_pairs={{0,2},{1,3},{2,0},{3,1},{4,6},{5,7},{6,4},{7,5},{8,10},{9,11},{10,... | collective-permute-start | bytes 1032200 | tf_op jit(solution)/shard_map/ppermute | solution.py:586
  51.4 0.0 collective-permute-done.8
  51.4 0.0 collective-permute-done.7.refs_2_
  51.4 0.1 collective-permute-start.9
  51.5 0.5 collective-permute-start.10
  52.0 1.3 %collective-permute-start.11 = (f32[24,128]{1,0:T(8,128)S(1)}, f32[24,128]{1,0:T(8,128)S(1)}, u32[]{:S(2)}, u32[]{:S(2)}) collective-permute-start(f32[24,128]{1,0:T(8,128)S(1)} %add.9), channel_id=1, source_target_pairs={{0,8},{4,12},{8,0},{12,4},{16,24},{20,28},{24,16},{28,20},{1,9},{5... | collective-permute-start | bytes 36872 | tf_op jit(solution)/shard_map/ppermute | solution.py:574
  53.2 0.3 fusion
  53.6 0.0 copy-start.12
  53.6 2.1 %collective-permute-done.11 = f32[24,128]{1,0:T(8,128)S(1)} collective-permute-done((f32[24,128]{1,0:T(8,128)S(1)}, f32[24,128]{1,0:T(8,128)S(1)}, u32[]{:S(2)}, u32[]{:S(2)}) %collective-permute-start.11) | collective-permute-done | bytes 12320 | tf_op jit(solution)/shard_map/ppermute | solution.py:574
  55.7 0.0 collective-permute-done.10.refs_3_
  55.7 1.8 %rotated.2 = (bf16[2,10,48,128]{3,2,1,0:T(8,128)(2,1)S(1)}, bf16[2,10,48,128]{3,2,1,0:T(8,128)(2,1)S(1)}) custom-call(bf16[4,10,48,128]{3,2,1,0:T(8,128)(2,1)S(1)} %get-tuple-element.53.refs_0_, bf16[4,10,48,128]{3,2,1,0:T(8,128)(2,1)S(1)} %collective-permute-done.9.refs_1_, bf16[4,10,48,128]{3,2,1,0:T(8,128)(2,1)} %collective-permute-done.7.refs_2_, ...), custom_call_target="tpu_custom_call" | custom-call | flops 15728640 | bytes 153600 | tf_op jit(solution)/shard_map/rotated/pallas_call | solution.py:463
  57.6 0.1 collective-permute-done.6.refs_2_
  57.7 0.5 collective-permute-start.16
  58.2 1.1 %collective-permute-start.20 = (bf16[2,14,48,128]{3,2,1,0:T(8,128)(2,1)S(1)}, bf16[2,14,48,128]{3,2,1,0:T(8,128)(2,1)S(1)}, u32[]{:S(2)}, u32[]{:S(2)}) collective-permute-start(bf16[2,14,48,128]{3,2,1,0:T(8,128)(2,1)S(1)} %get-tuple-element.69.a), channel_id=1, source_target_pairs={{0,2},{1,3},{2,0},{3,1},{4,6},{5,7},{6,4},{7,5},{8,10},{9,11},{10,... | collective-permute-start | bytes 1032200 | tf_op jit(solution)/shard_map/ppermute | solution.py:596
  59.3 1.0 %collective-permute-start.14 = (bf16[2,10,48,128]{3,2,1,0:T(8,128)(2,1)S(1)}, bf16[2,10,48,128]{3,2,1,0:T(8,128)(2,1)S(1)}, u32[]{:S(2)}, u32[]{:S(2)}) collective-permute-start(bf16[2,10,48,128]{3,2,1,0:T(8,128)(2,1)S(1)} %get-tuple-element.59), channel_id=1, source_target_pairs={{0,4},{4,0},{8,12},{12,8},{16,20},{20,16},{24,28},{28,24},{1,5},{5... | collective-permute-start | bytes 737288 | tf_op jit(solution)/shard_map/ppermute | solution.py:594
  60.4 3.0 %collective-permute-start.13 = (f32[24,128]{1,0:T(8,128)S(1)}, f32[24,128]{1,0:T(8,128)S(1)}, u32[]{:S(2)}, u32[]{:S(2)}) collective-permute-start(f32[24,128]{1,0:T(8,128)S(1)} %add.10), channel_id=1, source_target_pairs={{0,16},{4,20},{8,24},{12,28},{16,0},{20,4},{24,8},{28,12},{1,17},{... | collective-permute-start | bytes 36872 | tf_op jit(solution)/shard_map/ppermute | solution.py:574
  63.4 1.7 %collective-permute-done.13 = f32[24,128]{1,0:T(8,128)S(1)} collective-permute-done((f32[24,128]{1,0:T(8,128)S(1)}, f32[24,128]{1,0:T(8,128)S(1)}, u32[]{:S(2)}, u32[]{:S(2)}) %collective-permute-start.13) | collective-permute-done | bytes 12320 | tf_op jit(solution)/shard_map/ppermute | solution.py:574
  65.1 1.9 %collective-permute-done.14.got1 = bf16[2,10,48,128]{3,2,1,0:T(8,128)(2,1)S(1)} collective-permute-done((bf16[2,10,48,128]{3,2,1,0:T(8,128)(2,1)S(1)}, bf16[2,10,48,128]{3,2,1,0:T(8,128)(2,1)S(1)}, u32[]{:S(2)}, u32[]{:S(2)}) %collective-permute-start.14) | collective-permute-done | bytes 245792 | tf_op jit(solution)/shard_map/ppermute | solution.py:594
  67.0 0.0 collective-permute-done.12.refs_3_
  67.0 0.1 broadcast_in_dim.22.strength
  67.0 0.1 coefficients.1
  67.2 0.0 collective-permute-start.15
  67.2 0.5 collective-permute-start.19
  67.7 0.0 collective-permute-done.16.refs_1_
  67.7 0.7 rotated.3
  68.4 1.1 %collective-permute-start.18 = (bf16[2,14,48,128]{3,2,1,0:T(8,128)(2,1)S(1)}, bf16[2,14,48,128]{3,2,1,0:T(8,128)(2,1)S(1)}, u32[]{:S(2)}, u32[]{:S(2)}) collective-permute-start(bf16[2,14,48,128]{3,2,1,0:T(8,128)(2,1)S(1)} %rotated.3), channel_id=1, source_target_pairs={{0,4},{4,0},{8,12},{12,8},{16,20},{20,16},{24,28},{28,24},{1,5},{5... | collective-permute-start | bytes 1032200 | tf_op jit(solution)/shard_map/ppermute | solution.py:604
  69.5 0.0 collective-permute-done.15
  69.6 0.6 collective-permute-start.17
  70.1 3.1 %collective-permute-done.17 = bf16[32,128]{1,0:T(8,128)(2,1)S(1)} collective-permute-done((bf16[32,128]{1,0:T(8,128)(2,1)S(1)}, bf16[32,128]{1,0:T(8,128)(2,1)S(1)}, u32[]{:S(2)}, u32[]{:S(2)}) %collective-permute-start.17) | collective-permute-done | bytes 8224 | tf_op jit(solution)/shard_map/ppermute | solution.py:606
  73.3 1.9 %nonlocal.1.term = f32[2,48,48,128]{3,2,1,0:T(8,128)S(1)} custom-call(bf16[16,128]{1,0:T(8,128)(2,1)S(1)} %get-tuple-element.74.a, bf16[16,128]{1,0:T(8,128)(2,1)S(1)} %get-tuple-element.73.b, bf16[16,128]{1,0:T(8,128)(2,1)S(1)} %get-tuple-element.72.c, bf16[16,128]{1,0:T(8,128)(2,1)S(1)} %get-tuple-element.71.d, bf16[4,128,128]{2,1,0:T(8,128)(2,1)S(1)} %copy.18.refs_4_.q, ...), custom_call_target="tpu_custom_call" | custom-call | flops 256 | bytes 256 | tf_op jit(solution)/shard_map/nonlocal/pallas_call | solution.py:273
  75.2 0.0 collective-permute-done.21.d
  75.2 3.3 %collective-permute-done.18.got2 = bf16[2,14,48,128]{3,2,1,0:T(8,128)(2,1)S(1)} collective-permute-done((bf16[2,14,48,128]{3,2,1,0:T(8,128)(2,1)S(1)}, bf16[2,14,48,128]{3,2,1,0:T(8,128)(2,1)S(1)}, u32[]{:S(2)}, u32[]{:S(2)}) %collective-permute-start.18) | collective-permute-done | bytes 344096 | tf_op jit(solution)/shard_map/ppermute | solution.py:604
  78.5 1.9 %assembled.1 = bf16[2,48,48,128]{3,2,1,0:T(8,128)(2,1)} custom-call(f32[2,48,48,128]{3,2,1,0:T(8,128)S(1)} %nonlocal.1.term, bf16[2,10,48,128]{3,2,1,0:T(8,128)(2,1)S(1)} %get-tuple-element.67.keep1, bf16[2,10,48,128]{3,2,1,0:T(8,128)(2,1)S(1)} %collective-permute-done.14.got1, bf16[2,14,48,128]{3,2,1,0:T(8,128)(2,1)S(1)} %collective-permute-done.18.got2, ...), custom_call_target="tpu_custom_call" | custom-call | flops 256 | bytes 256 | tf_op jit(solution)/shard_map/assembled/pallas_call | solution.py:510
  (33 shorter events, 0.1 us)
Async XLA Ops:
  0.0 53.2 %copy-start = (bf16[12,128,128]{2,1,0:T(8,128)(2,1)S(1)}, bf16[12,128,128]{2,1,0:T(8,128)(2,1)}, u32[]{:S(2)}) copy-start(bf16[12,128,128]{2,1,0:T(8,128)(2,1)} %param.13) | copy-start | bytes 1179652
  0.0 25.7 %copy-start.1 = (bf16[2,48,48,128]{3,2,1,0:T(8,128)(2,1)S(1)}, bf16[2,48,48,128]{3,2,1,0:T(8,128)(2,1)}, u32[]{:S(2)}) copy-start(bf16[2,48,48,128]{3,2,1,0:T(8,128)(2,1)} %refs_0_.3) | copy-start | bytes 3538948
  0.0 25.7 %copy-start.4 = (f32[2,48,48]{2,1,0:T(8,128)S(1)}, f32[2,48,48]{2,1,0:T(8,128)}, u32[]{:S(2)}) copy-start(f32[2,48,48]{2,1,0:T(8,128)} %refs_1_.3) | copy-start | bytes 55300
  2.2 11.6 %collective-permute-start.1 = (bf16[2,15,48,128]{3,2,1,0:T(8,128)(2,1)S(1)}, bf16[2,15,48,128]{3,2,1,0:T(8,128)(2,1)S(1)}, u32[]{:S(2)}, u32[]{:S(2)}) collective-permute-start(bf16[2,15,48,128]{3,2,1,0:T(8,128)(2,1)S(1)} %get-tuple-element.39), channel_id=1, source_target_pairs={{0,4},{4,0},{8,12},{12,8},{16,20},{20,16},{24,28},{28,24},{1,5},{5... | collective-permute-start | bytes 1105928 | tf_op jit(solution)/shard_map/ppermute | solution.py:553
  5.2 20.5 %collective-permute-start = (bf16[2,27,48,128]{3,2,1,0:T(8,128)(2,1)}, bf16[2,27,48,128]{3,2,1,0:T(8,128)(2,1)S(1)}, u32[]{:S(2)}, u32[]{:S(2)}) collective-permute-start(bf16[2,27,48,128]{3,2,1,0:T(8,128)(2,1)} %get-tuple-element.38), channel_id=1, source_target_pairs={{4,12},{8,0},{12,20},{16,8},{20,28},{24,16},{5,13},{9,1},{13,21},{... | collective-permute-start | bytes 1990664 | tf_op jit(solution)/shard_map/ppermute | solution.py:554
  6.5 0.9 %copy-start.2 = (bf16[8,2,48,48]{3,2,1,0:T(8,128)(2,1)S(1)}, bf16[8,2,48,48]{3,2,1,0:T(8,128)(2,1)}, u32[]{:S(2)}) copy-start(bf16[8,2,48,48]{3,2,1,0:T(8,128)(2,1)} %beta.3) | copy-start | bytes 221188
  13.8 11.9 %collective-permute-start.3 = (bf16[2,16,48,128]{3,2,1,0:T(8,128)(2,1)}, bf16[2,16,48,128]{3,2,1,0:T(8,128)(2,1)S(1)}, u32[]{:S(2)}, u32[]{:S(2)}) collective-permute-start(bf16[2,16,48,128]{3,2,1,0:T(8,128)(2,1)} %get-tuple-element.41), channel_id=1, source_target_pairs={{0,4},{4,0},{8,12},{12,8},{16,20},{20,16},{24,28},{28,24},{1,5},{5... | collective-permute-start | bytes 1179656 | tf_op jit(solution)/shard_map/ppermute | solution.py:560
  15.5 10.2 %collective-permute-start.2 = (bf16[2,15,48,128]{3,2,1,0:T(8,128)(2,1)S(1)}, bf16[2,15,48,128]{3,2,1,0:T(8,128)(2,1)}, u32[]{:S(2)}, u32[]{:S(2)}) collective-permute-start(bf16[2,15,48,128]{3,2,1,0:T(8,128)(2,1)S(1)} %collective-permute-done.1.refs_3_), channel_id=1, source_target_pairs={{0,8},{8,16},{12,4},{16,24},{20,12},{28,20},{1,9},{9,17},{13,5},{1... | collective-permute-start | bytes 1105928 | tf_op jit(solution)/shard_map/ppermute | solution.py:558
  19.8 0.7 copy-start.5
  20.5 18.6 %collective-permute-start.5 = (bf16[8,48,48]{2,1,0:T(8,128)(2,1)}, bf16[8,48,48]{2,1,0:T(8,128)(2,1)S(1)}, u32[]{:S(2)}, u32[]{:S(2)}) collective-permute-start(bf16[8,48,48]{2,1,0:T(8,128)(2,1)} %get-tuple-element.45), channel_id=1, source_target_pairs={{4,8},{8,4},{12,16},{16,12},{20,24},{24,20},{5,9},{9,5},{13,17},{1... | collective-permute-start | bytes 110600 | tf_op jit(solution)/shard_map/ppermute | solution.py:552
  21.2 17.5 %copy-start.11 = (s32[8]{0:T(128)S(1)}, s32[8]{0:T(128)}, u32[]{:S(2)}) copy-start(s32[8]{0:T(128)} %atoms.1) | copy-start | bytes 100
  21.2 17.5 %copy-start.3 = (bf16[8,2,48,48]{3,2,1,0:T(8,128)(2,1)S(1)}, bf16[8,2,48,48]{3,2,1,0:T(8,128)(2,1)}, u32[]{:S(2)}) copy-start(bf16[8,2,48,48]{3,2,1,0:T(8,128)(2,1)} %beta.3) | copy-start | bytes 221188
  25.7 1.0 %copy-start.6 = (bf16[2,15,48,128]{3,2,1,0:T(8,128)(2,1)S(1)}, bf16[2,15,48,128]{3,2,1,0:T(8,128)(2,1)}, u32[]{:S(2)}) copy-start(bf16[2,15,48,128]{3,2,1,0:T(8,128)(2,1)} %copy-done.5) | copy-start | bytes 1105924
  30.6 0.7 copy-start.7
  31.3 0.7 copy-start.9
  32.0 19.4 %collective-permute-start.7 = (bf16[4,10,48,128]{3,2,1,0:T(8,128)(2,1)S(1)}, bf16[4,10,48,128]{3,2,1,0:T(8,128)(2,1)}, u32[]{:S(2)}, u32[]{:S(2)}) collective-permute-start(bf16[4,10,48,128]{3,2,1,0:T(8,128)(2,1)S(1)} %get-tuple-element.53.refs_0_), channel_id=1, source_target_pairs={{0,2},{1,3},{2,0},{3,1},{4,6},{5,7},{6,4},{7,5},{8,10},{9,11},{10,... | collective-permute-start | bytes 1474568 | tf_op jit(solution)/shard_map/ppermute | solution.py:567
  33.5 10.5 %collective-permute-start.4 = (bf16[2,16,48,128]{3,2,1,0:T(8,128)(2,1)S(1)}, bf16[2,16,48,128]{3,2,1,0:T(8,128)(2,1)}, u32[]{:S(2)}, u32[]{:S(2)}) collective-permute-start(bf16[2,16,48,128]{3,2,1,0:T(8,128)(2,1)S(1)} %collective-permute-done.3.b_x.refs_4_), channel_id=1, source_target_pairs={{0,8},{8,16},{12,4},{16,24},{20,12},{28,20},{1,9},{9,17},{13,5},{1... | collective-permute-start | bytes 1179656 | tf_op jit(solution)/shard_map/ppermute | solution.py:561
  39.1 6.4 %copy-start.8 = (bf16[2,9,48,128]{3,2,1,0:T(8,128)(2,1)S(1)}, bf16[2,9,48,128]{3,2,1,0:T(8,128)(2,1)}, u32[]{:S(2)}) copy-start(bf16[2,9,48,128]{3,2,1,0:T(8,128)(2,1)} %copy-done.7) | copy-start | bytes 663556
  39.1 6.4 %copy-start.10 = (bf16[2,9,48,128]{3,2,1,0:T(8,128)(2,1)S(1)}, bf16[2,9,48,128]{3,2,1,0:T(8,128)(2,1)}, u32[]{:S(2)}) copy-start(bf16[2,9,48,128]{3,2,1,0:T(8,128)(2,1)} %copy-done.9) | copy-start | bytes 663556
  44.0 7.4 %collective-permute-start.8 = (f32[24,128]{1,0:T(8,128)S(1)}, f32[24,128]{1,0:T(8,128)S(1)}, u32[]{:S(2)}, u32[]{:S(2)}) collective-permute-start(f32[24,128]{1,0:T(8,128)S(1)} %get-tuple-element.52), channel_id=1, source_target_pairs={{0,4},{4,0},{8,12},{12,8},{16,20},{20,16},{24,28},{28,24},{1,5},{5... | collective-permute-start | bytes 36872 | tf_op jit(solution)/shard_map/ppermute | solution.py:574
  45.5 6.4 %copy-start.13 = (s32[12,2]{0,1:T(2,128)S(1)}, s32[12,2]{0,1:T(2,128)}, u32[]{:S(2)}) copy-start(s32[12,2]{0,1:T(2,128)} %param.12) | copy-start | bytes 292
  50.4 7.3 %collective-permute-start.6 = (bf16[2,14,48,128]{3,2,1,0:T(8,128)(2,1)S(1)}, bf16[2,14,48,128]{3,2,1,0:T(8,128)(2,1)S(1)}, u32[]{:S(2)}, u32[]{:S(2)}) collective-permute-start(bf16[2,14,48,128]{3,2,1,0:T(8,128)(2,1)S(1)} %get-tuple-element.51.refs_0_), channel_id=1, source_target_pairs={{0,2},{1,3},{2,0},{3,1},{4,6},{5,7},{6,4},{7,5},{8,10},{9,11},{10,... | collective-permute-start | bytes 1032200 | tf_op jit(solution)/shard_map/ppermute | solution.py:586
  51.4 4.4 %collective-permute-start.9 = (bf16[4,10,48,128]{3,2,1,0:T(8,128)(2,1)S(1)}, bf16[4,10,48,128]{3,2,1,0:T(8,128)(2,1)S(1)}, u32[]{:S(2)}, u32[]{:S(2)}) collective-permute-start(bf16[4,10,48,128]{3,2,1,0:T(8,128)(2,1)S(1)} %get-tuple-element.53.refs_0_), channel_id=1, source_target_pairs={{0,1},{1,0},{2,3},{3,2},{4,5},{5,4},{6,7},{7,6},{8,9},{9,8},{10,11... | collective-permute-start | bytes 1474568 | tf_op jit(solution)/shard_map/ppermute | solution.py:589
  51.5 4.3 %collective-permute-start.10 = (bf16[4,10,48,128]{3,2,1,0:T(8,128)(2,1)}, bf16[4,10,48,128]{3,2,1,0:T(8,128)(2,1)S(1)}, u32[]{:S(2)}, u32[]{:S(2)}) collective-permute-start(bf16[4,10,48,128]{3,2,1,0:T(8,128)(2,1)} %collective-permute-done.7.refs_2_), channel_id=1, source_target_pairs={{0,1},{1,0},{2,3},{3,2},{4,5},{5,4},{6,7},{7,6},{8,9},{9,8},{10,11... | collective-permute-start | bytes 1474568 | tf_op jit(solution)/shard_map/ppermute | solution.py:590
  52.0 3.8 %collective-permute-start.11 = (f32[24,128]{1,0:T(8,128)S(1)}, f32[24,128]{1,0:T(8,128)S(1)}, u32[]{:S(2)}, u32[]{:S(2)}) collective-permute-start(f32[24,128]{1,0:T(8,128)S(1)} %add.9), channel_id=1, source_target_pairs={{0,8},{4,12},{8,0},{12,4},{16,24},{20,28},{24,16},{28,20},{1,9},{5... | collective-permute-start | bytes 36872 | tf_op jit(solution)/shard_map/ppermute | solution.py:574
  53.6 13.4 %copy-start.12 = (f32[8]{0:T(128)S(1)}, f32[8]{0:T(128)}, u32[]{:S(2)}) copy-start(f32[8]{0:T(128)} %param.10) | copy-start | bytes 100
  57.7 9.2 %collective-permute-start.12 = (bf16[2,14,48,128]{3,2,1,0:T(8,128)(2,1)S(1)}, bf16[2,14,48,128]{3,2,1,0:T(8,128)(2,1)S(1)}, u32[]{:S(2)}, u32[]{:S(2)}) collective-permute-start(bf16[2,14,48,128]{3,2,1,0:T(8,128)(2,1)S(1)} %collective-permute-done.6.refs_2_), channel_id=1, source_target_pairs={{0,1},{1,0},{2,3},{3,2},{4,5},{5,4},{6,7},{7,6},{8,9},{9,8},{10,11... | collective-permute-start | bytes 1032200 | tf_op jit(solution)/shard_map/ppermute | solution.py:597
  57.7 10.0 %collective-permute-start.16 = (bf16[2,14,48,128]{3,2,1,0:T(8,128)(2,1)S(1)}, bf16[2,14,48,128]{3,2,1,0:T(8,128)(2,1)S(1)}, u32[]{:S(2)}, u32[]{:S(2)}) collective-permute-start(bf16[2,14,48,128]{3,2,1,0:T(8,128)(2,1)S(1)} %get-tuple-element.51.refs_0_), channel_id=1, source_target_pairs={{0,1},{1,0},{2,3},{3,2},{4,5},{5,4},{6,7},{7,6},{8,9},{9,8},{10,11... | collective-permute-start | bytes 1032200 | tf_op jit(solution)/shard_map/ppermute | solution.py:584
  58.2 11.3 %collective-permute-start.20 = (bf16[2,14,48,128]{3,2,1,0:T(8,128)(2,1)S(1)}, bf16[2,14,48,128]{3,2,1,0:T(8,128)(2,1)S(1)}, u32[]{:S(2)}, u32[]{:S(2)}) collective-permute-start(bf16[2,14,48,128]{3,2,1,0:T(8,128)(2,1)S(1)} %get-tuple-element.69.a), channel_id=1, source_target_pairs={{0,2},{1,3},{2,0},{3,1},{4,6},{5,7},{6,4},{7,5},{8,10},{9,11},{10,... | collective-permute-start | bytes 1032200 | tf_op jit(solution)/shard_map/ppermute | solution.py:596
  59.3 7.7 %collective-permute-start.14 = (bf16[2,10,48,128]{3,2,1,0:T(8,128)(2,1)S(1)}, bf16[2,10,48,128]{3,2,1,0:T(8,128)(2,1)S(1)}, u32[]{:S(2)}, u32[]{:S(2)}) collective-permute-start(bf16[2,10,48,128]{3,2,1,0:T(8,128)(2,1)S(1)} %get-tuple-element.59), channel_id=1, source_target_pairs={{0,4},{4,0},{8,12},{12,8},{16,20},{20,16},{24,28},{28,24},{1,5},{5... | collective-permute-start | bytes 737288 | tf_op jit(solution)/shard_map/ppermute | solution.py:594
  60.4 4.7 %collective-permute-start.13 = (f32[24,128]{1,0:T(8,128)S(1)}, f32[24,128]{1,0:T(8,128)S(1)}, u32[]{:S(2)}, u32[]{:S(2)}) collective-permute-start(f32[24,128]{1,0:T(8,128)S(1)} %add.10), channel_id=1, source_target_pairs={{0,16},{4,20},{8,24},{12,28},{16,0},{20,4},{24,8},{28,12},{1,17},{... | collective-permute-start | bytes 36872 | tf_op jit(solution)/shard_map/ppermute | solution.py:574
  67.2 2.4 %collective-permute-start.15 = (bf16[16,128]{1,0:T(8,128)(2,1)S(1)}, bf16[16,128]{1,0:T(8,128)(2,1)S(1)}, u32[]{:S(2)}, u32[]{:S(2)}) collective-permute-start(bf16[16,128]{1,0:T(8,128)(2,1)S(1)} %coefficients.1), channel_id=1, source_target_pairs={{0,1},{1,0},{2,3},{3,2},{4,5},{5,4},{6,7},{7,6},{8,9},{9,8},{10,11... | collective-permute-start | bytes 12296 | tf_op jit(solution)/shard_map/ppermute | solution.py:602
  67.2 8.0 %collective-permute-start.19 = (bf16[2,14,48,128]{3,2,1,0:T(8,128)(2,1)S(1)}, bf16[2,14,48,128]{3,2,1,0:T(8,128)(2,1)S(1)}, u32[]{:S(2)}, u32[]{:S(2)}) collective-permute-start(bf16[2,14,48,128]{3,2,1,0:T(8,128)(2,1)S(1)} %get-tuple-element.69.a), channel_id=1, source_target_pairs={{0,1},{1,0},{2,3},{3,2},{4,5},{5,4},{6,7},{7,6},{8,9},{9,8},{10,11... | collective-permute-start | bytes 1032200 | tf_op jit(solution)/shard_map/ppermute | solution.py:585
  68.4 10.1 %collective-permute-start.18 = (bf16[2,14,48,128]{3,2,1,0:T(8,128)(2,1)S(1)}, bf16[2,14,48,128]{3,2,1,0:T(8,128)(2,1)S(1)}, u32[]{:S(2)}, u32[]{:S(2)}) collective-permute-start(bf16[2,14,48,128]{3,2,1,0:T(8,128)(2,1)S(1)} %rotated.3), channel_id=1, source_target_pairs={{0,4},{4,0},{8,12},{12,8},{16,20},{20,16},{24,28},{28,24},{1,5},{5... | collective-permute-start | bytes 1032200 | tf_op jit(solution)/shard_map/ppermute | solution.py:604
  69.5 5.7 %collective-permute-start.21 = (bf16[2,14,48,128]{3,2,1,0:T(8,128)(2,1)S(1)}, bf16[2,14,48,128]{3,2,1,0:T(8,128)(2,1)S(1)}, u32[]{:S(2)}, u32[]{:S(2)}) collective-permute-start(bf16[2,14,48,128]{3,2,1,0:T(8,128)(2,1)S(1)} %collective-permute-done.20.c), channel_id=1, source_target_pairs={{0,1},{1,0},{2,3},{3,2},{4,5},{5,4},{6,7},{7,6},{8,9},{9,8},{10,11... | collective-permute-start | bytes 1032200 | tf_op jit(solution)/shard_map/ppermute | solution.py:610
  69.6 3.7 %collective-permute-start.17 = (bf16[32,128]{1,0:T(8,128)(2,1)S(1)}, bf16[32,128]{1,0:T(8,128)(2,1)S(1)}, u32[]{:S(2)}, u32[]{:S(2)}) collective-permute-start(bf16[32,128]{1,0:T(8,128)(2,1)S(1)} %pad_maximum_fusion), channel_id=1, source_target_pairs={{0,2},{1,3},{2,0},{3,1},{4,6},{5,7},{6,4},{7,5},{8,10},{9,11},{10,... | collective-permute-start | bytes 24584 | tf_op jit(solution)/shard_map/ppermute | solution.py:606

commit v13 on v12

--- a/solution.py
+++ b/solution.py
@@ -284,7 +284,7 @@
 def filter_kernel(slabs, start, parts, joint, *refs):
     own, p_own, zo = refs[:3]
     xrs, zfs = refs[3 : 3 + parts], refs[3 + parts : 3 + 2 * parts]
-    extra = 5 if parts > 1 else 3
+    extra = 7
     outs, scratch = refs[3 + 2 * parts : -extra], refs[-extra:]
     first, lines, diagonals = scratch[:3]
     place = lax.axis_index("space")
@@ -300,30 +300,43 @@
     is_odd = x.astype(F32)
     has_zf = lower * (1.0 - is_odd) + upper * is_odd
     has_zo = upper * (1.0 - is_odd) + lower * is_odd
-    if parts > 1:
-        xr, zf = scratch[3], scratch[4]
-        early = start + 4
-        for target, pieces in ((xr, xrs), (zf, zfs)):
-            target[:, start - 4 : early] = pieces[0][:, 0:8]
-            target[:, early:] = pieces[1][:, 0 : target.shape[1] - early]
-        window = xr.shape[1] // 2
-    else:
-        xr, zf = xrs[0], zfs[0]
-        early = xr.shape[1] - 1
-        window = early // 2
-        for target, piece in ((outs[1], xr), (outs[2], zf)):
-            target[...] = piece[:, early - 8 :]
-    for c in range(1, 7):
-        plane = (c % 2) ^ x
-        if c in (2, 3):
-            lines[c - 1] = potential_block(p_own[plane])
-        else:
-            ref = zfs[0] if c < 2 else (xrs[0] if c < 6 else zo)
-            lines[c - 1] = ref[plane, ref.shape[1] - 1].astype(F32)
+    xr, zf, pots, sems = scratch[3:]
+    window = xr.shape[1] // 2
+    early = xrs[0].shape[1] - 1
+    copies = []
+    for k, (target, pieces) in enumerate(((xr, xrs), (zf, zfs))):
+        begin = 0 if parts == 1 else early - 8
+        moved = [
+            (pieces[0].at[:, pl.ds(early, 1)], pots.at[k]),
+            (
+                pieces[0].at[:, pl.ds(begin, early - begin)],
+                target.at[:, pl.ds(begin, early - begin)],
+            ),
+        ]
+        if parts > 1:
+            later = target.shape[1] - early
+            moved.append((pieces[1].at[:, pl.ds(0, later)], target.at[:, pl.ds(early, later)]))
+        copies += [
+            pltpu.make_async_copy(source, goal, sems.at[3 * k + i])
+            for i, (source, goal) in enumerate(moved)
+        ]
+    for copy in copies:
+        copy.start()
+
+    def fill(c, block):
+        lines[c - 1] = block
         for kind in range(2):
             even, odd = (lines[c - 1, pl.ds(k, half, stride=2)] for k in range(2))
             lanes = slice(64 * kind, 64 * kind + width)
             diagonals[c - 1, kind] = jnp.concatenate([even[:, lanes], odd[:, lanes]], axis=1)
+
+    for c in (2, 3):
+        fill(c, potential_block(p_own[(c % 2) ^ x]))
+    fill(6, zo[x, zo.shape[1] - 1].astype(F32))
+    for copy in copies:
+        copy.wait()
+    for c in (1, 4, 5):
+        fill(c, pots[1 if c < 2 else 0, (c % 2) ^ x, 0].astype(F32))
 
     here = neighbour_sum(width, True)
     i = lax.broadcasted_iota(jnp.int32, (cells, cells), 0)
@@ -405,22 +418,26 @@
     parts = len(xrs)
     shape = (2 * planes if joint else planes, rows, width, orbs)
     out = (jax.ShapeDtypeStruct(shape, BF16),) * (1 if joint else 2)
-    if parts == 1:
-        out += (jax.ShapeDtypeStruct((planes, 9, width, orbs), BF16),) * 2
     cells = 10 * rows * width
     scratch = [
         pltpu.VMEM((6, rows + 4, width, orbs), BF16),
         pltpu.VMEM((6, width, orbs), F32),
         pltpu.VMEM((6, 2, own.shape[1] // 2, 2 * width), F32),
     ]
-    if parts > 1:
-        window = own.shape[1] // 2 + 2
-        scratch += [pltpu.VMEM((planes, window, width, orbs), BF16)] * 2
+    window = own.shape[1] // 2 + 2 if parts > 1 else xrs[0].shape[1] - 1
+    scratch += [pltpu.VMEM((planes, window, width, orbs), BF16)] * 2
+    scratch += [pltpu.VMEM((2, planes, 1, width, orbs), BF16), pltpu.SemaphoreType.DMA((6,))]
+    local = pl.BlockSpec(memory_space=pltpu.VMEM)
+    distant = pl.BlockSpec(memory_space=pltpu.MemorySpace.HBM)
+    xrs, zfs = (
+        [pltpu.with_memory_space_constraint(piece, pltpu.MemorySpace.HBM) for piece in pieces]
+        for pieces in (xrs, zfs)
+    )
     return pl.pallas_call(
         functools.partial(filter_kernel, slabs, start, parts, joint),
         out_shape=out,
-        in_specs=[pl.BlockSpec(memory_space=pltpu.VMEM)] * (len(operands) + 2 * parts),
-        out_specs=(pl.BlockSpec(memory_space=pltpu.VMEM),) * len(out),
+        in_specs=[local] * len(operands) + [distant] * (2 * parts),
+        out_specs=(local,) * len(out),
         scratch_shapes=scratch,
         compiler_params=params(),
         cost_estimate=cost(2 * cells * 32 * orbs, FILTER * cells * orbs * 4),
@@ -530,7 +547,7 @@
     x = lax.rem(place, 2)
     half = width_x // 2
     window = half + 2
-    rows1 = half * 5 // 24 * 2
+    rows1 = half * 7 // 24 * 2
     rows2 = half - rows1
     early = rows1 + 4
 
@@ -555,15 +572,15 @@
     active = jnp.abs(place - atom_slab) <= 1
     beta_m = jnp.where(active[:, None, None, None], beta, jnp.zeros_like(beta))
     gram = jnp.einsum("pzxy,qzxy->pq", beta_m, beta_m, preferred_element_type=F32)
+    xr1, second = ordered(xr1, to_x2)
     zf1 = lax.ppermute(xr1, "space", other_way)
-    second, _ = ordered(to_x2, xr1)
     xr2 = lax.ppermute(second, "space", swap)
     zf2 = lax.ppermute(xr2, "space", other_way)
     strong = jnp.broadcast_to(strength[:, None], (count, orbs))
 
     zf1, _ = ordered(zf1, xr2)
     operands = (psi, potential, zo)
-    block1, xr_c, zf_c = filtered(slabs, 0, rows1, True, operands, (xr1,), (zf1,))
+    (block1,) = filtered(slabs, 0, rows1, True, operands, (xr1,), (zf1,))
     y1 = lax.ppermute(block1, "orb", across)
     f_d, _ = ordered(f_d, block1)
     sums, weights = partials(count, atom_slab, psi, beta, xr2, f_d, potential, gram)
@@ -574,7 +591,7 @@
         return values + lax.ppermute(values, "space", pairs)
 
     zf2, sums = ordered(zf2, sums)
-    give2, keep2 = filtered(slabs, rows1, rows2, False, operands, (xr_c, xr2), (zf_c, zf2))
+    give2, keep2 = filtered(slabs, rows1, rows2, False, operands, (xr1, xr2), (zf1, zf2))
     pattern, q_tiles, _ = ordered(pattern, q_tiles, give2)
     me = lax.axis_index("orb")
     which = jnp.bitwise_xor(me, jnp.arange(groups, dtype=jnp.int32))

time: 80.8 us -> 78 us (0.965)
  starting transfers between devices: 29.9 us -> 33.6 us
  waiting for transfers between devices: 23.2 us -> 20 us
  local copies, waits for them, and re-layouts: 4.15 us -> 1.05 us
    ppermute x1, waiting for transfers between devices: 0.01 us -> 6.56 us  [shards(): xr2 = lax.ppermute(second, 'space', swap)]
    ppermute x1, waiting for transfers between devices: 4.48 us -> 0.75 us  [shards(): zf1 = lax.ppermute(xr1, 'space', other_way)]
    unnamed x28 -> x18, local copies, waits for them, and re-layouts: 4.06 us -> 0.95 us
    ppermute x1, waiting for transfers between devices: 3.33 us -> 0.29 us  [shards(): got2 = lax.ppermute(give2, 'space', swap)]
    ppermute x1, waiting for transfers between devices: 4.62 us -> 6.91 us  [shards(): xr1 = lax.ppermute(to_x, 'space', swap)]
    ppermute x1, starting transfers between devices: 0.58 us -> 2.59 us  [shards(): coefs_y = lax.ppermute(coefs, 'orb', across)]
    ppermute x1, waiting for transfers between devices: 1.88 us -> 0.01 us  [shards(): got1 = lax.ppermute(give1, 'space', swap)]
    ppermute x1, waiting for transfers between devices: 1.78 us -> 0.01 us  [shards(): zf2 = lax.ppermute(xr2, 'space', other_way)]
  transfers between devices with their start and end apart: 22 -> 22, of which waited for: 9 -> 7; matrix products, arithmetic and copies ran while one was open for 1% -> 1% of each run, Pallas kernels for 22% -> 24%
where the time goes in v13:
time: 78 us; the launch traced here: 77.6 us
  starting transfers between devices  33.6 us (43%)
  Pallas kernels  22.1 us (28%)
  waiting for transfers between devices  20 us (26%)
  local copies, waits for them, and re-layouts  1.05 us (1%)
    pallas_call x2, Pallas kernels, filtered(): pl.pallas_call(functools.partial(filter_kernel, slabs, start, parts, join...  9.13 us
    ppermute x1, waiting for transfers between devices, shards(): xr1 = lax.ppermute(to_x, 'space', swap)  6.91 us
    ppermute x1, waiting for transfers between devices, shards(): xr2 = lax.ppermute(second, 'space', swap)  6.56 us
    ppermute x3, starting transfers between devices, added(): return values + lax.ppermute(values, 'space', pairs)  6.37 us
    ppermute x1, starting transfers between devices, shards(): zf2 = lax.ppermute(xr2, 'space', other_way)  5.11 us
    ppermute x1, starting transfers between devices, shards(): zf1 = lax.ppermute(xr1, 'space', other_way)  4.5 us
    ppermute x3, waiting for transfers between devices, added(): return values + lax.ppermute(values, 'space', pairs)  3.8 us
    pallas_call x1, Pallas kernels, partials(): pl.pallas_call(functools.partial(partial_kernel, count), out_shape=(jax.S...  3.42 us
  transfers between devices with their start and end apart: 22, of which 7 were waited for; matrix products, arithmetic and copies ran while one was open for 1% of the time, Pallas kernels for 24%

profile of v13, /device:TPU:0, one launch (start us, length us, event | category | flops | bytes accessed | tf_op | source)
XLA Modules:
  0.0 77.6 jit_solution(931760675213866453)
XLA Ops:
  0.0 0.0 copy-start
  0.0 1.4 %prepared.1 = (bf16[2,19,48,128]{3,2,1,0:T(8,128)(2,1)S(1)}, bf16[2,27,48,128]{3,2,1,0:T(8,128)(2,1)S(1)}) custom-call(bf16[2,48,48,128]{3,2,1,0:T(8,128)(2,1)} %refs_0_.3, f32[2,48,48]{2,1,0:T(8,128)} %refs_1_.3), custom_call_target="tpu_custom_call" | custom-call | flops 256 | bytes 256 | tf_op jit(solution)/shard_map/prepared/pallas_call | solution.py:81
  1.4 3.0 %collective-permute-start.1 = (bf16[2,19,48,128]{3,2,1,0:T(8,128)(2,1)S(1)}, bf16[2,19,48,128]{3,2,1,0:T(8,128)(2,1)}, u32[]{:S(2)}, u32[]{:S(2)}) collective-permute-start(bf16[2,19,48,128]{3,2,1,0:T(8,128)(2,1)S(1)} %get-tuple-element.37), channel_id=1, source_target_pairs={{0,4},{4,0},{8,12},{12,8},{16,20},{20,16},{24,28},{28,24},{1,5},{5... | collective-permute-start | bytes 1400840 | tf_op jit(solution)/shard_map/ppermute | solution.py:570
  4.4 1.3 %collective-permute-start = (bf16[2,27,48,128]{3,2,1,0:T(8,128)(2,1)S(1)}, bf16[2,27,48,128]{3,2,1,0:T(8,128)(2,1)S(1)}, u32[]{:S(2)}, u32[]{:S(2)}) collective-permute-start(bf16[2,27,48,128]{3,2,1,0:T(8,128)(2,1)S(1)} %get-tuple-element.36), channel_id=1, source_target_pairs={{4,12},{8,0},{12,20},{16,8},{20,28},{24,16},{5,13},{9,1},{13,21},{... | collective-permute-start | bytes 1990664 | tf_op jit(solution)/shard_map/ppermute | solution.py:571
  5.7 0.0 copy-start.2
  5.7 0.9 %copy-done.2 = bf16[8,2,48,48]{3,2,1,0:T(8,128)(2,1)S(1)} copy-done((bf16[8,2,48,48]{3,2,1,0:T(8,128)(2,1)S(1)}, bf16[8,2,48,48]{3,2,1,0:T(8,128)(2,1)}, u32[]{:S(2)}) %copy-start.2) | copy-done | bytes 73752
  6.6 1.7 %packed.1 = (bf16[2,12,48,128]{3,2,1,0:T(8,128)(2,1)}, bf16[8,48,48]{2,1,0:T(8,128)(2,1)}) custom-call(bf16[2,48,48,128]{3,2,1,0:T(8,128)(2,1)} %refs_0_.3, bf16[8,2,48,48]{3,2,1,0:T(8,128)(2,1)S(1)} %copy-done.2), custom_call_target="tpu_custom_call" | custom-call | flops 256 | bytes 256 | tf_op jit(solution)/shard_map/packed/pallas_call | solution.py:121
  8.3 6.9 %collective-permute-done.1.refs_3_ = bf16[2,19,48,128]{3,2,1,0:T(8,128)(2,1)} collective-permute-done((bf16[2,19,48,128]{3,2,1,0:T(8,128)(2,1)S(1)}, bf16[2,19,48,128]{3,2,1,0:T(8,128)(2,1)}, u32[]{:S(2)}, u32[]{:S(2)}) %collective-permute-start.1) | collective-permute-done | bytes 466976 | tf_op jit(solution)/shard_map/ppermute | solution.py:570
  15.2 4.5 %collective-permute-start.3 = (bf16[2,19,48,128]{3,2,1,0:T(8,128)(2,1)}, bf16[2,19,48,128]{3,2,1,0:T(8,128)(2,1)}, u32[]{:S(2)}, u32[]{:S(2)}) collective-permute-start(bf16[2,19,48,128]{3,2,1,0:T(8,128)(2,1)} %collective-permute-done.1.refs_3_), channel_id=1, source_target_pairs={{0,8},{8,16},{12,4},{16,24},{20,12},{28,20},{1,9},{9,17},{13,5},{1... | collective-permute-start | bytes 1400840 | tf_op jit(solution)/shard_map/ppermute | solution.py:576
  19.7 0.0 collective-permute-start.2
  19.7 1.3 %collective-permute-start.5 = (bf16[8,48,48]{2,1,0:T(8,128)(2,1)}, bf16[8,48,48]{2,1,0:T(8,128)(2,1)}, u32[]{:S(2)}, u32[]{:S(2)}) collective-permute-start(bf16[8,48,48]{2,1,0:T(8,128)(2,1)} %get-tuple-element.42), channel_id=1, source_target_pairs={{4,8},{8,4},{12,16},{16,12},{20,24},{24,20},{5,9},{9,5},{13,17},{1... | collective-permute-start | bytes 110600 | tf_op jit(solution)/shard_map/ppermute | solution.py:569
  21.0 6.6 %collective-permute-done.2.b_x.refs_4_ = bf16[2,12,48,128]{3,2,1,0:T(8,128)(2,1)S(1)} collective-permute-done((bf16[2,12,48,128]{3,2,1,0:T(8,128)(2,1)}, bf16[2,12,48,128]{3,2,1,0:T(8,128)(2,1)S(1)}, u32[]{:S(2)}, u32[]{:S(2)}) %collective-permute-start.2) | collective-permute-done | bytes 294944 | tf_op jit(solution)/shard_map/ppermute | solution.py:577
  27.6 0.8 collective-permute-done.3.refs_4_.refs_5_
  28.3 0.0 collective-permute-done.refs_2_
  28.3 0.0 copy-done.1
  28.3 0.0 copy-done.5
  28.3 5.0 %filtered.2.refs_0_ = bf16[4,14,48,128]{3,2,1,0:T(8,128)(2,1)S(1)} custom-call(bf16[2,48,48,128]{3,2,1,0:T(8,128)(2,1)S(1)} %copy-done.1, f32[2,48,48]{2,1,0:T(8,128)S(1)} %copy-done.5, bf16[2,27,48,128]{3,2,1,0:T(8,128)(2,1)S(1)} %collective-permute-done.refs_2_, bf16[2,19,48,128]{3,2,1,0:T(8,128)(2,1)} %collective-permute-done.1.refs_3_, ...), custom_call_target="tpu_custom_call" | custom-call | flops 3440640 | bytes 21504000 | tf_op jit(solution)/shard_map/filtered/pallas_call | solution.py:436
  33.3 1.6 %collective-permute-start.7 = (bf16[4,14,48,128]{3,2,1,0:T(8,128)(2,1)S(1)}, bf16[4,14,48,128]{3,2,1,0:T(8,128)(2,1)}, u32[]{:S(2)}, u32[]{:S(2)}) collective-permute-start(bf16[4,14,48,128]{3,2,1,0:T(8,128)(2,1)S(1)} %filtered.2.refs_0_), channel_id=1, source_target_pairs={{0,2},{1,3},{2,0},{3,1},{4,6},{5,7},{6,4},{7,5},{8,10},{9,11},{10,... | collective-permute-start | bytes 2064392 | tf_op jit(solution)/shard_map/ppermute | solution.py:584
  34.9 5.1 %collective-permute-start.4 = (bf16[2,12,48,128]{3,2,1,0:T(8,128)(2,1)S(1)}, bf16[2,12,48,128]{3,2,1,0:T(8,128)(2,1)}, u32[]{:S(2)}, u32[]{:S(2)}) collective-permute-start(bf16[2,12,48,128]{3,2,1,0:T(8,128)(2,1)S(1)} %collective-permute-done.2.b_x.refs_4_), channel_id=1, source_target_pairs={{0,8},{8,16},{12,4},{16,24},{20,12},{28,20},{1,9},{9,17},{13,5},{1... | collective-permute-start | bytes 884744 | tf_op jit(solution)/shard_map/ppermute | solution.py:578
  40.0 0.1 broadcast_select_fusion
  40.1 0.3 convolution_bitcast_fusion.gram
  40.4 0.0 collective-permute-done.5.b_d
  40.4 3.4 %partials.1 = (f32[24,128]{1,0:T(8,128)S(1)}, bf16[2,48,24,48]{3,2,1,0:T(8,128)(2,1)S(1)}) custom-call(s32[8]{0:T(128)S(1)} %copy-done.6, bf16[2,48,48,128]{3,2,1,0:T(8,128)(2,1)S(1)} %copy-done.1, bf16[8,2,48,48]{3,2,1,0:T(8,128)(2,1)S(1)} %copy-done.3, bf16[2,12,48,128]{3,2,1,0:T(8,128)(2,1)S(1)} %collective-permute-done.2.b_x.refs_4_, ...), custom_call_target="tpu_custom_call" | custom-call | flops 256 | bytes 256 | tf_op jit(solution)/shard_map/partials/pallas_call | solution.py:198
  43.8 0.0 collective-permute-done.4.refs_6_
  43.9 2.2 %collective-permute-start.8 = (f32[24,128]{1,0:T(8,128)S(1)}, f32[24,128]{1,0:T(8,128)S(1)}, u32[]{:S(2)}, u32[]{:S(2)}) collective-permute-start(f32[24,128]{1,0:T(8,128)S(1)} %get-tuple-element.48), channel_id=1, source_target_pairs={{0,4},{4,0},{8,12},{12,8},{16,20},{20,16},{24,28},{28,24},{1,5},{5... | collective-permute-start | bytes 36872 | tf_op jit(solution)/shard_map/ppermute | solution.py:591
  46.0 4.1 %filtered.3 = (bf16[2,10,48,128]{3,2,1,0:T(8,128)(2,1)S(1)}, bf16[2,10,48,128]{3,2,1,0:T(8,128)(2,1)S(1)}) custom-call(bf16[2,48,48,128]{3,2,1,0:T(8,128)(2,1)S(1)} %copy-done.1, f32[2,48,48]{2,1,0:T(8,128)S(1)} %copy-done.5, bf16[2,27,48,128]{3,2,1,0:T(8,128)(2,1)S(1)} %collective-permute-done.refs_2_, ...), custom_call_target="tpu_custom_call" | custom-call | flops 2457600 | bytes 15360000 | tf_op jit(solution)/shard_map/filtered/pallas_call | solution.py:436
  50.2 0.6 collective-permute-start.6
  50.8 0.0 collective-permute-done.8
  50.8 0.0 collective-permute-done.7.refs_2_
  50.8 0.1 collective-permute-start.9
  50.9 0.5 collective-permute-start.10
  51.4 0.0 copy-done.8
  51.4 1.6 %collective-permute-start.11 = (f32[24,128]{1,0:T(8,128)S(1)}, f32[24,128]{1,0:T(8,128)S(1)}, u32[]{:S(2)}, u32[]{:S(2)}) collective-permute-start(f32[24,128]{1,0:T(8,128)S(1)} %add.9), channel_id=1, source_target_pairs={{0,8},{4,12},{8,0},{12,4},{16,24},{20,28},{24,16},{28,20},{1,9},{5... | collective-permute-start | bytes 36872 | tf_op jit(solution)/shard_map/ppermute | solution.py:591
  53.0 0.3 fusion
  53.4 1.7 %collective-permute-done.11 = f32[24,128]{1,0:T(8,128)S(1)} collective-permute-done((f32[24,128]{1,0:T(8,128)S(1)}, f32[24,128]{1,0:T(8,128)S(1)}, u32[]{:S(2)}, u32[]{:S(2)}) %collective-permute-start.11) | collective-permute-done | bytes 12320 | tf_op jit(solution)/shard_map/ppermute | solution.py:591
  55.1 0.0 collective-permute-done.10.refs_3_
  55.2 0.0 collective-permute-done.9.refs_1_
  55.2 2.1 %rotated.2 = (bf16[2,14,48,128]{3,2,1,0:T(8,128)(2,1)S(1)}, bf16[2,14,48,128]{3,2,1,0:T(8,128)(2,1)S(1)}) custom-call(bf16[4,14,48,128]{3,2,1,0:T(8,128)(2,1)S(1)} %filtered.2.refs_0_, bf16[4,14,48,128]{3,2,1,0:T(8,128)(2,1)S(1)} %collective-permute-done.9.refs_1_, bf16[4,14,48,128]{3,2,1,0:T(8,128)(2,1)} %collective-permute-done.7.refs_2_, ...), custom_call_target="tpu_custom_call" | custom-call | flops 22020096 | bytes 215040 | tf_op jit(solution)/shard_map/rotated/pallas_call | solution.py:480
  57.3 1.6 %collective-permute-start.14 = (bf16[2,14,48,128]{3,2,1,0:T(8,128)(2,1)S(1)}, bf16[2,14,48,128]{3,2,1,0:T(8,128)(2,1)S(1)}, u32[]{:S(2)}, u32[]{:S(2)}) collective-permute-start(bf16[2,14,48,128]{3,2,1,0:T(8,128)(2,1)S(1)} %get-tuple-element.55), channel_id=1, source_target_pairs={{0,4},{4,0},{8,12},{12,8},{16,20},{20,16},{24,28},{28,24},{1,5},{5... | collective-permute-start | bytes 1032200 | tf_op jit(solution)/shard_map/ppermute | solution.py:611
  58.9 0.0 collective-permute-done.6.refs_2_
  58.9 0.0 collective-permute-start.12
  58.9 0.5 collective-permute-start.16
  59.4 2.5 %collective-permute-start.20 = (bf16[2,10,48,128]{3,2,1,0:T(8,128)(2,1)S(1)}, bf16[2,10,48,128]{3,2,1,0:T(8,128)(2,1)S(1)}, u32[]{:S(2)}, u32[]{:S(2)}) collective-permute-start(bf16[2,10,48,128]{3,2,1,0:T(8,128)(2,1)S(1)} %get-tuple-element.65.a), channel_id=1, source_target_pairs={{0,2},{1,3},{2,0},{3,1},{4,6},{5,7},{6,4},{7,5},{8,10},{9,11},{10,... | collective-permute-start | bytes 737288 | tf_op jit(solution)/shard_map/ppermute | solution.py:613
  62.0 2.5 %collective-permute-start.13 = (f32[24,128]{1,0:T(8,128)S(1)}, f32[24,128]{1,0:T(8,128)S(1)}, u32[]{:S(2)}, u32[]{:S(2)}) collective-permute-start(f32[24,128]{1,0:T(8,128)S(1)} %add.10), channel_id=1, source_target_pairs={{0,16},{4,20},{8,24},{12,28},{16,0},{20,4},{24,8},{28,12},{1,17},{... | collective-permute-start | bytes 36872 | tf_op jit(solution)/shard_map/ppermute | solution.py:591
  64.5 2.1 %collective-permute-done.13 = f32[24,128]{1,0:T(8,128)S(1)} collective-permute-done((f32[24,128]{1,0:T(8,128)S(1)}, f32[24,128]{1,0:T(8,128)S(1)}, u32[]{:S(2)}, u32[]{:S(2)}) %collective-permute-start.13) | collective-permute-done | bytes 12320 | tf_op jit(solution)/shard_map/ppermute | solution.py:591
  66.6 0.0 collective-permute-done.12.refs_3_
  66.6 0.0 collective-permute-done.14.got1
  66.6 0.1 broadcast_in_dim.22.strength
  66.6 0.1 coefficients.1
  66.8 0.0 collective-permute-start.15
  66.8 0.5 collective-permute-start.19
  67.3 0.0 collective-permute-done.16.refs_1_
  67.3 0.6 rotated.3
  67.9 1.5 %collective-permute-start.18 = (bf16[2,10,48,128]{3,2,1,0:T(8,128)(2,1)S(1)}, bf16[2,10,48,128]{3,2,1,0:T(8,128)(2,1)S(1)}, u32[]{:S(2)}, u32[]{:S(2)}) collective-permute-start(bf16[2,10,48,128]{3,2,1,0:T(8,128)(2,1)S(1)} %rotated.3), channel_id=1, source_target_pairs={{0,4},{4,0},{8,12},{12,8},{16,20},{20,16},{24,28},{28,24},{1,5},{5... | collective-permute-start | bytes 737288 | tf_op jit(solution)/shard_map/ppermute | solution.py:621
  69.4 0.0 collective-permute-done.20.c
  69.4 0.0 collective-permute-start.21
  69.4 0.0 collective-permute-done.15
  69.5 2.6 %collective-permute-start.17 = (bf16[32,128]{1,0:T(8,128)(2,1)S(1)}, bf16[32,128]{1,0:T(8,128)(2,1)S(1)}, u32[]{:S(2)}, u32[]{:S(2)}) collective-permute-start(bf16[32,128]{1,0:T(8,128)(2,1)S(1)} %pad_maximum_fusion), channel_id=1, source_target_pairs={{0,2},{1,3},{2,0},{3,1},{4,6},{5,7},{6,4},{7,5},{8,10},{9,11},{10,... | collective-permute-start | bytes 24584 | tf_op jit(solution)/shard_map/ppermute | solution.py:623
  72.0 1.6 %collective-permute-done.17 = bf16[32,128]{1,0:T(8,128)(2,1)S(1)} collective-permute-done((bf16[32,128]{1,0:T(8,128)(2,1)S(1)}, bf16[32,128]{1,0:T(8,128)(2,1)S(1)}, u32[]{:S(2)}, u32[]{:S(2)}) %collective-permute-start.17) | collective-permute-done | bytes 8224 | tf_op jit(solution)/shard_map/ppermute | solution.py:623
  73.7 1.9 %nonlocal.1.term = f32[2,48,48,128]{3,2,1,0:T(8,128)S(1)} custom-call(bf16[16,128]{1,0:T(8,128)(2,1)S(1)} %get-tuple-element.70.a, bf16[16,128]{1,0:T(8,128)(2,1)S(1)} %get-tuple-element.69.b, bf16[16,128]{1,0:T(8,128)(2,1)S(1)} %get-tuple-element.68.c, bf16[16,128]{1,0:T(8,128)(2,1)S(1)} %get-tuple-element.67.d, bf16[4,128,128]{2,1,0:T(8,128)(2,1)S(1)} %copy.18.refs_4_.q, ...), custom_call_target="tpu_custom_call" | custom-call | flops 256 | bytes 256 | tf_op jit(solution)/shard_map/nonlocal/pallas_call | solution.py:273
  75.6 0.0 collective-permute-done.19.b
  75.6 0.0 collective-permute-done.21.d
  75.6 0.3 collective-permute-done.18.got2
  75.9 1.7 %assembled.1 = bf16[2,48,48,128]{3,2,1,0:T(8,128)(2,1)} custom-call(f32[2,48,48,128]{3,2,1,0:T(8,128)S(1)} %nonlocal.1.term, bf16[2,14,48,128]{3,2,1,0:T(8,128)(2,1)S(1)} %get-tuple-element.63.keep1, bf16[2,14,48,128]{3,2,1,0:T(8,128)(2,1)S(1)} %collective-permute-done.14.got1, bf16[2,10,48,128]{3,2,1,0:T(8,128)(2,1)S(1)} %collective-permute-done.18.got2, ...), custom_call_target="tpu_custom_call" | custom-call | flops 256 | bytes 256 | tf_op jit(solution)/shard_map/assembled/pallas_call | solution.py:527
  (23 shorter events, 0.1 us)
Async XLA Ops:
  0.0 53.0 %copy-start = (bf16[12,128,128]{2,1,0:T(8,128)(2,1)S(1)}, bf16[12,128,128]{2,1,0:T(8,128)(2,1)}, u32[]{:S(2)}) copy-start(bf16[12,128,128]{2,1,0:T(8,128)(2,1)} %param.13) | copy-start | bytes 1179652
  0.0 28.3 %copy-start.1 = (bf16[2,48,48,128]{3,2,1,0:T(8,128)(2,1)S(1)}, bf16[2,48,48,128]{3,2,1,0:T(8,128)(2,1)}, u32[]{:S(2)}) copy-start(bf16[2,48,48,128]{3,2,1,0:T(8,128)(2,1)} %refs_0_.3) | copy-start | bytes 3538948
  0.0 28.3 %copy-start.5 = (f32[2,48,48]{2,1,0:T(8,128)S(1)}, f32[2,48,48]{2,1,0:T(8,128)}, u32[]{:S(2)}) copy-start(f32[2,48,48]{2,1,0:T(8,128)} %refs_1_.3) | copy-start | bytes 55300
  1.4 13.8 %collective-permute-start.1 = (bf16[2,19,48,128]{3,2,1,0:T(8,128)(2,1)S(1)}, bf16[2,19,48,128]{3,2,1,0:T(8,128)(2,1)}, u32[]{:S(2)}, u32[]{:S(2)}) collective-permute-start(bf16[2,19,48,128]{3,2,1,0:T(8,128)(2,1)S(1)} %get-tuple-element.37), channel_id=1, source_target_pairs={{0,4},{4,0},{8,12},{12,8},{16,20},{20,16},{24,28},{28,24},{1,5},{5... | collective-permute-start | bytes 1400840 | tf_op jit(solution)/shard_map/ppermute | solution.py:570
  4.4 23.9 %collective-permute-start = (bf16[2,27,48,128]{3,2,1,0:T(8,128)(2,1)S(1)}, bf16[2,27,48,128]{3,2,1,0:T(8,128)(2,1)S(1)}, u32[]{:S(2)}, u32[]{:S(2)}) collective-permute-start(bf16[2,27,48,128]{3,2,1,0:T(8,128)(2,1)S(1)} %get-tuple-element.36), channel_id=1, source_target_pairs={{4,12},{8,0},{12,20},{16,8},{20,28},{24,16},{5,13},{9,1},{13,21},{... | collective-permute-start | bytes 1990664 | tf_op jit(solution)/shard_map/ppermute | solution.py:571
  5.7 0.9 %copy-start.2 = (bf16[8,2,48,48]{3,2,1,0:T(8,128)(2,1)S(1)}, bf16[8,2,48,48]{3,2,1,0:T(8,128)(2,1)}, u32[]{:S(2)}) copy-start(bf16[8,2,48,48]{3,2,1,0:T(8,128)(2,1)} %beta.3) | copy-start | bytes 221188
  15.2 13.1 %collective-permute-start.3 = (bf16[2,19,48,128]{3,2,1,0:T(8,128)(2,1)}, bf16[2,19,48,128]{3,2,1,0:T(8,128)(2,1)}, u32[]{:S(2)}, u32[]{:S(2)}) collective-permute-start(bf16[2,19,48,128]{3,2,1,0:T(8,128)(2,1)} %collective-permute-done.1.refs_3_), channel_id=1, source_target_pairs={{0,8},{8,16},{12,4},{16,24},{20,12},{28,20},{1,9},{9,17},{13,5},{1... | collective-permute-start | bytes 1400840 | tf_op jit(solution)/shard_map/ppermute | solution.py:576
  19.7 7.9 %collective-permute-start.2 = (bf16[2,12,48,128]{3,2,1,0:T(8,128)(2,1)}, bf16[2,12,48,128]{3,2,1,0:T(8,128)(2,1)S(1)}, u32[]{:S(2)}, u32[]{:S(2)}) collective-permute-start(bf16[2,12,48,128]{3,2,1,0:T(8,128)(2,1)} %get-tuple-element.40), channel_id=1, source_target_pairs={{0,4},{4,0},{8,12},{12,8},{16,20},{20,16},{24,28},{28,24},{1,5},{5... | collective-permute-start | bytes 884744 | tf_op jit(solution)/shard_map/ppermute | solution.py:577
  19.7 20.7 %collective-permute-start.5 = (bf16[8,48,48]{2,1,0:T(8,128)(2,1)}, bf16[8,48,48]{2,1,0:T(8,128)(2,1)}, u32[]{:S(2)}, u32[]{:S(2)}) collective-permute-start(bf16[8,48,48]{2,1,0:T(8,128)(2,1)} %get-tuple-element.42), channel_id=1, source_target_pairs={{4,8},{8,4},{12,16},{16,12},{20,24},{24,20},{5,9},{9,5},{13,17},{1... | collective-permute-start | bytes 110600 | tf_op jit(solution)/shard_map/ppermute | solution.py:569
  21.0 13.9 %copy-start.6 = (s32[8]{0:T(128)S(1)}, s32[8]{0:T(128)}, u32[]{:S(2)}) copy-start(s32[8]{0:T(128)} %atoms.1) | copy-start | bytes 100
  21.0 19.0 %copy-start.3 = (bf16[8,2,48,48]{3,2,1,0:T(8,128)(2,1)S(1)}, bf16[8,2,48,48]{3,2,1,0:T(8,128)(2,1)}, u32[]{:S(2)}) copy-start(bf16[8,2,48,48]{3,2,1,0:T(8,128)(2,1)} %beta.3) | copy-start | bytes 221188
  27.6 12.9 %copy-start.4 = (bf16[2,12,48,128]{3,2,1,0:T(8,128)(2,1)}, bf16[2,12,48,128]{3,2,1,0:T(8,128)(2,1)S(1)}, u32[]{:S(2)}) copy-start(bf16[2,12,48,128]{3,2,1,0:T(8,128)(2,1)S(1)} %collective-permute-done.2.b_x.refs_4_) | copy-start | bytes 884740
  33.3 17.5 %collective-permute-start.7 = (bf16[4,14,48,128]{3,2,1,0:T(8,128)(2,1)S(1)}, bf16[4,14,48,128]{3,2,1,0:T(8,128)(2,1)}, u32[]{:S(2)}, u32[]{:S(2)}) collective-permute-start(bf16[4,14,48,128]{3,2,1,0:T(8,128)(2,1)S(1)} %filtered.2.refs_0_), channel_id=1, source_target_pairs={{0,2},{1,3},{2,0},{3,1},{4,6},{5,7},{6,4},{7,5},{8,10},{9,11},{10,... | collective-permute-start | bytes 2064392 | tf_op jit(solution)/shard_map/ppermute | solution.py:584
  34.9 8.9 %collective-permute-start.4 = (bf16[2,12,48,128]{3,2,1,0:T(8,128)(2,1)S(1)}, bf16[2,12,48,128]{3,2,1,0:T(8,128)(2,1)}, u32[]{:S(2)}, u32[]{:S(2)}) collective-permute-start(bf16[2,12,48,128]{3,2,1,0:T(8,128)(2,1)S(1)} %collective-permute-done.2.b_x.refs_4_), channel_id=1, source_target_pairs={{0,8},{8,16},{12,4},{16,24},{20,12},{28,20},{1,9},{9,17},{13,5},{1... | collective-permute-start | bytes 884744 | tf_op jit(solution)/shard_map/ppermute | solution.py:578
  43.9 6.9 %collective-permute-start.8 = (f32[24,128]{1,0:T(8,128)S(1)}, f32[24,128]{1,0:T(8,128)S(1)}, u32[]{:S(2)}, u32[]{:S(2)}) collective-permute-start(f32[24,128]{1,0:T(8,128)S(1)} %get-tuple-element.48), channel_id=1, source_target_pairs={{0,4},{4,0},{8,12},{12,8},{16,20},{20,16},{24,28},{28,24},{1,5},{5... | collective-permute-start | bytes 36872 | tf_op jit(solution)/shard_map/ppermute | solution.py:591
  46.0 5.3 %copy-start.8 = (s32[12,2]{0,1:T(2,128)S(1)}, s32[12,2]{0,1:T(2,128)}, u32[]{:S(2)}) copy-start(s32[12,2]{0,1:T(2,128)} %param.12) | copy-start | bytes 292
  50.2 8.7 %collective-permute-start.6 = (bf16[2,10,48,128]{3,2,1,0:T(8,128)(2,1)S(1)}, bf16[2,10,48,128]{3,2,1,0:T(8,128)(2,1)S(1)}, u32[]{:S(2)}, u32[]{:S(2)}) collective-permute-start(bf16[2,10,48,128]{3,2,1,0:T(8,128)(2,1)S(1)} %get-tuple-element.47.refs_0_), channel_id=1, source_target_pairs={{0,2},{1,3},{2,0},{3,1},{4,6},{5,7},{6,4},{7,5},{8,10},{9,11},{10,... | collective-permute-start | bytes 737288 | tf_op jit(solution)/shard_map/ppermute | solution.py:603
  50.8 4.4 %collective-permute-start.9 = (bf16[4,14,48,128]{3,2,1,0:T(8,128)(2,1)S(1)}, bf16[4,14,48,128]{3,2,1,0:T(8,128)(2,1)S(1)}, u32[]{:S(2)}, u32[]{:S(2)}) collective-permute-start(bf16[4,14,48,128]{3,2,1,0:T(8,128)(2,1)S(1)} %filtered.2.refs_0_), channel_id=1, source_target_pairs={{0,1},{1,0},{2,3},{3,2},{4,5},{5,4},{6,7},{7,6},{8,9},{9,8},{10,11... | collective-permute-start | bytes 2064392 | tf_op jit(solution)/shard_map/ppermute | solution.py:606
  50.9 4.3 %collective-permute-start.10 = (bf16[4,14,48,128]{3,2,1,0:T(8,128)(2,1)}, bf16[4,14,48,128]{3,2,1,0:T(8,128)(2,1)S(1)}, u32[]{:S(2)}, u32[]{:S(2)}) collective-permute-start(bf16[4,14,48,128]{3,2,1,0:T(8,128)(2,1)} %collective-permute-done.7.refs_2_), channel_id=1, source_target_pairs={{0,1},{1,0},{2,3},{3,2},{4,5},{5,4},{6,7},{7,6},{8,9},{9,8},{10,11... | collective-permute-start | bytes 2064392 | tf_op jit(solution)/shard_map/ppermute | solution.py:607
  51.4 3.8 %collective-permute-start.11 = (f32[24,128]{1,0:T(8,128)S(1)}, f32[24,128]{1,0:T(8,128)S(1)}, u32[]{:S(2)}, u32[]{:S(2)}) collective-permute-start(f32[24,128]{1,0:T(8,128)S(1)} %add.9), channel_id=1, source_target_pairs={{0,8},{4,12},{8,0},{12,4},{16,24},{20,28},{24,16},{28,20},{1,9},{5... | collective-permute-start | bytes 36872 | tf_op jit(solution)/shard_map/ppermute | solution.py:591
  55.1 11.4 %copy-start.7 = (f32[8]{0:T(128)S(1)}, f32[8]{0:T(128)}, u32[]{:S(2)}) copy-start(f32[8]{0:T(128)} %param.10) | copy-start | bytes 100
  57.3 9.3 %collective-permute-start.14 = (bf16[2,14,48,128]{3,2,1,0:T(8,128)(2,1)S(1)}, bf16[2,14,48,128]{3,2,1,0:T(8,128)(2,1)S(1)}, u32[]{:S(2)}, u32[]{:S(2)}) collective-permute-start(bf16[2,14,48,128]{3,2,1,0:T(8,128)(2,1)S(1)} %get-tuple-element.55), channel_id=1, source_target_pairs={{0,4},{4,0},{8,12},{12,8},{16,20},{20,16},{24,28},{28,24},{1,5},{5... | collective-permute-start | bytes 1032200 | tf_op jit(solution)/shard_map/ppermute | solution.py:611
  58.9 7.6 %collective-permute-start.12 = (bf16[2,10,48,128]{3,2,1,0:T(8,128)(2,1)S(1)}, bf16[2,10,48,128]{3,2,1,0:T(8,128)(2,1)S(1)}, u32[]{:S(2)}, u32[]{:S(2)}) collective-permute-start(bf16[2,10,48,128]{3,2,1,0:T(8,128)(2,1)S(1)} %collective-permute-done.6.refs_2_), channel_id=1, source_target_pairs={{0,1},{1,0},{2,3},{3,2},{4,5},{5,4},{6,7},{7,6},{8,9},{9,8},{10,11... | collective-permute-start | bytes 737288 | tf_op jit(solution)/shard_map/ppermute | solution.py:614
  58.9 8.4 %collective-permute-start.16 = (bf16[2,10,48,128]{3,2,1,0:T(8,128)(2,1)S(1)}, bf16[2,10,48,128]{3,2,1,0:T(8,128)(2,1)S(1)}, u32[]{:S(2)}, u32[]{:S(2)}) collective-permute-start(bf16[2,10,48,128]{3,2,1,0:T(8,128)(2,1)S(1)} %get-tuple-element.47.refs_0_), channel_id=1, source_target_pairs={{0,1},{1,0},{2,3},{3,2},{4,5},{5,4},{6,7},{7,6},{8,9},{9,8},{10,11... | collective-permute-start | bytes 737288 | tf_op jit(solution)/shard_map/ppermute | solution.py:601
  59.4 10.0 %collective-permute-start.20 = (bf16[2,10,48,128]{3,2,1,0:T(8,128)(2,1)S(1)}, bf16[2,10,48,128]{3,2,1,0:T(8,128)(2,1)S(1)}, u32[]{:S(2)}, u32[]{:S(2)}) collective-permute-start(bf16[2,10,48,128]{3,2,1,0:T(8,128)(2,1)S(1)} %get-tuple-element.65.a), channel_id=1, source_target_pairs={{0,2},{1,3},{2,0},{3,1},{4,6},{5,7},{6,4},{7,5},{8,10},{9,11},{10,... | collective-permute-start | bytes 737288 | tf_op jit(solution)/shard_map/ppermute | solution.py:613
  62.0 4.6 %collective-permute-start.13 = (f32[24,128]{1,0:T(8,128)S(1)}, f32[24,128]{1,0:T(8,128)S(1)}, u32[]{:S(2)}, u32[]{:S(2)}) collective-permute-start(f32[24,128]{1,0:T(8,128)S(1)} %add.10), channel_id=1, source_target_pairs={{0,16},{4,20},{8,24},{12,28},{16,0},{20,4},{24,8},{28,12},{1,17},{... | collective-permute-start | bytes 36872 | tf_op jit(solution)/shard_map/ppermute | solution.py:591
  66.8 2.7 %collective-permute-start.15 = (bf16[16,128]{1,0:T(8,128)(2,1)S(1)}, bf16[16,128]{1,0:T(8,128)(2,1)S(1)}, u32[]{:S(2)}, u32[]{:S(2)}) collective-permute-start(bf16[16,128]{1,0:T(8,128)(2,1)S(1)} %coefficients.1), channel_id=1, source_target_pairs={{0,1},{1,0},{2,3},{3,2},{4,5},{5,4},{6,7},{7,6},{8,9},{9,8},{10,11... | collective-permute-start | bytes 12296 | tf_op jit(solution)/shard_map/ppermute | solution.py:619
  66.8 8.8 %collective-permute-start.19 = (bf16[2,10,48,128]{3,2,1,0:T(8,128)(2,1)S(1)}, bf16[2,10,48,128]{3,2,1,0:T(8,128)(2,1)S(1)}, u32[]{:S(2)}, u32[]{:S(2)}) collective-permute-start(bf16[2,10,48,128]{3,2,1,0:T(8,128)(2,1)S(1)} %get-tuple-element.65.a), channel_id=1, source_target_pairs={{0,1},{1,0},{2,3},{3,2},{4,5},{5,4},{6,7},{7,6},{8,9},{9,8},{10,11... | collective-permute-start | bytes 737288 | tf_op jit(solution)/shard_map/ppermute | solution.py:602
  67.9 8.0 %collective-permute-start.18 = (bf16[2,10,48,128]{3,2,1,0:T(8,128)(2,1)S(1)}, bf16[2,10,48,128]{3,2,1,0:T(8,128)(2,1)S(1)}, u32[]{:S(2)}, u32[]{:S(2)}) collective-permute-start(bf16[2,10,48,128]{3,2,1,0:T(8,128)(2,1)S(1)} %rotated.3), channel_id=1, source_target_pairs={{0,4},{4,0},{8,12},{12,8},{16,20},{20,16},{24,28},{28,24},{1,5},{5... | collective-permute-start | bytes 737288 | tf_op jit(solution)/shard_map/ppermute | solution.py:621
  69.4 6.2 %collective-permute-start.21 = (bf16[2,10,48,128]{3,2,1,0:T(8,128)(2,1)S(1)}, bf16[2,10,48,128]{3,2,1,0:T(8,128)(2,1)S(1)}, u32[]{:S(2)}, u32[]{:S(2)}) collective-permute-start(bf16[2,10,48,128]{3,2,1,0:T(8,128)(2,1)S(1)} %collective-permute-done.20.c), channel_id=1, source_target_pairs={{0,1},{1,0},{2,3},{3,2},{4,5},{5,4},{6,7},{7,6},{8,9},{9,8},{10,11... | collective-permute-start | bytes 737288 | tf_op jit(solution)/shard_map/ppermute | solution.py:627
  69.5 4.2 %collective-permute-start.17 = (bf16[32,128]{1,0:T(8,128)(2,1)S(1)}, bf16[32,128]{1,0:T(8,128)(2,1)S(1)}, u32[]{:S(2)}, u32[]{:S(2)}) collective-permute-start(bf16[32,128]{1,0:T(8,128)(2,1)S(1)} %pad_maximum_fusion), channel_id=1, source_target_pairs={{0,2},{1,3},{2,0},{3,1},{4,6},{5,7},{6,4},{7,5},{8,10},{9,11},{10,... | collective-permute-start | bytes 24584 | tf_op jit(solution)/shard_map/ppermute | solution.py:623

commit v14 on v13

--- a/solution.py
+++ b/solution.py
@@ -90,45 +90,31 @@
     )(*(pltpu.with_memory_space_constraint(a, pltpu.MemorySpace.HBM) for a in (psi, potential)))
 
 
-def pack_kernel(early, psi, beta, to_x2, far, sem):
+def pack_kernel(early, psi, beta, to_x2, far, near, sem):
     x = lax.rem(lax.axis_index("space"), 2)
     half = psi.shape[1] // 2
     later = half + 2 - early
-    _, _, lines, width = beta.shape
-    gap = jnp.zeros((lines, 64 - width), F32)
     copy = pltpu.make_async_copy(
-        psi.at[:, pl.ds((half - 2) * (1 - x) + early, later)], to_x2.at[:, pl.ds(0, later)], sem
+        psi.at[:, pl.ds((half - 2) * (1 - x) + early, later)], to_x2, sem
     )
     copy.start()
-    each = beta.shape[0] // to_x2.shape[0]
-
-    def pack(i, carry):
-        for plane in range(to_x2.shape[0]):
-            first, second = (beta[plane * each + i, k].astype(F32) for k in range(2))
-            to_x2[plane, later + i] = jnp.concatenate(
-                [first, gap, second, gap], axis=1
-            ).astype(BF16)
-        return carry
-
     far[...] = beta[:, x]
-    lax.fori_loop(0, each, pack, 0)
+    near[...] = beta[:, 1 - x]
     copy.wait()
 
 
 def packed(psi, beta, early):
     planes, width_x, width_y, orbs = psi.shape
-    rows = width_x // 2 + 2 - early + beta.shape[0] // planes
+    side = jax.ShapeDtypeStruct((beta.shape[0], *beta.shape[2:]), BF16)
+    later = width_x // 2 + 2 - early
     return pl.pallas_call(
         functools.partial(pack_kernel, early),
-        out_shape=(
-            jax.ShapeDtypeStruct((planes, rows, width_y, orbs), BF16),
-            jax.ShapeDtypeStruct((beta.shape[0], *beta.shape[2:]), BF16),
-        ),
+        out_shape=(jax.ShapeDtypeStruct((planes, later, width_y, orbs), BF16), side, side),
         in_specs=[
             pl.BlockSpec(memory_space=pltpu.MemorySpace.HBM),
             pl.BlockSpec(memory_space=pltpu.VMEM),
         ],
-        out_specs=(pl.BlockSpec(memory_space=pltpu.VMEM),) * 2,
+        out_specs=(pl.BlockSpec(memory_space=pltpu.VMEM),) * 3,
         scratch_shapes=[pltpu.SemaphoreType.DMA],
         compiler_params=params(),
         cost_estimate=cost(4096, 4096),
@@ -148,9 +134,7 @@
 
     for k in range(2):
         plane = x if k == 0 else 1 - x
-        there = beyond if k == 0 else side
-        each = count // b_x.shape[0]
-        begin = b_x.shape[1] - each
+        outer, there = (b_d, beyond) if k == 0 else (b_x, side)
         u = (potential[plane] - 1.0) * 0.25
 
         def fill(i, carry):
@@ -160,12 +144,7 @@
                 next_to = (jnp.abs(there - atoms[p]) <= 1).astype(F32)
                 b32 = beta[p, plane].astype(F32) * here
                 b = b32.astype(BF16)
-                if k == 0:
-                    other = b_d[p].astype(F32)
-                else:
-                    both = b_x[p // each, begin + lax.rem(p, each)].astype(F32)
-                    other = jnp.where(x == 0, both[:, :width], both[:, 64 : 64 + width])
-                sides = beta[p, 1 - plane].astype(F32) * here + other * next_to
+                sides = beta[p, 1 - plane].astype(F32) * here + outer[p].astype(F32) * next_to
                 whole = jnp.dot(b, tri, preferred_element_type=F32)
                 whole = whole + jnp.dot(tri, b, preferred_element_type=F32)
                 whole = whole + u * b32 - 0.125 * sides
@@ -564,7 +543,8 @@
     theirs = (half - 2) * (1 - x)
 
     to_x, to_z = prepared(psi, potential, early)
-    to_x2, far = packed(psi, beta, early)
+    to_x2, far, near = packed(psi, beta, early)
+    f_x = lax.ppermute(near, "space", swap)
     raster = within([(i, i + 1 if i % 2 else i - 1) for i in range(slabs)])
     f_d = lax.ppermute(far, "space", raster)
     xr1 = lax.ppermute(to_x, "space", swap)
@@ -578,18 +558,19 @@
     zf2 = lax.ppermute(xr2, "space", other_way)
     strong = jnp.broadcast_to(strength[:, None], (count, orbs))
 
-    zf1, _ = ordered(zf1, xr2)
+    sums, weights = partials(count, atom_slab, psi, beta, f_x, f_d, potential, gram)
+    zf1, sums, _ = ordered(zf1, sums, xr2)
     operands = (psi, potential, zo)
     (block1,) = filtered(slabs, 0, rows1, True, operands, (xr1,), (zf1,))
     y1 = lax.ppermute(block1, "orb", across)
-    f_d, _ = ordered(f_d, block1)
-    sums, weights = partials(count, atom_slab, psi, beta, xr2, f_d, potential, gram)
     rounds = [1 << k for k in range((slabs - 1).bit_length())]
 
     def added(values, step):
         pairs = [(i, i ^ step) for i in range(slabs)]
         return values + lax.ppermute(values, "space", pairs)
 
+    for step in rounds[:2]:
+        sums = added(sums, step)
     zf2, sums = ordered(zf2, sums)
     give2, keep2 = filtered(slabs, rows1, rows2, False, operands, (xr1, xr2), (zf1, zf2))
     pattern, q_tiles, _ = ordered(pattern, q_tiles, give2)
@@ -601,22 +582,20 @@
     cg = lax.ppermute(give2, "orb", beside)
     ck = lax.ppermute(keep2, "orb", beside)
     yg = lax.ppermute(give2, "orb", across)
-    sums = added(sums, rounds[0])
-    y1, again, _, sums = ordered(y1, block1, give2, sums)
+    y1, again, _ = ordered(y1, block1, give2)
     c1 = lax.ppermute(again, "orb", beside)
     yc1 = lax.ppermute(y1, "orb", beside)
-    sums = added(sums, rounds[1])
+    for step in rounds[2:]:
+        sums = added(sums, step)
     yc1, sums = ordered(yc1, sums)
     give1, keep1 = rotated((block1, c1, y1, yc1), q, 2)
     got1 = lax.ppermute(give1, "space", swap)
     keep_y, yg, _, sums = ordered(keep2, yg, give1, sums)
     yk = lax.ppermute(keep_y, "orb", across)
     ycg = lax.ppermute(yg, "orb", beside)
-    for step in rounds[2:]:
-        sums = added(sums, step)
-    ycg, sums, got1 = ordered(ycg, sums, got1)
     coefs = coefficients(sums, strong)
     coefs = jnp.concatenate([coefs, lax.ppermute(coefs, "orb", beside)], axis=0)
+    ycg, coefs, got1 = ordered(ycg, coefs, got1)
     (give2,) = rotated((give2, cg, yg, ycg), q, 1)
     got2 = lax.ppermute(give2, "space", swap)
     coefs, _ = ordered(coefs, give2)

time: 78 us -> 81.2 us (1.041)
  waiting for transfers between devices: 20 us -> 28.8 us
  starting transfers between devices: 33.6 us -> 27.6 us
    ppermute x1, waiting for transfers between devices: 0.01 us -> 6.13 us  [shards(): got1 = lax.ppermute(give1, 'space', swap)]
    ppermute x1, waiting for transfers between devices: 6.56 us -> 2.18 us  [shards(): xr2 = lax.ppermute(second, 'space', swap)]
    ppermute x0 -> x1, starting transfers between devices: none -> 2.83 us  [shards(): f_x = lax.ppermute(near, 'space', swap)]
    ppermute x1, waiting for transfers between devices: 0.01 us -> 2.4 us  [shards(): yc1 = lax.ppermute(y1, 'orb', beside)]
    ppermute x3, starting transfers between devices: 6.37 us -> 4.27 us  [added(): return values + lax.ppermute(values, 'space', pairs)]
    ppermute x3, waiting for transfers between devices: 3.8 us -> 5.81 us  [added(): return values + lax.ppermute(values, 'space', pairs)]
    ppermute x1, waiting for transfers between devices: 0.75 us -> 2.54 us  [shards(): zf1 = lax.ppermute(xr1, 'space', other_way)]
    ppermute x1, waiting for transfers between devices: 6.91 us -> 5.25 us  [shards(): xr1 = lax.ppermute(to_x, 'space', swap)]
  transfers between devices with their start and end apart: 22 -> 23, of which waited for: 7 -> 10; matrix products, arithmetic and copies ran while one was open for 1% -> 1% of each run, Pallas kernels for 24% -> 17%
where the time goes in v14:
time: 81.2 us; the launch traced here: 80.8 us
  waiting for transfers between devices  28.8 us (35%)
  starting transfers between devices  27.6 us (34%)
  Pallas kernels  22.3 us (27%)
  local copies, waits for them, and re-layouts  0.94 us (1%)
    pallas_call x2, Pallas kernels, filtered(): pl.pallas_call(functools.partial(filter_kernel, slabs, start, parts, join...  9.12 us
    ppermute x1, waiting for transfers between devices, shards(): got1 = lax.ppermute(give1, 'space', swap)  6.13 us
    ppermute x3, waiting for transfers between devices, added(): return values + lax.ppermute(values, 'space', pairs)  5.81 us
    ppermute x1, waiting for transfers between devices, shards(): xr1 = lax.ppermute(to_x, 'space', swap)  5.25 us
    ppermute x1, starting transfers between devices, shards(): zf2 = lax.ppermute(xr2, 'space', other_way)  4.28 us
    ppermute x3, starting transfers between devices, added(): return values + lax.ppermute(values, 'space', pairs)  4.27 us
    ppermute x1, starting transfers between devices, shards(): zf1 = lax.ppermute(xr1, 'space', other_way)  3.97 us
    pallas_call x1, Pallas kernels, partials(): pl.pallas_call(functools.partial(partial_kernel, count), out_shape=(jax.S...  3.04 us
  transfers between devices with their start and end apart: 23, of which 10 were waited for; matrix products, arithmetic and copies ran while one was open for 1% of the time, Pallas kernels for 17%

profile of v14, /device:TPU:0, one launch (start us, length us, event | category | flops | bytes accessed | tf_op | source)
XLA Modules:
  0.0 80.8 jit_solution(13985038234850564026)
XLA Ops:
  0.0 2.2 %prepared.1 = (bf16[2,19,48,128]{3,2,1,0:T(8,128)(2,1)S(1)}, bf16[2,27,48,128]{3,2,1,0:T(8,128)(2,1)}) custom-call(bf16[2,48,48,128]{3,2,1,0:T(8,128)(2,1)} %refs_0_.3, f32[2,48,48]{2,1,0:T(8,128)} %refs_1_.3), custom_call_target="tpu_custom_call" | custom-call | flops 256 | bytes 256 | tf_op jit(solution)/shard_map/prepared/pallas_call | solution.py:81
  2.2 0.0 copy-start.1
  2.2 0.0 copy-start.3
  2.2 3.0 %collective-permute-start.1 = (bf16[2,19,48,128]{3,2,1,0:T(8,128)(2,1)S(1)}, bf16[2,19,48,128]{3,2,1,0:T(8,128)(2,1)}, u32[]{:S(2)}, u32[]{:S(2)}) collective-permute-start(bf16[2,19,48,128]{3,2,1,0:T(8,128)(2,1)S(1)} %get-tuple-element.37), channel_id=1, source_target_pairs={{0,4},{4,0},{8,12},{12,8},{16,20},{20,16},{24,28},{28,24},{1,5},{5... | collective-permute-start | bytes 1400840 | tf_op jit(solution)/shard_map/ppermute | solution.py:550
  5.2 1.3 %collective-permute-start = (bf16[2,27,48,128]{3,2,1,0:T(8,128)(2,1)}, bf16[2,27,48,128]{3,2,1,0:T(8,128)(2,1)S(1)}, u32[]{:S(2)}, u32[]{:S(2)}) collective-permute-start(bf16[2,27,48,128]{3,2,1,0:T(8,128)(2,1)} %get-tuple-element.36), channel_id=1, source_target_pairs={{4,12},{8,0},{12,20},{16,8},{20,28},{24,16},{5,13},{9,1},{13,21},{... | collective-permute-start | bytes 1990664 | tf_op jit(solution)/shard_map/ppermute | solution.py:551
  6.5 1.6 %packed.1 = (bf16[2,8,48,128]{3,2,1,0:T(8,128)(2,1)S(1)}, bf16[8,48,48]{2,1,0:T(8,128)(2,1)S(1)}, bf16[8,48,48]{2,1,0:T(8,128)(2,1)}) custom-call(bf16[2,48,48,128]{3,2,1,0:T(8,128)(2,1)} %refs_0_.3, bf16[8,2,48,48]{3,2,1,0:T(8,128)(2,1)S(1)} %copy-done.2), custom_call_target="tpu_custom_call" | custom-call | flops 256 | bytes 256 | tf_op jit(solution)/shard_map/packed/pallas_call | solution.py:110
  8.1 2.8 %collective-permute-start.4 = (bf16[8,48,48]{2,1,0:T(8,128)(2,1)}, bf16[8,48,48]{2,1,0:T(8,128)(2,1)S(1)}, u32[]{:S(2)}, u32[]{:S(2)}) collective-permute-start(bf16[8,48,48]{2,1,0:T(8,128)(2,1)} %get-tuple-element.41), channel_id=1, source_target_pairs={{0,4},{4,0},{8,12},{12,8},{16,20},{20,16},{24,28},{28,24},{1,5},{5... | collective-permute-start | bytes 110600 | tf_op jit(solution)/shard_map/ppermute | solution.py:547
  10.9 0.7 collective-permute-start.5
  11.6 5.2 %collective-permute-done.1.refs_3_ = bf16[2,19,48,128]{3,2,1,0:T(8,128)(2,1)} collective-permute-done((bf16[2,19,48,128]{3,2,1,0:T(8,128)(2,1)S(1)}, bf16[2,19,48,128]{3,2,1,0:T(8,128)(2,1)}, u32[]{:S(2)}, u32[]{:S(2)}) %collective-permute-start.1) | collective-permute-done | bytes 466976 | tf_op jit(solution)/shard_map/ppermute | solution.py:550
  16.8 4.0 %collective-permute-start.3 = (bf16[2,19,48,128]{3,2,1,0:T(8,128)(2,1)}, bf16[2,19,48,128]{3,2,1,0:T(8,128)(2,1)S(1)}, u32[]{:S(2)}, u32[]{:S(2)}) collective-permute-start(bf16[2,19,48,128]{3,2,1,0:T(8,128)(2,1)} %collective-permute-done.1.refs_3_), channel_id=1, source_target_pairs={{0,8},{8,16},{12,4},{16,24},{20,12},{28,20},{1,9},{9,17},{13,5},{1... | collective-permute-start | bytes 1400840 | tf_op jit(solution)/shard_map/ppermute | solution.py:556
  20.8 0.1 collective-permute-start.2
  20.9 0.1 broadcast_select_fusion
  21.0 0.3 convolution_bitcast_fusion.gram
  21.3 0.0 collective-permute-done.4.b_x
  21.3 0.0 collective-permute-done.5.b_d
  21.3 0.0 copy-done.1
  21.3 3.0 %partials.1 = (f32[24,128]{1,0:T(8,128)S(1)}, bf16[2,48,24,48]{3,2,1,0:T(8,128)(2,1)S(1)}) custom-call(s32[8]{0:T(128)S(1)} %copy-done.6, bf16[2,48,48,128]{3,2,1,0:T(8,128)(2,1)S(1)} %copy-done.1, bf16[8,2,48,48]{3,2,1,0:T(8,128)(2,1)S(1)} %copy-done.2, bf16[8,48,48]{2,1,0:T(8,128)(2,1)S(1)} %collective-permute-done.4.b_x, ...), custom_call_target="tpu_custom_call" | custom-call | flops 256 | bytes 256 | tf_op jit(solution)/shard_map/partials/pallas_call | solution.py:177
  24.4 2.2 %collective-permute-done.2.refs_4_ = bf16[2,8,48,128]{3,2,1,0:T(8,128)(2,1)S(1)} collective-permute-done((bf16[2,8,48,128]{3,2,1,0:T(8,128)(2,1)S(1)}, bf16[2,8,48,128]{3,2,1,0:T(8,128)(2,1)S(1)}, u32[]{:S(2)}, u32[]{:S(2)}) %collective-permute-start.2) | collective-permute-done | bytes 196640 | tf_op jit(solution)/shard_map/ppermute | solution.py:557
  26.6 2.5 %collective-permute-done.3.refs_5_.refs_4_ = bf16[2,19,48,128]{3,2,1,0:T(8,128)(2,1)S(1)} collective-permute-done((bf16[2,19,48,128]{3,2,1,0:T(8,128)(2,1)}, bf16[2,19,48,128]{3,2,1,0:T(8,128)(2,1)S(1)}, u32[]{:S(2)}, u32[]{:S(2)}) %collective-permute-start.3) | collective-permute-done | bytes 466976 | tf_op jit(solution)/shard_map/ppermute | solution.py:556
  29.1 0.0 collective-permute-done.refs_2_
  29.1 0.8 copy-done.7
  29.9 5.0 %filtered.3.refs_0_ = bf16[4,14,48,128]{3,2,1,0:T(8,128)(2,1)S(1)} custom-call(bf16[2,48,48,128]{3,2,1,0:T(8,128)(2,1)S(1)} %copy-done.1, f32[2,48,48]{2,1,0:T(8,128)S(1)} %copy-done.3, bf16[2,27,48,128]{3,2,1,0:T(8,128)(2,1)S(1)} %collective-permute-done.refs_2_, bf16[2,19,48,128]{3,2,1,0:T(8,128)(2,1)} %collective-permute-done.1.refs_3_, ...), custom_call_target="tpu_custom_call" | custom-call | flops 3440640 | bytes 21504000 | tf_op jit(solution)/shard_map/filtered/pallas_call | solution.py:415
  34.9 1.6 %collective-permute-start.10 = (bf16[4,14,48,128]{3,2,1,0:T(8,128)(2,1)S(1)}, bf16[4,14,48,128]{3,2,1,0:T(8,128)(2,1)}, u32[]{:S(2)}, u32[]{:S(2)}) collective-permute-start(bf16[4,14,48,128]{3,2,1,0:T(8,128)(2,1)S(1)} %filtered.3.refs_0_), channel_id=1, source_target_pairs={{0,2},{1,3},{2,0},{3,1},{4,6},{5,7},{6,4},{7,5},{8,10},{9,11},{10,... | collective-permute-start | bytes 2064392 | tf_op jit(solution)/shard_map/ppermute | solution.py:565
  36.5 4.3 %collective-permute-start.6 = (bf16[2,8,48,128]{3,2,1,0:T(8,128)(2,1)S(1)}, bf16[2,8,48,128]{3,2,1,0:T(8,128)(2,1)S(1)}, u32[]{:S(2)}, u32[]{:S(2)}) collective-permute-start(bf16[2,8,48,128]{3,2,1,0:T(8,128)(2,1)S(1)} %collective-permute-done.2.refs_4_), channel_id=1, source_target_pairs={{0,8},{8,16},{12,4},{16,24},{20,12},{28,20},{1,9},{9,17},{13,5},{1... | collective-permute-start | bytes 589832 | tf_op jit(solution)/shard_map/ppermute | solution.py:558
  40.8 0.1 collective-permute-start.7
  40.9 3.7 %collective-permute-done.7 = f32[24,128]{1,0:T(8,128)S(1)} collective-permute-done((f32[24,128]{1,0:T(8,128)S(1)}, f32[24,128]{1,0:T(8,128)S(1)}, u32[]{:S(2)}, u32[]{:S(2)}) %collective-permute-start.7) | collective-permute-done | bytes 12320 | tf_op jit(solution)/shard_map/ppermute | solution.py:570
  44.5 1.6 %collective-permute-start.8 = (f32[24,128]{1,0:T(8,128)S(1)}, f32[24,128]{1,0:T(8,128)S(1)}, u32[]{:S(2)}, u32[]{:S(2)}) collective-permute-start(f32[24,128]{1,0:T(8,128)S(1)} %add.9), channel_id=1, source_target_pairs={{0,8},{4,12},{8,0},{12,4},{16,24},{20,28},{24,16},{28,20},{1,9},{5... | collective-permute-start | bytes 36872 | tf_op jit(solution)/shard_map/ppermute | solution.py:570
  46.1 2.1 %collective-permute-done.8 = f32[24,128]{1,0:T(8,128)S(1)} collective-permute-done((f32[24,128]{1,0:T(8,128)S(1)}, f32[24,128]{1,0:T(8,128)S(1)}, u32[]{:S(2)}, u32[]{:S(2)}) %collective-permute-start.8) | collective-permute-done | bytes 12320 | tf_op jit(solution)/shard_map/ppermute | solution.py:570
  48.2 0.0 collective-permute-done.6.refs_6_
  48.3 0.0 copy-start.9
  48.3 2.6 %collective-permute-start.13 = (f32[24,128]{1,0:T(8,128)S(1)}, f32[24,128]{1,0:T(8,128)S(1)}, u32[]{:S(2)}, u32[]{:S(2)}) collective-permute-start(f32[24,128]{1,0:T(8,128)S(1)} %add.10), channel_id=1, source_target_pairs={{0,16},{4,20},{8,24},{12,28},{16,0},{20,4},{24,8},{28,12},{1,17},{... | collective-permute-start | bytes 36872 | tf_op jit(solution)/shard_map/ppermute | solution.py:570
  50.9 4.1 %filtered.2 = (bf16[2,10,48,128]{3,2,1,0:T(8,128)(2,1)S(1)}, bf16[2,10,48,128]{3,2,1,0:T(8,128)(2,1)S(1)}) custom-call(bf16[2,48,48,128]{3,2,1,0:T(8,128)(2,1)S(1)} %copy-done.1, f32[2,48,48]{2,1,0:T(8,128)S(1)} %copy-done.3, bf16[2,27,48,128]{3,2,1,0:T(8,128)(2,1)S(1)} %collective-permute-done.refs_2_, ...), custom_call_target="tpu_custom_call" | custom-call | flops 2457600 | bytes 15360000 | tf_op jit(solution)/shard_map/filtered/pallas_call | solution.py:415
  55.1 0.6 collective-permute-start.9
  55.6 0.0 collective-permute-done.10.refs_2_
  55.6 0.0 collective-permute-start.11
  55.6 0.5 collective-permute-start.12
  56.2 0.3 fusion
  56.6 0.0 collective-permute-done.13
  56.6 0.0 copy-start.10
  56.6 2.4 %collective-permute-done.12.refs_3_ = bf16[4,14,48,128]{3,2,1,0:T(8,128)(2,1)S(1)} collective-permute-done((bf16[4,14,48,128]{3,2,1,0:T(8,128)(2,1)}, bf16[4,14,48,128]{3,2,1,0:T(8,128)(2,1)S(1)}, u32[]{:S(2)}, u32[]{:S(2)}) %collective-permute-start.12) | collective-permute-done | bytes 688160 | tf_op jit(solution)/shard_map/ppermute | solution.py:587
  59.0 0.0 collective-permute-done.11.refs_1_
  59.0 2.1 %rotated.2 = (bf16[2,14,48,128]{3,2,1,0:T(8,128)(2,1)S(1)}, bf16[2,14,48,128]{3,2,1,0:T(8,128)(2,1)S(1)}) custom-call(bf16[4,14,48,128]{3,2,1,0:T(8,128)(2,1)S(1)} %filtered.3.refs_0_, bf16[4,14,48,128]{3,2,1,0:T(8,128)(2,1)S(1)} %collective-permute-done.11.refs_1_, bf16[4,14,48,128]{3,2,1,0:T(8,128)(2,1)} %collective-permute-done.10.refs_2_, ...), custom_call_target="tpu_custom_call" | custom-call | flops 22020096 | bytes 215040 | tf_op jit(solution)/shard_map/rotated/pallas_call | solution.py:459
  61.1 0.4 collective-permute-start.16
  61.6 0.0 collective-permute-done.9.refs_2_
  61.6 0.0 collective-permute-start.14
  61.6 0.5 collective-permute-start.17
  62.1 1.5 %collective-permute-start.21 = (bf16[2,10,48,128]{3,2,1,0:T(8,128)(2,1)S(1)}, bf16[2,10,48,128]{3,2,1,0:T(8,128)(2,1)S(1)}, u32[]{:S(2)}, u32[]{:S(2)}) collective-permute-start(bf16[2,10,48,128]{3,2,1,0:T(8,128)(2,1)S(1)} %get-tuple-element.65.a), channel_id=1, source_target_pairs={{0,2},{1,3},{2,0},{3,1},{4,6},{5,7},{6,4},{7,5},{8,10},{9,11},{10,... | collective-permute-start | bytes 737288 | tf_op jit(solution)/shard_map/ppermute | solution.py:594
  63.6 0.1 broadcast_in_dim.22.strength
  63.7 0.1 coefficients.1
  63.8 0.0 collective-permute-start.15
  63.9 1.2 %collective-permute-done.15 = bf16[16,128]{1,0:T(8,128)(2,1)S(1)} collective-permute-done((bf16[16,128]{1,0:T(8,128)(2,1)S(1)}, bf16[16,128]{1,0:T(8,128)(2,1)S(1)}, u32[]{:S(2)}, u32[]{:S(2)}) %collective-permute-start.15) | collective-permute-done | bytes 4128 | tf_op jit(solution)/shard_map/ppermute | solution.py:597
  65.0 0.2 collective-permute-start.20
  65.2 0.0 collective-permute-done.14.refs_3_
  65.2 6.1 %collective-permute-done.16.got1 = bf16[2,14,48,128]{3,2,1,0:T(8,128)(2,1)S(1)} collective-permute-done((bf16[2,14,48,128]{3,2,1,0:T(8,128)(2,1)S(1)}, bf16[2,14,48,128]{3,2,1,0:T(8,128)(2,1)S(1)}, u32[]{:S(2)}, u32[]{:S(2)}) %collective-permute-start.16) | collective-permute-done | bytes 344096 | tf_op jit(solution)/shard_map/ppermute | solution.py:592
  71.3 0.5 rotated.3
  71.9 0.4 collective-permute-start.19
  72.3 1.5 %collective-permute-start.18 = (bf16[32,128]{1,0:T(8,128)(2,1)S(1)}, bf16[32,128]{1,0:T(8,128)(2,1)S(1)}, u32[]{:S(2)}, u32[]{:S(2)}) collective-permute-start(bf16[32,128]{1,0:T(8,128)(2,1)S(1)} %pad_maximum_fusion), channel_id=1, source_target_pairs={{0,2},{1,3},{2,0},{3,1},{4,6},{5,7},{6,4},{7,5},{8,10},{9,11},{10,... | collective-permute-start | bytes 24584 | tf_op jit(solution)/shard_map/ppermute | solution.py:602
  73.8 0.0 collective-permute-start.22
  73.8 2.1 %collective-permute-done.18 = bf16[32,128]{1,0:T(8,128)(2,1)S(1)} collective-permute-done((bf16[32,128]{1,0:T(8,128)(2,1)S(1)}, bf16[32,128]{1,0:T(8,128)(2,1)S(1)}, u32[]{:S(2)}, u32[]{:S(2)}) %collective-permute-start.18) | collective-permute-done | bytes 8224 | tf_op jit(solution)/shard_map/ppermute | solution.py:602
  76.0 1.9 %nonlocal.1.term = f32[2,48,48,128]{3,2,1,0:T(8,128)S(1)} custom-call(bf16[16,128]{1,0:T(8,128)(2,1)S(1)} %get-tuple-element.70.a, bf16[16,128]{1,0:T(8,128)(2,1)S(1)} %get-tuple-element.69.b, bf16[16,128]{1,0:T(8,128)(2,1)S(1)} %get-tuple-element.68.c, bf16[16,128]{1,0:T(8,128)(2,1)S(1)} %get-tuple-element.67.d, bf16[4,128,128]{2,1,0:T(8,128)(2,1)S(1)} %copy.18.refs_4_.q, ...), custom_call_target="tpu_custom_call" | custom-call | flops 256 | bytes 256 | tf_op jit(solution)/shard_map/nonlocal/pallas_call | solution.py:252
  77.9 0.0 collective-permute-done.20.b
  77.9 0.0 collective-permute-done.22.d
  77.9 1.2 %collective-permute-done.19.got2 = bf16[2,10,48,128]{3,2,1,0:T(8,128)(2,1)S(1)} collective-permute-done((bf16[2,10,48,128]{3,2,1,0:T(8,128)(2,1)S(1)}, bf16[2,10,48,128]{3,2,1,0:T(8,128)(2,1)S(1)}, u32[]{:S(2)}, u32[]{:S(2)}) %collective-permute-start.19) | collective-permute-done | bytes 245792 | tf_op jit(solution)/shard_map/ppermute | solution.py:600
  79.1 1.7 %assembled.1 = bf16[2,48,48,128]{3,2,1,0:T(8,128)(2,1)} custom-call(f32[2,48,48,128]{3,2,1,0:T(8,128)S(1)} %nonlocal.1.term, bf16[2,14,48,128]{3,2,1,0:T(8,128)(2,1)S(1)} %get-tuple-element.63.keep1, bf16[2,14,48,128]{3,2,1,0:T(8,128)(2,1)S(1)} %collective-permute-done.16.got1, bf16[2,10,48,128]{3,2,1,0:T(8,128)(2,1)S(1)} %collective-permute-done.19.got2, ...), custom_call_target="tpu_custom_call" | custom-call | flops 256 | bytes 256 | tf_op jit(solution)/shard_map/assembled/pallas_call | solution.py:506
  (31 shorter events, 0.1 us)
Async XLA Ops:
  0.0 56.2 %copy-start = (bf16[12,128,128]{2,1,0:T(8,128)(2,1)S(1)}, bf16[12,128,128]{2,1,0:T(8,128)(2,1)}, u32[]{:S(2)}) copy-start(bf16[12,128,128]{2,1,0:T(8,128)(2,1)} %param.13) | copy-start | bytes 1179652
  0.0 6.5 %copy-start.2 = (bf16[8,2,48,48]{3,2,1,0:T(8,128)(2,1)S(1)}, bf16[8,2,48,48]{3,2,1,0:T(8,128)(2,1)}, u32[]{:S(2)}) copy-start(bf16[8,2,48,48]{3,2,1,0:T(8,128)(2,1)} %beta.3) | copy-start | bytes 221188
  0.0 20.8 %copy-start.6 = (s32[8]{0:T(128)S(1)}, s32[8]{0:T(128)}, u32[]{:S(2)}) copy-start(s32[8]{0:T(128)} %atoms.1) | copy-start | bytes 100
  2.2 19.1 %copy-start.1 = (bf16[2,48,48,128]{3,2,1,0:T(8,128)(2,1)S(1)}, bf16[2,48,48,128]{3,2,1,0:T(8,128)(2,1)}, u32[]{:S(2)}) copy-start(bf16[2,48,48,128]{3,2,1,0:T(8,128)(2,1)} %refs_0_.3) | copy-start | bytes 3538948
  2.2 19.1 %copy-start.3 = (f32[2,48,48]{2,1,0:T(8,128)S(1)}, f32[2,48,48]{2,1,0:T(8,128)}, u32[]{:S(2)}) copy-start(f32[2,48,48]{2,1,0:T(8,128)} %refs_1_.3) | copy-start | bytes 55300
  2.2 14.6 %collective-permute-start.1 = (bf16[2,19,48,128]{3,2,1,0:T(8,128)(2,1)S(1)}, bf16[2,19,48,128]{3,2,1,0:T(8,128)(2,1)}, u32[]{:S(2)}, u32[]{:S(2)}) collective-permute-start(bf16[2,19,48,128]{3,2,1,0:T(8,128)(2,1)S(1)} %get-tuple-element.37), channel_id=1, source_target_pairs={{0,4},{4,0},{8,12},{12,8},{16,20},{20,16},{24,28},{28,24},{1,5},{5... | collective-permute-start | bytes 1400840 | tf_op jit(solution)/shard_map/ppermute | solution.py:550
  5.2 23.9 %collective-permute-start = (bf16[2,27,48,128]{3,2,1,0:T(8,128)(2,1)}, bf16[2,27,48,128]{3,2,1,0:T(8,128)(2,1)S(1)}, u32[]{:S(2)}, u32[]{:S(2)}) collective-permute-start(bf16[2,27,48,128]{3,2,1,0:T(8,128)(2,1)} %get-tuple-element.36), channel_id=1, source_target_pairs={{4,12},{8,0},{12,20},{16,8},{20,28},{24,16},{5,13},{9,1},{13,21},{... | collective-permute-start | bytes 1990664 | tf_op jit(solution)/shard_map/ppermute | solution.py:551
  8.1 13.2 %collective-permute-start.4 = (bf16[8,48,48]{2,1,0:T(8,128)(2,1)}, bf16[8,48,48]{2,1,0:T(8,128)(2,1)S(1)}, u32[]{:S(2)}, u32[]{:S(2)}) collective-permute-start(bf16[8,48,48]{2,1,0:T(8,128)(2,1)} %get-tuple-element.41), channel_id=1, source_target_pairs={{0,4},{4,0},{8,12},{12,8},{16,20},{20,16},{24,28},{28,24},{1,5},{5... | collective-permute-start | bytes 110600 | tf_op jit(solution)/shard_map/ppermute | solution.py:547
  10.9 10.4 %collective-permute-start.5 = (bf16[8,48,48]{2,1,0:T(8,128)(2,1)S(1)}, bf16[8,48,48]{2,1,0:T(8,128)(2,1)S(1)}, u32[]{:S(2)}, u32[]{:S(2)}) collective-permute-start(bf16[8,48,48]{2,1,0:T(8,128)(2,1)S(1)} %get-tuple-element.42), channel_id=1, source_target_pairs={{4,8},{8,4},{12,16},{16,12},{20,24},{24,20},{5,9},{9,5},{13,17},{1... | collective-permute-start | bytes 110600 | tf_op jit(solution)/shard_map/ppermute | solution.py:549
  16.8 12.3 %collective-permute-start.3 = (bf16[2,19,48,128]{3,2,1,0:T(8,128)(2,1)}, bf16[2,19,48,128]{3,2,1,0:T(8,128)(2,1)S(1)}, u32[]{:S(2)}, u32[]{:S(2)}) collective-permute-start(bf16[2,19,48,128]{3,2,1,0:T(8,128)(2,1)} %collective-permute-done.1.refs_3_), channel_id=1, source_target_pairs={{0,8},{8,16},{12,4},{16,24},{20,12},{28,20},{1,9},{9,17},{13,5},{1... | collective-permute-start | bytes 1400840 | tf_op jit(solution)/shard_map/ppermute | solution.py:556
  20.8 5.7 %collective-permute-start.2 = (bf16[2,8,48,128]{3,2,1,0:T(8,128)(2,1)S(1)}, bf16[2,8,48,128]{3,2,1,0:T(8,128)(2,1)S(1)}, u32[]{:S(2)}, u32[]{:S(2)}) collective-permute-start(bf16[2,8,48,128]{3,2,1,0:T(8,128)(2,1)S(1)} %get-tuple-element.40), channel_id=1, source_target_pairs={{0,4},{4,0},{8,12},{12,8},{16,20},{20,16},{24,28},{28,24},{1,5},{5... | collective-permute-start | bytes 589832 | tf_op jit(solution)/shard_map/ppermute | solution.py:557
  24.4 10.5 %copy-start.4 = (bf16[2,48,24,48]{3,2,1,0:T(8,128)(2,1)}, bf16[2,48,24,48]{3,2,1,0:T(8,128)(2,1)S(1)}, u32[]{:S(2)}) copy-start(bf16[2,48,24,48]{3,2,1,0:T(8,128)(2,1)S(1)} %get-tuple-element.62.weights) | copy-start | bytes 663556
  26.6 24.3 %copy-start.8 = (bf16[2,8,48,128]{3,2,1,0:T(8,128)(2,1)}, bf16[2,8,48,128]{3,2,1,0:T(8,128)(2,1)S(1)}, u32[]{:S(2)}) copy-start(bf16[2,8,48,128]{3,2,1,0:T(8,128)(2,1)S(1)} %collective-permute-done.2.refs_4_) | copy-start | bytes 589828
  29.1 0.8 copy-start.7
  34.9 20.7 %collective-permute-start.10 = (bf16[4,14,48,128]{3,2,1,0:T(8,128)(2,1)S(1)}, bf16[4,14,48,128]{3,2,1,0:T(8,128)(2,1)}, u32[]{:S(2)}, u32[]{:S(2)}) collective-permute-start(bf16[4,14,48,128]{3,2,1,0:T(8,128)(2,1)S(1)} %filtered.3.refs_0_), channel_id=1, source_target_pairs={{0,2},{1,3},{2,0},{3,1},{4,6},{5,7},{6,4},{7,5},{8,10},{9,11},{10,... | collective-permute-start | bytes 2064392 | tf_op jit(solution)/shard_map/ppermute | solution.py:565
  36.5 11.8 %collective-permute-start.6 = (bf16[2,8,48,128]{3,2,1,0:T(8,128)(2,1)S(1)}, bf16[2,8,48,128]{3,2,1,0:T(8,128)(2,1)S(1)}, u32[]{:S(2)}, u32[]{:S(2)}) collective-permute-start(bf16[2,8,48,128]{3,2,1,0:T(8,128)(2,1)S(1)} %collective-permute-done.2.refs_4_), channel_id=1, source_target_pairs={{0,8},{8,16},{12,4},{16,24},{20,12},{28,20},{1,9},{9,17},{13,5},{1... | collective-permute-start | bytes 589832 | tf_op jit(solution)/shard_map/ppermute | solution.py:558
  40.8 3.8 %collective-permute-start.7 = (f32[24,128]{1,0:T(8,128)S(1)}, f32[24,128]{1,0:T(8,128)S(1)}, u32[]{:S(2)}, u32[]{:S(2)}) collective-permute-start(f32[24,128]{1,0:T(8,128)S(1)} %get-tuple-element.45), channel_id=1, source_target_pairs={{0,4},{4,0},{8,12},{12,8},{16,20},{20,16},{24,28},{28,24},{1,5},{5... | collective-permute-start | bytes 36872 | tf_op jit(solution)/shard_map/ppermute | solution.py:570
  44.5 3.7 %collective-permute-start.8 = (f32[24,128]{1,0:T(8,128)S(1)}, f32[24,128]{1,0:T(8,128)S(1)}, u32[]{:S(2)}, u32[]{:S(2)}) collective-permute-start(f32[24,128]{1,0:T(8,128)S(1)} %add.9), channel_id=1, source_target_pairs={{0,8},{4,12},{8,0},{12,4},{16,24},{20,28},{24,16},{28,20},{1,9},{5... | collective-permute-start | bytes 36872 | tf_op jit(solution)/shard_map/ppermute | solution.py:570
  48.2 7.9 %copy-start.11 = (s32[12,2]{0,1:T(2,128)S(1)}, s32[12,2]{0,1:T(2,128)}, u32[]{:S(2)}) copy-start(s32[12,2]{0,1:T(2,128)} %param.12) | copy-start | bytes 292
  48.3 2.7 %copy-start.9 = (bf16[2,8,48,128]{3,2,1,0:T(8,128)(2,1)}, bf16[2,8,48,128]{3,2,1,0:T(8,128)(2,1)S(1)}, u32[]{:S(2)}) copy-start(bf16[2,8,48,128]{3,2,1,0:T(8,128)(2,1)S(1)} %collective-permute-done.6.refs_6_) | copy-start | bytes 589828
  48.3 8.3 %collective-permute-start.13 = (f32[24,128]{1,0:T(8,128)S(1)}, f32[24,128]{1,0:T(8,128)S(1)}, u32[]{:S(2)}, u32[]{:S(2)}) collective-permute-start(f32[24,128]{1,0:T(8,128)S(1)} %add.10), channel_id=1, source_target_pairs={{0,16},{4,20},{8,24},{12,28},{16,0},{20,4},{24,8},{28,12},{1,17},{... | collective-permute-start | bytes 36872 | tf_op jit(solution)/shard_map/ppermute | solution.py:570
  55.1 6.5 %collective-permute-start.9 = (bf16[2,10,48,128]{3,2,1,0:T(8,128)(2,1)S(1)}, bf16[2,10,48,128]{3,2,1,0:T(8,128)(2,1)S(1)}, u32[]{:S(2)}, u32[]{:S(2)}) collective-permute-start(bf16[2,10,48,128]{3,2,1,0:T(8,128)(2,1)S(1)} %get-tuple-element.48.refs_0_), channel_id=1, source_target_pairs={{0,2},{1,3},{2,0},{3,1},{4,6},{5,7},{6,4},{7,5},{8,10},{9,11},{10,... | collective-permute-start | bytes 737288 | tf_op jit(solution)/shard_map/ppermute | solution.py:584
  55.6 3.3 %collective-permute-start.11 = (bf16[4,14,48,128]{3,2,1,0:T(8,128)(2,1)S(1)}, bf16[4,14,48,128]{3,2,1,0:T(8,128)(2,1)S(1)}, u32[]{:S(2)}, u32[]{:S(2)}) collective-permute-start(bf16[4,14,48,128]{3,2,1,0:T(8,128)(2,1)S(1)} %filtered.3.refs_0_), channel_id=1, source_target_pairs={{0,1},{1,0},{2,3},{3,2},{4,5},{5,4},{6,7},{7,6},{8,9},{9,8},{10,11... | collective-permute-start | bytes 2064392 | tf_op jit(solution)/shard_map/ppermute | solution.py:586
  55.6 3.3 %collective-permute-start.12 = (bf16[4,14,48,128]{3,2,1,0:T(8,128)(2,1)}, bf16[4,14,48,128]{3,2,1,0:T(8,128)(2,1)S(1)}, u32[]{:S(2)}, u32[]{:S(2)}) collective-permute-start(bf16[4,14,48,128]{3,2,1,0:T(8,128)(2,1)} %collective-permute-done.10.refs_2_), channel_id=1, source_target_pairs={{0,1},{1,0},{2,3},{3,2},{4,5},{5,4},{6,7},{7,6},{8,9},{9,8},{10,11... | collective-permute-start | bytes 2064392 | tf_op jit(solution)/shard_map/ppermute | solution.py:587
  56.6 7.0 %copy-start.10 = (f32[8]{0:T(128)S(1)}, f32[8]{0:T(128)}, u32[]{:S(2)}) copy-start(f32[8]{0:T(128)} %param.10) | copy-start | bytes 100
  61.1 14.8 %copy-start.5 = (bf16[2,48,24,48]{3,2,1,0:T(8,128)(2,1)S(1)}, bf16[2,48,24,48]{3,2,1,0:T(8,128)(2,1)}, u32[]{:S(2)}) copy-start(bf16[2,48,24,48]{3,2,1,0:T(8,128)(2,1)} %copy-done.4) | copy-start | bytes 663556
  61.1 10.2 %collective-permute-start.16 = (bf16[2,14,48,128]{3,2,1,0:T(8,128)(2,1)S(1)}, bf16[2,14,48,128]{3,2,1,0:T(8,128)(2,1)S(1)}, u32[]{:S(2)}, u32[]{:S(2)}) collective-permute-start(bf16[2,14,48,128]{3,2,1,0:T(8,128)(2,1)S(1)} %get-tuple-element.55), channel_id=1, source_target_pairs={{0,4},{4,0},{8,12},{12,8},{16,20},{20,16},{24,28},{28,24},{1,5},{5... | collective-permute-start | bytes 1032200 | tf_op jit(solution)/shard_map/ppermute | solution.py:592
  61.6 3.6 %collective-permute-start.14 = (bf16[2,10,48,128]{3,2,1,0:T(8,128)(2,1)S(1)}, bf16[2,10,48,128]{3,2,1,0:T(8,128)(2,1)S(1)}, u32[]{:S(2)}, u32[]{:S(2)}) collective-permute-start(bf16[2,10,48,128]{3,2,1,0:T(8,128)(2,1)S(1)} %collective-permute-done.9.refs_2_), channel_id=1, source_target_pairs={{0,1},{1,0},{2,3},{3,2},{4,5},{5,4},{6,7},{7,6},{8,9},{9,8},{10,11... | collective-permute-start | bytes 737288 | tf_op jit(solution)/shard_map/ppermute | solution.py:595
  61.6 9.7 %collective-permute-start.17 = (bf16[2,10,48,128]{3,2,1,0:T(8,128)(2,1)S(1)}, bf16[2,10,48,128]{3,2,1,0:T(8,128)(2,1)S(1)}, u32[]{:S(2)}, u32[]{:S(2)}) collective-permute-start(bf16[2,10,48,128]{3,2,1,0:T(8,128)(2,1)S(1)} %get-tuple-element.48.refs_0_), channel_id=1, source_target_pairs={{0,1},{1,0},{2,3},{3,2},{4,5},{5,4},{6,7},{7,6},{8,9},{9,8},{10,11... | collective-permute-start | bytes 737288 | tf_op jit(solution)/shard_map/ppermute | solution.py:582
  62.1 10.2 %collective-permute-start.21 = (bf16[2,10,48,128]{3,2,1,0:T(8,128)(2,1)S(1)}, bf16[2,10,48,128]{3,2,1,0:T(8,128)(2,1)S(1)}, u32[]{:S(2)}, u32[]{:S(2)}) collective-permute-start(bf16[2,10,48,128]{3,2,1,0:T(8,128)(2,1)S(1)} %get-tuple-element.65.a), channel_id=1, source_target_pairs={{0,2},{1,3},{2,0},{3,1},{4,6},{5,7},{6,4},{7,5},{8,10},{9,11},{10,... | collective-permute-start | bytes 737288 | tf_op jit(solution)/shard_map/ppermute | solution.py:594
  63.8 1.2 %collective-permute-start.15 = (bf16[16,128]{1,0:T(8,128)(2,1)S(1)}, bf16[16,128]{1,0:T(8,128)(2,1)S(1)}, u32[]{:S(2)}, u32[]{:S(2)}) collective-permute-start(bf16[16,128]{1,0:T(8,128)(2,1)S(1)} %coefficients.1), channel_id=1, source_target_pairs={{0,1},{1,0},{2,3},{3,2},{4,5},{5,4},{6,7},{7,6},{8,9},{9,8},{10,11... | collective-permute-start | bytes 12296 | tf_op jit(solution)/shard_map/ppermute | solution.py:597
  65.0 12.8 %collective-permute-start.20 = (bf16[2,10,48,128]{3,2,1,0:T(8,128)(2,1)S(1)}, bf16[2,10,48,128]{3,2,1,0:T(8,128)(2,1)S(1)}, u32[]{:S(2)}, u32[]{:S(2)}) collective-permute-start(bf16[2,10,48,128]{3,2,1,0:T(8,128)(2,1)S(1)} %get-tuple-element.65.a), channel_id=1, source_target_pairs={{0,1},{1,0},{2,3},{3,2},{4,5},{5,4},{6,7},{7,6},{8,9},{9,8},{10,11... | collective-permute-start | bytes 737288 | tf_op jit(solution)/shard_map/ppermute | solution.py:583
  71.9 7.2 %collective-permute-start.19 = (bf16[2,10,48,128]{3,2,1,0:T(8,128)(2,1)S(1)}, bf16[2,10,48,128]{3,2,1,0:T(8,128)(2,1)S(1)}, u32[]{:S(2)}, u32[]{:S(2)}) collective-permute-start(bf16[2,10,48,128]{3,2,1,0:T(8,128)(2,1)S(1)} %rotated.3), channel_id=1, source_target_pairs={{0,4},{4,0},{8,12},{12,8},{16,20},{20,16},{24,28},{28,24},{1,5},{5... | collective-permute-start | bytes 737288 | tf_op jit(solution)/shard_map/ppermute | solution.py:600
  72.3 3.7 %collective-permute-start.18 = (bf16[32,128]{1,0:T(8,128)(2,1)S(1)}, bf16[32,128]{1,0:T(8,128)(2,1)S(1)}, u32[]{:S(2)}, u32[]{:S(2)}) collective-permute-start(bf16[32,128]{1,0:T(8,128)(2,1)S(1)} %pad_maximum_fusion), channel_id=1, source_target_pairs={{0,2},{1,3},{2,0},{3,1},{4,6},{5,7},{6,4},{7,5},{8,10},{9,11},{10,... | collective-permute-start | bytes 24584 | tf_op jit(solution)/shard_map/ppermute | solution.py:602
  73.8 4.0 %collective-permute-start.22 = (bf16[2,10,48,128]{3,2,1,0:T(8,128)(2,1)S(1)}, bf16[2,10,48,128]{3,2,1,0:T(8,128)(2,1)S(1)}, u32[]{:S(2)}, u32[]{:S(2)}) collective-permute-start(bf16[2,10,48,128]{3,2,1,0:T(8,128)(2,1)S(1)} %collective-permute-done.21.c), channel_id=1, source_target_pairs={{0,1},{1,0},{2,3},{3,2},{4,5},{5,4},{6,7},{7,6},{8,9},{9,8},{10,11... | collective-permute-start | bytes 737288 | tf_op jit(solution)/shard_map/ppermute | solution.py:606

commit v15 on v14

--- a/solution.py
+++ b/solution.py
@@ -595,14 +595,14 @@
     ycg = lax.ppermute(yg, "orb", beside)
     coefs = coefficients(sums, strong)
     coefs = jnp.concatenate([coefs, lax.ppermute(coefs, "orb", beside)], axis=0)
-    ycg, coefs, got1 = ordered(ycg, coefs, got1)
+    ycg, coefs = ordered(ycg, coefs)
     (give2,) = rotated((give2, cg, yg, ycg), q, 1)
     got2 = lax.ppermute(give2, "space", swap)
     coefs, _ = ordered(coefs, give2)
     coefs_y = lax.ppermute(coefs, "orb", across)
     coefs = [half_of[k * 2 * count : (k + 1) * 2 * count] for half_of in (coefs, coefs_y) for k in (0, 1)]
     term = nonlocal_term(psi.shape, coefs, q, weights)
-    yk, _ = ordered(yk, give2)
+    yk, _, got1 = ordered(yk, give2, got1)
     yck = lax.ppermute(yk, "orb", beside)
     return assembled(term, keep1, got1, got2, (keep2, ck, yk, yck), q)
 

time: 81.2 us -> 78.6 us (0.968)
  waiting for transfers between devices: 28.8 us -> 26 us
    ppermute x1, waiting for transfers between devices: 6.13 us -> 2.16 us  [shards(): got1 = lax.ppermute(give1, 'space', swap)]
    ppermute x1, waiting for transfers between devices: 2.13 us -> 0.01 us  [shards(): coefs_y = lax.ppermute(coefs, 'orb', across)]
    ppermute x1, waiting for transfers between devices: 0.01 us -> 1.96 us  [shards(): yk = lax.ppermute(keep_y, 'orb', across)]
    ppermute x1, starting transfers between devices: 0.43 us -> 1.72 us  [shards(): got2 = lax.ppermute(give2, 'space', swap)]
    ppermute x1, waiting for transfers between devices: 1.23 us -> 2.52 us  [shards(): got2 = lax.ppermute(give2, 'space', swap)]
    ppermute x1, starting transfers between devices: 1.52 us -> 0.51 us  [shards(): coefs_y = lax.ppermute(coefs, 'orb', across)]
where the time goes in v15:
time: 78.6 us; the launch traced here: 78.3 us
  starting transfers between devices  27.9 us (35%)
  waiting for transfers between devices  26 us (33%)
  Pallas kernels  22.4 us (28%)
  local copies, waits for them, and re-layouts  0.95 us (1%)
    pallas_call x2, Pallas kernels, filtered(): pl.pallas_call(functools.partial(filter_kernel, slabs, start, parts, join...  9.12 us
    ppermute x3, waiting for transfers between devices, added(): return values + lax.ppermute(values, 'space', pairs)  5.81 us
    ppermute x1, waiting for transfers between devices, shards(): xr1 = lax.ppermute(to_x, 'space', swap)  5.25 us
    ppermute x1, starting transfers between devices, shards(): zf2 = lax.ppermute(xr2, 'space', other_way)  4.28 us
    ppermute x3, starting transfers between devices, added(): return values + lax.ppermute(values, 'space', pairs)  4.27 us
    ppermute x1, starting transfers between devices, shards(): zf1 = lax.ppermute(xr1, 'space', other_way)  3.97 us
    pallas_call x1, Pallas kernels, partials(): pl.pallas_call(functools.partial(partial_kernel, count), out_shape=(jax.S...  3.04 us
    ppermute x1, starting transfers between devices, shards(): xr1 = lax.ppermute(to_x, 'space', swap)  3.01 us
  transfers between devices with their start and end apart: 23, of which 10 were waited for; matrix products, arithmetic and copies ran while one was open for 1% of the time, Pallas kernels for 17%

profile of v15, /device:TPU:0, one launch (start us, length us, event | category | flops | bytes accessed | tf_op | source)
XLA Modules:
  0.0 78.3 jit_solution(4715927803552464546)
XLA Ops:
  0.0 2.2 %prepared.1 = (bf16[2,19,48,128]{3,2,1,0:T(8,128)(2,1)S(1)}, bf16[2,27,48,128]{3,2,1,0:T(8,128)(2,1)}) custom-call(bf16[2,48,48,128]{3,2,1,0:T(8,128)(2,1)} %refs_0_.3, f32[2,48,48]{2,1,0:T(8,128)} %refs_1_.3), custom_call_target="tpu_custom_call" | custom-call | flops 256 | bytes 256 | tf_op jit(solution)/shard_map/prepared/pallas_call | solution.py:81
  2.2 0.0 copy-start.1
  2.2 0.0 copy-start.3
  2.2 3.0 %collective-permute-start.1 = (bf16[2,19,48,128]{3,2,1,0:T(8,128)(2,1)S(1)}, bf16[2,19,48,128]{3,2,1,0:T(8,128)(2,1)}, u32[]{:S(2)}, u32[]{:S(2)}) collective-permute-start(bf16[2,19,48,128]{3,2,1,0:T(8,128)(2,1)S(1)} %get-tuple-element.37), channel_id=1, source_target_pairs={{0,4},{4,0},{8,12},{12,8},{16,20},{20,16},{24,28},{28,24},{1,5},{5... | collective-permute-start | bytes 1400840 | tf_op jit(solution)/shard_map/ppermute | solution.py:550
  5.2 1.3 %collective-permute-start = (bf16[2,27,48,128]{3,2,1,0:T(8,128)(2,1)}, bf16[2,27,48,128]{3,2,1,0:T(8,128)(2,1)S(1)}, u32[]{:S(2)}, u32[]{:S(2)}) collective-permute-start(bf16[2,27,48,128]{3,2,1,0:T(8,128)(2,1)} %get-tuple-element.36), channel_id=1, source_target_pairs={{4,12},{8,0},{12,20},{16,8},{20,28},{24,16},{5,13},{9,1},{13,21},{... | collective-permute-start | bytes 1990664 | tf_op jit(solution)/shard_map/ppermute | solution.py:551
  6.5 1.6 %packed.1 = (bf16[2,8,48,128]{3,2,1,0:T(8,128)(2,1)S(1)}, bf16[8,48,48]{2,1,0:T(8,128)(2,1)S(1)}, bf16[8,48,48]{2,1,0:T(8,128)(2,1)}) custom-call(bf16[2,48,48,128]{3,2,1,0:T(8,128)(2,1)} %refs_0_.3, bf16[8,2,48,48]{3,2,1,0:T(8,128)(2,1)S(1)} %copy-done.2), custom_call_target="tpu_custom_call" | custom-call | flops 256 | bytes 256 | tf_op jit(solution)/shard_map/packed/pallas_call | solution.py:110
  8.1 2.8 %collective-permute-start.4 = (bf16[8,48,48]{2,1,0:T(8,128)(2,1)}, bf16[8,48,48]{2,1,0:T(8,128)(2,1)S(1)}, u32[]{:S(2)}, u32[]{:S(2)}) collective-permute-start(bf16[8,48,48]{2,1,0:T(8,128)(2,1)} %get-tuple-element.41), channel_id=1, source_target_pairs={{0,4},{4,0},{8,12},{12,8},{16,20},{20,16},{24,28},{28,24},{1,5},{5... | collective-permute-start | bytes 110600 | tf_op jit(solution)/shard_map/ppermute | solution.py:547
  10.9 0.7 collective-permute-start.5
  11.6 5.2 %collective-permute-done.1.refs_3_ = bf16[2,19,48,128]{3,2,1,0:T(8,128)(2,1)} collective-permute-done((bf16[2,19,48,128]{3,2,1,0:T(8,128)(2,1)S(1)}, bf16[2,19,48,128]{3,2,1,0:T(8,128)(2,1)}, u32[]{:S(2)}, u32[]{:S(2)}) %collective-permute-start.1) | collective-permute-done | bytes 466976 | tf_op jit(solution)/shard_map/ppermute | solution.py:550
  16.8 4.0 %collective-permute-start.3 = (bf16[2,19,48,128]{3,2,1,0:T(8,128)(2,1)}, bf16[2,19,48,128]{3,2,1,0:T(8,128)(2,1)S(1)}, u32[]{:S(2)}, u32[]{:S(2)}) collective-permute-start(bf16[2,19,48,128]{3,2,1,0:T(8,128)(2,1)} %collective-permute-done.1.refs_3_), channel_id=1, source_target_pairs={{0,8},{8,16},{12,4},{16,24},{20,12},{28,20},{1,9},{9,17},{13,5},{1... | collective-permute-start | bytes 1400840 | tf_op jit(solution)/shard_map/ppermute | solution.py:556
  20.8 0.1 collective-permute-start.2
  20.9 0.1 broadcast_select_fusion
  21.0 0.3 convolution_bitcast_fusion.gram
  21.3 0.0 collective-permute-done.4.b_x
  21.3 0.0 collective-permute-done.5.b_d
  21.3 0.0 copy-done.1
  21.3 3.0 %partials.1 = (f32[24,128]{1,0:T(8,128)S(1)}, bf16[2,48,24,48]{3,2,1,0:T(8,128)(2,1)S(1)}) custom-call(s32[8]{0:T(128)S(1)} %copy-done.6, bf16[2,48,48,128]{3,2,1,0:T(8,128)(2,1)S(1)} %copy-done.1, bf16[8,2,48,48]{3,2,1,0:T(8,128)(2,1)S(1)} %copy-done.2, bf16[8,48,48]{2,1,0:T(8,128)(2,1)S(1)} %collective-permute-done.4.b_x, ...), custom_call_target="tpu_custom_call" | custom-call | flops 256 | bytes 256 | tf_op jit(solution)/shard_map/partials/pallas_call | solution.py:177
  24.4 2.2 %collective-permute-done.2.refs_4_ = bf16[2,8,48,128]{3,2,1,0:T(8,128)(2,1)S(1)} collective-permute-done((bf16[2,8,48,128]{3,2,1,0:T(8,128)(2,1)S(1)}, bf16[2,8,48,128]{3,2,1,0:T(8,128)(2,1)S(1)}, u32[]{:S(2)}, u32[]{:S(2)}) %collective-permute-start.2) | collective-permute-done | bytes 196640 | tf_op jit(solution)/shard_map/ppermute | solution.py:557
  26.6 2.5 %collective-permute-done.3.refs_5_.refs_4_ = bf16[2,19,48,128]{3,2,1,0:T(8,128)(2,1)S(1)} collective-permute-done((bf16[2,19,48,128]{3,2,1,0:T(8,128)(2,1)}, bf16[2,19,48,128]{3,2,1,0:T(8,128)(2,1)S(1)}, u32[]{:S(2)}, u32[]{:S(2)}) %collective-permute-start.3) | collective-permute-done | bytes 466976 | tf_op jit(solution)/shard_map/ppermute | solution.py:556
  29.1 0.0 collective-permute-done.refs_2_
  29.1 0.8 %copy-done.7 = bf16[2,19,48,128]{3,2,1,0:T(8,128)(2,1)} copy-done((bf16[2,19,48,128]{3,2,1,0:T(8,128)(2,1)}, bf16[2,19,48,128]{3,2,1,0:T(8,128)(2,1)S(1)}, u32[]{:S(2)}) %copy-start.7) | copy-done | bytes 466968
  29.9 5.0 %filtered.3.refs_0_ = bf16[4,14,48,128]{3,2,1,0:T(8,128)(2,1)S(1)} custom-call(bf16[2,48,48,128]{3,2,1,0:T(8,128)(2,1)S(1)} %copy-done.1, f32[2,48,48]{2,1,0:T(8,128)S(1)} %copy-done.3, bf16[2,27,48,128]{3,2,1,0:T(8,128)(2,1)S(1)} %collective-permute-done.refs_2_, bf16[2,19,48,128]{3,2,1,0:T(8,128)(2,1)} %collective-permute-done.1.refs_3_, ...), custom_call_target="tpu_custom_call" | custom-call | flops 3440640 | bytes 21504000 | tf_op jit(solution)/shard_map/filtered/pallas_call | solution.py:415
  34.9 1.6 %collective-permute-start.10 = (bf16[4,14,48,128]{3,2,1,0:T(8,128)(2,1)S(1)}, bf16[4,14,48,128]{3,2,1,0:T(8,128)(2,1)}, u32[]{:S(2)}, u32[]{:S(2)}) collective-permute-start(bf16[4,14,48,128]{3,2,1,0:T(8,128)(2,1)S(1)} %filtered.3.refs_0_), channel_id=1, source_target_pairs={{0,2},{1,3},{2,0},{3,1},{4,6},{5,7},{6,4},{7,5},{8,10},{9,11},{10,... | collective-permute-start | bytes 2064392 | tf_op jit(solution)/shard_map/ppermute | solution.py:565
  36.5 4.3 %collective-permute-start.6 = (bf16[2,8,48,128]{3,2,1,0:T(8,128)(2,1)S(1)}, bf16[2,8,48,128]{3,2,1,0:T(8,128)(2,1)S(1)}, u32[]{:S(2)}, u32[]{:S(2)}) collective-permute-start(bf16[2,8,48,128]{3,2,1,0:T(8,128)(2,1)S(1)} %collective-permute-done.2.refs_4_), channel_id=1, source_target_pairs={{0,8},{8,16},{12,4},{16,24},{20,12},{28,20},{1,9},{9,17},{13,5},{1... | collective-permute-start | bytes 589832 | tf_op jit(solution)/shard_map/ppermute | solution.py:558
  40.8 0.1 collective-permute-start.7
  40.9 3.7 %collective-permute-done.7 = f32[24,128]{1,0:T(8,128)S(1)} collective-permute-done((f32[24,128]{1,0:T(8,128)S(1)}, f32[24,128]{1,0:T(8,128)S(1)}, u32[]{:S(2)}, u32[]{:S(2)}) %collective-permute-start.7) | collective-permute-done | bytes 12320 | tf_op jit(solution)/shard_map/ppermute | solution.py:570
  44.5 1.6 %collective-permute-start.8 = (f32[24,128]{1,0:T(8,128)S(1)}, f32[24,128]{1,0:T(8,128)S(1)}, u32[]{:S(2)}, u32[]{:S(2)}) collective-permute-start(f32[24,128]{1,0:T(8,128)S(1)} %add.9), channel_id=1, source_target_pairs={{0,8},{4,12},{8,0},{12,4},{16,24},{20,28},{24,16},{28,20},{1,9},{5... | collective-permute-start | bytes 36872 | tf_op jit(solution)/shard_map/ppermute | solution.py:570
  46.1 2.1 %collective-permute-done.8 = f32[24,128]{1,0:T(8,128)S(1)} collective-permute-done((f32[24,128]{1,0:T(8,128)S(1)}, f32[24,128]{1,0:T(8,128)S(1)}, u32[]{:S(2)}, u32[]{:S(2)}) %collective-permute-start.8) | collective-permute-done | bytes 12320 | tf_op jit(solution)/shard_map/ppermute | solution.py:570
  48.2 0.0 collective-permute-done.6.refs_6_
  48.3 0.0 copy-start.9
  48.3 2.6 %collective-permute-start.13 = (f32[24,128]{1,0:T(8,128)S(1)}, f32[24,128]{1,0:T(8,128)S(1)}, u32[]{:S(2)}, u32[]{:S(2)}) collective-permute-start(f32[24,128]{1,0:T(8,128)S(1)} %add.10), channel_id=1, source_target_pairs={{0,16},{4,20},{8,24},{12,28},{16,0},{20,4},{24,8},{28,12},{1,17},{... | collective-permute-start | bytes 36872 | tf_op jit(solution)/shard_map/ppermute | solution.py:570
  50.9 4.1 %filtered.2 = (bf16[2,10,48,128]{3,2,1,0:T(8,128)(2,1)S(1)}, bf16[2,10,48,128]{3,2,1,0:T(8,128)(2,1)S(1)}) custom-call(bf16[2,48,48,128]{3,2,1,0:T(8,128)(2,1)S(1)} %copy-done.1, f32[2,48,48]{2,1,0:T(8,128)S(1)} %copy-done.3, bf16[2,27,48,128]{3,2,1,0:T(8,128)(2,1)S(1)} %collective-permute-done.refs_2_, ...), custom_call_target="tpu_custom_call" | custom-call | flops 2457600 | bytes 15360000 | tf_op jit(solution)/shard_map/filtered/pallas_call | solution.py:415
  55.1 0.6 collective-permute-start.9
  55.6 0.0 collective-permute-done.10.refs_2_
  55.6 0.0 collective-permute-start.11
  55.6 0.5 collective-permute-start.12
  56.2 0.3 fusion
  56.6 0.0 collective-permute-done.13
  56.6 0.0 copy-start.10
  56.6 2.4 %collective-permute-done.12.refs_3_ = bf16[4,14,48,128]{3,2,1,0:T(8,128)(2,1)S(1)} collective-permute-done((bf16[4,14,48,128]{3,2,1,0:T(8,128)(2,1)}, bf16[4,14,48,128]{3,2,1,0:T(8,128)(2,1)S(1)}, u32[]{:S(2)}, u32[]{:S(2)}) %collective-permute-start.12) | collective-permute-done | bytes 688160 | tf_op jit(solution)/shard_map/ppermute | solution.py:587
  59.0 0.0 collective-permute-done.11.refs_1_
  59.0 2.1 %rotated.2 = (bf16[2,14,48,128]{3,2,1,0:T(8,128)(2,1)S(1)}, bf16[2,14,48,128]{3,2,1,0:T(8,128)(2,1)S(1)}) custom-call(bf16[4,14,48,128]{3,2,1,0:T(8,128)(2,1)S(1)} %filtered.3.refs_0_, bf16[4,14,48,128]{3,2,1,0:T(8,128)(2,1)S(1)} %collective-permute-done.11.refs_1_, bf16[4,14,48,128]{3,2,1,0:T(8,128)(2,1)} %collective-permute-done.10.refs_2_, ...), custom_call_target="tpu_custom_call" | custom-call | flops 22020096 | bytes 215040 | tf_op jit(solution)/shard_map/rotated/pallas_call | solution.py:459
  61.1 0.4 collective-permute-start.19
  61.6 0.0 collective-permute-done.9.refs_2_
  61.6 0.5 collective-permute-start.16
  62.1 1.5 %collective-permute-start.18 = (bf16[2,10,48,128]{3,2,1,0:T(8,128)(2,1)S(1)}, bf16[2,10,48,128]{3,2,1,0:T(8,128)(2,1)S(1)}, u32[]{:S(2)}, u32[]{:S(2)}) collective-permute-start(bf16[2,10,48,128]{3,2,1,0:T(8,128)(2,1)S(1)} %get-tuple-element.64.a), channel_id=1, source_target_pairs={{0,2},{1,3},{2,0},{3,1},{4,6},{5,7},{6,4},{7,5},{8,10},{9,11},{10,... | collective-permute-start | bytes 737288 | tf_op jit(solution)/shard_map/ppermute | solution.py:594
  63.6 0.1 broadcast_in_dim.22.strength
  63.7 0.1 coefficients.1
  63.8 0.0 collective-permute-start.15
  63.9 1.2 %collective-permute-done.15 = bf16[16,128]{1,0:T(8,128)(2,1)S(1)} collective-permute-done((bf16[16,128]{1,0:T(8,128)(2,1)S(1)}, bf16[16,128]{1,0:T(8,128)(2,1)S(1)}, u32[]{:S(2)}, u32[]{:S(2)}) %collective-permute-start.15) | collective-permute-done | bytes 4128 | tf_op jit(solution)/shard_map/ppermute | solution.py:597
  65.0 0.2 collective-permute-start.21
  65.2 0.0 collective-permute-done.14.refs_3_
  65.2 0.0 collective-permute-done.16.refs_1_
  65.2 0.6 rotated.3
  65.8 1.7 %collective-permute-start.20 = (bf16[2,10,48,128]{3,2,1,0:T(8,128)(2,1)S(1)}, bf16[2,10,48,128]{3,2,1,0:T(8,128)(2,1)S(1)}, u32[]{:S(2)}, u32[]{:S(2)}) collective-permute-start(bf16[2,10,48,128]{3,2,1,0:T(8,128)(2,1)S(1)} %rotated.3), channel_id=1, source_target_pairs={{0,4},{4,0},{8,12},{12,8},{16,20},{20,16},{24,28},{28,24},{1,5},{5... | collective-permute-start | bytes 737288 | tf_op jit(solution)/shard_map/ppermute | solution.py:600
  67.5 0.5 collective-permute-start.17
  68.0 2.0 %collective-permute-done.18.c = bf16[2,10,48,128]{3,2,1,0:T(8,128)(2,1)S(1)} collective-permute-done((bf16[2,10,48,128]{3,2,1,0:T(8,128)(2,1)S(1)}, bf16[2,10,48,128]{3,2,1,0:T(8,128)(2,1)S(1)}, u32[]{:S(2)}, u32[]{:S(2)}) %collective-permute-start.18) | collective-permute-done | bytes 245792 | tf_op jit(solution)/shard_map/ppermute | solution.py:594
  70.0 2.2 %collective-permute-done.19.got1 = bf16[2,14,48,128]{3,2,1,0:T(8,128)(2,1)S(1)} collective-permute-done((bf16[2,14,48,128]{3,2,1,0:T(8,128)(2,1)S(1)}, bf16[2,14,48,128]{3,2,1,0:T(8,128)(2,1)S(1)}, u32[]{:S(2)}, u32[]{:S(2)}) %collective-permute-start.19) | collective-permute-done | bytes 344096 | tf_op jit(solution)/shard_map/ppermute | solution.py:592
  72.1 0.0 collective-permute-start.22
  72.1 0.0 collective-permute-done.17
  72.2 1.9 %nonlocal.1.term = f32[2,48,48,128]{3,2,1,0:T(8,128)S(1)} custom-call(bf16[16,128]{1,0:T(8,128)(2,1)S(1)} %get-tuple-element.70.a, bf16[16,128]{1,0:T(8,128)(2,1)S(1)} %get-tuple-element.69.b, bf16[16,128]{1,0:T(8,128)(2,1)S(1)} %get-tuple-element.68.c, bf16[16,128]{1,0:T(8,128)(2,1)S(1)} %get-tuple-element.67.d, bf16[4,128,128]{2,1,0:T(8,128)(2,1)S(1)} %copy.18.refs_4_.q, ...), custom_call_target="tpu_custom_call" | custom-call | flops 256 | bytes 256 | tf_op jit(solution)/shard_map/nonlocal/pallas_call | solution.py:252
  74.1 0.0 collective-permute-done.21.b
  74.1 2.5 %collective-permute-done.20.got2 = bf16[2,10,48,128]{3,2,1,0:T(8,128)(2,1)S(1)} collective-permute-done((bf16[2,10,48,128]{3,2,1,0:T(8,128)(2,1)S(1)}, bf16[2,10,48,128]{3,2,1,0:T(8,128)(2,1)S(1)}, u32[]{:S(2)}, u32[]{:S(2)}) %collective-permute-start.20) | collective-permute-done | bytes 245792 | tf_op jit(solution)/shard_map/ppermute | solution.py:600
  76.6 1.7 %assembled.1 = bf16[2,48,48,128]{3,2,1,0:T(8,128)(2,1)} custom-call(f32[2,48,48,128]{3,2,1,0:T(8,128)S(1)} %nonlocal.1.term, bf16[2,14,48,128]{3,2,1,0:T(8,128)(2,1)S(1)} %get-tuple-element.63.keep1, bf16[2,14,48,128]{3,2,1,0:T(8,128)(2,1)S(1)} %collective-permute-done.19.got1, bf16[2,10,48,128]{3,2,1,0:T(8,128)(2,1)S(1)} %collective-permute-done.20.got2, ...), custom_call_target="tpu_custom_call" | custom-call | flops 256 | bytes 256 | tf_op jit(solution)/shard_map/assembled/pallas_call | solution.py:506
  (31 shorter events, 0.1 us)
Async XLA Ops:
  0.0 56.2 %copy-start = (bf16[12,128,128]{2,1,0:T(8,128)(2,1)S(1)}, bf16[12,128,128]{2,1,0:T(8,128)(2,1)}, u32[]{:S(2)}) copy-start(bf16[12,128,128]{2,1,0:T(8,128)(2,1)} %param.13) | copy-start | bytes 1179652
  0.0 6.5 %copy-start.2 = (bf16[8,2,48,48]{3,2,1,0:T(8,128)(2,1)S(1)}, bf16[8,2,48,48]{3,2,1,0:T(8,128)(2,1)}, u32[]{:S(2)}) copy-start(bf16[8,2,48,48]{3,2,1,0:T(8,128)(2,1)} %beta.3) | copy-start | bytes 221188
  0.0 20.8 %copy-start.6 = (s32[8]{0:T(128)S(1)}, s32[8]{0:T(128)}, u32[]{:S(2)}) copy-start(s32[8]{0:T(128)} %atoms.1) | copy-start | bytes 100
  2.2 19.1 %copy-start.1 = (bf16[2,48,48,128]{3,2,1,0:T(8,128)(2,1)S(1)}, bf16[2,48,48,128]{3,2,1,0:T(8,128)(2,1)}, u32[]{:S(2)}) copy-start(bf16[2,48,48,128]{3,2,1,0:T(8,128)(2,1)} %refs_0_.3) | copy-start | bytes 3538948
  2.2 19.1 %copy-start.3 = (f32[2,48,48]{2,1,0:T(8,128)S(1)}, f32[2,48,48]{2,1,0:T(8,128)}, u32[]{:S(2)}) copy-start(f32[2,48,48]{2,1,0:T(8,128)} %refs_1_.3) | copy-start | bytes 55300
  2.2 14.6 %collective-permute-start.1 = (bf16[2,19,48,128]{3,2,1,0:T(8,128)(2,1)S(1)}, bf16[2,19,48,128]{3,2,1,0:T(8,128)(2,1)}, u32[]{:S(2)}, u32[]{:S(2)}) collective-permute-start(bf16[2,19,48,128]{3,2,1,0:T(8,128)(2,1)S(1)} %get-tuple-element.37), channel_id=1, source_target_pairs={{0,4},{4,0},{8,12},{12,8},{16,20},{20,16},{24,28},{28,24},{1,5},{5... | collective-permute-start | bytes 1400840 | tf_op jit(solution)/shard_map/ppermute | solution.py:550
  5.2 23.9 %collective-permute-start = (bf16[2,27,48,128]{3,2,1,0:T(8,128)(2,1)}, bf16[2,27,48,128]{3,2,1,0:T(8,128)(2,1)S(1)}, u32[]{:S(2)}, u32[]{:S(2)}) collective-permute-start(bf16[2,27,48,128]{3,2,1,0:T(8,128)(2,1)} %get-tuple-element.36), channel_id=1, source_target_pairs={{4,12},{8,0},{12,20},{16,8},{20,28},{24,16},{5,13},{9,1},{13,21},{... | collective-permute-start | bytes 1990664 | tf_op jit(solution)/shard_map/ppermute | solution.py:551
  8.1 13.2 %collective-permute-start.4 = (bf16[8,48,48]{2,1,0:T(8,128)(2,1)}, bf16[8,48,48]{2,1,0:T(8,128)(2,1)S(1)}, u32[]{:S(2)}, u32[]{:S(2)}) collective-permute-start(bf16[8,48,48]{2,1,0:T(8,128)(2,1)} %get-tuple-element.41), channel_id=1, source_target_pairs={{0,4},{4,0},{8,12},{12,8},{16,20},{20,16},{24,28},{28,24},{1,5},{5... | collective-permute-start | bytes 110600 | tf_op jit(solution)/shard_map/ppermute | solution.py:547
  10.9 10.4 %collective-permute-start.5 = (bf16[8,48,48]{2,1,0:T(8,128)(2,1)S(1)}, bf16[8,48,48]{2,1,0:T(8,128)(2,1)S(1)}, u32[]{:S(2)}, u32[]{:S(2)}) collective-permute-start(bf16[8,48,48]{2,1,0:T(8,128)(2,1)S(1)} %get-tuple-element.42), channel_id=1, source_target_pairs={{4,8},{8,4},{12,16},{16,12},{20,24},{24,20},{5,9},{9,5},{13,17},{1... | collective-permute-start | bytes 110600 | tf_op jit(solution)/shard_map/ppermute | solution.py:549
  16.8 12.3 %collective-permute-start.3 = (bf16[2,19,48,128]{3,2,1,0:T(8,128)(2,1)}, bf16[2,19,48,128]{3,2,1,0:T(8,128)(2,1)S(1)}, u32[]{:S(2)}, u32[]{:S(2)}) collective-permute-start(bf16[2,19,48,128]{3,2,1,0:T(8,128)(2,1)} %collective-permute-done.1.refs_3_), channel_id=1, source_target_pairs={{0,8},{8,16},{12,4},{16,24},{20,12},{28,20},{1,9},{9,17},{13,5},{1... | collective-permute-start | bytes 1400840 | tf_op jit(solution)/shard_map/ppermute | solution.py:556
  20.8 5.7 %collective-permute-start.2 = (bf16[2,8,48,128]{3,2,1,0:T(8,128)(2,1)S(1)}, bf16[2,8,48,128]{3,2,1,0:T(8,128)(2,1)S(1)}, u32[]{:S(2)}, u32[]{:S(2)}) collective-permute-start(bf16[2,8,48,128]{3,2,1,0:T(8,128)(2,1)S(1)} %get-tuple-element.40), channel_id=1, source_target_pairs={{0,4},{4,0},{8,12},{12,8},{16,20},{20,16},{24,28},{28,24},{1,5},{5... | collective-permute-start | bytes 589832 | tf_op jit(solution)/shard_map/ppermute | solution.py:557
  24.4 10.5 %copy-start.4 = (bf16[2,48,24,48]{3,2,1,0:T(8,128)(2,1)}, bf16[2,48,24,48]{3,2,1,0:T(8,128)(2,1)S(1)}, u32[]{:S(2)}) copy-start(bf16[2,48,24,48]{3,2,1,0:T(8,128)(2,1)S(1)} %get-tuple-element.62.weights) | copy-start | bytes 663556
  26.6 24.3 %copy-start.8 = (bf16[2,8,48,128]{3,2,1,0:T(8,128)(2,1)}, bf16[2,8,48,128]{3,2,1,0:T(8,128)(2,1)S(1)}, u32[]{:S(2)}) copy-start(bf16[2,8,48,128]{3,2,1,0:T(8,128)(2,1)S(1)} %collective-permute-done.2.refs_4_) | copy-start | bytes 589828
  29.1 0.8 %copy-start.7 = (bf16[2,19,48,128]{3,2,1,0:T(8,128)(2,1)}, bf16[2,19,48,128]{3,2,1,0:T(8,128)(2,1)S(1)}, u32[]{:S(2)}) copy-start(bf16[2,19,48,128]{3,2,1,0:T(8,128)(2,1)S(1)} %collective-permute-done.3.refs_5_.refs_4_) | copy-start | bytes 1400836
  34.9 20.7 %collective-permute-start.10 = (bf16[4,14,48,128]{3,2,1,0:T(8,128)(2,1)S(1)}, bf16[4,14,48,128]{3,2,1,0:T(8,128)(2,1)}, u32[]{:S(2)}, u32[]{:S(2)}) collective-permute-start(bf16[4,14,48,128]{3,2,1,0:T(8,128)(2,1)S(1)} %filtered.3.refs_0_), channel_id=1, source_target_pairs={{0,2},{1,3},{2,0},{3,1},{4,6},{5,7},{6,4},{7,5},{8,10},{9,11},{10,... | collective-permute-start | bytes 2064392 | tf_op jit(solution)/shard_map/ppermute | solution.py:565
  36.5 11.8 %collective-permute-start.6 = (bf16[2,8,48,128]{3,2,1,0:T(8,128)(2,1)S(1)}, bf16[2,8,48,128]{3,2,1,0:T(8,128)(2,1)S(1)}, u32[]{:S(2)}, u32[]{:S(2)}) collective-permute-start(bf16[2,8,48,128]{3,2,1,0:T(8,128)(2,1)S(1)} %collective-permute-done.2.refs_4_), channel_id=1, source_target_pairs={{0,8},{8,16},{12,4},{16,24},{20,12},{28,20},{1,9},{9,17},{13,5},{1... | collective-permute-start | bytes 589832 | tf_op jit(solution)/shard_map/ppermute | solution.py:558
  40.8 3.8 %collective-permute-start.7 = (f32[24,128]{1,0:T(8,128)S(1)}, f32[24,128]{1,0:T(8,128)S(1)}, u32[]{:S(2)}, u32[]{:S(2)}) collective-permute-start(f32[24,128]{1,0:T(8,128)S(1)} %get-tuple-element.45), channel_id=1, source_target_pairs={{0,4},{4,0},{8,12},{12,8},{16,20},{20,16},{24,28},{28,24},{1,5},{5... | collective-permute-start | bytes 36872 | tf_op jit(solution)/shard_map/ppermute | solution.py:570
  44.5 3.7 %collective-permute-start.8 = (f32[24,128]{1,0:T(8,128)S(1)}, f32[24,128]{1,0:T(8,128)S(1)}, u32[]{:S(2)}, u32[]{:S(2)}) collective-permute-start(f32[24,128]{1,0:T(8,128)S(1)} %add.9), channel_id=1, source_target_pairs={{0,8},{4,12},{8,0},{12,4},{16,24},{20,28},{24,16},{28,20},{1,9},{5... | collective-permute-start | bytes 36872 | tf_op jit(solution)/shard_map/ppermute | solution.py:570
  48.2 7.9 %copy-start.11 = (s32[12,2]{0,1:T(2,128)S(1)}, s32[12,2]{0,1:T(2,128)}, u32[]{:S(2)}) copy-start(s32[12,2]{0,1:T(2,128)} %param.12) | copy-start | bytes 292
  48.3 2.7 %copy-start.9 = (bf16[2,8,48,128]{3,2,1,0:T(8,128)(2,1)}, bf16[2,8,48,128]{3,2,1,0:T(8,128)(2,1)S(1)}, u32[]{:S(2)}) copy-start(bf16[2,8,48,128]{3,2,1,0:T(8,128)(2,1)S(1)} %collective-permute-done.6.refs_6_) | copy-start | bytes 589828
  48.3 8.3 %collective-permute-start.13 = (f32[24,128]{1,0:T(8,128)S(1)}, f32[24,128]{1,0:T(8,128)S(1)}, u32[]{:S(2)}, u32[]{:S(2)}) collective-permute-start(f32[24,128]{1,0:T(8,128)S(1)} %add.10), channel_id=1, source_target_pairs={{0,16},{4,20},{8,24},{12,28},{16,0},{20,4},{24,8},{28,12},{1,17},{... | collective-permute-start | bytes 36872 | tf_op jit(solution)/shard_map/ppermute | solution.py:570
  55.1 6.5 %collective-permute-start.9 = (bf16[2,10,48,128]{3,2,1,0:T(8,128)(2,1)S(1)}, bf16[2,10,48,128]{3,2,1,0:T(8,128)(2,1)S(1)}, u32[]{:S(2)}, u32[]{:S(2)}) collective-permute-start(bf16[2,10,48,128]{3,2,1,0:T(8,128)(2,1)S(1)} %get-tuple-element.48.refs_0_), channel_id=1, source_target_pairs={{0,2},{1,3},{2,0},{3,1},{4,6},{5,7},{6,4},{7,5},{8,10},{9,11},{10,... | collective-permute-start | bytes 737288 | tf_op jit(solution)/shard_map/ppermute | solution.py:584
  55.6 3.3 %collective-permute-start.11 = (bf16[4,14,48,128]{3,2,1,0:T(8,128)(2,1)S(1)}, bf16[4,14,48,128]{3,2,1,0:T(8,128)(2,1)S(1)}, u32[]{:S(2)}, u32[]{:S(2)}) collective-permute-start(bf16[4,14,48,128]{3,2,1,0:T(8,128)(2,1)S(1)} %filtered.3.refs_0_), channel_id=1, source_target_pairs={{0,1},{1,0},{2,3},{3,2},{4,5},{5,4},{6,7},{7,6},{8,9},{9,8},{10,11... | collective-permute-start | bytes 2064392 | tf_op jit(solution)/shard_map/ppermute | solution.py:586
  55.6 3.3 %collective-permute-start.12 = (bf16[4,14,48,128]{3,2,1,0:T(8,128)(2,1)}, bf16[4,14,48,128]{3,2,1,0:T(8,128)(2,1)S(1)}, u32[]{:S(2)}, u32[]{:S(2)}) collective-permute-start(bf16[4,14,48,128]{3,2,1,0:T(8,128)(2,1)} %collective-permute-done.10.refs_2_), channel_id=1, source_target_pairs={{0,1},{1,0},{2,3},{3,2},{4,5},{5,4},{6,7},{7,6},{8,9},{9,8},{10,11... | collective-permute-start | bytes 2064392 | tf_op jit(solution)/shard_map/ppermute | solution.py:587
  56.6 7.0 %copy-start.10 = (f32[8]{0:T(128)S(1)}, f32[8]{0:T(128)}, u32[]{:S(2)}) copy-start(f32[8]{0:T(128)} %param.10) | copy-start | bytes 100
  61.1 11.0 %copy-start.5 = (bf16[2,48,24,48]{3,2,1,0:T(8,128)(2,1)S(1)}, bf16[2,48,24,48]{3,2,1,0:T(8,128)(2,1)}, u32[]{:S(2)}) copy-start(bf16[2,48,24,48]{3,2,1,0:T(8,128)(2,1)} %copy-done.4) | copy-start | bytes 663556
  61.1 11.0 %collective-permute-start.19 = (bf16[2,14,48,128]{3,2,1,0:T(8,128)(2,1)S(1)}, bf16[2,14,48,128]{3,2,1,0:T(8,128)(2,1)S(1)}, u32[]{:S(2)}, u32[]{:S(2)}) collective-permute-start(bf16[2,14,48,128]{3,2,1,0:T(8,128)(2,1)S(1)} %get-tuple-element.55), channel_id=1, source_target_pairs={{0,4},{4,0},{8,12},{12,8},{16,20},{20,16},{24,28},{28,24},{1,5},{5... | collective-permute-start | bytes 1032200 | tf_op jit(solution)/shard_map/ppermute | solution.py:592
  61.6 3.6 %collective-permute-start.14 = (bf16[2,10,48,128]{3,2,1,0:T(8,128)(2,1)S(1)}, bf16[2,10,48,128]{3,2,1,0:T(8,128)(2,1)S(1)}, u32[]{:S(2)}, u32[]{:S(2)}) collective-permute-start(bf16[2,10,48,128]{3,2,1,0:T(8,128)(2,1)S(1)} %collective-permute-done.9.refs_2_), channel_id=1, source_target_pairs={{0,1},{1,0},{2,3},{3,2},{4,5},{5,4},{6,7},{7,6},{8,9},{9,8},{10,11... | collective-permute-start | bytes 737288 | tf_op jit(solution)/shard_map/ppermute | solution.py:595
  61.6 3.6 %collective-permute-start.16 = (bf16[2,10,48,128]{3,2,1,0:T(8,128)(2,1)S(1)}, bf16[2,10,48,128]{3,2,1,0:T(8,128)(2,1)S(1)}, u32[]{:S(2)}, u32[]{:S(2)}) collective-permute-start(bf16[2,10,48,128]{3,2,1,0:T(8,128)(2,1)S(1)} %get-tuple-element.48.refs_0_), channel_id=1, source_target_pairs={{0,1},{1,0},{2,3},{3,2},{4,5},{5,4},{6,7},{7,6},{8,9},{9,8},{10,11... | collective-permute-start | bytes 737288 | tf_op jit(solution)/shard_map/ppermute | solution.py:582
  62.1 7.9 %collective-permute-start.18 = (bf16[2,10,48,128]{3,2,1,0:T(8,128)(2,1)S(1)}, bf16[2,10,48,128]{3,2,1,0:T(8,128)(2,1)S(1)}, u32[]{:S(2)}, u32[]{:S(2)}) collective-permute-start(bf16[2,10,48,128]{3,2,1,0:T(8,128)(2,1)S(1)} %get-tuple-element.64.a), channel_id=1, source_target_pairs={{0,2},{1,3},{2,0},{3,1},{4,6},{5,7},{6,4},{7,5},{8,10},{9,11},{10,... | collective-permute-start | bytes 737288 | tf_op jit(solution)/shard_map/ppermute | solution.py:594
  63.8 1.2 %collective-permute-start.15 = (bf16[16,128]{1,0:T(8,128)(2,1)S(1)}, bf16[16,128]{1,0:T(8,128)(2,1)S(1)}, u32[]{:S(2)}, u32[]{:S(2)}) collective-permute-start(bf16[16,128]{1,0:T(8,128)(2,1)S(1)} %coefficients.1), channel_id=1, source_target_pairs={{0,1},{1,0},{2,3},{3,2},{4,5},{5,4},{6,7},{7,6},{8,9},{9,8},{10,11... | collective-permute-start | bytes 12296 | tf_op jit(solution)/shard_map/ppermute | solution.py:597
  65.0 9.0 %collective-permute-start.21 = (bf16[2,10,48,128]{3,2,1,0:T(8,128)(2,1)S(1)}, bf16[2,10,48,128]{3,2,1,0:T(8,128)(2,1)S(1)}, u32[]{:S(2)}, u32[]{:S(2)}) collective-permute-start(bf16[2,10,48,128]{3,2,1,0:T(8,128)(2,1)S(1)} %get-tuple-element.64.a), channel_id=1, source_target_pairs={{0,1},{1,0},{2,3},{3,2},{4,5},{5,4},{6,7},{7,6},{8,9},{9,8},{10,11... | collective-permute-start | bytes 737288 | tf_op jit(solution)/shard_map/ppermute | solution.py:583
  65.8 10.8 %collective-permute-start.20 = (bf16[2,10,48,128]{3,2,1,0:T(8,128)(2,1)S(1)}, bf16[2,10,48,128]{3,2,1,0:T(8,128)(2,1)S(1)}, u32[]{:S(2)}, u32[]{:S(2)}) collective-permute-start(bf16[2,10,48,128]{3,2,1,0:T(8,128)(2,1)S(1)} %rotated.3), channel_id=1, source_target_pairs={{0,4},{4,0},{8,12},{12,8},{16,20},{20,16},{24,28},{28,24},{1,5},{5... | collective-permute-start | bytes 737288 | tf_op jit(solution)/shard_map/ppermute | solution.py:600
  67.5 4.6 %collective-permute-start.17 = (bf16[32,128]{1,0:T(8,128)(2,1)S(1)}, bf16[32,128]{1,0:T(8,128)(2,1)S(1)}, u32[]{:S(2)}, u32[]{:S(2)}) collective-permute-start(bf16[32,128]{1,0:T(8,128)(2,1)S(1)} %pad_maximum_fusion), channel_id=1, source_target_pairs={{0,2},{1,3},{2,0},{3,1},{4,6},{5,7},{6,4},{7,5},{8,10},{9,11},{10,... | collective-permute-start | bytes 24584 | tf_op jit(solution)/shard_map/ppermute | solution.py:602
  72.1 4.5 %collective-permute-start.22 = (bf16[2,10,48,128]{3,2,1,0:T(8,128)(2,1)S(1)}, bf16[2,10,48,128]{3,2,1,0:T(8,128)(2,1)S(1)}, u32[]{:S(2)}, u32[]{:S(2)}) collective-permute-start(bf16[2,10,48,128]{3,2,1,0:T(8,128)(2,1)S(1)} %collective-permute-done.18.c), channel_id=1, source_target_pairs={{0,1},{1,0},{2,3},{3,2},{4,5},{5,4},{6,7},{7,6},{8,9},{9,8},{10,11... | collective-permute-start | bytes 737288 | tf_op jit(solution)/shard_map/ppermute | solution.py:606

commit v16 on v15

--- a/solution.py
+++ b/solution.py
@@ -569,7 +569,7 @@
         pairs = [(i, i ^ step) for i in range(slabs)]
         return values + lax.ppermute(values, "space", pairs)
 
-    for step in rounds[:2]:
+    for step in rounds[:1]:
         sums = added(sums, step)
     zf2, sums = ordered(zf2, sums)
     give2, keep2 = filtered(slabs, rows1, rows2, False, operands, (xr1, xr2), (zf1, zf2))
@@ -582,7 +582,9 @@
     cg = lax.ppermute(give2, "orb", beside)
     ck = lax.ppermute(keep2, "orb", beside)
     yg = lax.ppermute(give2, "orb", across)
-    y1, again, _ = ordered(y1, block1, give2)
+    for step in rounds[1:2]:
+        sums = added(sums, step)
+    y1, again, _, sums = ordered(y1, block1, give2, sums)
     c1 = lax.ppermute(again, "orb", beside)
     yc1 = lax.ppermute(y1, "orb", beside)
     for step in rounds[2:]:

time: 78.6 us -> 76.2 us (0.969)
  waiting for transfers between devices: 26 us -> 22.1 us
  starting transfers between devices: 27.9 us -> 29.4 us
    ppermute x1, waiting for transfers between devices: 2.4 us -> 0.01 us  [shards(): yc1 = lax.ppermute(y1, 'orb', beside)]
    ppermute x1, waiting for transfers between devices: 2.16 us -> 0.01 us  [shards(): got1 = lax.ppermute(give1, 'space', swap)]
    ppermute x1, waiting for transfers between devices: 1.96 us -> 3.73 us  [shards(): yk = lax.ppermute(keep_y, 'orb', across)]
    ppermute x1, starting transfers between devices: 0.43 us -> 1.93 us  [shards(): got1 = lax.ppermute(give1, 'space', swap)]
    ppermute x1, starting transfers between devices: 1.72 us -> 0.32 us  [shards(): got2 = lax.ppermute(give2, 'space', swap)]
    ppermute x3, starting transfers between devices: 4.27 us -> 5.22 us  [added(): return values + lax.ppermute(values, 'space', pairs)]
    ppermute x1, starting transfers between devices: 1.52 us -> 2.42 us  [shards(): yk = lax.ppermute(keep_y, 'orb', across)]
    ppermute x3, waiting for transfers between devices: 5.81 us -> 4.98 us  [added(): return values + lax.ppermute(values, 'space', pairs)]
  transfers between devices with their start and end apart: 23 -> 23, of which waited for: 10 -> 9; matrix products, arithmetic and copies ran while one was open for 1% -> 1% of each run, Pallas kernels for 17% -> 18%
where the time goes in v16:
time: 76.2 us; the launch traced here: 75.9 us
  starting transfers between devices  29.4 us (39%)
  Pallas kernels  22.4 us (29%)
  waiting for transfers between devices  22.1 us (29%)
  local copies, waits for them, and re-layouts  0.94 us (1%)
    pallas_call x2, Pallas kernels, filtered(): pl.pallas_call(functools.partial(filter_kernel, slabs, start, parts, join...  9.14 us
    ppermute x1, waiting for transfers between devices, shards(): xr1 = lax.ppermute(to_x, 'space', swap)  5.25 us
    ppermute x3, starting transfers between devices, added(): return values + lax.ppermute(values, 'space', pairs)  5.22 us
    ppermute x3, waiting for transfers between devices, added(): return values + lax.ppermute(values, 'space', pairs)  4.98 us
    ppermute x1, starting transfers between devices, shards(): zf2 = lax.ppermute(xr2, 'space', other_way)  4.28 us
    ppermute x1, starting transfers between devices, shards(): zf1 = lax.ppermute(xr1, 'space', other_way)  3.97 us
    ppermute x1, waiting for transfers between devices, shards(): yk = lax.ppermute(keep_y, 'orb', across)  3.73 us
    pallas_call x1, Pallas kernels, partials(): pl.pallas_call(functools.partial(partial_kernel, count), out_shape=(jax.S...  3.04 us
  transfers between devices with their start and end apart: 23, of which 9 were waited for; matrix products, arithmetic and copies ran while one was open for 1% of the time, Pallas kernels for 18%

profile of v16, /device:TPU:0, one launch (start us, length us, event | category | flops | bytes accessed | tf_op | source)
XLA Modules:
  0.0 75.9 jit_solution(4705069837489208067)
XLA Ops:
  0.0 2.2 %prepared.1 = (bf16[2,19,48,128]{3,2,1,0:T(8,128)(2,1)S(1)}, bf16[2,27,48,128]{3,2,1,0:T(8,128)(2,1)}) custom-call(bf16[2,48,48,128]{3,2,1,0:T(8,128)(2,1)} %refs_0_.3, f32[2,48,48]{2,1,0:T(8,128)} %refs_1_.3), custom_call_target="tpu_custom_call" | custom-call | flops 256 | bytes 256 | tf_op jit(solution)/shard_map/prepared/pallas_call | solution.py:81
  2.2 0.0 copy-start.1
  2.2 0.0 copy-start.3
  2.2 3.0 %collective-permute-start.1 = (bf16[2,19,48,128]{3,2,1,0:T(8,128)(2,1)S(1)}, bf16[2,19,48,128]{3,2,1,0:T(8,128)(2,1)}, u32[]{:S(2)}, u32[]{:S(2)}) collective-permute-start(bf16[2,19,48,128]{3,2,1,0:T(8,128)(2,1)S(1)} %get-tuple-element.38), channel_id=1, source_target_pairs={{0,4},{4,0},{8,12},{12,8},{16,20},{20,16},{24,28},{28,24},{1,5},{5... | collective-permute-start | bytes 1400840 | tf_op jit(solution)/shard_map/ppermute | solution.py:550
  5.2 1.3 %collective-permute-start = (bf16[2,27,48,128]{3,2,1,0:T(8,128)(2,1)}, bf16[2,27,48,128]{3,2,1,0:T(8,128)(2,1)S(1)}, u32[]{:S(2)}, u32[]{:S(2)}) collective-permute-start(bf16[2,27,48,128]{3,2,1,0:T(8,128)(2,1)} %get-tuple-element.37), channel_id=1, source_target_pairs={{4,12},{8,0},{12,20},{16,8},{20,28},{24,16},{5,13},{9,1},{13,21},{... | collective-permute-start | bytes 1990664 | tf_op jit(solution)/shard_map/ppermute | solution.py:551
  6.5 1.6 %packed.1 = (bf16[2,8,48,128]{3,2,1,0:T(8,128)(2,1)S(1)}, bf16[8,48,48]{2,1,0:T(8,128)(2,1)S(1)}, bf16[8,48,48]{2,1,0:T(8,128)(2,1)}) custom-call(bf16[2,48,48,128]{3,2,1,0:T(8,128)(2,1)} %refs_0_.3, bf16[8,2,48,48]{3,2,1,0:T(8,128)(2,1)S(1)} %copy-done.2), custom_call_target="tpu_custom_call" | custom-call | flops 256 | bytes 256 | tf_op jit(solution)/shard_map/packed/pallas_call | solution.py:110
  8.1 2.8 %collective-permute-start.4 = (bf16[8,48,48]{2,1,0:T(8,128)(2,1)}, bf16[8,48,48]{2,1,0:T(8,128)(2,1)S(1)}, u32[]{:S(2)}, u32[]{:S(2)}) collective-permute-start(bf16[8,48,48]{2,1,0:T(8,128)(2,1)} %get-tuple-element.42), channel_id=1, source_target_pairs={{0,4},{4,0},{8,12},{12,8},{16,20},{20,16},{24,28},{28,24},{1,5},{5... | collective-permute-start | bytes 110600 | tf_op jit(solution)/shard_map/ppermute | solution.py:547
  10.9 0.7 collective-permute-start.5
  11.6 5.2 %collective-permute-done.1.refs_3_ = bf16[2,19,48,128]{3,2,1,0:T(8,128)(2,1)} collective-permute-done((bf16[2,19,48,128]{3,2,1,0:T(8,128)(2,1)S(1)}, bf16[2,19,48,128]{3,2,1,0:T(8,128)(2,1)}, u32[]{:S(2)}, u32[]{:S(2)}) %collective-permute-start.1) | collective-permute-done | bytes 466976 | tf_op jit(solution)/shard_map/ppermute | solution.py:550
  16.8 4.0 %collective-permute-start.3 = (bf16[2,19,48,128]{3,2,1,0:T(8,128)(2,1)}, bf16[2,19,48,128]{3,2,1,0:T(8,128)(2,1)S(1)}, u32[]{:S(2)}, u32[]{:S(2)}) collective-permute-start(bf16[2,19,48,128]{3,2,1,0:T(8,128)(2,1)} %collective-permute-done.1.refs_3_), channel_id=1, source_target_pairs={{0,8},{8,16},{12,4},{16,24},{20,12},{28,20},{1,9},{9,17},{13,5},{1... | collective-permute-start | bytes 1400840 | tf_op jit(solution)/shard_map/ppermute | solution.py:556
  20.8 0.1 collective-permute-start.2
  20.9 0.1 broadcast_select_fusion
  21.0 0.3 convolution_bitcast_fusion.gram
  21.3 0.0 collective-permute-done.4.b_x
  21.3 0.0 collective-permute-done.5.b_d
  21.3 0.0 copy-done.1
  21.3 3.0 %partials.1 = (f32[24,128]{1,0:T(8,128)S(1)}, bf16[2,48,24,48]{3,2,1,0:T(8,128)(2,1)S(1)}) custom-call(s32[8]{0:T(128)S(1)} %copy-done.6, bf16[2,48,48,128]{3,2,1,0:T(8,128)(2,1)S(1)} %copy-done.1, bf16[8,2,48,48]{3,2,1,0:T(8,128)(2,1)S(1)} %copy-done.2, bf16[8,48,48]{2,1,0:T(8,128)(2,1)S(1)} %collective-permute-done.4.b_x, ...), custom_call_target="tpu_custom_call" | custom-call | flops 256 | bytes 256 | tf_op jit(solution)/shard_map/partials/pallas_call | solution.py:177
  24.4 2.2 %collective-permute-done.2.refs_4_ = bf16[2,8,48,128]{3,2,1,0:T(8,128)(2,1)S(1)} collective-permute-done((bf16[2,8,48,128]{3,2,1,0:T(8,128)(2,1)S(1)}, bf16[2,8,48,128]{3,2,1,0:T(8,128)(2,1)S(1)}, u32[]{:S(2)}, u32[]{:S(2)}) %collective-permute-start.2) | collective-permute-done | bytes 196640 | tf_op jit(solution)/shard_map/ppermute | solution.py:557
  26.6 2.5 %collective-permute-done.3.refs_5_.refs_4_ = bf16[2,19,48,128]{3,2,1,0:T(8,128)(2,1)S(1)} collective-permute-done((bf16[2,19,48,128]{3,2,1,0:T(8,128)(2,1)}, bf16[2,19,48,128]{3,2,1,0:T(8,128)(2,1)S(1)}, u32[]{:S(2)}, u32[]{:S(2)}) %collective-permute-start.3) | collective-permute-done | bytes 466976 | tf_op jit(solution)/shard_map/ppermute | solution.py:556
  29.1 0.0 collective-permute-done.refs_2_
  29.1 0.8 %copy-done.7 = bf16[2,19,48,128]{3,2,1,0:T(8,128)(2,1)} copy-done((bf16[2,19,48,128]{3,2,1,0:T(8,128)(2,1)}, bf16[2,19,48,128]{3,2,1,0:T(8,128)(2,1)S(1)}, u32[]{:S(2)}) %copy-start.7) | copy-done | bytes 466968
  29.9 5.0 %filtered.3.refs_0_ = bf16[4,14,48,128]{3,2,1,0:T(8,128)(2,1)S(1)} custom-call(bf16[2,48,48,128]{3,2,1,0:T(8,128)(2,1)S(1)} %copy-done.1, f32[2,48,48]{2,1,0:T(8,128)S(1)} %copy-done.3, bf16[2,27,48,128]{3,2,1,0:T(8,128)(2,1)S(1)} %collective-permute-done.refs_2_, bf16[2,19,48,128]{3,2,1,0:T(8,128)(2,1)} %collective-permute-done.1.refs_3_, ...), custom_call_target="tpu_custom_call" | custom-call | flops 3440640 | bytes 21504000 | tf_op jit(solution)/shard_map/filtered/pallas_call | solution.py:415
  34.9 1.6 %collective-permute-start.9 = (bf16[4,14,48,128]{3,2,1,0:T(8,128)(2,1)S(1)}, bf16[4,14,48,128]{3,2,1,0:T(8,128)(2,1)}, u32[]{:S(2)}, u32[]{:S(2)}) collective-permute-start(bf16[4,14,48,128]{3,2,1,0:T(8,128)(2,1)S(1)} %filtered.3.refs_0_), channel_id=1, source_target_pairs={{0,2},{1,3},{2,0},{3,1},{4,6},{5,7},{6,4},{7,5},{8,10},{9,11},{10,... | collective-permute-start | bytes 2064392 | tf_op jit(solution)/shard_map/ppermute | solution.py:565
  36.5 4.3 %collective-permute-start.6 = (bf16[2,8,48,128]{3,2,1,0:T(8,128)(2,1)S(1)}, bf16[2,8,48,128]{3,2,1,0:T(8,128)(2,1)S(1)}, u32[]{:S(2)}, u32[]{:S(2)}) collective-permute-start(bf16[2,8,48,128]{3,2,1,0:T(8,128)(2,1)S(1)} %collective-permute-done.2.refs_4_), channel_id=1, source_target_pairs={{0,8},{8,16},{12,4},{16,24},{20,12},{28,20},{1,9},{9,17},{13,5},{1... | collective-permute-start | bytes 589832 | tf_op jit(solution)/shard_map/ppermute | solution.py:558
  40.8 0.1 collective-permute-start.7
  40.9 3.7 %collective-permute-done.7 = f32[24,128]{1,0:T(8,128)S(1)} collective-permute-done((f32[24,128]{1,0:T(8,128)S(1)}, f32[24,128]{1,0:T(8,128)S(1)}, u32[]{:S(2)}, u32[]{:S(2)}) %collective-permute-start.7) | collective-permute-done | bytes 12320 | tf_op jit(solution)/shard_map/ppermute | solution.py:570
  44.5 0.0 collective-permute-done.6.refs_6_
  44.6 2.0 %collective-permute-start.10 = (f32[24,128]{1,0:T(8,128)S(1)}, f32[24,128]{1,0:T(8,128)S(1)}, u32[]{:S(2)}, u32[]{:S(2)}) collective-permute-start(f32[24,128]{1,0:T(8,128)S(1)} %add.9), channel_id=1, source_target_pairs={{0,8},{4,12},{8,0},{12,4},{16,24},{20,28},{24,16},{28,20},{1,9},{5... | collective-permute-start | bytes 36872 | tf_op jit(solution)/shard_map/ppermute | solution.py:570
  46.6 0.0 copy-start.11
  46.6 4.2 %filtered.2 = (bf16[2,10,48,128]{3,2,1,0:T(8,128)(2,1)S(1)}, bf16[2,10,48,128]{3,2,1,0:T(8,128)(2,1)S(1)}) custom-call(bf16[2,48,48,128]{3,2,1,0:T(8,128)(2,1)S(1)} %copy-done.1, f32[2,48,48]{2,1,0:T(8,128)S(1)} %copy-done.3, bf16[2,27,48,128]{3,2,1,0:T(8,128)(2,1)S(1)} %collective-permute-done.refs_2_, ...), custom_call_target="tpu_custom_call" | custom-call | flops 2457600 | bytes 15360000 | tf_op jit(solution)/shard_map/filtered/pallas_call | solution.py:415
  50.8 0.6 collective-permute-start.8
  51.3 0.0 collective-permute-done.10
  51.3 0.0 collective-permute-done.9.refs_2_
  51.3 0.1 collective-permute-start.11
  51.4 0.5 collective-permute-start.12
  51.9 3.1 %collective-permute-start.13 = (f32[24,128]{1,0:T(8,128)S(1)}, f32[24,128]{1,0:T(8,128)S(1)}, u32[]{:S(2)}, u32[]{:S(2)}) collective-permute-start(f32[24,128]{1,0:T(8,128)S(1)} %add.10), channel_id=1, source_target_pairs={{0,16},{4,20},{8,24},{12,28},{16,0},{20,4},{24,8},{28,12},{1,17},{... | collective-permute-start | bytes 36872 | tf_op jit(solution)/shard_map/ppermute | solution.py:570
  55.1 0.3 fusion
  55.4 1.3 %collective-permute-done.13 = f32[24,128]{1,0:T(8,128)S(1)} collective-permute-done((f32[24,128]{1,0:T(8,128)S(1)}, f32[24,128]{1,0:T(8,128)S(1)}, u32[]{:S(2)}, u32[]{:S(2)}) %collective-permute-start.13) | collective-permute-done | bytes 12320 | tf_op jit(solution)/shard_map/ppermute | solution.py:570
  56.7 0.0 collective-permute-done.12.refs_3_
  56.8 0.0 collective-permute-done.11.refs_1_
  56.8 2.1 %rotated.2 = (bf16[2,14,48,128]{3,2,1,0:T(8,128)(2,1)S(1)}, bf16[2,14,48,128]{3,2,1,0:T(8,128)(2,1)S(1)}) custom-call(bf16[4,14,48,128]{3,2,1,0:T(8,128)(2,1)S(1)} %filtered.3.refs_0_, bf16[4,14,48,128]{3,2,1,0:T(8,128)(2,1)S(1)} %collective-permute-done.11.refs_1_, bf16[4,14,48,128]{3,2,1,0:T(8,128)(2,1)} %collective-permute-done.9.refs_2_, ...), custom_call_target="tpu_custom_call" | custom-call | flops 22020096 | bytes 215040 | tf_op jit(solution)/shard_map/rotated/pallas_call | solution.py:459
  58.9 1.9 %collective-permute-start.19 = (bf16[2,14,48,128]{3,2,1,0:T(8,128)(2,1)S(1)}, bf16[2,14,48,128]{3,2,1,0:T(8,128)(2,1)S(1)}, u32[]{:S(2)}, u32[]{:S(2)}) collective-permute-start(bf16[2,14,48,128]{3,2,1,0:T(8,128)(2,1)S(1)} %get-tuple-element.57), channel_id=1, source_target_pairs={{0,4},{4,0},{8,12},{12,8},{16,20},{20,16},{24,28},{28,24},{1,5},{5... | collective-permute-start | bytes 1032200 | tf_op jit(solution)/shard_map/ppermute | solution.py:594
  60.9 0.0 collective-permute-done.8.refs_2_
  60.9 0.0 collective-permute-start.14
  60.9 0.5 collective-permute-start.16
  61.4 2.4 %collective-permute-start.18 = (bf16[2,10,48,128]{3,2,1,0:T(8,128)(2,1)S(1)}, bf16[2,10,48,128]{3,2,1,0:T(8,128)(2,1)S(1)}, u32[]{:S(2)}, u32[]{:S(2)}) collective-permute-start(bf16[2,10,48,128]{3,2,1,0:T(8,128)(2,1)S(1)} %get-tuple-element.66.a), channel_id=1, source_target_pairs={{0,2},{1,3},{2,0},{3,1},{4,6},{5,7},{6,4},{7,5},{8,10},{9,11},{10,... | collective-permute-start | bytes 737288 | tf_op jit(solution)/shard_map/ppermute | solution.py:596
  63.8 0.1 broadcast_in_dim.22.strength
  63.9 0.1 coefficients.1
  64.0 0.0 collective-permute-start.15
  64.0 1.2 %collective-permute-done.15 = bf16[16,128]{1,0:T(8,128)(2,1)S(1)} collective-permute-done((bf16[16,128]{1,0:T(8,128)(2,1)S(1)}, bf16[16,128]{1,0:T(8,128)(2,1)S(1)}, u32[]{:S(2)}, u32[]{:S(2)}) %collective-permute-start.15) | collective-permute-done | bytes 4128 | tf_op jit(solution)/shard_map/ppermute | solution.py:599
  65.2 0.2 collective-permute-start.21
  65.4 0.0 collective-permute-done.14.refs_3_
  65.4 0.0 collective-permute-done.16.refs_1_
  65.4 0.6 rotated.3
  65.9 0.3 collective-permute-start.20
  66.3 3.7 %collective-permute-done.18.c = bf16[2,10,48,128]{3,2,1,0:T(8,128)(2,1)S(1)} collective-permute-done((bf16[2,10,48,128]{3,2,1,0:T(8,128)(2,1)S(1)}, bf16[2,10,48,128]{3,2,1,0:T(8,128)(2,1)S(1)}, u32[]{:S(2)}, u32[]{:S(2)}) %collective-permute-start.18) | collective-permute-done | bytes 245792 | tf_op jit(solution)/shard_map/ppermute | solution.py:596
  70.0 0.0 collective-permute-done.19.got1
  70.0 0.0 collective-permute-start.22
  70.0 0.1 collective-permute-done.17
  70.1 1.9 %nonlocal.1.term = f32[2,48,48,128]{3,2,1,0:T(8,128)S(1)} custom-call(bf16[16,128]{1,0:T(8,128)(2,1)S(1)} %get-tuple-element.72.a, bf16[16,128]{1,0:T(8,128)(2,1)S(1)} %get-tuple-element.71.b, bf16[16,128]{1,0:T(8,128)(2,1)S(1)} %get-tuple-element.70.c, bf16[16,128]{1,0:T(8,128)(2,1)S(1)} %get-tuple-element.69.d, bf16[4,128,128]{2,1,0:T(8,128)(2,1)S(1)} %copy.18.refs_4_.q, ...), custom_call_target="tpu_custom_call" | custom-call | flops 256 | bytes 256 | tf_op jit(solution)/shard_map/nonlocal/pallas_call | solution.py:252
  72.0 0.0 collective-permute-done.21.b
  72.0 2.2 %collective-permute-done.20.got2 = bf16[2,10,48,128]{3,2,1,0:T(8,128)(2,1)S(1)} collective-permute-done((bf16[2,10,48,128]{3,2,1,0:T(8,128)(2,1)S(1)}, bf16[2,10,48,128]{3,2,1,0:T(8,128)(2,1)S(1)}, u32[]{:S(2)}, u32[]{:S(2)}) %collective-permute-start.20) | collective-permute-done | bytes 245792 | tf_op jit(solution)/shard_map/ppermute | solution.py:602
  74.2 0.0 collective-permute-done.22.d
  74.2 1.7 %assembled.1 = bf16[2,48,48,128]{3,2,1,0:T(8,128)(2,1)} custom-call(f32[2,48,48,128]{3,2,1,0:T(8,128)S(1)} %nonlocal.1.term, bf16[2,14,48,128]{3,2,1,0:T(8,128)(2,1)S(1)} %get-tuple-element.65.keep1, bf16[2,14,48,128]{3,2,1,0:T(8,128)(2,1)S(1)} %collective-permute-done.19.got1, bf16[2,10,48,128]{3,2,1,0:T(8,128)(2,1)S(1)} %collective-permute-done.20.got2, ...), custom_call_target="tpu_custom_call" | custom-call | flops 256 | bytes 256 | tf_op jit(solution)/shard_map/assembled/pallas_call | solution.py:506
  (31 shorter events, 0.1 us)
Async XLA Ops:
  0.0 55.1 %copy-start = (bf16[12,128,128]{2,1,0:T(8,128)(2,1)S(1)}, bf16[12,128,128]{2,1,0:T(8,128)(2,1)}, u32[]{:S(2)}) copy-start(bf16[12,128,128]{2,1,0:T(8,128)(2,1)} %param.13) | copy-start | bytes 1179652
  0.0 6.5 %copy-start.2 = (bf16[8,2,48,48]{3,2,1,0:T(8,128)(2,1)S(1)}, bf16[8,2,48,48]{3,2,1,0:T(8,128)(2,1)}, u32[]{:S(2)}) copy-start(bf16[8,2,48,48]{3,2,1,0:T(8,128)(2,1)} %beta.3) | copy-start | bytes 221188
  0.0 20.8 %copy-start.6 = (s32[8]{0:T(128)S(1)}, s32[8]{0:T(128)}, u32[]{:S(2)}) copy-start(s32[8]{0:T(128)} %atoms.1) | copy-start | bytes 100
  2.2 19.1 %copy-start.1 = (bf16[2,48,48,128]{3,2,1,0:T(8,128)(2,1)S(1)}, bf16[2,48,48,128]{3,2,1,0:T(8,128)(2,1)}, u32[]{:S(2)}) copy-start(bf16[2,48,48,128]{3,2,1,0:T(8,128)(2,1)} %refs_0_.3) | copy-start | bytes 3538948
  2.2 19.1 %copy-start.3 = (f32[2,48,48]{2,1,0:T(8,128)S(1)}, f32[2,48,48]{2,1,0:T(8,128)}, u32[]{:S(2)}) copy-start(f32[2,48,48]{2,1,0:T(8,128)} %refs_1_.3) | copy-start | bytes 55300
  2.2 14.6 %collective-permute-start.1 = (bf16[2,19,48,128]{3,2,1,0:T(8,128)(2,1)S(1)}, bf16[2,19,48,128]{3,2,1,0:T(8,128)(2,1)}, u32[]{:S(2)}, u32[]{:S(2)}) collective-permute-start(bf16[2,19,48,128]{3,2,1,0:T(8,128)(2,1)S(1)} %get-tuple-element.38), channel_id=1, source_target_pairs={{0,4},{4,0},{8,12},{12,8},{16,20},{20,16},{24,28},{28,24},{1,5},{5... | collective-permute-start | bytes 1400840 | tf_op jit(solution)/shard_map/ppermute | solution.py:550
  5.2 23.9 %collective-permute-start = (bf16[2,27,48,128]{3,2,1,0:T(8,128)(2,1)}, bf16[2,27,48,128]{3,2,1,0:T(8,128)(2,1)S(1)}, u32[]{:S(2)}, u32[]{:S(2)}) collective-permute-start(bf16[2,27,48,128]{3,2,1,0:T(8,128)(2,1)} %get-tuple-element.37), channel_id=1, source_target_pairs={{4,12},{8,0},{12,20},{16,8},{20,28},{24,16},{5,13},{9,1},{13,21},{... | collective-permute-start | bytes 1990664 | tf_op jit(solution)/shard_map/ppermute | solution.py:551
  8.1 13.2 %collective-permute-start.4 = (bf16[8,48,48]{2,1,0:T(8,128)(2,1)}, bf16[8,48,48]{2,1,0:T(8,128)(2,1)S(1)}, u32[]{:S(2)}, u32[]{:S(2)}) collective-permute-start(bf16[8,48,48]{2,1,0:T(8,128)(2,1)} %get-tuple-element.42), channel_id=1, source_target_pairs={{0,4},{4,0},{8,12},{12,8},{16,20},{20,16},{24,28},{28,24},{1,5},{5... | collective-permute-start | bytes 110600 | tf_op jit(solution)/shard_map/ppermute | solution.py:547
  10.9 10.4 %collective-permute-start.5 = (bf16[8,48,48]{2,1,0:T(8,128)(2,1)S(1)}, bf16[8,48,48]{2,1,0:T(8,128)(2,1)S(1)}, u32[]{:S(2)}, u32[]{:S(2)}) collective-permute-start(bf16[8,48,48]{2,1,0:T(8,128)(2,1)S(1)} %get-tuple-element.43), channel_id=1, source_target_pairs={{4,8},{8,4},{12,16},{16,12},{20,24},{24,20},{5,9},{9,5},{13,17},{1... | collective-permute-start | bytes 110600 | tf_op jit(solution)/shard_map/ppermute | solution.py:549
  16.8 12.3 %collective-permute-start.3 = (bf16[2,19,48,128]{3,2,1,0:T(8,128)(2,1)}, bf16[2,19,48,128]{3,2,1,0:T(8,128)(2,1)S(1)}, u32[]{:S(2)}, u32[]{:S(2)}) collective-permute-start(bf16[2,19,48,128]{3,2,1,0:T(8,128)(2,1)} %collective-permute-done.1.refs_3_), channel_id=1, source_target_pairs={{0,8},{8,16},{12,4},{16,24},{20,12},{28,20},{1,9},{9,17},{13,5},{1... | collective-permute-start | bytes 1400840 | tf_op jit(solution)/shard_map/ppermute | solution.py:556
  20.8 5.7 %collective-permute-start.2 = (bf16[2,8,48,128]{3,2,1,0:T(8,128)(2,1)S(1)}, bf16[2,8,48,128]{3,2,1,0:T(8,128)(2,1)S(1)}, u32[]{:S(2)}, u32[]{:S(2)}) collective-permute-start(bf16[2,8,48,128]{3,2,1,0:T(8,128)(2,1)S(1)} %get-tuple-element.41), channel_id=1, source_target_pairs={{0,4},{4,0},{8,12},{12,8},{16,20},{20,16},{24,28},{28,24},{1,5},{5... | collective-permute-start | bytes 589832 | tf_op jit(solution)/shard_map/ppermute | solution.py:557
  24.4 10.5 %copy-start.4 = (bf16[2,48,24,48]{3,2,1,0:T(8,128)(2,1)}, bf16[2,48,24,48]{3,2,1,0:T(8,128)(2,1)S(1)}, u32[]{:S(2)}) copy-start(bf16[2,48,24,48]{3,2,1,0:T(8,128)(2,1)S(1)} %get-tuple-element.64.weights) | copy-start | bytes 663556
  26.6 20.0 %copy-start.8 = (bf16[2,8,48,128]{3,2,1,0:T(8,128)(2,1)}, bf16[2,8,48,128]{3,2,1,0:T(8,128)(2,1)S(1)}, u32[]{:S(2)}) copy-start(bf16[2,8,48,128]{3,2,1,0:T(8,128)(2,1)S(1)} %collective-permute-done.2.refs_4_) | copy-start | bytes 589828
  29.1 0.8 %copy-start.7 = (bf16[2,19,48,128]{3,2,1,0:T(8,128)(2,1)}, bf16[2,19,48,128]{3,2,1,0:T(8,128)(2,1)S(1)}, u32[]{:S(2)}) copy-start(bf16[2,19,48,128]{3,2,1,0:T(8,128)(2,1)S(1)} %collective-permute-done.3.refs_5_.refs_4_) | copy-start | bytes 1400836
  34.9 16.4 %collective-permute-start.9 = (bf16[4,14,48,128]{3,2,1,0:T(8,128)(2,1)S(1)}, bf16[4,14,48,128]{3,2,1,0:T(8,128)(2,1)}, u32[]{:S(2)}, u32[]{:S(2)}) collective-permute-start(bf16[4,14,48,128]{3,2,1,0:T(8,128)(2,1)S(1)} %filtered.3.refs_0_), channel_id=1, source_target_pairs={{0,2},{1,3},{2,0},{3,1},{4,6},{5,7},{6,4},{7,5},{8,10},{9,11},{10,... | collective-permute-start | bytes 2064392 | tf_op jit(solution)/shard_map/ppermute | solution.py:565
  36.5 8.1 %collective-permute-start.6 = (bf16[2,8,48,128]{3,2,1,0:T(8,128)(2,1)S(1)}, bf16[2,8,48,128]{3,2,1,0:T(8,128)(2,1)S(1)}, u32[]{:S(2)}, u32[]{:S(2)}) collective-permute-start(bf16[2,8,48,128]{3,2,1,0:T(8,128)(2,1)S(1)} %collective-permute-done.2.refs_4_), channel_id=1, source_target_pairs={{0,8},{8,16},{12,4},{16,24},{20,12},{28,20},{1,9},{9,17},{13,5},{1... | collective-permute-start | bytes 589832 | tf_op jit(solution)/shard_map/ppermute | solution.py:558
  40.8 3.8 %collective-permute-start.7 = (f32[24,128]{1,0:T(8,128)S(1)}, f32[24,128]{1,0:T(8,128)S(1)}, u32[]{:S(2)}, u32[]{:S(2)}) collective-permute-start(f32[24,128]{1,0:T(8,128)S(1)} %get-tuple-element.46), channel_id=1, source_target_pairs={{0,4},{4,0},{8,12},{12,8},{16,20},{20,16},{24,28},{28,24},{1,5},{5... | collective-permute-start | bytes 36872 | tf_op jit(solution)/shard_map/ppermute | solution.py:570
  44.6 2.0 %copy-start.9 = (bf16[2,8,48,128]{3,2,1,0:T(8,128)(2,1)}, bf16[2,8,48,128]{3,2,1,0:T(8,128)(2,1)S(1)}, u32[]{:S(2)}) copy-start(bf16[2,8,48,128]{3,2,1,0:T(8,128)(2,1)S(1)} %collective-permute-done.6.refs_6_) | copy-start | bytes 589828
  44.6 6.8 %collective-permute-start.10 = (f32[24,128]{1,0:T(8,128)S(1)}, f32[24,128]{1,0:T(8,128)S(1)}, u32[]{:S(2)}, u32[]{:S(2)}) collective-permute-start(f32[24,128]{1,0:T(8,128)S(1)} %add.9), channel_id=1, source_target_pairs={{0,8},{4,12},{8,0},{12,4},{16,24},{20,28},{24,16},{28,20},{1,9},{5... | collective-permute-start | bytes 36872 | tf_op jit(solution)/shard_map/ppermute | solution.py:570
  46.6 5.3 %copy-start.11 = (s32[12,2]{0,1:T(2,128)S(1)}, s32[12,2]{0,1:T(2,128)}, u32[]{:S(2)}) copy-start(s32[12,2]{0,1:T(2,128)} %param.12) | copy-start | bytes 292
  50.8 10.1 %collective-permute-start.8 = (bf16[2,10,48,128]{3,2,1,0:T(8,128)(2,1)S(1)}, bf16[2,10,48,128]{3,2,1,0:T(8,128)(2,1)S(1)}, u32[]{:S(2)}, u32[]{:S(2)}) collective-permute-start(bf16[2,10,48,128]{3,2,1,0:T(8,128)(2,1)S(1)} %get-tuple-element.49.refs_0_), channel_id=1, source_target_pairs={{0,2},{1,3},{2,0},{3,1},{4,6},{5,7},{6,4},{7,5},{8,10},{9,11},{10,... | collective-permute-start | bytes 737288 | tf_op jit(solution)/shard_map/ppermute | solution.py:584
  51.3 5.4 %collective-permute-start.11 = (bf16[4,14,48,128]{3,2,1,0:T(8,128)(2,1)S(1)}, bf16[4,14,48,128]{3,2,1,0:T(8,128)(2,1)S(1)}, u32[]{:S(2)}, u32[]{:S(2)}) collective-permute-start(bf16[4,14,48,128]{3,2,1,0:T(8,128)(2,1)S(1)} %filtered.3.refs_0_), channel_id=1, source_target_pairs={{0,1},{1,0},{2,3},{3,2},{4,5},{5,4},{6,7},{7,6},{8,9},{9,8},{10,11... | collective-permute-start | bytes 2064392 | tf_op jit(solution)/shard_map/ppermute | solution.py:588
  51.4 5.3 %collective-permute-start.12 = (bf16[4,14,48,128]{3,2,1,0:T(8,128)(2,1)}, bf16[4,14,48,128]{3,2,1,0:T(8,128)(2,1)S(1)}, u32[]{:S(2)}, u32[]{:S(2)}) collective-permute-start(bf16[4,14,48,128]{3,2,1,0:T(8,128)(2,1)} %collective-permute-done.9.refs_2_), channel_id=1, source_target_pairs={{0,1},{1,0},{2,3},{3,2},{4,5},{5,4},{6,7},{7,6},{8,9},{9,8},{10,11... | collective-permute-start | bytes 2064392 | tf_op jit(solution)/shard_map/ppermute | solution.py:589
  51.9 4.8 %collective-permute-start.13 = (f32[24,128]{1,0:T(8,128)S(1)}, f32[24,128]{1,0:T(8,128)S(1)}, u32[]{:S(2)}, u32[]{:S(2)}) collective-permute-start(f32[24,128]{1,0:T(8,128)S(1)} %add.10), channel_id=1, source_target_pairs={{0,16},{4,20},{8,24},{12,28},{16,0},{20,4},{24,8},{28,12},{1,17},{... | collective-permute-start | bytes 36872 | tf_op jit(solution)/shard_map/ppermute | solution.py:570
  56.7 7.1 %copy-start.10 = (f32[8]{0:T(128)S(1)}, f32[8]{0:T(128)}, u32[]{:S(2)}) copy-start(f32[8]{0:T(128)} %param.10) | copy-start | bytes 100
  58.9 11.2 %copy-start.5 = (bf16[2,48,24,48]{3,2,1,0:T(8,128)(2,1)S(1)}, bf16[2,48,24,48]{3,2,1,0:T(8,128)(2,1)}, u32[]{:S(2)}) copy-start(bf16[2,48,24,48]{3,2,1,0:T(8,128)(2,1)} %copy-done.4) | copy-start | bytes 663556
  58.9 11.1 %collective-permute-start.19 = (bf16[2,14,48,128]{3,2,1,0:T(8,128)(2,1)S(1)}, bf16[2,14,48,128]{3,2,1,0:T(8,128)(2,1)S(1)}, u32[]{:S(2)}, u32[]{:S(2)}) collective-permute-start(bf16[2,14,48,128]{3,2,1,0:T(8,128)(2,1)S(1)} %get-tuple-element.57), channel_id=1, source_target_pairs={{0,4},{4,0},{8,12},{12,8},{16,20},{20,16},{24,28},{28,24},{1,5},{5... | collective-permute-start | bytes 1032200 | tf_op jit(solution)/shard_map/ppermute | solution.py:594
  60.9 4.5 %collective-permute-start.14 = (bf16[2,10,48,128]{3,2,1,0:T(8,128)(2,1)S(1)}, bf16[2,10,48,128]{3,2,1,0:T(8,128)(2,1)S(1)}, u32[]{:S(2)}, u32[]{:S(2)}) collective-permute-start(bf16[2,10,48,128]{3,2,1,0:T(8,128)(2,1)S(1)} %collective-permute-done.8.refs_2_), channel_id=1, source_target_pairs={{0,1},{1,0},{2,3},{3,2},{4,5},{5,4},{6,7},{7,6},{8,9},{9,8},{10,11... | collective-permute-start | bytes 737288 | tf_op jit(solution)/shard_map/ppermute | solution.py:597
  60.9 4.5 %collective-permute-start.16 = (bf16[2,10,48,128]{3,2,1,0:T(8,128)(2,1)S(1)}, bf16[2,10,48,128]{3,2,1,0:T(8,128)(2,1)S(1)}, u32[]{:S(2)}, u32[]{:S(2)}) collective-permute-start(bf16[2,10,48,128]{3,2,1,0:T(8,128)(2,1)S(1)} %get-tuple-element.49.refs_0_), channel_id=1, source_target_pairs={{0,1},{1,0},{2,3},{3,2},{4,5},{5,4},{6,7},{7,6},{8,9},{9,8},{10,11... | collective-permute-start | bytes 737288 | tf_op jit(solution)/shard_map/ppermute | solution.py:582
  61.4 8.6 %collective-permute-start.18 = (bf16[2,10,48,128]{3,2,1,0:T(8,128)(2,1)S(1)}, bf16[2,10,48,128]{3,2,1,0:T(8,128)(2,1)S(1)}, u32[]{:S(2)}, u32[]{:S(2)}) collective-permute-start(bf16[2,10,48,128]{3,2,1,0:T(8,128)(2,1)S(1)} %get-tuple-element.66.a), channel_id=1, source_target_pairs={{0,2},{1,3},{2,0},{3,1},{4,6},{5,7},{6,4},{7,5},{8,10},{9,11},{10,... | collective-permute-start | bytes 737288 | tf_op jit(solution)/shard_map/ppermute | solution.py:596
  64.0 1.2 %collective-permute-start.15 = (bf16[16,128]{1,0:T(8,128)(2,1)S(1)}, bf16[16,128]{1,0:T(8,128)(2,1)S(1)}, u32[]{:S(2)}, u32[]{:S(2)}) collective-permute-start(bf16[16,128]{1,0:T(8,128)(2,1)S(1)} %coefficients.1), channel_id=1, source_target_pairs={{0,1},{1,0},{2,3},{3,2},{4,5},{5,4},{6,7},{7,6},{8,9},{9,8},{10,11... | collective-permute-start | bytes 12296 | tf_op jit(solution)/shard_map/ppermute | solution.py:599
  65.2 6.8 %collective-permute-start.21 = (bf16[2,10,48,128]{3,2,1,0:T(8,128)(2,1)S(1)}, bf16[2,10,48,128]{3,2,1,0:T(8,128)(2,1)S(1)}, u32[]{:S(2)}, u32[]{:S(2)}) collective-permute-start(bf16[2,10,48,128]{3,2,1,0:T(8,128)(2,1)S(1)} %get-tuple-element.66.a), channel_id=1, source_target_pairs={{0,1},{1,0},{2,3},{3,2},{4,5},{5,4},{6,7},{7,6},{8,9},{9,8},{10,11... | collective-permute-start | bytes 737288 | tf_op jit(solution)/shard_map/ppermute | solution.py:583
  65.9 8.3 %collective-permute-start.20 = (bf16[2,10,48,128]{3,2,1,0:T(8,128)(2,1)S(1)}, bf16[2,10,48,128]{3,2,1,0:T(8,128)(2,1)S(1)}, u32[]{:S(2)}, u32[]{:S(2)}) collective-permute-start(bf16[2,10,48,128]{3,2,1,0:T(8,128)(2,1)S(1)} %rotated.3), channel_id=1, source_target_pairs={{0,4},{4,0},{8,12},{12,8},{16,20},{20,16},{24,28},{28,24},{1,5},{5... | collective-permute-start | bytes 737288 | tf_op jit(solution)/shard_map/ppermute | solution.py:602
  66.3 3.8 %collective-permute-start.17 = (bf16[32,128]{1,0:T(8,128)(2,1)S(1)}, bf16[32,128]{1,0:T(8,128)(2,1)S(1)}, u32[]{:S(2)}, u32[]{:S(2)}) collective-permute-start(bf16[32,128]{1,0:T(8,128)(2,1)S(1)} %pad_maximum_fusion), channel_id=1, source_target_pairs={{0,2},{1,3},{2,0},{3,1},{4,6},{5,7},{6,4},{7,5},{8,10},{9,11},{10,... | collective-permute-start | bytes 24584 | tf_op jit(solution)/shard_map/ppermute | solution.py:604
  70.0 4.2 %collective-permute-start.22 = (bf16[2,10,48,128]{3,2,1,0:T(8,128)(2,1)S(1)}, bf16[2,10,48,128]{3,2,1,0:T(8,128)(2,1)S(1)}, u32[]{:S(2)}, u32[]{:S(2)}) collective-permute-start(bf16[2,10,48,128]{3,2,1,0:T(8,128)(2,1)S(1)} %collective-permute-done.18.c), channel_id=1, source_target_pairs={{0,1},{1,0},{2,3},{3,2},{4,5},{5,4},{6,7},{7,6},{8,9},{9,8},{10,11... | collective-permute-start | bytes 737288 | tf_op jit(solution)/shard_map/ppermute | solution.py:608

commit v17 on v16

--- a/solution.py
+++ b/solution.py
@@ -284,6 +284,9 @@
     early = xrs[0].shape[1] - 1
     copies = []
     for k, (target, pieces) in enumerate(((xr, xrs), (zf, zfs))):
+        if parts == 1 and k == 1:
+            zf = pieces[0]
+            continue
         begin = 0 if parts == 1 else early - 8
         moved = [
             (pieces[0].at[:, pl.ds(early, 1)], pots.at[k]),
@@ -315,7 +318,10 @@
     for copy in copies:
         copy.wait()
     for c in (1, 4, 5):
-        fill(c, pots[1 if c < 2 else 0, (c % 2) ^ x, 0].astype(F32))
+        if parts == 1 and c == 1:
+            fill(c, zf[(c % 2) ^ x, early].astype(F32))
+        else:
+            fill(c, pots[1 if c < 2 else 0, (c % 2) ^ x, 0].astype(F32))
 
     here = neighbour_sum(width, True)
     i = lax.broadcasted_iota(jnp.int32, (cells, cells), 0)
@@ -408,14 +414,15 @@
     scratch += [pltpu.VMEM((2, planes, 1, width, orbs), BF16), pltpu.SemaphoreType.DMA((6,))]
     local = pl.BlockSpec(memory_space=pltpu.VMEM)
     distant = pl.BlockSpec(memory_space=pltpu.MemorySpace.HBM)
-    xrs, zfs = (
-        [pltpu.with_memory_space_constraint(piece, pltpu.MemorySpace.HBM) for piece in pieces]
-        for pieces in (xrs, zfs)
-    )
+    far_xr = [pltpu.with_memory_space_constraint(a, pltpu.MemorySpace.HBM) for a in xrs]
+    far_zf = [pltpu.with_memory_space_constraint(a, pltpu.MemorySpace.HBM) for a in zfs]
+    xrs, zfs = far_xr, (far_zf if parts > 1 else zfs)
     return pl.pallas_call(
         functools.partial(filter_kernel, slabs, start, parts, joint),
         out_shape=out,
-        in_specs=[local] * len(operands) + [distant] * (2 * parts),
+        in_specs=[local] * len(operands)
+        + [distant] * parts
+        + [distant if parts > 1 else local] * parts,
         out_specs=(local,) * len(out),
         scratch_shapes=scratch,
         compiler_params=params(),
@@ -526,7 +533,7 @@
     x = lax.rem(place, 2)
     half = width_x // 2
     window = half + 2
-    rows1 = half * 7 // 24 * 2
+    rows1 = half // 4 * 2
     rows2 = half - rows1
     early = rows1 + 4
 

time: 76.2 us -> 77 us (1.010)
  starting transfers between devices: 29.4 us -> 30.3 us
  local copies, waits for them, and re-layouts: 0.94 us -> 0.15 us
    ppermute x1, waiting for transfers between devices: 0.01 us -> 2.34 us  [shards(): got1 = lax.ppermute(give1, 'space', swap)]
    ppermute x1, waiting for transfers between devices: 2.54 us -> 0.86 us  [shards(): zf1 = lax.ppermute(xr1, 'space', other_way)]
    ppermute x1, starting transfers between devices: 4.28 us -> 5.72 us  [shards(): zf2 = lax.ppermute(xr2, 'space', other_way)]
    ppermute x1, waiting for transfers between devices: 5.25 us -> 4.12 us  [shards(): xr1 = lax.ppermute(to_x, 'space', swap)]
    ppermute x1, waiting for transfers between devices: 3.73 us -> 2.73 us  [shards(): yk = lax.ppermute(keep_y, 'orb', across)]
    ppermute x1, waiting for transfers between devices: 2.2 us -> 3.18 us  [shards(): got2 = lax.ppermute(give2, 'space', swap)]
    ppermute x1, starting transfers between devices: 2.42 us -> 1.51 us  [shards(): yk = lax.ppermute(keep_y, 'orb', across)]
    unnamed x24 -> x22, local copies, waits for them, and re-layouts: 0.85 us -> 0.05 us
  transfers between devices with their start and end apart: 23 -> 23, of which waited for: 9 -> 10; matrix products, arithmetic and copies ran while one was open for 1% -> 1% of each run, Pallas kernels for 18% -> 18%
where the time goes in v17:
time: 77 us; the launch traced here: 76.7 us
  starting transfers between devices  30.3 us (39%)
  waiting for transfers between devices  22.8 us (30%)
  Pallas kernels  22.5 us (29%)
    pallas_call x2, Pallas kernels, filtered(): pl.pallas_call(functools.partial(filter_kernel, slabs, start, parts, join...  9.13 us
    ppermute x1, starting transfers between devices, shards(): zf2 = lax.ppermute(xr2, 'space', other_way)  5.72 us
    ppermute x3, waiting for transfers between devices, added(): return values + lax.ppermute(values, 'space', pairs)  5.32 us
    ppermute x3, starting transfers between devices, added(): return values + lax.ppermute(values, 'space', pairs)  5.11 us
    ppermute x1, waiting for transfers between devices, shards(): xr1 = lax.ppermute(to_x, 'space', swap)  4.12 us
    ppermute x1, starting transfers between devices, shards(): zf1 = lax.ppermute(xr1, 'space', other_way)  3.97 us
    ppermute x1, waiting for transfers between devices, shards(): got2 = lax.ppermute(give2, 'space', swap)  3.18 us
    pallas_call x1, Pallas kernels, partials(): pl.pallas_call(functools.partial(partial_kernel, count), out_shape=(jax.S...  3.04 us
  transfers between devices with their start and end apart: 23, of which 10 were waited for; matrix products, arithmetic and copies ran while one was open for 1% of the time, Pallas kernels for 18%

profile of v17, /device:TPU:0, one launch (start us, length us, event | category | flops | bytes accessed | tf_op | source)
XLA Modules:
  0.0 76.7 jit_solution(1353035428510891917)
XLA Ops:
  0.0 2.2 %prepared.1 = (bf16[2,17,48,128]{3,2,1,0:T(8,128)(2,1)S(1)}, bf16[2,27,48,128]{3,2,1,0:T(8,128)(2,1)}) custom-call(bf16[2,48,48,128]{3,2,1,0:T(8,128)(2,1)} %refs_0_.3, f32[2,48,48]{2,1,0:T(8,128)} %refs_1_.3), custom_call_target="tpu_custom_call" | custom-call | flops 256 | bytes 256 | tf_op jit(solution)/shard_map/prepared/pallas_call | solution.py:81
  2.2 0.0 copy-start.1
  2.2 0.0 copy-start.4
  2.2 3.0 %collective-permute-start.1 = (bf16[2,17,48,128]{3,2,1,0:T(8,128)(2,1)S(1)}, bf16[2,17,48,128]{3,2,1,0:T(8,128)(2,1)}, u32[]{:S(2)}, u32[]{:S(2)}) collective-permute-start(bf16[2,17,48,128]{3,2,1,0:T(8,128)(2,1)S(1)} %get-tuple-element.38), channel_id=1, source_target_pairs={{0,4},{4,0},{8,12},{12,8},{16,20},{20,16},{24,28},{28,24},{1,5},{5... | collective-permute-start | bytes 1253384 | tf_op jit(solution)/shard_map/ppermute | solution.py:557
  5.2 1.3 %collective-permute-start = (bf16[2,27,48,128]{3,2,1,0:T(8,128)(2,1)}, bf16[2,27,48,128]{3,2,1,0:T(8,128)(2,1)S(1)}, u32[]{:S(2)}, u32[]{:S(2)}) collective-permute-start(bf16[2,27,48,128]{3,2,1,0:T(8,128)(2,1)} %get-tuple-element.37), channel_id=1, source_target_pairs={{4,12},{8,0},{12,20},{16,8},{20,28},{24,16},{5,13},{9,1},{13,21},{... | collective-permute-start | bytes 1990664 | tf_op jit(solution)/shard_map/ppermute | solution.py:558
  6.5 0.0 copy-done.2
  6.5 1.7 %packed.1 = (bf16[2,10,48,128]{3,2,1,0:T(8,128)(2,1)S(1)}, bf16[8,48,48]{2,1,0:T(8,128)(2,1)}, bf16[8,48,48]{2,1,0:T(8,128)(2,1)}) custom-call(bf16[2,48,48,128]{3,2,1,0:T(8,128)(2,1)} %refs_0_.3, bf16[8,2,48,48]{3,2,1,0:T(8,128)(2,1)S(1)} %copy-done.2), custom_call_target="tpu_custom_call" | custom-call | flops 256 | bytes 256 | tf_op jit(solution)/shard_map/packed/pallas_call | solution.py:110
  8.2 2.8 %collective-permute-start.4 = (bf16[8,48,48]{2,1,0:T(8,128)(2,1)}, bf16[8,48,48]{2,1,0:T(8,128)(2,1)S(1)}, u32[]{:S(2)}, u32[]{:S(2)}) collective-permute-start(bf16[8,48,48]{2,1,0:T(8,128)(2,1)} %get-tuple-element.42), channel_id=1, source_target_pairs={{0,4},{4,0},{8,12},{12,8},{16,20},{20,16},{24,28},{28,24},{1,5},{5... | collective-permute-start | bytes 110600 | tf_op jit(solution)/shard_map/ppermute | solution.py:554
  11.0 0.7 collective-permute-start.5
  11.7 4.1 %collective-permute-done.1.refs_3_ = bf16[2,17,48,128]{3,2,1,0:T(8,128)(2,1)} collective-permute-done((bf16[2,17,48,128]{3,2,1,0:T(8,128)(2,1)S(1)}, bf16[2,17,48,128]{3,2,1,0:T(8,128)(2,1)}, u32[]{:S(2)}, u32[]{:S(2)}) %collective-permute-start.1) | collective-permute-done | bytes 417824 | tf_op jit(solution)/shard_map/ppermute | solution.py:557
  15.8 4.0 %collective-permute-start.3 = (bf16[2,17,48,128]{3,2,1,0:T(8,128)(2,1)}, bf16[2,17,48,128]{3,2,1,0:T(8,128)(2,1)S(1)}, u32[]{:S(2)}, u32[]{:S(2)}) collective-permute-start(bf16[2,17,48,128]{3,2,1,0:T(8,128)(2,1)} %collective-permute-done.1.refs_3_), channel_id=1, source_target_pairs={{0,8},{8,16},{12,4},{16,24},{20,12},{28,20},{1,9},{9,17},{13,5},{1... | collective-permute-start | bytes 1253384 | tf_op jit(solution)/shard_map/ppermute | solution.py:563
  19.8 0.1 collective-permute-start.2
  19.9 0.1 broadcast_select_fusion
  19.9 0.3 convolution_bitcast_fusion.gram
  20.2 0.0 collective-permute-done.4.b_x
  20.2 0.0 collective-permute-done.5.b_d
  20.3 0.0 copy-done.1
  20.3 3.0 %partials.1 = (f32[24,128]{1,0:T(8,128)S(1)}, bf16[2,48,24,48]{3,2,1,0:T(8,128)(2,1)S(1)}) custom-call(s32[8]{0:T(128)S(1)} %copy-done.7, bf16[2,48,48,128]{3,2,1,0:T(8,128)(2,1)S(1)} %copy-done.1, bf16[8,2,48,48]{3,2,1,0:T(8,128)(2,1)S(1)} %copy-done.2, bf16[8,48,48]{2,1,0:T(8,128)(2,1)S(1)} %collective-permute-done.4.b_x, ...), custom_call_target="tpu_custom_call" | custom-call | flops 256 | bytes 256 | tf_op jit(solution)/shard_map/partials/pallas_call | solution.py:177
  23.3 2.8 %collective-permute-done.2.refs_4_ = bf16[2,10,48,128]{3,2,1,0:T(8,128)(2,1)} collective-permute-done((bf16[2,10,48,128]{3,2,1,0:T(8,128)(2,1)S(1)}, bf16[2,10,48,128]{3,2,1,0:T(8,128)(2,1)}, u32[]{:S(2)}, u32[]{:S(2)}) %collective-permute-start.2) | collective-permute-done | bytes 245792 | tf_op jit(solution)/shard_map/ppermute | solution.py:564
  26.1 0.9 %collective-permute-done.3.refs_5_.refs_4_ = bf16[2,17,48,128]{3,2,1,0:T(8,128)(2,1)S(1)} collective-permute-done((bf16[2,17,48,128]{3,2,1,0:T(8,128)(2,1)}, bf16[2,17,48,128]{3,2,1,0:T(8,128)(2,1)S(1)}, u32[]{:S(2)}, u32[]{:S(2)}) %collective-permute-start.3) | collective-permute-done | bytes 417824 | tf_op jit(solution)/shard_map/ppermute | solution.py:563
  27.0 0.0 collective-permute-done.refs_2_
  27.0 4.5 %filtered.3.refs_0_ = bf16[4,12,48,128]{3,2,1,0:T(8,128)(2,1)S(1)} custom-call(bf16[2,48,48,128]{3,2,1,0:T(8,128)(2,1)S(1)} %copy-done.1, f32[2,48,48]{2,1,0:T(8,128)S(1)} %copy-done.4, bf16[2,27,48,128]{3,2,1,0:T(8,128)(2,1)S(1)} %collective-permute-done.refs_2_, bf16[2,17,48,128]{3,2,1,0:T(8,128)(2,1)} %collective-permute-done.1.refs_3_, ...), custom_call_target="tpu_custom_call" | custom-call | flops 2949120 | bytes 18432000 | tf_op jit(solution)/shard_map/filtered/pallas_call | solution.py:420
  31.5 1.6 %collective-permute-start.9 = (bf16[4,12,48,128]{3,2,1,0:T(8,128)(2,1)S(1)}, bf16[4,12,48,128]{3,2,1,0:T(8,128)(2,1)}, u32[]{:S(2)}, u32[]{:S(2)}) collective-permute-start(bf16[4,12,48,128]{3,2,1,0:T(8,128)(2,1)S(1)} %filtered.3.refs_0_), channel_id=1, source_target_pairs={{0,2},{1,3},{2,0},{3,1},{4,6},{5,7},{6,4},{7,5},{8,10},{9,11},{10,... | collective-permute-start | bytes 1769480 | tf_op jit(solution)/shard_map/ppermute | solution.py:572
  33.1 5.7 %collective-permute-start.6 = (bf16[2,10,48,128]{3,2,1,0:T(8,128)(2,1)}, bf16[2,10,48,128]{3,2,1,0:T(8,128)(2,1)S(1)}, u32[]{:S(2)}, u32[]{:S(2)}) collective-permute-start(bf16[2,10,48,128]{3,2,1,0:T(8,128)(2,1)} %collective-permute-done.2.refs_4_), channel_id=1, source_target_pairs={{0,8},{8,16},{12,4},{16,24},{20,12},{28,20},{1,9},{9,17},{13,5},{1... | collective-permute-start | bytes 737288 | tf_op jit(solution)/shard_map/ppermute | solution.py:565
  38.8 0.1 collective-permute-start.7
  38.9 3.7 %collective-permute-done.7 = f32[24,128]{1,0:T(8,128)S(1)} collective-permute-done((f32[24,128]{1,0:T(8,128)S(1)}, f32[24,128]{1,0:T(8,128)S(1)}, u32[]{:S(2)}, u32[]{:S(2)}) %collective-permute-start.7) | collective-permute-done | bytes 12320 | tf_op jit(solution)/shard_map/ppermute | solution.py:577
  42.6 0.2 collective-permute-done.6.refs_6_
  42.8 2.4 %collective-permute-start.10 = (f32[24,128]{1,0:T(8,128)S(1)}, f32[24,128]{1,0:T(8,128)S(1)}, u32[]{:S(2)}, u32[]{:S(2)}) collective-permute-start(f32[24,128]{1,0:T(8,128)S(1)} %add.9), channel_id=1, source_target_pairs={{0,8},{4,12},{8,0},{12,4},{16,24},{20,28},{24,16},{28,20},{1,9},{5... | collective-permute-start | bytes 36872 | tf_op jit(solution)/shard_map/ppermute | solution.py:577
  45.2 4.6 %filtered.2 = (bf16[2,12,48,128]{3,2,1,0:T(8,128)(2,1)S(1)}, bf16[2,12,48,128]{3,2,1,0:T(8,128)(2,1)S(1)}) custom-call(bf16[2,48,48,128]{3,2,1,0:T(8,128)(2,1)S(1)} %copy-done.1, f32[2,48,48]{2,1,0:T(8,128)S(1)} %copy-done.4, bf16[2,27,48,128]{3,2,1,0:T(8,128)(2,1)S(1)} %collective-permute-done.refs_2_, ...), custom_call_target="tpu_custom_call" | custom-call | flops 2949120 | bytes 18432000 | tf_op jit(solution)/shard_map/filtered/pallas_call | solution.py:420
  49.9 0.6 collective-permute-start.8
  50.4 0.0 collective-permute-done.10
  50.5 0.0 collective-permute-done.9.refs_2_
  50.5 0.1 collective-permute-start.11
  50.5 0.5 collective-permute-start.12
  51.1 2.7 %collective-permute-start.13 = (f32[24,128]{1,0:T(8,128)S(1)}, f32[24,128]{1,0:T(8,128)S(1)}, u32[]{:S(2)}, u32[]{:S(2)}) collective-permute-start(f32[24,128]{1,0:T(8,128)S(1)} %add.10), channel_id=1, source_target_pairs={{0,16},{4,20},{8,24},{12,28},{16,0},{20,4},{24,8},{28,12},{1,17},{... | collective-permute-start | bytes 36872 | tf_op jit(solution)/shard_map/ppermute | solution.py:577
  53.7 0.3 fusion
  54.1 1.6 %collective-permute-done.13 = f32[24,128]{1,0:T(8,128)S(1)} collective-permute-done((f32[24,128]{1,0:T(8,128)S(1)}, f32[24,128]{1,0:T(8,128)S(1)}, u32[]{:S(2)}, u32[]{:S(2)}) %collective-permute-start.13) | collective-permute-done | bytes 12320 | tf_op jit(solution)/shard_map/ppermute | solution.py:577
  55.7 0.0 collective-permute-done.12.refs_3_
  55.7 0.0 collective-permute-done.11.refs_1_
  55.7 2.0 %rotated.2 = (bf16[2,12,48,128]{3,2,1,0:T(8,128)(2,1)S(1)}, bf16[2,12,48,128]{3,2,1,0:T(8,128)(2,1)S(1)}) custom-call(bf16[4,12,48,128]{3,2,1,0:T(8,128)(2,1)S(1)} %filtered.3.refs_0_, bf16[4,12,48,128]{3,2,1,0:T(8,128)(2,1)S(1)} %collective-permute-done.11.refs_1_, bf16[4,12,48,128]{3,2,1,0:T(8,128)(2,1)} %collective-permute-done.9.refs_2_, ...), custom_call_target="tpu_custom_call" | custom-call | flops 18874368 | bytes 184320 | tf_op jit(solution)/shard_map/rotated/pallas_call | solution.py:466
  57.8 0.0 collective-permute-done.8.refs_2_
  57.8 0.1 collective-permute-start.14
  57.9 0.5 collective-permute-start.16
  58.4 1.5 %collective-permute-start.18 = (bf16[2,12,48,128]{3,2,1,0:T(8,128)(2,1)S(1)}, bf16[2,12,48,128]{3,2,1,0:T(8,128)(2,1)S(1)}, u32[]{:S(2)}, u32[]{:S(2)}) collective-permute-start(bf16[2,12,48,128]{3,2,1,0:T(8,128)(2,1)S(1)} %get-tuple-element.66.a), channel_id=1, source_target_pairs={{0,2},{1,3},{2,0},{3,1},{4,6},{5,7},{6,4},{7,5},{8,10},{9,11},{10,... | collective-permute-start | bytes 884744 | tf_op jit(solution)/shard_map/ppermute | solution.py:603
  59.9 1.4 %collective-permute-start.19 = (bf16[2,12,48,128]{3,2,1,0:T(8,128)(2,1)S(1)}, bf16[2,12,48,128]{3,2,1,0:T(8,128)(2,1)S(1)}, u32[]{:S(2)}, u32[]{:S(2)}) collective-permute-start(bf16[2,12,48,128]{3,2,1,0:T(8,128)(2,1)S(1)} %get-tuple-element.57), channel_id=1, source_target_pairs={{0,4},{4,0},{8,12},{12,8},{16,20},{20,16},{24,28},{28,24},{1,5},{5... | collective-permute-start | bytes 884744 | tf_op jit(solution)/shard_map/ppermute | solution.py:601
  61.3 0.1 broadcast_in_dim.22.strength
  61.3 0.1 coefficients.1
  61.5 0.0 collective-permute-start.15
  61.5 1.2 %collective-permute-done.15 = bf16[16,128]{1,0:T(8,128)(2,1)S(1)} collective-permute-done((bf16[16,128]{1,0:T(8,128)(2,1)S(1)}, bf16[16,128]{1,0:T(8,128)(2,1)S(1)}, u32[]{:S(2)}, u32[]{:S(2)}) %collective-permute-start.15) | collective-permute-done | bytes 4128 | tf_op jit(solution)/shard_map/ppermute | solution.py:606
  62.7 0.2 collective-permute-start.21
  62.8 0.0 collective-permute-done.14.refs_3_
  62.8 0.0 collective-permute-done.16.refs_1_
  62.8 0.6 rotated.3
  63.5 0.7 collective-permute-start.20
  64.2 0.5 collective-permute-start.17
  64.7 2.7 %collective-permute-done.18.c = bf16[2,12,48,128]{3,2,1,0:T(8,128)(2,1)S(1)} collective-permute-done((bf16[2,12,48,128]{3,2,1,0:T(8,128)(2,1)S(1)}, bf16[2,12,48,128]{3,2,1,0:T(8,128)(2,1)S(1)}, u32[]{:S(2)}, u32[]{:S(2)}) %collective-permute-start.18) | collective-permute-done | bytes 294944 | tf_op jit(solution)/shard_map/ppermute | solution.py:603
  67.4 2.3 %collective-permute-done.19.got1 = bf16[2,12,48,128]{3,2,1,0:T(8,128)(2,1)S(1)} collective-permute-done((bf16[2,12,48,128]{3,2,1,0:T(8,128)(2,1)S(1)}, bf16[2,12,48,128]{3,2,1,0:T(8,128)(2,1)S(1)}, u32[]{:S(2)}, u32[]{:S(2)}) %collective-permute-start.19) | collective-permute-done | bytes 294944 | tf_op jit(solution)/shard_map/ppermute | solution.py:601
  69.8 0.0 collective-permute-start.22
  69.8 0.0 collective-permute-done.17
  69.8 1.9 %nonlocal.1.term = f32[2,48,48,128]{3,2,1,0:T(8,128)S(1)} custom-call(bf16[16,128]{1,0:T(8,128)(2,1)S(1)} %get-tuple-element.72.a, bf16[16,128]{1,0:T(8,128)(2,1)S(1)} %get-tuple-element.71.b, bf16[16,128]{1,0:T(8,128)(2,1)S(1)} %get-tuple-element.70.c, bf16[16,128]{1,0:T(8,128)(2,1)S(1)} %get-tuple-element.69.d, bf16[4,128,128]{2,1,0:T(8,128)(2,1)S(1)} %copy.18.refs_4_.q, ...), custom_call_target="tpu_custom_call" | custom-call | flops 256 | bytes 256 | tf_op jit(solution)/shard_map/nonlocal/pallas_call | solution.py:252
  71.7 0.0 collective-permute-done.21.b
  71.7 3.2 %collective-permute-done.20.got2 = bf16[2,12,48,128]{3,2,1,0:T(8,128)(2,1)S(1)} collective-permute-done((bf16[2,12,48,128]{3,2,1,0:T(8,128)(2,1)S(1)}, bf16[2,12,48,128]{3,2,1,0:T(8,128)(2,1)S(1)}, u32[]{:S(2)}, u32[]{:S(2)}) %collective-permute-start.20) | collective-permute-done | bytes 294944 | tf_op jit(solution)/shard_map/ppermute | solution.py:609
  74.9 0.0 collective-permute-done.22.d
  74.9 1.8 %assembled.1 = bf16[2,48,48,128]{3,2,1,0:T(8,128)(2,1)} custom-call(f32[2,48,48,128]{3,2,1,0:T(8,128)S(1)} %nonlocal.1.term, bf16[2,12,48,128]{3,2,1,0:T(8,128)(2,1)S(1)} %get-tuple-element.65.keep1, bf16[2,12,48,128]{3,2,1,0:T(8,128)(2,1)S(1)} %collective-permute-done.19.got1, bf16[2,12,48,128]{3,2,1,0:T(8,128)(2,1)S(1)} %collective-permute-done.20.got2, ...), custom_call_target="tpu_custom_call" | custom-call | flops 256 | bytes 256 | tf_op jit(solution)/shard_map/assembled/pallas_call | solution.py:513
  (29 shorter events, 0.1 us)
Async XLA Ops:
  0.0 53.7 %copy-start = (bf16[12,128,128]{2,1,0:T(8,128)(2,1)S(1)}, bf16[12,128,128]{2,1,0:T(8,128)(2,1)}, u32[]{:S(2)}) copy-start(bf16[12,128,128]{2,1,0:T(8,128)(2,1)} %param.13) | copy-start | bytes 1179652
  0.0 6.5 %copy-start.2 = (bf16[8,2,48,48]{3,2,1,0:T(8,128)(2,1)S(1)}, bf16[8,2,48,48]{3,2,1,0:T(8,128)(2,1)}, u32[]{:S(2)}) copy-start(bf16[8,2,48,48]{3,2,1,0:T(8,128)(2,1)} %beta.3) | copy-start | bytes 221188
  0.0 19.8 %copy-start.7 = (s32[8]{0:T(128)S(1)}, s32[8]{0:T(128)}, u32[]{:S(2)}) copy-start(s32[8]{0:T(128)} %atoms.1) | copy-start | bytes 100
  2.2 18.1 %copy-start.1 = (bf16[2,48,48,128]{3,2,1,0:T(8,128)(2,1)S(1)}, bf16[2,48,48,128]{3,2,1,0:T(8,128)(2,1)}, u32[]{:S(2)}) copy-start(bf16[2,48,48,128]{3,2,1,0:T(8,128)(2,1)} %refs_0_.3) | copy-start | bytes 3538948
  2.2 18.1 %copy-start.4 = (f32[2,48,48]{2,1,0:T(8,128)S(1)}, f32[2,48,48]{2,1,0:T(8,128)}, u32[]{:S(2)}) copy-start(f32[2,48,48]{2,1,0:T(8,128)} %refs_1_.3) | copy-start | bytes 55300
  2.2 13.6 %collective-permute-start.1 = (bf16[2,17,48,128]{3,2,1,0:T(8,128)(2,1)S(1)}, bf16[2,17,48,128]{3,2,1,0:T(8,128)(2,1)}, u32[]{:S(2)}, u32[]{:S(2)}) collective-permute-start(bf16[2,17,48,128]{3,2,1,0:T(8,128)(2,1)S(1)} %get-tuple-element.38), channel_id=1, source_target_pairs={{0,4},{4,0},{8,12},{12,8},{16,20},{20,16},{24,28},{28,24},{1,5},{5... | collective-permute-start | bytes 1253384 | tf_op jit(solution)/shard_map/ppermute | solution.py:557
  5.2 21.8 %collective-permute-start = (bf16[2,27,48,128]{3,2,1,0:T(8,128)(2,1)}, bf16[2,27,48,128]{3,2,1,0:T(8,128)(2,1)S(1)}, u32[]{:S(2)}, u32[]{:S(2)}) collective-permute-start(bf16[2,27,48,128]{3,2,1,0:T(8,128)(2,1)} %get-tuple-element.37), channel_id=1, source_target_pairs={{4,12},{8,0},{12,20},{16,8},{20,28},{24,16},{5,13},{9,1},{13,21},{... | collective-permute-start | bytes 1990664 | tf_op jit(solution)/shard_map/ppermute | solution.py:558
  8.2 12.1 %collective-permute-start.4 = (bf16[8,48,48]{2,1,0:T(8,128)(2,1)}, bf16[8,48,48]{2,1,0:T(8,128)(2,1)S(1)}, u32[]{:S(2)}, u32[]{:S(2)}) collective-permute-start(bf16[8,48,48]{2,1,0:T(8,128)(2,1)} %get-tuple-element.42), channel_id=1, source_target_pairs={{0,4},{4,0},{8,12},{12,8},{16,20},{20,16},{24,28},{28,24},{1,5},{5... | collective-permute-start | bytes 110600 | tf_op jit(solution)/shard_map/ppermute | solution.py:554
  11.0 9.3 %collective-permute-start.5 = (bf16[8,48,48]{2,1,0:T(8,128)(2,1)}, bf16[8,48,48]{2,1,0:T(8,128)(2,1)S(1)}, u32[]{:S(2)}, u32[]{:S(2)}) collective-permute-start(bf16[8,48,48]{2,1,0:T(8,128)(2,1)} %get-tuple-element.43), channel_id=1, source_target_pairs={{4,8},{8,4},{12,16},{16,12},{20,24},{24,20},{5,9},{9,5},{13,17},{1... | collective-permute-start | bytes 110600 | tf_op jit(solution)/shard_map/ppermute | solution.py:556
  15.8 11.2 %collective-permute-start.3 = (bf16[2,17,48,128]{3,2,1,0:T(8,128)(2,1)}, bf16[2,17,48,128]{3,2,1,0:T(8,128)(2,1)S(1)}, u32[]{:S(2)}, u32[]{:S(2)}) collective-permute-start(bf16[2,17,48,128]{3,2,1,0:T(8,128)(2,1)} %collective-permute-done.1.refs_3_), channel_id=1, source_target_pairs={{0,8},{8,16},{12,4},{16,24},{20,12},{28,20},{1,9},{9,17},{13,5},{1... | collective-permute-start | bytes 1253384 | tf_op jit(solution)/shard_map/ppermute | solution.py:563
  19.8 6.4 %collective-permute-start.2 = (bf16[2,10,48,128]{3,2,1,0:T(8,128)(2,1)S(1)}, bf16[2,10,48,128]{3,2,1,0:T(8,128)(2,1)}, u32[]{:S(2)}, u32[]{:S(2)}) collective-permute-start(bf16[2,10,48,128]{3,2,1,0:T(8,128)(2,1)S(1)} %get-tuple-element.41), channel_id=1, source_target_pairs={{0,4},{4,0},{8,12},{12,8},{16,20},{20,16},{24,28},{28,24},{1,5},{5... | collective-permute-start | bytes 737288 | tf_op jit(solution)/shard_map/ppermute | solution.py:564
  23.3 8.2 %copy-start.5 = (bf16[2,48,24,48]{3,2,1,0:T(8,128)(2,1)}, bf16[2,48,24,48]{3,2,1,0:T(8,128)(2,1)S(1)}, u32[]{:S(2)}) copy-start(bf16[2,48,24,48]{3,2,1,0:T(8,128)(2,1)S(1)} %get-tuple-element.64.weights) | copy-start | bytes 663556
  27.0 4.5 %copy-start.3 = (bf16[2,17,48,128]{3,2,1,0:T(8,128)(2,1)}, bf16[2,17,48,128]{3,2,1,0:T(8,128)(2,1)S(1)}, u32[]{:S(2)}) copy-start(bf16[2,17,48,128]{3,2,1,0:T(8,128)(2,1)S(1)} %collective-permute-done.3.refs_5_.refs_4_) | copy-start | bytes 1253380
  31.5 18.9 %collective-permute-start.9 = (bf16[4,12,48,128]{3,2,1,0:T(8,128)(2,1)S(1)}, bf16[4,12,48,128]{3,2,1,0:T(8,128)(2,1)}, u32[]{:S(2)}, u32[]{:S(2)}) collective-permute-start(bf16[4,12,48,128]{3,2,1,0:T(8,128)(2,1)S(1)} %filtered.3.refs_0_), channel_id=1, source_target_pairs={{0,2},{1,3},{2,0},{3,1},{4,6},{5,7},{6,4},{7,5},{8,10},{9,11},{10,... | collective-permute-start | bytes 1769480 | tf_op jit(solution)/shard_map/ppermute | solution.py:572
  33.1 9.7 %collective-permute-start.6 = (bf16[2,10,48,128]{3,2,1,0:T(8,128)(2,1)}, bf16[2,10,48,128]{3,2,1,0:T(8,128)(2,1)S(1)}, u32[]{:S(2)}, u32[]{:S(2)}) collective-permute-start(bf16[2,10,48,128]{3,2,1,0:T(8,128)(2,1)} %collective-permute-done.2.refs_4_), channel_id=1, source_target_pairs={{0,8},{8,16},{12,4},{16,24},{20,12},{28,20},{1,9},{9,17},{13,5},{1... | collective-permute-start | bytes 737288 | tf_op jit(solution)/shard_map/ppermute | solution.py:565
  38.8 3.8 %collective-permute-start.7 = (f32[24,128]{1,0:T(8,128)S(1)}, f32[24,128]{1,0:T(8,128)S(1)}, u32[]{:S(2)}, u32[]{:S(2)}) collective-permute-start(f32[24,128]{1,0:T(8,128)S(1)} %get-tuple-element.46), channel_id=1, source_target_pairs={{0,4},{4,0},{8,12},{12,8},{16,20},{20,16},{24,28},{28,24},{1,5},{5... | collective-permute-start | bytes 36872 | tf_op jit(solution)/shard_map/ppermute | solution.py:577
  42.8 2.4 %copy-start.8 = (bf16[2,10,48,128]{3,2,1,0:T(8,128)(2,1)}, bf16[2,10,48,128]{3,2,1,0:T(8,128)(2,1)S(1)}, u32[]{:S(2)}) copy-start(bf16[2,10,48,128]{3,2,1,0:T(8,128)(2,1)S(1)} %collective-permute-done.6.refs_6_) | copy-start | bytes 737284
  42.8 7.6 %collective-permute-start.10 = (f32[24,128]{1,0:T(8,128)S(1)}, f32[24,128]{1,0:T(8,128)S(1)}, u32[]{:S(2)}, u32[]{:S(2)}) collective-permute-start(f32[24,128]{1,0:T(8,128)S(1)} %add.9), channel_id=1, source_target_pairs={{0,8},{4,12},{8,0},{12,4},{16,24},{20,28},{24,16},{28,20},{1,9},{5... | collective-permute-start | bytes 36872 | tf_op jit(solution)/shard_map/ppermute | solution.py:577
  45.2 5.8 %copy-start.10 = (s32[12,2]{0,1:T(2,128)S(1)}, s32[12,2]{0,1:T(2,128)}, u32[]{:S(2)}) copy-start(s32[12,2]{0,1:T(2,128)} %param.12) | copy-start | bytes 292
  49.9 7.9 %collective-permute-start.8 = (bf16[2,12,48,128]{3,2,1,0:T(8,128)(2,1)S(1)}, bf16[2,12,48,128]{3,2,1,0:T(8,128)(2,1)S(1)}, u32[]{:S(2)}, u32[]{:S(2)}) collective-permute-start(bf16[2,12,48,128]{3,2,1,0:T(8,128)(2,1)S(1)} %get-tuple-element.49.refs_0_), channel_id=1, source_target_pairs={{0,2},{1,3},{2,0},{3,1},{4,6},{5,7},{6,4},{7,5},{8,10},{9,11},{10,... | collective-permute-start | bytes 884744 | tf_op jit(solution)/shard_map/ppermute | solution.py:591
  50.5 5.3 %collective-permute-start.11 = (bf16[4,12,48,128]{3,2,1,0:T(8,128)(2,1)S(1)}, bf16[4,12,48,128]{3,2,1,0:T(8,128)(2,1)S(1)}, u32[]{:S(2)}, u32[]{:S(2)}) collective-permute-start(bf16[4,12,48,128]{3,2,1,0:T(8,128)(2,1)S(1)} %filtered.3.refs_0_), channel_id=1, source_target_pairs={{0,1},{1,0},{2,3},{3,2},{4,5},{5,4},{6,7},{7,6},{8,9},{9,8},{10,11... | collective-permute-start | bytes 1769480 | tf_op jit(solution)/shard_map/ppermute | solution.py:595
  50.5 5.2 %collective-permute-start.12 = (bf16[4,12,48,128]{3,2,1,0:T(8,128)(2,1)}, bf16[4,12,48,128]{3,2,1,0:T(8,128)(2,1)S(1)}, u32[]{:S(2)}, u32[]{:S(2)}) collective-permute-start(bf16[4,12,48,128]{3,2,1,0:T(8,128)(2,1)} %collective-permute-done.9.refs_2_), channel_id=1, source_target_pairs={{0,1},{1,0},{2,3},{3,2},{4,5},{5,4},{6,7},{7,6},{8,9},{9,8},{10,11... | collective-permute-start | bytes 1769480 | tf_op jit(solution)/shard_map/ppermute | solution.py:596
  51.1 4.7 %collective-permute-start.13 = (f32[24,128]{1,0:T(8,128)S(1)}, f32[24,128]{1,0:T(8,128)S(1)}, u32[]{:S(2)}, u32[]{:S(2)}) collective-permute-start(f32[24,128]{1,0:T(8,128)S(1)} %add.10), channel_id=1, source_target_pairs={{0,16},{4,20},{8,24},{12,28},{16,0},{20,4},{24,8},{28,12},{1,17},{... | collective-permute-start | bytes 36872 | tf_op jit(solution)/shard_map/ppermute | solution.py:577
  55.7 5.5 %copy-start.9 = (f32[8]{0:T(128)S(1)}, f32[8]{0:T(128)}, u32[]{:S(2)}) copy-start(f32[8]{0:T(128)} %param.10) | copy-start | bytes 100
  57.8 12.0 %copy-start.6 = (bf16[2,48,24,48]{3,2,1,0:T(8,128)(2,1)S(1)}, bf16[2,48,24,48]{3,2,1,0:T(8,128)(2,1)}, u32[]{:S(2)}) copy-start(bf16[2,48,24,48]{3,2,1,0:T(8,128)(2,1)} %copy-done.5) | copy-start | bytes 663556
  57.8 5.1 %collective-permute-start.14 = (bf16[2,12,48,128]{3,2,1,0:T(8,128)(2,1)S(1)}, bf16[2,12,48,128]{3,2,1,0:T(8,128)(2,1)S(1)}, u32[]{:S(2)}, u32[]{:S(2)}) collective-permute-start(bf16[2,12,48,128]{3,2,1,0:T(8,128)(2,1)S(1)} %collective-permute-done.8.refs_2_), channel_id=1, source_target_pairs={{0,1},{1,0},{2,3},{3,2},{4,5},{5,4},{6,7},{7,6},{8,9},{9,8},{10,11... | collective-permute-start | bytes 884744 | tf_op jit(solution)/shard_map/ppermute | solution.py:604
  57.9 5.0 %collective-permute-start.16 = (bf16[2,12,48,128]{3,2,1,0:T(8,128)(2,1)S(1)}, bf16[2,12,48,128]{3,2,1,0:T(8,128)(2,1)S(1)}, u32[]{:S(2)}, u32[]{:S(2)}) collective-permute-start(bf16[2,12,48,128]{3,2,1,0:T(8,128)(2,1)S(1)} %get-tuple-element.49.refs_0_), channel_id=1, source_target_pairs={{0,1},{1,0},{2,3},{3,2},{4,5},{5,4},{6,7},{7,6},{8,9},{9,8},{10,11... | collective-permute-start | bytes 884744 | tf_op jit(solution)/shard_map/ppermute | solution.py:589
  58.4 9.1 %collective-permute-start.18 = (bf16[2,12,48,128]{3,2,1,0:T(8,128)(2,1)S(1)}, bf16[2,12,48,128]{3,2,1,0:T(8,128)(2,1)S(1)}, u32[]{:S(2)}, u32[]{:S(2)}) collective-permute-start(bf16[2,12,48,128]{3,2,1,0:T(8,128)(2,1)S(1)} %get-tuple-element.66.a), channel_id=1, source_target_pairs={{0,2},{1,3},{2,0},{3,1},{4,6},{5,7},{6,4},{7,5},{8,10},{9,11},{10,... | collective-permute-start | bytes 884744 | tf_op jit(solution)/shard_map/ppermute | solution.py:603
  59.9 9.9 %collective-permute-start.19 = (bf16[2,12,48,128]{3,2,1,0:T(8,128)(2,1)S(1)}, bf16[2,12,48,128]{3,2,1,0:T(8,128)(2,1)S(1)}, u32[]{:S(2)}, u32[]{:S(2)}) collective-permute-start(bf16[2,12,48,128]{3,2,1,0:T(8,128)(2,1)S(1)} %get-tuple-element.57), channel_id=1, source_target_pairs={{0,4},{4,0},{8,12},{12,8},{16,20},{20,16},{24,28},{28,24},{1,5},{5... | collective-permute-start | bytes 884744 | tf_op jit(solution)/shard_map/ppermute | solution.py:601
  61.5 1.2 %collective-permute-start.15 = (bf16[16,128]{1,0:T(8,128)(2,1)S(1)}, bf16[16,128]{1,0:T(8,128)(2,1)S(1)}, u32[]{:S(2)}, u32[]{:S(2)}) collective-permute-start(bf16[16,128]{1,0:T(8,128)(2,1)S(1)} %coefficients.1), channel_id=1, source_target_pairs={{0,1},{1,0},{2,3},{3,2},{4,5},{5,4},{6,7},{7,6},{8,9},{9,8},{10,11... | collective-permute-start | bytes 12296 | tf_op jit(solution)/shard_map/ppermute | solution.py:606
  62.7 9.0 %collective-permute-start.21 = (bf16[2,12,48,128]{3,2,1,0:T(8,128)(2,1)S(1)}, bf16[2,12,48,128]{3,2,1,0:T(8,128)(2,1)S(1)}, u32[]{:S(2)}, u32[]{:S(2)}) collective-permute-start(bf16[2,12,48,128]{3,2,1,0:T(8,128)(2,1)S(1)} %get-tuple-element.66.a), channel_id=1, source_target_pairs={{0,1},{1,0},{2,3},{3,2},{4,5},{5,4},{6,7},{7,6},{8,9},{9,8},{10,11... | collective-permute-start | bytes 884744 | tf_op jit(solution)/shard_map/ppermute | solution.py:590
  63.5 11.4 %collective-permute-start.20 = (bf16[2,12,48,128]{3,2,1,0:T(8,128)(2,1)S(1)}, bf16[2,12,48,128]{3,2,1,0:T(8,128)(2,1)S(1)}, u32[]{:S(2)}, u32[]{:S(2)}) collective-permute-start(bf16[2,12,48,128]{3,2,1,0:T(8,128)(2,1)S(1)} %rotated.3), channel_id=1, source_target_pairs={{0,4},{4,0},{8,12},{12,8},{16,20},{20,16},{24,28},{28,24},{1,5},{5... | collective-permute-start | bytes 884744 | tf_op jit(solution)/shard_map/ppermute | solution.py:609
  64.2 5.6 %collective-permute-start.17 = (bf16[32,128]{1,0:T(8,128)(2,1)S(1)}, bf16[32,128]{1,0:T(8,128)(2,1)S(1)}, u32[]{:S(2)}, u32[]{:S(2)}) collective-permute-start(bf16[32,128]{1,0:T(8,128)(2,1)S(1)} %pad_maximum_fusion), channel_id=1, source_target_pairs={{0,2},{1,3},{2,0},{3,1},{4,6},{5,7},{6,4},{7,5},{8,10},{9,11},{10,... | collective-permute-start | bytes 24584 | tf_op jit(solution)/shard_map/ppermute | solution.py:611
  69.8 5.1 %collective-permute-start.22 = (bf16[2,12,48,128]{3,2,1,0:T(8,128)(2,1)S(1)}, bf16[2,12,48,128]{3,2,1,0:T(8,128)(2,1)S(1)}, u32[]{:S(2)}, u32[]{:S(2)}) collective-permute-start(bf16[2,12,48,128]{3,2,1,0:T(8,128)(2,1)S(1)} %collective-permute-done.18.c), channel_id=1, source_target_pairs={{0,1},{1,0},{2,3},{3,2},{4,5},{5,4},{6,7},{7,6},{8,9},{9,8},{10,11... | collective-permute-start | bytes 884744 | tf_op jit(solution)/shard_map/ppermute | solution.py:615

commit v18 on v17

--- a/solution.py
+++ b/solution.py
@@ -307,10 +307,9 @@
 
     def fill(c, block):
         lines[c - 1] = block
-        for kind in range(2):
-            even, odd = (lines[c - 1, pl.ds(k, half, stride=2)] for k in range(2))
-            lanes = slice(64 * kind, 64 * kind + width)
-            diagonals[c - 1, kind] = jnp.concatenate([even[:, lanes], odd[:, lanes]], axis=1)
+        even, odd = (lines[c - 1, pl.ds(k, half, stride=2)] for k in range(2))
+        whole = [a[:, :width] + a[:, 64 : 64 + width] for a in (even, odd)]
+        diagonals[c - 1] = jnp.concatenate(whole, axis=1)
 
     for c in (2, 3):
         fill(c, potential_block(p_own[(c % 2) ^ x]))
@@ -328,13 +327,8 @@
     diagonal = i == lax.broadcasted_iota(jnp.int32, (cells, cells), 1)
 
     def local(c, p):
-        at = base // 2 + p
-        hi = diagonals[c - 1, 0, pl.ds(at, 1)]
-        lo = diagonals[c - 1, 1, pl.ds(at, 1)]
-        return (
-            jnp.where(diagonal, hi, here).astype(BF16),
-            jnp.where(diagonal, lo, 0.0).astype(BF16),
-        )
+        u = diagonals[c - 1, pl.ds(base // 2 + p, 1)]
+        return jnp.where(diagonal, u, here).astype(BF16)
 
     def rows_of(c, w, n):
         plane = (c % 2) ^ x
@@ -343,9 +337,8 @@
         ref = zf if c < 2 else (xr if c < 6 else zo)
         return ref[plane, pl.ds(w, n)]
 
-    def applied(pair, outer, zs, matrices):
-        near = jnp.dot(matrices[0], pair, preferred_element_type=F32)
-        near = near + jnp.dot(matrices[1], pair, preferred_element_type=F32)
+    def applied(pair, outer, zs, matrix):
+        near = jnp.dot(matrix, pair, preferred_element_type=F32)
         return near - 0.125 * (outer + zs)
 
     def step1(j, carry):
@@ -407,7 +400,7 @@
     scratch = [
         pltpu.VMEM((6, rows + 4, width, orbs), BF16),
         pltpu.VMEM((6, width, orbs), F32),
-        pltpu.VMEM((6, 2, own.shape[1] // 2, 2 * width), F32),
+        pltpu.VMEM((6, own.shape[1] // 2, 2 * width), F32),
     ]
     window = own.shape[1] // 2 + 2 if parts > 1 else xrs[0].shape[1] - 1
     scratch += [pltpu.VMEM((planes, window, width, orbs), BF16)] * 2
@@ -533,7 +526,7 @@
     x = lax.rem(place, 2)
     half = width_x // 2
     window = half + 2
-    rows1 = half // 4 * 2
+    rows1 = half * 7 // 24 * 2
     rows2 = half - rows1
     early = rows1 + 4
 

time: 77 us -> 75 us (0.974)
  Pallas kernels: 22.5 us -> 21.4 us
  waiting for transfers between devices: 22.8 us -> 22 us
    ppermute x1, waiting for transfers between devices: 2.34 us -> 0.01 us  [shards(): got1 = lax.ppermute(give1, 'space', swap)]
    ppermute x1, waiting for transfers between devices: 0.86 us -> 2.43 us  [shards(): zf1 = lax.ppermute(xr1, 'space', other_way)]
    ppermute x1, starting transfers between devices: 5.72 us -> 4.28 us  [shards(): zf2 = lax.ppermute(xr2, 'space', other_way)]
    ppermute x1, waiting for transfers between devices: 4.12 us -> 5.24 us  [shards(): xr1 = lax.ppermute(to_x, 'space', swap)]
    ppermute x1, waiting for transfers between devices: 3.18 us -> 2.2 us  [shards(): got2 = lax.ppermute(give2, 'space', swap)]
    pallas_call x2, Pallas kernels: 9.13 us -> 8.16 us  [filtered(): pl.pallas_call(functools.partial(filter_kernel, slabs, start, parts, join...]
    ppermute x1, waiting for transfers between devices: 2.73 us -> 3.55 us  [shards(): yk = lax.ppermute(keep_y, 'orb', across)]
    ppermute x3, starting transfers between devices: 5.11 us -> 5.91 us  [added(): return values + lax.ppermute(values, 'space', pairs)]
  transfers between devices with their start and end apart: 23 -> 23, of which waited for: 10 -> 9; matrix products, arithmetic and copies ran while one was open for 1% -> 1% of each run, Pallas kernels for 18% -> 18%
where the time goes in v18:
time: 75 us; the launch traced here: 74.7 us
  starting transfers between devices  30.1 us (40%)
  waiting for transfers between devices  22 us (29%)
  Pallas kernels  21.4 us (29%)
    pallas_call x2, Pallas kernels, filtered(): pl.pallas_call(functools.partial(filter_kernel, slabs, start, parts, join...  8.16 us
    ppermute x3, starting transfers between devices, added(): return values + lax.ppermute(values, 'space', pairs)  5.91 us
    ppermute x1, waiting for transfers between devices, shards(): xr1 = lax.ppermute(to_x, 'space', swap)  5.24 us
    ppermute x3, waiting for transfers between devices, added(): return values + lax.ppermute(values, 'space', pairs)  4.98 us
    ppermute x1, starting transfers between devices, shards(): zf2 = lax.ppermute(xr2, 'space', other_way)  4.28 us
    ppermute x1, starting transfers between devices, shards(): zf1 = lax.ppermute(xr1, 'space', other_way)  3.97 us
    ppermute x1, waiting for transfers between devices, shards(): yk = lax.ppermute(keep_y, 'orb', across)  3.55 us
    pallas_call x1, Pallas kernels, partials(): pl.pallas_call(functools.partial(partial_kernel, count), out_shape=(jax.S...  3.04 us
  transfers between devices with their start and end apart: 23, of which 9 were waited for; matrix products, arithmetic and copies ran while one was open for 1% of the time, Pallas kernels for 18%

profile of v18, /device:TPU:0, one launch (start us, length us, event | category | flops | bytes accessed | tf_op | source)
XLA Modules:
  0.0 74.7 jit_solution(7148489078194611879)
XLA Ops:
  0.0 2.2 %prepared.1 = (bf16[2,19,48,128]{3,2,1,0:T(8,128)(2,1)S(1)}, bf16[2,27,48,128]{3,2,1,0:T(8,128)(2,1)}) custom-call(bf16[2,48,48,128]{3,2,1,0:T(8,128)(2,1)} %refs_0_.3, f32[2,48,48]{2,1,0:T(8,128)} %refs_1_.3), custom_call_target="tpu_custom_call" | custom-call | flops 256 | bytes 256 | tf_op jit(solution)/shard_map/prepared/pallas_call | solution.py:81
  2.2 0.0 copy-start.1
  2.2 0.0 copy-start.4
  2.2 3.0 %collective-permute-start.1 = (bf16[2,19,48,128]{3,2,1,0:T(8,128)(2,1)S(1)}, bf16[2,19,48,128]{3,2,1,0:T(8,128)(2,1)}, u32[]{:S(2)}, u32[]{:S(2)}) collective-permute-start(bf16[2,19,48,128]{3,2,1,0:T(8,128)(2,1)S(1)} %get-tuple-element.38), channel_id=1, source_target_pairs={{0,4},{4,0},{8,12},{12,8},{16,20},{20,16},{24,28},{28,24},{1,5},{5... | collective-permute-start | bytes 1400840 | tf_op jit(solution)/shard_map/ppermute | solution.py:550
  5.2 1.3 %collective-permute-start = (bf16[2,27,48,128]{3,2,1,0:T(8,128)(2,1)}, bf16[2,27,48,128]{3,2,1,0:T(8,128)(2,1)S(1)}, u32[]{:S(2)}, u32[]{:S(2)}) collective-permute-start(bf16[2,27,48,128]{3,2,1,0:T(8,128)(2,1)} %get-tuple-element.37), channel_id=1, source_target_pairs={{4,12},{8,0},{12,20},{16,8},{20,28},{24,16},{5,13},{9,1},{13,21},{... | collective-permute-start | bytes 1990664 | tf_op jit(solution)/shard_map/ppermute | solution.py:551
  6.5 0.0 copy-done.3
  6.5 1.6 %packed.1 = (bf16[2,8,48,128]{3,2,1,0:T(8,128)(2,1)S(1)}, bf16[8,48,48]{2,1,0:T(8,128)(2,1)S(1)}, bf16[8,48,48]{2,1,0:T(8,128)(2,1)}) custom-call(bf16[2,48,48,128]{3,2,1,0:T(8,128)(2,1)} %refs_0_.3, bf16[8,2,48,48]{3,2,1,0:T(8,128)(2,1)S(1)} %copy-done.3), custom_call_target="tpu_custom_call" | custom-call | flops 256 | bytes 256 | tf_op jit(solution)/shard_map/packed/pallas_call | solution.py:110
  8.1 2.8 %collective-permute-start.4 = (bf16[8,48,48]{2,1,0:T(8,128)(2,1)}, bf16[8,48,48]{2,1,0:T(8,128)(2,1)S(1)}, u32[]{:S(2)}, u32[]{:S(2)}) collective-permute-start(bf16[8,48,48]{2,1,0:T(8,128)(2,1)} %get-tuple-element.42), channel_id=1, source_target_pairs={{0,4},{4,0},{8,12},{12,8},{16,20},{20,16},{24,28},{28,24},{1,5},{5... | collective-permute-start | bytes 110600 | tf_op jit(solution)/shard_map/ppermute | solution.py:547
  10.9 0.7 collective-permute-start.5
  11.6 5.2 %collective-permute-done.1.refs_3_ = bf16[2,19,48,128]{3,2,1,0:T(8,128)(2,1)} collective-permute-done((bf16[2,19,48,128]{3,2,1,0:T(8,128)(2,1)S(1)}, bf16[2,19,48,128]{3,2,1,0:T(8,128)(2,1)}, u32[]{:S(2)}, u32[]{:S(2)}) %collective-permute-start.1) | collective-permute-done | bytes 466976 | tf_op jit(solution)/shard_map/ppermute | solution.py:550
  16.8 4.0 %collective-permute-start.3 = (bf16[2,19,48,128]{3,2,1,0:T(8,128)(2,1)}, bf16[2,19,48,128]{3,2,1,0:T(8,128)(2,1)S(1)}, u32[]{:S(2)}, u32[]{:S(2)}) collective-permute-start(bf16[2,19,48,128]{3,2,1,0:T(8,128)(2,1)} %collective-permute-done.1.refs_3_), channel_id=1, source_target_pairs={{0,8},{8,16},{12,4},{16,24},{20,12},{28,20},{1,9},{9,17},{13,5},{1... | collective-permute-start | bytes 1400840 | tf_op jit(solution)/shard_map/ppermute | solution.py:556
  20.8 0.1 collective-permute-start.2
  20.9 0.1 broadcast_select_fusion
  21.0 0.3 convolution_bitcast_fusion.gram
  21.3 0.0 collective-permute-done.4.b_x
  21.3 0.0 collective-permute-done.5.b_d
  21.3 0.0 copy-done.1
  21.3 3.0 %partials.1 = (f32[24,128]{1,0:T(8,128)S(1)}, bf16[2,48,24,48]{3,2,1,0:T(8,128)(2,1)S(1)}) custom-call(s32[8]{0:T(128)S(1)} %copy-done.7, bf16[2,48,48,128]{3,2,1,0:T(8,128)(2,1)S(1)} %copy-done.1, bf16[8,2,48,48]{3,2,1,0:T(8,128)(2,1)S(1)} %copy-done.3, bf16[8,48,48]{2,1,0:T(8,128)(2,1)S(1)} %collective-permute-done.4.b_x, ...), custom_call_target="tpu_custom_call" | custom-call | flops 256 | bytes 256 | tf_op jit(solution)/shard_map/partials/pallas_call | solution.py:177
  24.4 2.3 %collective-permute-done.2.refs_4_ = bf16[2,8,48,128]{3,2,1,0:T(8,128)(2,1)} collective-permute-done((bf16[2,8,48,128]{3,2,1,0:T(8,128)(2,1)S(1)}, bf16[2,8,48,128]{3,2,1,0:T(8,128)(2,1)}, u32[]{:S(2)}, u32[]{:S(2)}) %collective-permute-start.2) | collective-permute-done | bytes 196640 | tf_op jit(solution)/shard_map/ppermute | solution.py:557
  26.7 2.4 %collective-permute-done.3.refs_5_.refs_4_ = bf16[2,19,48,128]{3,2,1,0:T(8,128)(2,1)S(1)} collective-permute-done((bf16[2,19,48,128]{3,2,1,0:T(8,128)(2,1)}, bf16[2,19,48,128]{3,2,1,0:T(8,128)(2,1)S(1)}, u32[]{:S(2)}, u32[]{:S(2)}) %collective-permute-start.3) | collective-permute-done | bytes 466976 | tf_op jit(solution)/shard_map/ppermute | solution.py:556
  29.1 0.0 collective-permute-done.refs_2_
  29.1 4.4 %filtered.3.refs_0_ = bf16[4,14,48,128]{3,2,1,0:T(8,128)(2,1)S(1)} custom-call(bf16[2,48,48,128]{3,2,1,0:T(8,128)(2,1)S(1)} %copy-done.1, f32[2,48,48]{2,1,0:T(8,128)S(1)} %copy-done.4, bf16[2,27,48,128]{3,2,1,0:T(8,128)(2,1)S(1)} %collective-permute-done.refs_2_, bf16[2,19,48,128]{3,2,1,0:T(8,128)(2,1)} %collective-permute-done.1.refs_3_, ...), custom_call_target="tpu_custom_call" | custom-call | flops 3440640 | bytes 21504000 | tf_op jit(solution)/shard_map/filtered/pallas_call | solution.py:413
  33.5 1.6 %collective-permute-start.9 = (bf16[4,14,48,128]{3,2,1,0:T(8,128)(2,1)S(1)}, bf16[4,14,48,128]{3,2,1,0:T(8,128)(2,1)}, u32[]{:S(2)}, u32[]{:S(2)}) collective-permute-start(bf16[4,14,48,128]{3,2,1,0:T(8,128)(2,1)S(1)} %filtered.3.refs_0_), channel_id=1, source_target_pairs={{0,2},{1,3},{2,0},{3,1},{4,6},{5,7},{6,4},{7,5},{8,10},{9,11},{10,... | collective-permute-start | bytes 2064392 | tf_op jit(solution)/shard_map/ppermute | solution.py:565
  35.1 4.3 %collective-permute-start.6 = (bf16[2,8,48,128]{3,2,1,0:T(8,128)(2,1)}, bf16[2,8,48,128]{3,2,1,0:T(8,128)(2,1)S(1)}, u32[]{:S(2)}, u32[]{:S(2)}) collective-permute-start(bf16[2,8,48,128]{3,2,1,0:T(8,128)(2,1)} %collective-permute-done.2.refs_4_), channel_id=1, source_target_pairs={{0,8},{8,16},{12,4},{16,24},{20,12},{28,20},{1,9},{9,17},{13,5},{1... | collective-permute-start | bytes 589832 | tf_op jit(solution)/shard_map/ppermute | solution.py:558
  39.4 0.1 collective-permute-start.7
  39.5 3.7 %collective-permute-done.7 = f32[24,128]{1,0:T(8,128)S(1)} collective-permute-done((f32[24,128]{1,0:T(8,128)S(1)}, f32[24,128]{1,0:T(8,128)S(1)}, u32[]{:S(2)}, u32[]{:S(2)}) %collective-permute-start.7) | collective-permute-done | bytes 12320 | tf_op jit(solution)/shard_map/ppermute | solution.py:570
  43.2 0.0 collective-permute-done.6.refs_6_
  43.2 2.2 %collective-permute-start.10 = (f32[24,128]{1,0:T(8,128)S(1)}, f32[24,128]{1,0:T(8,128)S(1)}, u32[]{:S(2)}, u32[]{:S(2)}) collective-permute-start(f32[24,128]{1,0:T(8,128)S(1)} %add.9), channel_id=1, source_target_pairs={{0,8},{4,12},{8,0},{12,4},{16,24},{20,28},{24,16},{28,20},{1,9},{5... | collective-permute-start | bytes 36872 | tf_op jit(solution)/shard_map/ppermute | solution.py:570
  45.4 3.8 %filtered.2 = (bf16[2,10,48,128]{3,2,1,0:T(8,128)(2,1)S(1)}, bf16[2,10,48,128]{3,2,1,0:T(8,128)(2,1)S(1)}) custom-call(bf16[2,48,48,128]{3,2,1,0:T(8,128)(2,1)S(1)} %copy-done.1, f32[2,48,48]{2,1,0:T(8,128)S(1)} %copy-done.4, bf16[2,27,48,128]{3,2,1,0:T(8,128)(2,1)S(1)} %collective-permute-done.refs_2_, ...), custom_call_target="tpu_custom_call" | custom-call | flops 2457600 | bytes 15360000 | tf_op jit(solution)/shard_map/filtered/pallas_call | solution.py:413
  49.2 0.6 collective-permute-start.8
  49.8 0.0 collective-permute-done.10
  49.8 0.0 collective-permute-done.9.refs_2_
  49.8 0.1 collective-permute-start.11
  49.9 0.5 collective-permute-start.12
  50.4 3.6 %collective-permute-start.13 = (f32[24,128]{1,0:T(8,128)S(1)}, f32[24,128]{1,0:T(8,128)S(1)}, u32[]{:S(2)}, u32[]{:S(2)}) collective-permute-start(f32[24,128]{1,0:T(8,128)S(1)} %add.10), channel_id=1, source_target_pairs={{0,16},{4,20},{8,24},{12,28},{16,0},{20,4},{24,8},{28,12},{1,17},{... | collective-permute-start | bytes 36872 | tf_op jit(solution)/shard_map/ppermute | solution.py:570
  54.0 0.3 fusion
  54.4 1.3 %collective-permute-done.13 = f32[24,128]{1,0:T(8,128)S(1)} collective-permute-done((f32[24,128]{1,0:T(8,128)S(1)}, f32[24,128]{1,0:T(8,128)S(1)}, u32[]{:S(2)}, u32[]{:S(2)}) %collective-permute-start.13) | collective-permute-done | bytes 12320 | tf_op jit(solution)/shard_map/ppermute | solution.py:570
  55.7 0.0 collective-permute-done.12.refs_3_
  55.7 0.0 collective-permute-done.11.refs_1_
  55.7 2.1 %rotated.2 = (bf16[2,14,48,128]{3,2,1,0:T(8,128)(2,1)S(1)}, bf16[2,14,48,128]{3,2,1,0:T(8,128)(2,1)S(1)}) custom-call(bf16[4,14,48,128]{3,2,1,0:T(8,128)(2,1)S(1)} %filtered.3.refs_0_, bf16[4,14,48,128]{3,2,1,0:T(8,128)(2,1)S(1)} %collective-permute-done.11.refs_1_, bf16[4,14,48,128]{3,2,1,0:T(8,128)(2,1)} %collective-permute-done.9.refs_2_, ...), custom_call_target="tpu_custom_call" | custom-call | flops 22020096 | bytes 215040 | tf_op jit(solution)/shard_map/rotated/pallas_call | solution.py:459
  57.9 1.9 %collective-permute-start.19 = (bf16[2,14,48,128]{3,2,1,0:T(8,128)(2,1)S(1)}, bf16[2,14,48,128]{3,2,1,0:T(8,128)(2,1)S(1)}, u32[]{:S(2)}, u32[]{:S(2)}) collective-permute-start(bf16[2,14,48,128]{3,2,1,0:T(8,128)(2,1)S(1)} %get-tuple-element.57), channel_id=1, source_target_pairs={{0,4},{4,0},{8,12},{12,8},{16,20},{20,16},{24,28},{28,24},{1,5},{5... | collective-permute-start | bytes 1032200 | tf_op jit(solution)/shard_map/ppermute | solution.py:594
  59.8 0.0 collective-permute-done.8.refs_2_
  59.8 0.0 collective-permute-start.14
  59.8 0.5 collective-permute-start.16
  60.3 2.3 %collective-permute-start.18 = (bf16[2,10,48,128]{3,2,1,0:T(8,128)(2,1)S(1)}, bf16[2,10,48,128]{3,2,1,0:T(8,128)(2,1)S(1)}, u32[]{:S(2)}, u32[]{:S(2)}) collective-permute-start(bf16[2,10,48,128]{3,2,1,0:T(8,128)(2,1)S(1)} %get-tuple-element.66.a), channel_id=1, source_target_pairs={{0,2},{1,3},{2,0},{3,1},{4,6},{5,7},{6,4},{7,5},{8,10},{9,11},{10,... | collective-permute-start | bytes 737288 | tf_op jit(solution)/shard_map/ppermute | solution.py:596
  62.6 0.1 broadcast_in_dim.22.strength
  62.6 0.1 coefficients.1
  62.8 0.0 collective-permute-start.15
  62.8 1.2 %collective-permute-done.15 = bf16[16,128]{1,0:T(8,128)(2,1)S(1)} collective-permute-done((bf16[16,128]{1,0:T(8,128)(2,1)S(1)}, bf16[16,128]{1,0:T(8,128)(2,1)S(1)}, u32[]{:S(2)}, u32[]{:S(2)}) %collective-permute-start.15) | collective-permute-done | bytes 4128 | tf_op jit(solution)/shard_map/ppermute | solution.py:599
  64.0 0.2 collective-permute-start.21
  64.1 0.0 collective-permute-done.14.refs_3_
  64.1 0.0 collective-permute-done.16.refs_1_
  64.1 0.6 rotated.3
  64.7 0.5 collective-permute-start.20
  65.2 0.0 collective-permute-start.17
  65.2 3.5 %collective-permute-done.18.c = bf16[2,10,48,128]{3,2,1,0:T(8,128)(2,1)S(1)} collective-permute-done((bf16[2,10,48,128]{3,2,1,0:T(8,128)(2,1)S(1)}, bf16[2,10,48,128]{3,2,1,0:T(8,128)(2,1)S(1)}, u32[]{:S(2)}, u32[]{:S(2)}) %collective-permute-start.18) | collective-permute-done | bytes 245792 | tf_op jit(solution)/shard_map/ppermute | solution.py:596
  68.8 0.0 collective-permute-done.19.got1
  68.8 0.0 collective-permute-start.22
  68.8 0.1 collective-permute-done.17
  68.9 1.9 %nonlocal.1.term = f32[2,48,48,128]{3,2,1,0:T(8,128)S(1)} custom-call(bf16[16,128]{1,0:T(8,128)(2,1)S(1)} %get-tuple-element.72.a, bf16[16,128]{1,0:T(8,128)(2,1)S(1)} %get-tuple-element.71.b, bf16[16,128]{1,0:T(8,128)(2,1)S(1)} %get-tuple-element.70.c, bf16[16,128]{1,0:T(8,128)(2,1)S(1)} %get-tuple-element.69.d, bf16[4,128,128]{2,1,0:T(8,128)(2,1)S(1)} %copy.18.refs_4_.q, ...), custom_call_target="tpu_custom_call" | custom-call | flops 256 | bytes 256 | tf_op jit(solution)/shard_map/nonlocal/pallas_call | solution.py:252
  70.8 0.0 collective-permute-done.21.b
  70.8 2.2 %collective-permute-done.20.got2 = bf16[2,10,48,128]{3,2,1,0:T(8,128)(2,1)S(1)} collective-permute-done((bf16[2,10,48,128]{3,2,1,0:T(8,128)(2,1)S(1)}, bf16[2,10,48,128]{3,2,1,0:T(8,128)(2,1)S(1)}, u32[]{:S(2)}, u32[]{:S(2)}) %collective-permute-start.20) | collective-permute-done | bytes 245792 | tf_op jit(solution)/shard_map/ppermute | solution.py:602
  73.0 0.0 collective-permute-done.22.d
  73.0 1.7 %assembled.1 = bf16[2,48,48,128]{3,2,1,0:T(8,128)(2,1)} custom-call(f32[2,48,48,128]{3,2,1,0:T(8,128)S(1)} %nonlocal.1.term, bf16[2,14,48,128]{3,2,1,0:T(8,128)(2,1)S(1)} %get-tuple-element.65.keep1, bf16[2,14,48,128]{3,2,1,0:T(8,128)(2,1)S(1)} %collective-permute-done.19.got1, bf16[2,10,48,128]{3,2,1,0:T(8,128)(2,1)S(1)} %collective-permute-done.20.got2, ...), custom_call_target="tpu_custom_call" | custom-call | flops 256 | bytes 256 | tf_op jit(solution)/shard_map/assembled/pallas_call | solution.py:506
  (29 shorter events, 0.1 us)
Async XLA Ops:
  0.0 54.0 %copy-start = (bf16[12,128,128]{2,1,0:T(8,128)(2,1)S(1)}, bf16[12,128,128]{2,1,0:T(8,128)(2,1)}, u32[]{:S(2)}) copy-start(bf16[12,128,128]{2,1,0:T(8,128)(2,1)} %param.13) | copy-start | bytes 1179652
  0.0 6.5 %copy-start.3 = (bf16[8,2,48,48]{3,2,1,0:T(8,128)(2,1)S(1)}, bf16[8,2,48,48]{3,2,1,0:T(8,128)(2,1)}, u32[]{:S(2)}) copy-start(bf16[8,2,48,48]{3,2,1,0:T(8,128)(2,1)} %beta.3) | copy-start | bytes 221188
  0.0 20.8 %copy-start.7 = (s32[8]{0:T(128)S(1)}, s32[8]{0:T(128)}, u32[]{:S(2)}) copy-start(s32[8]{0:T(128)} %atoms.1) | copy-start | bytes 100
  2.2 19.1 %copy-start.1 = (bf16[2,48,48,128]{3,2,1,0:T(8,128)(2,1)S(1)}, bf16[2,48,48,128]{3,2,1,0:T(8,128)(2,1)}, u32[]{:S(2)}) copy-start(bf16[2,48,48,128]{3,2,1,0:T(8,128)(2,1)} %refs_0_.3) | copy-start | bytes 3538948
  2.2 19.1 %copy-start.4 = (f32[2,48,48]{2,1,0:T(8,128)S(1)}, f32[2,48,48]{2,1,0:T(8,128)}, u32[]{:S(2)}) copy-start(f32[2,48,48]{2,1,0:T(8,128)} %refs_1_.3) | copy-start | bytes 55300
  2.2 14.6 %collective-permute-start.1 = (bf16[2,19,48,128]{3,2,1,0:T(8,128)(2,1)S(1)}, bf16[2,19,48,128]{3,2,1,0:T(8,128)(2,1)}, u32[]{:S(2)}, u32[]{:S(2)}) collective-permute-start(bf16[2,19,48,128]{3,2,1,0:T(8,128)(2,1)S(1)} %get-tuple-element.38), channel_id=1, source_target_pairs={{0,4},{4,0},{8,12},{12,8},{16,20},{20,16},{24,28},{28,24},{1,5},{5... | collective-permute-start | bytes 1400840 | tf_op jit(solution)/shard_map/ppermute | solution.py:550
  5.2 23.9 %collective-permute-start = (bf16[2,27,48,128]{3,2,1,0:T(8,128)(2,1)}, bf16[2,27,48,128]{3,2,1,0:T(8,128)(2,1)S(1)}, u32[]{:S(2)}, u32[]{:S(2)}) collective-permute-start(bf16[2,27,48,128]{3,2,1,0:T(8,128)(2,1)} %get-tuple-element.37), channel_id=1, source_target_pairs={{4,12},{8,0},{12,20},{16,8},{20,28},{24,16},{5,13},{9,1},{13,21},{... | collective-permute-start | bytes 1990664 | tf_op jit(solution)/shard_map/ppermute | solution.py:551
  8.1 13.2 %collective-permute-start.4 = (bf16[8,48,48]{2,1,0:T(8,128)(2,1)}, bf16[8,48,48]{2,1,0:T(8,128)(2,1)S(1)}, u32[]{:S(2)}, u32[]{:S(2)}) collective-permute-start(bf16[8,48,48]{2,1,0:T(8,128)(2,1)} %get-tuple-element.42), channel_id=1, source_target_pairs={{0,4},{4,0},{8,12},{12,8},{16,20},{20,16},{24,28},{28,24},{1,5},{5... | collective-permute-start | bytes 110600 | tf_op jit(solution)/shard_map/ppermute | solution.py:547
  10.9 10.4 %collective-permute-start.5 = (bf16[8,48,48]{2,1,0:T(8,128)(2,1)S(1)}, bf16[8,48,48]{2,1,0:T(8,128)(2,1)S(1)}, u32[]{:S(2)}, u32[]{:S(2)}) collective-permute-start(bf16[8,48,48]{2,1,0:T(8,128)(2,1)S(1)} %get-tuple-element.43), channel_id=1, source_target_pairs={{4,8},{8,4},{12,16},{16,12},{20,24},{24,20},{5,9},{9,5},{13,17},{1... | collective-permute-start | bytes 110600 | tf_op jit(solution)/shard_map/ppermute | solution.py:549
  16.8 12.3 %collective-permute-start.3 = (bf16[2,19,48,128]{3,2,1,0:T(8,128)(2,1)}, bf16[2,19,48,128]{3,2,1,0:T(8,128)(2,1)S(1)}, u32[]{:S(2)}, u32[]{:S(2)}) collective-permute-start(bf16[2,19,48,128]{3,2,1,0:T(8,128)(2,1)} %collective-permute-done.1.refs_3_), channel_id=1, source_target_pairs={{0,8},{8,16},{12,4},{16,24},{20,12},{28,20},{1,9},{9,17},{13,5},{1... | collective-permute-start | bytes 1400840 | tf_op jit(solution)/shard_map/ppermute | solution.py:556
  20.8 5.8 %collective-permute-start.2 = (bf16[2,8,48,128]{3,2,1,0:T(8,128)(2,1)S(1)}, bf16[2,8,48,128]{3,2,1,0:T(8,128)(2,1)}, u32[]{:S(2)}, u32[]{:S(2)}) collective-permute-start(bf16[2,8,48,128]{3,2,1,0:T(8,128)(2,1)S(1)} %get-tuple-element.41), channel_id=1, source_target_pairs={{0,4},{4,0},{8,12},{12,8},{16,20},{20,16},{24,28},{28,24},{1,5},{5... | collective-permute-start | bytes 589832 | tf_op jit(solution)/shard_map/ppermute | solution.py:557
  24.4 9.1 %copy-start.5 = (bf16[2,48,24,48]{3,2,1,0:T(8,128)(2,1)}, bf16[2,48,24,48]{3,2,1,0:T(8,128)(2,1)S(1)}, u32[]{:S(2)}) copy-start(bf16[2,48,24,48]{3,2,1,0:T(8,128)(2,1)S(1)} %get-tuple-element.64.weights) | copy-start | bytes 663556
  29.1 4.4 %copy-start.2 = (bf16[2,19,48,128]{3,2,1,0:T(8,128)(2,1)}, bf16[2,19,48,128]{3,2,1,0:T(8,128)(2,1)S(1)}, u32[]{:S(2)}) copy-start(bf16[2,19,48,128]{3,2,1,0:T(8,128)(2,1)S(1)} %collective-permute-done.3.refs_5_.refs_4_) | copy-start | bytes 1400836
  33.5 16.3 %collective-permute-start.9 = (bf16[4,14,48,128]{3,2,1,0:T(8,128)(2,1)S(1)}, bf16[4,14,48,128]{3,2,1,0:T(8,128)(2,1)}, u32[]{:S(2)}, u32[]{:S(2)}) collective-permute-start(bf16[4,14,48,128]{3,2,1,0:T(8,128)(2,1)S(1)} %filtered.3.refs_0_), channel_id=1, source_target_pairs={{0,2},{1,3},{2,0},{3,1},{4,6},{5,7},{6,4},{7,5},{8,10},{9,11},{10,... | collective-permute-start | bytes 2064392 | tf_op jit(solution)/shard_map/ppermute | solution.py:565
  35.1 8.1 %collective-permute-start.6 = (bf16[2,8,48,128]{3,2,1,0:T(8,128)(2,1)}, bf16[2,8,48,128]{3,2,1,0:T(8,128)(2,1)S(1)}, u32[]{:S(2)}, u32[]{:S(2)}) collective-permute-start(bf16[2,8,48,128]{3,2,1,0:T(8,128)(2,1)} %collective-permute-done.2.refs_4_), channel_id=1, source_target_pairs={{0,8},{8,16},{12,4},{16,24},{20,12},{28,20},{1,9},{9,17},{13,5},{1... | collective-permute-start | bytes 589832 | tf_op jit(solution)/shard_map/ppermute | solution.py:558
  39.4 3.8 %collective-permute-start.7 = (f32[24,128]{1,0:T(8,128)S(1)}, f32[24,128]{1,0:T(8,128)S(1)}, u32[]{:S(2)}, u32[]{:S(2)}) collective-permute-start(f32[24,128]{1,0:T(8,128)S(1)} %get-tuple-element.46), channel_id=1, source_target_pairs={{0,4},{4,0},{8,12},{12,8},{16,20},{20,16},{24,28},{28,24},{1,5},{5... | collective-permute-start | bytes 36872 | tf_op jit(solution)/shard_map/ppermute | solution.py:570
  43.2 2.2 %copy-start.8 = (bf16[2,8,48,128]{3,2,1,0:T(8,128)(2,1)}, bf16[2,8,48,128]{3,2,1,0:T(8,128)(2,1)S(1)}, u32[]{:S(2)}) copy-start(bf16[2,8,48,128]{3,2,1,0:T(8,128)(2,1)S(1)} %collective-permute-done.6.refs_6_) | copy-start | bytes 589828
  43.2 6.6 %collective-permute-start.10 = (f32[24,128]{1,0:T(8,128)S(1)}, f32[24,128]{1,0:T(8,128)S(1)}, u32[]{:S(2)}, u32[]{:S(2)}) collective-permute-start(f32[24,128]{1,0:T(8,128)S(1)} %add.9), channel_id=1, source_target_pairs={{0,8},{4,12},{8,0},{12,4},{16,24},{20,28},{24,16},{28,20},{1,9},{5... | collective-permute-start | bytes 36872 | tf_op jit(solution)/shard_map/ppermute | solution.py:570
  45.4 5.0 %copy-start.10 = (s32[12,2]{0,1:T(2,128)S(1)}, s32[12,2]{0,1:T(2,128)}, u32[]{:S(2)}) copy-start(s32[12,2]{0,1:T(2,128)} %param.12) | copy-start | bytes 292
  49.2 10.6 %collective-permute-start.8 = (bf16[2,10,48,128]{3,2,1,0:T(8,128)(2,1)S(1)}, bf16[2,10,48,128]{3,2,1,0:T(8,128)(2,1)S(1)}, u32[]{:S(2)}, u32[]{:S(2)}) collective-permute-start(bf16[2,10,48,128]{3,2,1,0:T(8,128)(2,1)S(1)} %get-tuple-element.49.refs_0_), channel_id=1, source_target_pairs={{0,2},{1,3},{2,0},{3,1},{4,6},{5,7},{6,4},{7,5},{8,10},{9,11},{10,... | collective-permute-start | bytes 737288 | tf_op jit(solution)/shard_map/ppermute | solution.py:584
  49.8 5.9 %collective-permute-start.11 = (bf16[4,14,48,128]{3,2,1,0:T(8,128)(2,1)S(1)}, bf16[4,14,48,128]{3,2,1,0:T(8,128)(2,1)S(1)}, u32[]{:S(2)}, u32[]{:S(2)}) collective-permute-start(bf16[4,14,48,128]{3,2,1,0:T(8,128)(2,1)S(1)} %filtered.3.refs_0_), channel_id=1, source_target_pairs={{0,1},{1,0},{2,3},{3,2},{4,5},{5,4},{6,7},{7,6},{8,9},{9,8},{10,11... | collective-permute-start | bytes 2064392 | tf_op jit(solution)/shard_map/ppermute | solution.py:588
  49.9 5.8 %collective-permute-start.12 = (bf16[4,14,48,128]{3,2,1,0:T(8,128)(2,1)}, bf16[4,14,48,128]{3,2,1,0:T(8,128)(2,1)S(1)}, u32[]{:S(2)}, u32[]{:S(2)}) collective-permute-start(bf16[4,14,48,128]{3,2,1,0:T(8,128)(2,1)} %collective-permute-done.9.refs_2_), channel_id=1, source_target_pairs={{0,1},{1,0},{2,3},{3,2},{4,5},{5,4},{6,7},{7,6},{8,9},{9,8},{10,11... | collective-permute-start | bytes 2064392 | tf_op jit(solution)/shard_map/ppermute | solution.py:589
  50.4 5.3 %collective-permute-start.13 = (f32[24,128]{1,0:T(8,128)S(1)}, f32[24,128]{1,0:T(8,128)S(1)}, u32[]{:S(2)}, u32[]{:S(2)}) collective-permute-start(f32[24,128]{1,0:T(8,128)S(1)} %add.10), channel_id=1, source_target_pairs={{0,16},{4,20},{8,24},{12,28},{16,0},{20,4},{24,8},{28,12},{1,17},{... | collective-permute-start | bytes 36872 | tf_op jit(solution)/shard_map/ppermute | solution.py:570
  55.7 6.9 %copy-start.9 = (f32[8]{0:T(128)S(1)}, f32[8]{0:T(128)}, u32[]{:S(2)}) copy-start(f32[8]{0:T(128)} %param.10) | copy-start | bytes 100
  57.8 11.0 %copy-start.6 = (bf16[2,48,24,48]{3,2,1,0:T(8,128)(2,1)S(1)}, bf16[2,48,24,48]{3,2,1,0:T(8,128)(2,1)}, u32[]{:S(2)}) copy-start(bf16[2,48,24,48]{3,2,1,0:T(8,128)(2,1)} %copy-done.5) | copy-start | bytes 663556
  57.9 10.9 %collective-permute-start.19 = (bf16[2,14,48,128]{3,2,1,0:T(8,128)(2,1)S(1)}, bf16[2,14,48,128]{3,2,1,0:T(8,128)(2,1)S(1)}, u32[]{:S(2)}, u32[]{:S(2)}) collective-permute-start(bf16[2,14,48,128]{3,2,1,0:T(8,128)(2,1)S(1)} %get-tuple-element.57), channel_id=1, source_target_pairs={{0,4},{4,0},{8,12},{12,8},{16,20},{20,16},{24,28},{28,24},{1,5},{5... | collective-permute-start | bytes 1032200 | tf_op jit(solution)/shard_map/ppermute | solution.py:594
  59.8 4.4 %collective-permute-start.14 = (bf16[2,10,48,128]{3,2,1,0:T(8,128)(2,1)S(1)}, bf16[2,10,48,128]{3,2,1,0:T(8,128)(2,1)S(1)}, u32[]{:S(2)}, u32[]{:S(2)}) collective-permute-start(bf16[2,10,48,128]{3,2,1,0:T(8,128)(2,1)S(1)} %collective-permute-done.8.refs_2_), channel_id=1, source_target_pairs={{0,1},{1,0},{2,3},{3,2},{4,5},{5,4},{6,7},{7,6},{8,9},{9,8},{10,11... | collective-permute-start | bytes 737288 | tf_op jit(solution)/shard_map/ppermute | solution.py:597
  59.8 4.4 %collective-permute-start.16 = (bf16[2,10,48,128]{3,2,1,0:T(8,128)(2,1)S(1)}, bf16[2,10,48,128]{3,2,1,0:T(8,128)(2,1)S(1)}, u32[]{:S(2)}, u32[]{:S(2)}) collective-permute-start(bf16[2,10,48,128]{3,2,1,0:T(8,128)(2,1)S(1)} %get-tuple-element.49.refs_0_), channel_id=1, source_target_pairs={{0,1},{1,0},{2,3},{3,2},{4,5},{5,4},{6,7},{7,6},{8,9},{9,8},{10,11... | collective-permute-start | bytes 737288 | tf_op jit(solution)/shard_map/ppermute | solution.py:582
  60.3 8.5 %collective-permute-start.18 = (bf16[2,10,48,128]{3,2,1,0:T(8,128)(2,1)S(1)}, bf16[2,10,48,128]{3,2,1,0:T(8,128)(2,1)S(1)}, u32[]{:S(2)}, u32[]{:S(2)}) collective-permute-start(bf16[2,10,48,128]{3,2,1,0:T(8,128)(2,1)S(1)} %get-tuple-element.66.a), channel_id=1, source_target_pairs={{0,2},{1,3},{2,0},{3,1},{4,6},{5,7},{6,4},{7,5},{8,10},{9,11},{10,... | collective-permute-start | bytes 737288 | tf_op jit(solution)/shard_map/ppermute | solution.py:596
  62.8 1.2 %collective-permute-start.15 = (bf16[16,128]{1,0:T(8,128)(2,1)S(1)}, bf16[16,128]{1,0:T(8,128)(2,1)S(1)}, u32[]{:S(2)}, u32[]{:S(2)}) collective-permute-start(bf16[16,128]{1,0:T(8,128)(2,1)S(1)} %coefficients.1), channel_id=1, source_target_pairs={{0,1},{1,0},{2,3},{3,2},{4,5},{5,4},{6,7},{7,6},{8,9},{9,8},{10,11... | collective-permute-start | bytes 12296 | tf_op jit(solution)/shard_map/ppermute | solution.py:599
  64.0 6.8 %collective-permute-start.21 = (bf16[2,10,48,128]{3,2,1,0:T(8,128)(2,1)S(1)}, bf16[2,10,48,128]{3,2,1,0:T(8,128)(2,1)S(1)}, u32[]{:S(2)}, u32[]{:S(2)}) collective-permute-start(bf16[2,10,48,128]{3,2,1,0:T(8,128)(2,1)S(1)} %get-tuple-element.66.a), channel_id=1, source_target_pairs={{0,1},{1,0},{2,3},{3,2},{4,5},{5,4},{6,7},{7,6},{8,9},{9,8},{10,11... | collective-permute-start | bytes 737288 | tf_op jit(solution)/shard_map/ppermute | solution.py:583
  64.7 8.3 %collective-permute-start.20 = (bf16[2,10,48,128]{3,2,1,0:T(8,128)(2,1)S(1)}, bf16[2,10,48,128]{3,2,1,0:T(8,128)(2,1)S(1)}, u32[]{:S(2)}, u32[]{:S(2)}) collective-permute-start(bf16[2,10,48,128]{3,2,1,0:T(8,128)(2,1)S(1)} %rotated.3), channel_id=1, source_target_pairs={{0,4},{4,0},{8,12},{12,8},{16,20},{20,16},{24,28},{28,24},{1,5},{5... | collective-permute-start | bytes 737288 | tf_op jit(solution)/shard_map/ppermute | solution.py:602
  65.2 3.7 %collective-permute-start.17 = (bf16[32,128]{1,0:T(8,128)(2,1)S(1)}, bf16[32,128]{1,0:T(8,128)(2,1)S(1)}, u32[]{:S(2)}, u32[]{:S(2)}) collective-permute-start(bf16[32,128]{1,0:T(8,128)(2,1)S(1)} %pad_maximum_fusion), channel_id=1, source_target_pairs={{0,2},{1,3},{2,0},{3,1},{4,6},{5,7},{6,4},{7,5},{8,10},{9,11},{10,... | collective-permute-start | bytes 24584 | tf_op jit(solution)/shard_map/ppermute | solution.py:604
  68.8 4.2 %collective-permute-start.22 = (bf16[2,10,48,128]{3,2,1,0:T(8,128)(2,1)S(1)}, bf16[2,10,48,128]{3,2,1,0:T(8,128)(2,1)S(1)}, u32[]{:S(2)}, u32[]{:S(2)}) collective-permute-start(bf16[2,10,48,128]{3,2,1,0:T(8,128)(2,1)S(1)} %collective-permute-done.18.c), channel_id=1, source_target_pairs={{0,1},{1,0},{2,3},{3,2},{4,5},{5,4},{6,7},{7,6},{8,9},{9,8},{10,11... | collective-permute-start | bytes 737288 | tf_op jit(solution)/shard_map/ppermute | solution.py:608

commit v19 on v18

--- a/solution.py
+++ b/solution.py
@@ -587,17 +587,16 @@
     y1, again, _, sums = ordered(y1, block1, give2, sums)
     c1 = lax.ppermute(again, "orb", beside)
     yc1 = lax.ppermute(y1, "orb", beside)
-    for step in rounds[2:]:
-        sums = added(sums, step)
-    yc1, sums = ordered(yc1, sums)
     give1, keep1 = rotated((block1, c1, y1, yc1), q, 2)
     got1 = lax.ppermute(give1, "space", swap)
     keep_y, yg, _, sums = ordered(keep2, yg, give1, sums)
+    for step in rounds[2:]:
+        sums = added(sums, step)
     yk = lax.ppermute(keep_y, "orb", across)
     ycg = lax.ppermute(yg, "orb", beside)
+    ycg, sums = ordered(ycg, sums)
     coefs = coefficients(sums, strong)
     coefs = jnp.concatenate([coefs, lax.ppermute(coefs, "orb", beside)], axis=0)
-    ycg, coefs = ordered(ycg, coefs)
     (give2,) = rotated((give2, cg, yg, ycg), q, 1)
     got2 = lax.ppermute(give2, "space", swap)
     coefs, _ = ordered(coefs, give2)

time: 75 us -> 76.8 us (1.024)
  waiting for transfers between devices: 22 us -> 23.5 us
    ppermute x1, waiting for transfers between devices: 3.55 us -> 0.01 us  [shards(): yk = lax.ppermute(keep_y, 'orb', across)]
    ppermute x1, waiting for transfers between devices: 0.09 us -> 3.53 us  [shards(): coefs_y = lax.ppermute(coefs, 'orb', across)]
    ppermute x1, waiting for transfers between devices: 0.01 us -> 1.42 us  [shards(): c1 = lax.ppermute(again, 'orb', beside)]
    ppermute x1, waiting for transfers between devices: 1.15 us -> 0.01 us  [shards(): coefs = jnp.concatenate([coefs, lax.ppermute(coefs, 'orb', beside)], axis=0)]
    ppermute x1, waiting for transfers between devices: 0.01 us -> 1 us  [shards(): yc1 = lax.ppermute(y1, 'orb', beside)]
  transfers between devices with their start and end apart: 23 -> 23, of which waited for: 9 -> 10; matrix products, arithmetic and copies ran while one was open for 1% -> 1% of each run, Pallas kernels for 18% -> 17%
where the time goes in v19:
time: 76.8 us; the launch traced here: 76.4 us
  starting transfers between devices  30.3 us (39%)
  waiting for transfers between devices  23.5 us (31%)
  Pallas kernels  21.4 us (28%)
    pallas_call x2, Pallas kernels, filtered(): pl.pallas_call(functools.partial(filter_kernel, slabs, start, parts, join...  8.16 us
    ppermute x3, waiting for transfers between devices, added(): return values + lax.ppermute(values, 'space', pairs)  5.44 us
    ppermute x1, waiting for transfers between devices, shards(): xr1 = lax.ppermute(to_x, 'space', swap)  5.24 us
    ppermute x3, starting transfers between devices, added(): return values + lax.ppermute(values, 'space', pairs)  5.24 us
    ppermute x1, starting transfers between devices, shards(): zf2 = lax.ppermute(xr2, 'space', other_way)  4.28 us
    ppermute x1, starting transfers between devices, shards(): zf1 = lax.ppermute(xr1, 'space', other_way)  3.97 us
    ppermute x1, waiting for transfers between devices, shards(): coefs_y = lax.ppermute(coefs, 'orb', across)  3.53 us
    pallas_call x1, Pallas kernels, partials(): pl.pallas_call(functools.partial(partial_kernel, count), out_shape=(jax.S...  3.04 us
  transfers between devices with their start and end apart: 23, of which 10 were waited for; matrix products, arithmetic and copies ran while one was open for 1% of the time, Pallas kernels for 17%

profile of v19, /device:TPU:0, one launch (start us, length us, event | category | flops | bytes accessed | tf_op | source)
XLA Modules:
  0.0 76.4 jit_solution(5026096744523078018)
XLA Ops:
  0.0 2.2 %prepared.1 = (bf16[2,19,48,128]{3,2,1,0:T(8,128)(2,1)S(1)}, bf16[2,27,48,128]{3,2,1,0:T(8,128)(2,1)}) custom-call(bf16[2,48,48,128]{3,2,1,0:T(8,128)(2,1)} %refs_0_.3, f32[2,48,48]{2,1,0:T(8,128)} %refs_1_.3), custom_call_target="tpu_custom_call" | custom-call | flops 256 | bytes 256 | tf_op jit(solution)/shard_map/prepared/pallas_call | solution.py:81
  2.2 0.0 copy-start.1
  2.2 0.0 copy-start.4
  2.2 3.0 %collective-permute-start.1 = (bf16[2,19,48,128]{3,2,1,0:T(8,128)(2,1)S(1)}, bf16[2,19,48,128]{3,2,1,0:T(8,128)(2,1)}, u32[]{:S(2)}, u32[]{:S(2)}) collective-permute-start(bf16[2,19,48,128]{3,2,1,0:T(8,128)(2,1)S(1)} %get-tuple-element.36), channel_id=1, source_target_pairs={{0,4},{4,0},{8,12},{12,8},{16,20},{20,16},{24,28},{28,24},{1,5},{5... | collective-permute-start | bytes 1400840 | tf_op jit(solution)/shard_map/ppermute | solution.py:550
  5.2 1.3 %collective-permute-start = (bf16[2,27,48,128]{3,2,1,0:T(8,128)(2,1)}, bf16[2,27,48,128]{3,2,1,0:T(8,128)(2,1)S(1)}, u32[]{:S(2)}, u32[]{:S(2)}) collective-permute-start(bf16[2,27,48,128]{3,2,1,0:T(8,128)(2,1)} %get-tuple-element.35), channel_id=1, source_target_pairs={{4,12},{8,0},{12,20},{16,8},{20,28},{24,16},{5,13},{9,1},{13,21},{... | collective-permute-start | bytes 1990664 | tf_op jit(solution)/shard_map/ppermute | solution.py:551
  6.5 1.6 %packed.1 = (bf16[2,8,48,128]{3,2,1,0:T(8,128)(2,1)S(1)}, bf16[8,48,48]{2,1,0:T(8,128)(2,1)S(1)}, bf16[8,48,48]{2,1,0:T(8,128)(2,1)}) custom-call(bf16[2,48,48,128]{3,2,1,0:T(8,128)(2,1)} %refs_0_.3, bf16[8,2,48,48]{3,2,1,0:T(8,128)(2,1)S(1)} %copy-done.3), custom_call_target="tpu_custom_call" | custom-call | flops 256 | bytes 256 | tf_op jit(solution)/shard_map/packed/pallas_call | solution.py:110
  8.1 2.8 %collective-permute-start.4 = (bf16[8,48,48]{2,1,0:T(8,128)(2,1)}, bf16[8,48,48]{2,1,0:T(8,128)(2,1)S(1)}, u32[]{:S(2)}, u32[]{:S(2)}) collective-permute-start(bf16[8,48,48]{2,1,0:T(8,128)(2,1)} %get-tuple-element.40), channel_id=1, source_target_pairs={{0,4},{4,0},{8,12},{12,8},{16,20},{20,16},{24,28},{28,24},{1,5},{5... | collective-permute-start | bytes 110600 | tf_op jit(solution)/shard_map/ppermute | solution.py:547
  10.9 0.7 collective-permute-start.5
  11.6 5.2 %collective-permute-done.1.refs_3_ = bf16[2,19,48,128]{3,2,1,0:T(8,128)(2,1)} collective-permute-done((bf16[2,19,48,128]{3,2,1,0:T(8,128)(2,1)S(1)}, bf16[2,19,48,128]{3,2,1,0:T(8,128)(2,1)}, u32[]{:S(2)}, u32[]{:S(2)}) %collective-permute-start.1) | collective-permute-done | bytes 466976 | tf_op jit(solution)/shard_map/ppermute | solution.py:550
  16.8 4.0 %collective-permute-start.3 = (bf16[2,19,48,128]{3,2,1,0:T(8,128)(2,1)}, bf16[2,19,48,128]{3,2,1,0:T(8,128)(2,1)S(1)}, u32[]{:S(2)}, u32[]{:S(2)}) collective-permute-start(bf16[2,19,48,128]{3,2,1,0:T(8,128)(2,1)} %collective-permute-done.1.refs_3_), channel_id=1, source_target_pairs={{0,8},{8,16},{12,4},{16,24},{20,12},{28,20},{1,9},{9,17},{13,5},{1... | collective-permute-start | bytes 1400840 | tf_op jit(solution)/shard_map/ppermute | solution.py:556
  20.8 0.1 collective-permute-start.2
  20.9 0.1 broadcast_select_fusion
  21.0 0.3 convolution_bitcast_fusion.gram
  21.3 0.0 collective-permute-done.4.b_x
  21.3 0.0 collective-permute-done.5.b_d
  21.3 0.0 copy-done.1
  21.3 3.0 %partials.1 = (f32[24,128]{1,0:T(8,128)S(1)}, bf16[2,48,24,48]{3,2,1,0:T(8,128)(2,1)S(1)}) custom-call(s32[8]{0:T(128)S(1)} %copy-done.7, bf16[2,48,48,128]{3,2,1,0:T(8,128)(2,1)S(1)} %copy-done.1, bf16[8,2,48,48]{3,2,1,0:T(8,128)(2,1)S(1)} %copy-done.3, bf16[8,48,48]{2,1,0:T(8,128)(2,1)S(1)} %collective-permute-done.4.b_x, ...), custom_call_target="tpu_custom_call" | custom-call | flops 256 | bytes 256 | tf_op jit(solution)/shard_map/partials/pallas_call | solution.py:177
  24.4 2.3 %collective-permute-done.2.refs_4_ = bf16[2,8,48,128]{3,2,1,0:T(8,128)(2,1)} collective-permute-done((bf16[2,8,48,128]{3,2,1,0:T(8,128)(2,1)S(1)}, bf16[2,8,48,128]{3,2,1,0:T(8,128)(2,1)}, u32[]{:S(2)}, u32[]{:S(2)}) %collective-permute-start.2) | collective-permute-done | bytes 196640 | tf_op jit(solution)/shard_map/ppermute | solution.py:557
  26.7 2.4 %collective-permute-done.3.refs_5_.refs_4_ = bf16[2,19,48,128]{3,2,1,0:T(8,128)(2,1)S(1)} collective-permute-done((bf16[2,19,48,128]{3,2,1,0:T(8,128)(2,1)}, bf16[2,19,48,128]{3,2,1,0:T(8,128)(2,1)S(1)}, u32[]{:S(2)}, u32[]{:S(2)}) %collective-permute-start.3) | collective-permute-done | bytes 466976 | tf_op jit(solution)/shard_map/ppermute | solution.py:556
  29.1 0.0 collective-permute-done.refs_2_
  29.1 4.4 %filtered.3.refs_0_ = bf16[4,14,48,128]{3,2,1,0:T(8,128)(2,1)S(1)} custom-call(bf16[2,48,48,128]{3,2,1,0:T(8,128)(2,1)S(1)} %copy-done.1, f32[2,48,48]{2,1,0:T(8,128)S(1)} %copy-done.4, bf16[2,27,48,128]{3,2,1,0:T(8,128)(2,1)S(1)} %collective-permute-done.refs_2_, bf16[2,19,48,128]{3,2,1,0:T(8,128)(2,1)} %collective-permute-done.1.refs_3_, ...), custom_call_target="tpu_custom_call" | custom-call | flops 3440640 | bytes 21504000 | tf_op jit(solution)/shard_map/filtered/pallas_call | solution.py:413
  33.5 1.6 %collective-permute-start.9 = (bf16[4,14,48,128]{3,2,1,0:T(8,128)(2,1)S(1)}, bf16[4,14,48,128]{3,2,1,0:T(8,128)(2,1)}, u32[]{:S(2)}, u32[]{:S(2)}) collective-permute-start(bf16[4,14,48,128]{3,2,1,0:T(8,128)(2,1)S(1)} %filtered.3.refs_0_), channel_id=1, source_target_pairs={{0,2},{1,3},{2,0},{3,1},{4,6},{5,7},{6,4},{7,5},{8,10},{9,11},{10,... | collective-permute-start | bytes 2064392 | tf_op jit(solution)/shard_map/ppermute | solution.py:565
  35.1 4.3 %collective-permute-start.6 = (bf16[2,8,48,128]{3,2,1,0:T(8,128)(2,1)}, bf16[2,8,48,128]{3,2,1,0:T(8,128)(2,1)S(1)}, u32[]{:S(2)}, u32[]{:S(2)}) collective-permute-start(bf16[2,8,48,128]{3,2,1,0:T(8,128)(2,1)} %collective-permute-done.2.refs_4_), channel_id=1, source_target_pairs={{0,8},{8,16},{12,4},{16,24},{20,12},{28,20},{1,9},{9,17},{13,5},{1... | collective-permute-start | bytes 589832 | tf_op jit(solution)/shard_map/ppermute | solution.py:558
  39.4 0.1 collective-permute-start.7
  39.5 3.7 %collective-permute-done.7 = f32[24,128]{1,0:T(8,128)S(1)} collective-permute-done((f32[24,128]{1,0:T(8,128)S(1)}, f32[24,128]{1,0:T(8,128)S(1)}, u32[]{:S(2)}, u32[]{:S(2)}) %collective-permute-start.7) | collective-permute-done | bytes 12320 | tf_op jit(solution)/shard_map/ppermute | solution.py:570
  43.2 0.0 collective-permute-done.6.refs_6_
  43.2 2.2 %collective-permute-start.10 = (f32[24,128]{1,0:T(8,128)S(1)}, f32[24,128]{1,0:T(8,128)S(1)}, u32[]{:S(2)}, u32[]{:S(2)}) collective-permute-start(f32[24,128]{1,0:T(8,128)S(1)} %add.9), channel_id=1, source_target_pairs={{0,8},{4,12},{8,0},{12,4},{16,24},{20,28},{24,16},{28,20},{1,9},{5... | collective-permute-start | bytes 36872 | tf_op jit(solution)/shard_map/ppermute | solution.py:570
  45.4 3.8 %filtered.2 = (bf16[2,10,48,128]{3,2,1,0:T(8,128)(2,1)S(1)}, bf16[2,10,48,128]{3,2,1,0:T(8,128)(2,1)S(1)}) custom-call(bf16[2,48,48,128]{3,2,1,0:T(8,128)(2,1)S(1)} %copy-done.1, f32[2,48,48]{2,1,0:T(8,128)S(1)} %copy-done.4, bf16[2,27,48,128]{3,2,1,0:T(8,128)(2,1)S(1)} %collective-permute-done.refs_2_, ...), custom_call_target="tpu_custom_call" | custom-call | flops 2457600 | bytes 15360000 | tf_op jit(solution)/shard_map/filtered/pallas_call | solution.py:413
  49.2 0.6 collective-permute-start.8
  49.8 0.0 collective-permute-done.10
  49.8 0.0 collective-permute-done.9.refs_2_
  49.8 0.1 collective-permute-start.11
  49.9 0.5 collective-permute-start.12
  50.4 0.3 fusion
  50.8 0.0 copy-start.9
  50.8 1.4 %collective-permute-done.11.refs_1_ = bf16[4,14,48,128]{3,2,1,0:T(8,128)(2,1)S(1)} collective-permute-done((bf16[4,14,48,128]{3,2,1,0:T(8,128)(2,1)S(1)}, bf16[4,14,48,128]{3,2,1,0:T(8,128)(2,1)S(1)}, u32[]{:S(2)}, u32[]{:S(2)}) %collective-permute-start.11) | collective-permute-done | bytes 688160 | tf_op jit(solution)/shard_map/ppermute | solution.py:588
  52.2 1.0 %collective-permute-done.12.refs_3_ = bf16[4,14,48,128]{3,2,1,0:T(8,128)(2,1)S(1)} collective-permute-done((bf16[4,14,48,128]{3,2,1,0:T(8,128)(2,1)}, bf16[4,14,48,128]{3,2,1,0:T(8,128)(2,1)S(1)}, u32[]{:S(2)}, u32[]{:S(2)}) %collective-permute-start.12) | collective-permute-done | bytes 688160 | tf_op jit(solution)/shard_map/ppermute | solution.py:589
  53.2 2.1 %rotated.2 = (bf16[2,14,48,128]{3,2,1,0:T(8,128)(2,1)S(1)}, bf16[2,14,48,128]{3,2,1,0:T(8,128)(2,1)S(1)}) custom-call(bf16[4,14,48,128]{3,2,1,0:T(8,128)(2,1)S(1)} %filtered.3.refs_0_, bf16[4,14,48,128]{3,2,1,0:T(8,128)(2,1)S(1)} %collective-permute-done.11.refs_1_, bf16[4,14,48,128]{3,2,1,0:T(8,128)(2,1)} %collective-permute-done.9.refs_2_, ...), custom_call_target="tpu_custom_call" | custom-call | flops 22020096 | bytes 215040 | tf_op jit(solution)/shard_map/rotated/pallas_call | solution.py:459
  55.3 0.1 collective-permute-done.8.refs_2_
  55.5 0.1 collective-permute-start.13
  55.6 0.4 collective-permute-start.16
  56.0 2.1 %collective-permute-start.19 = (bf16[2,14,48,128]{3,2,1,0:T(8,128)(2,1)S(1)}, bf16[2,14,48,128]{3,2,1,0:T(8,128)(2,1)S(1)}, u32[]{:S(2)}, u32[]{:S(2)}) collective-permute-start(bf16[2,14,48,128]{3,2,1,0:T(8,128)(2,1)S(1)} %get-tuple-element.53), channel_id=1, source_target_pairs={{0,4},{4,0},{8,12},{12,8},{16,20},{20,16},{24,28},{28,24},{1,5},{5... | collective-permute-start | bytes 1032200 | tf_op jit(solution)/shard_map/ppermute | solution.py:591
  58.1 2.5 %collective-permute-start.18 = (bf16[2,10,48,128]{3,2,1,0:T(8,128)(2,1)S(1)}, bf16[2,10,48,128]{3,2,1,0:T(8,128)(2,1)S(1)}, u32[]{:S(2)}, u32[]{:S(2)}) collective-permute-start(bf16[2,10,48,128]{3,2,1,0:T(8,128)(2,1)S(1)} %get-tuple-element.62.a), channel_id=1, source_target_pairs={{0,2},{1,3},{2,0},{3,1},{4,6},{5,7},{6,4},{7,5},{8,10},{9,11},{10,... | collective-permute-start | bytes 737288 | tf_op jit(solution)/shard_map/ppermute | solution.py:595
  60.6 3.0 %collective-permute-start.14 = (f32[24,128]{1,0:T(8,128)S(1)}, f32[24,128]{1,0:T(8,128)S(1)}, u32[]{:S(2)}, u32[]{:S(2)}) collective-permute-start(f32[24,128]{1,0:T(8,128)S(1)} %add.10), channel_id=1, source_target_pairs={{0,16},{4,20},{8,24},{12,28},{16,0},{20,4},{24,8},{28,12},{1,17},{... | collective-permute-start | bytes 36872 | tf_op jit(solution)/shard_map/ppermute | solution.py:570
  63.6 1.8 %collective-permute-done.14 = f32[24,128]{1,0:T(8,128)S(1)} collective-permute-done((f32[24,128]{1,0:T(8,128)S(1)}, f32[24,128]{1,0:T(8,128)S(1)}, u32[]{:S(2)}, u32[]{:S(2)}) %collective-permute-start.14) | collective-permute-done | bytes 12320 | tf_op jit(solution)/shard_map/ppermute | solution.py:570
  65.4 0.0 collective-permute-done.13.refs_3_
  65.4 0.1 broadcast_in_dim.22.strength
  65.5 0.1 coefficients.1
  65.6 0.0 collective-permute-start.15
  65.6 0.5 collective-permute-start.21
  66.1 0.0 collective-permute-done.16.refs_1_
  66.1 0.6 rotated.3
  66.7 0.4 collective-permute-start.20
  67.1 0.0 collective-permute-done.15
  67.1 0.0 collective-permute-start.17
  67.1 0.0 collective-permute-done.18.c
  67.1 0.0 collective-permute-done.19.got1
  67.1 0.1 collective-permute-start.22
  67.2 3.5 %collective-permute-done.17 = bf16[32,128]{1,0:T(8,128)(2,1)S(1)} collective-permute-done((bf16[32,128]{1,0:T(8,128)(2,1)S(1)}, bf16[32,128]{1,0:T(8,128)(2,1)S(1)}, u32[]{:S(2)}, u32[]{:S(2)}) %collective-permute-start.17) | collective-permute-done | bytes 8224 | tf_op jit(solution)/shard_map/ppermute | solution.py:603
  70.8 1.9 %nonlocal.1.term = f32[2,48,48,128]{3,2,1,0:T(8,128)S(1)} custom-call(bf16[16,128]{1,0:T(8,128)(2,1)S(1)} %get-tuple-element.68.a, bf16[16,128]{1,0:T(8,128)(2,1)S(1)} %get-tuple-element.67.b, bf16[16,128]{1,0:T(8,128)(2,1)S(1)} %get-tuple-element.66.c, bf16[16,128]{1,0:T(8,128)(2,1)S(1)} %get-tuple-element.65.d, bf16[4,128,128]{2,1,0:T(8,128)(2,1)S(1)} %copy.18.refs_4_.q, ...), custom_call_target="tpu_custom_call" | custom-call | flops 256 | bytes 256 | tf_op jit(solution)/shard_map/nonlocal/pallas_call | solution.py:252
  72.7 0.0 collective-permute-done.21.b
  72.7 2.0 %collective-permute-done.20.got2 = bf16[2,10,48,128]{3,2,1,0:T(8,128)(2,1)S(1)} collective-permute-done((bf16[2,10,48,128]{3,2,1,0:T(8,128)(2,1)S(1)}, bf16[2,10,48,128]{3,2,1,0:T(8,128)(2,1)S(1)}, u32[]{:S(2)}, u32[]{:S(2)}) %collective-permute-start.20) | collective-permute-done | bytes 245792 | tf_op jit(solution)/shard_map/ppermute | solution.py:601
  74.7 0.0 collective-permute-done.22.d
  74.7 1.7 %assembled.1 = bf16[2,48,48,128]{3,2,1,0:T(8,128)(2,1)} custom-call(f32[2,48,48,128]{3,2,1,0:T(8,128)S(1)} %nonlocal.1.term, bf16[2,14,48,128]{3,2,1,0:T(8,128)(2,1)S(1)} %get-tuple-element.61.keep1, bf16[2,14,48,128]{3,2,1,0:T(8,128)(2,1)S(1)} %collective-permute-done.19.got1, bf16[2,10,48,128]{3,2,1,0:T(8,128)(2,1)S(1)} %collective-permute-done.20.got2, ...), custom_call_target="tpu_custom_call" | custom-call | flops 256 | bytes 256 | tf_op jit(solution)/shard_map/assembled/pallas_call | solution.py:506
  (29 shorter events, 0.1 us)
Async XLA Ops:
  0.0 50.4 %copy-start = (bf16[12,128,128]{2,1,0:T(8,128)(2,1)S(1)}, bf16[12,128,128]{2,1,0:T(8,128)(2,1)}, u32[]{:S(2)}) copy-start(bf16[12,128,128]{2,1,0:T(8,128)(2,1)} %param.13) | copy-start | bytes 1179652
  0.0 6.5 %copy-start.3 = (bf16[8,2,48,48]{3,2,1,0:T(8,128)(2,1)S(1)}, bf16[8,2,48,48]{3,2,1,0:T(8,128)(2,1)}, u32[]{:S(2)}) copy-start(bf16[8,2,48,48]{3,2,1,0:T(8,128)(2,1)} %beta.3) | copy-start | bytes 221188
  0.0 20.8 %copy-start.7 = (s32[8]{0:T(128)S(1)}, s32[8]{0:T(128)}, u32[]{:S(2)}) copy-start(s32[8]{0:T(128)} %atoms.1) | copy-start | bytes 100
  2.2 19.1 %copy-start.1 = (bf16[2,48,48,128]{3,2,1,0:T(8,128)(2,1)S(1)}, bf16[2,48,48,128]{3,2,1,0:T(8,128)(2,1)}, u32[]{:S(2)}) copy-start(bf16[2,48,48,128]{3,2,1,0:T(8,128)(2,1)} %refs_0_.3) | copy-start | bytes 3538948
  2.2 19.1 %copy-start.4 = (f32[2,48,48]{2,1,0:T(8,128)S(1)}, f32[2,48,48]{2,1,0:T(8,128)}, u32[]{:S(2)}) copy-start(f32[2,48,48]{2,1,0:T(8,128)} %refs_1_.3) | copy-start | bytes 55300
  2.2 14.6 %collective-permute-start.1 = (bf16[2,19,48,128]{3,2,1,0:T(8,128)(2,1)S(1)}, bf16[2,19,48,128]{3,2,1,0:T(8,128)(2,1)}, u32[]{:S(2)}, u32[]{:S(2)}) collective-permute-start(bf16[2,19,48,128]{3,2,1,0:T(8,128)(2,1)S(1)} %get-tuple-element.36), channel_id=1, source_target_pairs={{0,4},{4,0},{8,12},{12,8},{16,20},{20,16},{24,28},{28,24},{1,5},{5... | collective-permute-start | bytes 1400840 | tf_op jit(solution)/shard_map/ppermute | solution.py:550
  5.2 23.9 %collective-permute-start = (bf16[2,27,48,128]{3,2,1,0:T(8,128)(2,1)}, bf16[2,27,48,128]{3,2,1,0:T(8,128)(2,1)S(1)}, u32[]{:S(2)}, u32[]{:S(2)}) collective-permute-start(bf16[2,27,48,128]{3,2,1,0:T(8,128)(2,1)} %get-tuple-element.35), channel_id=1, source_target_pairs={{4,12},{8,0},{12,20},{16,8},{20,28},{24,16},{5,13},{9,1},{13,21},{... | collective-permute-start | bytes 1990664 | tf_op jit(solution)/shard_map/ppermute | solution.py:551
  8.1 13.2 %collective-permute-start.4 = (bf16[8,48,48]{2,1,0:T(8,128)(2,1)}, bf16[8,48,48]{2,1,0:T(8,128)(2,1)S(1)}, u32[]{:S(2)}, u32[]{:S(2)}) collective-permute-start(bf16[8,48,48]{2,1,0:T(8,128)(2,1)} %get-tuple-element.40), channel_id=1, source_target_pairs={{0,4},{4,0},{8,12},{12,8},{16,20},{20,16},{24,28},{28,24},{1,5},{5... | collective-permute-start | bytes 110600 | tf_op jit(solution)/shard_map/ppermute | solution.py:547
  10.9 10.4 %collective-permute-start.5 = (bf16[8,48,48]{2,1,0:T(8,128)(2,1)S(1)}, bf16[8,48,48]{2,1,0:T(8,128)(2,1)S(1)}, u32[]{:S(2)}, u32[]{:S(2)}) collective-permute-start(bf16[8,48,48]{2,1,0:T(8,128)(2,1)S(1)} %get-tuple-element.41), channel_id=1, source_target_pairs={{4,8},{8,4},{12,16},{16,12},{20,24},{24,20},{5,9},{9,5},{13,17},{1... | collective-permute-start | bytes 110600 | tf_op jit(solution)/shard_map/ppermute | solution.py:549
  16.8 12.3 %collective-permute-start.3 = (bf16[2,19,48,128]{3,2,1,0:T(8,128)(2,1)}, bf16[2,19,48,128]{3,2,1,0:T(8,128)(2,1)S(1)}, u32[]{:S(2)}, u32[]{:S(2)}) collective-permute-start(bf16[2,19,48,128]{3,2,1,0:T(8,128)(2,1)} %collective-permute-done.1.refs_3_), channel_id=1, source_target_pairs={{0,8},{8,16},{12,4},{16,24},{20,12},{28,20},{1,9},{9,17},{13,5},{1... | collective-permute-start | bytes 1400840 | tf_op jit(solution)/shard_map/ppermute | solution.py:556
  20.8 5.8 %collective-permute-start.2 = (bf16[2,8,48,128]{3,2,1,0:T(8,128)(2,1)S(1)}, bf16[2,8,48,128]{3,2,1,0:T(8,128)(2,1)}, u32[]{:S(2)}, u32[]{:S(2)}) collective-permute-start(bf16[2,8,48,128]{3,2,1,0:T(8,128)(2,1)S(1)} %get-tuple-element.39), channel_id=1, source_target_pairs={{0,4},{4,0},{8,12},{12,8},{16,20},{20,16},{24,28},{28,24},{1,5},{5... | collective-permute-start | bytes 589832 | tf_op jit(solution)/shard_map/ppermute | solution.py:557
  24.4 9.1 %copy-start.5 = (bf16[2,48,24,48]{3,2,1,0:T(8,128)(2,1)}, bf16[2,48,24,48]{3,2,1,0:T(8,128)(2,1)S(1)}, u32[]{:S(2)}) copy-start(bf16[2,48,24,48]{3,2,1,0:T(8,128)(2,1)S(1)} %get-tuple-element.60.weights) | copy-start | bytes 663556
  29.1 4.4 %copy-start.2 = (bf16[2,19,48,128]{3,2,1,0:T(8,128)(2,1)}, bf16[2,19,48,128]{3,2,1,0:T(8,128)(2,1)S(1)}, u32[]{:S(2)}) copy-start(bf16[2,19,48,128]{3,2,1,0:T(8,128)(2,1)S(1)} %collective-permute-done.3.refs_5_.refs_4_) | copy-start | bytes 1400836
  33.5 16.3 %collective-permute-start.9 = (bf16[4,14,48,128]{3,2,1,0:T(8,128)(2,1)S(1)}, bf16[4,14,48,128]{3,2,1,0:T(8,128)(2,1)}, u32[]{:S(2)}, u32[]{:S(2)}) collective-permute-start(bf16[4,14,48,128]{3,2,1,0:T(8,128)(2,1)S(1)} %filtered.3.refs_0_), channel_id=1, source_target_pairs={{0,2},{1,3},{2,0},{3,1},{4,6},{5,7},{6,4},{7,5},{8,10},{9,11},{10,... | collective-permute-start | bytes 2064392 | tf_op jit(solution)/shard_map/ppermute | solution.py:565
  35.1 8.1 %collective-permute-start.6 = (bf16[2,8,48,128]{3,2,1,0:T(8,128)(2,1)}, bf16[2,8,48,128]{3,2,1,0:T(8,128)(2,1)S(1)}, u32[]{:S(2)}, u32[]{:S(2)}) collective-permute-start(bf16[2,8,48,128]{3,2,1,0:T(8,128)(2,1)} %collective-permute-done.2.refs_4_), channel_id=1, source_target_pairs={{0,8},{8,16},{12,4},{16,24},{20,12},{28,20},{1,9},{9,17},{13,5},{1... | collective-permute-start | bytes 589832 | tf_op jit(solution)/shard_map/ppermute | solution.py:558
  39.4 3.8 %collective-permute-start.7 = (f32[24,128]{1,0:T(8,128)S(1)}, f32[24,128]{1,0:T(8,128)S(1)}, u32[]{:S(2)}, u32[]{:S(2)}) collective-permute-start(f32[24,128]{1,0:T(8,128)S(1)} %get-tuple-element.44), channel_id=1, source_target_pairs={{0,4},{4,0},{8,12},{12,8},{16,20},{20,16},{24,28},{28,24},{1,5},{5... | collective-permute-start | bytes 36872 | tf_op jit(solution)/shard_map/ppermute | solution.py:570
  43.2 2.2 %copy-start.8 = (bf16[2,8,48,128]{3,2,1,0:T(8,128)(2,1)}, bf16[2,8,48,128]{3,2,1,0:T(8,128)(2,1)S(1)}, u32[]{:S(2)}) copy-start(bf16[2,8,48,128]{3,2,1,0:T(8,128)(2,1)S(1)} %collective-permute-done.6.refs_6_) | copy-start | bytes 589828
  43.2 6.6 %collective-permute-start.10 = (f32[24,128]{1,0:T(8,128)S(1)}, f32[24,128]{1,0:T(8,128)S(1)}, u32[]{:S(2)}, u32[]{:S(2)}) collective-permute-start(f32[24,128]{1,0:T(8,128)S(1)} %add.9), channel_id=1, source_target_pairs={{0,8},{4,12},{8,0},{12,4},{16,24},{20,28},{24,16},{28,20},{1,9},{5... | collective-permute-start | bytes 36872 | tf_op jit(solution)/shard_map/ppermute | solution.py:570
  45.4 5.0 %copy-start.10 = (s32[12,2]{0,1:T(2,128)S(1)}, s32[12,2]{0,1:T(2,128)}, u32[]{:S(2)}) copy-start(s32[12,2]{0,1:T(2,128)} %param.12) | copy-start | bytes 292
  49.2 6.3 %collective-permute-start.8 = (bf16[2,10,48,128]{3,2,1,0:T(8,128)(2,1)S(1)}, bf16[2,10,48,128]{3,2,1,0:T(8,128)(2,1)S(1)}, u32[]{:S(2)}, u32[]{:S(2)}) collective-permute-start(bf16[2,10,48,128]{3,2,1,0:T(8,128)(2,1)S(1)} %get-tuple-element.47.refs_0_), channel_id=1, source_target_pairs={{0,2},{1,3},{2,0},{3,1},{4,6},{5,7},{6,4},{7,5},{8,10},{9,11},{10,... | collective-permute-start | bytes 737288 | tf_op jit(solution)/shard_map/ppermute | solution.py:584
  49.8 2.4 %collective-permute-start.11 = (bf16[4,14,48,128]{3,2,1,0:T(8,128)(2,1)S(1)}, bf16[4,14,48,128]{3,2,1,0:T(8,128)(2,1)S(1)}, u32[]{:S(2)}, u32[]{:S(2)}) collective-permute-start(bf16[4,14,48,128]{3,2,1,0:T(8,128)(2,1)S(1)} %filtered.3.refs_0_), channel_id=1, source_target_pairs={{0,1},{1,0},{2,3},{3,2},{4,5},{5,4},{6,7},{7,6},{8,9},{9,8},{10,11... | collective-permute-start | bytes 2064392 | tf_op jit(solution)/shard_map/ppermute | solution.py:588
  49.9 3.3 %collective-permute-start.12 = (bf16[4,14,48,128]{3,2,1,0:T(8,128)(2,1)}, bf16[4,14,48,128]{3,2,1,0:T(8,128)(2,1)S(1)}, u32[]{:S(2)}, u32[]{:S(2)}) collective-permute-start(bf16[4,14,48,128]{3,2,1,0:T(8,128)(2,1)} %collective-permute-done.9.refs_2_), channel_id=1, source_target_pairs={{0,1},{1,0},{2,3},{3,2},{4,5},{5,4},{6,7},{7,6},{8,9},{9,8},{10,11... | collective-permute-start | bytes 2064392 | tf_op jit(solution)/shard_map/ppermute | solution.py:589
  50.8 14.6 %copy-start.9 = (f32[8]{0:T(128)S(1)}, f32[8]{0:T(128)}, u32[]{:S(2)}) copy-start(f32[8]{0:T(128)} %param.10) | copy-start | bytes 100
  55.3 15.4 %copy-start.6 = (bf16[2,48,24,48]{3,2,1,0:T(8,128)(2,1)S(1)}, bf16[2,48,24,48]{3,2,1,0:T(8,128)(2,1)}, u32[]{:S(2)}) copy-start(bf16[2,48,24,48]{3,2,1,0:T(8,128)(2,1)} %copy-done.5) | copy-start | bytes 663556
  55.5 9.9 %collective-permute-start.13 = (bf16[2,10,48,128]{3,2,1,0:T(8,128)(2,1)S(1)}, bf16[2,10,48,128]{3,2,1,0:T(8,128)(2,1)S(1)}, u32[]{:S(2)}, u32[]{:S(2)}) collective-permute-start(bf16[2,10,48,128]{3,2,1,0:T(8,128)(2,1)S(1)} %collective-permute-done.8.refs_2_), channel_id=1, source_target_pairs={{0,1},{1,0},{2,3},{3,2},{4,5},{5,4},{6,7},{7,6},{8,9},{9,8},{10,11... | collective-permute-start | bytes 737288 | tf_op jit(solution)/shard_map/ppermute | solution.py:596
  55.6 10.6 %collective-permute-start.16 = (bf16[2,10,48,128]{3,2,1,0:T(8,128)(2,1)S(1)}, bf16[2,10,48,128]{3,2,1,0:T(8,128)(2,1)S(1)}, u32[]{:S(2)}, u32[]{:S(2)}) collective-permute-start(bf16[2,10,48,128]{3,2,1,0:T(8,128)(2,1)S(1)} %get-tuple-element.47.refs_0_), channel_id=1, source_target_pairs={{0,1},{1,0},{2,3},{3,2},{4,5},{5,4},{6,7},{7,6},{8,9},{9,8},{10,11... | collective-permute-start | bytes 737288 | tf_op jit(solution)/shard_map/ppermute | solution.py:582
  56.0 11.2 %collective-permute-start.19 = (bf16[2,14,48,128]{3,2,1,0:T(8,128)(2,1)S(1)}, bf16[2,14,48,128]{3,2,1,0:T(8,128)(2,1)S(1)}, u32[]{:S(2)}, u32[]{:S(2)}) collective-permute-start(bf16[2,14,48,128]{3,2,1,0:T(8,128)(2,1)S(1)} %get-tuple-element.53), channel_id=1, source_target_pairs={{0,4},{4,0},{8,12},{12,8},{16,20},{20,16},{24,28},{28,24},{1,5},{5... | collective-permute-start | bytes 1032200 | tf_op jit(solution)/shard_map/ppermute | solution.py:591
  58.1 9.0 %collective-permute-start.18 = (bf16[2,10,48,128]{3,2,1,0:T(8,128)(2,1)S(1)}, bf16[2,10,48,128]{3,2,1,0:T(8,128)(2,1)S(1)}, u32[]{:S(2)}, u32[]{:S(2)}) collective-permute-start(bf16[2,10,48,128]{3,2,1,0:T(8,128)(2,1)S(1)} %get-tuple-element.62.a), channel_id=1, source_target_pairs={{0,2},{1,3},{2,0},{3,1},{4,6},{5,7},{6,4},{7,5},{8,10},{9,11},{10,... | collective-permute-start | bytes 737288 | tf_op jit(solution)/shard_map/ppermute | solution.py:595
  60.6 4.7 %collective-permute-start.14 = (f32[24,128]{1,0:T(8,128)S(1)}, f32[24,128]{1,0:T(8,128)S(1)}, u32[]{:S(2)}, u32[]{:S(2)}) collective-permute-start(f32[24,128]{1,0:T(8,128)S(1)} %add.10), channel_id=1, source_target_pairs={{0,16},{4,20},{8,24},{12,28},{16,0},{20,4},{24,8},{28,12},{1,17},{... | collective-permute-start | bytes 36872 | tf_op jit(solution)/shard_map/ppermute | solution.py:570
  65.6 1.5 %collective-permute-start.15 = (bf16[16,128]{1,0:T(8,128)(2,1)S(1)}, bf16[16,128]{1,0:T(8,128)(2,1)S(1)}, u32[]{:S(2)}, u32[]{:S(2)}) collective-permute-start(bf16[16,128]{1,0:T(8,128)(2,1)S(1)} %coefficients.1), channel_id=1, source_target_pairs={{0,1},{1,0},{2,3},{3,2},{4,5},{5,4},{6,7},{7,6},{8,9},{9,8},{10,11... | collective-permute-start | bytes 12296 | tf_op jit(solution)/shard_map/ppermute | solution.py:599
  65.6 7.0 %collective-permute-start.21 = (bf16[2,10,48,128]{3,2,1,0:T(8,128)(2,1)S(1)}, bf16[2,10,48,128]{3,2,1,0:T(8,128)(2,1)S(1)}, u32[]{:S(2)}, u32[]{:S(2)}) collective-permute-start(bf16[2,10,48,128]{3,2,1,0:T(8,128)(2,1)S(1)} %get-tuple-element.62.a), channel_id=1, source_target_pairs={{0,1},{1,0},{2,3},{3,2},{4,5},{5,4},{6,7},{7,6},{8,9},{9,8},{10,11... | collective-permute-start | bytes 737288 | tf_op jit(solution)/shard_map/ppermute | solution.py:583
  66.7 8.0 %collective-permute-start.20 = (bf16[2,10,48,128]{3,2,1,0:T(8,128)(2,1)S(1)}, bf16[2,10,48,128]{3,2,1,0:T(8,128)(2,1)S(1)}, u32[]{:S(2)}, u32[]{:S(2)}) collective-permute-start(bf16[2,10,48,128]{3,2,1,0:T(8,128)(2,1)S(1)} %rotated.3), channel_id=1, source_target_pairs={{0,4},{4,0},{8,12},{12,8},{16,20},{20,16},{24,28},{28,24},{1,5},{5... | collective-permute-start | bytes 737288 | tf_op jit(solution)/shard_map/ppermute | solution.py:601
  67.1 3.7 %collective-permute-start.17 = (bf16[32,128]{1,0:T(8,128)(2,1)S(1)}, bf16[32,128]{1,0:T(8,128)(2,1)S(1)}, u32[]{:S(2)}, u32[]{:S(2)}) collective-permute-start(bf16[32,128]{1,0:T(8,128)(2,1)S(1)} %pad_maximum_fusion), channel_id=1, source_target_pairs={{0,2},{1,3},{2,0},{3,1},{4,6},{5,7},{6,4},{7,5},{8,10},{9,11},{10,... | collective-permute-start | bytes 24584 | tf_op jit(solution)/shard_map/ppermute | solution.py:603
  67.1 7.6 %collective-permute-start.22 = (bf16[2,10,48,128]{3,2,1,0:T(8,128)(2,1)S(1)}, bf16[2,10,48,128]{3,2,1,0:T(8,128)(2,1)S(1)}, u32[]{:S(2)}, u32[]{:S(2)}) collective-permute-start(bf16[2,10,48,128]{3,2,1,0:T(8,128)(2,1)S(1)} %collective-permute-done.18.c), channel_id=1, source_target_pairs={{0,1},{1,0},{2,3},{3,2},{4,5},{5,4},{6,7},{7,6},{8,9},{9,8},{10,11... | collective-permute-start | bytes 737288 | tf_op jit(solution)/shard_map/ppermute | solution.py:607

commit v20 on v18

--- a/solution.py
+++ b/solution.py
@@ -90,17 +90,21 @@
     )(*(pltpu.with_memory_space_constraint(a, pltpu.MemorySpace.HBM) for a in (psi, potential)))
 
 
-def pack_kernel(early, psi, beta, to_x2, far, near, sem):
+def pack_kernel(early, psi, beta, to_x2, far, near, sems):
     x = lax.rem(lax.axis_index("space"), 2)
     half = psi.shape[1] // 2
     later = half + 2 - early
-    copy = pltpu.make_async_copy(
-        psi.at[:, pl.ds((half - 2) * (1 - x) + early, later)], to_x2, sem
-    )
-    copy.start()
-    far[...] = beta[:, x]
-    near[...] = beta[:, 1 - x]
-    copy.wait()
+    copies = [
+        pltpu.make_async_copy(beta.at[:, 1 - x], near, sems.at[0]),
+        pltpu.make_async_copy(beta.at[:, x], far, sems.at[1]),
+        pltpu.make_async_copy(
+            psi.at[:, pl.ds((half - 2) * (1 - x) + early, later)], to_x2, sems.at[2]
+        ),
+    ]
+    for copy in copies:
+        copy.start()
+    for copy in copies:
+        copy.wait()
 
 
 def packed(psi, beta, early):
@@ -110,16 +114,13 @@
     return pl.pallas_call(
         functools.partial(pack_kernel, early),
         out_shape=(jax.ShapeDtypeStruct((planes, later, width_y, orbs), BF16), side, side),
-        in_specs=[
-            pl.BlockSpec(memory_space=pltpu.MemorySpace.HBM),
-            pl.BlockSpec(memory_space=pltpu.VMEM),
-        ],
+        in_specs=[pl.BlockSpec(memory_space=pltpu.MemorySpace.HBM)] * 2,
         out_specs=(pl.BlockSpec(memory_space=pltpu.VMEM),) * 3,
-        scratch_shapes=[pltpu.SemaphoreType.DMA],
+        scratch_shapes=[pltpu.SemaphoreType.DMA((3,))],
         compiler_params=params(),
         cost_estimate=cost(4096, 4096),
         name="packed",
-    )(pltpu.with_memory_space_constraint(psi, pltpu.MemorySpace.HBM), beta)
+    )(*(pltpu.with_memory_space_constraint(a, pltpu.MemorySpace.HBM) for a in (psi, beta)))
 
 
 def partial_kernel(count, atoms, own, beta, b_x, b_d, potential, gram, out, weights_out, table, acc):
@@ -467,16 +468,12 @@
     )(*blocks, q)
 
 
-def assemble_kernel(group, term, keep1, got1, got2, a, b, c, d, q, out):
+def assemble_kernel(group, term, keep1, got1, a, b, c, d, q, out):
     half = term.shape[1] // 2
     width, orbs = term.shape[2:]
     x = lax.rem(lax.axis_index("space"), 2)
-    rows1, rows2 = keep1.shape[1], got2.shape[1]
-    for ref, at in (
-        (keep1, half * x),
-        (got1, half * (1 - x)),
-        (got2, half * (1 - x) + rows1),
-    ):
+    rows1, rows2 = keep1.shape[1], a.shape[1]
+    for ref, at in ((keep1, half * x), (got1, half * (1 - x))):
         where = pl.ds(at, ref.shape[1])
         out[:, where] = (ref[...].astype(F32) + term[:, where]).astype(BF16)
     low = jnp.concatenate([q[0], q[1]], axis=0)
@@ -501,17 +498,40 @@
     lax.fori_loop(0, rows2 // group, one, 0)
 
 
+def finish_kernel(rows1, term, got2, before, out, rows, sem):
+    half = term.shape[1] // 2
+    x = lax.rem(lax.axis_index("space"), 2)
+    where = pl.ds(half * (1 - x) + rows1, got2.shape[1])
+    rows[...] = (got2[...].astype(F32) + term[:, where]).astype(BF16)
+    copy = pltpu.make_async_copy(rows, out.at[:, where], sem)
+    copy.start()
+    copy.wait()
+
+
 def assembled(term, keep1, got1, got2, blocks, q):
     group = max(g for g in range(1, 9) if got2.shape[1] % g == 0)
-    return pl.pallas_call(
+    most = pl.pallas_call(
         functools.partial(assemble_kernel, group),
         out_shape=jax.ShapeDtypeStruct(term.shape, BF16),
-        in_specs=[pl.BlockSpec(memory_space=pltpu.VMEM)] * 9,
+        in_specs=[pl.BlockSpec(memory_space=pltpu.VMEM)] * 8,
         out_specs=pl.BlockSpec(memory_space=pltpu.VMEM),
         compiler_params=params(),
         cost_estimate=cost(4096, 4096),
         name="assembled",
-    )(term, keep1, got1, got2, *blocks, q)
+    )(term, keep1, got1, *blocks, q)
+    local = pl.BlockSpec(memory_space=pltpu.VMEM)
+    distant = pl.BlockSpec(memory_space=pltpu.MemorySpace.HBM)
+    return pl.pallas_call(
+        functools.partial(finish_kernel, keep1.shape[1]),
+        out_shape=jax.ShapeDtypeStruct(term.shape, BF16),
+        in_specs=[local, local, distant],
+        out_specs=distant,
+        input_output_aliases={2: 0},
+        scratch_shapes=[pltpu.VMEM(got2.shape, BF16), pltpu.SemaphoreType.DMA],
+        compiler_params=params(),
+        cost_estimate=cost(4096, 4096),
+        name="finished",
+    )(term, got2, pltpu.with_memory_space_constraint(most, pltpu.MemorySpace.HBM))
 
 
 def ordered(*arrays):

time: 75 us -> 74.6 us (level)
  waiting for transfers between devices: 22 us -> 20.1 us
  Pallas kernels: 21.4 us -> 22.3 us
    ppermute x1, waiting for transfers between devices: 2.2 us -> 0.49 us  [shards(): got2 = lax.ppermute(give2, 'space', swap)]
    pallas_call x0 -> x1, Pallas kernels: none -> 0.75 us  [assembled(): pl.pallas_call(functools.partial(finish_kernel, keep1.shape[1]), out_shap...]
  transfers between devices with their start and end apart: 23 -> 23, of which waited for: 9 -> 9; matrix products, arithmetic and copies ran while one was open for 1% -> 1% of each run, Pallas kernels for 18% -> 20%
where the time goes in v20:
time: 74.6 us; the launch traced here: 73.7 us
  starting transfers between devices  30.1 us (40%)
  Pallas kernels  22.3 us (30%)
  waiting for transfers between devices  20.1 us (27%)
    pallas_call x2, Pallas kernels, filtered(): pl.pallas_call(functools.partial(filter_kernel, slabs, start, parts, join...  8.16 us
    ppermute x3, starting transfers between devices, added(): return values + lax.ppermute(values, 'space', pairs)  5.91 us
    ppermute x1, waiting for transfers between devices, shards(): xr1 = lax.ppermute(to_x, 'space', swap)  5.14 us
    ppermute x3, waiting for transfers between devices, added(): return values + lax.ppermute(values, 'space', pairs)  4.98 us
    ppermute x1, starting transfers between devices, shards(): zf2 = lax.ppermute(xr2, 'space', other_way)  4.28 us
    ppermute x1, starting transfers between devices, shards(): zf1 = lax.ppermute(xr1, 'space', other_way)  3.97 us
    ppermute x1, waiting for transfers between devices, shards(): yk = lax.ppermute(keep_y, 'orb', across)  3.55 us
    pallas_call x1, Pallas kernels, partials(): pl.pallas_call(functools.partial(partial_kernel, count), out_shape=(jax.S...  3.04 us
  transfers between devices with their start and end apart: 23, of which 9 were waited for; matrix products, arithmetic and copies ran while one was open for 1% of the time, Pallas kernels for 20%

profile of v20, /device:TPU:0, one launch (start us, length us, event | category | flops | bytes accessed | tf_op | source)
XLA Modules:
  0.0 73.7 jit_solution(1022953372811163467)
XLA Ops:
  0.0 2.2 %prepared.1 = (bf16[2,19,48,128]{3,2,1,0:T(8,128)(2,1)S(1)}, bf16[2,27,48,128]{3,2,1,0:T(8,128)(2,1)}) custom-call(bf16[2,48,48,128]{3,2,1,0:T(8,128)(2,1)} %refs_0_.3, f32[2,48,48]{2,1,0:T(8,128)} %refs_1_.3), custom_call_target="tpu_custom_call" | custom-call | flops 256 | bytes 256 | tf_op jit(solution)/shard_map/prepared/pallas_call | solution.py:81
  2.2 0.0 copy-start.1
  2.2 0.0 copy-start.4
  2.2 3.0 %collective-permute-start.1 = (bf16[2,19,48,128]{3,2,1,0:T(8,128)(2,1)S(1)}, bf16[2,19,48,128]{3,2,1,0:T(8,128)(2,1)}, u32[]{:S(2)}, u32[]{:S(2)}) collective-permute-start(bf16[2,19,48,128]{3,2,1,0:T(8,128)(2,1)S(1)} %get-tuple-element.38), channel_id=1, source_target_pairs={{0,4},{4,0},{8,12},{12,8},{16,20},{20,16},{24,28},{28,24},{1,5},{5... | collective-permute-start | bytes 1400840 | tf_op jit(solution)/shard_map/ppermute | solution.py:570
  5.2 1.3 %collective-permute-start = (bf16[2,27,48,128]{3,2,1,0:T(8,128)(2,1)}, bf16[2,27,48,128]{3,2,1,0:T(8,128)(2,1)S(1)}, u32[]{:S(2)}, u32[]{:S(2)}) collective-permute-start(bf16[2,27,48,128]{3,2,1,0:T(8,128)(2,1)} %get-tuple-element.37), channel_id=1, source_target_pairs={{4,12},{8,0},{12,20},{16,8},{20,28},{24,16},{5,13},{9,1},{13,21},{... | collective-permute-start | bytes 1990664 | tf_op jit(solution)/shard_map/ppermute | solution.py:571
  6.5 1.7 %packed.1 = (bf16[2,8,48,128]{3,2,1,0:T(8,128)(2,1)S(1)}, bf16[8,48,48]{2,1,0:T(8,128)(2,1)S(1)}, bf16[8,48,48]{2,1,0:T(8,128)(2,1)}) custom-call(bf16[2,48,48,128]{3,2,1,0:T(8,128)(2,1)} %refs_0_.3, bf16[8,2,48,48]{3,2,1,0:T(8,128)(2,1)} %beta.3), custom_call_target="tpu_custom_call" | custom-call | flops 256 | bytes 256 | tf_op jit(solution)/shard_map/packed/pallas_call | solution.py:114
  8.2 2.8 %collective-permute-start.4 = (bf16[8,48,48]{2,1,0:T(8,128)(2,1)}, bf16[8,48,48]{2,1,0:T(8,128)(2,1)S(1)}, u32[]{:S(2)}, u32[]{:S(2)}) collective-permute-start(bf16[8,48,48]{2,1,0:T(8,128)(2,1)} %get-tuple-element.42), channel_id=1, source_target_pairs={{0,4},{4,0},{8,12},{12,8},{16,20},{20,16},{24,28},{28,24},{1,5},{5... | collective-permute-start | bytes 110600 | tf_op jit(solution)/shard_map/ppermute | solution.py:567
  11.0 0.7 collective-permute-start.5
  11.7 5.1 %collective-permute-done.1.refs_3_ = bf16[2,19,48,128]{3,2,1,0:T(8,128)(2,1)} collective-permute-done((bf16[2,19,48,128]{3,2,1,0:T(8,128)(2,1)S(1)}, bf16[2,19,48,128]{3,2,1,0:T(8,128)(2,1)}, u32[]{:S(2)}, u32[]{:S(2)}) %collective-permute-start.1) | collective-permute-done | bytes 466976 | tf_op jit(solution)/shard_map/ppermute | solution.py:570
  16.9 4.0 %collective-permute-start.3 = (bf16[2,19,48,128]{3,2,1,0:T(8,128)(2,1)}, bf16[2,19,48,128]{3,2,1,0:T(8,128)(2,1)S(1)}, u32[]{:S(2)}, u32[]{:S(2)}) collective-permute-start(bf16[2,19,48,128]{3,2,1,0:T(8,128)(2,1)} %collective-permute-done.1.refs_3_), channel_id=1, source_target_pairs={{0,8},{8,16},{12,4},{16,24},{20,12},{28,20},{1,9},{9,17},{13,5},{1... | collective-permute-start | bytes 1400840 | tf_op jit(solution)/shard_map/ppermute | solution.py:576
  20.9 0.1 collective-permute-start.2
  20.9 0.1 broadcast_select_fusion
  21.0 0.3 convolution_bitcast_fusion.gram
  21.3 0.0 collective-permute-done.4.b_x
  21.3 0.0 collective-permute-done.5.b_d
  21.3 0.0 copy-done.1
  21.4 3.0 %partials.1 = (f32[24,128]{1,0:T(8,128)S(1)}, bf16[2,48,24,48]{3,2,1,0:T(8,128)(2,1)S(1)}) custom-call(s32[8]{0:T(128)S(1)} %copy-done.7, bf16[2,48,48,128]{3,2,1,0:T(8,128)(2,1)S(1)} %copy-done.1, bf16[8,2,48,48]{3,2,1,0:T(8,128)(2,1)S(1)} %copy-done.3, bf16[8,48,48]{2,1,0:T(8,128)(2,1)S(1)} %collective-permute-done.4.b_x, ...), custom_call_target="tpu_custom_call" | custom-call | flops 256 | bytes 256 | tf_op jit(solution)/shard_map/partials/pallas_call | solution.py:178
  24.4 2.3 %collective-permute-done.2.refs_4_ = bf16[2,8,48,128]{3,2,1,0:T(8,128)(2,1)} collective-permute-done((bf16[2,8,48,128]{3,2,1,0:T(8,128)(2,1)S(1)}, bf16[2,8,48,128]{3,2,1,0:T(8,128)(2,1)}, u32[]{:S(2)}, u32[]{:S(2)}) %collective-permute-start.2) | collective-permute-done | bytes 196640 | tf_op jit(solution)/shard_map/ppermute | solution.py:577
  26.7 2.4 %collective-permute-done.3.refs_5_.refs_4_ = bf16[2,19,48,128]{3,2,1,0:T(8,128)(2,1)S(1)} collective-permute-done((bf16[2,19,48,128]{3,2,1,0:T(8,128)(2,1)}, bf16[2,19,48,128]{3,2,1,0:T(8,128)(2,1)S(1)}, u32[]{:S(2)}, u32[]{:S(2)}) %collective-permute-start.3) | collective-permute-done | bytes 466976 | tf_op jit(solution)/shard_map/ppermute | solution.py:576
  29.1 0.0 collective-permute-done.refs_2_
  29.1 4.4 %filtered.3.refs_0_ = bf16[4,14,48,128]{3,2,1,0:T(8,128)(2,1)S(1)} custom-call(bf16[2,48,48,128]{3,2,1,0:T(8,128)(2,1)S(1)} %copy-done.1, f32[2,48,48]{2,1,0:T(8,128)S(1)} %copy-done.4, bf16[2,27,48,128]{3,2,1,0:T(8,128)(2,1)S(1)} %collective-permute-done.refs_2_, bf16[2,19,48,128]{3,2,1,0:T(8,128)(2,1)} %collective-permute-done.1.refs_3_, ...), custom_call_target="tpu_custom_call" | custom-call | flops 3440640 | bytes 21504000 | tf_op jit(solution)/shard_map/filtered/pallas_call | solution.py:414
  33.5 1.6 %collective-permute-start.9 = (bf16[4,14,48,128]{3,2,1,0:T(8,128)(2,1)S(1)}, bf16[4,14,48,128]{3,2,1,0:T(8,128)(2,1)}, u32[]{:S(2)}, u32[]{:S(2)}) collective-permute-start(bf16[4,14,48,128]{3,2,1,0:T(8,128)(2,1)S(1)} %filtered.3.refs_0_), channel_id=1, source_target_pairs={{0,2},{1,3},{2,0},{3,1},{4,6},{5,7},{6,4},{7,5},{8,10},{9,11},{10,... | collective-permute-start | bytes 2064392 | tf_op jit(solution)/shard_map/ppermute | solution.py:585
  35.1 4.3 %collective-permute-start.6 = (bf16[2,8,48,128]{3,2,1,0:T(8,128)(2,1)}, bf16[2,8,48,128]{3,2,1,0:T(8,128)(2,1)S(1)}, u32[]{:S(2)}, u32[]{:S(2)}) collective-permute-start(bf16[2,8,48,128]{3,2,1,0:T(8,128)(2,1)} %collective-permute-done.2.refs_4_), channel_id=1, source_target_pairs={{0,8},{8,16},{12,4},{16,24},{20,12},{28,20},{1,9},{9,17},{13,5},{1... | collective-permute-start | bytes 589832 | tf_op jit(solution)/shard_map/ppermute | solution.py:578
  39.4 0.1 collective-permute-start.7
  39.5 3.7 %collective-permute-done.7 = f32[24,128]{1,0:T(8,128)S(1)} collective-permute-done((f32[24,128]{1,0:T(8,128)S(1)}, f32[24,128]{1,0:T(8,128)S(1)}, u32[]{:S(2)}, u32[]{:S(2)}) %collective-permute-start.7) | collective-permute-done | bytes 12320 | tf_op jit(solution)/shard_map/ppermute | solution.py:590
  43.2 0.0 collective-permute-done.6.refs_6_
  43.2 2.2 %collective-permute-start.10 = (f32[24,128]{1,0:T(8,128)S(1)}, f32[24,128]{1,0:T(8,128)S(1)}, u32[]{:S(2)}, u32[]{:S(2)}) collective-permute-start(f32[24,128]{1,0:T(8,128)S(1)} %add.9), channel_id=1, source_target_pairs={{0,8},{4,12},{8,0},{12,4},{16,24},{20,28},{24,16},{28,20},{1,9},{5... | collective-permute-start | bytes 36872 | tf_op jit(solution)/shard_map/ppermute | solution.py:590
  45.4 3.8 %filtered.2 = (bf16[2,10,48,128]{3,2,1,0:T(8,128)(2,1)S(1)}, bf16[2,10,48,128]{3,2,1,0:T(8,128)(2,1)S(1)}) custom-call(bf16[2,48,48,128]{3,2,1,0:T(8,128)(2,1)S(1)} %copy-done.1, f32[2,48,48]{2,1,0:T(8,128)S(1)} %copy-done.4, bf16[2,27,48,128]{3,2,1,0:T(8,128)(2,1)S(1)} %collective-permute-done.refs_2_, ...), custom_call_target="tpu_custom_call" | custom-call | flops 2457600 | bytes 15360000 | tf_op jit(solution)/shard_map/filtered/pallas_call | solution.py:414
  49.2 0.6 collective-permute-start.8
  49.8 0.0 collective-permute-done.10
  49.8 0.0 collective-permute-done.9.refs_2_
  49.8 0.1 collective-permute-start.11
  49.9 0.5 collective-permute-start.12
  50.4 3.6 %collective-permute-start.13 = (f32[24,128]{1,0:T(8,128)S(1)}, f32[24,128]{1,0:T(8,128)S(1)}, u32[]{:S(2)}, u32[]{:S(2)}) collective-permute-start(f32[24,128]{1,0:T(8,128)S(1)} %add.10), channel_id=1, source_target_pairs={{0,16},{4,20},{8,24},{12,28},{16,0},{20,4},{24,8},{28,12},{1,17},{... | collective-permute-start | bytes 36872 | tf_op jit(solution)/shard_map/ppermute | solution.py:590
  54.0 0.3 fusion
  54.4 1.3 %collective-permute-done.13 = f32[24,128]{1,0:T(8,128)S(1)} collective-permute-done((f32[24,128]{1,0:T(8,128)S(1)}, f32[24,128]{1,0:T(8,128)S(1)}, u32[]{:S(2)}, u32[]{:S(2)}) %collective-permute-start.13) | collective-permute-done | bytes 12320 | tf_op jit(solution)/shard_map/ppermute | solution.py:590
  55.7 0.0 collective-permute-done.12.refs_3_
  55.7 0.0 collective-permute-done.11.refs_1_
  55.7 2.1 %rotated.2 = (bf16[2,14,48,128]{3,2,1,0:T(8,128)(2,1)S(1)}, bf16[2,14,48,128]{3,2,1,0:T(8,128)(2,1)S(1)}) custom-call(bf16[4,14,48,128]{3,2,1,0:T(8,128)(2,1)S(1)} %filtered.3.refs_0_, bf16[4,14,48,128]{3,2,1,0:T(8,128)(2,1)S(1)} %collective-permute-done.11.refs_1_, bf16[4,14,48,128]{3,2,1,0:T(8,128)(2,1)} %collective-permute-done.9.refs_2_, ...), custom_call_target="tpu_custom_call" | custom-call | flops 22020096 | bytes 215040 | tf_op jit(solution)/shard_map/rotated/pallas_call | solution.py:460
  57.9 1.9 %collective-permute-start.20 = (bf16[2,14,48,128]{3,2,1,0:T(8,128)(2,1)S(1)}, bf16[2,14,48,128]{3,2,1,0:T(8,128)(2,1)S(1)}, u32[]{:S(2)}, u32[]{:S(2)}) collective-permute-start(bf16[2,14,48,128]{3,2,1,0:T(8,128)(2,1)S(1)} %get-tuple-element.57), channel_id=1, source_target_pairs={{0,4},{4,0},{8,12},{12,8},{16,20},{20,16},{24,28},{28,24},{1,5},{5... | collective-permute-start | bytes 1032200 | tf_op jit(solution)/shard_map/ppermute | solution.py:614
  59.8 0.0 collective-permute-done.8.refs_2_
  59.8 0.0 collective-permute-start.14
  59.8 0.5 collective-permute-start.16
  60.3 2.3 %collective-permute-start.19 = (bf16[2,10,48,128]{3,2,1,0:T(8,128)(2,1)S(1)}, bf16[2,10,48,128]{3,2,1,0:T(8,128)(2,1)S(1)}, u32[]{:S(2)}, u32[]{:S(2)}) collective-permute-start(bf16[2,10,48,128]{3,2,1,0:T(8,128)(2,1)S(1)} %get-tuple-element.66.a), channel_id=1, source_target_pairs={{0,2},{1,3},{2,0},{3,1},{4,6},{5,7},{6,4},{7,5},{8,10},{9,11},{10,... | collective-permute-start | bytes 737288 | tf_op jit(solution)/shard_map/ppermute | solution.py:616
  62.6 0.1 broadcast_in_dim.22.strength
  62.6 0.1 coefficients.1
  62.8 0.0 collective-permute-start.15
  62.8 1.2 %collective-permute-done.15 = bf16[16,128]{1,0:T(8,128)(2,1)S(1)} collective-permute-done((bf16[16,128]{1,0:T(8,128)(2,1)S(1)}, bf16[16,128]{1,0:T(8,128)(2,1)S(1)}, u32[]{:S(2)}, u32[]{:S(2)}) %collective-permute-start.15) | collective-permute-done | bytes 4128 | tf_op jit(solution)/shard_map/ppermute | solution.py:619
  64.0 0.2 collective-permute-start.21
  64.1 0.0 collective-permute-done.14.refs_3_
  64.1 0.0 collective-permute-done.16.refs_1_
  64.2 0.6 rotated.3
  64.7 0.5 collective-permute-start.18
  65.2 0.0 collective-permute-start.17
  65.2 3.6 %collective-permute-done.19.c = bf16[2,10,48,128]{3,2,1,0:T(8,128)(2,1)S(1)} collective-permute-done((bf16[2,10,48,128]{3,2,1,0:T(8,128)(2,1)S(1)}, bf16[2,10,48,128]{3,2,1,0:T(8,128)(2,1)S(1)}, u32[]{:S(2)}, u32[]{:S(2)}) %collective-permute-start.19) | collective-permute-done | bytes 245792 | tf_op jit(solution)/shard_map/ppermute | solution.py:616
  68.8 0.0 collective-permute-done.20.got1
  68.8 0.0 collective-permute-start.22
  68.8 0.1 collective-permute-done.17
  68.9 1.9 %nonlocal.1.term = f32[2,48,48,128]{3,2,1,0:T(8,128)S(1)} custom-call(bf16[16,128]{1,0:T(8,128)(2,1)S(1)} %get-tuple-element.72.a, bf16[16,128]{1,0:T(8,128)(2,1)S(1)} %get-tuple-element.71.b, bf16[16,128]{1,0:T(8,128)(2,1)S(1)} %get-tuple-element.70.c, bf16[16,128]{1,0:T(8,128)(2,1)S(1)} %get-tuple-element.69.d, bf16[4,128,128]{2,1,0:T(8,128)(2,1)S(1)} %copy.19.refs_4_.q, ...), custom_call_target="tpu_custom_call" | custom-call | flops 256 | bytes 256 | tf_op jit(solution)/shard_map/nonlocal/pallas_call | solution.py:253
  70.8 0.0 collective-permute-done.21.b
  70.8 0.0 collective-permute-done.22.d
  70.8 1.7 %assembled.1.before = bf16[2,48,48,128]{3,2,1,0:T(8,128)(2,1)} custom-call(f32[2,48,48,128]{3,2,1,0:T(8,128)S(1)} %nonlocal.1.term, bf16[2,14,48,128]{3,2,1,0:T(8,128)(2,1)S(1)} %get-tuple-element.65.keep1, bf16[2,14,48,128]{3,2,1,0:T(8,128)(2,1)S(1)} %collective-permute-done.20.got1, bf16[2,10,48,128]{3,2,1,0:T(8,128)(2,1)S(1)} %get-tuple-element.66.a, ...), custom_call_target="tpu_custom_call" | custom-call | flops 256 | bytes 256 | tf_op jit(solution)/shard_map/assembled/pallas_call | solution.py:513
  72.5 0.5 collective-permute-done.18.got2
  73.0 0.8 %finished.1 = bf16[2,48,48,128]{3,2,1,0:T(8,128)(2,1)} custom-call(f32[2,48,48,128]{3,2,1,0:T(8,128)S(1)} %nonlocal.1.term, bf16[2,10,48,128]{3,2,1,0:T(8,128)(2,1)S(1)} %collective-permute-done.18.got2, bf16[2,48,48,128]{3,2,1,0:T(8,128)(2,1)} %assembled.1.before), custom_call_target="tpu_custom_call", output_to_operand_aliasing={{}: (2, {})} | custom-call | flops 256 | bytes 256 | tf_op jit(solution)/shard_map/finished/pallas_call | solution.py:524
  (30 shorter events, 0.1 us)
Async XLA Ops:
  0.0 54.0 %copy-start = (bf16[12,128,128]{2,1,0:T(8,128)(2,1)S(1)}, bf16[12,128,128]{2,1,0:T(8,128)(2,1)}, u32[]{:S(2)}) copy-start(bf16[12,128,128]{2,1,0:T(8,128)(2,1)} %param.13) | copy-start | bytes 1179652
  0.0 20.9 %copy-start.3 = (bf16[8,2,48,48]{3,2,1,0:T(8,128)(2,1)S(1)}, bf16[8,2,48,48]{3,2,1,0:T(8,128)(2,1)}, u32[]{:S(2)}) copy-start(bf16[8,2,48,48]{3,2,1,0:T(8,128)(2,1)} %beta.3) | copy-start | bytes 221188
  0.0 20.8 %copy-start.7 = (s32[8]{0:T(128)S(1)}, s32[8]{0:T(128)}, u32[]{:S(2)}) copy-start(s32[8]{0:T(128)} %atoms.1) | copy-start | bytes 100
  2.2 19.2 %copy-start.1 = (bf16[2,48,48,128]{3,2,1,0:T(8,128)(2,1)S(1)}, bf16[2,48,48,128]{3,2,1,0:T(8,128)(2,1)}, u32[]{:S(2)}) copy-start(bf16[2,48,48,128]{3,2,1,0:T(8,128)(2,1)} %refs_0_.3) | copy-start | bytes 3538948
  2.2 19.2 %copy-start.4 = (f32[2,48,48]{2,1,0:T(8,128)S(1)}, f32[2,48,48]{2,1,0:T(8,128)}, u32[]{:S(2)}) copy-start(f32[2,48,48]{2,1,0:T(8,128)} %refs_1_.3) | copy-start | bytes 55300
  2.2 14.6 %collective-permute-start.1 = (bf16[2,19,48,128]{3,2,1,0:T(8,128)(2,1)S(1)}, bf16[2,19,48,128]{3,2,1,0:T(8,128)(2,1)}, u32[]{:S(2)}, u32[]{:S(2)}) collective-permute-start(bf16[2,19,48,128]{3,2,1,0:T(8,128)(2,1)S(1)} %get-tuple-element.38), channel_id=1, source_target_pairs={{0,4},{4,0},{8,12},{12,8},{16,20},{20,16},{24,28},{28,24},{1,5},{5... | collective-permute-start | bytes 1400840 | tf_op jit(solution)/shard_map/ppermute | solution.py:570
  5.2 23.9 %collective-permute-start = (bf16[2,27,48,128]{3,2,1,0:T(8,128)(2,1)}, bf16[2,27,48,128]{3,2,1,0:T(8,128)(2,1)S(1)}, u32[]{:S(2)}, u32[]{:S(2)}) collective-permute-start(bf16[2,27,48,128]{3,2,1,0:T(8,128)(2,1)} %get-tuple-element.37), channel_id=1, source_target_pairs={{4,12},{8,0},{12,20},{16,8},{20,28},{24,16},{5,13},{9,1},{13,21},{... | collective-permute-start | bytes 1990664 | tf_op jit(solution)/shard_map/ppermute | solution.py:571
  8.2 13.1 %collective-permute-start.4 = (bf16[8,48,48]{2,1,0:T(8,128)(2,1)}, bf16[8,48,48]{2,1,0:T(8,128)(2,1)S(1)}, u32[]{:S(2)}, u32[]{:S(2)}) collective-permute-start(bf16[8,48,48]{2,1,0:T(8,128)(2,1)} %get-tuple-element.42), channel_id=1, source_target_pairs={{0,4},{4,0},{8,12},{12,8},{16,20},{20,16},{24,28},{28,24},{1,5},{5... | collective-permute-start | bytes 110600 | tf_op jit(solution)/shard_map/ppermute | solution.py:567
  11.0 10.3 %collective-permute-start.5 = (bf16[8,48,48]{2,1,0:T(8,128)(2,1)S(1)}, bf16[8,48,48]{2,1,0:T(8,128)(2,1)S(1)}, u32[]{:S(2)}, u32[]{:S(2)}) collective-permute-start(bf16[8,48,48]{2,1,0:T(8,128)(2,1)S(1)} %get-tuple-element.43), channel_id=1, source_target_pairs={{4,8},{8,4},{12,16},{16,12},{20,24},{24,20},{5,9},{9,5},{13,17},{1... | collective-permute-start | bytes 110600 | tf_op jit(solution)/shard_map/ppermute | solution.py:569
  16.9 12.3 %collective-permute-start.3 = (bf16[2,19,48,128]{3,2,1,0:T(8,128)(2,1)}, bf16[2,19,48,128]{3,2,1,0:T(8,128)(2,1)S(1)}, u32[]{:S(2)}, u32[]{:S(2)}) collective-permute-start(bf16[2,19,48,128]{3,2,1,0:T(8,128)(2,1)} %collective-permute-done.1.refs_3_), channel_id=1, source_target_pairs={{0,8},{8,16},{12,4},{16,24},{20,12},{28,20},{1,9},{9,17},{13,5},{1... | collective-permute-start | bytes 1400840 | tf_op jit(solution)/shard_map/ppermute | solution.py:576
  20.9 5.8 %collective-permute-start.2 = (bf16[2,8,48,128]{3,2,1,0:T(8,128)(2,1)S(1)}, bf16[2,8,48,128]{3,2,1,0:T(8,128)(2,1)}, u32[]{:S(2)}, u32[]{:S(2)}) collective-permute-start(bf16[2,8,48,128]{3,2,1,0:T(8,128)(2,1)S(1)} %get-tuple-element.41), channel_id=1, source_target_pairs={{0,4},{4,0},{8,12},{12,8},{16,20},{20,16},{24,28},{28,24},{1,5},{5... | collective-permute-start | bytes 589832 | tf_op jit(solution)/shard_map/ppermute | solution.py:577
  24.4 9.1 %copy-start.5 = (bf16[2,48,24,48]{3,2,1,0:T(8,128)(2,1)}, bf16[2,48,24,48]{3,2,1,0:T(8,128)(2,1)S(1)}, u32[]{:S(2)}) copy-start(bf16[2,48,24,48]{3,2,1,0:T(8,128)(2,1)S(1)} %get-tuple-element.64.weights) | copy-start | bytes 663556
  29.1 4.4 %copy-start.2 = (bf16[2,19,48,128]{3,2,1,0:T(8,128)(2,1)}, bf16[2,19,48,128]{3,2,1,0:T(8,128)(2,1)S(1)}, u32[]{:S(2)}) copy-start(bf16[2,19,48,128]{3,2,1,0:T(8,128)(2,1)S(1)} %collective-permute-done.3.refs_5_.refs_4_) | copy-start | bytes 1400836
  33.5 16.3 %collective-permute-start.9 = (bf16[4,14,48,128]{3,2,1,0:T(8,128)(2,1)S(1)}, bf16[4,14,48,128]{3,2,1,0:T(8,128)(2,1)}, u32[]{:S(2)}, u32[]{:S(2)}) collective-permute-start(bf16[4,14,48,128]{3,2,1,0:T(8,128)(2,1)S(1)} %filtered.3.refs_0_), channel_id=1, source_target_pairs={{0,2},{1,3},{2,0},{3,1},{4,6},{5,7},{6,4},{7,5},{8,10},{9,11},{10,... | collective-permute-start | bytes 2064392 | tf_op jit(solution)/shard_map/ppermute | solution.py:585
  35.1 8.1 %collective-permute-start.6 = (bf16[2,8,48,128]{3,2,1,0:T(8,128)(2,1)}, bf16[2,8,48,128]{3,2,1,0:T(8,128)(2,1)S(1)}, u32[]{:S(2)}, u32[]{:S(2)}) collective-permute-start(bf16[2,8,48,128]{3,2,1,0:T(8,128)(2,1)} %collective-permute-done.2.refs_4_), channel_id=1, source_target_pairs={{0,8},{8,16},{12,4},{16,24},{20,12},{28,20},{1,9},{9,17},{13,5},{1... | collective-permute-start | bytes 589832 | tf_op jit(solution)/shard_map/ppermute | solution.py:578
  39.4 3.8 %collective-permute-start.7 = (f32[24,128]{1,0:T(8,128)S(1)}, f32[24,128]{1,0:T(8,128)S(1)}, u32[]{:S(2)}, u32[]{:S(2)}) collective-permute-start(f32[24,128]{1,0:T(8,128)S(1)} %get-tuple-element.46), channel_id=1, source_target_pairs={{0,4},{4,0},{8,12},{12,8},{16,20},{20,16},{24,28},{28,24},{1,5},{5... | collective-permute-start | bytes 36872 | tf_op jit(solution)/shard_map/ppermute | solution.py:590
  43.2 2.2 %copy-start.8 = (bf16[2,8,48,128]{3,2,1,0:T(8,128)(2,1)}, bf16[2,8,48,128]{3,2,1,0:T(8,128)(2,1)S(1)}, u32[]{:S(2)}) copy-start(bf16[2,8,48,128]{3,2,1,0:T(8,128)(2,1)S(1)} %collective-permute-done.6.refs_6_) | copy-start | bytes 589828
  43.2 6.6 %collective-permute-start.10 = (f32[24,128]{1,0:T(8,128)S(1)}, f32[24,128]{1,0:T(8,128)S(1)}, u32[]{:S(2)}, u32[]{:S(2)}) collective-permute-start(f32[24,128]{1,0:T(8,128)S(1)} %add.9), channel_id=1, source_target_pairs={{0,8},{4,12},{8,0},{12,4},{16,24},{20,28},{24,16},{28,20},{1,9},{5... | collective-permute-start | bytes 36872 | tf_op jit(solution)/shard_map/ppermute | solution.py:590
  45.4 5.0 %copy-start.10 = (s32[12,2]{0,1:T(2,128)S(1)}, s32[12,2]{0,1:T(2,128)}, u32[]{:S(2)}) copy-start(s32[12,2]{0,1:T(2,128)} %param.12) | copy-start | bytes 292
  49.2 10.6 %collective-permute-start.8 = (bf16[2,10,48,128]{3,2,1,0:T(8,128)(2,1)S(1)}, bf16[2,10,48,128]{3,2,1,0:T(8,128)(2,1)S(1)}, u32[]{:S(2)}, u32[]{:S(2)}) collective-permute-start(bf16[2,10,48,128]{3,2,1,0:T(8,128)(2,1)S(1)} %get-tuple-element.49.refs_0_), channel_id=1, source_target_pairs={{0,2},{1,3},{2,0},{3,1},{4,6},{5,7},{6,4},{7,5},{8,10},{9,11},{10,... | collective-permute-start | bytes 737288 | tf_op jit(solution)/shard_map/ppermute | solution.py:604
  49.8 5.9 %collective-permute-start.11 = (bf16[4,14,48,128]{3,2,1,0:T(8,128)(2,1)S(1)}, bf16[4,14,48,128]{3,2,1,0:T(8,128)(2,1)S(1)}, u32[]{:S(2)}, u32[]{:S(2)}) collective-permute-start(bf16[4,14,48,128]{3,2,1,0:T(8,128)(2,1)S(1)} %filtered.3.refs_0_), channel_id=1, source_target_pairs={{0,1},{1,0},{2,3},{3,2},{4,5},{5,4},{6,7},{7,6},{8,9},{9,8},{10,11... | collective-permute-start | bytes 2064392 | tf_op jit(solution)/shard_map/ppermute | solution.py:608
  49.9 5.8 %collective-permute-start.12 = (bf16[4,14,48,128]{3,2,1,0:T(8,128)(2,1)}, bf16[4,14,48,128]{3,2,1,0:T(8,128)(2,1)S(1)}, u32[]{:S(2)}, u32[]{:S(2)}) collective-permute-start(bf16[4,14,48,128]{3,2,1,0:T(8,128)(2,1)} %collective-permute-done.9.refs_2_), channel_id=1, source_target_pairs={{0,1},{1,0},{2,3},{3,2},{4,5},{5,4},{6,7},{7,6},{8,9},{9,8},{10,11... | collective-permute-start | bytes 2064392 | tf_op jit(solution)/shard_map/ppermute | solution.py:609
  50.4 5.3 %collective-permute-start.13 = (f32[24,128]{1,0:T(8,128)S(1)}, f32[24,128]{1,0:T(8,128)S(1)}, u32[]{:S(2)}, u32[]{:S(2)}) collective-permute-start(f32[24,128]{1,0:T(8,128)S(1)} %add.10), channel_id=1, source_target_pairs={{0,16},{4,20},{8,24},{12,28},{16,0},{20,4},{24,8},{28,12},{1,17},{... | collective-permute-start | bytes 36872 | tf_op jit(solution)/shard_map/ppermute | solution.py:590
  55.7 6.9 %copy-start.9 = (f32[8]{0:T(128)S(1)}, f32[8]{0:T(128)}, u32[]{:S(2)}) copy-start(f32[8]{0:T(128)} %param.10) | copy-start | bytes 100
  57.9 11.0 %copy-start.6 = (bf16[2,48,24,48]{3,2,1,0:T(8,128)(2,1)S(1)}, bf16[2,48,24,48]{3,2,1,0:T(8,128)(2,1)}, u32[]{:S(2)}) copy-start(bf16[2,48,24,48]{3,2,1,0:T(8,128)(2,1)} %copy-done.5) | copy-start | bytes 663556
  57.9 10.9 %collective-permute-start.20 = (bf16[2,14,48,128]{3,2,1,0:T(8,128)(2,1)S(1)}, bf16[2,14,48,128]{3,2,1,0:T(8,128)(2,1)S(1)}, u32[]{:S(2)}, u32[]{:S(2)}) collective-permute-start(bf16[2,14,48,128]{3,2,1,0:T(8,128)(2,1)S(1)} %get-tuple-element.57), channel_id=1, source_target_pairs={{0,4},{4,0},{8,12},{12,8},{16,20},{20,16},{24,28},{28,24},{1,5},{5... | collective-permute-start | bytes 1032200 | tf_op jit(solution)/shard_map/ppermute | solution.py:614
  59.8 4.4 %collective-permute-start.14 = (bf16[2,10,48,128]{3,2,1,0:T(8,128)(2,1)S(1)}, bf16[2,10,48,128]{3,2,1,0:T(8,128)(2,1)S(1)}, u32[]{:S(2)}, u32[]{:S(2)}) collective-permute-start(bf16[2,10,48,128]{3,2,1,0:T(8,128)(2,1)S(1)} %collective-permute-done.8.refs_2_), channel_id=1, source_target_pairs={{0,1},{1,0},{2,3},{3,2},{4,5},{5,4},{6,7},{7,6},{8,9},{9,8},{10,11... | collective-permute-start | bytes 737288 | tf_op jit(solution)/shard_map/ppermute | solution.py:617
  59.8 4.4 %collective-permute-start.16 = (bf16[2,10,48,128]{3,2,1,0:T(8,128)(2,1)S(1)}, bf16[2,10,48,128]{3,2,1,0:T(8,128)(2,1)S(1)}, u32[]{:S(2)}, u32[]{:S(2)}) collective-permute-start(bf16[2,10,48,128]{3,2,1,0:T(8,128)(2,1)S(1)} %get-tuple-element.49.refs_0_), channel_id=1, source_target_pairs={{0,1},{1,0},{2,3},{3,2},{4,5},{5,4},{6,7},{7,6},{8,9},{9,8},{10,11... | collective-permute-start | bytes 737288 | tf_op jit(solution)/shard_map/ppermute | solution.py:602
  60.3 8.5 %collective-permute-start.19 = (bf16[2,10,48,128]{3,2,1,0:T(8,128)(2,1)S(1)}, bf16[2,10,48,128]{3,2,1,0:T(8,128)(2,1)S(1)}, u32[]{:S(2)}, u32[]{:S(2)}) collective-permute-start(bf16[2,10,48,128]{3,2,1,0:T(8,128)(2,1)S(1)} %get-tuple-element.66.a), channel_id=1, source_target_pairs={{0,2},{1,3},{2,0},{3,1},{4,6},{5,7},{6,4},{7,5},{8,10},{9,11},{10,... | collective-permute-start | bytes 737288 | tf_op jit(solution)/shard_map/ppermute | solution.py:616
  62.8 1.2 %collective-permute-start.15 = (bf16[16,128]{1,0:T(8,128)(2,1)S(1)}, bf16[16,128]{1,0:T(8,128)(2,1)S(1)}, u32[]{:S(2)}, u32[]{:S(2)}) collective-permute-start(bf16[16,128]{1,0:T(8,128)(2,1)S(1)} %coefficients.1), channel_id=1, source_target_pairs={{0,1},{1,0},{2,3},{3,2},{4,5},{5,4},{6,7},{7,6},{8,9},{9,8},{10,11... | collective-permute-start | bytes 12296 | tf_op jit(solution)/shard_map/ppermute | solution.py:619
  64.0 6.8 %collective-permute-start.21 = (bf16[2,10,48,128]{3,2,1,0:T(8,128)(2,1)S(1)}, bf16[2,10,48,128]{3,2,1,0:T(8,128)(2,1)S(1)}, u32[]{:S(2)}, u32[]{:S(2)}) collective-permute-start(bf16[2,10,48,128]{3,2,1,0:T(8,128)(2,1)S(1)} %get-tuple-element.66.a), channel_id=1, source_target_pairs={{0,1},{1,0},{2,3},{3,2},{4,5},{5,4},{6,7},{7,6},{8,9},{9,8},{10,11... | collective-permute-start | bytes 737288 | tf_op jit(solution)/shard_map/ppermute | solution.py:603
  64.7 8.3 %collective-permute-start.18 = (bf16[2,10,48,128]{3,2,1,0:T(8,128)(2,1)S(1)}, bf16[2,10,48,128]{3,2,1,0:T(8,128)(2,1)S(1)}, u32[]{:S(2)}, u32[]{:S(2)}) collective-permute-start(bf16[2,10,48,128]{3,2,1,0:T(8,128)(2,1)S(1)} %rotated.3), channel_id=1, source_target_pairs={{0,4},{4,0},{8,12},{12,8},{16,20},{20,16},{24,28},{28,24},{1,5},{5... | collective-permute-start | bytes 737288 | tf_op jit(solution)/shard_map/ppermute | solution.py:622
  65.2 3.7 %collective-permute-start.17 = (bf16[32,128]{1,0:T(8,128)(2,1)S(1)}, bf16[32,128]{1,0:T(8,128)(2,1)S(1)}, u32[]{:S(2)}, u32[]{:S(2)}) collective-permute-start(bf16[32,128]{1,0:T(8,128)(2,1)S(1)} %pad_maximum_fusion), channel_id=1, source_target_pairs={{0,2},{1,3},{2,0},{3,1},{4,6},{5,7},{6,4},{7,5},{8,10},{9,11},{10,... | collective-permute-start | bytes 24584 | tf_op jit(solution)/shard_map/ppermute | solution.py:624
  68.8 2.0 %collective-permute-start.22 = (bf16[2,10,48,128]{3,2,1,0:T(8,128)(2,1)S(1)}, bf16[2,10,48,128]{3,2,1,0:T(8,128)(2,1)S(1)}, u32[]{:S(2)}, u32[]{:S(2)}) collective-permute-start(bf16[2,10,48,128]{3,2,1,0:T(8,128)(2,1)S(1)} %collective-permute-done.19.c), channel_id=1, source_target_pairs={{0,1},{1,0},{2,3},{3,2},{4,5},{5,4},{6,7},{7,6},{8,9},{9,8},{10,11... | collective-permute-start | bytes 737288 | tf_op jit(solution)/shard_map/ppermute | solution.py:628

commit v21 on v20

--- a/solution.py
+++ b/solution.py
@@ -546,7 +546,7 @@
     x = lax.rem(place, 2)
     half = width_x // 2
     window = half + 2
-    rows1 = half * 7 // 24 * 2
+    rows1 = half // 4 * 2
     rows2 = half - rows1
     early = rows1 + 4
 

time: 74.6 us -> 75 us (level)
  waiting for transfers between devices: 20.1 us -> 20.9 us
    ppermute x1, waiting for transfers between devices: 0.01 us -> 2.34 us  [shards(): got1 = lax.ppermute(give1, 'space', swap)]
    ppermute x1, waiting for transfers between devices: 2.43 us -> 0.86 us  [shards(): zf1 = lax.ppermute(xr1, 'space', other_way)]
    ppermute x1, starting transfers between devices: 4.28 us -> 5.73 us  [shards(): zf2 = lax.ppermute(xr2, 'space', other_way)]
    ppermute x1, waiting for transfers between devices: 5.14 us -> 4.02 us  [shards(): xr1 = lax.ppermute(to_x, 'space', swap)]
    ppermute x1, waiting for transfers between devices: 0.49 us -> 1.41 us  [shards(): got2 = lax.ppermute(give2, 'space', swap)]
    ppermute x1, waiting for transfers between devices: 3.55 us -> 2.73 us  [shards(): yk = lax.ppermute(keep_y, 'orb', across)]
    ppermute x3, starting transfers between devices: 5.91 us -> 5.11 us  [added(): return values + lax.ppermute(values, 'space', pairs)]
    ppermute x1, starting transfers between devices: 2.27 us -> 1.52 us  [shards(): yk = lax.ppermute(keep_y, 'orb', across)]
  transfers between devices with their start and end apart: 23 -> 23, of which waited for: 9 -> 10; matrix products, arithmetic and copies ran while one was open for 1% -> 1% of each run, Pallas kernels for 20% -> 21%
where the time goes in v21:
time: 75 us; the launch traced here: 74.7 us
  starting transfers between devices  30.3 us (40%)
  Pallas kernels  22.4 us (30%)
  waiting for transfers between devices  20.9 us (28%)
    pallas_call x2, Pallas kernels, filtered(): pl.pallas_call(functools.partial(filter_kernel, slabs, start, parts, join...  8.17 us
    ppermute x1, starting transfers between devices, shards(): zf2 = lax.ppermute(xr2, 'space', other_way)  5.73 us
    ppermute x3, waiting for transfers between devices, added(): return values + lax.ppermute(values, 'space', pairs)  5.32 us
    ppermute x3, starting transfers between devices, added(): return values + lax.ppermute(values, 'space', pairs)  5.11 us
    ppermute x1, waiting for transfers between devices, shards(): xr1 = lax.ppermute(to_x, 'space', swap)  4.02 us
    ppermute x1, starting transfers between devices, shards(): zf1 = lax.ppermute(xr1, 'space', other_way)  3.97 us
    pallas_call x1, Pallas kernels, partials(): pl.pallas_call(functools.partial(partial_kernel, count), out_shape=(jax.S...  3.04 us
    ppermute x1, starting transfers between devices, shards(): xr1 = lax.ppermute(to_x, 'space', swap)  3 us
  transfers between devices with their start and end apart: 23, of which 10 were waited for; matrix products, arithmetic and copies ran while one was open for 1% of the time, Pallas kernels for 21%

profile of v21, /device:TPU:0, one launch (start us, length us, event | category | flops | bytes accessed | tf_op | source)
XLA Modules:
  0.0 74.7 jit_solution(15469190727209186121)
XLA Ops:
  0.0 2.2 %prepared.1 = (bf16[2,17,48,128]{3,2,1,0:T(8,128)(2,1)S(1)}, bf16[2,27,48,128]{3,2,1,0:T(8,128)(2,1)}) custom-call(bf16[2,48,48,128]{3,2,1,0:T(8,128)(2,1)} %refs_0_.3, f32[2,48,48]{2,1,0:T(8,128)} %refs_1_.3), custom_call_target="tpu_custom_call" | custom-call | flops 256 | bytes 256 | tf_op jit(solution)/shard_map/prepared/pallas_call | solution.py:81
  2.2 0.0 copy-start.1
  2.2 0.0 copy-start.4
  2.2 3.0 %collective-permute-start.1 = (bf16[2,17,48,128]{3,2,1,0:T(8,128)(2,1)S(1)}, bf16[2,17,48,128]{3,2,1,0:T(8,128)(2,1)}, u32[]{:S(2)}, u32[]{:S(2)}) collective-permute-start(bf16[2,17,48,128]{3,2,1,0:T(8,128)(2,1)S(1)} %get-tuple-element.38), channel_id=1, source_target_pairs={{0,4},{4,0},{8,12},{12,8},{16,20},{20,16},{24,28},{28,24},{1,5},{5... | collective-permute-start | bytes 1253384 | tf_op jit(solution)/shard_map/ppermute | solution.py:570
  5.2 1.3 %collective-permute-start = (bf16[2,27,48,128]{3,2,1,0:T(8,128)(2,1)}, bf16[2,27,48,128]{3,2,1,0:T(8,128)(2,1)S(1)}, u32[]{:S(2)}, u32[]{:S(2)}) collective-permute-start(bf16[2,27,48,128]{3,2,1,0:T(8,128)(2,1)} %get-tuple-element.37), channel_id=1, source_target_pairs={{4,12},{8,0},{12,20},{16,8},{20,28},{24,16},{5,13},{9,1},{13,21},{... | collective-permute-start | bytes 1990664 | tf_op jit(solution)/shard_map/ppermute | solution.py:571
  6.5 1.8 %packed.1 = (bf16[2,10,48,128]{3,2,1,0:T(8,128)(2,1)S(1)}, bf16[8,48,48]{2,1,0:T(8,128)(2,1)}, bf16[8,48,48]{2,1,0:T(8,128)(2,1)}) custom-call(bf16[2,48,48,128]{3,2,1,0:T(8,128)(2,1)} %refs_0_.3, bf16[8,2,48,48]{3,2,1,0:T(8,128)(2,1)} %beta.3), custom_call_target="tpu_custom_call" | custom-call | flops 256 | bytes 256 | tf_op jit(solution)/shard_map/packed/pallas_call | solution.py:114
  8.3 2.8 %collective-permute-start.4 = (bf16[8,48,48]{2,1,0:T(8,128)(2,1)}, bf16[8,48,48]{2,1,0:T(8,128)(2,1)S(1)}, u32[]{:S(2)}, u32[]{:S(2)}) collective-permute-start(bf16[8,48,48]{2,1,0:T(8,128)(2,1)} %get-tuple-element.42), channel_id=1, source_target_pairs={{0,4},{4,0},{8,12},{12,8},{16,20},{20,16},{24,28},{28,24},{1,5},{5... | collective-permute-start | bytes 110600 | tf_op jit(solution)/shard_map/ppermute | solution.py:567
  11.1 0.7 collective-permute-start.5
  11.8 4.0 %collective-permute-done.1.refs_3_ = bf16[2,17,48,128]{3,2,1,0:T(8,128)(2,1)} collective-permute-done((bf16[2,17,48,128]{3,2,1,0:T(8,128)(2,1)S(1)}, bf16[2,17,48,128]{3,2,1,0:T(8,128)(2,1)}, u32[]{:S(2)}, u32[]{:S(2)}) %collective-permute-start.1) | collective-permute-done | bytes 417824 | tf_op jit(solution)/shard_map/ppermute | solution.py:570
  15.8 4.0 %collective-permute-start.3 = (bf16[2,17,48,128]{3,2,1,0:T(8,128)(2,1)}, bf16[2,17,48,128]{3,2,1,0:T(8,128)(2,1)S(1)}, u32[]{:S(2)}, u32[]{:S(2)}) collective-permute-start(bf16[2,17,48,128]{3,2,1,0:T(8,128)(2,1)} %collective-permute-done.1.refs_3_), channel_id=1, source_target_pairs={{0,8},{8,16},{12,4},{16,24},{20,12},{28,20},{1,9},{9,17},{13,5},{1... | collective-permute-start | bytes 1253384 | tf_op jit(solution)/shard_map/ppermute | solution.py:576
  19.8 0.1 collective-permute-start.2
  19.9 0.1 broadcast_select_fusion
  20.0 0.3 convolution_bitcast_fusion.gram
  20.3 0.0 collective-permute-done.4.b_x
  20.3 0.0 collective-permute-done.5.b_d
  20.3 0.0 copy-done.1
  20.3 3.0 %partials.1 = (f32[24,128]{1,0:T(8,128)S(1)}, bf16[2,48,24,48]{3,2,1,0:T(8,128)(2,1)S(1)}) custom-call(s32[8]{0:T(128)S(1)} %copy-done.7, bf16[2,48,48,128]{3,2,1,0:T(8,128)(2,1)S(1)} %copy-done.1, bf16[8,2,48,48]{3,2,1,0:T(8,128)(2,1)S(1)} %copy-done.2, bf16[8,48,48]{2,1,0:T(8,128)(2,1)S(1)} %collective-permute-done.4.b_x, ...), custom_call_target="tpu_custom_call" | custom-call | flops 256 | bytes 256 | tf_op jit(solution)/shard_map/partials/pallas_call | solution.py:178
  23.4 2.8 %collective-permute-done.2.refs_4_ = bf16[2,10,48,128]{3,2,1,0:T(8,128)(2,1)} collective-permute-done((bf16[2,10,48,128]{3,2,1,0:T(8,128)(2,1)S(1)}, bf16[2,10,48,128]{3,2,1,0:T(8,128)(2,1)}, u32[]{:S(2)}, u32[]{:S(2)}) %collective-permute-start.2) | collective-permute-done | bytes 245792 | tf_op jit(solution)/shard_map/ppermute | solution.py:577
  26.2 0.9 %collective-permute-done.3.refs_5_.refs_4_ = bf16[2,17,48,128]{3,2,1,0:T(8,128)(2,1)S(1)} collective-permute-done((bf16[2,17,48,128]{3,2,1,0:T(8,128)(2,1)}, bf16[2,17,48,128]{3,2,1,0:T(8,128)(2,1)S(1)}, u32[]{:S(2)}, u32[]{:S(2)}) %collective-permute-start.3) | collective-permute-done | bytes 417824 | tf_op jit(solution)/shard_map/ppermute | solution.py:576
  27.0 0.0 collective-permute-done.refs_2_
  27.0 4.0 %filtered.3.refs_0_ = bf16[4,12,48,128]{3,2,1,0:T(8,128)(2,1)S(1)} custom-call(bf16[2,48,48,128]{3,2,1,0:T(8,128)(2,1)S(1)} %copy-done.1, f32[2,48,48]{2,1,0:T(8,128)S(1)} %copy-done.4, bf16[2,27,48,128]{3,2,1,0:T(8,128)(2,1)S(1)} %collective-permute-done.refs_2_, bf16[2,17,48,128]{3,2,1,0:T(8,128)(2,1)} %collective-permute-done.1.refs_3_, ...), custom_call_target="tpu_custom_call" | custom-call | flops 2949120 | bytes 18432000 | tf_op jit(solution)/shard_map/filtered/pallas_call | solution.py:414
  31.0 1.6 %collective-permute-start.9 = (bf16[4,12,48,128]{3,2,1,0:T(8,128)(2,1)S(1)}, bf16[4,12,48,128]{3,2,1,0:T(8,128)(2,1)}, u32[]{:S(2)}, u32[]{:S(2)}) collective-permute-start(bf16[4,12,48,128]{3,2,1,0:T(8,128)(2,1)S(1)} %filtered.3.refs_0_), channel_id=1, source_target_pairs={{0,2},{1,3},{2,0},{3,1},{4,6},{5,7},{6,4},{7,5},{8,10},{9,11},{10,... | collective-permute-start | bytes 1769480 | tf_op jit(solution)/shard_map/ppermute | solution.py:585
  32.6 5.7 %collective-permute-start.6 = (bf16[2,10,48,128]{3,2,1,0:T(8,128)(2,1)}, bf16[2,10,48,128]{3,2,1,0:T(8,128)(2,1)S(1)}, u32[]{:S(2)}, u32[]{:S(2)}) collective-permute-start(bf16[2,10,48,128]{3,2,1,0:T(8,128)(2,1)} %collective-permute-done.2.refs_4_), channel_id=1, source_target_pairs={{0,8},{8,16},{12,4},{16,24},{20,12},{28,20},{1,9},{9,17},{13,5},{1... | collective-permute-start | bytes 737288 | tf_op jit(solution)/shard_map/ppermute | solution.py:578
  38.3 0.1 collective-permute-start.7
  38.4 3.7 %collective-permute-done.7 = f32[24,128]{1,0:T(8,128)S(1)} collective-permute-done((f32[24,128]{1,0:T(8,128)S(1)}, f32[24,128]{1,0:T(8,128)S(1)}, u32[]{:S(2)}, u32[]{:S(2)}) %collective-permute-start.7) | collective-permute-done | bytes 12320 | tf_op jit(solution)/shard_map/ppermute | solution.py:590
  42.1 0.2 collective-permute-done.6.refs_6_
  42.3 2.4 %collective-permute-start.10 = (f32[24,128]{1,0:T(8,128)S(1)}, f32[24,128]{1,0:T(8,128)S(1)}, u32[]{:S(2)}, u32[]{:S(2)}) collective-permute-start(f32[24,128]{1,0:T(8,128)S(1)} %add.9), channel_id=1, source_target_pairs={{0,8},{4,12},{8,0},{12,4},{16,24},{20,28},{24,16},{28,20},{1,9},{5... | collective-permute-start | bytes 36872 | tf_op jit(solution)/shard_map/ppermute | solution.py:590
  44.7 4.2 %filtered.2 = (bf16[2,12,48,128]{3,2,1,0:T(8,128)(2,1)S(1)}, bf16[2,12,48,128]{3,2,1,0:T(8,128)(2,1)S(1)}) custom-call(bf16[2,48,48,128]{3,2,1,0:T(8,128)(2,1)S(1)} %copy-done.1, f32[2,48,48]{2,1,0:T(8,128)S(1)} %copy-done.4, bf16[2,27,48,128]{3,2,1,0:T(8,128)(2,1)S(1)} %collective-permute-done.refs_2_, ...), custom_call_target="tpu_custom_call" | custom-call | flops 2949120 | bytes 18432000 | tf_op jit(solution)/shard_map/filtered/pallas_call | solution.py:414
  48.9 0.6 collective-permute-start.8
  49.5 0.0 collective-permute-done.10
  49.5 0.0 collective-permute-done.9.refs_2_
  49.5 0.1 collective-permute-start.11
  49.6 0.5 collective-permute-start.12
  50.1 2.7 %collective-permute-start.13 = (f32[24,128]{1,0:T(8,128)S(1)}, f32[24,128]{1,0:T(8,128)S(1)}, u32[]{:S(2)}, u32[]{:S(2)}) collective-permute-start(f32[24,128]{1,0:T(8,128)S(1)} %add.10), channel_id=1, source_target_pairs={{0,16},{4,20},{8,24},{12,28},{16,0},{20,4},{24,8},{28,12},{1,17},{... | collective-permute-start | bytes 36872 | tf_op jit(solution)/shard_map/ppermute | solution.py:590
  52.8 0.3 fusion
  53.1 1.6 %collective-permute-done.13 = f32[24,128]{1,0:T(8,128)S(1)} collective-permute-done((f32[24,128]{1,0:T(8,128)S(1)}, f32[24,128]{1,0:T(8,128)S(1)}, u32[]{:S(2)}, u32[]{:S(2)}) %collective-permute-start.13) | collective-permute-done | bytes 12320 | tf_op jit(solution)/shard_map/ppermute | solution.py:590
  54.8 0.0 collective-permute-done.12.refs_3_
  54.8 0.0 collective-permute-done.11.refs_1_
  54.8 2.0 %rotated.2 = (bf16[2,12,48,128]{3,2,1,0:T(8,128)(2,1)S(1)}, bf16[2,12,48,128]{3,2,1,0:T(8,128)(2,1)S(1)}) custom-call(bf16[4,12,48,128]{3,2,1,0:T(8,128)(2,1)S(1)} %filtered.3.refs_0_, bf16[4,12,48,128]{3,2,1,0:T(8,128)(2,1)S(1)} %collective-permute-done.11.refs_1_, bf16[4,12,48,128]{3,2,1,0:T(8,128)(2,1)} %collective-permute-done.9.refs_2_, ...), custom_call_target="tpu_custom_call" | custom-call | flops 18874368 | bytes 184320 | tf_op jit(solution)/shard_map/rotated/pallas_call | solution.py:460
  56.8 0.0 collective-permute-done.8.refs_2_
  56.8 0.1 collective-permute-start.14
  56.9 0.5 collective-permute-start.16
  57.4 1.5 %collective-permute-start.19 = (bf16[2,12,48,128]{3,2,1,0:T(8,128)(2,1)S(1)}, bf16[2,12,48,128]{3,2,1,0:T(8,128)(2,1)S(1)}, u32[]{:S(2)}, u32[]{:S(2)}) collective-permute-start(bf16[2,12,48,128]{3,2,1,0:T(8,128)(2,1)S(1)} %get-tuple-element.66.a), channel_id=1, source_target_pairs={{0,2},{1,3},{2,0},{3,1},{4,6},{5,7},{6,4},{7,5},{8,10},{9,11},{10,... | collective-permute-start | bytes 884744 | tf_op jit(solution)/shard_map/ppermute | solution.py:616
  58.9 1.4 %collective-permute-start.20 = (bf16[2,12,48,128]{3,2,1,0:T(8,128)(2,1)S(1)}, bf16[2,12,48,128]{3,2,1,0:T(8,128)(2,1)S(1)}, u32[]{:S(2)}, u32[]{:S(2)}) collective-permute-start(bf16[2,12,48,128]{3,2,1,0:T(8,128)(2,1)S(1)} %get-tuple-element.57), channel_id=1, source_target_pairs={{0,4},{4,0},{8,12},{12,8},{16,20},{20,16},{24,28},{28,24},{1,5},{5... | collective-permute-start | bytes 884744 | tf_op jit(solution)/shard_map/ppermute | solution.py:614
  60.3 0.1 broadcast_in_dim.22.strength
  60.4 0.1 coefficients.1
  60.5 0.0 collective-permute-start.15
  60.6 1.2 %collective-permute-done.15 = bf16[16,128]{1,0:T(8,128)(2,1)S(1)} collective-permute-done((bf16[16,128]{1,0:T(8,128)(2,1)S(1)}, bf16[16,128]{1,0:T(8,128)(2,1)S(1)}, u32[]{:S(2)}, u32[]{:S(2)}) %collective-permute-start.15) | collective-permute-done | bytes 4128 | tf_op jit(solution)/shard_map/ppermute | solution.py:619
  61.7 0.2 collective-permute-start.21
  61.9 0.0 collective-permute-done.14.refs_3_
  61.9 0.0 collective-permute-done.16.refs_1_
  61.9 0.6 rotated.3
  62.5 0.7 collective-permute-start.18
  63.2 0.5 collective-permute-start.17
  63.8 2.7 %collective-permute-done.19.c = bf16[2,12,48,128]{3,2,1,0:T(8,128)(2,1)S(1)} collective-permute-done((bf16[2,12,48,128]{3,2,1,0:T(8,128)(2,1)S(1)}, bf16[2,12,48,128]{3,2,1,0:T(8,128)(2,1)S(1)}, u32[]{:S(2)}, u32[]{:S(2)}) %collective-permute-start.19) | collective-permute-done | bytes 294944 | tf_op jit(solution)/shard_map/ppermute | solution.py:616
  66.5 2.3 %collective-permute-done.20.got1 = bf16[2,12,48,128]{3,2,1,0:T(8,128)(2,1)S(1)} collective-permute-done((bf16[2,12,48,128]{3,2,1,0:T(8,128)(2,1)S(1)}, bf16[2,12,48,128]{3,2,1,0:T(8,128)(2,1)S(1)}, u32[]{:S(2)}, u32[]{:S(2)}) %collective-permute-start.20) | collective-permute-done | bytes 294944 | tf_op jit(solution)/shard_map/ppermute | solution.py:614
  68.8 0.0 collective-permute-start.22
  68.8 0.0 collective-permute-done.17
  68.9 1.9 %nonlocal.1.term = f32[2,48,48,128]{3,2,1,0:T(8,128)S(1)} custom-call(bf16[16,128]{1,0:T(8,128)(2,1)S(1)} %get-tuple-element.72.a, bf16[16,128]{1,0:T(8,128)(2,1)S(1)} %get-tuple-element.71.b, bf16[16,128]{1,0:T(8,128)(2,1)S(1)} %get-tuple-element.70.c, bf16[16,128]{1,0:T(8,128)(2,1)S(1)} %get-tuple-element.69.d, bf16[4,128,128]{2,1,0:T(8,128)(2,1)S(1)} %copy.19.refs_4_.q, ...), custom_call_target="tpu_custom_call" | custom-call | flops 256 | bytes 256 | tf_op jit(solution)/shard_map/nonlocal/pallas_call | solution.py:253
  70.8 0.0 collective-permute-done.21.b
  70.8 0.0 collective-permute-done.22.d
  70.8 1.8 %assembled.1.before = bf16[2,48,48,128]{3,2,1,0:T(8,128)(2,1)} custom-call(f32[2,48,48,128]{3,2,1,0:T(8,128)S(1)} %nonlocal.1.term, bf16[2,12,48,128]{3,2,1,0:T(8,128)(2,1)S(1)} %get-tuple-element.65.keep1, bf16[2,12,48,128]{3,2,1,0:T(8,128)(2,1)S(1)} %collective-permute-done.20.got1, bf16[2,12,48,128]{3,2,1,0:T(8,128)(2,1)S(1)} %get-tuple-element.66.a, ...), custom_call_target="tpu_custom_call" | custom-call | flops 256 | bytes 256 | tf_op jit(solution)/shard_map/assembled/pallas_call | solution.py:513
  72.5 1.4 %collective-permute-done.18.got2 = bf16[2,12,48,128]{3,2,1,0:T(8,128)(2,1)S(1)} collective-permute-done((bf16[2,12,48,128]{3,2,1,0:T(8,128)(2,1)S(1)}, bf16[2,12,48,128]{3,2,1,0:T(8,128)(2,1)S(1)}, u32[]{:S(2)}, u32[]{:S(2)}) %collective-permute-start.18) | collective-permute-done | bytes 294944 | tf_op jit(solution)/shard_map/ppermute | solution.py:622
  74.0 0.8 %finished.1 = bf16[2,48,48,128]{3,2,1,0:T(8,128)(2,1)} custom-call(f32[2,48,48,128]{3,2,1,0:T(8,128)S(1)} %nonlocal.1.term, bf16[2,12,48,128]{3,2,1,0:T(8,128)(2,1)S(1)} %collective-permute-done.18.got2, bf16[2,48,48,128]{3,2,1,0:T(8,128)(2,1)} %assembled.1.before), custom_call_target="tpu_custom_call", output_to_operand_aliasing={{}: (2, {})} | custom-call | flops 256 | bytes 256 | tf_op jit(solution)/shard_map/finished/pallas_call | solution.py:524
  (30 shorter events, 0.1 us)
Async XLA Ops:
  0.0 52.8 %copy-start = (bf16[12,128,128]{2,1,0:T(8,128)(2,1)S(1)}, bf16[12,128,128]{2,1,0:T(8,128)(2,1)}, u32[]{:S(2)}) copy-start(bf16[12,128,128]{2,1,0:T(8,128)(2,1)} %param.13) | copy-start | bytes 1179652
  0.0 19.9 %copy-start.2 = (bf16[8,2,48,48]{3,2,1,0:T(8,128)(2,1)S(1)}, bf16[8,2,48,48]{3,2,1,0:T(8,128)(2,1)}, u32[]{:S(2)}) copy-start(bf16[8,2,48,48]{3,2,1,0:T(8,128)(2,1)} %beta.3) | copy-start | bytes 221188
  0.0 19.8 %copy-start.7 = (s32[8]{0:T(128)S(1)}, s32[8]{0:T(128)}, u32[]{:S(2)}) copy-start(s32[8]{0:T(128)} %atoms.1) | copy-start | bytes 100
  2.2 18.1 %copy-start.1 = (bf16[2,48,48,128]{3,2,1,0:T(8,128)(2,1)S(1)}, bf16[2,48,48,128]{3,2,1,0:T(8,128)(2,1)}, u32[]{:S(2)}) copy-start(bf16[2,48,48,128]{3,2,1,0:T(8,128)(2,1)} %refs_0_.3) | copy-start | bytes 3538948
  2.2 18.1 %copy-start.4 = (f32[2,48,48]{2,1,0:T(8,128)S(1)}, f32[2,48,48]{2,1,0:T(8,128)}, u32[]{:S(2)}) copy-start(f32[2,48,48]{2,1,0:T(8,128)} %refs_1_.3) | copy-start | bytes 55300
  2.2 13.6 %collective-permute-start.1 = (bf16[2,17,48,128]{3,2,1,0:T(8,128)(2,1)S(1)}, bf16[2,17,48,128]{3,2,1,0:T(8,128)(2,1)}, u32[]{:S(2)}, u32[]{:S(2)}) collective-permute-start(bf16[2,17,48,128]{3,2,1,0:T(8,128)(2,1)S(1)} %get-tuple-element.38), channel_id=1, source_target_pairs={{0,4},{4,0},{8,12},{12,8},{16,20},{20,16},{24,28},{28,24},{1,5},{5... | collective-permute-start | bytes 1253384 | tf_op jit(solution)/shard_map/ppermute | solution.py:570
  5.2 21.8 %collective-permute-start = (bf16[2,27,48,128]{3,2,1,0:T(8,128)(2,1)}, bf16[2,27,48,128]{3,2,1,0:T(8,128)(2,1)S(1)}, u32[]{:S(2)}, u32[]{:S(2)}) collective-permute-start(bf16[2,27,48,128]{3,2,1,0:T(8,128)(2,1)} %get-tuple-element.37), channel_id=1, source_target_pairs={{4,12},{8,0},{12,20},{16,8},{20,28},{24,16},{5,13},{9,1},{13,21},{... | collective-permute-start | bytes 1990664 | tf_op jit(solution)/shard_map/ppermute | solution.py:571
  8.3 12.0 %collective-permute-start.4 = (bf16[8,48,48]{2,1,0:T(8,128)(2,1)}, bf16[8,48,48]{2,1,0:T(8,128)(2,1)S(1)}, u32[]{:S(2)}, u32[]{:S(2)}) collective-permute-start(bf16[8,48,48]{2,1,0:T(8,128)(2,1)} %get-tuple-element.42), channel_id=1, source_target_pairs={{0,4},{4,0},{8,12},{12,8},{16,20},{20,16},{24,28},{28,24},{1,5},{5... | collective-permute-start | bytes 110600 | tf_op jit(solution)/shard_map/ppermute | solution.py:567
  11.1 9.2 %collective-permute-start.5 = (bf16[8,48,48]{2,1,0:T(8,128)(2,1)}, bf16[8,48,48]{2,1,0:T(8,128)(2,1)S(1)}, u32[]{:S(2)}, u32[]{:S(2)}) collective-permute-start(bf16[8,48,48]{2,1,0:T(8,128)(2,1)} %get-tuple-element.43), channel_id=1, source_target_pairs={{4,8},{8,4},{12,16},{16,12},{20,24},{24,20},{5,9},{9,5},{13,17},{1... | collective-permute-start | bytes 110600 | tf_op jit(solution)/shard_map/ppermute | solution.py:569
  15.8 11.2 %collective-permute-start.3 = (bf16[2,17,48,128]{3,2,1,0:T(8,128)(2,1)}, bf16[2,17,48,128]{3,2,1,0:T(8,128)(2,1)S(1)}, u32[]{:S(2)}, u32[]{:S(2)}) collective-permute-start(bf16[2,17,48,128]{3,2,1,0:T(8,128)(2,1)} %collective-permute-done.1.refs_3_), channel_id=1, source_target_pairs={{0,8},{8,16},{12,4},{16,24},{20,12},{28,20},{1,9},{9,17},{13,5},{1... | collective-permute-start | bytes 1253384 | tf_op jit(solution)/shard_map/ppermute | solution.py:576
  19.8 6.4 %collective-permute-start.2 = (bf16[2,10,48,128]{3,2,1,0:T(8,128)(2,1)S(1)}, bf16[2,10,48,128]{3,2,1,0:T(8,128)(2,1)}, u32[]{:S(2)}, u32[]{:S(2)}) collective-permute-start(bf16[2,10,48,128]{3,2,1,0:T(8,128)(2,1)S(1)} %get-tuple-element.41), channel_id=1, source_target_pairs={{0,4},{4,0},{8,12},{12,8},{16,20},{20,16},{24,28},{28,24},{1,5},{5... | collective-permute-start | bytes 737288 | tf_op jit(solution)/shard_map/ppermute | solution.py:577
  23.3 7.6 %copy-start.5 = (bf16[2,48,24,48]{3,2,1,0:T(8,128)(2,1)}, bf16[2,48,24,48]{3,2,1,0:T(8,128)(2,1)S(1)}, u32[]{:S(2)}) copy-start(bf16[2,48,24,48]{3,2,1,0:T(8,128)(2,1)S(1)} %get-tuple-element.64.weights) | copy-start | bytes 663556
  27.0 4.0 %copy-start.3 = (bf16[2,17,48,128]{3,2,1,0:T(8,128)(2,1)}, bf16[2,17,48,128]{3,2,1,0:T(8,128)(2,1)S(1)}, u32[]{:S(2)}) copy-start(bf16[2,17,48,128]{3,2,1,0:T(8,128)(2,1)S(1)} %collective-permute-done.3.refs_5_.refs_4_) | copy-start | bytes 1253380
  31.0 18.5 %collective-permute-start.9 = (bf16[4,12,48,128]{3,2,1,0:T(8,128)(2,1)S(1)}, bf16[4,12,48,128]{3,2,1,0:T(8,128)(2,1)}, u32[]{:S(2)}, u32[]{:S(2)}) collective-permute-start(bf16[4,12,48,128]{3,2,1,0:T(8,128)(2,1)S(1)} %filtered.3.refs_0_), channel_id=1, source_target_pairs={{0,2},{1,3},{2,0},{3,1},{4,6},{5,7},{6,4},{7,5},{8,10},{9,11},{10,... | collective-permute-start | bytes 1769480 | tf_op jit(solution)/shard_map/ppermute | solution.py:585
  32.6 9.7 %collective-permute-start.6 = (bf16[2,10,48,128]{3,2,1,0:T(8,128)(2,1)}, bf16[2,10,48,128]{3,2,1,0:T(8,128)(2,1)S(1)}, u32[]{:S(2)}, u32[]{:S(2)}) collective-permute-start(bf16[2,10,48,128]{3,2,1,0:T(8,128)(2,1)} %collective-permute-done.2.refs_4_), channel_id=1, source_target_pairs={{0,8},{8,16},{12,4},{16,24},{20,12},{28,20},{1,9},{9,17},{13,5},{1... | collective-permute-start | bytes 737288 | tf_op jit(solution)/shard_map/ppermute | solution.py:578
  38.3 3.8 %collective-permute-start.7 = (f32[24,128]{1,0:T(8,128)S(1)}, f32[24,128]{1,0:T(8,128)S(1)}, u32[]{:S(2)}, u32[]{:S(2)}) collective-permute-start(f32[24,128]{1,0:T(8,128)S(1)} %get-tuple-element.46), channel_id=1, source_target_pairs={{0,4},{4,0},{8,12},{12,8},{16,20},{20,16},{24,28},{28,24},{1,5},{5... | collective-permute-start | bytes 36872 | tf_op jit(solution)/shard_map/ppermute | solution.py:590
  42.3 2.4 %copy-start.8 = (bf16[2,10,48,128]{3,2,1,0:T(8,128)(2,1)}, bf16[2,10,48,128]{3,2,1,0:T(8,128)(2,1)S(1)}, u32[]{:S(2)}) copy-start(bf16[2,10,48,128]{3,2,1,0:T(8,128)(2,1)S(1)} %collective-permute-done.6.refs_6_) | copy-start | bytes 737284
  42.3 7.2 %collective-permute-start.10 = (f32[24,128]{1,0:T(8,128)S(1)}, f32[24,128]{1,0:T(8,128)S(1)}, u32[]{:S(2)}, u32[]{:S(2)}) collective-permute-start(f32[24,128]{1,0:T(8,128)S(1)} %add.9), channel_id=1, source_target_pairs={{0,8},{4,12},{8,0},{12,4},{16,24},{20,28},{24,16},{28,20},{1,9},{5... | collective-permute-start | bytes 36872 | tf_op jit(solution)/shard_map/ppermute | solution.py:590
  44.7 5.4 %copy-start.10 = (s32[12,2]{0,1:T(2,128)S(1)}, s32[12,2]{0,1:T(2,128)}, u32[]{:S(2)}) copy-start(s32[12,2]{0,1:T(2,128)} %param.12) | copy-start | bytes 292
  48.9 7.9 %collective-permute-start.8 = (bf16[2,12,48,128]{3,2,1,0:T(8,128)(2,1)S(1)}, bf16[2,12,48,128]{3,2,1,0:T(8,128)(2,1)S(1)}, u32[]{:S(2)}, u32[]{:S(2)}) collective-permute-start(bf16[2,12,48,128]{3,2,1,0:T(8,128)(2,1)S(1)} %get-tuple-element.49.refs_0_), channel_id=1, source_target_pairs={{0,2},{1,3},{2,0},{3,1},{4,6},{5,7},{6,4},{7,5},{8,10},{9,11},{10,... | collective-permute-start | bytes 884744 | tf_op jit(solution)/shard_map/ppermute | solution.py:604
  49.5 5.3 %collective-permute-start.11 = (bf16[4,12,48,128]{3,2,1,0:T(8,128)(2,1)S(1)}, bf16[4,12,48,128]{3,2,1,0:T(8,128)(2,1)S(1)}, u32[]{:S(2)}, u32[]{:S(2)}) collective-permute-start(bf16[4,12,48,128]{3,2,1,0:T(8,128)(2,1)S(1)} %filtered.3.refs_0_), channel_id=1, source_target_pairs={{0,1},{1,0},{2,3},{3,2},{4,5},{5,4},{6,7},{7,6},{8,9},{9,8},{10,11... | collective-permute-start | bytes 1769480 | tf_op jit(solution)/shard_map/ppermute | solution.py:608
  49.6 5.2 %collective-permute-start.12 = (bf16[4,12,48,128]{3,2,1,0:T(8,128)(2,1)}, bf16[4,12,48,128]{3,2,1,0:T(8,128)(2,1)S(1)}, u32[]{:S(2)}, u32[]{:S(2)}) collective-permute-start(bf16[4,12,48,128]{3,2,1,0:T(8,128)(2,1)} %collective-permute-done.9.refs_2_), channel_id=1, source_target_pairs={{0,1},{1,0},{2,3},{3,2},{4,5},{5,4},{6,7},{7,6},{8,9},{9,8},{10,11... | collective-permute-start | bytes 1769480 | tf_op jit(solution)/shard_map/ppermute | solution.py:609
  50.1 4.7 %collective-permute-start.13 = (f32[24,128]{1,0:T(8,128)S(1)}, f32[24,128]{1,0:T(8,128)S(1)}, u32[]{:S(2)}, u32[]{:S(2)}) collective-permute-start(f32[24,128]{1,0:T(8,128)S(1)} %add.10), channel_id=1, source_target_pairs={{0,16},{4,20},{8,24},{12,28},{16,0},{20,4},{24,8},{28,12},{1,17},{... | collective-permute-start | bytes 36872 | tf_op jit(solution)/shard_map/ppermute | solution.py:590
  54.8 5.5 %copy-start.9 = (f32[8]{0:T(128)S(1)}, f32[8]{0:T(128)}, u32[]{:S(2)}) copy-start(f32[8]{0:T(128)} %param.10) | copy-start | bytes 100
  56.8 12.0 %copy-start.6 = (bf16[2,48,24,48]{3,2,1,0:T(8,128)(2,1)S(1)}, bf16[2,48,24,48]{3,2,1,0:T(8,128)(2,1)}, u32[]{:S(2)}) copy-start(bf16[2,48,24,48]{3,2,1,0:T(8,128)(2,1)} %copy-done.5) | copy-start | bytes 663556
  56.8 5.1 %collective-permute-start.14 = (bf16[2,12,48,128]{3,2,1,0:T(8,128)(2,1)S(1)}, bf16[2,12,48,128]{3,2,1,0:T(8,128)(2,1)S(1)}, u32[]{:S(2)}, u32[]{:S(2)}) collective-permute-start(bf16[2,12,48,128]{3,2,1,0:T(8,128)(2,1)S(1)} %collective-permute-done.8.refs_2_), channel_id=1, source_target_pairs={{0,1},{1,0},{2,3},{3,2},{4,5},{5,4},{6,7},{7,6},{8,9},{9,8},{10,11... | collective-permute-start | bytes 884744 | tf_op jit(solution)/shard_map/ppermute | solution.py:617
  56.9 5.0 %collective-permute-start.16 = (bf16[2,12,48,128]{3,2,1,0:T(8,128)(2,1)S(1)}, bf16[2,12,48,128]{3,2,1,0:T(8,128)(2,1)S(1)}, u32[]{:S(2)}, u32[]{:S(2)}) collective-permute-start(bf16[2,12,48,128]{3,2,1,0:T(8,128)(2,1)S(1)} %get-tuple-element.49.refs_0_), channel_id=1, source_target_pairs={{0,1},{1,0},{2,3},{3,2},{4,5},{5,4},{6,7},{7,6},{8,9},{9,8},{10,11... | collective-permute-start | bytes 884744 | tf_op jit(solution)/shard_map/ppermute | solution.py:602
  57.4 9.1 %collective-permute-start.19 = (bf16[2,12,48,128]{3,2,1,0:T(8,128)(2,1)S(1)}, bf16[2,12,48,128]{3,2,1,0:T(8,128)(2,1)S(1)}, u32[]{:S(2)}, u32[]{:S(2)}) collective-permute-start(bf16[2,12,48,128]{3,2,1,0:T(8,128)(2,1)S(1)} %get-tuple-element.66.a), channel_id=1, source_target_pairs={{0,2},{1,3},{2,0},{3,1},{4,6},{5,7},{6,4},{7,5},{8,10},{9,11},{10,... | collective-permute-start | bytes 884744 | tf_op jit(solution)/shard_map/ppermute | solution.py:616
  58.9 9.9 %collective-permute-start.20 = (bf16[2,12,48,128]{3,2,1,0:T(8,128)(2,1)S(1)}, bf16[2,12,48,128]{3,2,1,0:T(8,128)(2,1)S(1)}, u32[]{:S(2)}, u32[]{:S(2)}) collective-permute-start(bf16[2,12,48,128]{3,2,1,0:T(8,128)(2,1)S(1)} %get-tuple-element.57), channel_id=1, source_target_pairs={{0,4},{4,0},{8,12},{12,8},{16,20},{20,16},{24,28},{28,24},{1,5},{5... | collective-permute-start | bytes 884744 | tf_op jit(solution)/shard_map/ppermute | solution.py:614
  60.5 1.2 %collective-permute-start.15 = (bf16[16,128]{1,0:T(8,128)(2,1)S(1)}, bf16[16,128]{1,0:T(8,128)(2,1)S(1)}, u32[]{:S(2)}, u32[]{:S(2)}) collective-permute-start(bf16[16,128]{1,0:T(8,128)(2,1)S(1)} %coefficients.1), channel_id=1, source_target_pairs={{0,1},{1,0},{2,3},{3,2},{4,5},{5,4},{6,7},{7,6},{8,9},{9,8},{10,11... | collective-permute-start | bytes 12296 | tf_op jit(solution)/shard_map/ppermute | solution.py:619
  61.7 9.0 %collective-permute-start.21 = (bf16[2,12,48,128]{3,2,1,0:T(8,128)(2,1)S(1)}, bf16[2,12,48,128]{3,2,1,0:T(8,128)(2,1)S(1)}, u32[]{:S(2)}, u32[]{:S(2)}) collective-permute-start(bf16[2,12,48,128]{3,2,1,0:T(8,128)(2,1)S(1)} %get-tuple-element.66.a), channel_id=1, source_target_pairs={{0,1},{1,0},{2,3},{3,2},{4,5},{5,4},{6,7},{7,6},{8,9},{9,8},{10,11... | collective-permute-start | bytes 884744 | tf_op jit(solution)/shard_map/ppermute | solution.py:603
  62.5 11.4 %collective-permute-start.18 = (bf16[2,12,48,128]{3,2,1,0:T(8,128)(2,1)S(1)}, bf16[2,12,48,128]{3,2,1,0:T(8,128)(2,1)S(1)}, u32[]{:S(2)}, u32[]{:S(2)}) collective-permute-start(bf16[2,12,48,128]{3,2,1,0:T(8,128)(2,1)S(1)} %rotated.3), channel_id=1, source_target_pairs={{0,4},{4,0},{8,12},{12,8},{16,20},{20,16},{24,28},{28,24},{1,5},{5... | collective-permute-start | bytes 884744 | tf_op jit(solution)/shard_map/ppermute | solution.py:622
  63.2 5.6 %collective-permute-start.17 = (bf16[32,128]{1,0:T(8,128)(2,1)S(1)}, bf16[32,128]{1,0:T(8,128)(2,1)S(1)}, u32[]{:S(2)}, u32[]{:S(2)}) collective-permute-start(bf16[32,128]{1,0:T(8,128)(2,1)S(1)} %pad_maximum_fusion), channel_id=1, source_target_pairs={{0,2},{1,3},{2,0},{3,1},{4,6},{5,7},{6,4},{7,5},{8,10},{9,11},{10,... | collective-permute-start | bytes 24584 | tf_op jit(solution)/shard_map/ppermute | solution.py:624
  68.8 1.9 %collective-permute-start.22 = (bf16[2,12,48,128]{3,2,1,0:T(8,128)(2,1)S(1)}, bf16[2,12,48,128]{3,2,1,0:T(8,128)(2,1)S(1)}, u32[]{:S(2)}, u32[]{:S(2)}) collective-permute-start(bf16[2,12,48,128]{3,2,1,0:T(8,128)(2,1)S(1)} %collective-permute-done.19.c), channel_id=1, source_target_pairs={{0,1},{1,0},{2,3},{3,2},{4,5},{5,4},{6,7},{7,6},{8,9},{9,8},{10,11... | collective-permute-start | bytes 884744 | tf_op jit(solution)/shard_map/ppermute | solution.py:628

commit v22 on v21

--- a/solution.py
+++ b/solution.py
@@ -546,7 +546,7 @@
     x = lax.rem(place, 2)
     half = width_x // 2
     window = half + 2
-    rows1 = half // 4 * 2
+    rows1 = half * 8 // 24 * 2
     rows2 = half - rows1
     early = rows1 + 4
 

time: 75 us -> 80 us (1.067)
  waiting for transfers between devices: 20.9 us -> 24 us
  local copies, waits for them, and re-layouts: 0.15 us -> 2.6 us
    ppermute x1, waiting for transfers between devices: 0.86 us -> 4.11 us  [shards(): zf1 = lax.ppermute(xr1, 'space', other_way)]
    unnamed x22 -> x28, local copies, waits for them, and re-layouts: 0.05 us -> 2.51 us
    ppermute x1, waiting for transfers between devices: 4.02 us -> 6.22 us  [shards(): xr1 = lax.ppermute(to_x, 'space', swap)]
    ppermute x1, waiting for transfers between devices: 2.8 us -> 0.81 us  [shards(): xr2 = lax.ppermute(second, 'space', swap)]
    ppermute x1, waiting for transfers between devices: 2.73 us -> 4.4 us  [shards(): yk = lax.ppermute(keep_y, 'orb', across)]
    ppermute x1, starting transfers between devices: 5.73 us -> 4.28 us  [shards(): zf2 = lax.ppermute(xr2, 'space', other_way)]
    ppermute x1, waiting for transfers between devices: 1.41 us -> 0.01 us  [shards(): got2 = lax.ppermute(give2, 'space', swap)]
    ppermute x1, waiting for transfers between devices: 0.01 us -> 1.11 us  [shards(): y1 = lax.ppermute(block1, 'orb', across)]
  transfers between devices with their start and end apart: 23 -> 23, of which waited for: 10 -> 9; matrix products, arithmetic and copies ran while one was open for 1% -> 1% of each run, Pallas kernels for 21% -> 18%
where the time goes in v22:
time: 80 us; the launch traced here: 79.6 us
  starting transfers between devices  30.1 us (38%)
  waiting for transfers between devices  24 us (30%)
  Pallas kernels  21.8 us (27%)
  local copies, waits for them, and re-layouts  2.6 us (3%)
    pallas_call x2, Pallas kernels, filtered(): pl.pallas_call(functools.partial(filter_kernel, slabs, start, parts, join...  7.94 us
    ppermute x1, waiting for transfers between devices, shards(): xr1 = lax.ppermute(to_x, 'space', swap)  6.22 us
    ppermute x3, starting transfers between devices, added(): return values + lax.ppermute(values, 'space', pairs)  5.16 us
    ppermute x3, waiting for transfers between devices, added(): return values + lax.ppermute(values, 'space', pairs)  5 us
    ppermute x1, waiting for transfers between devices, shards(): yk = lax.ppermute(keep_y, 'orb', across)  4.4 us
    ppermute x1, starting transfers between devices, shards(): zf2 = lax.ppermute(xr2, 'space', other_way)  4.28 us
    ppermute x1, waiting for transfers between devices, shards(): zf1 = lax.ppermute(xr1, 'space', other_way)  4.11 us
    ppermute x1, starting transfers between devices, shards(): zf1 = lax.ppermute(xr1, 'space', other_way)  3.97 us
  transfers between devices with their start and end apart: 23, of which 9 were waited for; matrix products, arithmetic and copies ran while one was open for 1% of the time, Pallas kernels for 18%

profile of v22, /device:TPU:0, one launch (start us, length us, event | category | flops | bytes accessed | tf_op | source)
XLA Modules:
  0.0 79.6 jit_solution(11180009650768412306)
XLA Ops:
  0.0 2.2 %prepared.1 = (bf16[2,21,48,128]{3,2,1,0:T(8,128)(2,1)S(1)}, bf16[2,27,48,128]{3,2,1,0:T(8,128)(2,1)}) custom-call(bf16[2,48,48,128]{3,2,1,0:T(8,128)(2,1)} %refs_0_.3, f32[2,48,48]{2,1,0:T(8,128)} %refs_1_.3), custom_call_target="tpu_custom_call" | custom-call | flops 256 | bytes 256 | tf_op jit(solution)/shard_map/prepared/pallas_call | solution.py:81
  2.2 0.0 copy-start.1
  2.2 0.0 copy-start.4
  2.2 3.0 %collective-permute-start.1 = (bf16[2,21,48,128]{3,2,1,0:T(8,128)(2,1)S(1)}, bf16[2,21,48,128]{3,2,1,0:T(8,128)(2,1)}, u32[]{:S(2)}, u32[]{:S(2)}) collective-permute-start(bf16[2,21,48,128]{3,2,1,0:T(8,128)(2,1)S(1)} %get-tuple-element.38), channel_id=1, source_target_pairs={{0,4},{4,0},{8,12},{12,8},{16,20},{20,16},{24,28},{28,24},{1,5},{5... | collective-permute-start | bytes 1548296 | tf_op jit(solution)/shard_map/ppermute | solution.py:570
  5.2 1.3 %collective-permute-start = (bf16[2,27,48,128]{3,2,1,0:T(8,128)(2,1)}, bf16[2,27,48,128]{3,2,1,0:T(8,128)(2,1)S(1)}, u32[]{:S(2)}, u32[]{:S(2)}) collective-permute-start(bf16[2,27,48,128]{3,2,1,0:T(8,128)(2,1)} %get-tuple-element.37), channel_id=1, source_target_pairs={{4,12},{8,0},{12,20},{16,8},{20,28},{24,16},{5,13},{9,1},{13,21},{... | collective-permute-start | bytes 1990664 | tf_op jit(solution)/shard_map/ppermute | solution.py:571
  6.5 1.7 %packed.1 = (bf16[2,6,48,128]{3,2,1,0:T(8,128)(2,1)S(1)}, bf16[8,48,48]{2,1,0:T(8,128)(2,1)S(1)}, bf16[8,48,48]{2,1,0:T(8,128)(2,1)}) custom-call(bf16[2,48,48,128]{3,2,1,0:T(8,128)(2,1)} %refs_0_.3, bf16[8,2,48,48]{3,2,1,0:T(8,128)(2,1)} %beta.3), custom_call_target="tpu_custom_call" | custom-call | flops 256 | bytes 256 | tf_op jit(solution)/shard_map/packed/pallas_call | solution.py:114
  8.2 2.8 %collective-permute-start.4 = (bf16[8,48,48]{2,1,0:T(8,128)(2,1)}, bf16[8,48,48]{2,1,0:T(8,128)(2,1)S(1)}, u32[]{:S(2)}, u32[]{:S(2)}) collective-permute-start(bf16[8,48,48]{2,1,0:T(8,128)(2,1)} %get-tuple-element.42), channel_id=1, source_target_pairs={{0,4},{4,0},{8,12},{12,8},{16,20},{20,16},{24,28},{28,24},{1,5},{5... | collective-permute-start | bytes 110600 | tf_op jit(solution)/shard_map/ppermute | solution.py:567
  11.0 0.7 collective-permute-start.5
  11.7 6.2 %collective-permute-done.1.refs_3_ = bf16[2,21,48,128]{3,2,1,0:T(8,128)(2,1)} collective-permute-done((bf16[2,21,48,128]{3,2,1,0:T(8,128)(2,1)S(1)}, bf16[2,21,48,128]{3,2,1,0:T(8,128)(2,1)}, u32[]{:S(2)}, u32[]{:S(2)}) %collective-permute-start.1) | collective-permute-done | bytes 516128 | tf_op jit(solution)/shard_map/ppermute | solution.py:570
  17.9 4.0 %collective-permute-start.3 = (bf16[2,21,48,128]{3,2,1,0:T(8,128)(2,1)}, bf16[2,21,48,128]{3,2,1,0:T(8,128)(2,1)S(1)}, u32[]{:S(2)}, u32[]{:S(2)}) collective-permute-start(bf16[2,21,48,128]{3,2,1,0:T(8,128)(2,1)} %collective-permute-done.1.refs_3_), channel_id=1, source_target_pairs={{0,8},{8,16},{12,4},{16,24},{20,12},{28,20},{1,9},{9,17},{13,5},{1... | collective-permute-start | bytes 1548296 | tf_op jit(solution)/shard_map/ppermute | solution.py:576
  21.9 0.1 collective-permute-start.2
  22.0 0.1 broadcast_select_fusion
  22.1 0.3 convolution_bitcast_fusion.gram
  22.4 0.0 collective-permute-done.4.b_x
  22.4 0.0 collective-permute-done.5.b_d
  22.4 0.0 copy-done.1
  22.4 3.0 %partials.1 = (f32[24,128]{1,0:T(8,128)S(1)}, bf16[2,48,24,48]{3,2,1,0:T(8,128)(2,1)S(1)}) custom-call(s32[8]{0:T(128)S(1)} %copy-done.9, bf16[2,48,48,128]{3,2,1,0:T(8,128)(2,1)S(1)} %copy-done.1, bf16[8,2,48,48]{3,2,1,0:T(8,128)(2,1)S(1)} %copy-done.3, bf16[8,48,48]{2,1,0:T(8,128)(2,1)S(1)} %collective-permute-done.4.b_x, ...), custom_call_target="tpu_custom_call" | custom-call | flops 256 | bytes 256 | tf_op jit(solution)/shard_map/partials/pallas_call | solution.py:178
  25.5 0.8 %copy-done.7 = bf16[2,48,24,48]{3,2,1,0:T(8,128)(2,1)} copy-done((bf16[2,48,24,48]{3,2,1,0:T(8,128)(2,1)}, bf16[2,48,24,48]{3,2,1,0:T(8,128)(2,1)S(1)}, u32[]{:S(2)}) %copy-start.7) | copy-done | bytes 221208
  26.3 0.8 %collective-permute-done.2.refs_4_ = bf16[2,6,48,128]{3,2,1,0:T(8,128)(2,1)S(1)} collective-permute-done((bf16[2,6,48,128]{3,2,1,0:T(8,128)(2,1)S(1)}, bf16[2,6,48,128]{3,2,1,0:T(8,128)(2,1)S(1)}, u32[]{:S(2)}, u32[]{:S(2)}) %collective-permute-start.2) | collective-permute-done | bytes 147488 | tf_op jit(solution)/shard_map/ppermute | solution.py:577
  27.1 4.1 %collective-permute-done.3.refs_5_.refs_4_ = bf16[2,21,48,128]{3,2,1,0:T(8,128)(2,1)S(1)} collective-permute-done((bf16[2,21,48,128]{3,2,1,0:T(8,128)(2,1)}, bf16[2,21,48,128]{3,2,1,0:T(8,128)(2,1)S(1)}, u32[]{:S(2)}, u32[]{:S(2)}) %collective-permute-start.3) | collective-permute-done | bytes 516128 | tf_op jit(solution)/shard_map/ppermute | solution.py:576
  31.3 0.0 collective-permute-done.refs_2_
  31.3 0.8 %copy-done.5 = f32[2,48,48]{2,1,0:T(8,128)S(1)} copy-done((f32[2,48,48]{2,1,0:T(8,128)S(1)}, f32[2,48,48]{2,1,0:T(8,128)}, u32[]{:S(2)}) %copy-start.5) | copy-done | bytes 18456
  32.1 4.6 %filtered.3.refs_0_ = bf16[4,16,48,128]{3,2,1,0:T(8,128)(2,1)S(1)} custom-call(bf16[2,48,48,128]{3,2,1,0:T(8,128)(2,1)S(1)} %copy-done.1, f32[2,48,48]{2,1,0:T(8,128)S(1)} %copy-done.5, bf16[2,27,48,128]{3,2,1,0:T(8,128)(2,1)S(1)} %collective-permute-done.refs_2_, bf16[2,21,48,128]{3,2,1,0:T(8,128)(2,1)} %collective-permute-done.1.refs_3_, ...), custom_call_target="tpu_custom_call" | custom-call | flops 3932160 | bytes 24576000 | tf_op jit(solution)/shard_map/filtered/pallas_call | solution.py:414
  36.7 1.6 %collective-permute-start.9 = (bf16[4,16,48,128]{3,2,1,0:T(8,128)(2,1)S(1)}, bf16[4,16,48,128]{3,2,1,0:T(8,128)(2,1)}, u32[]{:S(2)}, u32[]{:S(2)}) collective-permute-start(bf16[4,16,48,128]{3,2,1,0:T(8,128)(2,1)S(1)} %filtered.3.refs_0_), channel_id=1, source_target_pairs={{0,2},{1,3},{2,0},{3,1},{4,6},{5,7},{6,4},{7,5},{8,10},{9,11},{10,... | collective-permute-start | bytes 2359304 | tf_op jit(solution)/shard_map/ppermute | solution.py:585
  38.2 4.3 %collective-permute-start.6 = (bf16[2,6,48,128]{3,2,1,0:T(8,128)(2,1)S(1)}, bf16[2,6,48,128]{3,2,1,0:T(8,128)(2,1)S(1)}, u32[]{:S(2)}, u32[]{:S(2)}) collective-permute-start(bf16[2,6,48,128]{3,2,1,0:T(8,128)(2,1)S(1)} %collective-permute-done.2.refs_4_), channel_id=1, source_target_pairs={{0,8},{8,16},{12,4},{16,24},{20,12},{28,20},{1,9},{9,17},{13,5},{1... | collective-permute-start | bytes 442376 | tf_op jit(solution)/shard_map/ppermute | solution.py:578
  42.5 0.1 collective-permute-start.7
  42.6 3.7 %collective-permute-done.7 = f32[24,128]{1,0:T(8,128)S(1)} collective-permute-done((f32[24,128]{1,0:T(8,128)S(1)}, f32[24,128]{1,0:T(8,128)S(1)}, u32[]{:S(2)}, u32[]{:S(2)}) %collective-permute-start.7) | collective-permute-done | bytes 12320 | tf_op jit(solution)/shard_map/ppermute | solution.py:590
  46.3 0.0 collective-permute-done.6.refs_6_
  46.3 1.6 %collective-permute-start.10 = (f32[24,128]{1,0:T(8,128)S(1)}, f32[24,128]{1,0:T(8,128)S(1)}, u32[]{:S(2)}, u32[]{:S(2)}) collective-permute-start(f32[24,128]{1,0:T(8,128)S(1)} %add.9), channel_id=1, source_target_pairs={{0,8},{4,12},{8,0},{12,4},{16,24},{20,28},{24,16},{28,20},{1,9},{5... | collective-permute-start | bytes 36872 | tf_op jit(solution)/shard_map/ppermute | solution.py:590
  48.0 0.8 %copy-done.6 = f32[2,48,48]{2,1,0:T(8,128)S(1)} copy-done((f32[2,48,48]{2,1,0:T(8,128)S(1)}, f32[2,48,48]{2,1,0:T(8,128)}, u32[]{:S(2)}) %copy-start.6) | copy-done | bytes 18456
  48.8 3.4 %filtered.2 = (bf16[2,8,48,128]{3,2,1,0:T(8,128)(2,1)S(1)}, bf16[2,8,48,128]{3,2,1,0:T(8,128)(2,1)S(1)}) custom-call(bf16[2,48,48,128]{3,2,1,0:T(8,128)(2,1)S(1)} %copy-done.1, f32[2,48,48]{2,1,0:T(8,128)S(1)} %copy-done.6, bf16[2,27,48,128]{3,2,1,0:T(8,128)(2,1)S(1)} %collective-permute-done.refs_2_, ...), custom_call_target="tpu_custom_call" | custom-call | flops 1966080 | bytes 12288000 | tf_op jit(solution)/shard_map/filtered/pallas_call | solution.py:414
  52.1 0.0 collective-permute-done.10
  52.2 1.1 %collective-permute-done.9.refs_2_ = bf16[4,16,48,128]{3,2,1,0:T(8,128)(2,1)} collective-permute-done((bf16[4,16,48,128]{3,2,1,0:T(8,128)(2,1)S(1)}, bf16[4,16,48,128]{3,2,1,0:T(8,128)(2,1)}, u32[]{:S(2)}, u32[]{:S(2)}) %collective-permute-start.9) | collective-permute-done | bytes 786464 | tf_op jit(solution)/shard_map/ppermute | solution.py:585
  53.3 0.0 collective-permute-start.12
  53.3 0.5 collective-permute-start.11
  53.8 1.5 %collective-permute-start.8 = (bf16[2,8,48,128]{3,2,1,0:T(8,128)(2,1)S(1)}, bf16[2,8,48,128]{3,2,1,0:T(8,128)(2,1)S(1)}, u32[]{:S(2)}, u32[]{:S(2)}) collective-permute-start(bf16[2,8,48,128]{3,2,1,0:T(8,128)(2,1)S(1)} %get-tuple-element.49.refs_0_), channel_id=1, source_target_pairs={{0,2},{1,3},{2,0},{3,1},{4,6},{5,7},{6,4},{7,5},{8,10},{9,11},{10,... | collective-permute-start | bytes 589832 | tf_op jit(solution)/shard_map/ppermute | solution.py:604
  55.3 3.5 %collective-permute-start.13 = (f32[24,128]{1,0:T(8,128)S(1)}, f32[24,128]{1,0:T(8,128)S(1)}, u32[]{:S(2)}, u32[]{:S(2)}) collective-permute-start(f32[24,128]{1,0:T(8,128)S(1)} %add.10), channel_id=1, source_target_pairs={{0,16},{4,20},{8,24},{12,28},{16,0},{20,4},{24,8},{28,12},{1,17},{... | collective-permute-start | bytes 36872 | tf_op jit(solution)/shard_map/ppermute | solution.py:590
  58.8 0.3 fusion
  59.1 1.3 %collective-permute-done.13 = f32[24,128]{1,0:T(8,128)S(1)} collective-permute-done((f32[24,128]{1,0:T(8,128)S(1)}, f32[24,128]{1,0:T(8,128)S(1)}, u32[]{:S(2)}, u32[]{:S(2)}) %collective-permute-start.13) | collective-permute-done | bytes 12320 | tf_op jit(solution)/shard_map/ppermute | solution.py:590
  60.5 0.0 collective-permute-done.12.refs_3_
  60.5 0.0 collective-permute-done.11.refs_1_
  60.5 2.3 %rotated.2 = (bf16[2,16,48,128]{3,2,1,0:T(8,128)(2,1)S(1)}, bf16[2,16,48,128]{3,2,1,0:T(8,128)(2,1)S(1)}) custom-call(bf16[4,16,48,128]{3,2,1,0:T(8,128)(2,1)S(1)} %filtered.3.refs_0_, bf16[4,16,48,128]{3,2,1,0:T(8,128)(2,1)S(1)} %collective-permute-done.11.refs_1_, bf16[4,16,48,128]{3,2,1,0:T(8,128)(2,1)} %collective-permute-done.9.refs_2_, ...), custom_call_target="tpu_custom_call" | custom-call | flops 25165824 | bytes 245760 | tf_op jit(solution)/shard_map/rotated/pallas_call | solution.py:460
  62.8 0.0 collective-permute-done.8.refs_2_
  62.8 0.1 collective-permute-start.14
  62.9 0.5 collective-permute-start.16
  63.4 1.8 %collective-permute-start.20 = (bf16[2,16,48,128]{3,2,1,0:T(8,128)(2,1)S(1)}, bf16[2,16,48,128]{3,2,1,0:T(8,128)(2,1)S(1)}, u32[]{:S(2)}, u32[]{:S(2)}) collective-permute-start(bf16[2,16,48,128]{3,2,1,0:T(8,128)(2,1)S(1)} %get-tuple-element.57), channel_id=1, source_target_pairs={{0,4},{4,0},{8,12},{12,8},{16,20},{20,16},{24,28},{28,24},{1,5},{5... | collective-permute-start | bytes 1179656 | tf_op jit(solution)/shard_map/ppermute | solution.py:614
  65.2 0.1 broadcast_in_dim.22.strength
  65.3 0.1 coefficients.1
  65.4 0.0 collective-permute-start.15
  65.5 0.5 collective-permute-start.21
  66.0 0.7 collective-permute-done.15
  66.6 0.5 collective-permute-start.19
  67.1 0.0 collective-permute-done.16.refs_1_
  67.1 0.4 rotated.3
  67.5 1.6 %collective-permute-start.17 = (bf16[32,128]{1,0:T(8,128)(2,1)S(1)}, bf16[32,128]{1,0:T(8,128)(2,1)S(1)}, u32[]{:S(2)}, u32[]{:S(2)}) collective-permute-start(bf16[32,128]{1,0:T(8,128)(2,1)S(1)} %pad_maximum_fusion), channel_id=1, source_target_pairs={{0,2},{1,3},{2,0},{3,1},{4,6},{5,7},{6,4},{7,5},{8,10},{9,11},{10,... | collective-permute-start | bytes 24584 | tf_op jit(solution)/shard_map/ppermute | solution.py:624
  69.1 0.2 collective-permute-start.18
  69.3 4.4 %collective-permute-done.19.c = bf16[2,8,48,128]{3,2,1,0:T(8,128)(2,1)S(1)} collective-permute-done((bf16[2,8,48,128]{3,2,1,0:T(8,128)(2,1)S(1)}, bf16[2,8,48,128]{3,2,1,0:T(8,128)(2,1)S(1)}, u32[]{:S(2)}, u32[]{:S(2)}) %collective-permute-start.19) | collective-permute-done | bytes 196640 | tf_op jit(solution)/shard_map/ppermute | solution.py:616
  73.7 1.6 %collective-permute-done.20.got1 = bf16[2,16,48,128]{3,2,1,0:T(8,128)(2,1)S(1)} collective-permute-done((bf16[2,16,48,128]{3,2,1,0:T(8,128)(2,1)S(1)}, bf16[2,16,48,128]{3,2,1,0:T(8,128)(2,1)S(1)}, u32[]{:S(2)}, u32[]{:S(2)}) %collective-permute-start.20) | collective-permute-done | bytes 393248 | tf_op jit(solution)/shard_map/ppermute | solution.py:614
  75.3 1.9 %nonlocal.1.term = f32[2,48,48,128]{3,2,1,0:T(8,128)S(1)} custom-call(bf16[16,128]{1,0:T(8,128)(2,1)S(1)} %get-tuple-element.72.a, bf16[16,128]{1,0:T(8,128)(2,1)S(1)} %get-tuple-element.71.b, bf16[16,128]{1,0:T(8,128)(2,1)S(1)} %get-tuple-element.70.c, bf16[16,128]{1,0:T(8,128)(2,1)S(1)} %get-tuple-element.69.d, bf16[4,128,128]{2,1,0:T(8,128)(2,1)S(1)} %copy.19.refs_4_.q, ...), custom_call_target="tpu_custom_call" | custom-call | flops 256 | bytes 256 | tf_op jit(solution)/shard_map/nonlocal/pallas_call | solution.py:253
  77.2 0.0 collective-permute-done.21.b
  77.2 0.0 collective-permute-done.22.d
  77.3 1.6 %assembled.1.before = bf16[2,48,48,128]{3,2,1,0:T(8,128)(2,1)} custom-call(f32[2,48,48,128]{3,2,1,0:T(8,128)S(1)} %nonlocal.1.term, bf16[2,16,48,128]{3,2,1,0:T(8,128)(2,1)S(1)} %get-tuple-element.65.keep1, bf16[2,16,48,128]{3,2,1,0:T(8,128)(2,1)S(1)} %collective-permute-done.20.got1, bf16[2,8,48,128]{3,2,1,0:T(8,128)(2,1)S(1)} %get-tuple-element.66.a, ...), custom_call_target="tpu_custom_call" | custom-call | flops 256 | bytes 256 | tf_op jit(solution)/shard_map/assembled/pallas_call | solution.py:513
  78.8 0.0 collective-permute-done.18.got2
  78.9 0.7 finished.1
  (36 shorter events, 0.1 us)
Async XLA Ops:
  0.0 58.8 %copy-start = (bf16[12,128,128]{2,1,0:T(8,128)(2,1)S(1)}, bf16[12,128,128]{2,1,0:T(8,128)(2,1)}, u32[]{:S(2)}) copy-start(bf16[12,128,128]{2,1,0:T(8,128)(2,1)} %param.13) | copy-start | bytes 1179652
  0.0 22.0 %copy-start.3 = (bf16[8,2,48,48]{3,2,1,0:T(8,128)(2,1)S(1)}, bf16[8,2,48,48]{3,2,1,0:T(8,128)(2,1)}, u32[]{:S(2)}) copy-start(bf16[8,2,48,48]{3,2,1,0:T(8,128)(2,1)} %beta.3) | copy-start | bytes 221188
  0.0 21.9 %copy-start.9 = (s32[8]{0:T(128)S(1)}, s32[8]{0:T(128)}, u32[]{:S(2)}) copy-start(s32[8]{0:T(128)} %atoms.1) | copy-start | bytes 100
  2.2 20.2 %copy-start.1 = (bf16[2,48,48,128]{3,2,1,0:T(8,128)(2,1)S(1)}, bf16[2,48,48,128]{3,2,1,0:T(8,128)(2,1)}, u32[]{:S(2)}) copy-start(bf16[2,48,48,128]{3,2,1,0:T(8,128)(2,1)} %refs_0_.3) | copy-start | bytes 3538948
  2.2 20.2 %copy-start.4 = (f32[2,48,48]{2,1,0:T(8,128)S(1)}, f32[2,48,48]{2,1,0:T(8,128)}, u32[]{:S(2)}) copy-start(f32[2,48,48]{2,1,0:T(8,128)} %refs_1_.3) | copy-start | bytes 55300
  2.2 15.7 %collective-permute-start.1 = (bf16[2,21,48,128]{3,2,1,0:T(8,128)(2,1)S(1)}, bf16[2,21,48,128]{3,2,1,0:T(8,128)(2,1)}, u32[]{:S(2)}, u32[]{:S(2)}) collective-permute-start(bf16[2,21,48,128]{3,2,1,0:T(8,128)(2,1)S(1)} %get-tuple-element.38), channel_id=1, source_target_pairs={{0,4},{4,0},{8,12},{12,8},{16,20},{20,16},{24,28},{28,24},{1,5},{5... | collective-permute-start | bytes 1548296 | tf_op jit(solution)/shard_map/ppermute | solution.py:570
  5.2 26.0 %collective-permute-start = (bf16[2,27,48,128]{3,2,1,0:T(8,128)(2,1)}, bf16[2,27,48,128]{3,2,1,0:T(8,128)(2,1)S(1)}, u32[]{:S(2)}, u32[]{:S(2)}) collective-permute-start(bf16[2,27,48,128]{3,2,1,0:T(8,128)(2,1)} %get-tuple-element.37), channel_id=1, source_target_pairs={{4,12},{8,0},{12,20},{16,8},{20,28},{24,16},{5,13},{9,1},{13,21},{... | collective-permute-start | bytes 1990664 | tf_op jit(solution)/shard_map/ppermute | solution.py:571
  8.2 14.2 %collective-permute-start.4 = (bf16[8,48,48]{2,1,0:T(8,128)(2,1)}, bf16[8,48,48]{2,1,0:T(8,128)(2,1)S(1)}, u32[]{:S(2)}, u32[]{:S(2)}) collective-permute-start(bf16[8,48,48]{2,1,0:T(8,128)(2,1)} %get-tuple-element.42), channel_id=1, source_target_pairs={{0,4},{4,0},{8,12},{12,8},{16,20},{20,16},{24,28},{28,24},{1,5},{5... | collective-permute-start | bytes 110600 | tf_op jit(solution)/shard_map/ppermute | solution.py:567
  11.0 11.4 %collective-permute-start.5 = (bf16[8,48,48]{2,1,0:T(8,128)(2,1)S(1)}, bf16[8,48,48]{2,1,0:T(8,128)(2,1)S(1)}, u32[]{:S(2)}, u32[]{:S(2)}) collective-permute-start(bf16[8,48,48]{2,1,0:T(8,128)(2,1)S(1)} %get-tuple-element.43), channel_id=1, source_target_pairs={{4,8},{8,4},{12,16},{16,12},{20,24},{24,20},{5,9},{9,5},{13,17},{1... | collective-permute-start | bytes 110600 | tf_op jit(solution)/shard_map/ppermute | solution.py:569
  17.9 13.3 %collective-permute-start.3 = (bf16[2,21,48,128]{3,2,1,0:T(8,128)(2,1)}, bf16[2,21,48,128]{3,2,1,0:T(8,128)(2,1)S(1)}, u32[]{:S(2)}, u32[]{:S(2)}) collective-permute-start(bf16[2,21,48,128]{3,2,1,0:T(8,128)(2,1)} %collective-permute-done.1.refs_3_), channel_id=1, source_target_pairs={{0,8},{8,16},{12,4},{16,24},{20,12},{28,20},{1,9},{9,17},{13,5},{1... | collective-permute-start | bytes 1548296 | tf_op jit(solution)/shard_map/ppermute | solution.py:576
  21.9 5.2 %collective-permute-start.2 = (bf16[2,6,48,128]{3,2,1,0:T(8,128)(2,1)S(1)}, bf16[2,6,48,128]{3,2,1,0:T(8,128)(2,1)S(1)}, u32[]{:S(2)}, u32[]{:S(2)}) collective-permute-start(bf16[2,6,48,128]{3,2,1,0:T(8,128)(2,1)S(1)} %get-tuple-element.41), channel_id=1, source_target_pairs={{0,4},{4,0},{8,12},{12,8},{16,20},{20,16},{24,28},{28,24},{1,5},{5... | collective-permute-start | bytes 442376 | tf_op jit(solution)/shard_map/ppermute | solution.py:577
  25.5 0.8 %copy-start.7 = (bf16[2,48,24,48]{3,2,1,0:T(8,128)(2,1)}, bf16[2,48,24,48]{3,2,1,0:T(8,128)(2,1)S(1)}, u32[]{:S(2)}) copy-start(bf16[2,48,24,48]{3,2,1,0:T(8,128)(2,1)S(1)} %get-tuple-element.64.weights) | copy-start | bytes 663556
  27.1 11.1 %copy-start.10 = (bf16[2,6,48,128]{3,2,1,0:T(8,128)(2,1)}, bf16[2,6,48,128]{3,2,1,0:T(8,128)(2,1)S(1)}, u32[]{:S(2)}) copy-start(bf16[2,6,48,128]{3,2,1,0:T(8,128)(2,1)S(1)} %collective-permute-done.2.refs_4_) | copy-start | bytes 442372
  31.3 5.4 %copy-start.2 = (bf16[2,21,48,128]{3,2,1,0:T(8,128)(2,1)}, bf16[2,21,48,128]{3,2,1,0:T(8,128)(2,1)S(1)}, u32[]{:S(2)}) copy-start(bf16[2,21,48,128]{3,2,1,0:T(8,128)(2,1)S(1)} %collective-permute-done.3.refs_5_.refs_4_) | copy-start | bytes 1548292
  31.3 0.8 %copy-start.5 = (f32[2,48,48]{2,1,0:T(8,128)S(1)}, f32[2,48,48]{2,1,0:T(8,128)}, u32[]{:S(2)}) copy-start(f32[2,48,48]{2,1,0:T(8,128)} %refs_1_.3) | copy-start | bytes 55300
  36.7 16.6 %collective-permute-start.9 = (bf16[4,16,48,128]{3,2,1,0:T(8,128)(2,1)S(1)}, bf16[4,16,48,128]{3,2,1,0:T(8,128)(2,1)}, u32[]{:S(2)}, u32[]{:S(2)}) collective-permute-start(bf16[4,16,48,128]{3,2,1,0:T(8,128)(2,1)S(1)} %filtered.3.refs_0_), channel_id=1, source_target_pairs={{0,2},{1,3},{2,0},{3,1},{4,6},{5,7},{6,4},{7,5},{8,10},{9,11},{10,... | collective-permute-start | bytes 2359304 | tf_op jit(solution)/shard_map/ppermute | solution.py:585
  38.2 8.1 %collective-permute-start.6 = (bf16[2,6,48,128]{3,2,1,0:T(8,128)(2,1)S(1)}, bf16[2,6,48,128]{3,2,1,0:T(8,128)(2,1)S(1)}, u32[]{:S(2)}, u32[]{:S(2)}) collective-permute-start(bf16[2,6,48,128]{3,2,1,0:T(8,128)(2,1)S(1)} %collective-permute-done.2.refs_4_), channel_id=1, source_target_pairs={{0,8},{8,16},{12,4},{16,24},{20,12},{28,20},{1,9},{9,17},{13,5},{1... | collective-permute-start | bytes 442376 | tf_op jit(solution)/shard_map/ppermute | solution.py:578
  42.5 3.8 %collective-permute-start.7 = (f32[24,128]{1,0:T(8,128)S(1)}, f32[24,128]{1,0:T(8,128)S(1)}, u32[]{:S(2)}, u32[]{:S(2)}) collective-permute-start(f32[24,128]{1,0:T(8,128)S(1)} %get-tuple-element.46), channel_id=1, source_target_pairs={{0,4},{4,0},{8,12},{12,8},{16,20},{20,16},{24,28},{28,24},{1,5},{5... | collective-permute-start | bytes 36872 | tf_op jit(solution)/shard_map/ppermute | solution.py:590
  46.3 1.6 %copy-start.11 = (bf16[2,6,48,128]{3,2,1,0:T(8,128)(2,1)}, bf16[2,6,48,128]{3,2,1,0:T(8,128)(2,1)S(1)}, u32[]{:S(2)}) copy-start(bf16[2,6,48,128]{3,2,1,0:T(8,128)(2,1)S(1)} %collective-permute-done.6.refs_6_) | copy-start | bytes 442372
  46.3 5.8 %collective-permute-start.10 = (f32[24,128]{1,0:T(8,128)S(1)}, f32[24,128]{1,0:T(8,128)S(1)}, u32[]{:S(2)}, u32[]{:S(2)}) collective-permute-start(f32[24,128]{1,0:T(8,128)S(1)} %add.9), channel_id=1, source_target_pairs={{0,8},{4,12},{8,0},{12,4},{16,24},{20,28},{24,16},{28,20},{1,9},{5... | collective-permute-start | bytes 36872 | tf_op jit(solution)/shard_map/ppermute | solution.py:590
  47.9 0.8 %copy-start.6 = (f32[2,48,48]{2,1,0:T(8,128)S(1)}, f32[2,48,48]{2,1,0:T(8,128)}, u32[]{:S(2)}) copy-start(f32[2,48,48]{2,1,0:T(8,128)} %refs_1_.3) | copy-start | bytes 55300
  48.7 6.6 %copy-start.13 = (s32[12,2]{0,1:T(2,128)S(1)}, s32[12,2]{0,1:T(2,128)}, u32[]{:S(2)}) copy-start(s32[12,2]{0,1:T(2,128)} %param.12) | copy-start | bytes 292
  53.3 7.2 %collective-permute-start.12 = (bf16[4,16,48,128]{3,2,1,0:T(8,128)(2,1)}, bf16[4,16,48,128]{3,2,1,0:T(8,128)(2,1)S(1)}, u32[]{:S(2)}, u32[]{:S(2)}) collective-permute-start(bf16[4,16,48,128]{3,2,1,0:T(8,128)(2,1)} %collective-permute-done.9.refs_2_), channel_id=1, source_target_pairs={{0,1},{1,0},{2,3},{3,2},{4,5},{5,4},{6,7},{7,6},{8,9},{9,8},{10,11... | collective-permute-start | bytes 2359304 | tf_op jit(solution)/shard_map/ppermute | solution.py:609
  53.3 7.2 %collective-permute-start.11 = (bf16[4,16,48,128]{3,2,1,0:T(8,128)(2,1)S(1)}, bf16[4,16,48,128]{3,2,1,0:T(8,128)(2,1)S(1)}, u32[]{:S(2)}, u32[]{:S(2)}) collective-permute-start(bf16[4,16,48,128]{3,2,1,0:T(8,128)(2,1)S(1)} %filtered.3.refs_0_), channel_id=1, source_target_pairs={{0,1},{1,0},{2,3},{3,2},{4,5},{5,4},{6,7},{7,6},{8,9},{9,8},{10,11... | collective-permute-start | bytes 2359304 | tf_op jit(solution)/shard_map/ppermute | solution.py:608
  53.8 9.0 %collective-permute-start.8 = (bf16[2,8,48,128]{3,2,1,0:T(8,128)(2,1)S(1)}, bf16[2,8,48,128]{3,2,1,0:T(8,128)(2,1)S(1)}, u32[]{:S(2)}, u32[]{:S(2)}) collective-permute-start(bf16[2,8,48,128]{3,2,1,0:T(8,128)(2,1)S(1)} %get-tuple-element.49.refs_0_), channel_id=1, source_target_pairs={{0,2},{1,3},{2,0},{3,1},{4,6},{5,7},{6,4},{7,5},{8,10},{9,11},{10,... | collective-permute-start | bytes 589832 | tf_op jit(solution)/shard_map/ppermute | solution.py:604
  55.3 5.1 %collective-permute-start.13 = (f32[24,128]{1,0:T(8,128)S(1)}, f32[24,128]{1,0:T(8,128)S(1)}, u32[]{:S(2)}, u32[]{:S(2)}) collective-permute-start(f32[24,128]{1,0:T(8,128)S(1)} %add.10), channel_id=1, source_target_pairs={{0,16},{4,20},{8,24},{12,28},{16,0},{20,4},{24,8},{28,12},{1,17},{... | collective-permute-start | bytes 36872 | tf_op jit(solution)/shard_map/ppermute | solution.py:590
  60.5 4.7 %copy-start.12 = (f32[8]{0:T(128)S(1)}, f32[8]{0:T(128)}, u32[]{:S(2)}) copy-start(f32[8]{0:T(128)} %param.10) | copy-start | bytes 100
  62.8 12.6 %copy-start.8 = (bf16[2,48,24,48]{3,2,1,0:T(8,128)(2,1)S(1)}, bf16[2,48,24,48]{3,2,1,0:T(8,128)(2,1)}, u32[]{:S(2)}) copy-start(bf16[2,48,24,48]{3,2,1,0:T(8,128)(2,1)} %copy-done.7) | copy-start | bytes 663556
  62.8 4.3 %collective-permute-start.14 = (bf16[2,8,48,128]{3,2,1,0:T(8,128)(2,1)S(1)}, bf16[2,8,48,128]{3,2,1,0:T(8,128)(2,1)S(1)}, u32[]{:S(2)}, u32[]{:S(2)}) collective-permute-start(bf16[2,8,48,128]{3,2,1,0:T(8,128)(2,1)S(1)} %collective-permute-done.8.refs_2_), channel_id=1, source_target_pairs={{0,1},{1,0},{2,3},{3,2},{4,5},{5,4},{6,7},{7,6},{8,9},{9,8},{10,11... | collective-permute-start | bytes 589832 | tf_op jit(solution)/shard_map/ppermute | solution.py:617
  62.9 4.3 %collective-permute-start.16 = (bf16[2,8,48,128]{3,2,1,0:T(8,128)(2,1)S(1)}, bf16[2,8,48,128]{3,2,1,0:T(8,128)(2,1)S(1)}, u32[]{:S(2)}, u32[]{:S(2)}) collective-permute-start(bf16[2,8,48,128]{3,2,1,0:T(8,128)(2,1)S(1)} %get-tuple-element.49.refs_0_), channel_id=1, source_target_pairs={{0,1},{1,0},{2,3},{3,2},{4,5},{5,4},{6,7},{7,6},{8,9},{9,8},{10,11... | collective-permute-start | bytes 589832 | tf_op jit(solution)/shard_map/ppermute | solution.py:602
  63.4 12.0 %collective-permute-start.20 = (bf16[2,16,48,128]{3,2,1,0:T(8,128)(2,1)S(1)}, bf16[2,16,48,128]{3,2,1,0:T(8,128)(2,1)S(1)}, u32[]{:S(2)}, u32[]{:S(2)}) collective-permute-start(bf16[2,16,48,128]{3,2,1,0:T(8,128)(2,1)S(1)} %get-tuple-element.57), channel_id=1, source_target_pairs={{0,4},{4,0},{8,12},{12,8},{16,20},{20,16},{24,28},{28,24},{1,5},{5... | collective-permute-start | bytes 1179656 | tf_op jit(solution)/shard_map/ppermute | solution.py:614
  65.4 1.2 %collective-permute-start.15 = (bf16[16,128]{1,0:T(8,128)(2,1)S(1)}, bf16[16,128]{1,0:T(8,128)(2,1)S(1)}, u32[]{:S(2)}, u32[]{:S(2)}) collective-permute-start(bf16[16,128]{1,0:T(8,128)(2,1)S(1)} %coefficients.1), channel_id=1, source_target_pairs={{0,1},{1,0},{2,3},{3,2},{4,5},{5,4},{6,7},{7,6},{8,9},{9,8},{10,11... | collective-permute-start | bytes 12296 | tf_op jit(solution)/shard_map/ppermute | solution.py:619
  65.5 11.8 %collective-permute-start.21 = (bf16[2,8,48,128]{3,2,1,0:T(8,128)(2,1)S(1)}, bf16[2,8,48,128]{3,2,1,0:T(8,128)(2,1)S(1)}, u32[]{:S(2)}, u32[]{:S(2)}) collective-permute-start(bf16[2,8,48,128]{3,2,1,0:T(8,128)(2,1)S(1)} %get-tuple-element.66.a), channel_id=1, source_target_pairs={{0,1},{1,0},{2,3},{3,2},{4,5},{5,4},{6,7},{7,6},{8,9},{9,8},{10,11... | collective-permute-start | bytes 589832 | tf_op jit(solution)/shard_map/ppermute | solution.py:603
  66.6 7.1 %collective-permute-start.19 = (bf16[2,8,48,128]{3,2,1,0:T(8,128)(2,1)S(1)}, bf16[2,8,48,128]{3,2,1,0:T(8,128)(2,1)S(1)}, u32[]{:S(2)}, u32[]{:S(2)}) collective-permute-start(bf16[2,8,48,128]{3,2,1,0:T(8,128)(2,1)S(1)} %get-tuple-element.66.a), channel_id=1, source_target_pairs={{0,2},{1,3},{2,0},{3,1},{4,6},{5,7},{6,4},{7,5},{8,10},{9,11},{10,... | collective-permute-start | bytes 589832 | tf_op jit(solution)/shard_map/ppermute | solution.py:616
  67.5 7.8 %collective-permute-start.17 = (bf16[32,128]{1,0:T(8,128)(2,1)S(1)}, bf16[32,128]{1,0:T(8,128)(2,1)S(1)}, u32[]{:S(2)}, u32[]{:S(2)}) collective-permute-start(bf16[32,128]{1,0:T(8,128)(2,1)S(1)} %pad_maximum_fusion), channel_id=1, source_target_pairs={{0,2},{1,3},{2,0},{3,1},{4,6},{5,7},{6,4},{7,5},{8,10},{9,11},{10,... | collective-permute-start | bytes 24584 | tf_op jit(solution)/shard_map/ppermute | solution.py:624
  69.1 9.8 %collective-permute-start.18 = (bf16[2,8,48,128]{3,2,1,0:T(8,128)(2,1)S(1)}, bf16[2,8,48,128]{3,2,1,0:T(8,128)(2,1)S(1)}, u32[]{:S(2)}, u32[]{:S(2)}) collective-permute-start(bf16[2,8,48,128]{3,2,1,0:T(8,128)(2,1)S(1)} %rotated.3), channel_id=1, source_target_pairs={{0,4},{4,0},{8,12},{12,8},{16,20},{20,16},{24,28},{28,24},{1,5},{5... | collective-permute-start | bytes 589832 | tf_op jit(solution)/shard_map/ppermute | solution.py:622
  75.3 1.9 %collective-permute-start.22 = (bf16[2,8,48,128]{3,2,1,0:T(8,128)(2,1)S(1)}, bf16[2,8,48,128]{3,2,1,0:T(8,128)(2,1)S(1)}, u32[]{:S(2)}, u32[]{:S(2)}) collective-permute-start(bf16[2,8,48,128]{3,2,1,0:T(8,128)(2,1)S(1)} %collective-permute-done.19.c), channel_id=1, source_target_pairs={{0,1},{1,0},{2,3},{3,2},{4,5},{5,4},{6,7},{7,6},{8,9},{9,8},{10,11... | collective-permute-start | bytes 589832 | tf_op jit(solution)/shard_map/ppermute | solution.py:628
